TPU v7x, 32 devices: a whole 2x2x4 slice. The times are simulated.
32 devices in a mesh: node: 8 (over z, y), col: 4 (over x, core).
Axes of the slice: x: 2, y: 2, z: 4, core: 2. Of those that a mesh axis runs over, the one named last changes fastest.
Arguments:
- blocks: float32 [2304, 128, 128], P('node'), may hold values from 0.001 to 1
- owner_row: int32 [8, 288], P('node'), may hold values from 0 to 47, never falling along the last dimension, each value on 1 to 10 neighbouring positions
- block_col: int32 [8, 288], P('node'), may hold values from 0 to 383, as said below
- start: float32 [128, 49152], P('col', 'node'), may hold values from -160 to 160
Outputs:
- basis: float32 [128, 49152], P('col', 'node')
- projected_first: float32 [128, 128], P('col')
- projected: float32 [128, 128], P('col')
Inputs may be any that keep to these rules, and one draw needn't show every extreme that they name: `owner_row`: the stored blocks of one index of node are listed by block row, never falling; every block row has 1 to 10 stored blocks, one has exactly 10. `block_col`: A block stored at index g of node has its block column among the block rows of index g, among the last 24 block rows of index g - 1, or among the first 24 block rows of index g + 1, cyclically over node; every index has blocks at both of those bounds.
All inputs are finite; a program needn't handle non-finite values.
Results may differ from a plain program's by a relative error of at most 0.0003.
Values sent between devices are 32-bit elements; how exact they have to be, the bound alone decides.
No kernel may reach another device: no remote copies, remote signals or barrier semaphores. Data moves between devices by JAX's collectives and lax.ppermute only.
A program may use at most 128 MiB of HBM per device.

v0:
```python
import jax
import jax.numpy as jnp
from jax import lax
from jax.sharding import PartitionSpec as P

DEGREE = 4
ITERS = 2


precise = lax.Precision.HIGHEST
center = 1.025
half_width = 0.975


def extended_2(cells, sides, width):
    for axis, dim in sides:
        count = lax.axis_size(axis)
        head = lax.slice_in_dim(cells, 0, width, axis=dim)
        tail = lax.slice_in_dim(cells, cells.shape[dim] - width, cells.shape[dim], axis=dim)
        cells = jnp.concatenate(
            [
                lax.ppermute(tail, axis, [(i, (i + 1) % count) for i in range(count)]),
                cells,
                lax.ppermute(head, axis, [((i + 1) % count, i) for i in range(count)]),
            ],
            axis=dim,
        )
    return cells


def chebyshev(panel, operate):
    previous = panel
    current = (operate(panel) - center * panel) / half_width
    for step in range(DEGREE - 1):
        following = 2.0 * (operate(current) - center * current) / half_width - previous
        previous = current
        current = following
    return current


def body(blocks, owner_row, block_col, start):
    cols_here = start.shape[0]
    width = start.shape[1]
    block = blocks.shape[1]
    rows_blocks = width // block
    groups = lax.axis_size("node")
    nodes = width * groups
    row_ids = owner_row[0]
    col_ids = block_col[0]
    onehot = (row_ids[None, :] == jnp.arange(rows_blocks, dtype=jnp.int32)[:, None]).astype(
        jnp.float32
    )
    degree = jnp.einsum("rn,ni->ri", onehot, jnp.sum(blocks, axis=2), precision=precise).reshape(
        width
    )
    node_me = lax.axis_index("node")
    owner = col_ids // rows_blocks
    side = (owner - node_me + 1) % groups
    lookup = (side - 1) * rows_blocks + col_ids % rows_blocks + rows_blocks
    col_me = lax.axis_index("col")

    def operate(panel):
        extended = extended_2(panel, (("node", 1),), rows_blocks * block)
        pieces = extended.reshape(cols_here, -1, block)
        gathered = jnp.take(pieces, lookup, axis=1)
        product = jnp.einsum("nij,knj->nki", blocks, gathered, precision=precise)
        summed = jnp.einsum("rn,nki->kri", onehot, product, precision=precise).reshape(
            cols_here, width
        )
        return panel - summed / degree[None, :]

    def to_rows(panel):
        return lax.all_to_all(panel, "col", split_axis=1, concat_axis=0, tiled=True)

    basis = start
    results = []
    for step in range(ITERS):
        filtered = chebyshev(basis, operate)
        rows_now = to_rows(filtered)
        gram_part = jnp.dot(rows_now, rows_now.T, precision=precise) / nodes
        gram = lax.psum(gram_part, ("node", "col"))
        factor = jnp.linalg.cholesky(gram)
        rows_basis = jax.scipy.linalg.solve_triangular(factor, rows_now, lower=True)
        basis = lax.all_to_all(rows_basis, "col", split_axis=0, concat_axis=1, tiled=True)
        image = to_rows(operate(basis))
        part = jnp.dot(rows_basis, image.T, precision=precise) / nodes
        totals = lax.psum((part,), ("node", "col"))
        results.append(
            tuple(
                (
                    lax.dynamic_slice_in_dim(total, col_me * cols_here, cols_here, 0)
                    for total in totals
                )
            )[0]
        )
    return (basis, results[0], results[-1])


def solution(mesh):
    placed = (P("node", None, None), P("node", None), P("node", None), P("col", "node"))
    return jax.shard_map(
        body,
        mesh=mesh,
        in_specs=placed,
        out_specs=(P("col", "node"), P("col", None), P("col", None)),
        check_vma=False,
    )
```

profile of v0, /device:TPU:0, one launch (start us, length us, event | category | flops | bytes accessed | tf_op | source)
XLA Modules:
  0.0 1226.8 jit_solution(599584303518014007)
XLA Ops:
  14.1 9.6 reduce_sum.9
  23.9 20.3 %collective-permute-done = f32[32,6144]{1,0:T(8,128)S(1)} collective-permute-done((f32[32,6144]{1,0:T(8,128)}, f32[32,6144]{1,0:T(8,128)S(1)}, u32[]{:S(2)}, u32[]{:S(2)}) %collective-permute-start) | collective-permute-done | bytes 786464 | tf_op jit(solution)/shard_map/ppermute | solution.py:22
  51.4 33.4 %fusion.16 = f32[288,32,128]{2,1,0:T(8,128)S(1)} fusion(f32[288,128,128]{2,1,0:T(8,128)} %param.9, f32[288,32,128]{2,1,0:T(8,128)} %gather_fusion, pred[288]{0:T(512)(128)(4,1)S(1)} %get-tuple-element.25), kind=kOutput, calls=%fused_computation.25 | convolution fusion | flops 1813118976 | bytes 28311840 | tf_op jit(solution)/shard_map/nij,knj->nki/dot_general | solution.py:66
  84.8 4.8 fusion.34
  94.7 29.1 %collective-permute-done.2 = f32[32,6144]{1,0:T(8,128)S(1)} collective-permute-done((f32[32,6144]{1,0:T(8,128)S(1)}, f32[32,6144]{1,0:T(8,128)S(1)}, u32[]{:S(2)}, u32[]{:S(2)}) %collective-permute-start.2) | collective-permute-done | bytes 786464 | tf_op jit(solution)/shard_map/ppermute | solution.py:22
  130.7 33.1 %fusion.14 = f32[288,32,128]{2,1,0:T(8,128)S(1)} fusion(f32[288,128,128]{2,1,0:T(8,128)} %param.9, f32[288,32,128]{2,1,0:T(8,128)} %gather_fusion.1, pred[288]{0:T(512)(128)(4,1)S(1)} %get-tuple-element.25), kind=kOutput, calls=%fused_computation.23 | convolution fusion | flops 1813118976 | bytes 28311840 | tf_op jit(solution)/shard_map/nij,knj->nki/dot_general | solution.py:66
  163.8 4.8 fusion.32
  169.3 4.7 collective-permute-start.5
  174.1 28.7 %collective-permute-done.4 = f32[32,6144]{1,0:T(8,128)S(1)} collective-permute-done((f32[32,6144]{1,0:T(8,128)S(1)}, f32[32,6144]{1,0:T(8,128)S(1)}, u32[]{:S(2)}, u32[]{:S(2)}) %collective-permute-start.4) | collective-permute-done | bytes 786464 | tf_op jit(solution)/shard_map/ppermute | solution.py:22
  210.4 33.2 %fusion.12 = f32[288,32,128]{2,1,0:T(8,128)S(1)} fusion(f32[288,128,128]{2,1,0:T(8,128)} %param.9, f32[288,32,128]{2,1,0:T(8,128)} %gather_fusion.2, pred[288]{0:T(512)(128)(4,1)S(1)} %get-tuple-element.25), kind=kOutput, calls=%fused_computation.21 | convolution fusion | flops 1813118976 | bytes 28311840 | tf_op jit(solution)/shard_map/nij,knj->nki/dot_general | solution.py:66
  243.6 4.8 fusion.30
  249.2 4.7 collective-permute-start.7
  253.9 28.5 %collective-permute-done.6 = f32[32,6144]{1,0:T(8,128)S(1)} collective-permute-done((f32[32,6144]{1,0:T(8,128)S(1)}, f32[32,6144]{1,0:T(8,128)S(1)}, u32[]{:S(2)}, u32[]{:S(2)}) %collective-permute-start.6) | collective-permute-done | bytes 786464 | tf_op jit(solution)/shard_map/ppermute | solution.py:22
  282.4 4.0 collective-permute-done.7
  290.3 33.5 %fusion.10 = f32[288,32,128]{2,1,0:T(8,128)S(1)} fusion(f32[288,128,128]{2,1,0:T(8,128)} %param.9, f32[288,32,128]{2,1,0:T(8,128)} %gather_fusion.3, pred[288]{0:T(512)(128)(4,1)S(1)} %get-tuple-element.25), kind=kOutput, calls=%fused_computation.19 | convolution fusion | flops 1813118976 | bytes 28311840 | tf_op jit(solution)/shard_map/nij,knj->nki/dot_general | solution.py:66
  323.8 4.8 fusion.28
  329.1 14.2 %all_to_all.105 = f32[32,4,1536]{2,0,1:T(8,128)S(1)} all-to-all(f32[32,4,1536]{2,0,1:T(8,128)S(1)} %bitcast.287), channel_id=1, replica_groups=mesh['node'=8,'col'=4] {'col'}, dimensions={1} | all-to-all | bytes 1572864 | tf_op jit(solution)/shard_map/all_to_all | solution.py:73
  344.9 114.8 %all-reduce.5.cloned.1.call-done = f32[128,128]{0,1:T(8,128)} async-done(((f32[128,128]{0,1:T(8,128)}), f32[128,128]{0,1:T(8,128)}) %all-reduce.5.cloned.1.call-update) | async-done | bytes 65552 | tf_op jit(solution)/shard_map/psum | solution.py:81
  461.5 11.7 cholesky.44
  474.6 9.8 custom-call.6
  485.2 15.4 %all_to_all.106 = f32[4,32,1536]{2,1,0:T(8,128)S(1)} all-to-all(f32[4,32,1536]{2,1,0:T(8,128)S(1)} %bitcast.280), channel_id=1, replica_groups=mesh['node'=8,'col'=4] {'col'}, dimensions={0} | all-to-all | bytes 1572864 | tf_op jit(solution)/shard_map/all_to_all | solution.py:84
  501.5 4.2 collective-permute-start.9
  506.8 28.0 %collective-permute-done.8 = f32[32,6144]{1,0:T(8,128)} collective-permute-done((f32[32,6144]{1,0:T(8,128)S(1)}, f32[32,6144]{1,0:T(8,128)}, u32[]{:S(2)}, u32[]{:S(2)}) %collective-permute-start.8) | collective-permute-done | bytes 786464 | tf_op jit(solution)/shard_map/ppermute | solution.py:22
  541.3 33.2 %fusion.8 = f32[288,32,128]{2,1,0:T(8,128)S(1)} fusion(f32[288,128,128]{2,1,0:T(8,128)} %param.9, f32[288,32,128]{2,1,0:T(8,128)} %gather_fusion.4, pred[288]{0:T(512)(128)(4,1)S(1)} %get-tuple-element.25), kind=kOutput, calls=%fused_computation.17 | convolution fusion | flops 1813118976 | bytes 28311840 | tf_op jit(solution)/shard_map/nij,knj->nki/dot_general | solution.py:66
  574.5 4.8 fusion.26
  580.7 3.8 collective-permute-start.11
  584.5 28.6 %collective-permute-done.10 = f32[32,6144]{1,0:T(8,128)S(1)} collective-permute-done((f32[32,6144]{1,0:T(8,128)S(1)}, f32[32,6144]{1,0:T(8,128)S(1)}, u32[]{:S(2)}, u32[]{:S(2)}) %collective-permute-start.10) | collective-permute-done | bytes 786464 | tf_op jit(solution)/shard_map/ppermute | solution.py:22
  620.9 33.1 %fusion.6 = f32[288,32,128]{2,1,0:T(8,128)S(1)} fusion(f32[288,128,128]{2,1,0:T(8,128)} %param.9, f32[288,32,128]{2,1,0:T(8,128)} %gather_fusion.5, pred[288]{0:T(512)(128)(4,1)S(1)} %get-tuple-element.25), kind=kOutput, calls=%fused_computation.15 | convolution fusion | flops 1813118976 | bytes 28311840 | tf_op jit(solution)/shard_map/nij,knj->nki/dot_general | solution.py:66
  654.0 4.8 fusion.24
  659.5 4.7 collective-permute-start.13
  664.3 28.9 %collective-permute-done.12 = f32[32,6144]{1,0:T(8,128)S(1)} collective-permute-done((f32[32,6144]{1,0:T(8,128)S(1)}, f32[32,6144]{1,0:T(8,128)S(1)}, u32[]{:S(2)}, u32[]{:S(2)}) %collective-permute-start.12) | collective-permute-done | bytes 786464 | tf_op jit(solution)/shard_map/ppermute | solution.py:22
  699.4 33.2 %fusion.4 = f32[288,32,128]{2,1,0:T(8,128)S(1)} fusion(f32[288,128,128]{2,1,0:T(8,128)} %param.9, f32[288,32,128]{2,1,0:T(8,128)} %gather_fusion.6, pred[288]{0:T(512)(128)(4,1)S(1)} %get-tuple-element.25), kind=kOutput, calls=%fused_computation.13 | convolution fusion | flops 1813118976 | bytes 28311840 | tf_op jit(solution)/shard_map/nij,knj->nki/dot_general | solution.py:66
  732.6 4.8 fusion.22
  738.6 4.7 collective-permute-start.15
  745.8 25.4 %collective-permute-done.14 = f32[32,6144]{1,0:T(8,128)} collective-permute-done((f32[32,6144]{1,0:T(8,128)S(1)}, f32[32,6144]{1,0:T(8,128)}, u32[]{:S(2)}, u32[]{:S(2)}) %collective-permute-start.14) | collective-permute-done | bytes 786464 | tf_op jit(solution)/shard_map/ppermute | solution.py:22
  780.1 33.5 %fusion.2 = f32[288,32,128]{2,1,0:T(8,128)S(1)} fusion(f32[288,128,128]{2,1,0:T(8,128)} %param.9, f32[288,32,128]{2,1,0:T(8,128)} %gather_fusion.7, pred[288]{0:T(512)(128)(4,1)S(1)} %get-tuple-element.25), kind=kOutput, calls=%fused_computation.11 | convolution fusion | flops 1813118976 | bytes 28311840 | tf_op jit(solution)/shard_map/nij,knj->nki/dot_general | solution.py:66
  813.6 4.8 fusion.63
  823.1 14.7 %all_to_all.107 = f32[32,4,1536]{2,0,1:T(8,128)S(1)} all-to-all(f32[32,4,1536]{2,0,1:T(8,128)S(1)} %get-tuple-element.28), channel_id=1, replica_groups=mesh['node'=8,'col'=4] {'col'}, dimensions={1} | all-to-all | bytes 1572864 | tf_op jit(solution)/shard_map/all_to_all | solution.py:73
  839.2 115.3 %all-reduce.7.cloned.1.call-done = f32[128,128]{0,1:T(8,128)} async-done(((f32[128,128]{0,1:T(8,128)}), f32[128,128]{0,1:T(8,128)}) %all-reduce.7.cloned.1.call-update) | async-done | bytes 65552 | tf_op jit(solution)/shard_map/psum | solution.py:81
  956.3 11.7 cholesky.55
  969.3 9.8 custom-call.7
  980.0 15.4 %all_to_all.108 = f32[4,32,1536]{2,1,0:T(8,128)S(1)} all-to-all(f32[4,32,1536]{2,1,0:T(8,128)S(1)} %bitcast.281), channel_id=1, replica_groups=mesh['node'=8,'col'=4] {'col'}, dimensions={0} | all-to-all | bytes 1572864 | tf_op jit(solution)/shard_map/all_to_all | solution.py:84
  999.2 4.4 all-to-all-start.4
  1004.8 27.7 %collective-permute-done.17 = f32[32,6144]{1,0:T(8,128)} collective-permute-done((f32[32,6144]{1,0:T(8,128)}, f32[32,6144]{1,0:T(8,128)}, u32[]{:S(2)}, u32[]{:S(2)}) %collective-permute-start.17) | collective-permute-done | bytes 786464 | tf_op jit(solution)/shard_map/ppermute | solution.py:24
  1038.4 33.2 %fusion = f32[288,32,128]{2,1,0:T(8,128)S(1)} fusion(f32[288,128,128]{2,1,0:T(8,128)} %param.9, f32[288,32,128]{2,1,0:T(8,128)} %gather_fusion.8, pred[288]{0:T(512)(128)(4,1)S(1)} %get-tuple-element.25), kind=kOutput, calls=%fused_computation.9 | convolution fusion | flops 1813118976 | bytes 28311840 | tf_op jit(solution)/shard_map/nij,knj->nki/dot_general | solution.py:66
  1071.6 4.8 fusion.66
  1086.0 9.0 all-to-all-done.5
  1096.5 121.2 %all-reduce.9.cloned.1.call-done = (f32[128,128]{0,1:T(8,128)}, f32[128,128]{0,1:T(8,128)}) async-done(((f32[128,128]{0,1:T(8,128)}, f32[128,128]{0,1:T(8,128)}), (f32[128,128]{0,1:T(8,128)}, f32[128,128]{0,1:T(8,128)})) %all-reduce.9.cloned.1.call-update) | async-done | bytes 131088 | tf_op jit(solution)/shard_map/psum | solution.py:87
  (149 shorter events, 117.0 us)
Async XLA Ops:
  7.2 452.6 %all-reduce.5.cloned.1.call-start = ((), (), s32[]{:S(2)}) async-start(), calls=%async_computation.6 | async-start | bytes 131072 | tf_op jit(solution)/shard_map/psum | solution.py:81
  7.2 37.0 %collective-permute-start = (f32[32,6144]{1,0:T(8,128)}, f32[32,6144]{1,0:T(8,128)S(1)}, u32[]{:S(2)}, u32[]{:S(2)}) collective-permute-start(f32[32,6144]{1,0:T(8,128)} %param.12), channel_id=1, source_target_pairs={{0,4},{4,8},{8,12},{12,16},{16,20},{20,24},{24,28},{28,0},{1,5},{5... | collective-permute-start | bytes 2359304 | tf_op jit(solution)/shard_map/ppermute | solution.py:22
  10.2 36.2 %collective-permute-start.1 = (f32[32,6144]{1,0:T(8,128)}, f32[32,6144]{1,0:T(8,128)}, u32[]{:S(2)}, u32[]{:S(2)}) collective-permute-start(f32[32,6144]{1,0:T(8,128)} %param.12), channel_id=1, source_target_pairs={{4,0},{8,4},{12,8},{16,12},{20,16},{24,20},{28,24},{0,28},{5,1},{9... | collective-permute-start | bytes 2359304 | tf_op jit(solution)/shard_map/ppermute | solution.py:24
  14.0 9.6 copy-start.24
  14.0 32.4 %copy-start = (f32[32,6144]{1,0:T(8,128)S(1)}, f32[32,6144]{1,0:T(8,128)}, u32[]{:S(2)}) copy-start(f32[32,6144]{1,0:T(8,128)} %param.12) | copy-start | bytes 2359300
  44.2 0.9 copy-start.23
  89.6 34.3 %copy-start.7 = (f32[32,128,48]{1,2,0:T(8,128)}, f32[32,128,48]{1,2,0:T(8,128)S(1)}, u32[]{:S(2)}) copy-start(f32[32,128,48]{1,2,0:T(8,128)S(1)} %fusion.34) | copy-start | bytes 2359300
  90.0 33.9 %collective-permute-start.2 = (f32[32,6144]{1,0:T(8,128)S(1)}, f32[32,6144]{1,0:T(8,128)S(1)}, u32[]{:S(2)}, u32[]{:S(2)}) collective-permute-start(f32[32,6144]{1,0:T(8,128)S(1)} %broadcast_multiply_fusion.1), channel_id=1, source_target_pairs={{0,4},{4,8},{8,12},{12,16},{16,20},{20,24},{24,28},{28,0},{1,5},{5... | collective-permute-start | bytes 2359304 | tf_op jit(solution)/shard_map/ppermute | solution.py:22
  91.1 35.9 %collective-permute-start.3 = (f32[32,6144]{1,0:T(8,128)S(1)}, f32[32,6144]{1,0:T(8,128)S(1)}, u32[]{:S(2)}, u32[]{:S(2)}) collective-permute-start(f32[32,6144]{1,0:T(8,128)S(1)} %broadcast_multiply_fusion.1), channel_id=1, source_target_pairs={{4,0},{8,4},{12,8},{16,12},{20,16},{24,20},{28,24},{0,28},{5,1},{9... | collective-permute-start | bytes 2359304 | tf_op jit(solution)/shard_map/ppermute | solution.py:24
  163.8 4.8 copy-start.8
  169.3 37.3 %copy-start.10 = (f32[32,6144]{1,0:T(8,128)}, f32[32,6144]{1,0:T(8,128)S(1)}, u32[]{:S(2)}) copy-start(f32[32,6144]{1,0:T(8,128)S(1)} %fusion.90) | copy-start | bytes 2359300
  169.3 33.5 %collective-permute-start.4 = (f32[32,6144]{1,0:T(8,128)S(1)}, f32[32,6144]{1,0:T(8,128)S(1)}, u32[]{:S(2)}, u32[]{:S(2)}) collective-permute-start(f32[32,6144]{1,0:T(8,128)S(1)} %fusion.90), channel_id=1, source_target_pairs={{0,4},{4,8},{8,12},{12,16},{16,20},{20,24},{24,28},{28,0},{1,5},{5... | collective-permute-start | bytes 2359304 | tf_op jit(solution)/shard_map/ppermute | solution.py:22
  169.3 37.2 %collective-permute-start.5 = (f32[32,6144]{1,0:T(8,128)S(1)}, f32[32,6144]{1,0:T(8,128)S(1)}, u32[]{:S(2)}, u32[]{:S(2)}) collective-permute-start(f32[32,6144]{1,0:T(8,128)S(1)} %fusion.90), channel_id=1, source_target_pairs={{4,0},{8,4},{12,8},{16,12},{20,16},{24,20},{28,24},{0,28},{5,1},{9... | collective-permute-start | bytes 2359304 | tf_op jit(solution)/shard_map/ppermute | solution.py:24
  243.6 4.8 copy-start.9
  243.6 4.8 copy-start.11
  249.1 37.3 %copy-start.19 = (f32[32,6144]{1,0:T(8,128)}, f32[32,6144]{1,0:T(8,128)S(1)}, u32[]{:S(2)}) copy-start(f32[32,6144]{1,0:T(8,128)S(1)} %fusion.86) | copy-start | bytes 2359300
  249.1 33.3 %collective-permute-start.6 = (f32[32,6144]{1,0:T(8,128)S(1)}, f32[32,6144]{1,0:T(8,128)S(1)}, u32[]{:S(2)}, u32[]{:S(2)}) collective-permute-start(f32[32,6144]{1,0:T(8,128)S(1)} %fusion.86), channel_id=1, source_target_pairs={{0,4},{4,8},{8,12},{12,16},{16,20},{20,24},{24,28},{28,0},{1,5},{5... | collective-permute-start | bytes 2359304 | tf_op jit(solution)/shard_map/ppermute | solution.py:22
  249.2 37.2 %collective-permute-start.7 = (f32[32,6144]{1,0:T(8,128)S(1)}, f32[32,6144]{1,0:T(8,128)S(1)}, u32[]{:S(2)}, u32[]{:S(2)}) collective-permute-start(f32[32,6144]{1,0:T(8,128)S(1)} %fusion.86), channel_id=1, source_target_pairs={{4,0},{8,4},{12,8},{16,12},{20,16},{24,20},{28,24},{0,28},{5,1},{9... | collective-permute-start | bytes 2359304 | tf_op jit(solution)/shard_map/ppermute | solution.py:24
  323.8 4.8 copy-start.12
  323.8 4.8 copy-start.20
  344.7 609.8 %all-reduce.7.cloned.1.call-start = ((), (), s32[]{:S(2)}) async-start(), calls=%async_computation.7 | async-start | bytes 131072 | tf_op jit(solution)/shard_map/psum | solution.py:81
  485.2 15.5 %copy-start.15 = (f32[128,1536]{1,0:T(8,128)}, f32[128,1536]{1,0:T(8,128)S(1)}, u32[]{:S(2)}) copy-start(f32[128,1536]{1,0:T(8,128)S(1)} %fusion.123) | copy-start | bytes 2359300
  500.6 5.0 copy-start.1
  500.7 37.0 %copy-start.3 = (f32[4,4,8,1536]{3,2,0,1:T(8,128)}, f32[4,4,8,1536]{3,2,0,1:T(8,128)S(1)}, u32[]{:S(2)}) copy-start(f32[4,4,8,1536]{3,2,0,1:T(8,128)S(1)} %copy.168) | copy-start | bytes 2359300
  500.7 34.1 %collective-permute-start.8 = (f32[32,6144]{1,0:T(8,128)S(1)}, f32[32,6144]{1,0:T(8,128)}, u32[]{:S(2)}, u32[]{:S(2)}) collective-permute-start(f32[32,6144]{1,0:T(8,128)S(1)} %bitcast.269), channel_id=1, source_target_pairs={{0,4},{4,8},{8,12},{12,16},{16,20},{20,24},{24,28},{28,0},{1,5},{5... | collective-permute-start | bytes 2359304 | tf_op jit(solution)/shard_map/ppermute | solution.py:22
  501.5 36.2 %collective-permute-start.9 = (f32[32,6144]{1,0:T(8,128)S(1)}, f32[32,6144]{1,0:T(8,128)S(1)}, u32[]{:S(2)}, u32[]{:S(2)}) collective-permute-start(f32[32,6144]{1,0:T(8,128)S(1)} %bitcast.270), channel_id=1, source_target_pairs={{4,0},{8,4},{12,8},{16,12},{20,16},{24,20},{28,24},{0,28},{5,1},{9... | collective-permute-start | bytes 2359304 | tf_op jit(solution)/shard_map/ppermute | solution.py:24
  574.5 4.8 copy-start.4
  579.7 33.3 %collective-permute-start.10 = (f32[32,6144]{1,0:T(8,128)S(1)}, f32[32,6144]{1,0:T(8,128)S(1)}, u32[]{:S(2)}, u32[]{:S(2)}) collective-permute-start(f32[32,6144]{1,0:T(8,128)S(1)} %broadcast_multiply_fusion), channel_id=1, source_target_pairs={{0,4},{4,8},{8,12},{12,16},{16,20},{20,24},{24,28},{28,0},{1,5},{5... | collective-permute-start | bytes 2359304 | tf_op jit(solution)/shard_map/ppermute | solution.py:22
  580.7 36.1 %collective-permute-start.11 = (f32[32,6144]{1,0:T(8,128)S(1)}, f32[32,6144]{1,0:T(8,128)S(1)}, u32[]{:S(2)}, u32[]{:S(2)}) collective-permute-start(f32[32,6144]{1,0:T(8,128)S(1)} %broadcast_multiply_fusion), channel_id=1, source_target_pairs={{4,0},{8,4},{12,8},{16,12},{20,16},{24,20},{28,24},{0,28},{5,1},{9... | collective-permute-start | bytes 2359304 | tf_op jit(solution)/shard_map/ppermute | solution.py:24
  654.0 4.8 copy-start.5
  658.8 34.4 %copy-start.13 = (f32[32,128,48]{1,2,0:T(8,128)}, f32[32,128,48]{1,2,0:T(8,128)S(1)}, u32[]{:S(2)}) copy-start(f32[32,128,48]{1,2,0:T(8,128)S(1)} %fusion.24) | copy-start | bytes 2359300
  659.5 33.6 %collective-permute-start.12 = (f32[32,6144]{1,0:T(8,128)S(1)}, f32[32,6144]{1,0:T(8,128)S(1)}, u32[]{:S(2)}, u32[]{:S(2)}) collective-permute-start(f32[32,6144]{1,0:T(8,128)S(1)} %fusion.76), channel_id=1, source_target_pairs={{0,4},{4,8},{8,12},{12,16},{16,20},{20,24},{24,28},{28,0},{1,5},{5... | collective-permute-start | bytes 2359304 | tf_op jit(solution)/shard_map/ppermute | solution.py:22
  659.5 36.0 %collective-permute-start.13 = (f32[32,6144]{1,0:T(8,128)S(1)}, f32[32,6144]{1,0:T(8,128)S(1)}, u32[]{:S(2)}, u32[]{:S(2)}) collective-permute-start(f32[32,6144]{1,0:T(8,128)S(1)} %fusion.76), channel_id=1, source_target_pairs={{4,0},{8,4},{12,8},{16,12},{20,16},{24,20},{28,24},{0,28},{5,1},{9... | collective-permute-start | bytes 2359304 | tf_op jit(solution)/shard_map/ppermute | solution.py:24
  732.6 4.8 copy-start.6
  732.6 4.8 copy-start.14
  738.5 32.8 %copy-start.21 = (f32[32,6144]{1,0:T(8,128)}, f32[32,6144]{1,0:T(8,128)S(1)}, u32[]{:S(2)}) copy-start(f32[32,6144]{1,0:T(8,128)S(1)} %fusion.72) | copy-start | bytes 2359300
  738.5 32.8 %collective-permute-start.14 = (f32[32,6144]{1,0:T(8,128)S(1)}, f32[32,6144]{1,0:T(8,128)}, u32[]{:S(2)}, u32[]{:S(2)}) collective-permute-start(f32[32,6144]{1,0:T(8,128)S(1)} %fusion.72), channel_id=1, source_target_pairs={{0,4},{4,8},{8,12},{12,16},{16,20},{20,24},{24,28},{28,0},{1,5},{5... | collective-permute-start | bytes 2359304 | tf_op jit(solution)/shard_map/ppermute | solution.py:22
  738.6 36.0 %collective-permute-start.15 = (f32[32,6144]{1,0:T(8,128)S(1)}, f32[32,6144]{1,0:T(8,128)}, u32[]{:S(2)}, u32[]{:S(2)}) collective-permute-start(f32[32,6144]{1,0:T(8,128)S(1)} %fusion.72), channel_id=1, source_target_pairs={{4,0},{8,4},{12,8},{16,12},{20,16},{24,20},{28,24},{0,28},{5,1},{9... | collective-permute-start | bytes 2359304 | tf_op jit(solution)/shard_map/ppermute | solution.py:24
  813.6 5.9 copy-start.2
  813.6 5.9 copy-start.22
  980.0 24.7 %copy-start.17 = (f32[128,1536]{1,0:T(8,128)}, f32[128,1536]{1,0:T(8,128)S(1)}, u32[]{:S(2)}) copy-start(f32[128,1536]{1,0:T(8,128)S(1)} %fusion.120) | copy-start | bytes 2359300
  996.3 36.1 %collective-permute-start.17 = (f32[32,6144]{1,0:T(8,128)}, f32[32,6144]{1,0:T(8,128)}, u32[]{:S(2)}, u32[]{:S(2)}) collective-permute-start(f32[32,6144]{1,0:T(8,128)} %bitcast.69), channel_id=1, source_target_pairs={{4,0},{8,4},{12,8},{16,12},{20,16},{24,20},{28,24},{0,28},{5,1},{9... | collective-permute-start | bytes 2359304 | tf_op jit(solution)/shard_map/ppermute | solution.py:24
  999.2 34.4 %collective-permute-start.16 = (f32[32,6144]{1,0:T(8,128)}, f32[32,6144]{1,0:T(8,128)}, u32[]{:S(2)}, u32[]{:S(2)}) collective-permute-start(f32[32,6144]{1,0:T(8,128)} %bitcast.69), channel_id=1, source_target_pairs={{0,4},{4,8},{8,12},{12,16},{16,20},{20,24},{24,28},{28,0},{1,5},{5... | collective-permute-start | bytes 2359304 | tf_op jit(solution)/shard_map/ppermute | solution.py:22
  999.2 80.7 %all-to-all-start.4 = ((f32[32,4,1536]{2,0,1:T(8,128)}), f32[32,4,1536]{2,0,1:T(8,128)}, u32[]{:S(2)}, u32[]{:S(2)}) async-start(f32[32,4,1536]{2,0,1:T(8,128)} %get-tuple-element.27), calls=%async_computation.4 | async-start | bytes 1572864 | tf_op jit(solution)/shard_map/all_to_all | solution.py:73
  1071.6 11.9 copy-start.16
  1076.4 18.6 %copy-start.18 = (f32[128,1536]{1,0:T(8,128)S(1)}, f32[128,1536]{1,0:T(8,128)}, u32[]{:S(2)}) copy-start(f32[128,1536]{1,0:T(8,128)} %copy-done.17) | copy-start | bytes 2359300
  1079.9 15.1 %all-to-all-start.5 = ((f32[32,4,1536]{2,0,1:T(8,128)}), f32[32,4,1536]{2,0,1:T(8,128)S(1)}, u32[]{:S(2)}, u32[]{:S(2)}) async-start(f32[32,4,1536]{2,0,1:T(8,128)} %fusion.93), calls=%async_computation.5 | async-start | bytes 1572864 | tf_op jit(solution)/shard_map/all_to_all | solution.py:73
  1083.4 134.2 %all-reduce.9.cloned.1.call-start = ((), (), s32[]{:S(2)}) async-start(), calls=%async_computation.8 | async-start | bytes 262144 | tf_op jit(solution)/shard_map/psum | solution.py:87
Sparse Core Ops, SparseCore 0:
  344.8 114.8 all-reduce.4
  839.3 115.1 all-reduce.6
  1096.6 120.9 all-reduce.8
where the time goes:
time: 1230 us
  waiting for transfers between devices  629 us (51%)
  matrix products  351 us (29%)
  other arithmetic  73.4 us (6%)
  blocking collectives  59.6 us (5%)
  starting transfers between devices  50.8 us (4%)
  local copies, waits for them, and re-layouts  48.3 us (4%)
  between operations  14.8 us (1%)
    dot_general x9, matrix products, operate(): product = jnp.einsum('nij,knj->nki', blocks, gathered, precision=precise)  299 us
    psum x2, waiting for transfers between devices, body(): gram = lax.psum(gram_part, ('node', 'col'))  230 us
    ppermute x9, waiting for transfers between devices, extended_2(): lax.ppermute(tail, axis, [(i, (i + 1) % count) for i in range(count)])  218 us
    psum x1, waiting for transfers between devices, body(): totals = lax.psum((part,), ('node', 'col'))  121 us
    ppermute x9, waiting for transfers between devices, extended_2(): lax.ppermute(head, axis, [((i + 1) % count, i) for i in range(count)])  51 us
    dot_general x9, matrix products, operate(): jnp.einsum('rn,nki->kri', onehot, product, precision=precise)  42.9 us
    ppermute x9, starting transfers between devices, extended_2(): lax.ppermute(head, axis, [((i + 1) % count, i) for i in range(count)])  36.4 us
    gather x9, local copies, waits for them, and re-layouts, operate(): gathered = jnp.take(pieces, lookup, axis=1)  31.3 us
  transfers between devices with their start and end apart: 23, of which 21 were waited for; matrix products, arithmetic and copies ran while one was open for 5% of the time, Pallas kernels for 0%

commit v1 on v0

v1 whole, which is shorter than its diff:
```python
import functools
import jax
import jax.numpy as jnp
from jax import lax
from jax.experimental import pallas as pl
from jax.experimental.pallas import tpu as pltpu
from jax.sharding import PartitionSpec as P

DEGREE = 4
UNROLL = 16
F32, BF16, I32 = jnp.float32, jnp.bfloat16, jnp.int32
precise = lax.Precision.HIGHEST
center = 1.025
half_width = 0.975
MIB = 1 << 20
IN_VMEM = pl.BlockSpec(memory_space=pltpu.VMEM)
IN_SMEM = pl.BlockSpec(memory_space=pltpu.SMEM)


def prep_kernel(UN, R, half, groups, own_ref, col_ref, me_ref, blk_ref, w_ref, deg_ref, src_ref, row_ref, num_ref, pos_ref, cnt_ref):
    chunk = blk_ref.shape[0]
    total = own_ref.shape[1]
    step = pl.program_id(0)

    @pl.when(step == 0)
    def _():
        me = me_ref[0]
        odd = me % 2
        for r in range(R):
            cnt_ref[r] = 0
        def count(b, c):
            r = own_ref[0, b]
            cnt_ref[r] = cnt_ref[r] + 1
            return c
        lax.fori_loop(0, total, count, 0)
        zero = jnp.zeros(w_ref.shape[1:], BF16)
        def slots(r, at):
            n = cnt_ref[r]
            pairs = (n + 1) // 2
            cnt_ref[r] = 2 * at
            row_at = jnp.where(odd == 1, r, jnp.where(r >= half, r - half, r + half))
            def put(p, c):
                row_ref[p] = row_at
                return c
            lax.fori_loop(at, at + pairs, put, 0)
            @pl.when(n % 2 == 1)
            def _():
                w_ref[2 * at + n] = zero
                src_ref[2 * at + n] = 0
            return at + pairs
        used = lax.fori_loop(0, R, slots, 0)
        upto = (used + UN - 1) // UN * UN
        def fill(p, c):
            row_ref[p] = R
            for s in range(2):
                w_ref[2 * p + s] = zero
                src_ref[2 * p + s] = 0
            return c
        lax.fori_loop(used, upto, fill, 0)
        num_ref[0] = upto // UN
        def place(b, c):
            r = own_ref[0, b]
            at = cnt_ref[r]
            cnt_ref[r] = at + 1
            pos_ref[b] = at
            k = col_ref[0, b]
            owner = k // R
            local = k - owner * R
            upper = (local >= half).astype(I32)
            near = local - half * upper
            own_at = near + half * jnp.where(odd == 1, upper, 1 - upper)
            halo_at = 2 * half + near + half * jnp.where(odd == 1, 1 - upper, upper)
            src_ref[at] = jnp.where(owner == me, own_at, halo_at)
            return c
        lax.fori_loop(0, total, place, 0)
        deg_ref[...] = jnp.zeros(deg_ref.shape, F32)

    for c in range(chunk):
        b = step * chunk + c
        at = pos_ref[b]
        r = row_ref[at // 2]
        t = blk_ref[c].T
        hi = t.astype(BF16)
        lo = (t - hi.astype(F32)).astype(BF16)
        w_ref[at, :, :t.shape[1]] = hi
        w_ref[at, :, t.shape[1]:] = lo
        deg_ref[r] = deg_ref[r] + jnp.sum(t, axis=0, keepdims=True)

    @pl.when(step == pl.num_programs(0) - 1)
    def _():
        deg_ref[...] = 1.0 / deg_ref[...]

def prep(own, col, me, blocks, R, groups, UN, chunk=24):
    total, n, _ = blocks.shape
    half = R // 2
    slots = total + R
    slots = (slots // 2 + UN - 1) // UN * UN * 2
    return pl.pallas_call(
        functools.partial(prep_kernel, UN, R, half, groups),
        grid=(total // chunk,),
        in_specs=[IN_SMEM, IN_SMEM, IN_SMEM, pl.BlockSpec((chunk, n, n), lambda i: (i, 0, 0))],
        out_specs=[IN_VMEM, IN_VMEM, IN_SMEM, IN_SMEM, IN_SMEM],
        out_shape=[pltpu.VMEM((slots, n, 2 * n), BF16),
                   jax.ShapeDtypeStruct((R, 1, n), F32),
                   jax.ShapeDtypeStruct((slots,), I32),
                   jax.ShapeDtypeStruct((slots // 2,), I32),
                   jax.ShapeDtypeStruct((1,), I32)],
        scratch_shapes=[pltpu.SMEM((total,), I32), pltpu.SMEM((R,), I32)],
        compiler_params=pltpu.CompilerParams(vmem_limit_bytes=32 * MIB),
        name="prep",
    )(own, col, me, blocks)

def apply_kernel(UN, mode, src_ref, row_ref, num_ref, w_ref, inv_ref, pe_ref, po_ref, he_ref, ho_ref, *rest):
    if mode == "first" or mode == "plain":
        ne_ref, no_ref, sp_ref, acc_ref = rest
    else:
        qe_ref, qo_ref, ne_ref, no_ref, sp_ref, acc_ref = rest
    half, kk, n = pe_ref.shape
    for i, ref in enumerate((pe_ref, po_ref, he_ref, ho_ref)):
        v = ref[...]
        hi = v.astype(BF16)
        sp_ref[i * half:(i + 1) * half, :kk] = hi
        sp_ref[i * half:(i + 1) * half, kk:] = (v - hi.astype(F32)).astype(BF16)
    acc_ref[...] = jnp.zeros(acc_ref.shape, F32)

    def group(g, c):
        for u in range(UN):
            p = g * UN + u
            lhs = jnp.concatenate([sp_ref[src_ref[2 * p]], sp_ref[src_ref[2 * p + 1]]], axis=1)
            w = w_ref[pl.ds(2 * p, 2)].reshape(2 * n, 2 * n)
            y = jnp.dot(lhs, w, preferred_element_type=F32)
            r = row_ref[p]
            acc_ref[r] = acc_ref[r] + ((y[:kk, :n] + y[kk:, :n]) + (y[:kk, n:] + y[kk:, n:]))
        return c
    lax.fori_loop(0, num_ref[0], group, 0)
    for i, (p_ref, n_ref) in enumerate(((pe_ref, ne_ref), (po_ref, no_ref))):
        now = p_ref[...]
        image = now - acc_ref[i * half:(i + 1) * half] * inv_ref[i * half:(i + 1) * half]
        if mode == "plain":
            n_ref[...] = image
        elif mode == "first":
            n_ref[...] = (image - center * now) * (1.0 / half_width)
        else:
            q_ref = (qe_ref, qo_ref)[i]
            n_ref[...] = (image - center * now) * (2.0 / half_width) - q_ref[...]

def apply(UN, mode, meta, w, inv, *panels):
    half, kk, n = panels[0].shape
    out = jax.ShapeDtypeStruct((half, kk, n), F32)
    return pl.pallas_call(
        functools.partial(apply_kernel, UN, mode),
        in_specs=[IN_SMEM] * 3 + [IN_VMEM] * (2 + len(panels)),
        out_specs=[IN_VMEM, IN_VMEM],
        out_shape=[out, out],
        scratch_shapes=[pltpu.VMEM((4 * half, 2 * kk, n), BF16), pltpu.VMEM((2 * half + 1, kk, n), F32)],
        compiler_params=pltpu.CompilerParams(vmem_limit_bytes=16 * MIB),
        cost_estimate=pl.CostEstimate(flops=2 * 4 * w.shape[0] * n * n * kk, bytes_accessed=w.size * 2, transcendentals=0),
        name="apply_" + mode,
    )(*meta, w, inv, *panels)


def nt(a, b):
    return lax.dot_general(
        a, b, (((1,), (1,)), ((), ())), precision=precise, preferred_element_type=F32
    )


def nn(a, b):
    return jnp.dot(a, b, precision=precise, preferred_element_type=F32)


def rows_at(b, *refs):
    return jnp.concatenate([ref[c, b] for c in range(refs[0].shape[0]) for ref in refs], axis=0)


def gram_kernel(fa_ref, fb_ref, za_ref, zb_ref, g_ref, k_ref):
    g_ref[...] = jnp.zeros(g_ref.shape, F32)
    k_ref[...] = jnp.zeros(k_ref.shape, F32)

    def one(b, c):
        f = rows_at(b, fa_ref, fb_ref)
        z = rows_at(b, za_ref, zb_ref)
        g_ref[...] = g_ref[...] + nt(f, f)
        k_ref[...] = k_ref[...] + nt(f, z)
        return c

    lax.fori_loop(0, fa_ref.shape[1], one, 0)


def turn_kernel(inv_ref, fa_ref, fb_ref, f_ref, g_ref):
    g_ref[...] = jnp.zeros(g_ref.shape, F32)

    def one(b, c):
        f = nn(inv_ref[...], rows_at(b, fa_ref, fb_ref))
        f_ref[b] = f
        g_ref[...] = g_ref[...] + nt(f, f)
        return c

    lax.fori_loop(0, fa_ref.shape[1], one, 0)


def cross_kernel(inv_ref, f_ref, za_ref, zb_ref, k_ref):
    k_ref[...] = jnp.zeros(k_ref.shape, F32)

    def one(b, c):
        z = nn(inv_ref[...], rows_at(b, za_ref, zb_ref))
        k_ref[...] = k_ref[...] + nt(f_ref[b], z)
        return c

    lax.fori_loop(0, za_ref.shape[1], one, 0)


def basis_kernel(inv_ref, f_ref, q_ref):
    count, _, each, _ = q_ref.shape

    def one(b, c):
        q = nn(inv_ref[...], f_ref[b])
        for i in range(count):
            q_ref[i, b] = q[i * each:(i + 1) * each]
        return c

    lax.fori_loop(0, f_ref.shape[0], one, 0)


def proj_kernel(nodes, inv_ref, k_ref, g_ref, out_ref):
    image = (half_width * k_ref[...] + center * g_ref[...]) / nodes
    out_ref[...] = nt(nn(inv_ref[...], image), inv_ref[...])


def call(kernel, name, outs, *args):
    return pl.pallas_call(
        kernel,
        in_specs=[IN_VMEM] * len(args),
        out_specs=[IN_VMEM] * len(outs),
        out_shape=[jax.ShapeDtypeStruct(o, F32) for o in outs],
        compiler_params=pltpu.CompilerParams(vmem_limit_bytes=16 * MIB),
        name=name,
    )(*args)


def exchange(pair):
    count = lax.axis_size("node")
    even = [(i, i ^ 1) for i in range(count)]
    odd = [(i, (i - 1 if i % 2 == 0 else i + 1) % count) for i in range(count)]
    return lax.ppermute(pair[0], "node", even), lax.ppermute(pair[1], "node", odd)


def total(value):
    for axis in ("col", "node"):
        count = lax.axis_size(axis)
        hop = 1
        while hop < count:
            value = value + lax.ppermute(value, axis, [(i, i ^ hop) for i in range(count)])
            hop *= 2
    return value


def to_rows(pair):
    count = lax.axis_size("col")
    whole = jnp.concatenate(pair, axis=0)
    slots, each, n = whole.shape
    return lax.all_to_all(
        whole.reshape(count, slots // count, each, n), "col", split_axis=0, concat_axis=0, tiled=True
    )


def inverse_factor(gram, nodes):
    factor = jnp.linalg.cholesky(gram / nodes)
    return jax.scipy.linalg.solve_triangular(
        factor, jnp.eye(gram.shape[0], dtype=F32), lower=True
    )


def body(blocks, owner_row, block_col, start):
    cols_here, width = start.shape
    block = blocks.shape[1]
    slots = width // block
    half = slots // 2
    count = lax.axis_size("col")
    groups = lax.axis_size("node")
    nodes = width * groups
    vecs = cols_here * count
    each = cols_here // 2
    me = lax.axis_index("node").astype(I32)
    odd = me % 2 == 1

    tiles = start.reshape(2, each, slots, block).transpose(0, 2, 1, 3)
    low, high = tiles[:, :half], tiles[:, half:]
    left = jnp.where(odd, low, high)
    right = jnp.where(odd, high, low)
    chains = [(left[i], right[i]) for i in range(2)]

    w, inv, src, row, num = prep(owner_row, block_col, me.reshape(1), blocks, slots, groups, UNROLL)
    meta = (src, row, num)

    def first(pair):
        return tuple(apply(UNROLL, "first", meta, w, inv, *pair, *exchange(pair)))

    def later(pair, previous):
        return tuple(apply(UNROLL, "cheb", meta, w, inv, *pair, *exchange(pair), *previous))

    before = chains
    now = [first(c) for c in before]
    for _ in range(DEGREE - 1):
        before, now = now, [later(c, p) for c, p in zip(now, before)]
    filtered = now
    rows = [to_rows(c) for c in filtered]
    before, now = now, [first(c) for c in now]
    image = [to_rows(c) for c in now]
    square = (vecs, vecs)
    gram, cross = call(gram_kernel, "gram", [square] * 2, *rows, *image)
    gram, cross = total(jnp.stack([gram, cross]))
    for _ in range(DEGREE - 1):
        before, now = now, [later(c, p) for c, p in zip(now, before)]
    inverse = inverse_factor(gram, nodes)
    (projected_first,) = call(functools.partial(proj_kernel, nodes), "proj", [square], inverse, cross, gram)

    rows = [to_rows(c) for c in now]
    turned, gram = call(
        turn_kernel, "turn", [(slots // count, vecs, block), square], inverse, *rows
    )
    gram = total(gram)
    last = [first(c) for c in now]
    image = [to_rows(c) for c in last]
    (cross,) = call(cross_kernel, "cross", [square], inverse, turned, *image)
    cross = total(cross)
    inverse = inverse_factor(gram, nodes)
    (q,) = call(basis_kernel, "basis", [(count, slots // count, cols_here, block)], inverse, turned)
    q = lax.all_to_all(q, "col", split_axis=0, concat_axis=0, tiled=True)
    q = q.reshape(slots, cols_here, block)
    low = jnp.where(odd, q[:half], q[half:])
    high = jnp.where(odd, q[half:], q[:half])
    basis = jnp.concatenate([low, high], axis=0).transpose(1, 0, 2).reshape(cols_here, width)
    (projected,) = call(functools.partial(proj_kernel, nodes), "proj", [square], inverse, cross, gram)

    def mine(value):
        at = lax.axis_index("col") * cols_here
        return lax.dynamic_slice_in_dim(value, at, cols_here, 0)

    return basis, mine(projected_first), mine(projected)


def solution(mesh):
    placed = (P("node", None, None), P("node", None), P("node", None), P("col", "node"))
    return jax.shard_map(
        body,
        mesh=mesh,
        in_specs=placed,
        out_specs=(P("col", "node"), P("col", None), P("col", None)),
        check_vma=False,
    )
```

time: 1230 us -> 407 us (0.33)
  waiting for transfers between devices: 629 us -> 43.8 us
  matrix products: 351 us -> 0.57 us
  Pallas kernels: 0 us -> 160 us
  blocking collectives: 59.6 us -> 0 us
  starting transfers between devices: 50.8 us -> 103 us
  other arithmetic: 73.4 us -> 53.2 us
  between operations: 14.8 us -> 1.39 us
    psum x3 -> x0, waiting for transfers between devices: 351 us -> none  [the longest x2 230 us: body(): gram = lax.psum(gram_part, ('node', 'col'))]
    dot_general x23 -> x0, matrix products: 349 us -> none  [the longest x9 299 us: operate(): product = jnp.einsum('nij,knj->nki', blocks, gathered, precision=precise)]
    ppermute x18 -> x51, waiting for transfers between devices: 269 us -> 42.1 us  [the longest x15 37.8 us: total(): lax.ppermute(value, axis, [(i, i ^ hop) for i in range(count)])]
    pallas_call x0 -> x25, Pallas kernels: none -> 160 us  [the longest x18 114 us: apply(): pl.pallas_call(functools.partial(apply_kernel, UN, mode), in_specs=[IN_SM...]
    all_to_all x4 -> x0, blocking collectives: 59.6 us -> none  [the longest x2 30.8 us: body(): lax.all_to_all(rows_basis, 'col', split_axis=0, concat_axis=1, tiled=True)]
    unnamed x52 -> x25, local copies, waits for them, and re-layouts: 2.37 us -> 41.3 us
    gather x9 -> x0, local copies, waits for them, and re-layouts: 31.3 us -> none  [operate(): gathered = jnp.take(pieces, lookup, axis=1)]
    ppermute x18 -> x51, starting transfers between devices: 42.6 us -> 71.6 us  [the longest x18 46 us: exchange(): lax.ppermute(pair[1], 'node', odd)]
  transfers between devices with their start and end apart: 23 -> 60, of which waited for: 21 -> 10; matrix products, arithmetic and copies ran while one was open for 5% -> 13% of each run, Pallas kernels for 0% -> 40%
where the time goes in v1:
time: 407 us; the launch traced here: 405 us
  Pallas kernels  160 us (39%)
  starting transfers between devices  103 us (25%)
  other arithmetic  53.2 us (13%)
  waiting for transfers between devices  43.8 us (11%)
  local copies, waits for them, and re-layouts  43.1 us (11%)
    pallas_call x18, Pallas kernels, apply(): pl.pallas_call(functools.partial(apply_kernel, UN, mode), in_specs=[IN_SM...  114 us
    ppermute x18, starting transfers between devices, exchange(): lax.ppermute(pair[1], 'node', odd)  46 us
    unnamed x25, local copies, waits for them, and re-layouts  41.3 us
    ppermute x15, waiting for transfers between devices, total(): lax.ppermute(value, axis, [(i, i ^ hop) for i in range(count)])  37.8 us
    all_to_all x8, starting transfers between devices, to_rows(): lax.all_to_all(whole.reshape(count, slots // count, each, n), 'col', spli...  27.9 us
    another operation x6, other arithmetic, inverse_factor(): factor = jnp.linalg.cholesky(gram / nodes)  24.8 us
    pallas_call x1, Pallas kernels, prep(): pl.pallas_call(functools.partial(prep_kernel, UN, R, half, groups), grid=...  24.6 us
    pallas_call x6, Pallas kernels, call(): pl.pallas_call(kernel, in_specs=[IN_VMEM] * len(args), out_specs=[IN_VMEM...  21.6 us
  transfers between devices with their start and end apart: 60, of which 10 were waited for; matrix products, arithmetic and copies ran while one was open for 13% of the time, Pallas kernels for 40%

profile of v1, /device:TPU:0, one launch (start us, length us, event | category | flops | bytes accessed | tf_op | source)
XLA Modules:
  0.0 405.3 jit_solution(12586965357611918308)
XLA Ops:
  2.3 6.1 %collective-permute-start.1 = (f32[24,16,128]{2,1,0:T(8,128)S(1)}, f32[24,16,128]{2,1,0:T(8,128)S(1)}, u32[]{:S(2)}, u32[]{:S(2)}) collective-permute-start(f32[24,16,128]{2,1,0:T(8,128)S(1)} %get-tuple-element.102.po_ref.rest_1_), channel_id=1, source_target_pairs={{0,28},{4,8},{8,4},{12,16},{16,12},{20,24},{24,20},{28,0},{1,29},{... | collective-permute-start | bytes 589832 | tf_op jit(solution)/shard_map/ppermute | solution.py:245
  10.5 24.6 %prep.1 = (bf16[352,128,256]{2,1,0:T(8,128)(2,1)S(1)}, f32[48,1,128]{2,1,0:T(1,128)}, s32[352]{0:T(512)}, s32[176]{0:T(256)}, s32[1]{0:T(128)}) custom-call(s32[1,288]{1,0:T(1,128)} %own_ref.1, s32[1,288]{1,0:T(1,128)} %col_ref.1, s32[1]{0:T(128)} %bitcast.me_ref, f32[288,128,128]{2,1,0:T(8,128)} %blk_ref.1), custom_call_target="tpu_custom_call" | custom-call | tf_op jit(solution)/shard_map/prep/pallas_call | solution.py:98
  37.3 6.3 %apply_first.6 = (f32[24,16,128]{2,1,0:T(8,128)S(1)}, f32[24,16,128]{2,1,0:T(8,128)S(1)}) custom-call(s32[352]{0:T(512)S(1)} %copy-done.8, s32[176]{0:T(256)S(1)} %copy-done.10, s32[1]{0:T(128)} %get-tuple-element.52.num_ref, bf16[352,128,256]{2,1,0:T(8,128)(2,1)S(1)} %get-tuple-element.53.w_ref, f32[48,1,128]{2,1,0:T(1,128)S(1)} %copy-done.6, ...), custom_call_target="tpu_custom_call" | custom-call | flops 738197504 | bytes 23068672 | tf_op jit(solution)/shard_map/apply_first/pallas_call | solution.py:150
  48.5 6.3 %apply_first.7 = (f32[24,16,128]{2,1,0:T(8,128)S(1)}, f32[24,16,128]{2,1,0:T(8,128)S(1)}) custom-call(s32[352]{0:T(512)S(1)} %copy-done.8, s32[176]{0:T(256)S(1)} %copy-done.10, s32[1]{0:T(128)} %get-tuple-element.52.num_ref, bf16[352,128,256]{2,1,0:T(8,128)(2,1)S(1)} %get-tuple-element.53.w_ref, f32[48,1,128]{2,1,0:T(1,128)S(1)} %copy-done.6, ...), custom_call_target="tpu_custom_call" | custom-call | flops 738197504 | bytes 23068672 | tf_op jit(solution)/shard_map/apply_first/pallas_call | solution.py:150
  56.8 6.3 %apply_cheb.12 = (f32[24,16,128]{2,1,0:T(8,128)S(1)}, f32[24,16,128]{2,1,0:T(8,128)S(1)}) custom-call(s32[352]{0:T(512)S(1)} %copy-done.8, s32[176]{0:T(256)S(1)} %copy-done.10, s32[1]{0:T(128)} %get-tuple-element.52.num_ref, bf16[352,128,256]{2,1,0:T(8,128)(2,1)S(1)} %get-tuple-element.53.w_ref, f32[48,1,128]{2,1,0:T(1,128)S(1)} %copy-done.7, ...), custom_call_target="tpu_custom_call" | custom-call | flops 738197504 | bytes 23068672 | tf_op jit(solution)/shard_map/apply_cheb/pallas_call | solution.py:150
  66.2 6.3 %apply_cheb.15 = (f32[24,16,128]{2,1,0:T(8,128)S(1)}, f32[24,16,128]{2,1,0:T(8,128)S(1)}) custom-call(s32[352]{0:T(512)S(1)} %copy-done.8, s32[176]{0:T(256)S(1)} %copy-done.10, s32[1]{0:T(128)} %get-tuple-element.52.num_ref, bf16[352,128,256]{2,1,0:T(8,128)(2,1)S(1)} %get-tuple-element.53.w_ref, f32[48,1,128]{2,1,0:T(1,128)S(1)} %copy-done.7, ...), custom_call_target="tpu_custom_call" | custom-call | flops 738197504 | bytes 23068672 | tf_op jit(solution)/shard_map/apply_cheb/pallas_call | solution.py:150
  72.5 4.0 collective-permute-start.12
  76.5 6.3 %apply_cheb.13 = (f32[24,16,128]{2,1,0:T(8,128)S(1)}, f32[24,16,128]{2,1,0:T(8,128)S(1)}) custom-call(s32[352]{0:T(512)S(1)} %copy-done.9, s32[176]{0:T(256)S(1)} %copy-done.11, s32[1]{0:T(128)} %get-tuple-element.52.num_ref, bf16[352,128,256]{2,1,0:T(8,128)(2,1)S(1)} %get-tuple-element.53.w_ref, f32[48,1,128]{2,1,0:T(1,128)S(1)} %copy-done.7, ...), custom_call_target="tpu_custom_call" | custom-call | flops 738197504 | bytes 23068672 | tf_op jit(solution)/shard_map/apply_cheb/pallas_call | solution.py:150
  83.0 4.7 %collective-permute-start.7 = (f32[24,16,128]{2,1,0:T(8,128)S(1)}, f32[24,16,128]{2,1,0:T(8,128)S(1)}, u32[]{:S(2)}, u32[]{:S(2)}) collective-permute-start(f32[24,16,128]{2,1,0:T(8,128)S(1)} %get-tuple-element.60.po_ref), channel_id=1, source_target_pairs={{0,28},{4,8},{8,4},{12,16},{16,12},{20,24},{24,20},{28,0},{1,29},{... | collective-permute-start | bytes 589832 | tf_op jit(solution)/shard_map/ppermute | solution.py:245
  87.7 6.3 %apply_cheb.16 = (f32[24,16,128]{2,1,0:T(8,128)S(1)}, f32[24,16,128]{2,1,0:T(8,128)S(1)}) custom-call(s32[352]{0:T(512)S(1)} %copy-done.9, s32[176]{0:T(256)S(1)} %copy-done.11, s32[1]{0:T(128)} %get-tuple-element.52.num_ref, bf16[352,128,256]{2,1,0:T(8,128)(2,1)S(1)} %get-tuple-element.53.w_ref, f32[48,1,128]{2,1,0:T(1,128)S(1)} %copy-done.7, ...), custom_call_target="tpu_custom_call" | custom-call | flops 738197504 | bytes 23068672 | tf_op jit(solution)/shard_map/apply_cheb/pallas_call | solution.py:150
  96.0 6.3 %apply_cheb.14 = (f32[24,16,128]{2,1,0:T(8,128)S(1)}, f32[24,16,128]{2,1,0:T(8,128)S(1)}) custom-call(s32[352]{0:T(512)S(1)} %copy-done.9, s32[176]{0:T(256)S(1)} %copy-done.11, s32[1]{0:T(128)} %get-tuple-element.52.num_ref, bf16[352,128,256]{2,1,0:T(8,128)(2,1)S(1)} %get-tuple-element.53.w_ref, f32[48,1,128]{2,1,0:T(1,128)S(1)} %copy-done.7, ...), custom_call_target="tpu_custom_call" | custom-call | flops 738197504 | bytes 23068672 | tf_op jit(solution)/shard_map/apply_cheb/pallas_call | solution.py:150
  109.8 7.6 %copy-done.1 = bf16[352,128,256]{2,1,0:T(8,128)(2,1)S(1)} copy-done((bf16[352,128,256]{2,1,0:T(8,128)(2,1)S(1)}, bf16[352,128,256]{2,1,0:T(8,128)(2,1)}, u32[]{:S(2)}) %copy-start.1) | copy-done | bytes 23068696
  117.3 6.3 %apply_cheb.17 = (f32[24,16,128]{2,1,0:T(8,128)S(1)}, f32[24,16,128]{2,1,0:T(8,128)S(1)}) custom-call(s32[352]{0:T(512)S(1)} %copy-done.9, s32[176]{0:T(256)S(1)} %copy-done.11, s32[1]{0:T(128)} %get-tuple-element.52.num_ref, bf16[352,128,256]{2,1,0:T(8,128)(2,1)S(1)} %copy-done.1, f32[48,1,128]{2,1,0:T(1,128)S(1)} %copy-done.7, ...), custom_call_target="tpu_custom_call" | custom-call | flops 738197504 | bytes 23068672 | tf_op jit(solution)/shard_map/apply_cheb/pallas_call | solution.py:150
  129.9 7.6 %copy-done.2 = bf16[352,128,256]{2,1,0:T(8,128)(2,1)S(1)} copy-done((bf16[352,128,256]{2,1,0:T(8,128)(2,1)S(1)}, bf16[352,128,256]{2,1,0:T(8,128)(2,1)}, u32[]{:S(2)}) %copy-start.2) | copy-done | bytes 23068696
  137.4 6.2 %apply_first.8 = (f32[24,16,128]{2,1,0:T(8,128)S(1)}, f32[24,16,128]{2,1,0:T(8,128)S(1)}) custom-call(s32[352]{0:T(512)S(1)} %copy-done.9, s32[176]{0:T(256)S(1)} %copy-done.11, s32[1]{0:T(128)} %get-tuple-element.52.num_ref, bf16[352,128,256]{2,1,0:T(8,128)(2,1)S(1)} %copy-done.2, f32[48,1,128]{2,1,0:T(1,128)S(1)} %copy-done.7, ...), custom_call_target="tpu_custom_call" | custom-call | flops 738197504 | bytes 23068672 | tf_op jit(solution)/shard_map/apply_first/pallas_call | solution.py:150
  148.0 7.6 %copy-done.3 = bf16[352,128,256]{2,1,0:T(8,128)(2,1)S(1)} copy-done((bf16[352,128,256]{2,1,0:T(8,128)(2,1)S(1)}, bf16[352,128,256]{2,1,0:T(8,128)(2,1)}, u32[]{:S(2)}) %copy-start.3) | copy-done | bytes 23068696
  155.5 6.2 %apply_first.9 = (f32[24,16,128]{2,1,0:T(8,128)S(1)}, f32[24,16,128]{2,1,0:T(8,128)S(1)}) custom-call(s32[352]{0:T(512)S(1)} %copy-done.9, s32[176]{0:T(256)S(1)} %copy-done.11, s32[1]{0:T(128)} %get-tuple-element.52.num_ref, bf16[352,128,256]{2,1,0:T(8,128)(2,1)S(1)} %copy-done.3, f32[48,1,128]{2,1,0:T(1,128)S(1)} %copy-done.7, ...), custom_call_target="tpu_custom_call" | custom-call | flops 738197504 | bytes 23068672 | tf_op jit(solution)/shard_map/apply_first/pallas_call | solution.py:150
  166.2 3.6 collective-permute-start.26
  173.4 4.7 %gram.1 = (f32[128,128]{1,0:T(8,128)S(1)}, f32[128,128]{1,0:T(8,128)S(1)}) custom-call(f32[4,12,16,128]{3,2,1,0:T(8,128)S(1)} %all-to-all-done.fa_ref, f32[4,12,16,128]{3,2,1,0:T(8,128)S(1)} %all-to-all-done.1.fb_ref, f32[4,12,16,128]{3,2,1,0:T(8,128)S(1)} %all-to-all-done.2.za_ref, f32[4,12,16,128]{3,2,1,0:T(8,128)S(1)} %all-to-all-done.3.zb_ref), custom_call_target="tpu_custom_call" | custom-call | tf_op jit(solution)/shard_map/gram/pallas_call | solution.py:231
  178.2 4.1 %collective-permute-done.25.he_ref = f32[24,16,128]{2,1,0:T(8,128)} collective-permute-done((f32[24,16,128]{2,1,0:T(8,128)S(1)}, f32[24,16,128]{2,1,0:T(8,128)}, u32[]{:S(2)}, u32[]{:S(2)}) %collective-permute-start.25) | collective-permute-done | bytes 196640 | tf_op jit(solution)/shard_map/ppermute | solution.py:245
  182.3 7.6 %copy-done.4 = bf16[352,128,256]{2,1,0:T(8,128)(2,1)S(1)} copy-done((bf16[352,128,256]{2,1,0:T(8,128)(2,1)S(1)}, bf16[352,128,256]{2,1,0:T(8,128)(2,1)}, u32[]{:S(2)}) %copy-start.4) | copy-done | bytes 23068696
  189.9 6.7 %apply_cheb.18 = (f32[24,16,128]{2,1,0:T(8,128)S(1)}, f32[24,16,128]{2,1,0:T(8,128)S(1)}) custom-call(s32[352]{0:T(512)S(1)} %copy-done.9, s32[176]{0:T(256)S(1)} %copy-done.11, s32[1]{0:T(128)} %get-tuple-element.52.num_ref, bf16[352,128,256]{2,1,0:T(8,128)(2,1)S(1)} %copy-done.4, f32[48,1,128]{2,1,0:T(1,128)S(1)} %copy-done.7, ...), custom_call_target="tpu_custom_call" | custom-call | flops 738197504 | bytes 23068672 | tf_op jit(solution)/shard_map/apply_cheb/pallas_call | solution.py:150
  196.9 3.6 collective-permute-start.28
  200.5 6.6 %apply_cheb.21 = (f32[24,16,128]{2,1,0:T(8,128)S(1)}, f32[24,16,128]{2,1,0:T(8,128)S(1)}) custom-call(s32[352]{0:T(512)S(1)} %copy-done.9, s32[176]{0:T(256)S(1)} %copy-done.11, s32[1]{0:T(128)} %get-tuple-element.52.num_ref, bf16[352,128,256]{2,1,0:T(8,128)(2,1)S(1)} %copy-done.4, f32[48,1,128]{2,1,0:T(1,128)S(1)} %copy-done.7, ...), custom_call_target="tpu_custom_call" | custom-call | flops 738197504 | bytes 23068672 | tf_op jit(solution)/shard_map/apply_cheb/pallas_call | solution.py:150
  211.2 6.3 %apply_cheb.19 = (f32[24,16,128]{2,1,0:T(8,128)S(1)}, f32[24,16,128]{2,1,0:T(8,128)S(1)}) custom-call(s32[352]{0:T(512)S(1)} %copy-done.9, s32[176]{0:T(256)S(1)} %copy-done.11, s32[1]{0:T(128)} %get-tuple-element.52.num_ref, bf16[352,128,256]{2,1,0:T(8,128)(2,1)S(1)} %copy-done.4, f32[48,1,128]{2,1,0:T(1,128)S(1)} %copy-done.7, ...), custom_call_target="tpu_custom_call" | custom-call | flops 738197504 | bytes 23068672 | tf_op jit(solution)/shard_map/apply_cheb/pallas_call | solution.py:150
  220.7 6.4 %apply_cheb.22 = (f32[24,16,128]{2,1,0:T(8,128)S(1)}, f32[24,16,128]{2,1,0:T(8,128)S(1)}) custom-call(s32[352]{0:T(512)S(1)} %copy-done.9, s32[176]{0:T(256)S(1)} %copy-done.11, s32[1]{0:T(128)} %get-tuple-element.52.num_ref, bf16[352,128,256]{2,1,0:T(8,128)(2,1)S(1)} %copy-done.4, f32[48,1,128]{2,1,0:T(1,128)S(1)} %copy-done.7, ...), custom_call_target="tpu_custom_call" | custom-call | flops 738197504 | bytes 23068672 | tf_op jit(solution)/shard_map/apply_cheb/pallas_call | solution.py:150
  229.4 6.3 %apply_cheb.20 = (f32[24,16,128]{2,1,0:T(8,128)S(1)}, f32[24,16,128]{2,1,0:T(8,128)S(1)}) custom-call(s32[352]{0:T(512)S(1)} %copy-done.9, s32[176]{0:T(256)S(1)} %copy-done.11, s32[1]{0:T(128)} %get-tuple-element.52.num_ref, bf16[352,128,256]{2,1,0:T(8,128)(2,1)S(1)} %copy-done.4, f32[48,1,128]{2,1,0:T(1,128)S(1)} %copy-done.7, ...), custom_call_target="tpu_custom_call" | custom-call | flops 738197504 | bytes 23068672 | tf_op jit(solution)/shard_map/apply_cheb/pallas_call | solution.py:150
  237.7 3.6 collective-permute-start.43
  241.4 6.3 %apply_cheb.23 = (f32[24,16,128]{2,1,0:T(8,128)S(1)}, f32[24,16,128]{2,1,0:T(8,128)S(1)}) custom-call(s32[352]{0:T(512)S(1)} %copy-done.9, s32[176]{0:T(256)S(1)} %copy-done.11, s32[1]{0:T(128)} %get-tuple-element.52.num_ref, bf16[352,128,256]{2,1,0:T(8,128)(2,1)S(1)} %copy-done.4, f32[48,1,128]{2,1,0:T(1,128)S(1)} %copy-done.7, ...), custom_call_target="tpu_custom_call" | custom-call | flops 738197504 | bytes 23068672 | tf_op jit(solution)/shard_map/apply_cheb/pallas_call | solution.py:150
  256.3 7.6 %copy-done.5 = bf16[352,128,256]{2,1,0:T(8,128)(2,1)S(1)} copy-done((bf16[352,128,256]{2,1,0:T(8,128)(2,1)S(1)}, bf16[352,128,256]{2,1,0:T(8,128)(2,1)}, u32[]{:S(2)}) %copy-start.5) | copy-done | bytes 23068696
  263.9 6.3 %apply_first.10 = (f32[24,16,128]{2,1,0:T(8,128)S(1)}, f32[24,16,128]{2,1,0:T(8,128)S(1)}) custom-call(s32[352]{0:T(512)S(1)} %copy-done.9, s32[176]{0:T(256)S(1)} %copy-done.11, s32[1]{0:T(128)} %get-tuple-element.52.num_ref, bf16[352,128,256]{2,1,0:T(8,128)(2,1)S(1)} %copy-done.5, f32[48,1,128]{2,1,0:T(1,128)S(1)} %copy-done.7, ...), custom_call_target="tpu_custom_call" | custom-call | flops 738197504 | bytes 23068672 | tf_op jit(solution)/shard_map/apply_first/pallas_call | solution.py:150
  270.3 6.3 %apply_first.11 = (f32[24,16,128]{2,1,0:T(8,128)S(1)}, f32[24,16,128]{2,1,0:T(8,128)S(1)}) custom-call(s32[352]{0:T(512)S(1)} %copy-done.9, s32[176]{0:T(256)S(1)} %copy-done.11, s32[1]{0:T(128)} %get-tuple-element.52.num_ref, bf16[352,128,256]{2,1,0:T(8,128)(2,1)S(1)} %copy-done.5, f32[48,1,128]{2,1,0:T(1,128)S(1)} %copy-done.7, ...), custom_call_target="tpu_custom_call" | custom-call | flops 738197504 | bytes 23068672 | tf_op jit(solution)/shard_map/apply_first/pallas_call | solution.py:150
  279.5 11.7 %cholesky.44 = f32[128,128]{1,0:T(8,128)S(1)} custom-call(f32[128,128]{1,0:T(8,128)S(1)} %copy.14), custom_call_target="Cholesky" | custom-call | tf_op jit(solution)/shard_map/jit(cholesky)/cholesky | solution.py:268
  291.3 3.5 all-to-all-start.5
  296.0 9.8 %custom-call.6 = f32[1,128,128]{1,2,0:T(8,128)S(1)} custom-call(f32[1,128,128]{2,1,0:T(8,128)S(1)} %fusion.4), custom_call_target="InvertDiagBlocksLowerTriangular" | custom-call | tf_op jit(solution)/shard_map/jit(_solve_triangular)/triangular_solve | solution.py:269
  305.9 3.5 all-to-all-start.7
  309.6 6.4 %turn.1 = (f32[12,128,128]{2,1,0:T(8,128)S(1)}, f32[128,128]{1,0:T(8,128)S(1)}) custom-call(f32[128,128]{1,0:T(8,128)S(1)} %fusion.2.inv_ref, f32[4,12,16,128]{3,2,1,0:T(8,128)S(1)} %all-to-all-done.4.fa_ref, f32[4,12,16,128]{3,2,1,0:T(8,128)S(1)} %all-to-all-done.5.fb_ref), custom_call_target="tpu_custom_call" | custom-call | tf_op jit(solution)/shard_map/turn/pallas_call | solution.py:231
  317.4 3.7 all-to-all-start.8
  322.9 6.8 %collective-permute-done.38 = f32[128,128]{1,0:T(8,128)S(1)} collective-permute-done((f32[128,128]{1,0:T(8,128)S(1)}, f32[128,128]{1,0:T(8,128)S(1)}, u32[]{:S(2)}, u32[]{:S(2)}) %collective-permute-start.38) | collective-permute-done | bytes 65568 | tf_op jit(solution)/shard_map/ppermute | solution.py:253
  330.3 3.8 collective-permute-done.39
  334.2 4.3 %collective-permute-done.40 = f32[128,128]{1,0:T(8,128)S(1)} collective-permute-done((f32[128,128]{1,0:T(8,128)S(1)}, f32[128,128]{1,0:T(8,128)S(1)}, u32[]{:S(2)}, u32[]{:S(2)}) %collective-permute-start.40) | collective-permute-done | bytes 65568 | tf_op jit(solution)/shard_map/ppermute | solution.py:253
  339.5 6.2 %cross.1 = f32[128,128]{1,0:T(8,128)S(1)} custom-call(f32[128,128]{1,0:T(8,128)S(1)} %fusion.2.inv_ref, f32[12,128,128]{2,1,0:T(8,128)S(1)} %get-tuple-element.90.f_ref, f32[4,12,16,128]{3,2,1,0:T(8,128)S(1)} %all-to-all-done.7.za_ref, f32[4,12,16,128]{3,2,1,0:T(8,128)S(1)} %all-to-all-done.8.zb_ref), custom_call_target="tpu_custom_call" | custom-call | tf_op jit(solution)/shard_map/cross/pallas_call | solution.py:231
  346.0 11.7 %cholesky.55 = f32[128,128]{1,0:T(8,128)S(1)} custom-call(f32[128,128]{1,0:T(8,128)S(1)} %copy.16), custom_call_target="Cholesky" | custom-call | tf_op jit(solution)/shard_map/jit(cholesky)/cholesky | solution.py:268
  359.1 9.8 %custom-call.7 = f32[1,128,128]{1,2,0:T(8,128)S(1)} custom-call(f32[1,128,128]{2,1,0:T(8,128)S(1)} %fusion.5), custom_call_target="InvertDiagBlocksLowerTriangular" | custom-call | tf_op jit(solution)/shard_map/jit(_solve_triangular)/triangular_solve | solution.py:269
  372.5 3.5 all-to-all-start.6
  378.1 11.0 %collective-permute-done.47 = f32[128,128]{1,0:T(8,128)S(1)} collective-permute-done((f32[128,128]{1,0:T(8,128)S(1)}, f32[128,128]{1,0:T(8,128)S(1)}, u32[]{:S(2)}, u32[]{:S(2)}) %collective-permute-start.47) | collective-permute-done | bytes 65568 | tf_op jit(solution)/shard_map/ppermute | solution.py:253
  389.1 4.2 %collective-permute-done.48 = f32[128,128]{1,0:T(8,128)S(1)} collective-permute-done((f32[128,128]{1,0:T(8,128)S(1)}, f32[128,128]{1,0:T(8,128)S(1)}, u32[]{:S(2)}, u32[]{:S(2)}) %collective-permute-start.48) | collective-permute-done | bytes 65568 | tf_op jit(solution)/shard_map/ppermute | solution.py:253
  394.0 3.7 collective-permute-done.49
  (174 shorter events, 89.6 us)
Async XLA Ops:
  2.3 32.8 %collective-permute-start.1 = (f32[24,16,128]{2,1,0:T(8,128)S(1)}, f32[24,16,128]{2,1,0:T(8,128)S(1)}, u32[]{:S(2)}, u32[]{:S(2)}) collective-permute-start(f32[24,16,128]{2,1,0:T(8,128)S(1)} %get-tuple-element.102.po_ref.rest_1_), channel_id=1, source_target_pairs={{0,28},{4,8},{8,4},{12,16},{16,12},{20,24},{24,20},{28,0},{1,29},{... | collective-permute-start | bytes 589832 | tf_op jit(solution)/shard_map/ppermute | solution.py:245
  8.4 26.7 %collective-permute-start = (f32[24,16,128]{2,1,0:T(8,128)S(1)}, f32[24,16,128]{2,1,0:T(8,128)S(1)}, u32[]{:S(2)}, u32[]{:S(2)}) collective-permute-start(f32[24,16,128]{2,1,0:T(8,128)S(1)} %get-tuple-element.104.pe_ref.rest_0_), channel_id=1, source_target_pairs={{0,4},{4,0},{8,12},{12,8},{16,20},{20,16},{24,28},{28,24},{1,5},{5... | collective-permute-start | bytes 589832 | tf_op jit(solution)/shard_map/ppermute | solution.py:245
  8.4 40.1 %collective-permute-start.9 = (f32[24,16,128]{2,1,0:T(8,128)S(1)}, f32[24,16,128]{2,1,0:T(8,128)S(1)}, u32[]{:S(2)}, u32[]{:S(2)}) collective-permute-start(f32[24,16,128]{2,1,0:T(8,128)S(1)} %get-tuple-element.101.po_ref.rest_1_), channel_id=1, source_target_pairs={{0,28},{4,8},{8,4},{12,16},{16,12},{20,24},{24,20},{28,0},{1,29},{... | collective-permute-start | bytes 589832 | tf_op jit(solution)/shard_map/ppermute | solution.py:245
  10.3 38.2 %collective-permute-start.8 = (f32[24,16,128]{2,1,0:T(8,128)S(1)}, f32[24,16,128]{2,1,0:T(8,128)S(1)}, u32[]{:S(2)}, u32[]{:S(2)}) collective-permute-start(f32[24,16,128]{2,1,0:T(8,128)S(1)} %get-tuple-element.103.pe_ref.rest_0_), channel_id=1, source_target_pairs={{0,4},{4,0},{8,12},{12,8},{16,20},{20,16},{24,28},{28,24},{1,5},{5... | collective-permute-start | bytes 589832 | tf_op jit(solution)/shard_map/ppermute | solution.py:245
  43.6 13.2 %collective-permute-start.2 = (f32[24,16,128]{2,1,0:T(8,128)S(1)}, f32[24,16,128]{2,1,0:T(8,128)S(1)}, u32[]{:S(2)}, u32[]{:S(2)}) collective-permute-start(f32[24,16,128]{2,1,0:T(8,128)S(1)} %get-tuple-element.55.pe_ref.rest_0_), channel_id=1, source_target_pairs={{0,4},{4,0},{8,12},{12,8},{16,20},{20,16},{24,28},{28,24},{1,5},{5... | collective-permute-start | bytes 589832 | tf_op jit(solution)/shard_map/ppermute | solution.py:245
  54.8 11.4 %collective-permute-start.10 = (f32[24,16,128]{2,1,0:T(8,128)S(1)}, f32[24,16,128]{2,1,0:T(8,128)S(1)}, u32[]{:S(2)}, u32[]{:S(2)}) collective-permute-start(f32[24,16,128]{2,1,0:T(8,128)S(1)} %get-tuple-element.63.pe_ref.rest_0_), channel_id=1, source_target_pairs={{0,4},{4,0},{8,12},{12,8},{16,20},{20,16},{24,28},{28,24},{1,5},{5... | collective-permute-start | bytes 589832 | tf_op jit(solution)/shard_map/ppermute | solution.py:245
  55.0 11.2 %collective-permute-start.11 = (f32[24,16,128]{2,1,0:T(8,128)S(1)}, f32[24,16,128]{2,1,0:T(8,128)S(1)}, u32[]{:S(2)}, u32[]{:S(2)}) collective-permute-start(f32[24,16,128]{2,1,0:T(8,128)S(1)} %get-tuple-element.64.po_ref.rest_1_), channel_id=1, source_target_pairs={{0,28},{4,8},{8,4},{12,16},{16,12},{20,24},{24,20},{28,0},{1,29},{... | collective-permute-start | bytes 589832 | tf_op jit(solution)/shard_map/ppermute | solution.py:245
  63.1 13.3 %collective-permute-start.4 = (f32[24,16,128]{2,1,0:T(8,128)S(1)}, f32[24,16,128]{2,1,0:T(8,128)S(1)}, u32[]{:S(2)}, u32[]{:S(2)}) collective-permute-start(f32[24,16,128]{2,1,0:T(8,128)S(1)} %get-tuple-element.57.pe_ref.rest_0_), channel_id=1, source_target_pairs={{0,4},{4,0},{8,12},{12,8},{16,20},{20,16},{24,28},{28,24},{1,5},{5... | collective-permute-start | bytes 589832 | tf_op jit(solution)/shard_map/ppermute | solution.py:245
  63.3 13.2 %collective-permute-start.5 = (f32[24,16,128]{2,1,0:T(8,128)S(1)}, f32[24,16,128]{2,1,0:T(8,128)S(1)}, u32[]{:S(2)}, u32[]{:S(2)}) collective-permute-start(f32[24,16,128]{2,1,0:T(8,128)S(1)} %get-tuple-element.58.po_ref.rest_1_), channel_id=1, source_target_pairs={{0,28},{4,8},{8,4},{12,16},{16,12},{20,24},{24,20},{28,0},{1,29},{... | collective-permute-start | bytes 589832 | tf_op jit(solution)/shard_map/ppermute | solution.py:245
  72.5 15.2 %collective-permute-start.12 = (f32[24,16,128]{2,1,0:T(8,128)S(1)}, f32[24,16,128]{2,1,0:T(8,128)S(1)}, u32[]{:S(2)}, u32[]{:S(2)}) collective-permute-start(f32[24,16,128]{2,1,0:T(8,128)S(1)} %get-tuple-element.65.pe_ref.rest_0_), channel_id=1, source_target_pairs={{0,4},{4,0},{8,12},{12,8},{16,20},{20,16},{24,28},{28,24},{1,5},{5... | collective-permute-start | bytes 589832 | tf_op jit(solution)/shard_map/ppermute | solution.py:245
  82.8 13.2 %collective-permute-start.6 = (f32[24,16,128]{2,1,0:T(8,128)S(1)}, f32[24,16,128]{2,1,0:T(8,128)S(1)}, u32[]{:S(2)}, u32[]{:S(2)}) collective-permute-start(f32[24,16,128]{2,1,0:T(8,128)S(1)} %get-tuple-element.59.pe_ref), channel_id=1, source_target_pairs={{0,4},{4,0},{8,12},{12,8},{16,20},{20,16},{24,28},{28,24},{1,5},{5... | collective-permute-start | bytes 589832 | tf_op jit(solution)/shard_map/ppermute | solution.py:245
  83.0 13.0 %collective-permute-start.7 = (f32[24,16,128]{2,1,0:T(8,128)S(1)}, f32[24,16,128]{2,1,0:T(8,128)S(1)}, u32[]{:S(2)}, u32[]{:S(2)}) collective-permute-start(f32[24,16,128]{2,1,0:T(8,128)S(1)} %get-tuple-element.60.po_ref), channel_id=1, source_target_pairs={{0,28},{4,8},{8,4},{12,16},{16,12},{20,24},{24,20},{28,0},{1,29},{... | collective-permute-start | bytes 589832 | tf_op jit(solution)/shard_map/ppermute | solution.py:245
  93.9 15.8 %collective-permute-start.14 = (f32[24,16,128]{2,1,0:T(8,128)S(1)}, f32[24,16,128]{2,1,0:T(8,128)S(1)}, u32[]{:S(2)}, u32[]{:S(2)}) collective-permute-start(f32[24,16,128]{2,1,0:T(8,128)S(1)} %get-tuple-element.67.pe_ref), channel_id=1, source_target_pairs={{0,4},{4,0},{8,12},{12,8},{16,20},{20,16},{24,28},{28,24},{1,5},{5... | collective-permute-start | bytes 589832 | tf_op jit(solution)/shard_map/ppermute | solution.py:245
  94.0 15.8 %collective-permute-start.15 = (f32[24,16,128]{2,1,0:T(8,128)S(1)}, f32[24,16,128]{2,1,0:T(8,128)S(1)}, u32[]{:S(2)}, u32[]{:S(2)}) collective-permute-start(f32[24,16,128]{2,1,0:T(8,128)S(1)} %get-tuple-element.68.po_ref), channel_id=1, source_target_pairs={{0,28},{4,8},{8,4},{12,16},{16,12},{20,24},{24,20},{28,0},{1,29},{... | collective-permute-start | bytes 589832 | tf_op jit(solution)/shard_map/ppermute | solution.py:245
  103.0 21.4 %all-to-all-start = ((f32[4,12,16,128]{3,2,1,0:T(8,128)}), f32[4,12,16,128]{3,2,1,0:T(8,128)S(1)}, u32[]{:S(2)}, u32[]{:S(2)}) async-start(f32[4,12,16,128]{3,2,1,0:T(8,128)} %bitcast.4), calls=%async_computation | async-start | bytes 786432 | tf_op jit(solution)/shard_map/all_to_all | solution.py:262
  106.5 23.4 %collective-permute-start.16 = (f32[24,16,128]{2,1,0:T(8,128)S(1)}, f32[24,16,128]{2,1,0:T(8,128)S(1)}, u32[]{:S(2)}, u32[]{:S(2)}) collective-permute-start(f32[24,16,128]{2,1,0:T(8,128)S(1)} %get-tuple-element.61.pe_ref.rest_0_), channel_id=1, source_target_pairs={{0,4},{4,0},{8,12},{12,8},{16,20},{20,16},{24,28},{28,24},{1,5},{5... | collective-permute-start | bytes 589832 | tf_op jit(solution)/shard_map/ppermute | solution.py:245
  106.6 23.3 %collective-permute-start.17 = (f32[24,16,128]{2,1,0:T(8,128)S(1)}, f32[24,16,128]{2,1,0:T(8,128)S(1)}, u32[]{:S(2)}, u32[]{:S(2)}) collective-permute-start(f32[24,16,128]{2,1,0:T(8,128)S(1)} %get-tuple-element.62.po_ref.rest_1_), channel_id=1, source_target_pairs={{0,28},{4,8},{8,4},{12,16},{16,12},{20,24},{24,20},{28,0},{1,29},{... | collective-permute-start | bytes 589832 | tf_op jit(solution)/shard_map/ppermute | solution.py:245
  124.4 20.1 %all-to-all-start.1 = ((f32[4,12,16,128]{3,2,1,0:T(8,128)}), f32[4,12,16,128]{3,2,1,0:T(8,128)S(1)}, u32[]{:S(2)}, u32[]{:S(2)}) async-start(f32[4,12,16,128]{3,2,1,0:T(8,128)} %bitcast.7), calls=%async_computation.1 | async-start | bytes 786432 | tf_op jit(solution)/shard_map/all_to_all | solution.py:262
  127.8 20.1 %collective-permute-start.18 = (f32[24,16,128]{2,1,0:T(8,128)S(1)}, f32[24,16,128]{2,1,0:T(8,128)S(1)}, u32[]{:S(2)}, u32[]{:S(2)}) collective-permute-start(f32[24,16,128]{2,1,0:T(8,128)S(1)} %get-tuple-element.69.pe_ref.rest_0_), channel_id=1, source_target_pairs={{0,4},{4,0},{8,12},{12,8},{16,20},{20,16},{24,28},{28,24},{1,5},{5... | collective-permute-start | bytes 589832 | tf_op jit(solution)/shard_map/ppermute | solution.py:245
  128.8 19.2 %collective-permute-start.19 = (f32[24,16,128]{2,1,0:T(8,128)S(1)}, f32[24,16,128]{2,1,0:T(8,128)S(1)}, u32[]{:S(2)}, u32[]{:S(2)}) collective-permute-start(f32[24,16,128]{2,1,0:T(8,128)S(1)} %get-tuple-element.70.po_ref.rest_1_), channel_id=1, source_target_pairs={{0,28},{4,8},{8,4},{12,16},{16,12},{20,24},{24,20},{28,0},{1,29},{... | collective-permute-start | bytes 589832 | tf_op jit(solution)/shard_map/ppermute | solution.py:245
  144.5 18.1 %all-to-all-start.2 = ((f32[4,12,16,128]{3,2,1,0:T(8,128)}), f32[4,12,16,128]{3,2,1,0:T(8,128)S(1)}, u32[]{:S(2)}, u32[]{:S(2)}) async-start(f32[4,12,16,128]{3,2,1,0:T(8,128)} %bitcast.8), calls=%async_computation.2 | async-start | bytes 786432 | tf_op jit(solution)/shard_map/all_to_all | solution.py:262
  166.0 16.3 %collective-permute-start.25 = (f32[24,16,128]{2,1,0:T(8,128)S(1)}, f32[24,16,128]{2,1,0:T(8,128)}, u32[]{:S(2)}, u32[]{:S(2)}) collective-permute-start(f32[24,16,128]{2,1,0:T(8,128)S(1)} %get-tuple-element.71.pe_ref.rest_0_), channel_id=1, source_target_pairs={{0,4},{4,0},{8,12},{12,8},{16,20},{20,16},{24,28},{28,24},{1,5},{5... | collective-permute-start | bytes 589832 | tf_op jit(solution)/shard_map/ppermute | solution.py:245
  166.2 16.2 %collective-permute-start.26 = (f32[24,16,128]{2,1,0:T(8,128)S(1)}, f32[24,16,128]{2,1,0:T(8,128)}, u32[]{:S(2)}, u32[]{:S(2)}) collective-permute-start(f32[24,16,128]{2,1,0:T(8,128)S(1)} %get-tuple-element.72.po_ref.rest_1_), channel_id=1, source_target_pairs={{0,28},{4,8},{8,4},{12,16},{16,12},{20,24},{24,20},{28,0},{1,29},{... | collective-permute-start | bytes 589832 | tf_op jit(solution)/shard_map/ppermute | solution.py:245
  169.8 30.7 %collective-permute-start.31 = (f32[24,16,128]{2,1,0:T(8,128)S(1)}, f32[24,16,128]{2,1,0:T(8,128)S(1)}, u32[]{:S(2)}, u32[]{:S(2)}) collective-permute-start(f32[24,16,128]{2,1,0:T(8,128)S(1)} %get-tuple-element.73.pe_ref.rest_0_), channel_id=1, source_target_pairs={{0,4},{4,0},{8,12},{12,8},{16,20},{20,16},{24,28},{28,24},{1,5},{5... | collective-permute-start | bytes 589832 | tf_op jit(solution)/shard_map/ppermute | solution.py:245
  170.1 30.4 %collective-permute-start.32 = (f32[24,16,128]{2,1,0:T(8,128)S(1)}, f32[24,16,128]{2,1,0:T(8,128)}, u32[]{:S(2)}, u32[]{:S(2)}) collective-permute-start(f32[24,16,128]{2,1,0:T(8,128)S(1)} %get-tuple-element.74.po_ref.rest_1_), channel_id=1, source_target_pairs={{0,28},{4,8},{8,4},{12,16},{16,12},{20,24},{24,20},{28,0},{1,29},{... | collective-permute-start | bytes 589832 | tf_op jit(solution)/shard_map/ppermute | solution.py:245
  178.1 31.0 %collective-permute-start.20 = (f32[2,128,128]{2,1,0:T(8,128)S(1)}, f32[2,128,128]{2,1,0:T(8,128)S(1)}, u32[]{:S(2)}, u32[]{:S(2)}) collective-permute-start(f32[2,128,128]{2,1,0:T(8,128)S(1)} %pad_maximum_fusion.8), channel_id=1, source_target_pairs={{0,1},{1,0},{2,3},{3,2},{4,5},{5,4},{6,7},{7,6},{8,9},{9,8},{10,11... | collective-permute-start | bytes 393224 | tf_op jit(solution)/shard_map/ppermute | solution.py:253
  196.6 14.6 %collective-permute-start.27 = (f32[24,16,128]{2,1,0:T(8,128)S(1)}, f32[24,16,128]{2,1,0:T(8,128)S(1)}, u32[]{:S(2)}, u32[]{:S(2)}) collective-permute-start(f32[24,16,128]{2,1,0:T(8,128)S(1)} %get-tuple-element.77.pe_ref.rest_0_), channel_id=1, source_target_pairs={{0,4},{4,0},{8,12},{12,8},{16,20},{20,16},{24,28},{28,24},{1,5},{5... | collective-permute-start | bytes 589832 | tf_op jit(solution)/shard_map/ppermute | solution.py:245
  196.9 14.3 %collective-permute-start.28 = (f32[24,16,128]{2,1,0:T(8,128)S(1)}, f32[24,16,128]{2,1,0:T(8,128)S(1)}, u32[]{:S(2)}, u32[]{:S(2)}) collective-permute-start(f32[24,16,128]{2,1,0:T(8,128)S(1)} %get-tuple-element.78.po_ref.rest_1_), channel_id=1, source_target_pairs={{0,28},{4,8},{8,4},{12,16},{16,12},{20,24},{24,20},{28,0},{1,29},{... | collective-permute-start | bytes 589832 | tf_op jit(solution)/shard_map/ppermute | solution.py:245
  207.1 13.6 %collective-permute-start.33 = (f32[24,16,128]{2,1,0:T(8,128)S(1)}, f32[24,16,128]{2,1,0:T(8,128)S(1)}, u32[]{:S(2)}, u32[]{:S(2)}) collective-permute-start(f32[24,16,128]{2,1,0:T(8,128)S(1)} %get-tuple-element.83.pe_ref.rest_0_), channel_id=1, source_target_pairs={{0,4},{4,0},{8,12},{12,8},{16,20},{20,16},{24,28},{28,24},{1,5},{5... | collective-permute-start | bytes 589832 | tf_op jit(solution)/shard_map/ppermute | solution.py:245
  207.4 13.3 %collective-permute-start.34 = (f32[24,16,128]{2,1,0:T(8,128)S(1)}, f32[24,16,128]{2,1,0:T(8,128)S(1)}, u32[]{:S(2)}, u32[]{:S(2)}) collective-permute-start(f32[24,16,128]{2,1,0:T(8,128)S(1)} %get-tuple-element.84.po_ref.rest_1_), channel_id=1, source_target_pairs={{0,28},{4,8},{8,4},{12,16},{16,12},{20,24},{24,20},{28,0},{1,29},{... | collective-permute-start | bytes 589832 | tf_op jit(solution)/shard_map/ppermute | solution.py:245
  209.1 20.1 %collective-permute-start.21 = (f32[2,128,128]{2,1,0:T(8,128)S(1)}, f32[2,128,128]{2,1,0:T(8,128)S(1)}, u32[]{:S(2)}, u32[]{:S(2)}) collective-permute-start(f32[2,128,128]{2,1,0:T(8,128)S(1)} %fusion.12), channel_id=1, source_target_pairs={{0,2},{1,3},{2,0},{3,1},{4,6},{5,7},{6,4},{7,5},{8,10},{9,11},{10,... | collective-permute-start | bytes 393224 | tf_op jit(solution)/shard_map/ppermute | solution.py:253
  217.5 11.9 %collective-permute-start.29 = (f32[24,16,128]{2,1,0:T(8,128)S(1)}, f32[24,16,128]{2,1,0:T(8,128)S(1)}, u32[]{:S(2)}, u32[]{:S(2)}) collective-permute-start(f32[24,16,128]{2,1,0:T(8,128)S(1)} %get-tuple-element.79.pe_ref), channel_id=1, source_target_pairs={{0,4},{4,0},{8,12},{12,8},{16,20},{20,16},{24,28},{28,24},{1,5},{5... | collective-permute-start | bytes 589832 | tf_op jit(solution)/shard_map/ppermute | solution.py:245
  217.6 11.8 %collective-permute-start.30 = (f32[24,16,128]{2,1,0:T(8,128)S(1)}, f32[24,16,128]{2,1,0:T(8,128)S(1)}, u32[]{:S(2)}, u32[]{:S(2)}) collective-permute-start(f32[24,16,128]{2,1,0:T(8,128)S(1)} %get-tuple-element.80.po_ref), channel_id=1, source_target_pairs={{0,28},{4,8},{8,4},{12,16},{16,12},{20,24},{24,20},{28,0},{1,29},{... | collective-permute-start | bytes 589832 | tf_op jit(solution)/shard_map/ppermute | solution.py:245
  227.2 14.2 %collective-permute-start.35 = (f32[24,16,128]{2,1,0:T(8,128)S(1)}, f32[24,16,128]{2,1,0:T(8,128)S(1)}, u32[]{:S(2)}, u32[]{:S(2)}) collective-permute-start(f32[24,16,128]{2,1,0:T(8,128)S(1)} %get-tuple-element.85.pe_ref), channel_id=1, source_target_pairs={{0,4},{4,0},{8,12},{12,8},{16,20},{20,16},{24,28},{28,24},{1,5},{5... | collective-permute-start | bytes 589832 | tf_op jit(solution)/shard_map/ppermute | solution.py:245
  228.1 13.2 %collective-permute-start.36 = (f32[24,16,128]{2,1,0:T(8,128)S(1)}, f32[24,16,128]{2,1,0:T(8,128)S(1)}, u32[]{:S(2)}, u32[]{:S(2)}) collective-permute-start(f32[24,16,128]{2,1,0:T(8,128)S(1)} %get-tuple-element.86.po_ref), channel_id=1, source_target_pairs={{0,28},{4,8},{8,4},{12,16},{16,12},{20,24},{24,20},{28,0},{1,29},{... | collective-permute-start | bytes 589832 | tf_op jit(solution)/shard_map/ppermute | solution.py:245
  229.2 23.9 %collective-permute-start.22 = (f32[2,128,128]{2,1,0:T(8,128)S(1)}, f32[2,128,128]{2,1,0:T(8,128)S(1)}, u32[]{:S(2)}, u32[]{:S(2)}) collective-permute-start(f32[2,128,128]{2,1,0:T(8,128)S(1)} %fusion.13), channel_id=1, source_target_pairs={{0,4},{4,0},{8,12},{12,8},{16,20},{20,16},{24,28},{28,24},{1,5},{5... | collective-permute-start | bytes 393224 | tf_op jit(solution)/shard_map/ppermute | solution.py:253
  235.7 20.6 %collective-permute-start.42 = (f32[24,16,128]{2,1,0:T(8,128)S(1)}, f32[24,16,128]{2,1,0:T(8,128)S(1)}, u32[]{:S(2)}, u32[]{:S(2)}) collective-permute-start(f32[24,16,128]{2,1,0:T(8,128)S(1)} %get-tuple-element.81.pe_ref), channel_id=1, source_target_pairs={{0,4},{4,0},{8,12},{12,8},{16,20},{20,16},{24,28},{28,24},{1,5},{5... | collective-permute-start | bytes 589832 | tf_op jit(solution)/shard_map/ppermute | solution.py:245
  237.7 18.6 %collective-permute-start.43 = (f32[24,16,128]{2,1,0:T(8,128)S(1)}, f32[24,16,128]{2,1,0:T(8,128)S(1)}, u32[]{:S(2)}, u32[]{:S(2)}) collective-permute-start(f32[24,16,128]{2,1,0:T(8,128)S(1)} %get-tuple-element.82.po_ref), channel_id=1, source_target_pairs={{0,28},{4,8},{8,4},{12,16},{16,12},{20,24},{24,20},{28,0},{1,29},{... | collective-permute-start | bytes 589832 | tf_op jit(solution)/shard_map/ppermute | solution.py:245
  247.6 22.6 %collective-permute-start.44 = (f32[24,16,128]{2,1,0:T(8,128)S(1)}, f32[24,16,128]{2,1,0:T(8,128)S(1)}, u32[]{:S(2)}, u32[]{:S(2)}) collective-permute-start(f32[24,16,128]{2,1,0:T(8,128)S(1)} %get-tuple-element.87.pe_ref), channel_id=1, source_target_pairs={{0,4},{4,0},{8,12},{12,8},{16,20},{20,16},{24,28},{28,24},{1,5},{5... | collective-permute-start | bytes 589832 | tf_op jit(solution)/shard_map/ppermute | solution.py:245
  247.7 22.5 %collective-permute-start.45 = (f32[24,16,128]{2,1,0:T(8,128)S(1)}, f32[24,16,128]{2,1,0:T(8,128)S(1)}, u32[]{:S(2)}, u32[]{:S(2)}) collective-permute-start(f32[24,16,128]{2,1,0:T(8,128)S(1)} %get-tuple-element.88.po_ref), channel_id=1, source_target_pairs={{0,28},{4,8},{8,4},{12,16},{16,12},{20,24},{24,20},{28,0},{1,29},{... | collective-permute-start | bytes 589832 | tf_op jit(solution)/shard_map/ppermute | solution.py:245
  249.7 41.6 %all-to-all-start.4 = ((f32[4,12,16,128]{3,2,1,0:T(8,128)}), f32[4,12,16,128]{3,2,1,0:T(8,128)S(1)}, u32[]{:S(2)}, u32[]{:S(2)}) async-start(f32[4,12,16,128]{3,2,1,0:T(8,128)} %bitcast.16), calls=%async_computation.4 | async-start | bytes 786432 | tf_op jit(solution)/shard_map/all_to_all | solution.py:262
  253.2 17.0 %collective-permute-start.23 = (f32[2,128,128]{2,1,0:T(8,128)S(1)}, f32[2,128,128]{2,1,0:T(8,128)S(1)}, u32[]{:S(2)}, u32[]{:S(2)}) collective-permute-start(f32[2,128,128]{2,1,0:T(8,128)S(1)} %add.65), channel_id=1, source_target_pairs={{0,8},{4,12},{8,0},{12,4},{16,24},{20,28},{24,16},{28,20},{1,9},{5... | collective-permute-start | bytes 393224 | tf_op jit(solution)/shard_map/ppermute | solution.py:253
  291.3 14.6 %all-to-all-start.5 = ((f32[4,12,16,128]{3,2,1,0:T(8,128)}), f32[4,12,16,128]{3,2,1,0:T(8,128)S(1)}, u32[]{:S(2)}, u32[]{:S(2)}) async-start(f32[4,12,16,128]{3,2,1,0:T(8,128)} %bitcast.17), calls=%async_computation.5 | async-start | bytes 786432 | tf_op jit(solution)/shard_map/all_to_all | solution.py:262
  305.9 11.5 %all-to-all-start.7 = ((f32[4,12,16,128]{3,2,1,0:T(8,128)}), f32[4,12,16,128]{3,2,1,0:T(8,128)S(1)}, u32[]{:S(2)}, u32[]{:S(2)}) async-start(f32[4,12,16,128]{3,2,1,0:T(8,128)} %bitcast.25), calls=%async_computation.7 | async-start | bytes 786432 | tf_op jit(solution)/shard_map/all_to_all | solution.py:262
  317.4 22.1 %all-to-all-start.8 = ((f32[4,12,16,128]{3,2,1,0:T(8,128)}), f32[4,12,16,128]{3,2,1,0:T(8,128)S(1)}, u32[]{:S(2)}, u32[]{:S(2)}) async-start(f32[4,12,16,128]{3,2,1,0:T(8,128)} %bitcast.26), calls=%async_computation.8 | async-start | bytes 786432 | tf_op jit(solution)/shard_map/all_to_all | solution.py:262
  345.7 30.3 %collective-permute-start.46 = (f32[128,128]{1,0:T(8,128)S(1)}, f32[128,128]{1,0:T(8,128)S(1)}, u32[]{:S(2)}, u32[]{:S(2)}) collective-permute-start(f32[128,128]{1,0:T(8,128)S(1)} %cross.1), channel_id=1, source_target_pairs={{0,1},{1,0},{2,3},{3,2},{4,5},{5,4},{6,7},{7,6},{8,9},{9,8},{10,11... | collective-permute-start | bytes 196616 | tf_op jit(solution)/shard_map/ppermute | solution.py:253
  372.5 31.7 %all-to-all-start.6 = ((f32[4,12,32,128]{3,2,1,0:T(8,128)}), f32[4,12,32,128]{3,2,1,0:T(8,128)S(1)}, u32[]{:S(2)}, u32[]{:S(2)}) async-start(f32[4,12,32,128]{3,2,1,0:T(8,128)} %basis.1), calls=%async_computation.6 | async-start | bytes 1572864 | tf_op jit(solution)/shard_map/all_to_all | solution.py:329
  376.0 13.0 %collective-permute-start.47 = (f32[128,128]{1,0:T(8,128)S(1)}, f32[128,128]{1,0:T(8,128)S(1)}, u32[]{:S(2)}, u32[]{:S(2)}) collective-permute-start(f32[128,128]{1,0:T(8,128)S(1)} %add.74), channel_id=1, source_target_pairs={{0,2},{1,3},{2,0},{3,1},{4,6},{5,7},{6,4},{7,5},{8,10},{9,11},{10,... | collective-permute-start | bytes 196616 | tf_op jit(solution)/shard_map/ppermute | solution.py:253
  (24 other events, 249.4 us)

commit v2 on v0

v2 whole, which is shorter than its diff:
```python
import functools
import jax
import jax.numpy as jnp
from jax import lax
from jax.experimental import pallas as pl
from jax.experimental.pallas import tpu as pltpu
from jax.sharding import PartitionSpec as P

DEGREE = 4
UNROLL = 16
CHUNK = 24
F32, BF16, I32 = jnp.float32, jnp.bfloat16, jnp.int32
precise = lax.Precision.HIGHEST
center = 1.025
half_width = 0.975
MIB = 1 << 20
IN_VMEM = pl.BlockSpec(memory_space=pltpu.VMEM)
IN_SMEM = pl.BlockSpec(memory_space=pltpu.SMEM)


def nt(a, b):
    return lax.dot_general(
        a, b, (((1,), (1,)), ((), ())), precision=precise, preferred_element_type=F32
    )


def tn(a, b):
    return lax.dot_general(
        a, b, (((0,), (0,)), ((), ())), precision=precise, preferred_element_type=F32
    )


def nn(a, b):
    return jnp.dot(a, b, precision=precise, preferred_element_type=F32)


def call(kernel, name, outs, *args, scalars=0, scratch=(), cost=None):
    return pl.pallas_call(
        kernel,
        in_specs=[IN_SMEM] * scalars + [IN_VMEM] * (len(args) - scalars),
        out_specs=[IN_VMEM] * len(outs),
        out_shape=[jax.ShapeDtypeStruct(o, F32) for o in outs],
        scratch_shapes=list(scratch),
        compiler_params=pltpu.CompilerParams(vmem_limit_bytes=12 * MIB),
        cost_estimate=cost,
        name=name,
    )(*args)


def prep_kernel(rows, ids_ref, own_ref, col_ref, blk_ref, w_ref, inv_ref, src_ref, row_ref, num_ref,
                eye_ref, state_ref):
    chunk, n, _ = blk_ref.shape
    half = rows // 2
    step = pl.program_id(0)
    me = ids_ref[0]
    odd = me % 2
    zero = jnp.zeros(w_ref.shape[1:], BF16)

    @pl.when(step == 0)
    def _():
        state_ref[0] = 0
        state_ref[1] = -1
        inv_ref[...] = jnp.zeros(inv_ref.shape, F32)
        lines = lax.broadcasted_iota(I32, eye_ref.shape, 0)
        lanes = lax.broadcasted_iota(I32, eye_ref.shape, 1)
        eye_ref[...] = jnp.where((lines == lanes) | (lines >= n), 1.0, 0.0).astype(BF16)

    at = state_ref[0]
    last = state_ref[1]
    for c in range(chunk):
        b = step * chunk + c
        r = own_ref[0, b]
        k = col_ref[0, b]
        at = jnp.where(r == last, at, (at + 1) // 2 * 2)
        last = r
        owner = k // rows
        local = k - owner * rows
        upper = (local >= half).astype(I32)
        near = local - half * upper
        swap = odd * upper + (1 - odd) * (1 - upper)
        src_ref[at] = jnp.where(owner == me, near + half * swap, 2 * half + near + half * (1 - swap))
        src_ref[at + 1] = 0
        top = (r >= half).astype(I32)
        r_at = r + half * (1 - odd) * (1 - 2 * top)
        row_ref[at // 2] = r_at
        w_ref[at + 1] = zero
        a = blk_ref[c]
        high = a.astype(BF16)
        low = (a - high.astype(F32)).astype(BF16)
        both = jnp.concatenate([high, low], axis=0)
        t = lax.dot_general(
            eye_ref[...], both, (((1,), (1,)), ((), ())), preferred_element_type=F32
        )
        w_ref[at] = t[:n].astype(BF16)
        inv_ref[r_at] = inv_ref[r_at] + (t[n:n + 1, :n] + t[n:n + 1, n:])
        at = at + 1
    state_ref[0] = at
    state_ref[1] = last

    @pl.when(step == pl.num_programs(0) - 1)
    def _():
        used = (at + 1) // 2
        upto = (used + UNROLL - 1) // UNROLL * UNROLL
        def fill(p, c):
            row_ref[p] = rows
            for s in range(2):
                w_ref[2 * p + s] = zero
                src_ref[2 * p + s] = 0
            return c
        lax.fori_loop(used, upto, fill, 0)
        num_ref[0] = upto // UNROLL
        inv_ref[...] = 1.0 / inv_ref[...]


def prep(ids, own, col, blocks, rows):
    count, n, _ = blocks.shape
    chunk = CHUNK if count % CHUNK == 0 else 1
    slots = ((count + rows) // 2 + UNROLL) // UNROLL * UNROLL * 2
    return pl.pallas_call(
        functools.partial(prep_kernel, rows),
        grid=(count // chunk,),
        in_specs=[IN_SMEM, IN_SMEM, IN_SMEM, pl.BlockSpec((chunk, n, n), lambda i: (i, 0, 0))],
        out_specs=[IN_VMEM, IN_VMEM, IN_SMEM, IN_SMEM, IN_SMEM],
        out_shape=[pltpu.VMEM((slots, n, 2 * n), BF16),
                   jax.ShapeDtypeStruct((rows, 1, n), F32),
                   jax.ShapeDtypeStruct((slots,), I32),
                   jax.ShapeDtypeStruct((slots // 2,), I32),
                   jax.ShapeDtypeStruct((1,), I32)],
        scratch_shapes=[pltpu.VMEM((n + 16, n), BF16), pltpu.SMEM((2,), I32)],
        compiler_params=pltpu.CompilerParams(vmem_limit_bytes=12 * MIB),
        cost_estimate=pl.CostEstimate(
            flops=2 * count * n * n * n, bytes_accessed=4 * blocks.size, transcendentals=0
        ),
        name="prep",
    )(ids, own, col, blocks)


def apply_kernel(recur, mate, *refs):
    refs = list(refs)
    ids_ref, src_ref, row_ref, num_ref, w_ref, inv_ref = refs[:6]
    panels = refs[6:10]
    del refs[:10]
    olds = [refs.pop(0) for _ in range(2 if recur else 0)]
    mates = [refs.pop(0) for _ in range(2 if mate else 0)]
    outs = [refs.pop(0) for _ in range(2)]
    parts = refs[:-2]
    sp_ref, acc_ref = refs[-2:]
    half, kk, n = panels[0].shape
    for i, ref in enumerate(panels):
        v = ref[...]
        high = v.astype(BF16)
        sp_ref[i * half:(i + 1) * half, :kk] = high
        sp_ref[i * half:(i + 1) * half, kk:] = (v - high.astype(F32)).astype(BF16)
    acc_ref[...] = jnp.zeros(acc_ref.shape, F32)

    def group(g, c):
        for u in range(UNROLL):
            p = g * UNROLL + u
            piece = jnp.concatenate([sp_ref[src_ref[2 * p]], sp_ref[src_ref[2 * p + 1]]], axis=1)
            w = w_ref[pl.ds(2 * p, 2)].reshape(2 * n, 2 * n)
            y = jnp.dot(piece, w, preferred_element_type=F32)
            r = row_ref[p]
            acc_ref[r] = acc_ref[r] + ((y[:kk, :n] + y[kk:, :n]) + (y[:kk, n:] + y[kk:, n:]))
        return c

    lax.fori_loop(0, num_ref[0], group, 0)
    scale = (2.0 if recur else 1.0) / half_width
    for i in range(2):
        span = slice(i * half, (i + 1) * half)
        now = panels[i][...]
        image = (now - acc_ref[span] * inv_ref[span] - center * now) * scale
        if recur:
            image = image - olds[i][...]
        outs[i][...] = image
        if mate:
            acc_ref[span] = image
            sp_ref2 = parts[-1]
            sp_ref2[span] = mates[i][...]
    if mate:
        count = len(parts) - 1
        me = ids_ref[1]
        each = 2 * half // count
        for s in range(count):
            at = pl.ds((me ^ s) * each, each)
            parts[s][:, :kk] = parts[-1][at]
            parts[s][:, kk:] = acc_ref[at]


def apply(ids, meta, pair, halo, old=(), mate=(), count=0):
    half, kk, n = pair[0].shape
    w = meta[3]
    out = [jax.ShapeDtypeStruct((half, kk, n), F32)] * 2
    if mate:
        out += [jax.ShapeDtypeStruct((2 * half // count, 2 * kk, n), F32)] * count
    args = (*pair, *halo, *old, *mate)
    scratch = [pltpu.VMEM((4 * half, 2 * kk, n), BF16), pltpu.VMEM((2 * half + 1, kk, n), F32)]
    if mate:
        scratch = [pltpu.VMEM((2 * half, kk, n), F32)] + scratch
    res = pl.pallas_call(
        functools.partial(apply_kernel, bool(old), bool(mate)),
        in_specs=[IN_SMEM] * 4 + [IN_VMEM] * (2 + len(args)),
        out_specs=[IN_VMEM] * len(out),
        out_shape=out,
        scratch_shapes=scratch,
        compiler_params=pltpu.CompilerParams(vmem_limit_bytes=12 * MIB),
        cost_estimate=pl.CostEstimate(
            flops=8 * w.shape[0] * n * n * kk, bytes_accessed=2 * w.size, transcendentals=0
        ),
        name="apply" + "_recur" * bool(old) + "_parts" * bool(mate),
    )(ids, *meta, *args)
    return tuple(res[:2]), tuple(res[2:])


def factor_kernel(nodes, g_ref, out_ref, both_ref):
    n = g_ref.shape[0]
    p = 8
    lines = lax.broadcasted_iota(I32, (n, n), 0)
    lanes = lax.broadcasted_iota(I32, (n, n), 1)
    both_ref[:, :n] = g_ref[...] * (1.0 / nodes)
    both_ref[:, n:] = jnp.where(lines == lanes, 1.0, 0.0).astype(F32)
    sub = lax.broadcasted_iota(I32, (p, n), 0)
    for j in range(0, n, p):
        left = both_ref[j:j + p, :n]
        right = both_ref[j:j + p, n:]
        cols = [jnp.broadcast_to(left[:, j + i:j + i + 1], (p, n)) for i in range(p)]
        pivot = jnp.zeros((p, n), F32)
        for i in range(p):
            own = jnp.broadcast_to(cols[i][i:i + 1], (p, n))
            pivot = jnp.where(sub == i, own, pivot)
            if i + 1 < p:
                ratio = jnp.where(sub > i, cols[i] / own, 0.0)
                for k in range(i + 1, p):
                    cols[k] = cols[k] - ratio * jnp.broadcast_to(cols[k][i:i + 1], (p, n))
                left = left - ratio * jnp.broadcast_to(left[i:i + 1], (p, n))
                right = right - ratio * jnp.broadcast_to(right[i:i + 1], (p, n))
        root = lax.rsqrt(pivot)
        left = left * root
        right = right * root
        out_ref[j:j + p] = right
        if j + p < n:
            change = tn(left, jnp.concatenate([left, right], axis=1))
            both_ref[j + p:] = both_ref[j + p:] - change[j + p:]


def inverse_factor(gram, nodes):
    n = gram.shape[0]
    return call(
        functools.partial(factor_kernel, nodes), "factor", [(n, n)], gram,
        scratch=[pltpu.VMEM((n, 2 * n), F32)],
    )[0]


def gathered(ids_ref, parts, b, x_ref):
    each = parts[0].shape[1]
    me = ids_ref[1]
    for s, part in enumerate(parts):
        x_ref[b, pl.ds(pl.multiple_of((me ^ s) * each, each), each)] = part[b]
    return x_ref[b]


def gram_kernel(ids_ref, *refs):
    parts, (f_ref, g_ref) = refs[:-2], refs[-2:]
    total = jnp.zeros(g_ref.shape, F32)
    for b in range(f_ref.shape[0]):
        f = gathered(ids_ref, parts, b, f_ref)
        total = total + nt(f, f)
    g_ref[...] = total


def cross_kernel(ids_ref, f_ref, *refs):
    parts, (k_ref, x_ref) = refs[:-2], refs[-2:]
    total = jnp.zeros(k_ref.shape, F32)
    for b in range(f_ref.shape[0]):
        total = total + nt(f_ref[b], gathered(ids_ref, parts, b, x_ref))
    k_ref[...] = total


def turn_kernel(ids_ref, inv_ref, *refs):
    parts, (f_ref, g_ref, x_ref) = refs[:-3], refs[-3:]
    total = jnp.zeros(g_ref.shape, F32)
    for b in range(f_ref.shape[0]):
        f = nn(inv_ref[...], gathered(ids_ref, parts, b, x_ref))
        f_ref[b] = f
        total = total + nt(f, f)
    g_ref[...] = total


def turn_cross_kernel(ids_ref, inv_ref, f_ref, *refs):
    parts, (k_ref, x_ref) = refs[:-2], refs[-2:]
    total = jnp.zeros(k_ref.shape, F32)
    for b in range(f_ref.shape[0]):
        z = nn(inv_ref[...], gathered(ids_ref, parts, b, x_ref))
        total = total + nt(f_ref[b], z)
    k_ref[...] = total


def basis_kernel(ids_ref, inv_ref, f_ref, *refs):
    parts, x_ref = refs[:-1], refs[-1]
    each = parts[0].shape[1]
    me = ids_ref[1]
    for b in range(f_ref.shape[0]):
        x_ref[b] = nn(inv_ref[...], f_ref[b])
        for s, part in enumerate(parts):
            part[b] = x_ref[b, pl.ds(pl.multiple_of((me ^ s) * each, each), each)]


def proj_kernel(nodes, ids_ref, *refs):
    pairs = len(refs[:6]) // 3
    parts, x_ref = refs[6:-1], refs[-1]
    each = parts[0].shape[1]
    me = ids_ref[1]
    for i in range(pairs):
        inv_ref, k_ref, g_ref = refs[3 * i:3 * i + 3]
        image = (half_width * k_ref[...] + center * g_ref[...]) * (1.0 / nodes)
        x_ref[...] = nt(nn(inv_ref[...], image), inv_ref[...])
        for s, part in enumerate(parts):
            part[i] = x_ref[pl.ds(pl.multiple_of((me ^ s) * each, each), each)]


def slot_row(slot, half, odd):
    return slot + half * (1 - odd) * jnp.where(slot >= half, -1, 1)


def split_kernel(ids_ref, start_ref, *outs):
    half, kk, n = outs[0].shape
    odd = ids_ref[0] % 2
    for slot in range(2 * half):
        row = slot_row(slot, half, odd)
        piece = start_ref[:, pl.ds(pl.multiple_of(row * n, n), n)]
        for i in range(2):
            outs[2 * i + slot // half][slot % half] = piece[i * kk:(i + 1) * kk]


def join_kernel(half, ids_ref, *refs):
    parts, out_ref = refs[:-1], refs[-1]
    each, _, n = parts[0].shape
    odd = ids_ref[0] % 2
    me = ids_ref[1]
    for s, part in enumerate(parts):
        for b in range(each):
            row = slot_row((me ^ s) * each + b, half, odd)
            out_ref[:, pl.ds(pl.multiple_of(row * n, n), n)] = part[b]


def exchange(pair):
    count = lax.axis_size("node")
    even = [(i, i ^ 1) for i in range(count)]
    odd = [(i, (i - 1 if i % 2 == 0 else i + 1) % count) for i in range(count)]
    return lax.ppermute(pair[0], "node", even), lax.ppermute(pair[1], "node", odd)


def swap(value, axis, hop):
    return lax.ppermute(value, axis, [(i, i ^ hop) for i in range(lax.axis_size(axis))])


def swapped(parts):
    return [parts[0]] + [swap(parts[s], "col", s) for s in range(1, len(parts))]


def summed(value, *axes):
    for axis in axes:
        hop = 1
        while hop < lax.axis_size(axis):
            value = value + swap(value, axis, hop)
            hop *= 2
    return value


def body(blocks, owner_row, block_col, start):
    cols_here, width = start.shape
    block = blocks.shape[1]
    slots = width // block
    half = slots // 2
    count = lax.axis_size("col")
    nodes = width * lax.axis_size("node")
    vecs = cols_here * count
    each = cols_here // 2
    quarter = slots // count
    square = (vecs, vecs)
    wide = (quarter, vecs, block)
    held = pltpu.VMEM(wide, F32)
    ids = jnp.stack([lax.axis_index("node"), lax.axis_index("col")]).astype(I32)

    halves = call(split_kernel, "split", [(half, each, block)] * 4, ids, start, scalars=1)
    before = [tuple(halves[:2]), tuple(halves[2:])]
    w, inv, src, row, num = prep(ids, owner_row, block_col, blocks, slots)
    meta = (src, row, num, w, inv)

    def advance(now, before=((), ()), parts=False):
        first, _ = apply(ids, meta, now[0], exchange(now[0]), before[0])
        mate = first if parts else ()
        second, out = apply(ids, meta, now[1], exchange(now[1]), before[1], mate, count)
        return [first, second], (swapped(out) if parts else None)

    now, _ = advance(before)
    for step in range(DEGREE - 1):
        after, parts = advance(now, before, step == DEGREE - 2)
        before, now = now, after
    panel, gram_first = call(gram_kernel, "gram", [wide, square], ids, *parts, scalars=1)
    gram = summed(gram_first, "col", "node")
    after, parts = advance(now, parts=True)
    before, now = now, after
    (cross_first,) = call(
        cross_kernel, "cross", [square], ids, panel, *parts, scalars=1, scratch=[held]
    )
    inverse_first = inverse_factor(gram, nodes)
    for step in range(DEGREE - 1):
        if step == DEGREE - 2:
            now, inverse_first = lax.optimization_barrier((now, inverse_first))
        after, parts = advance(now, before, step == DEGREE - 2)
        before, now = now, after

    turned, gram_last = call(
        turn_kernel, "turn", [wide, square], ids, inverse_first, *parts, scalars=1, scratch=[held]
    )
    gram = summed(gram_last, "col", "node")
    _, parts = advance(now, parts=True)
    (cross_last,) = call(
        turn_cross_kernel, "turn_cross", [square], ids, inverse_first, turned, *parts,
        scalars=1, scratch=[held],
    )
    inverse_last = inverse_factor(gram, nodes)
    parts = call(
        basis_kernel, "basis", [(quarter, cols_here, block)] * count, ids, inverse_last, turned,
        scalars=1, scratch=[held],
    )
    (basis,) = call(
        functools.partial(join_kernel, half), "join", [(cols_here, width)], ids, *swapped(parts), scalars=1
    )
    parts = call(
        functools.partial(proj_kernel, nodes), "proj", [(2, cols_here, vecs)] * count, ids,
        inverse_first, cross_first, gram_first, inverse_last, cross_last, gram_last,
        scalars=1, scratch=[pltpu.VMEM(square, F32)],
    )
    projected = summed(sum(swapped(parts)), "node")
    return basis, projected[0], projected[1]


def solution(mesh):
    placed = (P("node", None, None), P("node", None), P("node", None), P("col", "node"))
    return jax.shard_map(
        body,
        mesh=mesh,
        in_specs=placed,
        out_specs=(P("col", "node"), P("col", None), P("col", None)),
        check_vma=False,
    )
```

time: 1230 us -> 320 us (0.26)
  waiting for transfers between devices: 629 us -> 45.3 us
  matrix products: 351 us -> 0 us
  Pallas kernels: 0 us -> 161 us
  other arithmetic: 73.4 us -> 0.2 us
  blocking collectives: 59.6 us -> 0 us
  starting transfers between devices: 50.8 us -> 86.5 us
  local copies, waits for them, and re-layouts: 48.3 us -> 24.7 us
  between operations: 14.8 us -> 1.2 us
    psum x3 -> x0, waiting for transfers between devices: 351 us -> none  [the longest x2 230 us: body(): gram = lax.psum(gram_part, ('node', 'col'))]
    dot_general x23 -> x0, matrix products: 349 us -> none  [the longest x9 299 us: operate(): product = jnp.einsum('nij,knj->nki', blocks, gathered, precision=precise)]
    ppermute x18 -> x67, waiting for transfers between devices: 269 us -> 45.3 us  [the longest x31 35.5 us: swap(): lax.ppermute(value, axis, [(i, i ^ hop) for i in range(lax.axis_size(axis...]
    pallas_call x0 -> x29, Pallas kernels: none -> 161 us  [the longest x18 117 us: apply(): pl.pallas_call(functools.partial(apply_kernel, bool(old), bool(mate)), in...]
    all_to_all x4 -> x0, blocking collectives: 59.6 us -> none  [the longest x2 30.8 us: body(): lax.all_to_all(rows_basis, 'col', split_axis=0, concat_axis=1, tiled=True)]
    another operation x10 -> x1, other arithmetic: 45.7 us -> 0.08 us  [body(): ids = jnp.stack([lax.axis_index('node'), lax.axis_index('col')]).astype(I32)]
    ppermute x18 -> x67, starting transfers between devices: 42.6 us -> 86.5 us  [the longest x18 42 us: exchange(): lax.ppermute(pair[1], 'node', odd)]
    gather x9 -> x0, local copies, waits for them, and re-layouts: 31.3 us -> none  [operate(): gathered = jnp.take(pieces, lookup, axis=1)]
  transfers between devices with their start and end apart: 23 -> 67, of which waited for: 21 -> 14; matrix products, arithmetic and copies ran while one was open for 5% -> 0% of each run, Pallas kernels for 0% -> 43%
where the time goes in v2:
time: 320 us; the launch traced here: 319 us
  Pallas kernels  161 us (50%)
  starting transfers between devices  86.5 us (27%)
  waiting for transfers between devices  45.3 us (14%)
  local copies, waits for them, and re-layouts  24.7 us (8%)
    pallas_call x18, Pallas kernels, apply(): pl.pallas_call(functools.partial(apply_kernel, bool(old), bool(mate)), in...  117 us
    ppermute x18, starting transfers between devices, exchange(): lax.ppermute(pair[1], 'node', odd)  42 us
    ppermute x31, waiting for transfers between devices, swap(): lax.ppermute(value, axis, [(i, i ^ hop) for i in range(lax.axis_size(axis...  35.5 us
    pallas_call x10, Pallas kernels, call(): pl.pallas_call(kernel, in_specs=[IN_SMEM] * scalars + [IN_VMEM] * (len(ar...  33.9 us
    ppermute x31, starting transfers between devices, swap(): lax.ppermute(value, axis, [(i, i ^ hop) for i in range(lax.axis_size(axis...  29.6 us
    unnamed x24, local copies, waits for them, and re-layouts  24 us
    ppermute x18, starting transfers between devices, exchange(): lax.ppermute(pair[0], 'node', even)  14.9 us
    pallas_call x1, Pallas kernels, prep(): pl.pallas_call(functools.partial(prep_kernel, rows), grid=(count // chunk...  11.1 us
  transfers between devices with their start and end apart: 67, of which 14 were waited for; matrix products, arithmetic and copies ran while one was open for 0% of the time, Pallas kernels for 43%

profile of v2, /device:TPU:0, one launch (start us, length us, event | category | flops | bytes accessed | tf_op | source)
XLA Modules:
  0.0 319.3 jit_solution(940649812630174964)
XLA Ops:
  2.5 3.0 collective-permute-start
  5.5 3.5 %collective-permute-start.1 = (f32[24,16,128]{2,1,0:T(8,128)S(1)}, f32[24,16,128]{2,1,0:T(8,128)S(1)}, u32[]{:S(2)}, u32[]{:S(2)}) collective-permute-start(f32[24,16,128]{2,1,0:T(8,128)S(1)} %get-tuple-element.85.refs_7_.refs_11_), channel_id=1, source_target_pairs={{0,28},{4,8},{8,4},{12,16},{16,12},{20,24},{24,20},{28,0},{1,29},{... | collective-permute-start | bytes 589832 | tf_op jit(solution)/shard_map/ppermute | solution.py:349
  11.0 6.4 %copy-done.2 = f32[288,128,128]{2,1,0:T(8,128)S(1)} copy-done((f32[288,128,128]{2,1,0:T(8,128)S(1)}, f32[288,128,128]{2,1,0:T(8,128)}, u32[]{:S(2)}) %copy-start.2) | copy-done | bytes 18874392
  18.7 11.1 %prep.1 = (bf16[352,128,256]{2,1,0:T(8,128)(2,1)S(1)}, f32[48,1,128]{2,1,0:T(1,128)S(1)}, s32[352]{0:T(512)S(1)}, s32[176]{0:T(256)S(1)}, s32[1]{0:T(128)}) custom-call(s32[2]{0:T(128)S(1)} %pad_add_fusion.ids_ref.refs_0_, s32[1,288]{1,0:T(1,128)S(1)} %copy-done.4, s32[1,288]{1,0:T(1,128)S(1)} %copy-done.5, f32[288,128,128]{2,1,0:T(8,128)S(1)} %copy-done.2), custom_call_target="tpu_custom_call" | custom-call | flops 1207959552 | bytes 18874368 | tf_op jit(solution)/shard_map/prep/pallas_call | solution.py:119
  29.8 7.6 %copy-done = bf16[352,128,256]{2,1,0:T(8,128)(2,1)} copy-done((bf16[352,128,256]{2,1,0:T(8,128)(2,1)}, bf16[352,128,256]{2,1,0:T(8,128)(2,1)S(1)}, u32[]{:S(2)}) %copy-start) | copy-done | bytes 23068696
  37.4 7.6 %copy-done.1 = bf16[352,128,256]{2,1,0:T(8,128)(2,1)S(1)} copy-done((bf16[352,128,256]{2,1,0:T(8,128)(2,1)S(1)}, bf16[352,128,256]{2,1,0:T(8,128)(2,1)}, u32[]{:S(2)}) %copy-start.1) | copy-done | bytes 23068696
  45.0 6.3 %apply.4 = (f32[24,16,128]{2,1,0:T(8,128)S(1)}, f32[24,16,128]{2,1,0:T(8,128)S(1)}) custom-call(s32[2]{0:T(128)S(1)} %pad_add_fusion.ids_ref.refs_0_, s32[352]{0:T(512)S(1)} %get-tuple-element.79.refs_1_, s32[176]{0:T(256)S(1)} %get-tuple-element.80.refs_2_, s32[1]{0:T(128)} %get-tuple-element.81.refs_3_, bf16[352,128,256]{2,1,0:T(8,128)(2,1)S(1)} %copy-done.1, ...), custom_call_target="tpu_custom_call" | custom-call | flops 738197504 | bytes 23068672 | tf_op jit(solution)/shard_map/apply/pallas_call | solution.py:199
  52.0 2.3 collective-permute-start.3
  54.3 6.3 %apply.6 = (f32[24,16,128]{2,1,0:T(8,128)S(1)}, f32[24,16,128]{2,1,0:T(8,128)S(1)}) custom-call(s32[2]{0:T(128)S(1)} %pad_add_fusion.ids_ref.refs_0_, s32[352]{0:T(512)S(1)} %get-tuple-element.79.refs_1_, s32[176]{0:T(256)S(1)} %get-tuple-element.80.refs_2_, s32[1]{0:T(128)} %get-tuple-element.81.refs_3_, bf16[352,128,256]{2,1,0:T(8,128)(2,1)S(1)} %copy-done.1, ...), custom_call_target="tpu_custom_call" | custom-call | flops 738197504 | bytes 23068672 | tf_op jit(solution)/shard_map/apply/pallas_call | solution.py:199
  63.2 6.3 %apply_recur.10 = (f32[24,16,128]{2,1,0:T(8,128)S(1)}, f32[24,16,128]{2,1,0:T(8,128)S(1)}) custom-call(s32[2]{0:T(128)S(1)} %pad_add_fusion.ids_ref.refs_0_, s32[352]{0:T(512)S(1)} %get-tuple-element.79.refs_1_, s32[176]{0:T(256)S(1)} %get-tuple-element.80.refs_2_, s32[1]{0:T(128)} %get-tuple-element.81.refs_3_, bf16[352,128,256]{2,1,0:T(8,128)(2,1)S(1)} %copy-done.1, ...), custom_call_target="tpu_custom_call" | custom-call | flops 738197504 | bytes 23068672 | tf_op jit(solution)/shard_map/apply_recur/pallas_call | solution.py:199
  69.6 3.5 %collective-permute-start.5 = (f32[24,16,128]{2,1,0:T(8,128)S(1)}, f32[24,16,128]{2,1,0:T(8,128)S(1)}, u32[]{:S(2)}, u32[]{:S(2)}) collective-permute-start(f32[24,16,128]{2,1,0:T(8,128)S(1)} %get-tuple-element.89.refs_7_.refs_11_), channel_id=1, source_target_pairs={{0,28},{4,8},{8,4},{12,16},{16,12},{20,24},{24,20},{28,0},{1,29},{... | collective-permute-start | bytes 589832 | tf_op jit(solution)/shard_map/ppermute | solution.py:349
  73.1 6.3 %apply_recur.15 = (f32[24,16,128]{2,1,0:T(8,128)S(1)}, f32[24,16,128]{2,1,0:T(8,128)S(1)}) custom-call(s32[2]{0:T(128)S(1)} %pad_add_fusion.ids_ref.refs_0_, s32[352]{0:T(512)S(1)} %get-tuple-element.79.refs_1_, s32[176]{0:T(256)S(1)} %get-tuple-element.80.refs_2_, s32[1]{0:T(128)} %get-tuple-element.81.refs_3_, bf16[352,128,256]{2,1,0:T(8,128)(2,1)S(1)} %copy-done.1, ...), custom_call_target="tpu_custom_call" | custom-call | flops 738197504 | bytes 23068672 | tf_op jit(solution)/shard_map/apply_recur/pallas_call | solution.py:199
  81.4 6.3 %apply_recur.11 = (f32[24,16,128]{2,1,0:T(8,128)S(1)}, f32[24,16,128]{2,1,0:T(8,128)S(1)}) custom-call(s32[2]{0:T(128)S(1)} %pad_add_fusion.ids_ref.refs_0_, s32[352]{0:T(512)S(1)} %get-tuple-element.79.refs_1_, s32[176]{0:T(256)S(1)} %get-tuple-element.80.refs_2_, s32[1]{0:T(128)} %get-tuple-element.81.refs_3_, bf16[352,128,256]{2,1,0:T(8,128)(2,1)S(1)} %copy-done.1, ...), custom_call_target="tpu_custom_call" | custom-call | flops 738197504 | bytes 23068672 | tf_op jit(solution)/shard_map/apply_recur/pallas_call | solution.py:199
  88.5 2.3 collective-permute-start.7
  90.8 6.3 %apply_recur.16 = (f32[24,16,128]{2,1,0:T(8,128)S(1)}, f32[24,16,128]{2,1,0:T(8,128)S(1)}) custom-call(s32[2]{0:T(128)S(1)} %pad_add_fusion.ids_ref.refs_0_, s32[352]{0:T(512)S(1)} %get-tuple-element.79.refs_1_, s32[176]{0:T(256)S(1)} %get-tuple-element.80.refs_2_, s32[1]{0:T(128)} %get-tuple-element.81.refs_3_, bf16[352,128,256]{2,1,0:T(8,128)(2,1)S(1)} %copy-done.1, ...), custom_call_target="tpu_custom_call" | custom-call | flops 738197504 | bytes 23068672 | tf_op jit(solution)/shard_map/apply_recur/pallas_call | solution.py:199
  99.7 6.4 %apply_recur.12 = (f32[24,16,128]{2,1,0:T(8,128)S(1)}, f32[24,16,128]{2,1,0:T(8,128)S(1)}) custom-call(s32[2]{0:T(128)S(1)} %pad_add_fusion.ids_ref.refs_0_, s32[352]{0:T(512)S(1)} %get-tuple-element.79.refs_1_, s32[176]{0:T(256)S(1)} %get-tuple-element.80.refs_2_, s32[1]{0:T(128)} %get-tuple-element.81.refs_3_, bf16[352,128,256]{2,1,0:T(8,128)(2,1)S(1)} %copy-done.1, ...), custom_call_target="tpu_custom_call" | custom-call | flops 738197504 | bytes 23068672 | tf_op jit(solution)/shard_map/apply_recur/pallas_call | solution.py:199
  106.2 3.4 %collective-permute-start.9 = (f32[24,16,128]{2,1,0:T(8,128)S(1)}, f32[24,16,128]{2,1,0:T(8,128)S(1)}, u32[]{:S(2)}, u32[]{:S(2)}) collective-permute-start(f32[24,16,128]{2,1,0:T(8,128)S(1)} %get-tuple-element.93.refs_7_.refs_11_.refs_13_), channel_id=1, source_target_pairs={{0,28},{4,8},{8,4},{12,16},{16,12},{20,24},{24,20},{28,0},{1,29},{... | collective-permute-start | bytes 589832 | tf_op jit(solution)/shard_map/ppermute | solution.py:349
  109.6 6.7 %apply_recur_parts.2 = (f32[24,16,128]{2,1,0:T(8,128)S(1)}, f32[24,16,128]{2,1,0:T(8,128)S(1)}, f32[12,32,128]{2,1,0:T(8,128)S(1)}, f32[12,32,128]{2,1,0:T(8,128...) custom-call(s32[2]{0:T(128)S(1)} %pad_add_fusion.ids_ref.refs_0_, s32[352]{0:T(512)S(1)} %get-tuple-element.79.refs_1_, ...), custom_call_target="tpu_custom_call" | custom-call | flops 738197504 | bytes 23068672 | tf_op jit(solution)/shard_map/apply_recur_parts/pallas_call | solution.py:199
  120.2 7.1 %apply.5 = (f32[24,16,128]{2,1,0:T(8,128)S(1)}, f32[24,16,128]{2,1,0:T(8,128)S(1)}) custom-call(s32[2]{0:T(128)S(1)} %pad_add_fusion.ids_ref.refs_0_, s32[352]{0:T(512)S(1)} %get-tuple-element.79.refs_1_, s32[176]{0:T(256)S(1)} %get-tuple-element.80.refs_2_, s32[1]{0:T(128)} %get-tuple-element.81.refs_3_, bf16[352,128,256]{2,1,0:T(8,128)(2,1)S(1)} %copy-done.1, ...), custom_call_target="tpu_custom_call" | custom-call | flops 738197504 | bytes 23068672 | tf_op jit(solution)/shard_map/apply/pallas_call | solution.py:199
  128.0 2.2 collective-permute-start.11
  132.4 6.5 %apply_parts.2 = (f32[24,16,128]{2,1,0:T(8,128)S(1)}, f32[24,16,128]{2,1,0:T(8,128)S(1)}, f32[12,32,128]{2,1,0:T(8,128)S(1)}, f32[12,32,128]{2,1,0:T(8,128)S(1)}...) custom-call(s32[2]{0:T(128)S(1)} %pad_add_fusion.ids_ref.refs_0_, s32[352]{0:T(512)S(1)} %get-tuple-element.79.refs_1_, ...), custom_call_target="tpu_custom_call" | custom-call | flops 738197504 | bytes 23068672 | tf_op jit(solution)/shard_map/apply_parts/pallas_call | solution.py:199
  143.0 2.8 collective-permute-done.32
  146.4 6.3 %apply_recur.13 = (f32[24,16,128]{2,1,0:T(8,128)S(1)}, f32[24,16,128]{2,1,0:T(8,128)S(1)}) custom-call(s32[2]{0:T(128)S(1)} %pad_add_fusion.ids_ref.refs_0_, s32[352]{0:T(512)S(1)} %get-tuple-element.79.refs_1_, s32[176]{0:T(256)S(1)} %get-tuple-element.80.refs_2_, s32[1]{0:T(128)} %get-tuple-element.81.refs_3_, bf16[352,128,256]{2,1,0:T(8,128)(2,1)S(1)} %bitcast.7, ...), custom_call_target="tpu_custom_call" | custom-call | flops 738197504 | bytes 23068672 | tf_op jit(solution)/shard_map/apply_recur/pallas_call | solution.py:199
  154.3 2.7 collective-permute-start.13
  157.1 6.5 %apply_recur.17 = (f32[24,16,128]{2,1,0:T(8,128)S(1)}, f32[24,16,128]{2,1,0:T(8,128)S(1)}) custom-call(s32[2]{0:T(128)S(1)} %pad_add_fusion.ids_ref.refs_0_, s32[352]{0:T(512)S(1)} %get-tuple-element.79.refs_1_, s32[176]{0:T(256)S(1)} %get-tuple-element.80.refs_2_, s32[1]{0:T(128)} %get-tuple-element.81.refs_3_, bf16[352,128,256]{2,1,0:T(8,128)(2,1)S(1)} %bitcast.7, ...), custom_call_target="tpu_custom_call" | custom-call | flops 738197504 | bytes 23068672 | tf_op jit(solution)/shard_map/apply_recur/pallas_call | solution.py:199
  164.0 2.5 collective-permute-start.27
  168.7 5.2 %collective-permute-done.35 = f32[128,128]{1,0:T(8,128)S(1)} collective-permute-done((f32[128,128]{1,0:T(8,128)S(1)}, f32[128,128]{1,0:T(8,128)S(1)}, u32[]{:S(2)}, u32[]{:S(2)}) %collective-permute-start.35) | collective-permute-done | bytes 65568 | tf_op jit(solution)/shard_map/ppermute | solution.py:353
  173.9 8.5 %factor.2.inv_ref.refs_0_ = f32[128,128]{1,0:T(8,128)S(1)} custom-call(f32[128,128]{1,0:T(8,128)S(1)} %add.52.g_ref), custom_call_target="tpu_custom_call" | custom-call | tf_op jit(solution)/shard_map/factor/pallas_call | solution.py:38
  182.4 6.3 %apply_recur.14 = (f32[24,16,128]{2,1,0:T(8,128)S(1)}, f32[24,16,128]{2,1,0:T(8,128)S(1)}) custom-call(s32[2]{0:T(128)S(1)} %pad_add_fusion.ids_ref.refs_0_, s32[352]{0:T(512)S(1)} %get-tuple-element.79.refs_1_, s32[176]{0:T(256)S(1)} %get-tuple-element.80.refs_2_, s32[1]{0:T(128)} %get-tuple-element.81.refs_3_, bf16[352,128,256]{2,1,0:T(8,128)(2,1)S(1)} %bitcast.7, ...), custom_call_target="tpu_custom_call" | custom-call | flops 738197504 | bytes 23068672 | tf_op jit(solution)/shard_map/apply_recur/pallas_call | solution.py:199
  188.8 6.3 %apply_recur.18 = (f32[24,16,128]{2,1,0:T(8,128)S(1)}, f32[24,16,128]{2,1,0:T(8,128)S(1)}) custom-call(s32[2]{0:T(128)S(1)} %pad_add_fusion.ids_ref.refs_0_, s32[352]{0:T(512)S(1)} %get-tuple-element.79.refs_1_, s32[176]{0:T(256)S(1)} %get-tuple-element.80.refs_2_, s32[1]{0:T(128)} %get-tuple-element.81.refs_3_, bf16[352,128,256]{2,1,0:T(8,128)(2,1)S(1)} %bitcast.7, ...), custom_call_target="tpu_custom_call" | custom-call | flops 738197504 | bytes 23068672 | tf_op jit(solution)/shard_map/apply_recur/pallas_call | solution.py:199
  196.2 2.3 collective-permute-start.39
  198.4 2.5 collective-permute-start.37
  200.9 9.6 %collective-permute-done.38.refs_8_ = f32[24,16,128]{2,1,0:T(8,128)S(1)} collective-permute-done((f32[24,16,128]{2,1,0:T(8,128)S(1)}, f32[24,16,128]{2,1,0:T(8,128)S(1)}, u32[]{:S(2)}, u32[]{:S(2)}) %collective-permute-start.38) | collective-permute-done | bytes 196640 | tf_op jit(solution)/shard_map/ppermute | solution.py:349
  210.5 6.3 %apply_recur.19 = (f32[24,16,128]{2,1,0:T(8,128)S(1)}, f32[24,16,128]{2,1,0:T(8,128)S(1)}) custom-call(s32[2]{0:T(128)S(1)} %pad_add_fusion.ids_ref.refs_0_, s32[352]{0:T(512)S(1)} %get-tuple-element.79.refs_1_, s32[176]{0:T(256)S(1)} %get-tuple-element.80.refs_2_, s32[1]{0:T(128)} %get-tuple-element.81.refs_3_, bf16[352,128,256]{2,1,0:T(8,128)(2,1)S(1)} %bitcast.7, ...), custom_call_target="tpu_custom_call" | custom-call | flops 738197504 | bytes 23068672 | tf_op jit(solution)/shard_map/apply_recur/pallas_call | solution.py:199
  216.9 6.5 %apply_recur_parts.3 = (f32[24,16,128]{2,1,0:T(8,128)S(1)}, f32[24,16,128]{2,1,0:T(8,128)S(1)}, f32[12,32,128]{2,1,0:T(8,128)S(1)}, f32[12,32,128]{2,1,0:T(8,128...) custom-call(s32[2]{0:T(128)S(1)} %pad_add_fusion.ids_ref.refs_0_, s32[352]{0:T(512)S(1)} %get-tuple-element.79.refs_1_, ...), custom_call_target="tpu_custom_call" | custom-call | flops 738197504 | bytes 23068672 | tf_op jit(solution)/shard_map/apply_recur_parts/pallas_call | solution.py:199
  231.2 3.3 %collective-permute-done.42.refs_3_ = f32[12,32,128]{2,1,0:T(8,128)S(1)} collective-permute-done((f32[12,32,128]{2,1,0:T(8,128)S(1)}, f32[12,32,128]{2,1,0:T(8,128)S(1)}, u32[]{:S(2)}, u32[]{:S(2)}) %collective-permute-start.42) | collective-permute-done | bytes 196640 | tf_op jit(solution)/shard_map/ppermute | solution.py:353
  234.5 4.0 %turn.1 = (f32[12,128,128]{2,1,0:T(8,128)S(1)}, f32[128,128]{1,0:T(8,128)S(1)}) custom-call(s32[2]{0:T(128)S(1)} %pad_add_fusion.ids_ref.refs_0_, f32[128,128]{1,0:T(8,128)S(1)} %factor.2.inv_ref.refs_0_, f32[12,32,128]{2,1,0:T(8,128)S(1)} %get-tuple-element.128.refs_0_, f32[12,32,128]{2,1,0:T(8,128)S(1)} %collective-permute-done.40.refs_1_, ...), custom_call_target="tpu_custom_call" | custom-call | tf_op jit(solution)/shard_map/turn/pallas_call | solution.py:38
  244.7 2.8 collective-permute-done.44
  249.1 6.3 %apply.7 = (f32[24,16,128]{2,1,0:T(8,128)S(1)}, f32[24,16,128]{2,1,0:T(8,128)S(1)}) custom-call(s32[2]{0:T(128)S(1)} %pad_add_fusion.ids_ref.refs_0_, s32[352]{0:T(512)S(1)} %get-tuple-element.79.refs_1_, s32[176]{0:T(256)S(1)} %get-tuple-element.80.refs_2_, s32[1]{0:T(128)} %get-tuple-element.81.refs_3_, bf16[352,128,256]{2,1,0:T(8,128)(2,1)S(1)} %bitcast.7, ...), custom_call_target="tpu_custom_call" | custom-call | flops 738197504 | bytes 23068672 | tf_op jit(solution)/shard_map/apply/pallas_call | solution.py:199
  255.9 7.3 %apply_parts.3 = (f32[24,16,128]{2,1,0:T(8,128)}, f32[24,16,128]{2,1,0:T(8,128)}, f32[12,32,128]{2,1,0:T(8,128)S(1)}, f32[12,32,128]{2,1,0:T(8,128)S(1)}, f32[12...) custom-call(s32[2]{0:T(128)S(1)} %pad_add_fusion.ids_ref.refs_0_, s32[352]{0:T(512)S(1)} %get-tuple-element.79.refs_1_, ...), custom_call_target="tpu_custom_call" | custom-call | flops 738197504 | bytes 23068672 | tf_op jit(solution)/shard_map/apply_parts/pallas_call | solution.py:199
  265.1 3.6 %collective-permute-start.47 = (f32[128,128]{1,0:T(8,128)S(1)}, f32[128,128]{1,0:T(8,128)S(1)}, u32[]{:S(2)}, u32[]{:S(2)}) collective-permute-start(f32[128,128]{1,0:T(8,128)S(1)} %add.56), channel_id=1, source_target_pairs={{0,16},{4,20},{8,24},{12,28},{16,0},{20,4},{24,8},{28,12},{1,17},{... | collective-permute-start | bytes 196616 | tf_op jit(solution)/shard_map/ppermute | solution.py:353
  271.3 2.8 collective-permute-done.60.refs_3_
  274.1 4.0 %turn_cross.1.refs_4_ = f32[128,128]{1,0:T(8,128)S(1)} custom-call(s32[2]{0:T(128)S(1)} %pad_add_fusion.ids_ref.refs_0_, f32[128,128]{1,0:T(8,128)S(1)} %factor.2.inv_ref.refs_0_, f32[12,128,128]{2,1,0:T(8,128)S(1)} %get-tuple-element.133.f_ref, f32[12,32,128]{2,1,0:T(8,128)S(1)} %get-tuple-element.147.refs_0_, ...), custom_call_target="tpu_custom_call" | custom-call | tf_op jit(solution)/shard_map/turn_cross/pallas_call | solution.py:38
  278.1 8.5 %factor.3.inv_ref.refs_3_ = f32[128,128]{1,0:T(8,128)S(1)} custom-call(f32[128,128]{1,0:T(8,128)S(1)} %add.57.g_ref), custom_call_target="tpu_custom_call" | custom-call | tf_op jit(solution)/shard_map/factor/pallas_call | solution.py:38
  289.9 2.4 collective-permute-done.62
  301.5 3.7 %collective-permute-start.66 = (f32[2,32,128]{2,1,0:T(8,128)S(1)}, f32[2,32,128]{2,1,0:T(8,128)S(1)}, u32[]{:S(2)}, u32[]{:S(2)}) collective-permute-start(f32[2,32,128]{2,1,0:T(8,128)S(1)} %add.62), channel_id=1, source_target_pairs={{0,16},{4,20},{8,24},{12,28},{16,0},{20,4},{24,8},{28,12},{1,17},{... | collective-permute-start | bytes 98312 | tf_op jit(solution)/shard_map/ppermute | solution.py:353
  309.1 5.3 %collective-permute-done.49.refs_2_ = f32[12,32,128]{2,1,0:T(8,128)S(1)} collective-permute-done((f32[12,32,128]{2,1,0:T(8,128)S(1)}, f32[12,32,128]{2,1,0:T(8,128)S(1)}, u32[]{:S(2)}, u32[]{:S(2)}) %collective-permute-start.49) | collective-permute-done | bytes 196640 | tf_op jit(solution)/shard_map/ppermute | solution.py:353
  314.4 3.3 %collective-permute-done.50.refs_3_ = f32[12,32,128]{2,1,0:T(8,128)S(1)} collective-permute-done((f32[12,32,128]{2,1,0:T(8,128)S(1)}, f32[12,32,128]{2,1,0:T(8,128)S(1)}, u32[]{:S(2)}, u32[]{:S(2)}) %collective-permute-start.50) | collective-permute-done | bytes 196640 | tf_op jit(solution)/shard_map/ppermute | solution.py:353
  (156 shorter events, 69.1 us)
Async XLA Ops:
  2.5 34.9 %collective-permute-start = (f32[24,16,128]{2,1,0:T(8,128)S(1)}, f32[24,16,128]{2,1,0:T(8,128)S(1)}, u32[]{:S(2)}, u32[]{:S(2)}) collective-permute-start(f32[24,16,128]{2,1,0:T(8,128)S(1)} %get-tuple-element.84.refs_6_.refs_10_), channel_id=1, source_target_pairs={{0,4},{4,0},{8,12},{12,8},{16,20},{20,16},{24,28},{28,24},{1,5},{5... | collective-permute-start | bytes 589832 | tf_op jit(solution)/shard_map/ppermute | solution.py:349
  5.5 31.9 %collective-permute-start.1 = (f32[24,16,128]{2,1,0:T(8,128)S(1)}, f32[24,16,128]{2,1,0:T(8,128)S(1)}, u32[]{:S(2)}, u32[]{:S(2)}) collective-permute-start(f32[24,16,128]{2,1,0:T(8,128)S(1)} %get-tuple-element.85.refs_7_.refs_11_), channel_id=1, source_target_pairs={{0,28},{4,8},{8,4},{12,16},{16,12},{20,24},{24,20},{28,0},{1,29},{... | collective-permute-start | bytes 589832 | tf_op jit(solution)/shard_map/ppermute | solution.py:349
  9.1 45.2 %collective-permute-start.14 = (f32[24,16,128]{2,1,0:T(8,128)S(1)}, f32[24,16,128]{2,1,0:T(8,128)S(1)}, u32[]{:S(2)}, u32[]{:S(2)}) collective-permute-start(f32[24,16,128]{2,1,0:T(8,128)S(1)} %get-tuple-element.100.refs_6_.refs_10_), channel_id=1, source_target_pairs={{0,4},{4,0},{8,12},{12,8},{16,20},{20,16},{24,28},{28,24},{1,5},{5... | collective-permute-start | bytes 589832 | tf_op jit(solution)/shard_map/ppermute | solution.py:349
  9.1 45.2 %collective-permute-start.15 = (f32[24,16,128]{2,1,0:T(8,128)S(1)}, f32[24,16,128]{2,1,0:T(8,128)S(1)}, u32[]{:S(2)}, u32[]{:S(2)}) collective-permute-start(f32[24,16,128]{2,1,0:T(8,128)S(1)} %get-tuple-element.101.refs_7_.refs_11_), channel_id=1, source_target_pairs={{0,28},{4,8},{8,4},{12,16},{16,12},{20,24},{24,20},{28,0},{1,29},{... | collective-permute-start | bytes 589832 | tf_op jit(solution)/shard_map/ppermute | solution.py:349
  51.3 11.9 %collective-permute-start.2 = (f32[24,16,128]{2,1,0:T(8,128)S(1)}, f32[24,16,128]{2,1,0:T(8,128)S(1)}, u32[]{:S(2)}, u32[]{:S(2)}) collective-permute-start(f32[24,16,128]{2,1,0:T(8,128)S(1)} %get-tuple-element.86.refs_6_.refs_10_), channel_id=1, source_target_pairs={{0,4},{4,0},{8,12},{12,8},{16,20},{20,16},{24,28},{28,24},{1,5},{5... | collective-permute-start | bytes 589832 | tf_op jit(solution)/shard_map/ppermute | solution.py:349
  52.0 11.2 %collective-permute-start.3 = (f32[24,16,128]{2,1,0:T(8,128)S(1)}, f32[24,16,128]{2,1,0:T(8,128)S(1)}, u32[]{:S(2)}, u32[]{:S(2)}) collective-permute-start(f32[24,16,128]{2,1,0:T(8,128)S(1)} %get-tuple-element.87.refs_7_.refs_11_), channel_id=1, source_target_pairs={{0,28},{4,8},{8,4},{12,16},{16,12},{20,24},{24,20},{28,0},{1,29},{... | collective-permute-start | bytes 589832 | tf_op jit(solution)/shard_map/ppermute | solution.py:349
  60.7 12.4 %collective-permute-start.16 = (f32[24,16,128]{2,1,0:T(8,128)S(1)}, f32[24,16,128]{2,1,0:T(8,128)S(1)}, u32[]{:S(2)}, u32[]{:S(2)}) collective-permute-start(f32[24,16,128]{2,1,0:T(8,128)S(1)} %get-tuple-element.102.refs_6_.refs_10_), channel_id=1, source_target_pairs={{0,4},{4,0},{8,12},{12,8},{16,20},{20,16},{24,28},{28,24},{1,5},{5... | collective-permute-start | bytes 589832 | tf_op jit(solution)/shard_map/ppermute | solution.py:349
  61.5 11.6 %collective-permute-start.17 = (f32[24,16,128]{2,1,0:T(8,128)S(1)}, f32[24,16,128]{2,1,0:T(8,128)S(1)}, u32[]{:S(2)}, u32[]{:S(2)}) collective-permute-start(f32[24,16,128]{2,1,0:T(8,128)S(1)} %get-tuple-element.103.refs_7_.refs_11_), channel_id=1, source_target_pairs={{0,28},{4,8},{8,4},{12,16},{16,12},{20,24},{24,20},{28,0},{1,29},{... | collective-permute-start | bytes 589832 | tf_op jit(solution)/shard_map/ppermute | solution.py:349
  69.6 11.9 %collective-permute-start.4 = (f32[24,16,128]{2,1,0:T(8,128)S(1)}, f32[24,16,128]{2,1,0:T(8,128)S(1)}, u32[]{:S(2)}, u32[]{:S(2)}) collective-permute-start(f32[24,16,128]{2,1,0:T(8,128)S(1)} %get-tuple-element.88.refs_6_.refs_10_), channel_id=1, source_target_pairs={{0,4},{4,0},{8,12},{12,8},{16,20},{20,16},{24,28},{28,24},{1,5},{5... | collective-permute-start | bytes 589832 | tf_op jit(solution)/shard_map/ppermute | solution.py:349
  69.6 11.8 %collective-permute-start.5 = (f32[24,16,128]{2,1,0:T(8,128)S(1)}, f32[24,16,128]{2,1,0:T(8,128)S(1)}, u32[]{:S(2)}, u32[]{:S(2)}) collective-permute-start(f32[24,16,128]{2,1,0:T(8,128)S(1)} %get-tuple-element.89.refs_7_.refs_11_), channel_id=1, source_target_pairs={{0,28},{4,8},{8,4},{12,16},{16,12},{20,24},{24,20},{28,0},{1,29},{... | collective-permute-start | bytes 589832 | tf_op jit(solution)/shard_map/ppermute | solution.py:349
  79.5 11.3 %collective-permute-start.18 = (f32[24,16,128]{2,1,0:T(8,128)S(1)}, f32[24,16,128]{2,1,0:T(8,128)S(1)}, u32[]{:S(2)}, u32[]{:S(2)}) collective-permute-start(f32[24,16,128]{2,1,0:T(8,128)S(1)} %get-tuple-element.104.refs_6_.refs_10_), channel_id=1, source_target_pairs={{0,4},{4,0},{8,12},{12,8},{16,20},{20,16},{24,28},{28,24},{1,5},{5... | collective-permute-start | bytes 589832 | tf_op jit(solution)/shard_map/ppermute | solution.py:349
  79.5 11.3 %collective-permute-start.19 = (f32[24,16,128]{2,1,0:T(8,128)S(1)}, f32[24,16,128]{2,1,0:T(8,128)S(1)}, u32[]{:S(2)}, u32[]{:S(2)}) collective-permute-start(f32[24,16,128]{2,1,0:T(8,128)S(1)} %get-tuple-element.105.refs_7_.refs_11_), channel_id=1, source_target_pairs={{0,28},{4,8},{8,4},{12,16},{16,12},{20,24},{24,20},{28,0},{1,29},{... | collective-permute-start | bytes 589832 | tf_op jit(solution)/shard_map/ppermute | solution.py:349
  87.8 11.9 %collective-permute-start.6 = (f32[24,16,128]{2,1,0:T(8,128)S(1)}, f32[24,16,128]{2,1,0:T(8,128)S(1)}, u32[]{:S(2)}, u32[]{:S(2)}) collective-permute-start(f32[24,16,128]{2,1,0:T(8,128)S(1)} %get-tuple-element.90.refs_6_), channel_id=1, source_target_pairs={{0,4},{4,0},{8,12},{12,8},{16,20},{20,16},{24,28},{28,24},{1,5},{5... | collective-permute-start | bytes 589832 | tf_op jit(solution)/shard_map/ppermute | solution.py:349
  88.5 11.2 %collective-permute-start.7 = (f32[24,16,128]{2,1,0:T(8,128)S(1)}, f32[24,16,128]{2,1,0:T(8,128)S(1)}, u32[]{:S(2)}, u32[]{:S(2)}) collective-permute-start(f32[24,16,128]{2,1,0:T(8,128)S(1)} %get-tuple-element.91.refs_7_), channel_id=1, source_target_pairs={{0,28},{4,8},{8,4},{12,16},{16,12},{20,24},{24,20},{28,0},{1,29},{... | collective-permute-start | bytes 589832 | tf_op jit(solution)/shard_map/ppermute | solution.py:349
  97.2 12.4 %collective-permute-start.20 = (f32[24,16,128]{2,1,0:T(8,128)S(1)}, f32[24,16,128]{2,1,0:T(8,128)S(1)}, u32[]{:S(2)}, u32[]{:S(2)}) collective-permute-start(f32[24,16,128]{2,1,0:T(8,128)S(1)} %get-tuple-element.106.refs_6_), channel_id=1, source_target_pairs={{0,4},{4,0},{8,12},{12,8},{16,20},{20,16},{24,28},{28,24},{1,5},{5... | collective-permute-start | bytes 589832 | tf_op jit(solution)/shard_map/ppermute | solution.py:349
  97.9 11.7 %collective-permute-start.21 = (f32[24,16,128]{2,1,0:T(8,128)S(1)}, f32[24,16,128]{2,1,0:T(8,128)S(1)}, u32[]{:S(2)}, u32[]{:S(2)}) collective-permute-start(f32[24,16,128]{2,1,0:T(8,128)S(1)} %get-tuple-element.107.refs_7_), channel_id=1, source_target_pairs={{0,28},{4,8},{8,4},{12,16},{16,12},{20,24},{24,20},{28,0},{1,29},{... | collective-permute-start | bytes 589832 | tf_op jit(solution)/shard_map/ppermute | solution.py:349
  106.1 12.2 %collective-permute-start.8 = (f32[24,16,128]{2,1,0:T(8,128)S(1)}, f32[24,16,128]{2,1,0:T(8,128)S(1)}, u32[]{:S(2)}, u32[]{:S(2)}) collective-permute-start(f32[24,16,128]{2,1,0:T(8,128)S(1)} %get-tuple-element.92.refs_6_.refs_10_.refs_12_), channel_id=1, source_target_pairs={{0,4},{4,0},{8,12},{12,8},{16,20},{20,16},{24,28},{28,24},{1,5},{5... | collective-permute-start | bytes 589832 | tf_op jit(solution)/shard_map/ppermute | solution.py:349
  106.2 12.6 %collective-permute-start.9 = (f32[24,16,128]{2,1,0:T(8,128)S(1)}, f32[24,16,128]{2,1,0:T(8,128)S(1)}, u32[]{:S(2)}, u32[]{:S(2)}) collective-permute-start(f32[24,16,128]{2,1,0:T(8,128)S(1)} %get-tuple-element.93.refs_7_.refs_11_.refs_13_), channel_id=1, source_target_pairs={{0,28},{4,8},{8,4},{12,16},{16,12},{20,24},{24,20},{28,0},{1,29},{... | collective-permute-start | bytes 589832 | tf_op jit(solution)/shard_map/ppermute | solution.py:349
  116.3 11.0 %collective-permute-start.28 = (f32[12,32,128]{2,1,0:T(8,128)S(1)}, f32[12,32,128]{2,1,0:T(8,128)S(1)}, u32[]{:S(2)}, u32[]{:S(2)}) collective-permute-start(f32[12,32,128]{2,1,0:T(8,128)S(1)} %get-tuple-element.117), channel_id=1, source_target_pairs={{0,1},{1,0},{2,3},{3,2},{4,5},{5,4},{6,7},{7,6},{8,9},{9,8},{10,11... | collective-permute-start | bytes 589832 | tf_op jit(solution)/shard_map/ppermute | solution.py:353
  116.4 11.6 %collective-permute-start.29 = (f32[12,32,128]{2,1,0:T(8,128)S(1)}, f32[12,32,128]{2,1,0:T(8,128)S(1)}, u32[]{:S(2)}, u32[]{:S(2)}) collective-permute-start(f32[12,32,128]{2,1,0:T(8,128)S(1)} %get-tuple-element.118), channel_id=1, source_target_pairs={{0,2},{1,3},{2,0},{3,1},{4,6},{5,7},{6,4},{7,5},{8,10},{9,11},{10,... | collective-permute-start | bytes 589832 | tf_op jit(solution)/shard_map/ppermute | solution.py:353
  117.9 12.3 %collective-permute-start.30 = (f32[12,32,128]{2,1,0:T(8,128)S(1)}, f32[12,32,128]{2,1,0:T(8,128)S(1)}, u32[]{:S(2)}, u32[]{:S(2)}) collective-permute-start(f32[12,32,128]{2,1,0:T(8,128)S(1)} %get-tuple-element.119), channel_id=1, source_target_pairs={{0,3},{1,2},{2,1},{3,0},{4,7},{5,6},{6,5},{7,4},{8,11},{9,10},{10,... | collective-permute-start | bytes 589832 | tf_op jit(solution)/shard_map/ppermute | solution.py:353
  118.2 14.0 %collective-permute-start.22 = (f32[24,16,128]{2,1,0:T(8,128)S(1)}, f32[24,16,128]{2,1,0:T(8,128)S(1)}, u32[]{:S(2)}, u32[]{:S(2)}) collective-permute-start(f32[24,16,128]{2,1,0:T(8,128)S(1)} %get-tuple-element.108.refs_6_.refs_10_), channel_id=1, source_target_pairs={{0,4},{4,0},{8,12},{12,8},{16,20},{20,16},{24,28},{28,24},{1,5},{5... | collective-permute-start | bytes 589832 | tf_op jit(solution)/shard_map/ppermute | solution.py:349
  118.8 13.5 %collective-permute-start.23 = (f32[24,16,128]{2,1,0:T(8,128)S(1)}, f32[24,16,128]{2,1,0:T(8,128)S(1)}, u32[]{:S(2)}, u32[]{:S(2)}) collective-permute-start(f32[24,16,128]{2,1,0:T(8,128)S(1)} %get-tuple-element.109.refs_7_.refs_11_), channel_id=1, source_target_pairs={{0,28},{4,8},{8,4},{12,16},{16,12},{20,24},{24,20},{28,0},{1,29},{... | collective-permute-start | bytes 589832 | tf_op jit(solution)/shard_map/ppermute | solution.py:349
  127.3 19.1 %collective-permute-start.10 = (f32[24,16,128]{2,1,0:T(8,128)S(1)}, f32[24,16,128]{2,1,0:T(8,128)S(1)}, u32[]{:S(2)}, u32[]{:S(2)}) collective-permute-start(f32[24,16,128]{2,1,0:T(8,128)S(1)} %get-tuple-element.94.refs_6_.refs_10_), channel_id=1, source_target_pairs={{0,4},{4,0},{8,12},{12,8},{16,20},{20,16},{24,28},{28,24},{1,5},{5... | collective-permute-start | bytes 589832 | tf_op jit(solution)/shard_map/ppermute | solution.py:349
  128.0 18.4 %collective-permute-start.11 = (f32[24,16,128]{2,1,0:T(8,128)S(1)}, f32[24,16,128]{2,1,0:T(8,128)S(1)}, u32[]{:S(2)}, u32[]{:S(2)}) collective-permute-start(f32[24,16,128]{2,1,0:T(8,128)S(1)} %get-tuple-element.95.refs_7_.refs_11_), channel_id=1, source_target_pairs={{0,28},{4,8},{8,4},{12,16},{16,12},{20,24},{24,20},{28,0},{1,29},{... | collective-permute-start | bytes 589832 | tf_op jit(solution)/shard_map/ppermute | solution.py:349
  132.2 9.3 %collective-permute-start.31 = (f32[128,128]{1,0:T(8,128)S(1)}, f32[128,128]{1,0:T(8,128)S(1)}, u32[]{:S(2)}, u32[]{:S(2)}) collective-permute-start(f32[128,128]{1,0:T(8,128)S(1)} %get-tuple-element.120.refs_2_), channel_id=1, source_target_pairs={{0,1},{1,0},{2,3},{3,2},{4,5},{5,4},{6,7},{7,6},{8,9},{9,8},{10,11... | collective-permute-start | bytes 196616 | tf_op jit(solution)/shard_map/ppermute | solution.py:353
  138.8 18.3 %collective-permute-start.24 = (f32[24,16,128]{2,1,0:T(8,128)S(1)}, f32[24,16,128]{2,1,0:T(8,128)S(1)}, u32[]{:S(2)}, u32[]{:S(2)}) collective-permute-start(f32[24,16,128]{2,1,0:T(8,128)S(1)} %get-tuple-element.110.refs_6_.refs_10_), channel_id=1, source_target_pairs={{0,4},{4,0},{8,12},{12,8},{16,20},{20,16},{24,28},{28,24},{1,5},{5... | collective-permute-start | bytes 589832 | tf_op jit(solution)/shard_map/ppermute | solution.py:349
  139.4 17.7 %collective-permute-start.25 = (f32[24,16,128]{2,1,0:T(8,128)S(1)}, f32[24,16,128]{2,1,0:T(8,128)S(1)}, u32[]{:S(2)}, u32[]{:S(2)}) collective-permute-start(f32[24,16,128]{2,1,0:T(8,128)S(1)} %get-tuple-element.111.refs_7_.refs_11_), channel_id=1, source_target_pairs={{0,28},{4,8},{8,4},{12,16},{16,12},{20,24},{24,20},{28,0},{1,29},{... | collective-permute-start | bytes 589832 | tf_op jit(solution)/shard_map/ppermute | solution.py:349
  145.8 11.2 %collective-permute-start.33 = (f32[128,128]{1,0:T(8,128)S(1)}, f32[128,128]{1,0:T(8,128)S(1)}, u32[]{:S(2)}, u32[]{:S(2)}) collective-permute-start(f32[128,128]{1,0:T(8,128)S(1)} %add.49), channel_id=1, source_target_pairs={{0,4},{4,0},{8,12},{12,8},{16,20},{20,16},{24,28},{28,24},{1,5},{5... | collective-permute-start | bytes 196616 | tf_op jit(solution)/shard_map/ppermute | solution.py:353
  152.7 29.7 %collective-permute-start.12 = (f32[24,16,128]{2,1,0:T(8,128)S(1)}, f32[24,16,128]{2,1,0:T(8,128)S(1)}, u32[]{:S(2)}, u32[]{:S(2)}) collective-permute-start(f32[24,16,128]{2,1,0:T(8,128)S(1)} %get-tuple-element.96.refs_6_.refs_10_), channel_id=1, source_target_pairs={{0,4},{4,0},{8,12},{12,8},{16,20},{20,16},{24,28},{28,24},{1,5},{5... | collective-permute-start | bytes 589832 | tf_op jit(solution)/shard_map/ppermute | solution.py:349
  154.3 28.1 %collective-permute-start.13 = (f32[24,16,128]{2,1,0:T(8,128)S(1)}, f32[24,16,128]{2,1,0:T(8,128)S(1)}, u32[]{:S(2)}, u32[]{:S(2)}) collective-permute-start(f32[24,16,128]{2,1,0:T(8,128)S(1)} %get-tuple-element.97.refs_7_.refs_11_), channel_id=1, source_target_pairs={{0,28},{4,8},{8,4},{12,16},{16,12},{20,24},{24,20},{28,0},{1,29},{... | collective-permute-start | bytes 589832 | tf_op jit(solution)/shard_map/ppermute | solution.py:349
  157.0 9.5 %collective-permute-start.34 = (f32[128,128]{1,0:T(8,128)S(1)}, f32[128,128]{1,0:T(8,128)S(1)}, u32[]{:S(2)}, u32[]{:S(2)}) collective-permute-start(f32[128,128]{1,0:T(8,128)S(1)} %add.50), channel_id=1, source_target_pairs={{0,8},{4,12},{8,0},{12,4},{16,24},{20,28},{24,16},{28,20},{1,9},{5... | collective-permute-start | bytes 196616 | tf_op jit(solution)/shard_map/ppermute | solution.py:353
  163.6 25.1 %collective-permute-start.26 = (f32[24,16,128]{2,1,0:T(8,128)S(1)}, f32[24,16,128]{2,1,0:T(8,128)S(1)}, u32[]{:S(2)}, u32[]{:S(2)}) collective-permute-start(f32[24,16,128]{2,1,0:T(8,128)S(1)} %get-tuple-element.112.refs_6_.refs_10_), channel_id=1, source_target_pairs={{0,4},{4,0},{8,12},{12,8},{16,20},{20,16},{24,28},{28,24},{1,5},{5... | collective-permute-start | bytes 589832 | tf_op jit(solution)/shard_map/ppermute | solution.py:349
  164.0 24.8 %collective-permute-start.27 = (f32[24,16,128]{2,1,0:T(8,128)S(1)}, f32[24,16,128]{2,1,0:T(8,128)S(1)}, u32[]{:S(2)}, u32[]{:S(2)}) collective-permute-start(f32[24,16,128]{2,1,0:T(8,128)S(1)} %get-tuple-element.113.refs_7_.refs_11_), channel_id=1, source_target_pairs={{0,28},{4,8},{8,4},{12,16},{16,12},{20,24},{24,20},{28,0},{1,29},{... | collective-permute-start | bytes 589832 | tf_op jit(solution)/shard_map/ppermute | solution.py:349
  195.1 15.4 %collective-permute-start.38 = (f32[24,16,128]{2,1,0:T(8,128)S(1)}, f32[24,16,128]{2,1,0:T(8,128)S(1)}, u32[]{:S(2)}, u32[]{:S(2)}) collective-permute-start(f32[24,16,128]{2,1,0:T(8,128)S(1)} %get-tuple-element.124.refs_6_), channel_id=1, source_target_pairs={{0,4},{4,0},{8,12},{12,8},{16,20},{20,16},{24,28},{28,24},{1,5},{5... | collective-permute-start | bytes 589832 | tf_op jit(solution)/shard_map/ppermute | solution.py:349
  196.2 14.4 %collective-permute-start.39 = (f32[24,16,128]{2,1,0:T(8,128)S(1)}, f32[24,16,128]{2,1,0:T(8,128)S(1)}, u32[]{:S(2)}, u32[]{:S(2)}) collective-permute-start(f32[24,16,128]{2,1,0:T(8,128)S(1)} %get-tuple-element.125.refs_7_), channel_id=1, source_target_pairs={{0,28},{4,8},{8,4},{12,16},{16,12},{20,24},{24,20},{28,0},{1,29},{... | collective-permute-start | bytes 589832 | tf_op jit(solution)/shard_map/ppermute | solution.py:349
  198.4 18.5 %collective-permute-start.36 = (f32[24,16,128]{2,1,0:T(8,128)S(1)}, f32[24,16,128]{2,1,0:T(8,128)S(1)}, u32[]{:S(2)}, u32[]{:S(2)}) collective-permute-start(f32[24,16,128]{2,1,0:T(8,128)S(1)} %get-tuple-element.122.refs_6_), channel_id=1, source_target_pairs={{0,4},{4,0},{8,12},{12,8},{16,20},{20,16},{24,28},{28,24},{1,5},{5... | collective-permute-start | bytes 589832 | tf_op jit(solution)/shard_map/ppermute | solution.py:349
  198.4 18.5 %collective-permute-start.37 = (f32[24,16,128]{2,1,0:T(8,128)S(1)}, f32[24,16,128]{2,1,0:T(8,128)S(1)}, u32[]{:S(2)}, u32[]{:S(2)}) collective-permute-start(f32[24,16,128]{2,1,0:T(8,128)S(1)} %get-tuple-element.123.refs_7_), channel_id=1, source_target_pairs={{0,28},{4,8},{8,4},{12,16},{16,12},{20,24},{24,20},{28,0},{1,29},{... | collective-permute-start | bytes 589832 | tf_op jit(solution)/shard_map/ppermute | solution.py:349
  225.1 9.5 %collective-permute-start.42 = (f32[12,32,128]{2,1,0:T(8,128)S(1)}, f32[12,32,128]{2,1,0:T(8,128)S(1)}, u32[]{:S(2)}, u32[]{:S(2)}) collective-permute-start(f32[12,32,128]{2,1,0:T(8,128)S(1)} %get-tuple-element.131), channel_id=1, source_target_pairs={{0,3},{1,2},{2,1},{3,0},{4,7},{5,6},{6,5},{7,4},{8,11},{9,10},{10,... | collective-permute-start | bytes 589832 | tf_op jit(solution)/shard_map/ppermute | solution.py:353
  225.3 22.1 %collective-permute-start.56 = (f32[24,16,128]{2,1,0:T(8,128)S(1)}, f32[24,16,128]{2,1,0:T(8,128)S(1)}, u32[]{:S(2)}, u32[]{:S(2)}) collective-permute-start(f32[24,16,128]{2,1,0:T(8,128)S(1)} %get-tuple-element.126.refs_12_.refs_6_), channel_id=1, source_target_pairs={{0,4},{4,0},{8,12},{12,8},{16,20},{20,16},{24,28},{28,24},{1,5},{5... | collective-permute-start | bytes 589832 | tf_op jit(solution)/shard_map/ppermute | solution.py:349
  227.2 21.9 %collective-permute-start.57 = (f32[24,16,128]{2,1,0:T(8,128)S(1)}, f32[24,16,128]{2,1,0:T(8,128)S(1)}, u32[]{:S(2)}, u32[]{:S(2)}) collective-permute-start(f32[24,16,128]{2,1,0:T(8,128)S(1)} %get-tuple-element.127.refs_13_.refs_7_), channel_id=1, source_target_pairs={{0,28},{4,8},{8,4},{12,16},{16,12},{20,24},{24,20},{28,0},{1,29},{... | collective-permute-start | bytes 589832 | tf_op jit(solution)/shard_map/ppermute | solution.py:349
  239.2 16.6 %collective-permute-start.54 = (f32[24,16,128]{2,1,0:T(8,128)S(1)}, f32[24,16,128]{2,1,0:T(8,128)S(1)}, u32[]{:S(2)}, u32[]{:S(2)}) collective-permute-start(f32[24,16,128]{2,1,0:T(8,128)S(1)} %get-tuple-element.143.refs_6_), channel_id=1, source_target_pairs={{0,4},{4,0},{8,12},{12,8},{16,20},{20,16},{24,28},{28,24},{1,5},{5... | collective-permute-start | bytes 589832 | tf_op jit(solution)/shard_map/ppermute | solution.py:349
  241.0 14.9 %collective-permute-start.55 = (f32[24,16,128]{2,1,0:T(8,128)S(1)}, f32[24,16,128]{2,1,0:T(8,128)S(1)}, u32[]{:S(2)}, u32[]{:S(2)}) collective-permute-start(f32[24,16,128]{2,1,0:T(8,128)S(1)} %get-tuple-element.144.refs_7_), channel_id=1, source_target_pairs={{0,28},{4,8},{8,4},{12,16},{16,12},{20,24},{24,20},{28,0},{1,29},{... | collective-permute-start | bytes 589832 | tf_op jit(solution)/shard_map/ppermute | solution.py:349
  247.4 16.1 %collective-permute-start.51 = (f32[12,32,128]{2,1,0:T(8,128)S(1)}, f32[12,32,128]{2,1,0:T(8,128)S(1)}, u32[]{:S(2)}, u32[]{:S(2)}) collective-permute-start(f32[12,32,128]{2,1,0:T(8,128)S(1)} %get-tuple-element.140), channel_id=1, source_target_pairs={{0,1},{1,0},{2,3},{3,2},{4,5},{5,4},{6,7},{7,6},{8,9},{9,8},{10,11... | collective-permute-start | bytes 589832 | tf_op jit(solution)/shard_map/ppermute | solution.py:353
  247.5 17.7 %collective-permute-start.52 = (f32[12,32,128]{2,1,0:T(8,128)S(1)}, f32[12,32,128]{2,1,0:T(8,128)S(1)}, u32[]{:S(2)}, u32[]{:S(2)}) collective-permute-start(f32[12,32,128]{2,1,0:T(8,128)S(1)} %get-tuple-element.141), channel_id=1, source_target_pairs={{0,2},{1,3},{2,0},{3,1},{4,6},{5,7},{6,4},{7,5},{8,10},{9,11},{10,... | collective-permute-start | bytes 589832 | tf_op jit(solution)/shard_map/ppermute | solution.py:353
  255.4 13.3 %collective-permute-start.53 = (f32[12,32,128]{2,1,0:T(8,128)S(1)}, f32[12,32,128]{2,1,0:T(8,128)S(1)}, u32[]{:S(2)}, u32[]{:S(2)}) collective-permute-start(f32[12,32,128]{2,1,0:T(8,128)S(1)} %get-tuple-element.142), channel_id=1, source_target_pairs={{0,3},{1,2},{2,1},{3,0},{4,7},{5,6},{6,5},{7,4},{8,11},{9,10},{10,... | collective-permute-start | bytes 589832 | tf_op jit(solution)/shard_map/ppermute | solution.py:353
  265.1 13.0 %collective-permute-start.47 = (f32[128,128]{1,0:T(8,128)S(1)}, f32[128,128]{1,0:T(8,128)S(1)}, u32[]{:S(2)}, u32[]{:S(2)}) collective-permute-start(f32[128,128]{1,0:T(8,128)S(1)} %add.56), channel_id=1, source_target_pairs={{0,16},{4,20},{8,24},{12,28},{16,0},{20,4},{24,8},{28,12},{1,17},{... | collective-permute-start | bytes 196616 | tf_op jit(solution)/shard_map/ppermute | solution.py:353
  307.2 10.5 %collective-permute-start.50 = (f32[12,32,128]{2,1,0:T(8,128)S(1)}, f32[12,32,128]{2,1,0:T(8,128)S(1)}, u32[]{:S(2)}, u32[]{:S(2)}) collective-permute-start(f32[12,32,128]{2,1,0:T(8,128)S(1)} %get-tuple-element.137), channel_id=1, source_target_pairs={{0,3},{1,2},{2,1},{3,0},{4,7},{5,6},{6,5},{7,4},{8,11},{9,10},{10,... | collective-permute-start | bytes 589832 | tf_op jit(solution)/shard_map/ppermute | solution.py:353
  (31 other events, 252.8 us)

commit v3 on v2

--- a/solution.py
+++ b/solution.py
@@ -132,7 +132,7 @@
             flops=2 * count * n * n * n, bytes_accessed=4 * blocks.size, transcendentals=0
         ),
         name="prep",
-    )(ids, own, col, blocks)
+    )(ids, own, col, pltpu.with_memory_space_constraint(blocks, pltpu.HBM))
 
 
 def apply_kernel(recur, mate, *refs):
@@ -357,9 +357,10 @@
     return [parts[0]] + [swap(parts[s], "col", s) for s in range(1, len(parts))]
 
 
-def summed(value, *axes):
+def summed(value, *axes, hop=1):
+    first = hop
     for axis in axes:
-        hop = 1
+        hop = first
         while hop < lax.axis_size(axis):
             value = value + swap(value, axis, hop)
             hop *= 2
@@ -386,8 +387,8 @@
     w, inv, src, row, num = prep(ids, owner_row, block_col, blocks, slots)
     meta = (src, row, num, w, inv)
 
-    def advance(now, before=((), ()), parts=False):
-        first, _ = apply(ids, meta, now[0], exchange(now[0]), before[0])
+    def advance(now, before=((), ()), parts=False, halo=None):
+        first, _ = apply(ids, meta, now[0], halo or exchange(now[0]), before[0])
         mate = first if parts else ()
         second, out = apply(ids, meta, now[1], exchange(now[1]), before[1], mate, count)
         return [first, second], (swapped(out) if parts else None)
@@ -406,15 +407,17 @@
     inverse_first = inverse_factor(gram, nodes)
     for step in range(DEGREE - 1):
         if step == DEGREE - 2:
-            now, inverse_first = lax.optimization_barrier((now, inverse_first))
+            held_back, inverse_first = lax.optimization_barrier((before[1], inverse_first))
+            before = [before[0], held_back]
         after, parts = advance(now, before, step == DEGREE - 2)
         before, now = now, after
 
+    parts, halo = lax.optimization_barrier((parts, exchange(now[0])))
     turned, gram_last = call(
         turn_kernel, "turn", [wide, square], ids, inverse_first, *parts, scalars=1, scratch=[held]
     )
     gram = summed(gram_last, "col", "node")
-    _, parts = advance(now, parts=True)
+    _, parts = advance(now, parts=True, halo=halo)
     (cross_last,) = call(
         turn_cross_kernel, "turn_cross", [square], ids, inverse_first, turned, *parts,
         scalars=1, scratch=[held],
@@ -424,15 +427,19 @@
         basis_kernel, "basis", [(quarter, cols_here, block)] * count, ids, inverse_last, turned,
         scalars=1, scratch=[held],
     )
-    (basis,) = call(
-        functools.partial(join_kernel, half), "join", [(cols_here, width)], ids, *swapped(parts), scalars=1
-    )
+    arrived = swapped(parts)
     parts = call(
         functools.partial(proj_kernel, nodes), "proj", [(2, cols_here, vecs)] * count, ids,
         inverse_first, cross_first, gram_first, inverse_last, cross_last, gram_last,
         scalars=1, scratch=[pltpu.VMEM(square, F32)],
     )
-    projected = summed(sum(swapped(parts)), "node")
+    projected = sum(swapped(parts))
+    projected = projected + swap(projected, "node", 1)
+    projected, arrived = lax.optimization_barrier((projected, arrived))
+    (basis,) = call(
+        functools.partial(join_kernel, half), "join", [(cols_here, width)], ids, *arrived, scalars=1
+    )
+    projected = summed(projected, "node", hop=2)
     return basis, projected[0], projected[1]
 
 

time: 320 us -> 291 us (0.909)
  local copies, waits for them, and re-layouts: 24.7 us -> 3.11 us
  waiting for transfers between devices: 45.3 us -> 38 us
  Pallas kernels: 161 us -> 165 us
    unnamed x24 -> x6, local copies, waits for them, and re-layouts: 24 us -> 2.49 us
    ppermute x18, waiting for transfers between devices: 9.69 us -> 2.72 us  [exchange(): lax.ppermute(pair[0], 'node', even)]
    pallas_call x1, Pallas kernels: 11.1 us -> 15.4 us  [prep(): pl.pallas_call(functools.partial(prep_kernel, rows), grid=(count // chunk...]
    ppermute x31, starting transfers between devices: 29.6 us -> 26.3 us  [swap(): lax.ppermute(value, axis, [(i, i ^ hop) for i in range(lax.axis_size(axis...]
  transfers between devices with their start and end apart: 67 -> 67, of which waited for: 14 -> 15; matrix products, arithmetic and copies ran while one was open for 0% -> 0% of each run, Pallas kernels for 43% -> 49%
where the time goes in v3:
time: 291 us
  Pallas kernels  165 us (57%)
  starting transfers between devices  83.7 us (29%)
  waiting for transfers between devices  38 us (13%)
  local copies, waits for them, and re-layouts  3.11 us (1%)
    pallas_call x18, Pallas kernels, apply(): pl.pallas_call(functools.partial(apply_kernel, bool(old), bool(mate)), in...  115 us
    ppermute x18, starting transfers between devices, exchange(): lax.ppermute(pair[1], 'node', odd)  42.3 us
    ppermute x31, waiting for transfers between devices, swap(): lax.ppermute(value, axis, [(i, i ^ hop) for i in range(lax.axis_size(axis...  34.5 us
    pallas_call x10, Pallas kernels, call(): pl.pallas_call(kernel, in_specs=[IN_SMEM] * scalars + [IN_VMEM] * (len(ar...  33.9 us
    ppermute x31, starting transfers between devices, swap(): lax.ppermute(value, axis, [(i, i ^ hop) for i in range(lax.axis_size(axis...  26.3 us
    pallas_call x1, Pallas kernels, prep(): pl.pallas_call(functools.partial(prep_kernel, rows), grid=(count // chunk...  15.4 us
    ppermute x18, starting transfers between devices, exchange(): lax.ppermute(pair[0], 'node', even)  15.1 us
  transfers between devices with their start and end apart: 67, of which 15 were waited for; matrix products, arithmetic and copies ran while one was open for 0% of the time, Pallas kernels for 49%

profile of v3, /device:TPU:0, one launch (start us, length us, event | category | flops | bytes accessed | tf_op | source)
XLA Modules:
  0.0 290.7 jit_solution(8556498852640922744)
XLA Ops:
  2.5 3.0 %collective-permute-start.8 = (f32[24,16,128]{2,1,0:T(8,128)S(1)}, f32[24,16,128]{2,1,0:T(8,128)S(1)}, u32[]{:S(2)}, u32[]{:S(2)}) collective-permute-start(f32[24,16,128]{2,1,0:T(8,128)S(1)} %get-tuple-element.101.refs_6_.refs_10_), channel_id=1, source_target_pairs={{0,4},{4,0},{8,12},{12,8},{16,20},{20,16},{24,28},{28,24},{1,5},{5... | collective-permute-start | bytes 589832 | tf_op jit(solution)/shard_map/ppermute | solution.py:349
  5.5 3.5 %collective-permute-start.9 = (f32[24,16,128]{2,1,0:T(8,128)S(1)}, f32[24,16,128]{2,1,0:T(8,128)S(1)}, u32[]{:S(2)}, u32[]{:S(2)}) collective-permute-start(f32[24,16,128]{2,1,0:T(8,128)S(1)} %get-tuple-element.102.refs_7_.refs_11_), channel_id=1, source_target_pairs={{0,28},{4,8},{8,4},{12,16},{16,12},{20,24},{24,20},{28,0},{1,29},{... | collective-permute-start | bytes 589832 | tf_op jit(solution)/shard_map/ppermute | solution.py:349
  12.4 15.4 %prep.1 = (bf16[352,128,256]{2,1,0:T(8,128)(2,1)S(1)}, f32[48,1,128]{2,1,0:T(1,128)S(1)}, s32[352]{0:T(512)S(1)}, s32[176]{0:T(256)S(1)}, s32[1]{0:T(128)}) custom-call(s32[2]{0:T(128)S(1)} %pad_add_fusion.ids_ref.refs_0_, s32[1,288]{1,0:T(1,128)S(1)} %copy-done.1, s32[1,288]{1,0:T(1,128)S(1)} %copy-done.2, f32[288,128,128]{2,1,0:T(8,128)} %blk_ref.1), custom_call_target="tpu_custom_call" | custom-call | flops 1207959552 | bytes 18874368 | tf_op jit(solution)/shard_map/prep/pallas_call | solution.py:119
  27.8 6.3 %apply.5 = (f32[24,16,128]{2,1,0:T(8,128)S(1)}, f32[24,16,128]{2,1,0:T(8,128)S(1)}) custom-call(s32[2]{0:T(128)S(1)} %pad_add_fusion.ids_ref.refs_0_, s32[352]{0:T(512)S(1)} %get-tuple-element.88.refs_1_, s32[176]{0:T(256)S(1)} %get-tuple-element.89.refs_2_, s32[1]{0:T(128)} %get-tuple-element.90.refs_3_, ...), custom_call_target="tpu_custom_call" | custom-call | flops 738197504 | bytes 23068672 | tf_op jit(solution)/shard_map/apply/pallas_call | solution.py:199
  34.8 2.2 collective-permute-start.11
  37.0 6.3 %apply.4 = (f32[24,16,128]{2,1,0:T(8,128)S(1)}, f32[24,16,128]{2,1,0:T(8,128)S(1)}) custom-call(s32[2]{0:T(128)S(1)} %pad_add_fusion.ids_ref.refs_0_, s32[352]{0:T(512)S(1)} %get-tuple-element.88.refs_1_, s32[176]{0:T(256)S(1)} %get-tuple-element.89.refs_2_, s32[1]{0:T(128)} %get-tuple-element.90.refs_3_, ...), custom_call_target="tpu_custom_call" | custom-call | flops 738197504 | bytes 23068672 | tf_op jit(solution)/shard_map/apply/pallas_call | solution.py:199
  46.0 6.3 %apply_recur.12 = (f32[24,16,128]{2,1,0:T(8,128)S(1)}, f32[24,16,128]{2,1,0:T(8,128)S(1)}) custom-call(s32[2]{0:T(128)S(1)} %pad_add_fusion.ids_ref.refs_0_, s32[352]{0:T(512)S(1)} %get-tuple-element.88.refs_1_, s32[176]{0:T(256)S(1)} %get-tuple-element.89.refs_2_, s32[1]{0:T(128)} %get-tuple-element.90.refs_3_, ...), custom_call_target="tpu_custom_call" | custom-call | flops 738197504 | bytes 23068672 | tf_op jit(solution)/shard_map/apply_recur/pallas_call | solution.py:199
  52.4 3.4 %collective-permute-start.13 = (f32[24,16,128]{2,1,0:T(8,128)S(1)}, f32[24,16,128]{2,1,0:T(8,128)S(1)}, u32[]{:S(2)}, u32[]{:S(2)}) collective-permute-start(f32[24,16,128]{2,1,0:T(8,128)S(1)} %get-tuple-element.106.refs_7_.refs_11_), channel_id=1, source_target_pairs={{0,28},{4,8},{8,4},{12,16},{16,12},{20,24},{24,20},{28,0},{1,29},{... | collective-permute-start | bytes 589832 | tf_op jit(solution)/shard_map/ppermute | solution.py:349
  55.9 6.3 %apply_recur.10 = (f32[24,16,128]{2,1,0:T(8,128)S(1)}, f32[24,16,128]{2,1,0:T(8,128)S(1)}) custom-call(s32[2]{0:T(128)S(1)} %pad_add_fusion.ids_ref.refs_0_, s32[352]{0:T(512)S(1)} %get-tuple-element.88.refs_1_, s32[176]{0:T(256)S(1)} %get-tuple-element.89.refs_2_, s32[1]{0:T(128)} %get-tuple-element.90.refs_3_, ...), custom_call_target="tpu_custom_call" | custom-call | flops 738197504 | bytes 23068672 | tf_op jit(solution)/shard_map/apply_recur/pallas_call | solution.py:199
  64.2 6.3 %apply_recur.13 = (f32[24,16,128]{2,1,0:T(8,128)S(1)}, f32[24,16,128]{2,1,0:T(8,128)S(1)}) custom-call(s32[2]{0:T(128)S(1)} %pad_add_fusion.ids_ref.refs_0_, s32[352]{0:T(512)S(1)} %get-tuple-element.88.refs_1_, s32[176]{0:T(256)S(1)} %get-tuple-element.89.refs_2_, s32[1]{0:T(128)} %get-tuple-element.90.refs_3_, ...), custom_call_target="tpu_custom_call" | custom-call | flops 738197504 | bytes 23068672 | tf_op jit(solution)/shard_map/apply_recur/pallas_call | solution.py:199
  71.3 2.3 collective-permute-start.15
  73.6 6.3 %apply_recur.11 = (f32[24,16,128]{2,1,0:T(8,128)S(1)}, f32[24,16,128]{2,1,0:T(8,128)S(1)}) custom-call(s32[2]{0:T(128)S(1)} %pad_add_fusion.ids_ref.refs_0_, s32[352]{0:T(512)S(1)} %get-tuple-element.88.refs_1_, s32[176]{0:T(256)S(1)} %get-tuple-element.89.refs_2_, s32[1]{0:T(128)} %get-tuple-element.90.refs_3_, ...), custom_call_target="tpu_custom_call" | custom-call | flops 738197504 | bytes 23068672 | tf_op jit(solution)/shard_map/apply_recur/pallas_call | solution.py:199
  82.5 6.3 %apply_recur.14 = (f32[24,16,128]{2,1,0:T(8,128)S(1)}, f32[24,16,128]{2,1,0:T(8,128)S(1)}) custom-call(s32[2]{0:T(128)S(1)} %pad_add_fusion.ids_ref.refs_0_, s32[352]{0:T(512)S(1)} %get-tuple-element.88.refs_1_, s32[176]{0:T(256)S(1)} %get-tuple-element.89.refs_2_, s32[1]{0:T(128)} %get-tuple-element.90.refs_3_, ...), custom_call_target="tpu_custom_call" | custom-call | flops 738197504 | bytes 23068672 | tf_op jit(solution)/shard_map/apply_recur/pallas_call | solution.py:199
  89.0 3.3 %collective-permute-start.19 = (f32[24,16,128]{2,1,0:T(8,128)S(1)}, f32[24,16,128]{2,1,0:T(8,128)S(1)}, u32[]{:S(2)}, u32[]{:S(2)}) collective-permute-start(f32[24,16,128]{2,1,0:T(8,128)S(1)} %get-tuple-element.110.refs_13_.refs_7_.refs_11_), channel_id=1, source_target_pairs={{0,28},{4,8},{8,4},{12,16},{16,12},{20,24},{24,20},{28,0},{1,29},{... | collective-permute-start | bytes 589832 | tf_op jit(solution)/shard_map/ppermute | solution.py:349
  92.3 6.5 %apply_recur_parts.2 = (f32[24,16,128]{2,1,0:T(8,128)S(1)}, f32[24,16,128]{2,1,0:T(8,128)S(1)}, f32[12,32,128]{2,1,0:T(8,128)S(1)}, f32[12,32,128]{2,1,0:T(8,128...) custom-call(s32[2]{0:T(128)S(1)} %pad_add_fusion.ids_ref.refs_0_, s32[352]{0:T(512)S(1)} %get-tuple-element.88.refs_1_, ...), custom_call_target="tpu_custom_call" | custom-call | flops 738197504 | bytes 23068672 | tf_op jit(solution)/shard_map/apply_recur_parts/pallas_call | solution.py:199
  102.6 6.3 %apply.6 = (f32[24,16,128]{2,1,0:T(8,128)S(1)}, f32[24,16,128]{2,1,0:T(8,128)S(1)}) custom-call(s32[2]{0:T(128)S(1)} %pad_add_fusion.ids_ref.refs_0_, s32[352]{0:T(512)S(1)} %get-tuple-element.88.refs_1_, s32[176]{0:T(256)S(1)} %get-tuple-element.89.refs_2_, s32[1]{0:T(128)} %get-tuple-element.90.refs_3_, ...), custom_call_target="tpu_custom_call" | custom-call | flops 738197504 | bytes 23068672 | tf_op jit(solution)/shard_map/apply/pallas_call | solution.py:199
  109.8 2.3 collective-permute-start.38
  112.1 6.4 %apply_parts.2 = (f32[24,16,128]{2,1,0:T(8,128)S(1)}, f32[24,16,128]{2,1,0:T(8,128)S(1)}, f32[12,32,128]{2,1,0:T(8,128)S(1)}, f32[12,32,128]{2,1,0:T(8,128)S(1)}...) custom-call(s32[2]{0:T(128)S(1)} %pad_add_fusion.ids_ref.refs_0_, s32[352]{0:T(512)S(1)} %get-tuple-element.88.refs_1_, ...), custom_call_target="tpu_custom_call" | custom-call | flops 738197504 | bytes 23068672 | tf_op jit(solution)/shard_map/apply_parts/pallas_call | solution.py:199
  126.0 6.3 %apply_recur.17 = (f32[24,16,128]{2,1,0:T(8,128)S(1)}, f32[24,16,128]{2,1,0:T(8,128)S(1)}) custom-call(s32[2]{0:T(128)S(1)} %pad_add_fusion.ids_ref.refs_0_, s32[352]{0:T(512)S(1)} %get-tuple-element.88.refs_1_, s32[176]{0:T(256)S(1)} %get-tuple-element.89.refs_2_, s32[1]{0:T(128)} %get-tuple-element.90.refs_3_, ...), custom_call_target="tpu_custom_call" | custom-call | flops 738197504 | bytes 23068672 | tf_op jit(solution)/shard_map/apply_recur/pallas_call | solution.py:199
  132.5 3.3 %collective-permute-start.40 = (f32[24,16,128]{2,1,0:T(8,128)S(1)}, f32[24,16,128]{2,1,0:T(8,128)S(1)}, u32[]{:S(2)}, u32[]{:S(2)}) collective-permute-start(f32[24,16,128]{2,1,0:T(8,128)S(1)} %get-tuple-element.135.refs_7_.refs_11_), channel_id=1, source_target_pairs={{0,28},{4,8},{8,4},{12,16},{16,12},{20,24},{24,20},{28,0},{1,29},{... | collective-permute-start | bytes 589832 | tf_op jit(solution)/shard_map/ppermute | solution.py:349
  135.8 6.3 %apply_recur.15 = (f32[24,16,128]{2,1,0:T(8,128)S(1)}, f32[24,16,128]{2,1,0:T(8,128)S(1)}) custom-call(s32[2]{0:T(128)S(1)} %pad_add_fusion.ids_ref.refs_0_, s32[352]{0:T(512)S(1)} %get-tuple-element.88.refs_1_, s32[176]{0:T(256)S(1)} %get-tuple-element.89.refs_2_, s32[1]{0:T(128)} %get-tuple-element.90.refs_3_, ...), custom_call_target="tpu_custom_call" | custom-call | flops 738197504 | bytes 23068672 | tf_op jit(solution)/shard_map/apply_recur/pallas_call | solution.py:199
  144.9 9.0 %collective-permute-done.27 = f32[128,128]{1,0:T(8,128)S(1)} collective-permute-done((f32[128,128]{1,0:T(8,128)S(1)}, f32[128,128]{1,0:T(8,128)S(1)}, u32[]{:S(2)}, u32[]{:S(2)}) %collective-permute-start.27) | collective-permute-done | bytes 65568 | tf_op jit(solution)/shard_map/ppermute | solution.py:353
  154.2 6.5 %apply_recur.18 = (f32[24,16,128]{2,1,0:T(8,128)S(1)}, f32[24,16,128]{2,1,0:T(8,128)S(1)}) custom-call(s32[2]{0:T(128)S(1)} %pad_add_fusion.ids_ref.refs_0_, s32[352]{0:T(512)S(1)} %get-tuple-element.88.refs_1_, s32[176]{0:T(256)S(1)} %get-tuple-element.89.refs_2_, s32[1]{0:T(128)} %get-tuple-element.90.refs_3_, ...), custom_call_target="tpu_custom_call" | custom-call | flops 738197504 | bytes 23068672 | tf_op jit(solution)/shard_map/apply_recur/pallas_call | solution.py:199
  161.8 2.2 collective-permute-start.42
  164.1 6.3 %apply_recur.16 = (f32[24,16,128]{2,1,0:T(8,128)S(1)}, f32[24,16,128]{2,1,0:T(8,128)S(1)}) custom-call(s32[2]{0:T(128)S(1)} %pad_add_fusion.ids_ref.refs_0_, s32[352]{0:T(512)S(1)} %get-tuple-element.88.refs_1_, s32[176]{0:T(256)S(1)} %get-tuple-element.89.refs_2_, s32[1]{0:T(128)} %get-tuple-element.90.refs_3_, ...), custom_call_target="tpu_custom_call" | custom-call | flops 738197504 | bytes 23068672 | tf_op jit(solution)/shard_map/apply_recur/pallas_call | solution.py:199
  170.8 2.3 collective-permute-start.36
  173.7 4.9 %collective-permute-done.29 = f32[128,128]{1,0:T(8,128)S(1)} collective-permute-done((f32[128,128]{1,0:T(8,128)S(1)}, f32[128,128]{1,0:T(8,128)S(1)}, u32[]{:S(2)}, u32[]{:S(2)}) %collective-permute-start.29) | collective-permute-done | bytes 65568 | tf_op jit(solution)/shard_map/ppermute | solution.py:353
  178.6 8.4 %factor.2.inv_ref.refs_0_ = f32[128,128]{1,0:T(8,128)S(1)} custom-call(f32[128,128]{1,0:T(8,128)S(1)} %add.52.g_ref), custom_call_target="tpu_custom_call" | custom-call | tf_op jit(solution)/shard_map/factor/pallas_call | solution.py:38
  187.1 6.3 %apply_recur.19 = (f32[24,16,128]{2,1,0:T(8,128)S(1)}, f32[24,16,128]{2,1,0:T(8,128)S(1)}) custom-call(s32[2]{0:T(128)S(1)} %pad_add_fusion.ids_ref.refs_0_, s32[352]{0:T(512)S(1)} %get-tuple-element.88.refs_1_, s32[176]{0:T(256)S(1)} %get-tuple-element.89.refs_2_, s32[1]{0:T(128)} %get-tuple-element.90.refs_3_, ...), custom_call_target="tpu_custom_call" | custom-call | flops 738197504 | bytes 23068672 | tf_op jit(solution)/shard_map/apply_recur/pallas_call | solution.py:199
  193.4 6.5 %apply_recur_parts.3 = (f32[24,16,128]{2,1,0:T(8,128)S(1)}, f32[24,16,128]{2,1,0:T(8,128)S(1)}, f32[12,32,128]{2,1,0:T(8,128)S(1)}, f32[12,32,128]{2,1,0:T(8,128...) custom-call(s32[2]{0:T(128)S(1)} %pad_add_fusion.ids_ref.refs_0_, s32[352]{0:T(512)S(1)} %get-tuple-element.88.refs_1_, ...), custom_call_target="tpu_custom_call" | custom-call | flops 738197504 | bytes 23068672 | tf_op jit(solution)/shard_map/apply_recur_parts/pallas_call | solution.py:199
  201.8 3.0 %collective-permute-start.46 = (f32[24,16,128]{2,1,0:T(8,128)S(1)}, f32[24,16,128]{2,1,0:T(8,128)S(1)}, u32[]{:S(2)}, u32[]{:S(2)}) collective-permute-start(f32[24,16,128]{2,1,0:T(8,128)S(1)} %get-tuple-element.138.refs_12_.refs_6_), channel_id=1, source_target_pairs={{0,4},{4,0},{8,12},{12,8},{16,20},{20,16},{24,28},{28,24},{1,5},{5... | collective-permute-start | bytes 589832 | tf_op jit(solution)/shard_map/ppermute | solution.py:349
  204.8 2.4 collective-permute-start.47
  207.7 3.3 %collective-permute-done.45.refs_3_ = f32[12,32,128]{2,1,0:T(8,128)S(1)} collective-permute-done((f32[12,32,128]{2,1,0:T(8,128)S(1)}, f32[12,32,128]{2,1,0:T(8,128)S(1)}, u32[]{:S(2)}, u32[]{:S(2)}) %collective-permute-start.45) | collective-permute-done | bytes 196640 | tf_op jit(solution)/shard_map/ppermute | solution.py:353
  211.0 2.7 collective-permute-done.46.refs_8_
  214.4 4.0 %turn.1 = (f32[12,128,128]{2,1,0:T(8,128)S(1)}, f32[128,128]{1,0:T(8,128)S(1)}) custom-call(s32[2]{0:T(128)S(1)} %pad_add_fusion.ids_ref.refs_0_, f32[128,128]{1,0:T(8,128)S(1)} %factor.2.inv_ref.refs_0_, f32[12,32,128]{2,1,0:T(8,128)S(1)} %get-tuple-element.144.refs_0_, f32[12,32,128]{2,1,0:T(8,128)S(1)} %collective-permute-done.43.refs_1_, ...), custom_call_target="tpu_custom_call" | custom-call | tf_op jit(solution)/shard_map/turn/pallas_call | solution.py:38
  220.4 2.4 collective-permute-start.54
  224.9 2.9 collective-permute-done.49
  227.8 6.3 %apply.7 = (f32[24,16,128]{2,1,0:T(8,128)S(1)}, f32[24,16,128]{2,1,0:T(8,128)S(1)}) custom-call(s32[2]{0:T(128)S(1)} %pad_add_fusion.ids_ref.refs_0_, s32[352]{0:T(512)S(1)} %get-tuple-element.88.refs_1_, s32[176]{0:T(256)S(1)} %get-tuple-element.89.refs_2_, s32[1]{0:T(128)} %get-tuple-element.90.refs_3_, ...), custom_call_target="tpu_custom_call" | custom-call | flops 738197504 | bytes 23068672 | tf_op jit(solution)/shard_map/apply/pallas_call | solution.py:199
  234.3 7.3 %apply_parts.3 = (f32[24,16,128]{2,1,0:T(8,128)}, f32[24,16,128]{2,1,0:T(8,128)}, f32[12,32,128]{2,1,0:T(8,128)S(1)}, f32[12,32,128]{2,1,0:T(8,128)S(1)}, f32[12...) custom-call(s32[2]{0:T(128)S(1)} %pad_add_fusion.ids_ref.refs_0_, s32[352]{0:T(512)S(1)} %get-tuple-element.88.refs_1_, ...), custom_call_target="tpu_custom_call" | custom-call | flops 738197504 | bytes 23068672 | tf_op jit(solution)/shard_map/apply_parts/pallas_call | solution.py:199
  243.8 3.2 %collective-permute-start.52 = (f32[128,128]{1,0:T(8,128)S(1)}, f32[128,128]{1,0:T(8,128)S(1)}, u32[]{:S(2)}, u32[]{:S(2)}) collective-permute-start(f32[128,128]{1,0:T(8,128)S(1)} %add.56), channel_id=1, source_target_pairs={{0,16},{4,20},{8,24},{12,28},{16,0},{20,4},{24,8},{28,12},{1,17},{... | collective-permute-start | bytes 196616 | tf_op jit(solution)/shard_map/ppermute | solution.py:353
  247.1 2.1 cross.1.refs_1_
  249.5 3.2 %collective-permute-done.57.refs_3_ = f32[12,32,128]{2,1,0:T(8,128)S(1)} collective-permute-done((f32[12,32,128]{2,1,0:T(8,128)S(1)}, f32[12,32,128]{2,1,0:T(8,128)S(1)}, u32[]{:S(2)}, u32[]{:S(2)}) %collective-permute-start.57) | collective-permute-done | bytes 196640 | tf_op jit(solution)/shard_map/ppermute | solution.py:353
  252.7 4.0 %turn_cross.1.refs_4_ = f32[128,128]{1,0:T(8,128)S(1)} custom-call(s32[2]{0:T(128)S(1)} %pad_add_fusion.ids_ref.refs_0_, f32[128,128]{1,0:T(8,128)S(1)} %factor.2.inv_ref.refs_0_, f32[12,128,128]{2,1,0:T(8,128)S(1)} %get-tuple-element.149.f_ref, f32[12,32,128]{2,1,0:T(8,128)S(1)} %get-tuple-element.156.refs_0_, ...), custom_call_target="tpu_custom_call" | custom-call | tf_op jit(solution)/shard_map/turn_cross/pallas_call | solution.py:38
  256.7 8.5 %factor.3.refs_3_.inv_ref = f32[128,128]{1,0:T(8,128)S(1)} custom-call(f32[128,128]{1,0:T(8,128)S(1)} %add.57.g_ref), custom_call_target="tpu_custom_call" | custom-call | tf_op jit(solution)/shard_map/factor/pallas_call | solution.py:38
  272.1 2.1 collective-permute-start.61
  278.2 2.6 collective-permute-done.64.refs_3_
  282.6 2.3 collective-permute-done.65
  284.9 3.2 %collective-permute-start.66 = (f32[2,32,128]{2,1,0:T(8,128)S(1)}, f32[2,32,128]{2,1,0:T(8,128)S(1)}, u32[]{:S(2)}, u32[]{:S(2)}) collective-permute-start(f32[2,32,128]{2,1,0:T(8,128)S(1)} %add.62), channel_id=1, source_target_pairs={{0,16},{4,20},{8,24},{12,28},{16,0},{20,4},{24,8},{28,12},{1,17},{... | collective-permute-start | bytes 98312 | tf_op jit(solution)/shard_map/ppermute | solution.py:353
  (137 shorter events, 56.8 us)
Async XLA Ops:
  2.5 25.3 %collective-permute-start.8 = (f32[24,16,128]{2,1,0:T(8,128)S(1)}, f32[24,16,128]{2,1,0:T(8,128)S(1)}, u32[]{:S(2)}, u32[]{:S(2)}) collective-permute-start(f32[24,16,128]{2,1,0:T(8,128)S(1)} %get-tuple-element.101.refs_6_.refs_10_), channel_id=1, source_target_pairs={{0,4},{4,0},{8,12},{12,8},{16,20},{20,16},{24,28},{28,24},{1,5},{5... | collective-permute-start | bytes 589832 | tf_op jit(solution)/shard_map/ppermute | solution.py:349
  5.5 22.2 %collective-permute-start.9 = (f32[24,16,128]{2,1,0:T(8,128)S(1)}, f32[24,16,128]{2,1,0:T(8,128)S(1)}, u32[]{:S(2)}, u32[]{:S(2)}) collective-permute-start(f32[24,16,128]{2,1,0:T(8,128)S(1)} %get-tuple-element.102.refs_7_.refs_11_), channel_id=1, source_target_pairs={{0,28},{4,8},{8,4},{12,16},{16,12},{20,24},{24,20},{28,0},{1,29},{... | collective-permute-start | bytes 589832 | tf_op jit(solution)/shard_map/ppermute | solution.py:349
  9.1 28.0 %collective-permute-start = (f32[24,16,128]{2,1,0:T(8,128)S(1)}, f32[24,16,128]{2,1,0:T(8,128)S(1)}, u32[]{:S(2)}, u32[]{:S(2)}) collective-permute-start(f32[24,16,128]{2,1,0:T(8,128)S(1)} %get-tuple-element.93.refs_6_.refs_10_), channel_id=1, source_target_pairs={{0,4},{4,0},{8,12},{12,8},{16,20},{20,16},{24,28},{28,24},{1,5},{5... | collective-permute-start | bytes 589832 | tf_op jit(solution)/shard_map/ppermute | solution.py:349
  9.1 28.0 %collective-permute-start.1 = (f32[24,16,128]{2,1,0:T(8,128)S(1)}, f32[24,16,128]{2,1,0:T(8,128)S(1)}, u32[]{:S(2)}, u32[]{:S(2)}) collective-permute-start(f32[24,16,128]{2,1,0:T(8,128)S(1)} %get-tuple-element.94.refs_7_.refs_11_), channel_id=1, source_target_pairs={{0,28},{4,8},{8,4},{12,16},{16,12},{20,24},{24,20},{28,0},{1,29},{... | collective-permute-start | bytes 589832 | tf_op jit(solution)/shard_map/ppermute | solution.py:349
  34.1 11.9 %collective-permute-start.10 = (f32[24,16,128]{2,1,0:T(8,128)S(1)}, f32[24,16,128]{2,1,0:T(8,128)S(1)}, u32[]{:S(2)}, u32[]{:S(2)}) collective-permute-start(f32[24,16,128]{2,1,0:T(8,128)S(1)} %get-tuple-element.103.refs_6_.refs_10_), channel_id=1, source_target_pairs={{0,4},{4,0},{8,12},{12,8},{16,20},{20,16},{24,28},{28,24},{1,5},{5... | collective-permute-start | bytes 589832 | tf_op jit(solution)/shard_map/ppermute | solution.py:349
  34.8 11.2 %collective-permute-start.11 = (f32[24,16,128]{2,1,0:T(8,128)S(1)}, f32[24,16,128]{2,1,0:T(8,128)S(1)}, u32[]{:S(2)}, u32[]{:S(2)}) collective-permute-start(f32[24,16,128]{2,1,0:T(8,128)S(1)} %get-tuple-element.104.refs_7_.refs_11_), channel_id=1, source_target_pairs={{0,28},{4,8},{8,4},{12,16},{16,12},{20,24},{24,20},{28,0},{1,29},{... | collective-permute-start | bytes 589832 | tf_op jit(solution)/shard_map/ppermute | solution.py:349
  43.4 12.5 %collective-permute-start.2 = (f32[24,16,128]{2,1,0:T(8,128)S(1)}, f32[24,16,128]{2,1,0:T(8,128)S(1)}, u32[]{:S(2)}, u32[]{:S(2)}) collective-permute-start(f32[24,16,128]{2,1,0:T(8,128)S(1)} %get-tuple-element.95.refs_6_.refs_10_), channel_id=1, source_target_pairs={{0,4},{4,0},{8,12},{12,8},{16,20},{20,16},{24,28},{28,24},{1,5},{5... | collective-permute-start | bytes 589832 | tf_op jit(solution)/shard_map/ppermute | solution.py:349
  44.3 11.6 %collective-permute-start.3 = (f32[24,16,128]{2,1,0:T(8,128)S(1)}, f32[24,16,128]{2,1,0:T(8,128)S(1)}, u32[]{:S(2)}, u32[]{:S(2)}) collective-permute-start(f32[24,16,128]{2,1,0:T(8,128)S(1)} %get-tuple-element.96.refs_7_.refs_11_), channel_id=1, source_target_pairs={{0,28},{4,8},{8,4},{12,16},{16,12},{20,24},{24,20},{28,0},{1,29},{... | collective-permute-start | bytes 589832 | tf_op jit(solution)/shard_map/ppermute | solution.py:349
  52.4 11.8 %collective-permute-start.12 = (f32[24,16,128]{2,1,0:T(8,128)S(1)}, f32[24,16,128]{2,1,0:T(8,128)S(1)}, u32[]{:S(2)}, u32[]{:S(2)}) collective-permute-start(f32[24,16,128]{2,1,0:T(8,128)S(1)} %get-tuple-element.105.refs_6_.refs_10_), channel_id=1, source_target_pairs={{0,4},{4,0},{8,12},{12,8},{16,20},{20,16},{24,28},{28,24},{1,5},{5... | collective-permute-start | bytes 589832 | tf_op jit(solution)/shard_map/ppermute | solution.py:349
  52.4 11.7 %collective-permute-start.13 = (f32[24,16,128]{2,1,0:T(8,128)S(1)}, f32[24,16,128]{2,1,0:T(8,128)S(1)}, u32[]{:S(2)}, u32[]{:S(2)}) collective-permute-start(f32[24,16,128]{2,1,0:T(8,128)S(1)} %get-tuple-element.106.refs_7_.refs_11_), channel_id=1, source_target_pairs={{0,28},{4,8},{8,4},{12,16},{16,12},{20,24},{24,20},{28,0},{1,29},{... | collective-permute-start | bytes 589832 | tf_op jit(solution)/shard_map/ppermute | solution.py:349
  62.2 11.4 %collective-permute-start.4 = (f32[24,16,128]{2,1,0:T(8,128)S(1)}, f32[24,16,128]{2,1,0:T(8,128)S(1)}, u32[]{:S(2)}, u32[]{:S(2)}) collective-permute-start(f32[24,16,128]{2,1,0:T(8,128)S(1)} %get-tuple-element.97.refs_6_.refs_10_), channel_id=1, source_target_pairs={{0,4},{4,0},{8,12},{12,8},{16,20},{20,16},{24,28},{28,24},{1,5},{5... | collective-permute-start | bytes 589832 | tf_op jit(solution)/shard_map/ppermute | solution.py:349
  62.3 11.3 %collective-permute-start.5 = (f32[24,16,128]{2,1,0:T(8,128)S(1)}, f32[24,16,128]{2,1,0:T(8,128)S(1)}, u32[]{:S(2)}, u32[]{:S(2)}) collective-permute-start(f32[24,16,128]{2,1,0:T(8,128)S(1)} %get-tuple-element.98.refs_7_.refs_11_), channel_id=1, source_target_pairs={{0,28},{4,8},{8,4},{12,16},{16,12},{20,24},{24,20},{28,0},{1,29},{... | collective-permute-start | bytes 589832 | tf_op jit(solution)/shard_map/ppermute | solution.py:349
  70.5 12.0 %collective-permute-start.14 = (f32[24,16,128]{2,1,0:T(8,128)S(1)}, f32[24,16,128]{2,1,0:T(8,128)S(1)}, u32[]{:S(2)}, u32[]{:S(2)}) collective-permute-start(f32[24,16,128]{2,1,0:T(8,128)S(1)} %get-tuple-element.107.refs_6_), channel_id=1, source_target_pairs={{0,4},{4,0},{8,12},{12,8},{16,20},{20,16},{24,28},{28,24},{1,5},{5... | collective-permute-start | bytes 589832 | tf_op jit(solution)/shard_map/ppermute | solution.py:349
  71.3 11.2 %collective-permute-start.15 = (f32[24,16,128]{2,1,0:T(8,128)S(1)}, f32[24,16,128]{2,1,0:T(8,128)S(1)}, u32[]{:S(2)}, u32[]{:S(2)}) collective-permute-start(f32[24,16,128]{2,1,0:T(8,128)S(1)} %get-tuple-element.108.refs_7_), channel_id=1, source_target_pairs={{0,28},{4,8},{8,4},{12,16},{16,12},{20,24},{24,20},{28,0},{1,29},{... | collective-permute-start | bytes 589832 | tf_op jit(solution)/shard_map/ppermute | solution.py:349
  79.9 12.4 %collective-permute-start.6 = (f32[24,16,128]{2,1,0:T(8,128)S(1)}, f32[24,16,128]{2,1,0:T(8,128)S(1)}, u32[]{:S(2)}, u32[]{:S(2)}) collective-permute-start(f32[24,16,128]{2,1,0:T(8,128)S(1)} %get-tuple-element.99.refs_6_), channel_id=1, source_target_pairs={{0,4},{4,0},{8,12},{12,8},{16,20},{20,16},{24,28},{28,24},{1,5},{5... | collective-permute-start | bytes 589832 | tf_op jit(solution)/shard_map/ppermute | solution.py:349
  80.7 11.6 %collective-permute-start.7 = (f32[24,16,128]{2,1,0:T(8,128)S(1)}, f32[24,16,128]{2,1,0:T(8,128)S(1)}, u32[]{:S(2)}, u32[]{:S(2)}) collective-permute-start(f32[24,16,128]{2,1,0:T(8,128)S(1)} %get-tuple-element.100.refs_7_), channel_id=1, source_target_pairs={{0,28},{4,8},{8,4},{12,16},{16,12},{20,24},{24,20},{28,0},{1,29},{... | collective-permute-start | bytes 589832 | tf_op jit(solution)/shard_map/ppermute | solution.py:349
  88.8 11.9 %collective-permute-start.18 = (f32[24,16,128]{2,1,0:T(8,128)S(1)}, f32[24,16,128]{2,1,0:T(8,128)S(1)}, u32[]{:S(2)}, u32[]{:S(2)}) collective-permute-start(f32[24,16,128]{2,1,0:T(8,128)S(1)} %get-tuple-element.109.refs_12_.refs_6_.refs_10_), channel_id=1, source_target_pairs={{0,4},{4,0},{8,12},{12,8},{16,20},{20,16},{24,28},{28,24},{1,5},{5... | collective-permute-start | bytes 589832 | tf_op jit(solution)/shard_map/ppermute | solution.py:349
  89.0 13.3 %collective-permute-start.19 = (f32[24,16,128]{2,1,0:T(8,128)S(1)}, f32[24,16,128]{2,1,0:T(8,128)S(1)}, u32[]{:S(2)}, u32[]{:S(2)}) collective-permute-start(f32[24,16,128]{2,1,0:T(8,128)S(1)} %get-tuple-element.110.refs_13_.refs_7_.refs_11_), channel_id=1, source_target_pairs={{0,28},{4,8},{8,4},{12,16},{16,12},{20,24},{24,20},{28,0},{1,29},{... | collective-permute-start | bytes 589832 | tf_op jit(solution)/shard_map/ppermute | solution.py:349
  98.8 10.1 %collective-permute-start.16 = (f32[24,16,128]{2,1,0:T(8,128)S(1)}, f32[24,16,128]{2,1,0:T(8,128)S(1)}, u32[]{:S(2)}, u32[]{:S(2)}) collective-permute-start(f32[24,16,128]{2,1,0:T(8,128)S(1)} %get-tuple-element.111.refs_6_.refs_10_), channel_id=1, source_target_pairs={{0,4},{4,0},{8,12},{12,8},{16,20},{20,16},{24,28},{28,24},{1,5},{5... | collective-permute-start | bytes 589832 | tf_op jit(solution)/shard_map/ppermute | solution.py:349
  99.0 10.8 %collective-permute-start.17 = (f32[24,16,128]{2,1,0:T(8,128)S(1)}, f32[24,16,128]{2,1,0:T(8,128)S(1)}, u32[]{:S(2)}, u32[]{:S(2)}) collective-permute-start(f32[24,16,128]{2,1,0:T(8,128)S(1)} %get-tuple-element.112.refs_7_.refs_11_), channel_id=1, source_target_pairs={{0,28},{4,8},{8,4},{12,16},{16,12},{20,24},{24,20},{28,0},{1,29},{... | collective-permute-start | bytes 589832 | tf_op jit(solution)/shard_map/ppermute | solution.py:349
  100.7 17.8 %collective-permute-start.22 = (f32[12,32,128]{2,1,0:T(8,128)S(1)}, f32[12,32,128]{2,1,0:T(8,128)S(1)}, u32[]{:S(2)}, u32[]{:S(2)}) collective-permute-start(f32[12,32,128]{2,1,0:T(8,128)S(1)} %get-tuple-element.120), channel_id=1, source_target_pairs={{0,1},{1,0},{2,3},{3,2},{4,5},{5,4},{6,7},{7,6},{8,9},{9,8},{10,11... | collective-permute-start | bytes 589832 | tf_op jit(solution)/shard_map/ppermute | solution.py:353
  100.7 18.6 %collective-permute-start.23 = (f32[12,32,128]{2,1,0:T(8,128)S(1)}, f32[12,32,128]{2,1,0:T(8,128)S(1)}, u32[]{:S(2)}, u32[]{:S(2)}) collective-permute-start(f32[12,32,128]{2,1,0:T(8,128)S(1)} %get-tuple-element.121), channel_id=1, source_target_pairs={{0,2},{1,3},{2,0},{3,1},{4,6},{5,7},{6,4},{7,5},{8,10},{9,11},{10,... | collective-permute-start | bytes 589832 | tf_op jit(solution)/shard_map/ppermute | solution.py:353
  102.2 18.9 %collective-permute-start.24 = (f32[12,32,128]{2,1,0:T(8,128)S(1)}, f32[12,32,128]{2,1,0:T(8,128)S(1)}, u32[]{:S(2)}, u32[]{:S(2)}) collective-permute-start(f32[12,32,128]{2,1,0:T(8,128)S(1)} %get-tuple-element.122), channel_id=1, source_target_pairs={{0,3},{1,2},{2,1},{3,0},{4,7},{5,6},{6,5},{7,4},{8,11},{9,10},{10,... | collective-permute-start | bytes 589832 | tf_op jit(solution)/shard_map/ppermute | solution.py:353
  108.9 17.1 %collective-permute-start.37 = (f32[24,16,128]{2,1,0:T(8,128)S(1)}, f32[24,16,128]{2,1,0:T(8,128)S(1)}, u32[]{:S(2)}, u32[]{:S(2)}) collective-permute-start(f32[24,16,128]{2,1,0:T(8,128)S(1)} %get-tuple-element.113.refs_10_.refs_6_), channel_id=1, source_target_pairs={{0,4},{4,0},{8,12},{12,8},{16,20},{20,16},{24,28},{28,24},{1,5},{5... | collective-permute-start | bytes 589832 | tf_op jit(solution)/shard_map/ppermute | solution.py:349
  109.8 16.2 %collective-permute-start.38 = (f32[24,16,128]{2,1,0:T(8,128)S(1)}, f32[24,16,128]{2,1,0:T(8,128)S(1)}, u32[]{:S(2)}, u32[]{:S(2)}) collective-permute-start(f32[24,16,128]{2,1,0:T(8,128)S(1)} %get-tuple-element.114.refs_11_.refs_7_), channel_id=1, source_target_pairs={{0,28},{4,8},{8,4},{12,16},{16,12},{20,24},{24,20},{28,0},{1,29},{... | collective-permute-start | bytes 589832 | tf_op jit(solution)/shard_map/ppermute | solution.py:349
  118.5 17.3 %collective-permute-start.20 = (f32[24,16,128]{2,1,0:T(8,128)S(1)}, f32[24,16,128]{2,1,0:T(8,128)S(1)}, u32[]{:S(2)}, u32[]{:S(2)}) collective-permute-start(f32[24,16,128]{2,1,0:T(8,128)S(1)} %get-tuple-element.115.refs_6_.refs_10_), channel_id=1, source_target_pairs={{0,4},{4,0},{8,12},{12,8},{16,20},{20,16},{24,28},{28,24},{1,5},{5... | collective-permute-start | bytes 589832 | tf_op jit(solution)/shard_map/ppermute | solution.py:349
  119.3 16.5 %collective-permute-start.21 = (f32[24,16,128]{2,1,0:T(8,128)S(1)}, f32[24,16,128]{2,1,0:T(8,128)S(1)}, u32[]{:S(2)}, u32[]{:S(2)}) collective-permute-start(f32[24,16,128]{2,1,0:T(8,128)S(1)} %get-tuple-element.116.refs_7_.refs_11_), channel_id=1, source_target_pairs={{0,28},{4,8},{8,4},{12,16},{16,12},{20,24},{24,20},{28,0},{1,29},{... | collective-permute-start | bytes 589832 | tf_op jit(solution)/shard_map/ppermute | solution.py:349
  124.4 19.6 %collective-permute-start.26 = (f32[128,128]{1,0:T(8,128)S(1)}, f32[128,128]{1,0:T(8,128)S(1)}, u32[]{:S(2)}, u32[]{:S(2)}) collective-permute-start(f32[128,128]{1,0:T(8,128)S(1)} %add.48), channel_id=1, source_target_pairs={{0,2},{1,3},{2,0},{3,1},{4,6},{5,7},{6,4},{7,5},{8,10},{9,11},{10,... | collective-permute-start | bytes 196616 | tf_op jit(solution)/shard_map/ppermute | solution.py:353
  132.3 21.9 %collective-permute-start.39 = (f32[24,16,128]{2,1,0:T(8,128)S(1)}, f32[24,16,128]{2,1,0:T(8,128)S(1)}, u32[]{:S(2)}, u32[]{:S(2)}) collective-permute-start(f32[24,16,128]{2,1,0:T(8,128)S(1)} %get-tuple-element.134.refs_6_.refs_10_), channel_id=1, source_target_pairs={{0,4},{4,0},{8,12},{12,8},{16,20},{20,16},{24,28},{28,24},{1,5},{5... | collective-permute-start | bytes 589832 | tf_op jit(solution)/shard_map/ppermute | solution.py:349
  132.5 21.7 %collective-permute-start.40 = (f32[24,16,128]{2,1,0:T(8,128)S(1)}, f32[24,16,128]{2,1,0:T(8,128)S(1)}, u32[]{:S(2)}, u32[]{:S(2)}) collective-permute-start(f32[24,16,128]{2,1,0:T(8,128)S(1)} %get-tuple-element.135.refs_7_.refs_11_), channel_id=1, source_target_pairs={{0,28},{4,8},{8,4},{12,16},{16,12},{20,24},{24,20},{28,0},{1,29},{... | collective-permute-start | bytes 589832 | tf_op jit(solution)/shard_map/ppermute | solution.py:349
  142.1 21.9 %collective-permute-start.33 = (f32[24,16,128]{2,1,0:T(8,128)S(1)}, f32[24,16,128]{2,1,0:T(8,128)S(1)}, u32[]{:S(2)}, u32[]{:S(2)}) collective-permute-start(f32[24,16,128]{2,1,0:T(8,128)S(1)} %get-tuple-element.132.refs_6_.refs_10_), channel_id=1, source_target_pairs={{0,4},{4,0},{8,12},{12,8},{16,20},{20,16},{24,28},{28,24},{1,5},{5... | collective-permute-start | bytes 589832 | tf_op jit(solution)/shard_map/ppermute | solution.py:349
  142.3 21.7 %collective-permute-start.34 = (f32[24,16,128]{2,1,0:T(8,128)S(1)}, f32[24,16,128]{2,1,0:T(8,128)S(1)}, u32[]{:S(2)}, u32[]{:S(2)}) collective-permute-start(f32[24,16,128]{2,1,0:T(8,128)S(1)} %get-tuple-element.133.refs_7_.refs_11_), channel_id=1, source_target_pairs={{0,28},{4,8},{8,4},{12,16},{16,12},{20,24},{24,20},{28,0},{1,29},{... | collective-permute-start | bytes 589832 | tf_op jit(solution)/shard_map/ppermute | solution.py:349
  144.1 9.9 %collective-permute-start.27 = (f32[128,128]{1,0:T(8,128)S(1)}, f32[128,128]{1,0:T(8,128)S(1)}, u32[]{:S(2)}, u32[]{:S(2)}) collective-permute-start(f32[128,128]{1,0:T(8,128)S(1)} %add.49), channel_id=1, source_target_pairs={{0,4},{4,0},{8,12},{12,8},{16,20},{20,16},{24,28},{28,24},{1,5},{5... | collective-permute-start | bytes 196616 | tf_op jit(solution)/shard_map/ppermute | solution.py:353
  153.9 19.1 %collective-permute-start.28 = (f32[128,128]{1,0:T(8,128)S(1)}, f32[128,128]{1,0:T(8,128)S(1)}, u32[]{:S(2)}, u32[]{:S(2)}) collective-permute-start(f32[128,128]{1,0:T(8,128)S(1)} %add.50), channel_id=1, source_target_pairs={{0,8},{4,12},{8,0},{12,4},{16,24},{20,28},{24,16},{28,20},{1,9},{5... | collective-permute-start | bytes 196616 | tf_op jit(solution)/shard_map/ppermute | solution.py:353
  160.7 26.3 %collective-permute-start.41 = (f32[24,16,128]{2,1,0:T(8,128)S(1)}, f32[24,16,128]{2,1,0:T(8,128)S(1)}, u32[]{:S(2)}, u32[]{:S(2)}) collective-permute-start(f32[24,16,128]{2,1,0:T(8,128)S(1)} %get-tuple-element.136.refs_6_), channel_id=1, source_target_pairs={{0,4},{4,0},{8,12},{12,8},{16,20},{20,16},{24,28},{28,24},{1,5},{5... | collective-permute-start | bytes 589832 | tf_op jit(solution)/shard_map/ppermute | solution.py:349
  161.8 25.2 %collective-permute-start.42 = (f32[24,16,128]{2,1,0:T(8,128)S(1)}, f32[24,16,128]{2,1,0:T(8,128)S(1)}, u32[]{:S(2)}, u32[]{:S(2)}) collective-permute-start(f32[24,16,128]{2,1,0:T(8,128)S(1)} %get-tuple-element.137.refs_7_), channel_id=1, source_target_pairs={{0,28},{4,8},{8,4},{12,16},{16,12},{20,24},{24,20},{28,0},{1,29},{... | collective-permute-start | bytes 589832 | tf_op jit(solution)/shard_map/ppermute | solution.py:349
  170.4 23.0 %collective-permute-start.35 = (f32[24,16,128]{2,1,0:T(8,128)S(1)}, f32[24,16,128]{2,1,0:T(8,128)S(1)}, u32[]{:S(2)}, u32[]{:S(2)}) collective-permute-start(f32[24,16,128]{2,1,0:T(8,128)S(1)} %get-tuple-element.130.refs_6_), channel_id=1, source_target_pairs={{0,4},{4,0},{8,12},{12,8},{16,20},{20,16},{24,28},{28,24},{1,5},{5... | collective-permute-start | bytes 589832 | tf_op jit(solution)/shard_map/ppermute | solution.py:349
  170.8 22.6 %collective-permute-start.36 = (f32[24,16,128]{2,1,0:T(8,128)S(1)}, f32[24,16,128]{2,1,0:T(8,128)S(1)}, u32[]{:S(2)}, u32[]{:S(2)}) collective-permute-start(f32[24,16,128]{2,1,0:T(8,128)S(1)} %get-tuple-element.131.refs_7_), channel_id=1, source_target_pairs={{0,28},{4,8},{8,4},{12,16},{16,12},{20,24},{24,20},{28,0},{1,29},{... | collective-permute-start | bytes 589832 | tf_op jit(solution)/shard_map/ppermute | solution.py:349
  200.5 10.5 %collective-permute-start.45 = (f32[12,32,128]{2,1,0:T(8,128)S(1)}, f32[12,32,128]{2,1,0:T(8,128)S(1)}, u32[]{:S(2)}, u32[]{:S(2)}) collective-permute-start(f32[12,32,128]{2,1,0:T(8,128)S(1)} %get-tuple-element.143), channel_id=1, source_target_pairs={{0,3},{1,2},{2,1},{3,0},{4,7},{5,6},{6,5},{7,4},{8,11},{9,10},{10,... | collective-permute-start | bytes 589832 | tf_op jit(solution)/shard_map/ppermute | solution.py:353
  201.8 11.9 %collective-permute-start.46 = (f32[24,16,128]{2,1,0:T(8,128)S(1)}, f32[24,16,128]{2,1,0:T(8,128)S(1)}, u32[]{:S(2)}, u32[]{:S(2)}) collective-permute-start(f32[24,16,128]{2,1,0:T(8,128)S(1)} %get-tuple-element.138.refs_12_.refs_6_), channel_id=1, source_target_pairs={{0,4},{4,0},{8,12},{12,8},{16,20},{20,16},{24,28},{28,24},{1,5},{5... | collective-permute-start | bytes 589832 | tf_op jit(solution)/shard_map/ppermute | solution.py:349
  204.8 9.6 %collective-permute-start.47 = (f32[24,16,128]{2,1,0:T(8,128)S(1)}, f32[24,16,128]{2,1,0:T(8,128)S(1)}, u32[]{:S(2)}, u32[]{:S(2)}) collective-permute-start(f32[24,16,128]{2,1,0:T(8,128)S(1)} %get-tuple-element.139.refs_13_.refs_7_), channel_id=1, source_target_pairs={{0,28},{4,8},{8,4},{12,16},{16,12},{20,24},{24,20},{28,0},{1,29},{... | collective-permute-start | bytes 589832 | tf_op jit(solution)/shard_map/ppermute | solution.py:349
  218.6 15.7 %collective-permute-start.53 = (f32[24,16,128]{2,1,0:T(8,128)S(1)}, f32[24,16,128]{2,1,0:T(8,128)S(1)}, u32[]{:S(2)}, u32[]{:S(2)}) collective-permute-start(f32[24,16,128]{2,1,0:T(8,128)S(1)} %get-tuple-element.150.refs_6_), channel_id=1, source_target_pairs={{0,4},{4,0},{8,12},{12,8},{16,20},{20,16},{24,28},{28,24},{1,5},{5... | collective-permute-start | bytes 589832 | tf_op jit(solution)/shard_map/ppermute | solution.py:349
  220.4 14.0 %collective-permute-start.54 = (f32[24,16,128]{2,1,0:T(8,128)S(1)}, f32[24,16,128]{2,1,0:T(8,128)S(1)}, u32[]{:S(2)}, u32[]{:S(2)}) collective-permute-start(f32[24,16,128]{2,1,0:T(8,128)S(1)} %get-tuple-element.151.refs_7_), channel_id=1, source_target_pairs={{0,28},{4,8},{8,4},{12,16},{16,12},{20,24},{24,20},{28,0},{1,29},{... | collective-permute-start | bytes 589832 | tf_op jit(solution)/shard_map/ppermute | solution.py:349
  223.4 18.3 %collective-permute-start.30 = (f32[12,32,128]{2,1,0:T(8,128)S(1)}, f32[12,32,128]{2,1,0:T(8,128)S(1)}, u32[]{:S(2)}, u32[]{:S(2)}) collective-permute-start(f32[12,32,128]{2,1,0:T(8,128)S(1)} %get-tuple-element.127), channel_id=1, source_target_pairs={{0,1},{1,0},{2,3},{3,2},{4,5},{5,4},{6,7},{7,6},{8,9},{9,8},{10,11... | collective-permute-start | bytes 589832 | tf_op jit(solution)/shard_map/ppermute | solution.py:353
  223.4 20.4 %collective-permute-start.31 = (f32[12,32,128]{2,1,0:T(8,128)S(1)}, f32[12,32,128]{2,1,0:T(8,128)S(1)}, u32[]{:S(2)}, u32[]{:S(2)}) collective-permute-start(f32[12,32,128]{2,1,0:T(8,128)S(1)} %get-tuple-element.128), channel_id=1, source_target_pairs={{0,2},{1,3},{2,0},{3,1},{4,6},{5,7},{6,4},{7,5},{8,10},{9,11},{10,... | collective-permute-start | bytes 589832 | tf_op jit(solution)/shard_map/ppermute | solution.py:353
  234.1 12.9 %collective-permute-start.32 = (f32[12,32,128]{2,1,0:T(8,128)S(1)}, f32[12,32,128]{2,1,0:T(8,128)S(1)}, u32[]{:S(2)}, u32[]{:S(2)}) collective-permute-start(f32[12,32,128]{2,1,0:T(8,128)S(1)} %get-tuple-element.129), channel_id=1, source_target_pairs={{0,3},{1,2},{2,1},{3,0},{4,7},{5,6},{6,5},{7,4},{8,11},{9,10},{10,... | collective-permute-start | bytes 589832 | tf_op jit(solution)/shard_map/ppermute | solution.py:353
  234.3 9.5 %collective-permute-start.51 = (f32[128,128]{1,0:T(8,128)S(1)}, f32[128,128]{1,0:T(8,128)S(1)}, u32[]{:S(2)}, u32[]{:S(2)}) collective-permute-start(f32[128,128]{1,0:T(8,128)S(1)} %add.55), channel_id=1, source_target_pairs={{0,8},{4,12},{8,0},{12,4},{16,24},{20,28},{24,16},{28,20},{1,9},{5... | collective-permute-start | bytes 196616 | tf_op jit(solution)/shard_map/ppermute | solution.py:353
  243.8 12.9 %collective-permute-start.52 = (f32[128,128]{1,0:T(8,128)S(1)}, f32[128,128]{1,0:T(8,128)S(1)}, u32[]{:S(2)}, u32[]{:S(2)}) collective-permute-start(f32[128,128]{1,0:T(8,128)S(1)} %add.56), channel_id=1, source_target_pairs={{0,16},{4,20},{8,24},{12,28},{16,0},{20,4},{24,8},{28,12},{1,17},{... | collective-permute-start | bytes 196616 | tf_op jit(solution)/shard_map/ppermute | solution.py:353
  (22 other events, 113.9 us)

commit v4 on v2

--- a/solution.py
+++ b/solution.py
@@ -1,4 +1,5 @@
 import functools
+import math
 import jax
 import jax.numpy as jnp
 from jax import lax
@@ -7,8 +8,10 @@
 from jax.sharding import PartitionSpec as P
 
 DEGREE = 4
-UNROLL = 16
-CHUNK = 24
+UNROLL = 48
+CHUNK = 6
+STREAMS = 4
+APPLY_BYTES = 4 << 20
 F32, BF16, I32 = jnp.float32, jnp.bfloat16, jnp.int32
 precise = lax.Precision.HIGHEST
 center = 1.025
@@ -47,123 +50,108 @@
     )(*args)
 
 
-def prep_kernel(rows, ids_ref, own_ref, col_ref, blk_ref, w_ref, inv_ref, src_ref, row_ref, num_ref,
-                eye_ref, state_ref):
-    chunk, n, _ = blk_ref.shape
+def prep_kernel(rows, ids_ref, own_ref, col_ref, *refs):
+    blks, (w_ref, inv_ref, table_ref, eye_ref) = refs[:-4], refs[-4:]
+    chunk, n, _ = blks[0].shape
     half = rows // 2
     step = pl.program_id(0)
     me = ids_ref[0]
     odd = me % 2
-    zero = jnp.zeros(w_ref.shape[1:], BF16)
+    count = own_ref.shape[1]
 
     @pl.when(step == 0)
     def _():
-        state_ref[0] = 0
-        state_ref[1] = -1
+        table_ref[0] = me
+        table_ref[1] = ids_ref[1]
         inv_ref[...] = jnp.zeros(inv_ref.shape, F32)
         lines = lax.broadcasted_iota(I32, eye_ref.shape, 0)
         lanes = lax.broadcasted_iota(I32, eye_ref.shape, 1)
         eye_ref[...] = jnp.where((lines == lanes) | (lines >= n), 1.0, 0.0).astype(BF16)
 
-    at = state_ref[0]
-    last = state_ref[1]
-    for c in range(chunk):
-        b = step * chunk + c
-        r = own_ref[0, b]
-        k = col_ref[0, b]
-        at = jnp.where(r == last, at, (at + 1) // 2 * 2)
-        last = r
-        owner = k // rows
-        local = k - owner * rows
-        upper = (local >= half).astype(I32)
-        near = local - half * upper
-        swap = odd * upper + (1 - odd) * (1 - upper)
-        src_ref[at] = jnp.where(owner == me, near + half * swap, 2 * half + near + half * (1 - swap))
-        src_ref[at + 1] = 0
-        top = (r >= half).astype(I32)
-        r_at = r + half * (1 - odd) * (1 - 2 * top)
-        row_ref[at // 2] = r_at
-        w_ref[at + 1] = zero
-        a = blk_ref[c]
-        high = a.astype(BF16)
-        low = (a - high.astype(F32)).astype(BF16)
-        both = jnp.concatenate([high, low], axis=0)
-        t = lax.dot_general(
-            eye_ref[...], both, (((1,), (1,)), ((), ())), preferred_element_type=F32
-        )
-        w_ref[at] = t[:n].astype(BF16)
-        inv_ref[r_at] = inv_ref[r_at] + (t[n:n + 1, :n] + t[n:n + 1, n:])
-        at = at + 1
-    state_ref[0] = at
-    state_ref[1] = last
+    for i, blk_ref in enumerate(blks):
+        for c in range(chunk):
+            b = (step * len(blks) + i) * chunk + c
+            r = own_ref[0, b]
+            k = col_ref[0, b]
+            owner = k // rows
+            local = k - owner * rows
+            upper = (local >= half).astype(I32)
+            near = local - half * upper
+            swap = odd * upper + (1 - odd) * (1 - upper)
+            slot = jnp.where(owner == me, near + half * swap, 2 * half + near + half * (1 - swap))
+            top = (r >= half).astype(I32)
+            r_at = r + half * (1 - odd) * (1 - 2 * top)
+            table_ref[2 + b] = slot
+            table_ref[2 + count + b] = r_at
+            a = blk_ref[c]
+            high = a.astype(BF16)
+            low = (a - high.astype(F32)).astype(BF16)
+            both = jnp.concatenate([high, low], axis=0)
+            t = lax.dot_general(
+                eye_ref[...], both, (((1,), (1,)), ((), ())), preferred_element_type=F32
+            )
+            w_ref[b] = t[:n].astype(BF16)
+            inv_ref[r_at] = inv_ref[r_at] + (t[n:n + 1, :n] + t[n:n + 1, n:])
 
     @pl.when(step == pl.num_programs(0) - 1)
     def _():
-        used = (at + 1) // 2
-        upto = (used + UNROLL - 1) // UNROLL * UNROLL
-        def fill(p, c):
-            row_ref[p] = rows
-            for s in range(2):
-                w_ref[2 * p + s] = zero
-                src_ref[2 * p + s] = 0
-            return c
-        lax.fori_loop(used, upto, fill, 0)
-        num_ref[0] = upto // UNROLL
         inv_ref[...] = 1.0 / inv_ref[...]
 
 
 def prep(ids, own, col, blocks, rows):
     count, n, _ = blocks.shape
-    chunk = CHUNK if count % CHUNK == 0 else 1
-    slots = ((count + rows) // 2 + UNROLL) // UNROLL * UNROLL * 2
+    chunk = math.gcd(count, STREAMS * CHUNK) // STREAMS
+    blocks = pltpu.with_memory_space_constraint(blocks, pltpu.HBM)
+
+    def stream(i):
+        return pl.BlockSpec((chunk, n, n), lambda step: (STREAMS * step + i, 0, 0))
+
     return pl.pallas_call(
         functools.partial(prep_kernel, rows),
-        grid=(count // chunk,),
-        in_specs=[IN_SMEM, IN_SMEM, IN_SMEM, pl.BlockSpec((chunk, n, n), lambda i: (i, 0, 0))],
-        out_specs=[IN_VMEM, IN_VMEM, IN_SMEM, IN_SMEM, IN_SMEM],
-        out_shape=[pltpu.VMEM((slots, n, 2 * n), BF16),
+        grid=(count // (STREAMS * chunk),),
+        in_specs=[IN_SMEM] * 3 + [stream(i) for i in range(STREAMS)],
+        out_specs=[IN_VMEM, IN_VMEM, IN_SMEM],
+        out_shape=[pltpu.VMEM((count, n, 2 * n), BF16),
                    jax.ShapeDtypeStruct((rows, 1, n), F32),
-                   jax.ShapeDtypeStruct((slots,), I32),
-                   jax.ShapeDtypeStruct((slots // 2,), I32),
-                   jax.ShapeDtypeStruct((1,), I32)],
-        scratch_shapes=[pltpu.VMEM((n + 16, n), BF16), pltpu.SMEM((2,), I32)],
+                   jax.ShapeDtypeStruct((2 + 2 * count,), I32)],
+        scratch_shapes=[pltpu.VMEM((n + 16, n), BF16)],
         compiler_params=pltpu.CompilerParams(vmem_limit_bytes=12 * MIB),
         cost_estimate=pl.CostEstimate(
             flops=2 * count * n * n * n, bytes_accessed=4 * blocks.size, transcendentals=0
         ),
         name="prep",
-    )(ids, own, col, blocks)
+    )(ids, own, col, *[blocks] * STREAMS)
 
 
 def apply_kernel(recur, mate, *refs):
     refs = list(refs)
-    ids_ref, src_ref, row_ref, num_ref, w_ref, inv_ref = refs[:6]
-    panels = refs[6:10]
-    del refs[:10]
+    table_ref, w_ref, inv_ref = refs[:3]
+    panels = refs[3:7]
+    del refs[:7]
     olds = [refs.pop(0) for _ in range(2 if recur else 0)]
     mates = [refs.pop(0) for _ in range(2 if mate else 0)]
     outs = [refs.pop(0) for _ in range(2)]
     parts = refs[:-2]
     sp_ref, acc_ref = refs[-2:]
     half, kk, n = panels[0].shape
+    blocks = w_ref.shape[0]
     for i, ref in enumerate(panels):
         v = ref[...]
         high = v.astype(BF16)
         sp_ref[i * half:(i + 1) * half, :kk] = high
         sp_ref[i * half:(i + 1) * half, kk:] = (v - high.astype(F32)).astype(BF16)
     acc_ref[...] = jnp.zeros(acc_ref.shape, F32)
+    unroll = math.gcd(blocks, UNROLL)
 
     def group(g, c):
-        for u in range(UNROLL):
-            p = g * UNROLL + u
-            piece = jnp.concatenate([sp_ref[src_ref[2 * p]], sp_ref[src_ref[2 * p + 1]]], axis=1)
-            w = w_ref[pl.ds(2 * p, 2)].reshape(2 * n, 2 * n)
-            y = jnp.dot(piece, w, preferred_element_type=F32)
-            r = row_ref[p]
+        for u in range(unroll):
+            b = g * unroll + u
+            y = jnp.dot(sp_ref[table_ref[2 + b]], w_ref[b], preferred_element_type=F32)
+            r = table_ref[2 + blocks + b]
             acc_ref[r] = acc_ref[r] + ((y[:kk, :n] + y[kk:, :n]) + (y[:kk, n:] + y[kk:, n:]))
         return c
 
-    lax.fori_loop(0, num_ref[0], group, 0)
+    lax.fori_loop(0, blocks // unroll, group, 0)
     scale = (2.0 if recur else 1.0) / half_width
     for i in range(2):
         span = slice(i * half, (i + 1) * half)
@@ -174,11 +162,10 @@
         outs[i][...] = image
         if mate:
             acc_ref[span] = image
-            sp_ref2 = parts[-1]
-            sp_ref2[span] = mates[i][...]
+            parts[-1][span] = mates[i][...]
     if mate:
         count = len(parts) - 1
-        me = ids_ref[1]
+        me = table_ref[1]
         each = 2 * half // count
         for s in range(count):
             at = pl.ds((me ^ s) * each, each)
@@ -186,28 +173,27 @@
             parts[s][:, kk:] = acc_ref[at]
 
 
-def apply(ids, meta, pair, halo, old=(), mate=(), count=0):
+def apply(meta, pair, halo, old=(), mate=(), count=0):
     half, kk, n = pair[0].shape
-    w = meta[3]
     out = [jax.ShapeDtypeStruct((half, kk, n), F32)] * 2
     if mate:
         out += [jax.ShapeDtypeStruct((2 * half // count, 2 * kk, n), F32)] * count
     args = (*pair, *halo, *old, *mate)
-    scratch = [pltpu.VMEM((4 * half, 2 * kk, n), BF16), pltpu.VMEM((2 * half + 1, kk, n), F32)]
+    scratch = [pltpu.VMEM((4 * half, 2 * kk, n), BF16), pltpu.VMEM((2 * half, kk, n), F32)]
     if mate:
         scratch = [pltpu.VMEM((2 * half, kk, n), F32)] + scratch
     res = pl.pallas_call(
         functools.partial(apply_kernel, bool(old), bool(mate)),
-        in_specs=[IN_SMEM] * 4 + [IN_VMEM] * (2 + len(args)),
+        in_specs=[IN_SMEM] + [IN_VMEM] * (2 + len(args)),
         out_specs=[IN_VMEM] * len(out),
         out_shape=out,
         scratch_shapes=scratch,
         compiler_params=pltpu.CompilerParams(vmem_limit_bytes=12 * MIB),
         cost_estimate=pl.CostEstimate(
-            flops=8 * w.shape[0] * n * n * kk, bytes_accessed=2 * w.size, transcendentals=0
+            flops=0, bytes_accessed=APPLY_BYTES, transcendentals=0
         ),
         name="apply" + "_recur" * bool(old) + "_parts" * bool(mate),
-    )(ids, *meta, *args)
+    )(*meta, *args)
     return tuple(res[:2]), tuple(res[2:])
 
 
@@ -357,13 +343,8 @@
     return [parts[0]] + [swap(parts[s], "col", s) for s in range(1, len(parts))]
 
 
-def summed(value, *axes):
-    for axis in axes:
-        hop = 1
-        while hop < lax.axis_size(axis):
-            value = value + swap(value, axis, hop)
-            hop *= 2
-    return value
+def hops_of(*axes):
+    return [(axis, 1 << i) for axis in axes for i in range((lax.axis_size(axis) - 1).bit_length())]
 
 
 def body(blocks, owner_row, block_col, start):
@@ -383,40 +364,61 @@
 
     halves = call(split_kernel, "split", [(half, each, block)] * 4, ids, start, scalars=1)
     before = [tuple(halves[:2]), tuple(halves[2:])]
-    w, inv, src, row, num = prep(ids, owner_row, block_col, blocks, slots)
-    meta = (src, row, num, w, inv)
+    w, inv, table = prep(ids, owner_row, block_col, blocks, slots)
+    meta = (table, w, inv)
 
     def advance(now, before=((), ()), parts=False):
-        first, _ = apply(ids, meta, now[0], exchange(now[0]), before[0])
+        first, _ = apply(meta, now[0], exchange(now[0]), before[0])
         mate = first if parts else ()
-        second, out = apply(ids, meta, now[1], exchange(now[1]), before[1], mate, count)
-        return [first, second], (swapped(out) if parts else None)
+        second, out = apply(meta, now[1], exchange(now[1]), before[1], mate, count)
+        return [first, second], out
 
     now, _ = advance(before)
     for step in range(DEGREE - 1):
         after, parts = advance(now, before, step == DEGREE - 2)
         before, now = now, after
-    panel, gram_first = call(gram_kernel, "gram", [wide, square], ids, *parts, scalars=1)
-    gram = summed(gram_first, "col", "node")
+    panel, gram_first = call(gram_kernel, "gram", [wide, square], ids, *swapped(parts), scalars=1)
     after, parts = advance(now, parts=True)
     before, now = now, after
     (cross_first,) = call(
-        cross_kernel, "cross", [square], ids, panel, *parts, scalars=1, scratch=[held]
-    )
+        cross_kernel, "cross", [square], ids, panel, *swapped(parts), scalars=1, scratch=[held]
+    )
+    got, hops = None, hops_of("col", "node")
+    gram = gram_first
+    for step in range(DEGREE - 1):
+        after = []
+        for i in range(2):
+            old, gram, got = lax.optimization_barrier((before[i], gram, got))
+            if got is not None:
+                gram = gram + got
+            got = swap(gram, *hops.pop(0)) if hops else None
+            mate = after[0] if i == 1 and step == DEGREE - 2 else ()
+            done, parts = apply(meta, now[i], exchange(now[i]), old, mate, count)
+            after.append(done)
+            if got is not None:
+                gram, got, _ = lax.optimization_barrier((gram, got, done))
+        before, now = now, after
+    if got is not None:
+        gram = gram + got
+    for hop in hops:
+        gram = gram + swap(gram, *hop)
     inverse_first = inverse_factor(gram, nodes)
-    for step in range(DEGREE - 1):
-        if step == DEGREE - 2:
-            now, inverse_first = lax.optimization_barrier((now, inverse_first))
-        after, parts = advance(now, before, step == DEGREE - 2)
-        before, now = now, after
-
+
+    arrived, halo = lax.optimization_barrier((swapped(parts), exchange(now[0])))
+    halos = [halo, exchange(now[1])]
     turned, gram_last = call(
-        turn_kernel, "turn", [wide, square], ids, inverse_first, *parts, scalars=1, scratch=[held]
-    )
-    gram = summed(gram_last, "col", "node")
-    _, parts = advance(now, parts=True)
+        turn_kernel, "turn", [wide, square], ids, inverse_first, *arrived, scalars=1, scratch=[held]
+    )
+    gram = gram_last
+    for i, hop in enumerate(hops_of("col", "node")):
+        got = swap(gram, *hop)
+        if i == 2:
+            got, halos[1] = lax.optimization_barrier((got, halos[1]))
+        gram = gram + got
+    first, _ = apply(meta, now[0], halos[0])
+    _, parts = apply(meta, now[1], halos[1], (), first, count)
     (cross_last,) = call(
-        turn_cross_kernel, "turn_cross", [square], ids, inverse_first, turned, *parts,
+        turn_cross_kernel, "turn_cross", [square], ids, inverse_first, turned, *swapped(parts),
         scalars=1, scratch=[held],
     )
     inverse_last = inverse_factor(gram, nodes)
@@ -424,15 +426,20 @@
         basis_kernel, "basis", [(quarter, cols_here, block)] * count, ids, inverse_last, turned,
         scalars=1, scratch=[held],
     )
-    (basis,) = call(
-        functools.partial(join_kernel, half), "join", [(cols_here, width)], ids, *swapped(parts), scalars=1
-    )
+    arrived = swapped(parts)
     parts = call(
         functools.partial(proj_kernel, nodes), "proj", [(2, cols_here, vecs)] * count, ids,
         inverse_first, cross_first, gram_first, inverse_last, cross_last, gram_last,
         scalars=1, scratch=[pltpu.VMEM(square, F32)],
     )
-    projected = summed(sum(swapped(parts)), "node")
+    projected = sum(swapped(parts))
+    for i, hop in enumerate(hops_of("node")):
+        projected = projected + swap(projected, *hop)
+        if i == 0:
+            projected, arrived = lax.optimization_barrier((projected, arrived))
+            (basis,) = call(
+                functools.partial(join_kernel, half), "join", [(cols_here, width)], ids, *arrived, scalars=1
+            )
     return basis, projected[0], projected[1]
 
 

time: 320 us -> 262 us (0.82)
  Pallas kernels: 161 us -> 131 us
  local copies, waits for them, and re-layouts: 24.7 us -> 3.11 us
  waiting for transfers between devices: 45.3 us -> 35.7 us
  starting transfers between devices: 86.5 us -> 90.2 us
    pallas_call x18, Pallas kernels: 117 us -> 83.2 us  [apply(): pl.pallas_call(functools.partial(apply_kernel, bool(old), bool(mate)), in...]
    unnamed x24 -> x6, local copies, waits for them, and re-layouts: 24 us -> 2.49 us
    ppermute x31, starting transfers between devices: 29.6 us -> 21.1 us  [swap(): lax.ppermute(value, axis, [(i, i ^ hop) for i in range(lax.axis_size(axis...]
    ppermute x31, waiting for transfers between devices: 35.5 us -> 27.7 us  [swap(): lax.ppermute(value, axis, [(i, i ^ hop) for i in range(lax.axis_size(axis...]
    ppermute x18, starting transfers between devices: 42 us -> 49.1 us  [exchange(): lax.ppermute(pair[1], 'node', odd)]
    ppermute x18, starting transfers between devices: 14.9 us -> 19.9 us  [exchange(): lax.ppermute(pair[0], 'node', even)]
  transfers between devices with their start and end apart: 67 -> 67, of which waited for: 14 -> 17; matrix products, arithmetic and copies ran while one was open for 0% -> 0% of each run, Pallas kernels for 43% -> 46%
where the time goes in v4:
time: 262 us
  Pallas kernels  131 us (50%)
  starting transfers between devices  90.2 us (34%)
  waiting for transfers between devices  35.7 us (14%)
  local copies, waits for them, and re-layouts  3.11 us (1%)
    pallas_call x18, Pallas kernels, apply(): pl.pallas_call(functools.partial(apply_kernel, bool(old), bool(mate)), in...  83.2 us
    ppermute x18, starting transfers between devices, exchange(): lax.ppermute(pair[1], 'node', odd)  49.1 us
    pallas_call x10, Pallas kernels, call(): pl.pallas_call(kernel, in_specs=[IN_SMEM] * scalars + [IN_VMEM] * (len(ar...  33.9 us
    ppermute x31, waiting for transfers between devices, swap(): lax.ppermute(value, axis, [(i, i ^ hop) for i in range(lax.axis_size(axis...  27.7 us
    ppermute x31, starting transfers between devices, swap(): lax.ppermute(value, axis, [(i, i ^ hop) for i in range(lax.axis_size(axis...  21.1 us
    ppermute x18, starting transfers between devices, exchange(): lax.ppermute(pair[0], 'node', even)  19.9 us
    pallas_call x1, Pallas kernels, prep(): pl.pallas_call(functools.partial(prep_kernel, rows), grid=(count // (STRE...  14.3 us
    ppermute x18, waiting for transfers between devices, exchange(): lax.ppermute(pair[0], 'node', even)  8.04 us
  transfers between devices with their start and end apart: 67, of which 17 were waited for; matrix products, arithmetic and copies ran while one was open for 0% of the time, Pallas kernels for 46%

profile of v4, /device:TPU:0, one launch (start us, length us, event | category | flops | bytes accessed | tf_op | source)
XLA Modules:
  0.0 261.7 jit_solution(8023755321851284697)
XLA Ops:
  2.5 3.0 %collective-permute-start.8 = (f32[24,16,128]{2,1,0:T(8,128)S(1)}, f32[24,16,128]{2,1,0:T(8,128)S(1)}, u32[]{:S(2)}, u32[]{:S(2)}) collective-permute-start(f32[24,16,128]{2,1,0:T(8,128)S(1)} %get-tuple-element.130.refs_3_.refs_7_), channel_id=1, source_target_pairs={{0,4},{4,0},{8,12},{12,8},{16,20},{20,16},{24,28},{28,24},{1,5},{5... | collective-permute-start | bytes 589832 | tf_op jit(solution)/shard_map/ppermute | solution.py:335
  5.5 3.5 %collective-permute-start.9 = (f32[24,16,128]{2,1,0:T(8,128)S(1)}, f32[24,16,128]{2,1,0:T(8,128)S(1)}, u32[]{:S(2)}, u32[]{:S(2)}) collective-permute-start(f32[24,16,128]{2,1,0:T(8,128)S(1)} %get-tuple-element.131.refs_4_.refs_8_), channel_id=1, source_target_pairs={{0,28},{4,8},{8,4},{12,16},{16,12},{20,24},{24,20},{28,0},{1,29},{... | collective-permute-start | bytes 589832 | tf_op jit(solution)/shard_map/ppermute | solution.py:335
  12.4 14.3 %prep.1 = (bf16[288,128,256]{2,1,0:T(8,128)(2,1)S(1)}, f32[48,1,128]{2,1,0:T(1,128)S(1)}, s32[578]{0:T(1024)S(1)}) custom-call(s32[2]{0:T(128)S(1)} %pad_add_fusion.ids_ref, s32[1,288]{1,0:T(1,128)S(1)} %copy-done.1, s32[1,288]{1,0:T(1,128)S(1)} %copy-done.2, f32[288,128,128]{2,1,0:T(8,128)} %refs_3_.1, f32[288,128,128]{2,1,0:T(8,128)} %refs_3_.1, ...), custom_call_target="tpu_custom_call" | custom-call | flops 1207959552 | bytes 18874368 | tf_op jit(solution)/shard_map/prep/pallas_call | solution.py:109
  26.6 4.5 %apply.5 = (f32[24,16,128]{2,1,0:T(8,128)S(1)}, f32[24,16,128]{2,1,0:T(8,128)S(1)}) custom-call(s32[578]{0:T(1024)S(1)} %get-tuple-element.119.refs_0_, bf16[288,128,256]{2,1,0:T(8,128)(2,1)S(1)} %get-tuple-element.120.refs_1_, f32[48,1,128]{2,1,0:T(1,128)S(1)} %get-tuple-element.121.refs_2_, f32[24,16,128]{2,1,0:T(8,128)S(1)} %get-tuple-element.130.refs_3_.refs_7_, ...), custom_call_target="tpu_custom_call" | custom-call | bytes 4194304 | tf_op jit(solution)/shard_map/apply/pallas_call | solution.py:185
  31.9 2.2 collective-permute-start.11
  34.1 4.5 %apply.4 = (f32[24,16,128]{2,1,0:T(8,128)S(1)}, f32[24,16,128]{2,1,0:T(8,128)S(1)}) custom-call(s32[578]{0:T(1024)S(1)} %get-tuple-element.119.refs_0_, bf16[288,128,256]{2,1,0:T(8,128)(2,1)S(1)} %get-tuple-element.120.refs_1_, f32[48,1,128]{2,1,0:T(1,128)S(1)} %get-tuple-element.121.refs_2_, f32[24,16,128]{2,1,0:T(8,128)S(1)} %get-tuple-element.122.refs_3_.refs_7_, ...), custom_call_target="tpu_custom_call" | custom-call | bytes 4194304 | tf_op jit(solution)/shard_map/apply/pallas_call | solution.py:185
  41.9 4.5 %apply_recur.12 = (f32[24,16,128]{2,1,0:T(8,128)S(1)}, f32[24,16,128]{2,1,0:T(8,128)S(1)}) custom-call(s32[578]{0:T(1024)S(1)} %get-tuple-element.119.refs_0_, bf16[288,128,256]{2,1,0:T(8,128)(2,1)S(1)} %get-tuple-element.120.refs_1_, f32[48,1,128]{2,1,0:T(1,128)S(1)} %get-tuple-element.121.refs_2_, f32[24,16,128]{2,1,0:T(8,128)S(1)} %get-tuple-element.132.refs_3_.refs_7_, ...), custom_call_target="tpu_custom_call" | custom-call | bytes 4194304 | tf_op jit(solution)/shard_map/apply_recur/pallas_call | solution.py:185
  46.4 3.1 %collective-permute-start.12 = (f32[24,16,128]{2,1,0:T(8,128)S(1)}, f32[24,16,128]{2,1,0:T(8,128)S(1)}, u32[]{:S(2)}, u32[]{:S(2)}) collective-permute-start(f32[24,16,128]{2,1,0:T(8,128)S(1)} %get-tuple-element.134.refs_3_.refs_7_), channel_id=1, source_target_pairs={{0,4},{4,0},{8,12},{12,8},{16,20},{20,16},{24,28},{28,24},{1,5},{5... | collective-permute-start | bytes 589832 | tf_op jit(solution)/shard_map/ppermute | solution.py:335
  49.5 5.3 %collective-permute-start.13 = (f32[24,16,128]{2,1,0:T(8,128)S(1)}, f32[24,16,128]{2,1,0:T(8,128)S(1)}, u32[]{:S(2)}, u32[]{:S(2)}) collective-permute-start(f32[24,16,128]{2,1,0:T(8,128)S(1)} %get-tuple-element.135.refs_4_.refs_8_), channel_id=1, source_target_pairs={{0,28},{4,8},{8,4},{12,16},{16,12},{20,24},{24,20},{28,0},{1,29},{... | collective-permute-start | bytes 589832 | tf_op jit(solution)/shard_map/ppermute | solution.py:335
  54.8 4.5 %apply_recur.10 = (f32[24,16,128]{2,1,0:T(8,128)S(1)}, f32[24,16,128]{2,1,0:T(8,128)S(1)}) custom-call(s32[578]{0:T(1024)S(1)} %get-tuple-element.119.refs_0_, bf16[288,128,256]{2,1,0:T(8,128)(2,1)S(1)} %get-tuple-element.120.refs_1_, f32[48,1,128]{2,1,0:T(1,128)S(1)} %get-tuple-element.121.refs_2_, f32[24,16,128]{2,1,0:T(8,128)S(1)} %get-tuple-element.124.refs_3_.refs_7_, ...), custom_call_target="tpu_custom_call" | custom-call | bytes 4194304 | tf_op jit(solution)/shard_map/apply_recur/pallas_call | solution.py:185
  61.1 4.5 %apply_recur.13 = (f32[24,16,128]{2,1,0:T(8,128)S(1)}, f32[24,16,128]{2,1,0:T(8,128)S(1)}) custom-call(s32[578]{0:T(1024)S(1)} %get-tuple-element.119.refs_0_, bf16[288,128,256]{2,1,0:T(8,128)(2,1)S(1)} %get-tuple-element.120.refs_1_, f32[48,1,128]{2,1,0:T(1,128)S(1)} %get-tuple-element.121.refs_2_, f32[24,16,128]{2,1,0:T(8,128)S(1)} %get-tuple-element.134.refs_3_.refs_7_, ...), custom_call_target="tpu_custom_call" | custom-call | bytes 4194304 | tf_op jit(solution)/shard_map/apply_recur/pallas_call | solution.py:185
  66.1 4.9 %collective-permute-start.15 = (f32[24,16,128]{2,1,0:T(8,128)S(1)}, f32[24,16,128]{2,1,0:T(8,128)S(1)}, u32[]{:S(2)}, u32[]{:S(2)}) collective-permute-start(f32[24,16,128]{2,1,0:T(8,128)S(1)} %get-tuple-element.137.refs_4_), channel_id=1, source_target_pairs={{0,28},{4,8},{8,4},{12,16},{16,12},{20,24},{24,20},{28,0},{1,29},{... | collective-permute-start | bytes 589832 | tf_op jit(solution)/shard_map/ppermute | solution.py:335
  71.3 4.5 %apply_recur.11 = (f32[24,16,128]{2,1,0:T(8,128)S(1)}, f32[24,16,128]{2,1,0:T(8,128)S(1)}) custom-call(s32[578]{0:T(1024)S(1)} %get-tuple-element.119.refs_0_, bf16[288,128,256]{2,1,0:T(8,128)(2,1)S(1)} %get-tuple-element.120.refs_1_, f32[48,1,128]{2,1,0:T(1,128)S(1)} %get-tuple-element.121.refs_2_, f32[24,16,128]{2,1,0:T(8,128)S(1)} %get-tuple-element.126.refs_3_.refs_7_, ...), custom_call_target="tpu_custom_call" | custom-call | bytes 4194304 | tf_op jit(solution)/shard_map/apply_recur/pallas_call | solution.py:185
  75.9 3.5 %collective-permute-start.7 = (f32[24,16,128]{2,1,0:T(8,128)S(1)}, f32[24,16,128]{2,1,0:T(8,128)S(1)}, u32[]{:S(2)}, u32[]{:S(2)}) collective-permute-start(f32[24,16,128]{2,1,0:T(8,128)S(1)} %get-tuple-element.129.refs_4_), channel_id=1, source_target_pairs={{0,28},{4,8},{8,4},{12,16},{16,12},{20,24},{24,20},{28,0},{1,29},{... | collective-permute-start | bytes 589832 | tf_op jit(solution)/shard_map/ppermute | solution.py:335
  79.7 4.5 %apply_recur.14 = (f32[24,16,128]{2,1,0:T(8,128)S(1)}, f32[24,16,128]{2,1,0:T(8,128)S(1)}) custom-call(s32[578]{0:T(1024)S(1)} %get-tuple-element.119.refs_0_, bf16[288,128,256]{2,1,0:T(8,128)(2,1)S(1)} %get-tuple-element.120.refs_1_, f32[48,1,128]{2,1,0:T(1,128)S(1)} %get-tuple-element.121.refs_2_, f32[24,16,128]{2,1,0:T(8,128)S(1)} %get-tuple-element.136.refs_3_, ...), custom_call_target="tpu_custom_call" | custom-call | bytes 4194304 | tf_op jit(solution)/shard_map/apply_recur/pallas_call | solution.py:185
  84.3 2.4 collective-permute-start.19
  86.8 4.7 %apply_recur_parts.2 = (f32[24,16,128]{2,1,0:T(8,128)S(1)}, f32[24,16,128]{2,1,0:T(8,128)S(1)}, f32[12,32,128]{2,1,0:T(8,128)S(1)}, f32[12,32,128]{2,1,0:T(8,128...) custom-call(s32[578]{0:T(1024)S(1)} %get-tuple-element.119.refs_0_, ...), custom_call_target="tpu_custom_call" | custom-call | bytes 4194304 | tf_op jit(solution)/shard_map/apply_recur_parts/pallas_call | solution.py:185
  91.5 5.0 %collective-permute-start.17 = (f32[24,16,128]{2,1,0:T(8,128)S(1)}, f32[24,16,128]{2,1,0:T(8,128)S(1)}, u32[]{:S(2)}, u32[]{:S(2)}) collective-permute-start(f32[24,16,128]{2,1,0:T(8,128)S(1)} %get-tuple-element.159.refs_4_.refs_8_), channel_id=1, source_target_pairs={{0,28},{4,8},{8,4},{12,16},{16,12},{20,24},{24,20},{28,0},{1,29},{... | collective-permute-start | bytes 589832 | tf_op jit(solution)/shard_map/ppermute | solution.py:335
  98.8 4.5 %apply.6 = (f32[24,16,128]{2,1,0:T(8,128)S(1)}, f32[24,16,128]{2,1,0:T(8,128)S(1)}) custom-call(s32[578]{0:T(1024)S(1)} %get-tuple-element.119.refs_0_, bf16[288,128,256]{2,1,0:T(8,128)(2,1)S(1)} %get-tuple-element.120.refs_1_, f32[48,1,128]{2,1,0:T(1,128)S(1)} %get-tuple-element.121.refs_2_, f32[24,16,128]{2,1,0:T(8,128)S(1)} %get-tuple-element.152.refs_9_.refs_3_.refs_7_, ...), custom_call_target="tpu_custom_call" | custom-call | bytes 4194304 | tf_op jit(solution)/shard_map/apply/pallas_call | solution.py:185
  103.4 2.3 collective-permute-start.26
  106.0 4.6 %apply_parts.2 = (f32[24,16,128]{2,1,0:T(8,128)S(1)}, f32[24,16,128]{2,1,0:T(8,128)S(1)}, f32[12,32,128]{2,1,0:T(8,128)S(1)}, f32[12,32,128]{2,1,0:T(8,128)S(1)}...) custom-call(s32[578]{0:T(1024)S(1)} %get-tuple-element.119.refs_0_, ...), custom_call_target="tpu_custom_call" | custom-call | bytes 4194304 | tf_op jit(solution)/shard_map/apply_parts/pallas_call | solution.py:185
  111.7 3.6 %collective-permute-start.21 = (f32[24,16,128]{2,1,0:T(8,128)S(1)}, f32[24,16,128]{2,1,0:T(8,128)S(1)}, u32[]{:S(2)}, u32[]{:S(2)}) collective-permute-start(f32[24,16,128]{2,1,0:T(8,128)S(1)} %get-tuple-element.177.refs_4_.refs_8_), channel_id=1, source_target_pairs={{0,28},{4,8},{8,4},{12,16},{16,12},{20,24},{24,20},{28,0},{1,29},{... | collective-permute-start | bytes 589832 | tf_op jit(solution)/shard_map/ppermute | solution.py:335
  119.4 4.5 %apply_recur.15 = (f32[24,16,128]{2,1,0:T(8,128)S(1)}, f32[24,16,128]{2,1,0:T(8,128)S(1)}) custom-call(s32[578]{0:T(1024)S(1)} %get-tuple-element.119.refs_0_, bf16[288,128,256]{2,1,0:T(8,128)(2,1)S(1)} %get-tuple-element.120.refs_1_, f32[48,1,128]{2,1,0:T(1,128)S(1)} %get-tuple-element.121.refs_2_, f32[24,16,128]{2,1,0:T(8,128)S(1)} %get-tuple-element.168.refs_7_.refs_3_, ...), custom_call_target="tpu_custom_call" | custom-call | bytes 4194304 | tf_op jit(solution)/shard_map/apply_recur/pallas_call | solution.py:185
  124.0 2.6 collective-permute-start.30
  126.5 4.7 %apply_recur.16 = (f32[24,16,128]{2,1,0:T(8,128)S(1)}, f32[24,16,128]{2,1,0:T(8,128)S(1)}) custom-call(s32[578]{0:T(1024)S(1)} %get-tuple-element.119.refs_0_, bf16[288,128,256]{2,1,0:T(8,128)(2,1)S(1)} %get-tuple-element.120.refs_1_, f32[48,1,128]{2,1,0:T(1,128)S(1)} %get-tuple-element.121.refs_2_, f32[24,16,128]{2,1,0:T(8,128)S(1)} %get-tuple-element.176.refs_3_.refs_7_, ...), custom_call_target="tpu_custom_call" | custom-call | bytes 4194304 | tf_op jit(solution)/shard_map/apply_recur/pallas_call | solution.py:185
  132.6 3.7 %collective-permute-start.34 = (f32[24,16,128]{2,1,0:T(8,128)S(1)}, f32[24,16,128]{2,1,0:T(8,128)S(1)}, u32[]{:S(2)}, u32[]{:S(2)}) collective-permute-start(f32[24,16,128]{2,1,0:T(8,128)S(1)} %get-tuple-element.198.refs_4_.refs_8_), channel_id=1, source_target_pairs={{0,28},{4,8},{8,4},{12,16},{16,12},{20,24},{24,20},{28,0},{1,29},{... | collective-permute-start | bytes 589832 | tf_op jit(solution)/shard_map/ppermute | solution.py:335
  137.8 2.8 %collective-permute-done.28 = f32[128,128]{1,0:T(8,128)S(1)} collective-permute-done((f32[128,128]{1,0:T(8,128)S(1)}, f32[128,128]{1,0:T(8,128)S(1)}, u32[]{:S(2)}, u32[]{:S(2)}) %collective-permute-start.28) | collective-permute-done | bytes 65568 | tf_op jit(solution)/shard_map/ppermute | solution.py:339
  140.7 4.5 %apply_recur.17 = (f32[24,16,128]{2,1,0:T(8,128)S(1)}, f32[24,16,128]{2,1,0:T(8,128)S(1)}) custom-call(s32[578]{0:T(1024)S(1)} %get-tuple-element.119.refs_0_, bf16[288,128,256]{2,1,0:T(8,128)(2,1)S(1)} %get-tuple-element.120.refs_1_, f32[48,1,128]{2,1,0:T(1,128)S(1)} %get-tuple-element.121.refs_2_, f32[24,16,128]{2,1,0:T(8,128)S(1)} %get-tuple-element.184.refs_3_.refs_7_, ...), custom_call_target="tpu_custom_call" | custom-call | bytes 4194304 | tf_op jit(solution)/shard_map/apply_recur/pallas_call | solution.py:185
  148.4 4.5 %apply_recur.18 = (f32[24,16,128]{2,1,0:T(8,128)S(1)}, f32[24,16,128]{2,1,0:T(8,128)S(1)}) custom-call(s32[578]{0:T(1024)S(1)} %get-tuple-element.119.refs_0_, bf16[288,128,256]{2,1,0:T(8,128)(2,1)S(1)} %get-tuple-element.120.refs_1_, f32[48,1,128]{2,1,0:T(1,128)S(1)} %get-tuple-element.121.refs_2_, f32[24,16,128]{2,1,0:T(8,128)S(1)} %get-tuple-element.197.refs_3_.refs_7_, ...), custom_call_target="tpu_custom_call" | custom-call | bytes 4194304 | tf_op jit(solution)/shard_map/apply_recur/pallas_call | solution.py:185
  153.0 3.7 %collective-permute-start.42 = (f32[24,16,128]{2,1,0:T(8,128)S(1)}, f32[24,16,128]{2,1,0:T(8,128)S(1)}, u32[]{:S(2)}, u32[]{:S(2)}) collective-permute-start(f32[24,16,128]{2,1,0:T(8,128)S(1)} %get-tuple-element.179.refs_4_), channel_id=1, source_target_pairs={{0,28},{4,8},{8,4},{12,16},{16,12},{20,24},{24,20},{28,0},{1,29},{... | collective-permute-start | bytes 589832 | tf_op jit(solution)/shard_map/ppermute | solution.py:335
  156.8 4.8 %collective-permute-done.32 = f32[128,128]{1,0:T(8,128)S(1)} collective-permute-done((f32[128,128]{1,0:T(8,128)S(1)}, f32[128,128]{1,0:T(8,128)S(1)}, u32[]{:S(2)}, u32[]{:S(2)}) %collective-permute-start.32) | collective-permute-done | bytes 65568 | tf_op jit(solution)/shard_map/ppermute | solution.py:339
  162.4 4.5 %apply_recur.19 = (f32[24,16,128]{2,1,0:T(8,128)S(1)}, f32[24,16,128]{2,1,0:T(8,128)S(1)}) custom-call(s32[578]{0:T(1024)S(1)} %get-tuple-element.119.refs_0_, bf16[288,128,256]{2,1,0:T(8,128)(2,1)S(1)} %get-tuple-element.120.refs_1_, f32[48,1,128]{2,1,0:T(1,128)S(1)} %get-tuple-element.121.refs_2_, f32[24,16,128]{2,1,0:T(8,128)S(1)} %get-tuple-element.170.refs_3_, ...), custom_call_target="tpu_custom_call" | custom-call | bytes 4194304 | tf_op jit(solution)/shard_map/apply_recur/pallas_call | solution.py:185
  168.7 3.7 %collective-permute-start.47 = (f32[24,16,128]{2,1,0:T(8,128)S(1)}, f32[24,16,128]{2,1,0:T(8,128)S(1)}, u32[]{:S(2)}, u32[]{:S(2)}) collective-permute-start(f32[24,16,128]{2,1,0:T(8,128)S(1)} %get-tuple-element.187.refs_10_.refs_4_), channel_id=1, source_target_pairs={{0,28},{4,8},{8,4},{12,16},{16,12},{20,24},{24,20},{28,0},{1,29},{... | collective-permute-start | bytes 589832 | tf_op jit(solution)/shard_map/ppermute | solution.py:335
  172.4 4.7 %apply_recur_parts.3 = (f32[24,16,128]{2,1,0:T(8,128)S(1)}, f32[24,16,128]{2,1,0:T(8,128)S(1)}, f32[12,32,128]{2,1,0:T(8,128)S(1)}, f32[12,32,128]{2,1,0:T(8,128...) custom-call(s32[578]{0:T(1024)S(1)} %get-tuple-element.119.refs_0_, ...), custom_call_target="tpu_custom_call" | custom-call | bytes 4194304 | tf_op jit(solution)/shard_map/apply_recur_parts/pallas_call | solution.py:185
  179.0 8.4 %factor.2.inv_ref.refs_0_ = f32[128,128]{1,0:T(8,128)S(1)} custom-call(f32[128,128]{1,0:T(8,128)S(1)} %add.52.g_ref), custom_call_target="tpu_custom_call" | custom-call | tf_op jit(solution)/shard_map/factor/pallas_call | solution.py:41
  188.2 4.0 %turn.1 = (f32[12,128,128]{2,1,0:T(8,128)S(1)}, f32[128,128]{1,0:T(8,128)S(1)}) custom-call(s32[2]{0:T(128)S(1)} %pad_add_fusion.ids_ref, f32[128,128]{1,0:T(8,128)S(1)} %factor.2.inv_ref.refs_0_, f32[12,32,128]{2,1,0:T(8,128)S(1)} %get-tuple-element.203.refs_0_, f32[12,32,128]{2,1,0:T(8,128)S(1)} %collective-permute-done.43.refs_1_, ...), custom_call_target="tpu_custom_call" | custom-call | tf_op jit(solution)/shard_map/turn/pallas_call | solution.py:41
  195.4 2.8 %collective-permute-done.49 = f32[128,128]{1,0:T(8,128)S(1)} collective-permute-done((f32[128,128]{1,0:T(8,128)S(1)}, f32[128,128]{1,0:T(8,128)S(1)}, u32[]{:S(2)}, u32[]{:S(2)}) %collective-permute-start.49) | collective-permute-done | bytes 65568 | tf_op jit(solution)/shard_map/ppermute | solution.py:339
  200.5 4.0 %collective-permute-done.51.refs_5_ = f32[24,16,128]{2,1,0:T(8,128)S(1)} collective-permute-done((f32[24,16,128]{2,1,0:T(8,128)S(1)}, f32[24,16,128]{2,1,0:T(8,128)S(1)}, u32[]{:S(2)}, u32[]{:S(2)}) %collective-permute-start.51) | collective-permute-done | bytes 196640 | tf_op jit(solution)/shard_map/ppermute | solution.py:335
  206.0 4.7 %apply.7 = (f32[24,16,128]{2,1,0:T(8,128)S(1)}, f32[24,16,128]{2,1,0:T(8,128)S(1)}) custom-call(s32[578]{0:T(1024)S(1)} %get-tuple-element.119.refs_0_, bf16[288,128,256]{2,1,0:T(8,128)(2,1)S(1)} %get-tuple-element.120.refs_1_, f32[48,1,128]{2,1,0:T(1,128)S(1)} %get-tuple-element.121.refs_2_, f32[24,16,128]{2,1,0:T(8,128)S(1)} %get-tuple-element.186.refs_9_.refs_3_, ...), custom_call_target="tpu_custom_call" | custom-call | bytes 4194304 | tf_op jit(solution)/shard_map/apply/pallas_call | solution.py:185
  210.7 5.3 %apply_parts.3 = (f32[24,16,128]{2,1,0:T(8,128)}, f32[24,16,128]{2,1,0:T(8,128)}, f32[12,32,128]{2,1,0:T(8,128)S(1)}, f32[12,32,128]{2,1,0:T(8,128)S(1)}, f32[12...) custom-call(s32[578]{0:T(1024)S(1)} %get-tuple-element.119.refs_0_, ...), custom_call_target="tpu_custom_call" | custom-call | bytes 4194304 | tf_op jit(solution)/shard_map/apply_parts/pallas_call | solution.py:185
  218.9 2.2 cross.1.refs_1_
  221.1 3.1 %collective-permute-done.54 = f32[128,128]{1,0:T(8,128)S(1)} collective-permute-done((f32[128,128]{1,0:T(8,128)S(1)}, f32[128,128]{1,0:T(8,128)S(1)}, u32[]{:S(2)}, u32[]{:S(2)}) %collective-permute-start.54) | collective-permute-done | bytes 65568 | tf_op jit(solution)/shard_map/ppermute | solution.py:339
  224.3 8.4 %factor.3.refs_3_.inv_ref = f32[128,128]{1,0:T(8,128)S(1)} custom-call(f32[128,128]{1,0:T(8,128)S(1)} %add.57.g_ref), custom_call_target="tpu_custom_call" | custom-call | tf_op jit(solution)/shard_map/factor/pallas_call | solution.py:41
  232.7 4.0 %turn_cross.1.refs_4_ = f32[128,128]{1,0:T(8,128)S(1)} custom-call(s32[2]{0:T(128)S(1)} %pad_add_fusion.ids_ref, f32[128,128]{1,0:T(8,128)S(1)} %factor.2.inv_ref.refs_0_, f32[12,128,128]{2,1,0:T(8,128)S(1)} %get-tuple-element.211.f_ref, f32[12,32,128]{2,1,0:T(8,128)S(1)} %get-tuple-element.218.refs_0_, f32[12,32,128]{2,1,0:T(8,128)S(1)} %collective-permute-done.55.refs_1_, ...), custom_call_target="tpu_custom_call" | custom-call | tf_op jit(solution)/shard_map/turn_cross/pallas_call | solution.py:41
  243.6 3.7 %collective-permute-done.61 = f32[2,32,128]{2,1,0:T(8,128)S(1)} collective-permute-done((f32[2,32,128]{2,1,0:T(8,128)S(1)}, f32[2,32,128]{2,1,0:T(8,128)S(1)}, u32[]{:S(2)}, u32[]{:S(2)}) %collective-permute-start.61) | collective-permute-done | bytes 32800 | tf_op jit(solution)/shard_map/ppermute | solution.py:339
  247.3 2.2 collective-permute-done.63.refs_2_
  249.5 2.6 %collective-permute-done.64.refs_3_ = f32[12,32,128]{2,1,0:T(8,128)S(1)} collective-permute-done((f32[12,32,128]{2,1,0:T(8,128)S(1)}, f32[12,32,128]{2,1,0:T(8,128)S(1)}, u32[]{:S(2)}, u32[]{:S(2)}) %collective-permute-start.64) | collective-permute-done | bytes 196640 | tf_op jit(solution)/shard_map/ppermute | solution.py:339
  254.1 2.2 collective-permute-done.65
  (137 shorter events, 55.2 us)
Async XLA Ops:
  2.5 24.1 %collective-permute-start.8 = (f32[24,16,128]{2,1,0:T(8,128)S(1)}, f32[24,16,128]{2,1,0:T(8,128)S(1)}, u32[]{:S(2)}, u32[]{:S(2)}) collective-permute-start(f32[24,16,128]{2,1,0:T(8,128)S(1)} %get-tuple-element.130.refs_3_.refs_7_), channel_id=1, source_target_pairs={{0,4},{4,0},{8,12},{12,8},{16,20},{20,16},{24,28},{28,24},{1,5},{5... | collective-permute-start | bytes 589832 | tf_op jit(solution)/shard_map/ppermute | solution.py:335
  5.5 21.1 %collective-permute-start.9 = (f32[24,16,128]{2,1,0:T(8,128)S(1)}, f32[24,16,128]{2,1,0:T(8,128)S(1)}, u32[]{:S(2)}, u32[]{:S(2)}) collective-permute-start(f32[24,16,128]{2,1,0:T(8,128)S(1)} %get-tuple-element.131.refs_4_.refs_8_), channel_id=1, source_target_pairs={{0,28},{4,8},{8,4},{12,16},{16,12},{20,24},{24,20},{28,0},{1,29},{... | collective-permute-start | bytes 589832 | tf_op jit(solution)/shard_map/ppermute | solution.py:335
  9.1 25.0 %collective-permute-start = (f32[24,16,128]{2,1,0:T(8,128)S(1)}, f32[24,16,128]{2,1,0:T(8,128)S(1)}, u32[]{:S(2)}, u32[]{:S(2)}) collective-permute-start(f32[24,16,128]{2,1,0:T(8,128)S(1)} %get-tuple-element.122.refs_3_.refs_7_), channel_id=1, source_target_pairs={{0,4},{4,0},{8,12},{12,8},{16,20},{20,16},{24,28},{28,24},{1,5},{5... | collective-permute-start | bytes 589832 | tf_op jit(solution)/shard_map/ppermute | solution.py:335
  9.1 25.0 %collective-permute-start.1 = (f32[24,16,128]{2,1,0:T(8,128)S(1)}, f32[24,16,128]{2,1,0:T(8,128)S(1)}, u32[]{:S(2)}, u32[]{:S(2)}) collective-permute-start(f32[24,16,128]{2,1,0:T(8,128)S(1)} %get-tuple-element.123.refs_4_.refs_8_), channel_id=1, source_target_pairs={{0,28},{4,8},{8,4},{12,16},{16,12},{20,24},{24,20},{28,0},{1,29},{... | collective-permute-start | bytes 589832 | tf_op jit(solution)/shard_map/ppermute | solution.py:335
  31.2 10.7 %collective-permute-start.10 = (f32[24,16,128]{2,1,0:T(8,128)S(1)}, f32[24,16,128]{2,1,0:T(8,128)S(1)}, u32[]{:S(2)}, u32[]{:S(2)}) collective-permute-start(f32[24,16,128]{2,1,0:T(8,128)S(1)} %get-tuple-element.132.refs_3_.refs_7_), channel_id=1, source_target_pairs={{0,4},{4,0},{8,12},{12,8},{16,20},{20,16},{24,28},{28,24},{1,5},{5... | collective-permute-start | bytes 589832 | tf_op jit(solution)/shard_map/ppermute | solution.py:335
  38.6 16.2 %collective-permute-start.2 = (f32[24,16,128]{2,1,0:T(8,128)S(1)}, f32[24,16,128]{2,1,0:T(8,128)S(1)}, u32[]{:S(2)}, u32[]{:S(2)}) collective-permute-start(f32[24,16,128]{2,1,0:T(8,128)S(1)} %get-tuple-element.124.refs_3_.refs_7_), channel_id=1, source_target_pairs={{0,4},{4,0},{8,12},{12,8},{16,20},{20,16},{24,28},{28,24},{1,5},{5... | collective-permute-start | bytes 589832 | tf_op jit(solution)/shard_map/ppermute | solution.py:335
  39.5 15.3 %collective-permute-start.3 = (f32[24,16,128]{2,1,0:T(8,128)S(1)}, f32[24,16,128]{2,1,0:T(8,128)S(1)}, u32[]{:S(2)}, u32[]{:S(2)}) collective-permute-start(f32[24,16,128]{2,1,0:T(8,128)S(1)} %get-tuple-element.125.refs_4_.refs_8_), channel_id=1, source_target_pairs={{0,28},{4,8},{8,4},{12,16},{16,12},{20,24},{24,20},{28,0},{1,29},{... | collective-permute-start | bytes 589832 | tf_op jit(solution)/shard_map/ppermute | solution.py:335
  46.4 14.7 %collective-permute-start.12 = (f32[24,16,128]{2,1,0:T(8,128)S(1)}, f32[24,16,128]{2,1,0:T(8,128)S(1)}, u32[]{:S(2)}, u32[]{:S(2)}) collective-permute-start(f32[24,16,128]{2,1,0:T(8,128)S(1)} %get-tuple-element.134.refs_3_.refs_7_), channel_id=1, source_target_pairs={{0,4},{4,0},{8,12},{12,8},{16,20},{20,16},{24,28},{28,24},{1,5},{5... | collective-permute-start | bytes 589832 | tf_op jit(solution)/shard_map/ppermute | solution.py:335
  49.5 11.6 %collective-permute-start.13 = (f32[24,16,128]{2,1,0:T(8,128)S(1)}, f32[24,16,128]{2,1,0:T(8,128)S(1)}, u32[]{:S(2)}, u32[]{:S(2)}) collective-permute-start(f32[24,16,128]{2,1,0:T(8,128)S(1)} %get-tuple-element.135.refs_4_.refs_8_), channel_id=1, source_target_pairs={{0,28},{4,8},{8,4},{12,16},{16,12},{20,24},{24,20},{28,0},{1,29},{... | collective-permute-start | bytes 589832 | tf_op jit(solution)/shard_map/ppermute | solution.py:335
  59.4 11.9 %collective-permute-start.4 = (f32[24,16,128]{2,1,0:T(8,128)S(1)}, f32[24,16,128]{2,1,0:T(8,128)S(1)}, u32[]{:S(2)}, u32[]{:S(2)}) collective-permute-start(f32[24,16,128]{2,1,0:T(8,128)S(1)} %get-tuple-element.126.refs_3_.refs_7_), channel_id=1, source_target_pairs={{0,4},{4,0},{8,12},{12,8},{16,20},{20,16},{24,28},{28,24},{1,5},{5... | collective-permute-start | bytes 589832 | tf_op jit(solution)/shard_map/ppermute | solution.py:335
  59.7 11.6 %collective-permute-start.5 = (f32[24,16,128]{2,1,0:T(8,128)S(1)}, f32[24,16,128]{2,1,0:T(8,128)S(1)}, u32[]{:S(2)}, u32[]{:S(2)}) collective-permute-start(f32[24,16,128]{2,1,0:T(8,128)S(1)} %get-tuple-element.127.refs_4_.refs_8_), channel_id=1, source_target_pairs={{0,28},{4,8},{8,4},{12,16},{16,12},{20,24},{24,20},{28,0},{1,29},{... | collective-permute-start | bytes 589832 | tf_op jit(solution)/shard_map/ppermute | solution.py:335
  65.7 14.0 %collective-permute-start.14 = (f32[24,16,128]{2,1,0:T(8,128)S(1)}, f32[24,16,128]{2,1,0:T(8,128)S(1)}, u32[]{:S(2)}, u32[]{:S(2)}) collective-permute-start(f32[24,16,128]{2,1,0:T(8,128)S(1)} %get-tuple-element.136.refs_3_), channel_id=1, source_target_pairs={{0,4},{4,0},{8,12},{12,8},{16,20},{20,16},{24,28},{28,24},{1,5},{5... | collective-permute-start | bytes 589832 | tf_op jit(solution)/shard_map/ppermute | solution.py:335
  66.1 13.6 %collective-permute-start.15 = (f32[24,16,128]{2,1,0:T(8,128)S(1)}, f32[24,16,128]{2,1,0:T(8,128)S(1)}, u32[]{:S(2)}, u32[]{:S(2)}) collective-permute-start(f32[24,16,128]{2,1,0:T(8,128)S(1)} %get-tuple-element.137.refs_4_), channel_id=1, source_target_pairs={{0,28},{4,8},{8,4},{12,16},{16,12},{20,24},{24,20},{28,0},{1,29},{... | collective-permute-start | bytes 589832 | tf_op jit(solution)/shard_map/ppermute | solution.py:335
  75.8 11.0 %collective-permute-start.6 = (f32[24,16,128]{2,1,0:T(8,128)S(1)}, f32[24,16,128]{2,1,0:T(8,128)S(1)}, u32[]{:S(2)}, u32[]{:S(2)}) collective-permute-start(f32[24,16,128]{2,1,0:T(8,128)S(1)} %get-tuple-element.128.refs_3_), channel_id=1, source_target_pairs={{0,4},{4,0},{8,12},{12,8},{16,20},{20,16},{24,28},{28,24},{1,5},{5... | collective-permute-start | bytes 589832 | tf_op jit(solution)/shard_map/ppermute | solution.py:335
  75.9 10.9 %collective-permute-start.7 = (f32[24,16,128]{2,1,0:T(8,128)S(1)}, f32[24,16,128]{2,1,0:T(8,128)S(1)}, u32[]{:S(2)}, u32[]{:S(2)}) collective-permute-start(f32[24,16,128]{2,1,0:T(8,128)S(1)} %get-tuple-element.129.refs_4_), channel_id=1, source_target_pairs={{0,28},{4,8},{8,4},{12,16},{16,12},{20,24},{24,20},{28,0},{1,29},{... | collective-permute-start | bytes 589832 | tf_op jit(solution)/shard_map/ppermute | solution.py:335
  84.3 13.1 %collective-permute-start.18 = (f32[24,16,128]{2,1,0:T(8,128)S(1)}, f32[24,16,128]{2,1,0:T(8,128)S(1)}, u32[]{:S(2)}, u32[]{:S(2)}) collective-permute-start(f32[24,16,128]{2,1,0:T(8,128)S(1)} %get-tuple-element.152.refs_9_.refs_3_.refs_7_), channel_id=1, source_target_pairs={{0,4},{4,0},{8,12},{12,8},{16,20},{20,16},{24,28},{28,24},{1,5},{5... | collective-permute-start | bytes 589832 | tf_op jit(solution)/shard_map/ppermute | solution.py:335
  84.3 14.5 %collective-permute-start.19 = (f32[24,16,128]{2,1,0:T(8,128)S(1)}, f32[24,16,128]{2,1,0:T(8,128)S(1)}, u32[]{:S(2)}, u32[]{:S(2)}) collective-permute-start(f32[24,16,128]{2,1,0:T(8,128)S(1)} %get-tuple-element.153.refs_10_.refs_4_.refs_8_), channel_id=1, source_target_pairs={{0,28},{4,8},{8,4},{12,16},{16,12},{20,24},{24,20},{28,0},{1,29},{... | collective-permute-start | bytes 589832 | tf_op jit(solution)/shard_map/ppermute | solution.py:335
  91.5 11.9 %collective-permute-start.16 = (f32[24,16,128]{2,1,0:T(8,128)S(1)}, f32[24,16,128]{2,1,0:T(8,128)S(1)}, u32[]{:S(2)}, u32[]{:S(2)}) collective-permute-start(f32[24,16,128]{2,1,0:T(8,128)S(1)} %get-tuple-element.158.refs_3_.refs_7_), channel_id=1, source_target_pairs={{0,4},{4,0},{8,12},{12,8},{16,20},{20,16},{24,28},{28,24},{1,5},{5... | collective-permute-start | bytes 589832 | tf_op jit(solution)/shard_map/ppermute | solution.py:335
  91.5 14.2 %collective-permute-start.17 = (f32[24,16,128]{2,1,0:T(8,128)S(1)}, f32[24,16,128]{2,1,0:T(8,128)S(1)}, u32[]{:S(2)}, u32[]{:S(2)}) collective-permute-start(f32[24,16,128]{2,1,0:T(8,128)S(1)} %get-tuple-element.159.refs_4_.refs_8_), channel_id=1, source_target_pairs={{0,28},{4,8},{8,4},{12,16},{16,12},{20,24},{24,20},{28,0},{1,29},{... | collective-permute-start | bytes 589832 | tf_op jit(solution)/shard_map/ppermute | solution.py:335
  96.5 14.1 %collective-permute-start.22 = (f32[12,32,128]{2,1,0:T(8,128)S(1)}, f32[12,32,128]{2,1,0:T(8,128)S(1)}, u32[]{:S(2)}, u32[]{:S(2)}) collective-permute-start(f32[12,32,128]{2,1,0:T(8,128)S(1)} %get-tuple-element.147), channel_id=1, source_target_pairs={{0,1},{1,0},{2,3},{3,2},{4,5},{5,4},{6,7},{7,6},{8,9},{9,8},{10,11... | collective-permute-start | bytes 589832 | tf_op jit(solution)/shard_map/ppermute | solution.py:339
  97.3 14.4 %collective-permute-start.23 = (f32[12,32,128]{2,1,0:T(8,128)S(1)}, f32[12,32,128]{2,1,0:T(8,128)S(1)}, u32[]{:S(2)}, u32[]{:S(2)}) collective-permute-start(f32[12,32,128]{2,1,0:T(8,128)S(1)} %get-tuple-element.148), channel_id=1, source_target_pairs={{0,2},{1,3},{2,0},{3,1},{4,6},{5,7},{6,4},{7,5},{8,10},{9,11},{10,... | collective-permute-start | bytes 589832 | tf_op jit(solution)/shard_map/ppermute | solution.py:339
  98.8 16.5 %collective-permute-start.24 = (f32[12,32,128]{2,1,0:T(8,128)S(1)}, f32[12,32,128]{2,1,0:T(8,128)S(1)}, u32[]{:S(2)}, u32[]{:S(2)}) collective-permute-start(f32[12,32,128]{2,1,0:T(8,128)S(1)} %get-tuple-element.149), channel_id=1, source_target_pairs={{0,3},{1,2},{2,1},{3,0},{4,7},{5,6},{6,5},{7,4},{8,11},{9,10},{10,... | collective-permute-start | bytes 589832 | tf_op jit(solution)/shard_map/ppermute | solution.py:339
  103.4 16.0 %collective-permute-start.26 = (f32[24,16,128]{2,1,0:T(8,128)S(1)}, f32[24,16,128]{2,1,0:T(8,128)S(1)}, u32[]{:S(2)}, u32[]{:S(2)}) collective-permute-start(f32[24,16,128]{2,1,0:T(8,128)S(1)} %get-tuple-element.168.refs_7_.refs_3_), channel_id=1, source_target_pairs={{0,4},{4,0},{8,12},{12,8},{16,20},{20,16},{24,28},{28,24},{1,5},{5... | collective-permute-start | bytes 589832 | tf_op jit(solution)/shard_map/ppermute | solution.py:335
  105.7 13.7 %collective-permute-start.27 = (f32[24,16,128]{2,1,0:T(8,128)S(1)}, f32[24,16,128]{2,1,0:T(8,128)S(1)}, u32[]{:S(2)}, u32[]{:S(2)}) collective-permute-start(f32[24,16,128]{2,1,0:T(8,128)S(1)} %get-tuple-element.169.refs_8_.refs_4_), channel_id=1, source_target_pairs={{0,28},{4,8},{8,4},{12,16},{16,12},{20,24},{24,20},{28,0},{1,29},{... | collective-permute-start | bytes 589832 | tf_op jit(solution)/shard_map/ppermute | solution.py:335
  110.6 15.9 %collective-permute-start.20 = (f32[24,16,128]{2,1,0:T(8,128)S(1)}, f32[24,16,128]{2,1,0:T(8,128)S(1)}, u32[]{:S(2)}, u32[]{:S(2)}) collective-permute-start(f32[24,16,128]{2,1,0:T(8,128)S(1)} %get-tuple-element.176.refs_3_.refs_7_), channel_id=1, source_target_pairs={{0,4},{4,0},{8,12},{12,8},{16,20},{20,16},{24,28},{28,24},{1,5},{5... | collective-permute-start | bytes 589832 | tf_op jit(solution)/shard_map/ppermute | solution.py:335
  111.7 14.8 %collective-permute-start.21 = (f32[24,16,128]{2,1,0:T(8,128)S(1)}, f32[24,16,128]{2,1,0:T(8,128)S(1)}, u32[]{:S(2)}, u32[]{:S(2)}) collective-permute-start(f32[24,16,128]{2,1,0:T(8,128)S(1)} %get-tuple-element.177.refs_4_.refs_8_), channel_id=1, source_target_pairs={{0,28},{4,8},{8,4},{12,16},{16,12},{20,24},{24,20},{28,0},{1,29},{... | collective-permute-start | bytes 589832 | tf_op jit(solution)/shard_map/ppermute | solution.py:335
  124.0 16.7 %collective-permute-start.30 = (f32[24,16,128]{2,1,0:T(8,128)S(1)}, f32[24,16,128]{2,1,0:T(8,128)S(1)}, u32[]{:S(2)}, u32[]{:S(2)}) collective-permute-start(f32[24,16,128]{2,1,0:T(8,128)S(1)} %get-tuple-element.184.refs_3_.refs_7_), channel_id=1, source_target_pairs={{0,4},{4,0},{8,12},{12,8},{16,20},{20,16},{24,28},{28,24},{1,5},{5... | collective-permute-start | bytes 589832 | tf_op jit(solution)/shard_map/ppermute | solution.py:335
  126.5 14.2 %collective-permute-start.31 = (f32[24,16,128]{2,1,0:T(8,128)S(1)}, f32[24,16,128]{2,1,0:T(8,128)S(1)}, u32[]{:S(2)}, u32[]{:S(2)}) collective-permute-start(f32[24,16,128]{2,1,0:T(8,128)S(1)} %get-tuple-element.185.refs_4_.refs_8_), channel_id=1, source_target_pairs={{0,28},{4,8},{8,4},{12,16},{16,12},{20,24},{24,20},{28,0},{1,29},{... | collective-permute-start | bytes 589832 | tf_op jit(solution)/shard_map/ppermute | solution.py:335
  131.3 17.1 %collective-permute-start.33 = (f32[24,16,128]{2,1,0:T(8,128)S(1)}, f32[24,16,128]{2,1,0:T(8,128)S(1)}, u32[]{:S(2)}, u32[]{:S(2)}) collective-permute-start(f32[24,16,128]{2,1,0:T(8,128)S(1)} %get-tuple-element.197.refs_3_.refs_7_), channel_id=1, source_target_pairs={{0,4},{4,0},{8,12},{12,8},{16,20},{20,16},{24,28},{28,24},{1,5},{5... | collective-permute-start | bytes 589832 | tf_op jit(solution)/shard_map/ppermute | solution.py:335
  132.6 15.8 %collective-permute-start.34 = (f32[24,16,128]{2,1,0:T(8,128)S(1)}, f32[24,16,128]{2,1,0:T(8,128)S(1)}, u32[]{:S(2)}, u32[]{:S(2)}) collective-permute-start(f32[24,16,128]{2,1,0:T(8,128)S(1)} %get-tuple-element.198.refs_4_.refs_8_), channel_id=1, source_target_pairs={{0,28},{4,8},{8,4},{12,16},{16,12},{20,24},{24,20},{28,0},{1,29},{... | collective-permute-start | bytes 589832 | tf_op jit(solution)/shard_map/ppermute | solution.py:335
  145.2 17.1 %collective-permute-start.36 = (f32[24,16,128]{2,1,0:T(8,128)S(1)}, f32[24,16,128]{2,1,0:T(8,128)S(1)}, u32[]{:S(2)}, u32[]{:S(2)}) collective-permute-start(f32[24,16,128]{2,1,0:T(8,128)S(1)} %get-tuple-element.170.refs_3_), channel_id=1, source_target_pairs={{0,4},{4,0},{8,12},{12,8},{16,20},{20,16},{24,28},{28,24},{1,5},{5... | collective-permute-start | bytes 589832 | tf_op jit(solution)/shard_map/ppermute | solution.py:335
  147.3 15.1 %collective-permute-start.37 = (f32[24,16,128]{2,1,0:T(8,128)S(1)}, f32[24,16,128]{2,1,0:T(8,128)S(1)}, u32[]{:S(2)}, u32[]{:S(2)}) collective-permute-start(f32[24,16,128]{2,1,0:T(8,128)S(1)} %get-tuple-element.171.refs_4_), channel_id=1, source_target_pairs={{0,28},{4,8},{8,4},{12,16},{16,12},{20,24},{24,20},{28,0},{1,29},{... | collective-permute-start | bytes 589832 | tf_op jit(solution)/shard_map/ppermute | solution.py:335
  152.9 19.5 %collective-permute-start.41 = (f32[24,16,128]{2,1,0:T(8,128)S(1)}, f32[24,16,128]{2,1,0:T(8,128)S(1)}, u32[]{:S(2)}, u32[]{:S(2)}) collective-permute-start(f32[24,16,128]{2,1,0:T(8,128)S(1)} %get-tuple-element.178.refs_3_), channel_id=1, source_target_pairs={{0,4},{4,0},{8,12},{12,8},{16,20},{20,16},{24,28},{28,24},{1,5},{5... | collective-permute-start | bytes 589832 | tf_op jit(solution)/shard_map/ppermute | solution.py:335
  153.0 19.4 %collective-permute-start.42 = (f32[24,16,128]{2,1,0:T(8,128)S(1)}, f32[24,16,128]{2,1,0:T(8,128)S(1)}, u32[]{:S(2)}, u32[]{:S(2)}) collective-permute-start(f32[24,16,128]{2,1,0:T(8,128)S(1)} %get-tuple-element.179.refs_4_), channel_id=1, source_target_pairs={{0,28},{4,8},{8,4},{12,16},{16,12},{20,24},{24,20},{28,0},{1,29},{... | collective-permute-start | bytes 589832 | tf_op jit(solution)/shard_map/ppermute | solution.py:335
  161.6 10.8 %collective-permute-start.35 = (f32[128,128]{1,0:T(8,128)S(1)}, f32[128,128]{1,0:T(8,128)S(1)}, u32[]{:S(2)}, u32[]{:S(2)}) collective-permute-start(f32[128,128]{1,0:T(8,128)S(1)} %add.51), channel_id=1, source_target_pairs={{0,16},{4,20},{8,24},{12,28},{16,0},{20,4},{24,8},{28,12},{1,17},{... | collective-permute-start | bytes 196616 | tf_op jit(solution)/shard_map/ppermute | solution.py:339
  166.9 20.6 %collective-permute-start.46 = (f32[24,16,128]{2,1,0:T(8,128)S(1)}, f32[24,16,128]{2,1,0:T(8,128)S(1)}, u32[]{:S(2)}, u32[]{:S(2)}) collective-permute-start(f32[24,16,128]{2,1,0:T(8,128)S(1)} %get-tuple-element.186.refs_9_.refs_3_), channel_id=1, source_target_pairs={{0,4},{4,0},{8,12},{12,8},{16,20},{20,16},{24,28},{28,24},{1,5},{5... | collective-permute-start | bytes 589832 | tf_op jit(solution)/shard_map/ppermute | solution.py:335
  168.7 18.8 %collective-permute-start.47 = (f32[24,16,128]{2,1,0:T(8,128)S(1)}, f32[24,16,128]{2,1,0:T(8,128)S(1)}, u32[]{:S(2)}, u32[]{:S(2)}) collective-permute-start(f32[24,16,128]{2,1,0:T(8,128)S(1)} %get-tuple-element.187.refs_10_.refs_4_), channel_id=1, source_target_pairs={{0,28},{4,8},{8,4},{12,16},{16,12},{20,24},{24,20},{28,0},{1,29},{... | collective-permute-start | bytes 589832 | tf_op jit(solution)/shard_map/ppermute | solution.py:335
  177.1 10.4 %collective-permute-start.43 = (f32[12,32,128]{2,1,0:T(8,128)S(1)}, f32[12,32,128]{2,1,0:T(8,128)S(1)}, u32[]{:S(2)}, u32[]{:S(2)}) collective-permute-start(f32[12,32,128]{2,1,0:T(8,128)S(1)} %get-tuple-element.200), channel_id=1, source_target_pairs={{0,1},{1,0},{2,3},{3,2},{4,5},{5,4},{6,7},{7,6},{8,9},{9,8},{10,11... | collective-permute-start | bytes 589832 | tf_op jit(solution)/shard_map/ppermute | solution.py:339
  177.1 10.4 %collective-permute-start.44 = (f32[12,32,128]{2,1,0:T(8,128)S(1)}, f32[12,32,128]{2,1,0:T(8,128)S(1)}, u32[]{:S(2)}, u32[]{:S(2)}) collective-permute-start(f32[12,32,128]{2,1,0:T(8,128)S(1)} %get-tuple-element.201), channel_id=1, source_target_pairs={{0,2},{1,3},{2,0},{3,1},{4,6},{5,7},{6,4},{7,5},{8,10},{9,11},{10,... | collective-permute-start | bytes 589832 | tf_op jit(solution)/shard_map/ppermute | solution.py:339
  192.6 11.9 %collective-permute-start.51 = (f32[24,16,128]{2,1,0:T(8,128)S(1)}, f32[24,16,128]{2,1,0:T(8,128)S(1)}, u32[]{:S(2)}, u32[]{:S(2)}) collective-permute-start(f32[24,16,128]{2,1,0:T(8,128)S(1)} %get-tuple-element.208.refs_3_), channel_id=1, source_target_pairs={{0,4},{4,0},{8,12},{12,8},{16,20},{20,16},{24,28},{28,24},{1,5},{5... | collective-permute-start | bytes 589832 | tf_op jit(solution)/shard_map/ppermute | solution.py:335
  192.7 11.8 %collective-permute-start.52 = (f32[24,16,128]{2,1,0:T(8,128)S(1)}, f32[24,16,128]{2,1,0:T(8,128)S(1)}, u32[]{:S(2)}, u32[]{:S(2)}) collective-permute-start(f32[24,16,128]{2,1,0:T(8,128)S(1)} %get-tuple-element.209.refs_4_), channel_id=1, source_target_pairs={{0,28},{4,8},{8,4},{12,16},{16,12},{20,24},{24,20},{28,0},{1,29},{... | collective-permute-start | bytes 589832 | tf_op jit(solution)/shard_map/ppermute | solution.py:335
  195.4 21.7 %collective-permute-start.38 = (f32[12,32,128]{2,1,0:T(8,128)S(1)}, f32[12,32,128]{2,1,0:T(8,128)S(1)}, u32[]{:S(2)}, u32[]{:S(2)}) collective-permute-start(f32[12,32,128]{2,1,0:T(8,128)S(1)} %get-tuple-element.194), channel_id=1, source_target_pairs={{0,1},{1,0},{2,3},{3,2},{4,5},{5,4},{6,7},{7,6},{8,9},{9,8},{10,11... | collective-permute-start | bytes 589832 | tf_op jit(solution)/shard_map/ppermute | solution.py:339
  199.1 19.5 %collective-permute-start.39 = (f32[12,32,128]{2,1,0:T(8,128)S(1)}, f32[12,32,128]{2,1,0:T(8,128)S(1)}, u32[]{:S(2)}, u32[]{:S(2)}) collective-permute-start(f32[12,32,128]{2,1,0:T(8,128)S(1)} %get-tuple-element.195), channel_id=1, source_target_pairs={{0,2},{1,3},{2,0},{3,1},{4,6},{5,7},{6,4},{7,5},{8,10},{9,11},{10,... | collective-permute-start | bytes 589832 | tf_op jit(solution)/shard_map/ppermute | solution.py:339
  205.3 12.4 %collective-permute-start.53 = (f32[128,128]{1,0:T(8,128)S(1)}, f32[128,128]{1,0:T(8,128)S(1)}, u32[]{:S(2)}, u32[]{:S(2)}) collective-permute-start(f32[128,128]{1,0:T(8,128)S(1)} %add.55), channel_id=1, source_target_pairs={{0,8},{4,12},{8,0},{12,4},{16,24},{20,28},{24,16},{28,20},{1,9},{5... | collective-permute-start | bytes 196616 | tf_op jit(solution)/shard_map/ppermute | solution.py:339
  205.3 13.6 %collective-permute-start.40 = (f32[12,32,128]{2,1,0:T(8,128)S(1)}, f32[12,32,128]{2,1,0:T(8,128)S(1)}, u32[]{:S(2)}, u32[]{:S(2)}) collective-permute-start(f32[12,32,128]{2,1,0:T(8,128)S(1)} %get-tuple-element.196), channel_id=1, source_target_pairs={{0,3},{1,2},{2,1},{3,0},{4,7},{5,6},{6,5},{7,4},{8,11},{9,10},{10,... | collective-permute-start | bytes 589832 | tf_op jit(solution)/shard_map/ppermute | solution.py:339
  216.0 16.7 %collective-permute-start.55 = (f32[12,32,128]{2,1,0:T(8,128)S(1)}, f32[12,32,128]{2,1,0:T(8,128)S(1)}, u32[]{:S(2)}, u32[]{:S(2)}) collective-permute-start(f32[12,32,128]{2,1,0:T(8,128)S(1)} %get-tuple-element.219), channel_id=1, source_target_pairs={{0,1},{1,0},{2,3},{3,2},{4,5},{5,4},{6,7},{7,6},{8,9},{9,8},{10,11... | collective-permute-start | bytes 589832 | tf_op jit(solution)/shard_map/ppermute | solution.py:339
  217.1 15.6 %collective-permute-start.56 = (f32[12,32,128]{2,1,0:T(8,128)S(1)}, f32[12,32,128]{2,1,0:T(8,128)S(1)}, u32[]{:S(2)}, u32[]{:S(2)}) collective-permute-start(f32[12,32,128]{2,1,0:T(8,128)S(1)} %get-tuple-element.220), channel_id=1, source_target_pairs={{0,2},{1,3},{2,0},{3,1},{4,6},{5,7},{6,4},{7,5},{8,10},{9,11},{10,... | collective-permute-start | bytes 589832 | tf_op jit(solution)/shard_map/ppermute | solution.py:339
  217.6 15.1 %collective-permute-start.57 = (f32[12,32,128]{2,1,0:T(8,128)S(1)}, f32[12,32,128]{2,1,0:T(8,128)S(1)}, u32[]{:S(2)}, u32[]{:S(2)}) collective-permute-start(f32[12,32,128]{2,1,0:T(8,128)S(1)} %get-tuple-element.221), channel_id=1, source_target_pairs={{0,3},{1,2},{2,1},{3,0},{4,7},{5,6},{6,5},{7,4},{8,11},{9,10},{10,... | collective-permute-start | bytes 589832 | tf_op jit(solution)/shard_map/ppermute | solution.py:339
  (22 other events, 117.4 us)

commit v5 on v4

--- a/solution.py
+++ b/solution.py
@@ -9,8 +9,10 @@
 
 DEGREE = 4
 UNROLL = 48
-CHUNK = 6
-STREAMS = 4
+CHUNK = 24
+TURNS = 3
+TIE_HALO = 1
+TIE_IMAGE = 1
 APPLY_BYTES = 4 << 20
 F32, BF16, I32 = jnp.float32, jnp.bfloat16, jnp.int32
 precise = lax.Precision.HIGHEST
@@ -50,27 +52,31 @@
     )(*args)
 
 
-def prep_kernel(rows, ids_ref, own_ref, col_ref, *refs):
-    blks, (w_ref, inv_ref, table_ref, eye_ref) = refs[:-4], refs[-4:]
-    chunk, n, _ = blks[0].shape
+def prep_kernel(rows, ids_ref, own_ref, col_ref, blk_ref, w_ref, inv_ref, table_ref, held_ref, eye_ref, sem_ref):
+    count, n, _ = held_ref.shape
+    steps = sem_ref.shape[0]
+    chunk = count // steps
     half = rows // 2
-    step = pl.program_id(0)
     me = ids_ref[0]
     odd = me % 2
-    count = own_ref.shape[1]
-
-    @pl.when(step == 0)
-    def _():
-        table_ref[0] = me
-        table_ref[1] = ids_ref[1]
-        inv_ref[...] = jnp.zeros(inv_ref.shape, F32)
-        lines = lax.broadcasted_iota(I32, eye_ref.shape, 0)
-        lanes = lax.broadcasted_iota(I32, eye_ref.shape, 1)
-        eye_ref[...] = jnp.where((lines == lanes) | (lines >= n), 1.0, 0.0).astype(BF16)
-
-    for i, blk_ref in enumerate(blks):
+
+    def fetch(step):
+        span = pl.ds(step * chunk, chunk)
+        return pltpu.make_async_copy(blk_ref.at[span], held_ref.at[span], sem_ref.at[step])
+
+    for step in range(steps):
+        fetch(step).start()
+    table_ref[0] = me
+    table_ref[1] = ids_ref[1]
+    inv_ref[...] = jnp.zeros(inv_ref.shape, F32)
+    lines = lax.broadcasted_iota(I32, eye_ref.shape, 0)
+    lanes = lax.broadcasted_iota(I32, eye_ref.shape, 1)
+    eye_ref[...] = jnp.where((lines == lanes) | (lines >= n), 1.0, 0.0).astype(BF16)
+
+    def pack(step, carry):
+        fetch(step).wait()
         for c in range(chunk):
-            b = (step * len(blks) + i) * chunk + c
+            b = step * chunk + c
             r = own_ref[0, b]
             k = col_ref[0, b]
             owner = k // rows
@@ -83,44 +89,49 @@
             r_at = r + half * (1 - odd) * (1 - 2 * top)
             table_ref[2 + b] = slot
             table_ref[2 + count + b] = r_at
-            a = blk_ref[c]
-            high = a.astype(BF16)
-            low = (a - high.astype(F32)).astype(BF16)
-            both = jnp.concatenate([high, low], axis=0)
-            t = lax.dot_general(
-                eye_ref[...], both, (((1,), (1,)), ((), ())), preferred_element_type=F32
-            )
-            w_ref[b] = t[:n].astype(BF16)
-            inv_ref[r_at] = inv_ref[r_at] + (t[n:n + 1, :n] + t[n:n + 1, n:])
-
-    @pl.when(step == pl.num_programs(0) - 1)
-    def _():
-        inv_ref[...] = 1.0 / inv_ref[...]
+            a = held_ref[b]
+            if c % TURNS:
+                t = a.T
+                high = t.astype(BF16)
+                w_ref[b, :, :n] = high
+                w_ref[b, :, n:] = (t - high.astype(F32)).astype(BF16)
+                inv_ref[r_at] = inv_ref[r_at] + jnp.sum(t, axis=0, keepdims=True)
+            else:
+                high = a.astype(BF16)
+                low = (a - high.astype(F32)).astype(BF16)
+                both = jnp.concatenate([high, low], axis=0)
+                t = lax.dot_general(
+                    eye_ref[...], both, (((1,), (1,)), ((), ())), preferred_element_type=F32
+                )
+                w_ref[b] = t[:n].astype(BF16)
+                inv_ref[r_at] = inv_ref[r_at] + (t[n:n + 1, :n] + t[n:n + 1, n:])
+        return carry
+
+    lax.fori_loop(0, steps, pack, 0)
+    inv_ref[...] = 1.0 / inv_ref[...]
 
 
 def prep(ids, own, col, blocks, rows):
     count, n, _ = blocks.shape
-    chunk = math.gcd(count, STREAMS * CHUNK) // STREAMS
-    blocks = pltpu.with_memory_space_constraint(blocks, pltpu.HBM)
-
-    def stream(i):
-        return pl.BlockSpec((chunk, n, n), lambda step: (STREAMS * step + i, 0, 0))
-
+    own, col, blocks = (pltpu.with_memory_space_constraint(x, pltpu.HBM) for x in (own, col, blocks))
     return pl.pallas_call(
         functools.partial(prep_kernel, rows),
-        grid=(count // (STREAMS * chunk),),
-        in_specs=[IN_SMEM] * 3 + [stream(i) for i in range(STREAMS)],
+        in_specs=[IN_SMEM] * 3 + [pl.BlockSpec(memory_space=pl.ANY)],
         out_specs=[IN_VMEM, IN_VMEM, IN_SMEM],
         out_shape=[pltpu.VMEM((count, n, 2 * n), BF16),
                    jax.ShapeDtypeStruct((rows, 1, n), F32),
                    jax.ShapeDtypeStruct((2 + 2 * count,), I32)],
-        scratch_shapes=[pltpu.VMEM((n + 16, n), BF16)],
-        compiler_params=pltpu.CompilerParams(vmem_limit_bytes=12 * MIB),
+        scratch_shapes=[
+            pltpu.VMEM(blocks.shape, F32),
+            pltpu.VMEM((n + 16, n), BF16),
+            pltpu.SemaphoreType.DMA((count // math.gcd(count, CHUNK),)),
+        ],
+        compiler_params=pltpu.CompilerParams(vmem_limit_bytes=24 * MIB),
         cost_estimate=pl.CostEstimate(
             flops=2 * count * n * n * n, bytes_accessed=4 * blocks.size, transcendentals=0
         ),
         name="prep",
-    )(ids, own, col, *[blocks] * STREAMS)
+    )(ids, own, col, blocks)
 
 
 def apply_kernel(recur, mate, *refs):
@@ -197,42 +208,35 @@
     return tuple(res[:2]), tuple(res[2:])
 
 
-def factor_kernel(nodes, g_ref, out_ref, both_ref):
+def factor_kernel(nodes, g_ref, out_ref):
     n = g_ref.shape[0]
     p = 8
-    lines = lax.broadcasted_iota(I32, (n, n), 0)
-    lanes = lax.broadcasted_iota(I32, (n, n), 1)
-    both_ref[:, :n] = g_ref[...] * (1.0 / nodes)
-    both_ref[:, n:] = jnp.where(lines == lanes, 1.0, 0.0).astype(F32)
+    out_ref[...] = g_ref[...] * (1.0 / nodes)
     sub = lax.broadcasted_iota(I32, (p, n), 0)
+    lane = lax.broadcasted_iota(I32, (p, n), 1)
     for j in range(0, n, p):
-        left = both_ref[j:j + p, :n]
-        right = both_ref[j:j + p, n:]
-        cols = [jnp.broadcast_to(left[:, j + i:j + i + 1], (p, n)) for i in range(p)]
-        pivot = jnp.zeros((p, n), F32)
+        rows = out_ref[j:j + p]
+        cols = [jnp.broadcast_to(rows[:, j + i:j + i + 1], (p, n)) for i in range(p)]
+        rows = jnp.where((lane >= j) & (lane < j + p), jnp.where(lane - j == sub, 1.0, 0.0), rows)
         for i in range(p):
-            own = jnp.broadcast_to(cols[i][i:i + 1], (p, n))
-            pivot = jnp.where(sub == i, own, pivot)
-            if i + 1 < p:
-                ratio = jnp.where(sub > i, cols[i] / own, 0.0)
-                for k in range(i + 1, p):
-                    cols[k] = cols[k] - ratio * jnp.broadcast_to(cols[k][i:i + 1], (p, n))
-                left = left - ratio * jnp.broadcast_to(left[i:i + 1], (p, n))
-                right = right - ratio * jnp.broadcast_to(right[i:i + 1], (p, n))
-        root = lax.rsqrt(pivot)
-        left = left * root
-        right = right * root
-        out_ref[j:j + p] = right
+            root = lax.rsqrt(jnp.broadcast_to(cols[i][i:i + 1], (p, n)))
+            ratio = jnp.where(sub > i, cols[i] * root, 0.0)
+            scale = jnp.where(sub == i, root, 1.0)
+            for k in range(i + 1, p):
+                cols[k] = cols[k] - ratio * (jnp.broadcast_to(cols[k][i:i + 1], (p, n)) * root)
+            rows = rows * scale - ratio * (jnp.broadcast_to(rows[i:i + 1], (p, n)) * root)
+        out_ref[j:j + p] = jnp.where(lane < j + p, rows, 0.0)
         if j + p < n:
-            change = tn(left, jnp.concatenate([left, right], axis=1))
-            both_ref[j + p:] = both_ref[j + p:] - change[j + p:]
+            change = nn(rows.T[j + p:], rows)
+            lanes = lax.broadcasted_iota(I32, change.shape, 1)
+            rest = out_ref[j + p:]
+            out_ref[j + p:] = jnp.where((lanes >= j) & (lanes < j + p), 0.0, rest) - change
 
 
 def inverse_factor(gram, nodes):
     n = gram.shape[0]
     return call(
         functools.partial(factor_kernel, nodes), "factor", [(n, n)], gram,
-        scratch=[pltpu.VMEM((n, 2 * n), F32)],
     )[0]
 
 
@@ -253,12 +257,12 @@
     g_ref[...] = total
 
 
-def cross_kernel(ids_ref, f_ref, *refs):
+def cross_kernel(ids_ref, f_ref, g_ref, *refs):
     parts, (k_ref, x_ref) = refs[:-2], refs[-2:]
     total = jnp.zeros(k_ref.shape, F32)
     for b in range(f_ref.shape[0]):
         total = total + nt(f_ref[b], gathered(ids_ref, parts, b, x_ref))
-    k_ref[...] = total
+    k_ref[...] = half_width * total + center * g_ref[...]
 
 
 def turn_kernel(ids_ref, inv_ref, *refs):
@@ -271,13 +275,14 @@
     g_ref[...] = total
 
 
-def turn_cross_kernel(ids_ref, inv_ref, f_ref, *refs):
+def turn_cross_kernel(ids_ref, inv_ref, f_ref, g_ref, first_ref, *refs):
     parts, (k_ref, x_ref) = refs[:-2], refs[-2:]
-    total = jnp.zeros(k_ref.shape, F32)
+    total = jnp.zeros(g_ref.shape, F32)
     for b in range(f_ref.shape[0]):
         z = nn(inv_ref[...], gathered(ids_ref, parts, b, x_ref))
         total = total + nt(f_ref[b], z)
-    k_ref[...] = total
+    k_ref[0] = first_ref[...]
+    k_ref[1] = half_width * total + center * g_ref[...]
 
 
 def basis_kernel(ids_ref, inv_ref, f_ref, *refs):
@@ -290,15 +295,12 @@
             part[b] = x_ref[b, pl.ds(pl.multiple_of((me ^ s) * each, each), each)]
 
 
-def proj_kernel(nodes, ids_ref, *refs):
-    pairs = len(refs[:6]) // 3
-    parts, x_ref = refs[6:-1], refs[-1]
+def proj_kernel(nodes, ids_ref, first_ref, last_ref, image_ref, *refs):
+    parts, x_ref = refs[:-1], refs[-1]
     each = parts[0].shape[1]
     me = ids_ref[1]
-    for i in range(pairs):
-        inv_ref, k_ref, g_ref = refs[3 * i:3 * i + 3]
-        image = (half_width * k_ref[...] + center * g_ref[...]) * (1.0 / nodes)
-        x_ref[...] = nt(nn(inv_ref[...], image), inv_ref[...])
+    for i, inv_ref in enumerate((first_ref, last_ref)):
+        x_ref[...] = nt(nn(inv_ref[...], image_ref[i] * (1.0 / nodes)), inv_ref[...])
         for s, part in enumerate(parts):
             part[i] = x_ref[pl.ds(pl.multiple_of((me ^ s) * each, each), each)]
 
@@ -380,15 +382,15 @@
     panel, gram_first = call(gram_kernel, "gram", [wide, square], ids, *swapped(parts), scalars=1)
     after, parts = advance(now, parts=True)
     before, now = now, after
-    (cross_first,) = call(
-        cross_kernel, "cross", [square], ids, panel, *swapped(parts), scalars=1, scratch=[held]
-    )
+    image = swapped(parts)
     got, hops = None, hops_of("col", "node")
     gram = gram_first
     for step in range(DEGREE - 1):
         after = []
         for i in range(2):
             old, gram, got = lax.optimization_barrier((before[i], gram, got))
+            if (step, i) == (1, 1):
+                old, image = lax.optimization_barrier((old, image))
             if got is not None:
                 gram = gram + got
             got = swap(gram, *hops.pop(0)) if hops else None
@@ -402,44 +404,46 @@
         gram = gram + got
     for hop in hops:
         gram = gram + swap(gram, *hop)
+    halos = [exchange(panels) for panels in now]
+    halos[0], gram = lax.optimization_barrier((halos[0], gram))
     inverse_first = inverse_factor(gram, nodes)
-
-    arrived, halo = lax.optimization_barrier((swapped(parts), exchange(now[0])))
-    halos = [halo, exchange(now[1])]
+    (cross_first,) = call(
+        cross_kernel, "cross", [square], ids, panel, gram_first, *image, scalars=1, scratch=[held]
+    )
     turned, gram_last = call(
-        turn_kernel, "turn", [wide, square], ids, inverse_first, *arrived, scalars=1, scratch=[held]
-    )
+        turn_kernel, "turn", [wide, square], ids, inverse_first, *swapped(parts), scalars=1, scratch=[held]
+    )
+    first, _ = apply(meta, now[0], halos[0])
     gram = gram_last
-    for i, hop in enumerate(hops_of("col", "node")):
+    hops = hops_of("col", "node")
+    for i, hop in enumerate(hops):
         got = swap(gram, *hop)
-        if i == 2:
+        if i == TIE_HALO:
             got, halos[1] = lax.optimization_barrier((got, halos[1]))
+            _, parts = apply(meta, now[1], halos[1], (), first, count)
+            parts = swapped(parts)
+        if i == len(hops) - TIE_IMAGE:
+            got, parts = lax.optimization_barrier((got, parts))
         gram = gram + got
-    first, _ = apply(meta, now[0], halos[0])
-    _, parts = apply(meta, now[1], halos[1], (), first, count)
-    (cross_last,) = call(
-        turn_cross_kernel, "turn_cross", [square], ids, inverse_first, turned, *swapped(parts),
-        scalars=1, scratch=[held],
-    )
+    (images,) = call(
+        turn_cross_kernel, "turn_cross", [(2, vecs, vecs)], ids, inverse_first, turned, gram_last,
+        cross_first, *parts, scalars=1, scratch=[held],
+    )
+    for hop in hops_of("node"):
+        images = images + swap(images, *hop)
     inverse_last = inverse_factor(gram, nodes)
     parts = call(
         basis_kernel, "basis", [(quarter, cols_here, block)] * count, ids, inverse_last, turned,
         scalars=1, scratch=[held],
     )
-    arrived = swapped(parts)
+    (basis,) = call(
+        functools.partial(join_kernel, half), "join", [(cols_here, width)], ids, *swapped(parts), scalars=1
+    )
     parts = call(
         functools.partial(proj_kernel, nodes), "proj", [(2, cols_here, vecs)] * count, ids,
-        inverse_first, cross_first, gram_first, inverse_last, cross_last, gram_last,
-        scalars=1, scratch=[pltpu.VMEM(square, F32)],
+        inverse_first, inverse_last, images, scalars=1, scratch=[pltpu.VMEM(square, F32)],
     )
     projected = sum(swapped(parts))
-    for i, hop in enumerate(hops_of("node")):
-        projected = projected + swap(projected, *hop)
-        if i == 0:
-            projected, arrived = lax.optimization_barrier((projected, arrived))
-            (basis,) = call(
-                functools.partial(join_kernel, half), "join", [(cols_here, width)], ids, *arrived, scalars=1
-            )
     return basis, projected[0], projected[1]
 
 

time: 262 us -> 254 us (0.969)
  Pallas kernels: 131 us -> 123 us
    ppermute x18, starting transfers between devices: 49.1 us -> 60 us  [exchange(): lax.ppermute(pair[1], 'node', odd)]
    ppermute x18, starting transfers between devices: 19.9 us -> 10.8 us  [exchange(): lax.ppermute(pair[0], 'node', even)]
    ppermute x31, waiting for transfers between devices: 27.7 us -> 35.4 us  [swap(): lax.ppermute(value, axis, [(i, i ^ hop) for i in range(lax.axis_size(axis...]
    ppermute x18, waiting for transfers between devices: 8.04 us -> 0.34 us  [exchange(): lax.ppermute(pair[0], 'node', even)]
    pallas_call x1, Pallas kernels: 14.3 us -> 8.93 us  [prep(): pl.pallas_call(functools.partial(prep_kernel, rows), in_specs=[IN_SMEM] *...]
    pallas_call x10, Pallas kernels: 33.9 us -> 31.1 us  [call(): pl.pallas_call(kernel, in_specs=[IN_SMEM] * scalars + [IN_VMEM] * (len(ar...]
  transfers between devices with their start and end apart: 67 -> 67, of which waited for: 17 -> 12; matrix products, arithmetic and copies ran while one was open for 0% -> 0% of each run, Pallas kernels for 46% -> 45%
where the time goes in v5:
time: 254 us
  Pallas kernels  123 us (48%)
  starting transfers between devices  91.6 us (36%)
  waiting for transfers between devices  35.8 us (14%)
    pallas_call x18, Pallas kernels, apply(): pl.pallas_call(functools.partial(apply_kernel, bool(old), bool(mate)), in...  83.4 us
    ppermute x18, starting transfers between devices, exchange(): lax.ppermute(pair[1], 'node', odd)  60 us
    ppermute x31, waiting for transfers between devices, swap(): lax.ppermute(value, axis, [(i, i ^ hop) for i in range(lax.axis_size(axis...  35.4 us
    pallas_call x10, Pallas kernels, call(): pl.pallas_call(kernel, in_specs=[IN_SMEM] * scalars + [IN_VMEM] * (len(ar...  31.1 us
    ppermute x31, starting transfers between devices, swap(): lax.ppermute(value, axis, [(i, i ^ hop) for i in range(lax.axis_size(axis...  20.8 us
    ppermute x18, starting transfers between devices, exchange(): lax.ppermute(pair[0], 'node', even)  10.8 us
    pallas_call x1, Pallas kernels, prep(): pl.pallas_call(functools.partial(prep_kernel, rows), in_specs=[IN_SMEM] *...  8.93 us
  transfers between devices with their start and end apart: 67, of which 12 were waited for; matrix products, arithmetic and copies ran while one was open for 0% of the time, Pallas kernels for 45%

profile of v5, /device:TPU:0, one launch (start us, length us, event | category | flops | bytes accessed | tf_op | source)
XLA Modules:
  0.0 253.9 jit_solution(17046549049634213059)
XLA Ops:
  2.5 3.0 %collective-permute-start = (f32[24,16,128]{2,1,0:T(8,128)S(1)}, f32[24,16,128]{2,1,0:T(8,128)S(1)}, u32[]{:S(2)}, u32[]{:S(2)}) collective-permute-start(f32[24,16,128]{2,1,0:T(8,128)S(1)} %get-tuple-element.125.refs_3_.refs_7_), channel_id=1, source_target_pairs={{0,4},{4,0},{8,12},{12,8},{16,20},{20,16},{24,28},{28,24},{1,5},{5... | collective-permute-start | bytes 589832 | tf_op jit(solution)/shard_map/ppermute | solution.py:337
  5.5 3.5 %collective-permute-start.1 = (f32[24,16,128]{2,1,0:T(8,128)S(1)}, f32[24,16,128]{2,1,0:T(8,128)S(1)}, u32[]{:S(2)}, u32[]{:S(2)}) collective-permute-start(f32[24,16,128]{2,1,0:T(8,128)S(1)} %get-tuple-element.126.refs_4_.refs_8_), channel_id=1, source_target_pairs={{0,28},{4,8},{8,4},{12,16},{16,12},{20,24},{24,20},{28,0},{1,29},{... | collective-permute-start | bytes 589832 | tf_op jit(solution)/shard_map/ppermute | solution.py:337
  11.0 8.9 %prep.1 = (bf16[288,128,256]{2,1,0:T(8,128)(2,1)S(1)}, f32[48,1,128]{2,1,0:T(1,128)S(1)}, s32[578]{0:T(1024)S(1)}) custom-call(s32[2]{0:T(128)S(1)} %pad_add_fusion.ids_ref, s32[1,288]{1,0:T(1,128)} %own_ref.1, s32[1,288]{1,0:T(1,128)} %col_ref.1, f32[288,128,128]{2,1,0:T(8,128)} %blk_ref.1), custom_call_target="tpu_custom_call" | custom-call | flops 1207959552 | bytes 18874368 | tf_op jit(solution)/shard_map/prep/pallas_call | solution.py:117
  20.0 4.5 %apply.4 = (f32[24,16,128]{2,1,0:T(8,128)S(1)}, f32[24,16,128]{2,1,0:T(8,128)S(1)}) custom-call(s32[578]{0:T(1024)S(1)} %get-tuple-element.122.refs_0_, bf16[288,128,256]{2,1,0:T(8,128)(2,1)S(1)} %get-tuple-element.123.refs_1_, f32[48,1,128]{2,1,0:T(1,128)S(1)} %get-tuple-element.124.refs_2_, f32[24,16,128]{2,1,0:T(8,128)S(1)} %get-tuple-element.125.refs_3_.refs_7_, ...), custom_call_target="tpu_custom_call" | custom-call | bytes 4194304 | tf_op jit(solution)/shard_map/apply/pallas_call | solution.py:196
  26.3 3.5 %collective-permute-start.3 = (f32[24,16,128]{2,1,0:T(8,128)S(1)}, f32[24,16,128]{2,1,0:T(8,128)S(1)}, u32[]{:S(2)}, u32[]{:S(2)}) collective-permute-start(f32[24,16,128]{2,1,0:T(8,128)S(1)} %get-tuple-element.128.refs_4_.refs_8_), channel_id=1, source_target_pairs={{0,28},{4,8},{8,4},{12,16},{16,12},{20,24},{24,20},{28,0},{1,29},{... | collective-permute-start | bytes 589832 | tf_op jit(solution)/shard_map/ppermute | solution.py:337
  29.9 4.5 %apply.6 = (f32[24,16,128]{2,1,0:T(8,128)S(1)}, f32[24,16,128]{2,1,0:T(8,128)S(1)}) custom-call(s32[578]{0:T(1024)S(1)} %get-tuple-element.122.refs_0_, bf16[288,128,256]{2,1,0:T(8,128)(2,1)S(1)} %get-tuple-element.123.refs_1_, f32[48,1,128]{2,1,0:T(1,128)S(1)} %get-tuple-element.124.refs_2_, f32[24,16,128]{2,1,0:T(8,128)S(1)} %get-tuple-element.137.refs_3_.refs_7_, ...), custom_call_target="tpu_custom_call" | custom-call | bytes 4194304 | tf_op jit(solution)/shard_map/apply/pallas_call | solution.py:196
  36.4 4.6 %apply_recur.10 = (f32[24,16,128]{2,1,0:T(8,128)S(1)}, f32[24,16,128]{2,1,0:T(8,128)S(1)}) custom-call(s32[578]{0:T(1024)S(1)} %get-tuple-element.122.refs_0_, bf16[288,128,256]{2,1,0:T(8,128)(2,1)S(1)} %get-tuple-element.123.refs_1_, f32[48,1,128]{2,1,0:T(1,128)S(1)} %get-tuple-element.124.refs_2_, f32[24,16,128]{2,1,0:T(8,128)S(1)} %get-tuple-element.127.refs_3_.refs_7_, ...), custom_call_target="tpu_custom_call" | custom-call | bytes 4194304 | tf_op jit(solution)/shard_map/apply_recur/pallas_call | solution.py:196
  41.7 5.5 %collective-permute-start.5 = (f32[24,16,128]{2,1,0:T(8,128)S(1)}, f32[24,16,128]{2,1,0:T(8,128)S(1)}, u32[]{:S(2)}, u32[]{:S(2)}) collective-permute-start(f32[24,16,128]{2,1,0:T(8,128)S(1)} %get-tuple-element.130.refs_4_.refs_8_), channel_id=1, source_target_pairs={{0,28},{4,8},{8,4},{12,16},{16,12},{20,24},{24,20},{28,0},{1,29},{... | collective-permute-start | bytes 589832 | tf_op jit(solution)/shard_map/ppermute | solution.py:337
  47.2 4.6 %apply_recur.13 = (f32[24,16,128]{2,1,0:T(8,128)S(1)}, f32[24,16,128]{2,1,0:T(8,128)S(1)}) custom-call(s32[578]{0:T(1024)S(1)} %get-tuple-element.122.refs_0_, bf16[288,128,256]{2,1,0:T(8,128)(2,1)S(1)} %get-tuple-element.123.refs_1_, f32[48,1,128]{2,1,0:T(1,128)S(1)} %get-tuple-element.124.refs_2_, f32[24,16,128]{2,1,0:T(8,128)S(1)} %get-tuple-element.139.refs_3_.refs_7_, ...), custom_call_target="tpu_custom_call" | custom-call | bytes 4194304 | tf_op jit(solution)/shard_map/apply_recur/pallas_call | solution.py:196
  51.8 3.8 %collective-permute-start.17 = (f32[24,16,128]{2,1,0:T(8,128)S(1)}, f32[24,16,128]{2,1,0:T(8,128)S(1)}, u32[]{:S(2)}, u32[]{:S(2)}) collective-permute-start(f32[24,16,128]{2,1,0:T(8,128)S(1)} %get-tuple-element.142.refs_4_.refs_8_), channel_id=1, source_target_pairs={{0,28},{4,8},{8,4},{12,16},{16,12},{20,24},{24,20},{28,0},{1,29},{... | collective-permute-start | bytes 589832 | tf_op jit(solution)/shard_map/ppermute | solution.py:337
  55.6 4.5 %apply_recur.11 = (f32[24,16,128]{2,1,0:T(8,128)S(1)}, f32[24,16,128]{2,1,0:T(8,128)S(1)}) custom-call(s32[578]{0:T(1024)S(1)} %get-tuple-element.122.refs_0_, bf16[288,128,256]{2,1,0:T(8,128)(2,1)S(1)} %get-tuple-element.123.refs_1_, f32[48,1,128]{2,1,0:T(1,128)S(1)} %get-tuple-element.124.refs_2_, f32[24,16,128]{2,1,0:T(8,128)S(1)} %get-tuple-element.129.refs_3_.refs_7_, ...), custom_call_target="tpu_custom_call" | custom-call | bytes 4194304 | tf_op jit(solution)/shard_map/apply_recur/pallas_call | solution.py:196
  62.1 4.5 %apply_recur.14 = (f32[24,16,128]{2,1,0:T(8,128)S(1)}, f32[24,16,128]{2,1,0:T(8,128)S(1)}) custom-call(s32[578]{0:T(1024)S(1)} %get-tuple-element.122.refs_0_, bf16[288,128,256]{2,1,0:T(8,128)(2,1)S(1)} %get-tuple-element.123.refs_1_, f32[48,1,128]{2,1,0:T(1,128)S(1)} %get-tuple-element.124.refs_2_, f32[24,16,128]{2,1,0:T(8,128)S(1)} %get-tuple-element.141.refs_3_.refs_7_, ...), custom_call_target="tpu_custom_call" | custom-call | bytes 4194304 | tf_op jit(solution)/shard_map/apply_recur/pallas_call | solution.py:196
  67.5 8.1 %collective-permute-start.19 = (f32[24,16,128]{2,1,0:T(8,128)S(1)}, f32[24,16,128]{2,1,0:T(8,128)S(1)}, u32[]{:S(2)}, u32[]{:S(2)}) collective-permute-start(f32[24,16,128]{2,1,0:T(8,128)S(1)} %get-tuple-element.144.refs_4_), channel_id=1, source_target_pairs={{0,28},{4,8},{8,4},{12,16},{16,12},{20,24},{24,20},{28,0},{1,29},{... | collective-permute-start | bytes 589832 | tf_op jit(solution)/shard_map/ppermute | solution.py:337
  75.7 4.5 %apply_recur.12 = (f32[24,16,128]{2,1,0:T(8,128)S(1)}, f32[24,16,128]{2,1,0:T(8,128)S(1)}) custom-call(s32[578]{0:T(1024)S(1)} %get-tuple-element.122.refs_0_, bf16[288,128,256]{2,1,0:T(8,128)(2,1)S(1)} %get-tuple-element.123.refs_1_, f32[48,1,128]{2,1,0:T(1,128)S(1)} %get-tuple-element.124.refs_2_, f32[24,16,128]{2,1,0:T(8,128)S(1)} %get-tuple-element.131.refs_3_, ...), custom_call_target="tpu_custom_call" | custom-call | bytes 4194304 | tf_op jit(solution)/shard_map/apply_recur/pallas_call | solution.py:196
  82.2 4.7 %apply_recur_parts.2 = (f32[24,16,128]{2,1,0:T(8,128)S(1)}, f32[24,16,128]{2,1,0:T(8,128)S(1)}, f32[12,32,128]{2,1,0:T(8,128)S(1)}, f32[12,32,128]{2,1,0:T(8,128...) custom-call(s32[578]{0:T(1024)S(1)} %get-tuple-element.122.refs_0_, ...), custom_call_target="tpu_custom_call" | custom-call | bytes 4194304 | tf_op jit(solution)/shard_map/apply_recur_parts/pallas_call | solution.py:196
  87.0 5.3 %collective-permute-start.28 = (f32[24,16,128]{2,1,0:T(8,128)S(1)}, f32[24,16,128]{2,1,0:T(8,128)S(1)}, u32[]{:S(2)}, u32[]{:S(2)}) collective-permute-start(f32[24,16,128]{2,1,0:T(8,128)S(1)} %get-tuple-element.164.refs_4_.refs_8_), channel_id=1, source_target_pairs={{0,28},{4,8},{8,4},{12,16},{16,12},{20,24},{24,20},{28,0},{1,29},{... | collective-permute-start | bytes 589832 | tf_op jit(solution)/shard_map/ppermute | solution.py:337
  94.2 4.5 %apply.5 = (f32[24,16,128]{2,1,0:T(8,128)S(1)}, f32[24,16,128]{2,1,0:T(8,128)S(1)}) custom-call(s32[578]{0:T(1024)S(1)} %get-tuple-element.122.refs_0_, bf16[288,128,256]{2,1,0:T(8,128)(2,1)S(1)} %get-tuple-element.123.refs_1_, f32[48,1,128]{2,1,0:T(1,128)S(1)} %get-tuple-element.124.refs_2_, f32[24,16,128]{2,1,0:T(8,128)S(1)} %get-tuple-element.150.refs_3_.refs_9_.refs_7_, ...), custom_call_target="tpu_custom_call" | custom-call | bytes 4194304 | tf_op jit(solution)/shard_map/apply/pallas_call | solution.py:196
  98.8 3.2 %collective-permute-start.11 = (f32[24,16,128]{2,1,0:T(8,128)S(1)}, f32[24,16,128]{2,1,0:T(8,128)S(1)}, u32[]{:S(2)}, u32[]{:S(2)}) collective-permute-start(f32[24,16,128]{2,1,0:T(8,128)S(1)} %get-tuple-element.170.refs_4_.refs_8_), channel_id=1, source_target_pairs={{0,28},{4,8},{8,4},{12,16},{16,12},{20,24},{24,20},{28,0},{1,29},{... | collective-permute-start | bytes 589832 | tf_op jit(solution)/shard_map/ppermute | solution.py:337
  102.0 4.6 %apply_parts.2 = (f32[24,16,128]{2,1,0:T(8,128)S(1)}, f32[24,16,128]{2,1,0:T(8,128)S(1)}, f32[12,32,128]{2,1,0:T(8,128)S(1)}, f32[12,32,128]{2,1,0:T(8,128)S(1)}...) custom-call(s32[578]{0:T(1024)S(1)} %get-tuple-element.122.refs_0_, ...), custom_call_target="tpu_custom_call" | custom-call | bytes 4194304 | tf_op jit(solution)/shard_map/apply_parts/pallas_call | solution.py:196
  110.7 4.7 %apply_recur.15 = (f32[24,16,128]{2,1,0:T(8,128)S(1)}, f32[24,16,128]{2,1,0:T(8,128)S(1)}) custom-call(s32[578]{0:T(1024)S(1)} %get-tuple-element.122.refs_0_, bf16[288,128,256]{2,1,0:T(8,128)(2,1)S(1)} %get-tuple-element.123.refs_1_, f32[48,1,128]{2,1,0:T(1,128)S(1)} %get-tuple-element.124.refs_2_, f32[24,16,128]{2,1,0:T(8,128)S(1)} %get-tuple-element.169.refs_3_.refs_7_, ...), custom_call_target="tpu_custom_call" | custom-call | bytes 4194304 | tf_op jit(solution)/shard_map/apply_recur/pallas_call | solution.py:196
  117.6 6.7 %collective-permute-start.24 = (f32[24,16,128]{2,1,0:T(8,128)S(1)}, f32[24,16,128]{2,1,0:T(8,128)S(1)}, u32[]{:S(2)}, u32[]{:S(2)}) collective-permute-start(f32[24,16,128]{2,1,0:T(8,128)S(1)} %get-tuple-element.192.refs_4_.refs_8_), channel_id=1, source_target_pairs={{0,28},{4,8},{8,4},{12,16},{16,12},{20,24},{24,20},{28,0},{1,29},{... | collective-permute-start | bytes 589832 | tf_op jit(solution)/shard_map/ppermute | solution.py:337
  124.3 2.0 collective-permute-start.38
  126.3 4.5 %apply_recur.16 = (f32[24,16,128]{2,1,0:T(8,128)S(1)}, f32[24,16,128]{2,1,0:T(8,128)S(1)}) custom-call(s32[578]{0:T(1024)S(1)} %get-tuple-element.122.refs_0_, bf16[288,128,256]{2,1,0:T(8,128)(2,1)S(1)} %get-tuple-element.123.refs_1_, f32[48,1,128]{2,1,0:T(1,128)S(1)} %get-tuple-element.124.refs_2_, f32[24,16,128]{2,1,0:T(8,128)S(1)} %get-tuple-element.185.refs_3_.refs_7_, ...), custom_call_target="tpu_custom_call" | custom-call | bytes 4194304 | tf_op jit(solution)/shard_map/apply_recur/pallas_call | solution.py:196
  131.0 2.1 collective-permute-start.36
  134.2 4.6 %apply_recur.17 = (f32[24,16,128]{2,1,0:T(8,128)S(1)}, f32[24,16,128]{2,1,0:T(8,128)S(1)}) custom-call(s32[578]{0:T(1024)S(1)} %get-tuple-element.122.refs_0_, bf16[288,128,256]{2,1,0:T(8,128)(2,1)S(1)} %get-tuple-element.123.refs_1_, f32[48,1,128]{2,1,0:T(1,128)S(1)} %get-tuple-element.124.refs_2_, f32[24,16,128]{2,1,0:T(8,128)S(1)} %get-tuple-element.191.refs_3_.refs_7_, ...), custom_call_target="tpu_custom_call" | custom-call | bytes 4194304 | tf_op jit(solution)/shard_map/apply_recur/pallas_call | solution.py:196
  139.8 4.5 %collective-permute-done.33 = f32[128,128]{1,0:T(8,128)S(1)} collective-permute-done((f32[128,128]{1,0:T(8,128)S(1)}, f32[128,128]{1,0:T(8,128)S(1)}, u32[]{:S(2)}, u32[]{:S(2)}) %collective-permute-start.33) | collective-permute-done | bytes 65568 | tf_op jit(solution)/shard_map/ppermute | solution.py:341
  145.1 4.6 %apply_recur.18 = (f32[24,16,128]{2,1,0:T(8,128)S(1)}, f32[24,16,128]{2,1,0:T(8,128)S(1)}) custom-call(s32[578]{0:T(1024)S(1)} %get-tuple-element.122.refs_0_, bf16[288,128,256]{2,1,0:T(8,128)(2,1)S(1)} %get-tuple-element.123.refs_1_, f32[48,1,128]{2,1,0:T(1,128)S(1)} %get-tuple-element.124.refs_2_, f32[24,16,128]{2,1,0:T(8,128)S(1)} %get-tuple-element.202.refs_3_.refs_7_, ...), custom_call_target="tpu_custom_call" | custom-call | bytes 4194304 | tf_op jit(solution)/shard_map/apply_recur/pallas_call | solution.py:196
  149.7 4.0 %collective-permute-start.44 = (f32[24,16,128]{2,1,0:T(8,128)S(1)}, f32[24,16,128]{2,1,0:T(8,128)S(1)}, u32[]{:S(2)}, u32[]{:S(2)}) collective-permute-start(f32[24,16,128]{2,1,0:T(8,128)S(1)} %get-tuple-element.188.refs_4_), channel_id=1, source_target_pairs={{0,28},{4,8},{8,4},{12,16},{16,12},{20,24},{24,20},{28,0},{1,29},{... | collective-permute-start | bytes 589832 | tf_op jit(solution)/shard_map/ppermute | solution.py:337
  153.8 4.3 %collective-permute-done.34 = f32[128,128]{1,0:T(8,128)S(1)} collective-permute-done((f32[128,128]{1,0:T(8,128)S(1)}, f32[128,128]{1,0:T(8,128)S(1)}, u32[]{:S(2)}, u32[]{:S(2)}) %collective-permute-start.34) | collective-permute-done | bytes 65568 | tf_op jit(solution)/shard_map/ppermute | solution.py:341
  158.2 3.0 %collective-permute-start.42 = (f32[128,128]{1,0:T(8,128)S(1)}, f32[128,128]{1,0:T(8,128)S(1)}, u32[]{:S(2)}, u32[]{:S(2)}) collective-permute-start(f32[128,128]{1,0:T(8,128)S(1)} %add.51), channel_id=1, source_target_pairs={{0,16},{4,20},{8,24},{12,28},{16,0},{20,4},{24,8},{28,12},{1,17},{... | collective-permute-start | bytes 196616 | tf_op jit(solution)/shard_map/ppermute | solution.py:341
  161.1 4.5 %apply_recur.19 = (f32[24,16,128]{2,1,0:T(8,128)S(1)}, f32[24,16,128]{2,1,0:T(8,128)S(1)}) custom-call(s32[578]{0:T(1024)S(1)} %get-tuple-element.122.refs_0_, bf16[288,128,256]{2,1,0:T(8,128)(2,1)S(1)} %get-tuple-element.123.refs_1_, f32[48,1,128]{2,1,0:T(1,128)S(1)} %get-tuple-element.124.refs_2_, f32[24,16,128]{2,1,0:T(8,128)S(1)} %get-tuple-element.171.refs_3_, ...), custom_call_target="tpu_custom_call" | custom-call | bytes 4194304 | tf_op jit(solution)/shard_map/apply_recur/pallas_call | solution.py:196
  166.8 2.0 collective-permute-start.41
  168.8 4.7 %apply_recur_parts.3 = (f32[24,16,128]{2,1,0:T(8,128)S(1)}, f32[24,16,128]{2,1,0:T(8,128)S(1)}, f32[12,32,128]{2,1,0:T(8,128)S(1)}, f32[12,32,128]{2,1,0:T(8,128...) custom-call(s32[578]{0:T(1024)S(1)} %get-tuple-element.122.refs_0_, ...), custom_call_target="tpu_custom_call" | custom-call | bytes 4194304 | tf_op jit(solution)/shard_map/apply_recur_parts/pallas_call | solution.py:196
  173.6 2.7 %collective-permute-start.46 = (f32[12,32,128]{2,1,0:T(8,128)S(1)}, f32[12,32,128]{2,1,0:T(8,128)S(1)}, u32[]{:S(2)}, u32[]{:S(2)}) collective-permute-start(f32[12,32,128]{2,1,0:T(8,128)S(1)} %get-tuple-element.206), channel_id=1, source_target_pairs={{0,2},{1,3},{2,0},{3,1},{4,6},{5,7},{6,4},{7,5},{8,10},{9,11},{10,... | collective-permute-start | bytes 589832 | tf_op jit(solution)/shard_map/ppermute | solution.py:341
  177.1 2.2 collective-permute-start.51
  179.3 7.1 %factor.2.inv_ref.first_ref = f32[128,128]{1,0:T(8,128)S(1)} custom-call(f32[128,128]{1,0:T(8,128)S(1)} %add.52.g_ref), custom_call_target="tpu_custom_call" | custom-call | tf_op jit(solution)/shard_map/factor/pallas_call | solution.py:43
  186.4 4.0 %turn.1 = (f32[12,128,128]{2,1,0:T(8,128)S(1)}, f32[128,128]{1,0:T(8,128)S(1)}) custom-call(s32[2]{0:T(128)S(1)} %pad_add_fusion.ids_ref, f32[128,128]{1,0:T(8,128)S(1)} %factor.2.inv_ref.first_ref, f32[12,32,128]{2,1,0:T(8,128)S(1)} %get-tuple-element.204.refs_0_, f32[12,32,128]{2,1,0:T(8,128)S(1)} %collective-permute-done.45.refs_1_, ...), custom_call_target="tpu_custom_call" | custom-call | tf_op jit(solution)/shard_map/turn/pallas_call | solution.py:43
  191.8 2.5 collective-permute-start.49
  194.3 4.5 %apply.7 = (f32[24,16,128]{2,1,0:T(8,128)S(1)}, f32[24,16,128]{2,1,0:T(8,128)S(1)}) custom-call(s32[578]{0:T(1024)S(1)} %get-tuple-element.122.refs_0_, bf16[288,128,256]{2,1,0:T(8,128)(2,1)S(1)} %get-tuple-element.123.refs_1_, f32[48,1,128]{2,1,0:T(1,128)S(1)} %get-tuple-element.124.refs_2_, f32[24,16,128]{2,1,0:T(8,128)S(1)} %get-tuple-element.193.refs_9_.refs_3_, ...), custom_call_target="tpu_custom_call" | custom-call | bytes 4194304 | tf_op jit(solution)/shard_map/apply/pallas_call | solution.py:196
  198.8 5.6 %apply_parts.3 = (f32[24,16,128]{2,1,0:T(8,128)}, f32[24,16,128]{2,1,0:T(8,128)}, f32[12,32,128]{2,1,0:T(8,128)S(1)}, f32[12,32,128]{2,1,0:T(8,128)S(1)}, f32[12...) custom-call(s32[578]{0:T(1024)S(1)} %get-tuple-element.122.refs_0_, ...), custom_call_target="tpu_custom_call" | custom-call | bytes 4194304 | tf_op jit(solution)/shard_map/apply_parts/pallas_call | solution.py:196
  206.4 2.6 %collective-permute-done.52 = f32[128,128]{1,0:T(8,128)S(1)} collective-permute-done((f32[128,128]{1,0:T(8,128)S(1)}, f32[128,128]{1,0:T(8,128)S(1)}, u32[]{:S(2)}, u32[]{:S(2)}) %collective-permute-start.52) | collective-permute-done | bytes 65568 | tf_op jit(solution)/shard_map/ppermute | solution.py:341
  209.1 4.3 %collective-permute-done.53 = f32[128,128]{1,0:T(8,128)S(1)} collective-permute-done((f32[128,128]{1,0:T(8,128)S(1)}, f32[128,128]{1,0:T(8,128)S(1)}, u32[]{:S(2)}, u32[]{:S(2)}) %collective-permute-start.53) | collective-permute-done | bytes 65568 | tf_op jit(solution)/shard_map/ppermute | solution.py:341
  213.4 2.2 cross.1.first_ref
  215.7 3.0 %collective-permute-done.54 = f32[128,128]{1,0:T(8,128)S(1)} collective-permute-done((f32[128,128]{1,0:T(8,128)S(1)}, f32[128,128]{1,0:T(8,128)S(1)}, u32[]{:S(2)}, u32[]{:S(2)}) %collective-permute-start.54) | collective-permute-done | bytes 65568 | tf_op jit(solution)/shard_map/ppermute | solution.py:341
  218.7 4.0 %turn_cross.1 = f32[2,128,128]{2,1,0:T(8,128)S(1)} custom-call(s32[2]{0:T(128)S(1)} %pad_add_fusion.ids_ref, f32[128,128]{1,0:T(8,128)S(1)} %factor.2.inv_ref.first_ref, f32[12,128,128]{2,1,0:T(8,128)S(1)} %get-tuple-element.223.f_ref, f32[128,128]{1,0:T(8,128)S(1)} %get-tuple-element.208.g_ref, f32[128,128]{1,0:T(8,128)S(1)} %cross.1.first_ref, ...), custom_call_target="tpu_custom_call" | custom-call | tf_op jit(solution)/shard_map/turn_cross/pallas_call | solution.py:43
  223.1 4.7 %collective-permute-done.61 = f32[2,128,128]{2,1,0:T(8,128)S(1)} collective-permute-done((f32[2,128,128]{2,1,0:T(8,128)S(1)}, f32[2,128,128]{2,1,0:T(8,128)S(1)}, u32[]{:S(2)}, u32[]{:S(2)}) %collective-permute-start.61) | collective-permute-done | bytes 131104 | tf_op jit(solution)/shard_map/ppermute | solution.py:341
  227.9 7.1 %factor.3.inv_ref.last_ref = f32[128,128]{1,0:T(8,128)S(1)} custom-call(f32[128,128]{1,0:T(8,128)S(1)} %add.57.g_ref), custom_call_target="tpu_custom_call" | custom-call | tf_op jit(solution)/shard_map/factor/pallas_call | solution.py:43
  238.9 8.9 %collective-permute-done.63 = f32[2,128,128]{2,1,0:T(8,128)S(1)} collective-permute-done((f32[2,128,128]{2,1,0:T(8,128)S(1)}, f32[2,128,128]{2,1,0:T(8,128)S(1)}, u32[]{:S(2)}, u32[]{:S(2)}) %collective-permute-start.63) | collective-permute-done | bytes 131104 | tf_op jit(solution)/shard_map/ppermute | solution.py:341
  (133 shorter events, 40.6 us)
Async XLA Ops:
  2.5 17.4 %collective-permute-start = (f32[24,16,128]{2,1,0:T(8,128)S(1)}, f32[24,16,128]{2,1,0:T(8,128)S(1)}, u32[]{:S(2)}, u32[]{:S(2)}) collective-permute-start(f32[24,16,128]{2,1,0:T(8,128)S(1)} %get-tuple-element.125.refs_3_.refs_7_), channel_id=1, source_target_pairs={{0,4},{4,0},{8,12},{12,8},{16,20},{20,16},{24,28},{28,24},{1,5},{5... | collective-permute-start | bytes 589832 | tf_op jit(solution)/shard_map/ppermute | solution.py:337
  5.5 14.4 %collective-permute-start.1 = (f32[24,16,128]{2,1,0:T(8,128)S(1)}, f32[24,16,128]{2,1,0:T(8,128)S(1)}, u32[]{:S(2)}, u32[]{:S(2)}) collective-permute-start(f32[24,16,128]{2,1,0:T(8,128)S(1)} %get-tuple-element.126.refs_4_.refs_8_), channel_id=1, source_target_pairs={{0,28},{4,8},{8,4},{12,16},{16,12},{20,24},{24,20},{28,0},{1,29},{... | collective-permute-start | bytes 589832 | tf_op jit(solution)/shard_map/ppermute | solution.py:337
  9.1 20.8 %collective-permute-start.12 = (f32[24,16,128]{2,1,0:T(8,128)S(1)}, f32[24,16,128]{2,1,0:T(8,128)S(1)}, u32[]{:S(2)}, u32[]{:S(2)}) collective-permute-start(f32[24,16,128]{2,1,0:T(8,128)S(1)} %get-tuple-element.137.refs_3_.refs_7_), channel_id=1, source_target_pairs={{0,4},{4,0},{8,12},{12,8},{16,20},{20,16},{24,28},{28,24},{1,5},{5... | collective-permute-start | bytes 589832 | tf_op jit(solution)/shard_map/ppermute | solution.py:337
  9.1 20.8 %collective-permute-start.13 = (f32[24,16,128]{2,1,0:T(8,128)S(1)}, f32[24,16,128]{2,1,0:T(8,128)S(1)}, u32[]{:S(2)}, u32[]{:S(2)}) collective-permute-start(f32[24,16,128]{2,1,0:T(8,128)S(1)} %get-tuple-element.138.refs_4_.refs_8_), channel_id=1, source_target_pairs={{0,28},{4,8},{8,4},{12,16},{16,12},{20,24},{24,20},{28,0},{1,29},{... | collective-permute-start | bytes 589832 | tf_op jit(solution)/shard_map/ppermute | solution.py:337
  24.5 11.9 %collective-permute-start.2 = (f32[24,16,128]{2,1,0:T(8,128)S(1)}, f32[24,16,128]{2,1,0:T(8,128)S(1)}, u32[]{:S(2)}, u32[]{:S(2)}) collective-permute-start(f32[24,16,128]{2,1,0:T(8,128)S(1)} %get-tuple-element.127.refs_3_.refs_7_), channel_id=1, source_target_pairs={{0,4},{4,0},{8,12},{12,8},{16,20},{20,16},{24,28},{28,24},{1,5},{5... | collective-permute-start | bytes 589832 | tf_op jit(solution)/shard_map/ppermute | solution.py:337
  34.4 12.7 %collective-permute-start.14 = (f32[24,16,128]{2,1,0:T(8,128)S(1)}, f32[24,16,128]{2,1,0:T(8,128)S(1)}, u32[]{:S(2)}, u32[]{:S(2)}) collective-permute-start(f32[24,16,128]{2,1,0:T(8,128)S(1)} %get-tuple-element.139.refs_3_.refs_7_), channel_id=1, source_target_pairs={{0,4},{4,0},{8,12},{12,8},{16,20},{20,16},{24,28},{28,24},{1,5},{5... | collective-permute-start | bytes 589832 | tf_op jit(solution)/shard_map/ppermute | solution.py:337
  34.5 12.7 %collective-permute-start.15 = (f32[24,16,128]{2,1,0:T(8,128)S(1)}, f32[24,16,128]{2,1,0:T(8,128)S(1)}, u32[]{:S(2)}, u32[]{:S(2)}) collective-permute-start(f32[24,16,128]{2,1,0:T(8,128)S(1)} %get-tuple-element.140.refs_4_.refs_8_), channel_id=1, source_target_pairs={{0,28},{4,8},{8,4},{12,16},{16,12},{20,24},{24,20},{28,0},{1,29},{... | collective-permute-start | bytes 589832 | tf_op jit(solution)/shard_map/ppermute | solution.py:337
  41.0 14.6 %collective-permute-start.4 = (f32[24,16,128]{2,1,0:T(8,128)S(1)}, f32[24,16,128]{2,1,0:T(8,128)S(1)}, u32[]{:S(2)}, u32[]{:S(2)}) collective-permute-start(f32[24,16,128]{2,1,0:T(8,128)S(1)} %get-tuple-element.129.refs_3_.refs_7_), channel_id=1, source_target_pairs={{0,4},{4,0},{8,12},{12,8},{16,20},{20,16},{24,28},{28,24},{1,5},{5... | collective-permute-start | bytes 589832 | tf_op jit(solution)/shard_map/ppermute | solution.py:337
  41.7 13.9 %collective-permute-start.5 = (f32[24,16,128]{2,1,0:T(8,128)S(1)}, f32[24,16,128]{2,1,0:T(8,128)S(1)}, u32[]{:S(2)}, u32[]{:S(2)}) collective-permute-start(f32[24,16,128]{2,1,0:T(8,128)S(1)} %get-tuple-element.130.refs_4_.refs_8_), channel_id=1, source_target_pairs={{0,28},{4,8},{8,4},{12,16},{16,12},{20,24},{24,20},{28,0},{1,29},{... | collective-permute-start | bytes 589832 | tf_op jit(solution)/shard_map/ppermute | solution.py:337
  60.1 15.5 %collective-permute-start.6 = (f32[24,16,128]{2,1,0:T(8,128)S(1)}, f32[24,16,128]{2,1,0:T(8,128)S(1)}, u32[]{:S(2)}, u32[]{:S(2)}) collective-permute-start(f32[24,16,128]{2,1,0:T(8,128)S(1)} %get-tuple-element.131.refs_3_), channel_id=1, source_target_pairs={{0,4},{4,0},{8,12},{12,8},{16,20},{20,16},{24,28},{28,24},{1,5},{5... | collective-permute-start | bytes 589832 | tf_op jit(solution)/shard_map/ppermute | solution.py:337
  60.2 15.4 %collective-permute-start.7 = (f32[24,16,128]{2,1,0:T(8,128)S(1)}, f32[24,16,128]{2,1,0:T(8,128)S(1)}, u32[]{:S(2)}, u32[]{:S(2)}) collective-permute-start(f32[24,16,128]{2,1,0:T(8,128)S(1)} %get-tuple-element.132.refs_4_), channel_id=1, source_target_pairs={{0,28},{4,8},{8,4},{12,16},{16,12},{20,24},{24,20},{28,0},{1,29},{... | collective-permute-start | bytes 589832 | tf_op jit(solution)/shard_map/ppermute | solution.py:337
  66.7 15.5 %collective-permute-start.18 = (f32[24,16,128]{2,1,0:T(8,128)S(1)}, f32[24,16,128]{2,1,0:T(8,128)S(1)}, u32[]{:S(2)}, u32[]{:S(2)}) collective-permute-start(f32[24,16,128]{2,1,0:T(8,128)S(1)} %get-tuple-element.143.refs_3_), channel_id=1, source_target_pairs={{0,4},{4,0},{8,12},{12,8},{16,20},{20,16},{24,28},{28,24},{1,5},{5... | collective-permute-start | bytes 589832 | tf_op jit(solution)/shard_map/ppermute | solution.py:337
  67.5 14.7 %collective-permute-start.19 = (f32[24,16,128]{2,1,0:T(8,128)S(1)}, f32[24,16,128]{2,1,0:T(8,128)S(1)}, u32[]{:S(2)}, u32[]{:S(2)}) collective-permute-start(f32[24,16,128]{2,1,0:T(8,128)S(1)} %get-tuple-element.144.refs_4_), channel_id=1, source_target_pairs={{0,28},{4,8},{8,4},{12,16},{16,12},{20,24},{24,20},{28,0},{1,29},{... | collective-permute-start | bytes 589832 | tf_op jit(solution)/shard_map/ppermute | solution.py:337
  80.2 12.1 %collective-permute-start.8 = (f32[24,16,128]{2,1,0:T(8,128)S(1)}, f32[24,16,128]{2,1,0:T(8,128)S(1)}, u32[]{:S(2)}, u32[]{:S(2)}) collective-permute-start(f32[24,16,128]{2,1,0:T(8,128)S(1)} %get-tuple-element.150.refs_3_.refs_9_.refs_7_), channel_id=1, source_target_pairs={{0,4},{4,0},{8,12},{12,8},{16,20},{20,16},{24,28},{28,24},{1,5},{5... | collective-permute-start | bytes 589832 | tf_op jit(solution)/shard_map/ppermute | solution.py:337
  80.3 13.5 %collective-permute-start.9 = (f32[24,16,128]{2,1,0:T(8,128)S(1)}, f32[24,16,128]{2,1,0:T(8,128)S(1)}, u32[]{:S(2)}, u32[]{:S(2)}) collective-permute-start(f32[24,16,128]{2,1,0:T(8,128)S(1)} %get-tuple-element.151.refs_4_.refs_10_.refs_8_), channel_id=1, source_target_pairs={{0,28},{4,8},{8,4},{12,16},{16,12},{20,24},{24,20},{28,0},{1,29},{... | collective-permute-start | bytes 589832 | tf_op jit(solution)/shard_map/ppermute | solution.py:337
  86.9 11.8 %collective-permute-start.27 = (f32[24,16,128]{2,1,0:T(8,128)S(1)}, f32[24,16,128]{2,1,0:T(8,128)S(1)}, u32[]{:S(2)}, u32[]{:S(2)}) collective-permute-start(f32[24,16,128]{2,1,0:T(8,128)S(1)} %get-tuple-element.163.refs_3_.refs_7_), channel_id=1, source_target_pairs={{0,4},{4,0},{8,12},{12,8},{16,20},{20,16},{24,28},{28,24},{1,5},{5... | collective-permute-start | bytes 589832 | tf_op jit(solution)/shard_map/ppermute | solution.py:337
  87.0 11.8 %collective-permute-start.28 = (f32[24,16,128]{2,1,0:T(8,128)S(1)}, f32[24,16,128]{2,1,0:T(8,128)S(1)}, u32[]{:S(2)}, u32[]{:S(2)}) collective-permute-start(f32[24,16,128]{2,1,0:T(8,128)S(1)} %get-tuple-element.164.refs_4_.refs_8_), channel_id=1, source_target_pairs={{0,28},{4,8},{8,4},{12,16},{16,12},{20,24},{24,20},{28,0},{1,29},{... | collective-permute-start | bytes 589832 | tf_op jit(solution)/shard_map/ppermute | solution.py:337
  92.3 14.3 %collective-permute-start.20 = (f32[12,32,128]{2,1,0:T(8,128)S(1)}, f32[12,32,128]{2,1,0:T(8,128)S(1)}, u32[]{:S(2)}, u32[]{:S(2)}) collective-permute-start(f32[12,32,128]{2,1,0:T(8,128)S(1)} %get-tuple-element.146), channel_id=1, source_target_pairs={{0,1},{1,0},{2,3},{3,2},{4,5},{5,4},{6,7},{7,6},{8,9},{9,8},{10,11... | collective-permute-start | bytes 589832 | tf_op jit(solution)/shard_map/ppermute | solution.py:341
  92.3 14.4 %collective-permute-start.21 = (f32[12,32,128]{2,1,0:T(8,128)S(1)}, f32[12,32,128]{2,1,0:T(8,128)S(1)}, u32[]{:S(2)}, u32[]{:S(2)}) collective-permute-start(f32[12,32,128]{2,1,0:T(8,128)S(1)} %get-tuple-element.147), channel_id=1, source_target_pairs={{0,2},{1,3},{2,0},{3,1},{4,6},{5,7},{6,4},{7,5},{8,10},{9,11},{10,... | collective-permute-start | bytes 589832 | tf_op jit(solution)/shard_map/ppermute | solution.py:341
  93.8 14.7 %collective-permute-start.22 = (f32[12,32,128]{2,1,0:T(8,128)S(1)}, f32[12,32,128]{2,1,0:T(8,128)S(1)}, u32[]{:S(2)}, u32[]{:S(2)}) collective-permute-start(f32[12,32,128]{2,1,0:T(8,128)S(1)} %get-tuple-element.148), channel_id=1, source_target_pairs={{0,3},{1,2},{2,1},{3,0},{4,7},{5,6},{6,5},{7,4},{8,11},{9,10},{10,... | collective-permute-start | bytes 589832 | tf_op jit(solution)/shard_map/ppermute | solution.py:341
  98.7 12.0 %collective-permute-start.10 = (f32[24,16,128]{2,1,0:T(8,128)S(1)}, f32[24,16,128]{2,1,0:T(8,128)S(1)}, u32[]{:S(2)}, u32[]{:S(2)}) collective-permute-start(f32[24,16,128]{2,1,0:T(8,128)S(1)} %get-tuple-element.169.refs_3_.refs_7_), channel_id=1, source_target_pairs={{0,4},{4,0},{8,12},{12,8},{16,20},{20,16},{24,28},{28,24},{1,5},{5... | collective-permute-start | bytes 589832 | tf_op jit(solution)/shard_map/ppermute | solution.py:337
  98.8 11.9 %collective-permute-start.11 = (f32[24,16,128]{2,1,0:T(8,128)S(1)}, f32[24,16,128]{2,1,0:T(8,128)S(1)}, u32[]{:S(2)}, u32[]{:S(2)}) collective-permute-start(f32[24,16,128]{2,1,0:T(8,128)S(1)} %get-tuple-element.170.refs_4_.refs_8_), channel_id=1, source_target_pairs={{0,28},{4,8},{8,4},{12,16},{16,12},{20,24},{24,20},{28,0},{1,29},{... | collective-permute-start | bytes 589832 | tf_op jit(solution)/shard_map/ppermute | solution.py:337
  106.7 17.6 %collective-permute-start.29 = (f32[24,16,128]{2,1,0:T(8,128)S(1)}, f32[24,16,128]{2,1,0:T(8,128)S(1)}, u32[]{:S(2)}, u32[]{:S(2)}) collective-permute-start(f32[24,16,128]{2,1,0:T(8,128)S(1)} %get-tuple-element.185.refs_3_.refs_7_), channel_id=1, source_target_pairs={{0,4},{4,0},{8,12},{12,8},{16,20},{20,16},{24,28},{28,24},{1,5},{5... | collective-permute-start | bytes 589832 | tf_op jit(solution)/shard_map/ppermute | solution.py:337
  106.8 17.6 %collective-permute-start.30 = (f32[24,16,128]{2,1,0:T(8,128)S(1)}, f32[24,16,128]{2,1,0:T(8,128)S(1)}, u32[]{:S(2)}, u32[]{:S(2)}) collective-permute-start(f32[24,16,128]{2,1,0:T(8,128)S(1)} %get-tuple-element.186.refs_4_.refs_8_), channel_id=1, source_target_pairs={{0,28},{4,8},{8,4},{12,16},{16,12},{20,24},{24,20},{28,0},{1,29},{... | collective-permute-start | bytes 589832 | tf_op jit(solution)/shard_map/ppermute | solution.py:337
  108.5 17.9 %collective-permute-start.37 = (f32[12,32,128]{2,1,0:T(8,128)S(1)}, f32[12,32,128]{2,1,0:T(8,128)S(1)}, u32[]{:S(2)}, u32[]{:S(2)}) collective-permute-start(f32[12,32,128]{2,1,0:T(8,128)S(1)} %get-tuple-element.182), channel_id=1, source_target_pairs={{0,1},{1,0},{2,3},{3,2},{4,5},{5,4},{6,7},{7,6},{8,9},{9,8},{10,11... | collective-permute-start | bytes 589832 | tf_op jit(solution)/shard_map/ppermute | solution.py:341
  115.5 15.5 %collective-permute-start.23 = (f32[24,16,128]{2,1,0:T(8,128)S(1)}, f32[24,16,128]{2,1,0:T(8,128)S(1)}, u32[]{:S(2)}, u32[]{:S(2)}) collective-permute-start(f32[24,16,128]{2,1,0:T(8,128)S(1)} %get-tuple-element.191.refs_3_.refs_7_), channel_id=1, source_target_pairs={{0,4},{4,0},{8,12},{12,8},{16,20},{20,16},{24,28},{28,24},{1,5},{5... | collective-permute-start | bytes 589832 | tf_op jit(solution)/shard_map/ppermute | solution.py:337
  117.6 15.5 %collective-permute-start.24 = (f32[24,16,128]{2,1,0:T(8,128)S(1)}, f32[24,16,128]{2,1,0:T(8,128)S(1)}, u32[]{:S(2)}, u32[]{:S(2)}) collective-permute-start(f32[24,16,128]{2,1,0:T(8,128)S(1)} %get-tuple-element.192.refs_4_.refs_8_), channel_id=1, source_target_pairs={{0,28},{4,8},{8,4},{12,16},{16,12},{20,24},{24,20},{28,0},{1,29},{... | collective-permute-start | bytes 589832 | tf_op jit(solution)/shard_map/ppermute | solution.py:337
  124.3 14.5 %collective-permute-start.38 = (f32[12,32,128]{2,1,0:T(8,128)S(1)}, f32[12,32,128]{2,1,0:T(8,128)S(1)}, u32[]{:S(2)}, u32[]{:S(2)}) collective-permute-start(f32[12,32,128]{2,1,0:T(8,128)S(1)} %get-tuple-element.183), channel_id=1, source_target_pairs={{0,2},{1,3},{2,0},{3,1},{4,6},{5,7},{6,4},{7,5},{8,10},{9,11},{10,... | collective-permute-start | bytes 589832 | tf_op jit(solution)/shard_map/ppermute | solution.py:341
  126.3 18.7 %collective-permute-start.39 = (f32[12,32,128]{2,1,0:T(8,128)S(1)}, f32[12,32,128]{2,1,0:T(8,128)S(1)}, u32[]{:S(2)}, u32[]{:S(2)}) collective-permute-start(f32[12,32,128]{2,1,0:T(8,128)S(1)} %get-tuple-element.184), channel_id=1, source_target_pairs={{0,3},{1,2},{2,1},{3,0},{4,7},{5,6},{6,5},{7,4},{8,11},{9,10},{10,... | collective-permute-start | bytes 589832 | tf_op jit(solution)/shard_map/ppermute | solution.py:341
  130.9 14.2 %collective-permute-start.35 = (f32[24,16,128]{2,1,0:T(8,128)S(1)}, f32[24,16,128]{2,1,0:T(8,128)S(1)}, u32[]{:S(2)}, u32[]{:S(2)}) collective-permute-start(f32[24,16,128]{2,1,0:T(8,128)S(1)} %get-tuple-element.202.refs_3_.refs_7_), channel_id=1, source_target_pairs={{0,4},{4,0},{8,12},{12,8},{16,20},{20,16},{24,28},{28,24},{1,5},{5... | collective-permute-start | bytes 589832 | tf_op jit(solution)/shard_map/ppermute | solution.py:337
  131.0 14.1 %collective-permute-start.36 = (f32[24,16,128]{2,1,0:T(8,128)S(1)}, f32[24,16,128]{2,1,0:T(8,128)S(1)}, u32[]{:S(2)}, u32[]{:S(2)}) collective-permute-start(f32[24,16,128]{2,1,0:T(8,128)S(1)} %get-tuple-element.203.refs_4_.refs_8_), channel_id=1, source_target_pairs={{0,28},{4,8},{8,4},{12,16},{16,12},{20,24},{24,20},{28,0},{1,29},{... | collective-permute-start | bytes 589832 | tf_op jit(solution)/shard_map/ppermute | solution.py:337
  133.1 11.2 %collective-permute-start.33 = (f32[128,128]{1,0:T(8,128)S(1)}, f32[128,128]{1,0:T(8,128)S(1)}, u32[]{:S(2)}, u32[]{:S(2)}) collective-permute-start(f32[128,128]{1,0:T(8,128)S(1)} %add.49), channel_id=1, source_target_pairs={{0,4},{4,0},{8,12},{12,8},{16,20},{20,16},{24,28},{28,24},{1,5},{5... | collective-permute-start | bytes 196616 | tf_op jit(solution)/shard_map/ppermute | solution.py:341
  138.8 22.3 %collective-permute-start.31 = (f32[24,16,128]{2,1,0:T(8,128)S(1)}, f32[24,16,128]{2,1,0:T(8,128)S(1)}, u32[]{:S(2)}, u32[]{:S(2)}) collective-permute-start(f32[24,16,128]{2,1,0:T(8,128)S(1)} %get-tuple-element.171.refs_3_), channel_id=1, source_target_pairs={{0,4},{4,0},{8,12},{12,8},{16,20},{20,16},{24,28},{28,24},{1,5},{5... | collective-permute-start | bytes 589832 | tf_op jit(solution)/shard_map/ppermute | solution.py:337
  144.3 16.8 %collective-permute-start.32 = (f32[24,16,128]{2,1,0:T(8,128)S(1)}, f32[24,16,128]{2,1,0:T(8,128)S(1)}, u32[]{:S(2)}, u32[]{:S(2)}) collective-permute-start(f32[24,16,128]{2,1,0:T(8,128)S(1)} %get-tuple-element.172.refs_4_), channel_id=1, source_target_pairs={{0,28},{4,8},{8,4},{12,16},{16,12},{20,24},{24,20},{28,0},{1,29},{... | collective-permute-start | bytes 589832 | tf_op jit(solution)/shard_map/ppermute | solution.py:337
  149.6 19.2 %collective-permute-start.43 = (f32[24,16,128]{2,1,0:T(8,128)S(1)}, f32[24,16,128]{2,1,0:T(8,128)S(1)}, u32[]{:S(2)}, u32[]{:S(2)}) collective-permute-start(f32[24,16,128]{2,1,0:T(8,128)S(1)} %get-tuple-element.187.refs_3_), channel_id=1, source_target_pairs={{0,4},{4,0},{8,12},{12,8},{16,20},{20,16},{24,28},{28,24},{1,5},{5... | collective-permute-start | bytes 589832 | tf_op jit(solution)/shard_map/ppermute | solution.py:337
  149.7 19.1 %collective-permute-start.44 = (f32[24,16,128]{2,1,0:T(8,128)S(1)}, f32[24,16,128]{2,1,0:T(8,128)S(1)}, u32[]{:S(2)}, u32[]{:S(2)}) collective-permute-start(f32[24,16,128]{2,1,0:T(8,128)S(1)} %get-tuple-element.188.refs_4_), channel_id=1, source_target_pairs={{0,28},{4,8},{8,4},{12,16},{16,12},{20,24},{24,20},{28,0},{1,29},{... | collective-permute-start | bytes 589832 | tf_op jit(solution)/shard_map/ppermute | solution.py:337
  158.2 10.6 %collective-permute-start.42 = (f32[128,128]{1,0:T(8,128)S(1)}, f32[128,128]{1,0:T(8,128)S(1)}, u32[]{:S(2)}, u32[]{:S(2)}) collective-permute-start(f32[128,128]{1,0:T(8,128)S(1)} %add.51), channel_id=1, source_target_pairs={{0,16},{4,20},{8,24},{12,28},{16,0},{20,4},{24,8},{28,12},{1,17},{... | collective-permute-start | bytes 196616 | tf_op jit(solution)/shard_map/ppermute | solution.py:341
  165.7 10.7 %collective-permute-start.40 = (f32[24,16,128]{2,1,0:T(8,128)S(1)}, f32[24,16,128]{2,1,0:T(8,128)S(1)}, u32[]{:S(2)}, u32[]{:S(2)}) collective-permute-start(f32[24,16,128]{2,1,0:T(8,128)S(1)} %get-tuple-element.193.refs_9_.refs_3_), channel_id=1, source_target_pairs={{0,4},{4,0},{8,12},{12,8},{16,20},{20,16},{24,28},{28,24},{1,5},{5... | collective-permute-start | bytes 589832 | tf_op jit(solution)/shard_map/ppermute | solution.py:337
  173.5 12.9 %collective-permute-start.45 = (f32[12,32,128]{2,1,0:T(8,128)S(1)}, f32[12,32,128]{2,1,0:T(8,128)S(1)}, u32[]{:S(2)}, u32[]{:S(2)}) collective-permute-start(f32[12,32,128]{2,1,0:T(8,128)S(1)} %get-tuple-element.205), channel_id=1, source_target_pairs={{0,1},{1,0},{2,3},{3,2},{4,5},{5,4},{6,7},{7,6},{8,9},{9,8},{10,11... | collective-permute-start | bytes 589832 | tf_op jit(solution)/shard_map/ppermute | solution.py:341
  173.6 12.8 %collective-permute-start.46 = (f32[12,32,128]{2,1,0:T(8,128)S(1)}, f32[12,32,128]{2,1,0:T(8,128)S(1)}, u32[]{:S(2)}, u32[]{:S(2)}) collective-permute-start(f32[12,32,128]{2,1,0:T(8,128)S(1)} %get-tuple-element.206), channel_id=1, source_target_pairs={{0,2},{1,3},{2,0},{3,1},{4,6},{5,7},{6,4},{7,5},{8,10},{9,11},{10,... | collective-permute-start | bytes 589832 | tf_op jit(solution)/shard_map/ppermute | solution.py:341
  176.4 22.4 %collective-permute-start.50 = (f32[24,16,128]{2,1,0:T(8,128)S(1)}, f32[24,16,128]{2,1,0:T(8,128)S(1)}, u32[]{:S(2)}, u32[]{:S(2)}) collective-permute-start(f32[24,16,128]{2,1,0:T(8,128)S(1)} %get-tuple-element.209.refs_3_), channel_id=1, source_target_pairs={{0,4},{4,0},{8,12},{12,8},{16,20},{20,16},{24,28},{28,24},{1,5},{5... | collective-permute-start | bytes 589832 | tf_op jit(solution)/shard_map/ppermute | solution.py:337
  177.1 21.7 %collective-permute-start.51 = (f32[24,16,128]{2,1,0:T(8,128)S(1)}, f32[24,16,128]{2,1,0:T(8,128)S(1)}, u32[]{:S(2)}, u32[]{:S(2)}) collective-permute-start(f32[24,16,128]{2,1,0:T(8,128)S(1)} %get-tuple-element.210.refs_4_), channel_id=1, source_target_pairs={{0,28},{4,8},{8,4},{12,16},{16,12},{20,24},{24,20},{28,0},{1,29},{... | collective-permute-start | bytes 589832 | tf_op jit(solution)/shard_map/ppermute | solution.py:337
  204.4 11.2 %collective-permute-start.55 = (f32[12,32,128]{2,1,0:T(8,128)S(1)}, f32[12,32,128]{2,1,0:T(8,128)S(1)}, u32[]{:S(2)}, u32[]{:S(2)}) collective-permute-start(f32[12,32,128]{2,1,0:T(8,128)S(1)} %get-tuple-element.219), channel_id=1, source_target_pairs={{0,1},{1,0},{2,3},{3,2},{4,5},{5,4},{6,7},{7,6},{8,9},{9,8},{10,11... | collective-permute-start | bytes 589832 | tf_op jit(solution)/shard_map/ppermute | solution.py:341
  204.5 11.1 %collective-permute-start.56 = (f32[12,32,128]{2,1,0:T(8,128)S(1)}, f32[12,32,128]{2,1,0:T(8,128)S(1)}, u32[]{:S(2)}, u32[]{:S(2)}) collective-permute-start(f32[12,32,128]{2,1,0:T(8,128)S(1)} %get-tuple-element.220), channel_id=1, source_target_pairs={{0,2},{1,3},{2,0},{3,1},{4,6},{5,7},{6,4},{7,5},{8,10},{9,11},{10,... | collective-permute-start | bytes 589832 | tf_op jit(solution)/shard_map/ppermute | solution.py:341
  204.7 11.0 %collective-permute-start.57 = (f32[12,32,128]{2,1,0:T(8,128)S(1)}, f32[12,32,128]{2,1,0:T(8,128)S(1)}, u32[]{:S(2)}, u32[]{:S(2)}) collective-permute-start(f32[12,32,128]{2,1,0:T(8,128)S(1)} %get-tuple-element.221), channel_id=1, source_target_pairs={{0,3},{1,2},{2,1},{3,0},{4,7},{5,6},{6,5},{7,4},{8,11},{9,10},{10,... | collective-permute-start | bytes 589832 | tf_op jit(solution)/shard_map/ppermute | solution.py:341
  236.3 13.0 %collective-permute-start.58 = (f32[12,32,128]{2,1,0:T(8,128)S(1)}, f32[12,32,128]{2,1,0:T(8,128)S(1)}, u32[]{:S(2)}, u32[]{:S(2)}) collective-permute-start(f32[12,32,128]{2,1,0:T(8,128)S(1)} %get-tuple-element.225), channel_id=1, source_target_pairs={{0,1},{1,0},{2,3},{3,2},{4,5},{5,4},{6,7},{7,6},{8,9},{9,8},{10,11... | collective-permute-start | bytes 589832 | tf_op jit(solution)/shard_map/ppermute | solution.py:341
  236.4 14.6 %collective-permute-start.59 = (f32[12,32,128]{2,1,0:T(8,128)S(1)}, f32[12,32,128]{2,1,0:T(8,128)S(1)}, u32[]{:S(2)}, u32[]{:S(2)}) collective-permute-start(f32[12,32,128]{2,1,0:T(8,128)S(1)} %get-tuple-element.226), channel_id=1, source_target_pairs={{0,2},{1,3},{2,0},{3,1},{4,6},{5,7},{6,4},{7,5},{8,10},{9,11},{10,... | collective-permute-start | bytes 589832 | tf_op jit(solution)/shard_map/ppermute | solution.py:341
  236.7 14.4 %collective-permute-start.60 = (f32[12,32,128]{2,1,0:T(8,128)S(1)}, f32[12,32,128]{2,1,0:T(8,128)S(1)}, u32[]{:S(2)}, u32[]{:S(2)}) collective-permute-start(f32[12,32,128]{2,1,0:T(8,128)S(1)} %get-tuple-element.227), channel_id=1, source_target_pairs={{0,3},{1,2},{2,1},{3,0},{4,7},{5,6},{6,5},{7,4},{8,11},{9,10},{10,... | collective-permute-start | bytes 589832 | tf_op jit(solution)/shard_map/ppermute | solution.py:341
  (20 other events, 123.9 us)

commit v6 on v5

--- a/solution.py
+++ b/solution.py
@@ -8,11 +8,9 @@
 from jax.sharding import PartitionSpec as P
 
 DEGREE = 4
-UNROLL = 48
+UNROLL = 72
 CHUNK = 24
 TURNS = 3
-TIE_HALO = 1
-TIE_IMAGE = 1
 APPLY_BYTES = 4 << 20
 F32, BF16, I32 = jnp.float32, jnp.bfloat16, jnp.int32
 precise = lax.Precision.HIGHEST
@@ -275,14 +273,12 @@
     g_ref[...] = total
 
 
-def turn_cross_kernel(ids_ref, inv_ref, f_ref, g_ref, first_ref, *refs):
+def turn_cross_kernel(ids_ref, inv_ref, f_ref, g_ref, *refs):
     parts, (k_ref, x_ref) = refs[:-2], refs[-2:]
     total = jnp.zeros(g_ref.shape, F32)
     for b in range(f_ref.shape[0]):
-        z = nn(inv_ref[...], gathered(ids_ref, parts, b, x_ref))
-        total = total + nt(f_ref[b], z)
-    k_ref[0] = first_ref[...]
-    k_ref[1] = half_width * total + center * g_ref[...]
+        total = total + nt(f_ref[b], gathered(ids_ref, parts, b, x_ref))
+    k_ref[...] = half_width * nt(total, inv_ref[...]) + center * g_ref[...]
 
 
 def basis_kernel(ids_ref, inv_ref, f_ref, *refs):
@@ -295,12 +291,12 @@
             part[b] = x_ref[b, pl.ds(pl.multiple_of((me ^ s) * each, each), each)]
 
 
-def proj_kernel(nodes, ids_ref, first_ref, last_ref, image_ref, *refs):
-    parts, x_ref = refs[:-1], refs[-1]
+def proj_kernel(nodes, ids_ref, *refs):
+    pairs, parts, x_ref = (refs[:2], refs[2:4]), refs[4:-1], refs[-1]
     each = parts[0].shape[1]
     me = ids_ref[1]
-    for i, inv_ref in enumerate((first_ref, last_ref)):
-        x_ref[...] = nt(nn(inv_ref[...], image_ref[i] * (1.0 / nodes)), inv_ref[...])
+    for i, (inv_ref, image_ref) in enumerate(pairs):
+        x_ref[...] = nt(nn(inv_ref[...], image_ref[...] * (1.0 / nodes)), inv_ref[...])
         for s, part in enumerate(parts):
             part[i] = x_ref[pl.ds(pl.multiple_of((me ^ s) * each, each), each)]
 
@@ -407,7 +403,7 @@
     halos = [exchange(panels) for panels in now]
     halos[0], gram = lax.optimization_barrier((halos[0], gram))
     inverse_first = inverse_factor(gram, nodes)
-    (cross_first,) = call(
+    (image_first,) = call(
         cross_kernel, "cross", [square], ids, panel, gram_first, *image, scalars=1, scratch=[held]
     )
     turned, gram_last = call(
@@ -418,20 +414,25 @@
     hops = hops_of("col", "node")
     for i, hop in enumerate(hops):
         got = swap(gram, *hop)
-        if i == TIE_HALO:
+        if i == 1:
             got, halos[1] = lax.optimization_barrier((got, halos[1]))
             _, parts = apply(meta, now[1], halos[1], (), first, count)
-            parts = swapped(parts)
-        if i == len(hops) - TIE_IMAGE:
-            got, parts = lax.optimization_barrier((got, parts))
+            (image_last,) = call(
+                turn_cross_kernel, "turn_cross", [square], ids, inverse_first, turned, gram_last,
+                *swapped(parts), scalars=1, scratch=[held],
+            )
+        if i == len(hops) - 2:
+            got, image_first = lax.optimization_barrier((got, image_first))
+        if i == len(hops) - 1:
+            got, image_last = lax.optimization_barrier((got, image_last))
         gram = gram + got
-    (images,) = call(
-        turn_cross_kernel, "turn_cross", [(2, vecs, vecs)], ids, inverse_first, turned, gram_last,
-        cross_first, *parts, scalars=1, scratch=[held],
-    )
-    for hop in hops_of("node"):
-        images = images + swap(images, *hop)
     inverse_last = inverse_factor(gram, nodes)
+    for i, hop in enumerate(hops_of("node")):
+        image_first = image_first + swap(image_first, *hop)
+        got = swap(image_last, *hop)
+        if i == 0:
+            got, image_last, _ = lax.optimization_barrier((got, image_last, inverse_last))
+        image_last = image_last + got
     parts = call(
         basis_kernel, "basis", [(quarter, cols_here, block)] * count, ids, inverse_last, turned,
         scalars=1, scratch=[held],
@@ -441,7 +442,7 @@
     )
     parts = call(
         functools.partial(proj_kernel, nodes), "proj", [(2, cols_here, vecs)] * count, ids,
-        inverse_first, inverse_last, images, scalars=1, scratch=[pltpu.VMEM(square, F32)],
+        inverse_first, image_first, inverse_last, image_last, scalars=1, scratch=[pltpu.VMEM(square, F32)],
     )
     projected = sum(swapped(parts))
     return basis, projected[0], projected[1]

time: 254 us -> 244 us (0.961)
  waiting for transfers between devices: 35.8 us -> 28.5 us
  Pallas kernels: 123 us -> 117 us
  starting transfers between devices: 91.6 us -> 95.5 us
    ppermute x31 -> x34, waiting for transfers between devices: 35.4 us -> 26.6 us  [swap(): lax.ppermute(value, axis, [(i, i ^ hop) for i in range(lax.axis_size(axis...]
    pallas_call x18, Pallas kernels: 83.4 us -> 78.2 us  [apply(): pl.pallas_call(functools.partial(apply_kernel, bool(old), bool(mate)), in...]
    ppermute x18, starting transfers between devices: 10.8 us -> 14.4 us  [exchange(): lax.ppermute(pair[0], 'node', even)]
    ppermute x31 -> x34, starting transfers between devices: 20.8 us -> 24.1 us  [swap(): lax.ppermute(value, axis, [(i, i ^ hop) for i in range(lax.axis_size(axis...]
    ppermute x18, starting transfers between devices: 60 us -> 56.9 us  [exchange(): lax.ppermute(pair[1], 'node', odd)]
  transfers between devices with their start and end apart: 67 -> 70, of which waited for: 12 -> 14; matrix products, arithmetic and copies ran while one was open for 0% -> 0% of each run, Pallas kernels for 45% -> 48%
where the time goes in v6:
time: 244 us
  Pallas kernels  117 us (48%)
  starting transfers between devices  95.5 us (39%)
  waiting for transfers between devices  28.5 us (12%)
    pallas_call x18, Pallas kernels, apply(): pl.pallas_call(functools.partial(apply_kernel, bool(old), bool(mate)), in...  78.2 us
    ppermute x18, starting transfers between devices, exchange(): lax.ppermute(pair[1], 'node', odd)  56.9 us
    pallas_call x10, Pallas kernels, call(): pl.pallas_call(kernel, in_specs=[IN_SMEM] * scalars + [IN_VMEM] * (len(ar...  29.8 us
    ppermute x34, waiting for transfers between devices, swap(): lax.ppermute(value, axis, [(i, i ^ hop) for i in range(lax.axis_size(axis...  26.6 us
    ppermute x34, starting transfers between devices, swap(): lax.ppermute(value, axis, [(i, i ^ hop) for i in range(lax.axis_size(axis...  24.1 us
    ppermute x18, starting transfers between devices, exchange(): lax.ppermute(pair[0], 'node', even)  14.4 us
    pallas_call x1, Pallas kernels, prep(): pl.pallas_call(functools.partial(prep_kernel, rows), in_specs=[IN_SMEM] *...  8.93 us
  transfers between devices with their start and end apart: 70, of which 14 were waited for; matrix products, arithmetic and copies ran while one was open for 0% of the time, Pallas kernels for 48%

profile of v6, /device:TPU:0, one launch (start us, length us, event | category | flops | bytes accessed | tf_op | source)
XLA Modules:
  0.0 244.1 jit_solution(2896407030496194503)
XLA Ops:
  2.5 3.0 %collective-permute-start = (f32[24,16,128]{2,1,0:T(8,128)S(1)}, f32[24,16,128]{2,1,0:T(8,128)S(1)}, u32[]{:S(2)}, u32[]{:S(2)}) collective-permute-start(f32[24,16,128]{2,1,0:T(8,128)S(1)} %get-tuple-element.126.refs_3_.refs_7_), channel_id=1, source_target_pairs={{0,4},{4,0},{8,12},{12,8},{16,20},{20,16},{24,28},{28,24},{1,5},{5... | collective-permute-start | bytes 589832 | tf_op jit(solution)/shard_map/ppermute | solution.py:333
  5.5 3.5 %collective-permute-start.1 = (f32[24,16,128]{2,1,0:T(8,128)S(1)}, f32[24,16,128]{2,1,0:T(8,128)S(1)}, u32[]{:S(2)}, u32[]{:S(2)}) collective-permute-start(f32[24,16,128]{2,1,0:T(8,128)S(1)} %get-tuple-element.127.refs_4_.refs_8_), channel_id=1, source_target_pairs={{0,28},{4,8},{8,4},{12,16},{16,12},{20,24},{24,20},{28,0},{1,29},{... | collective-permute-start | bytes 589832 | tf_op jit(solution)/shard_map/ppermute | solution.py:333
  11.0 8.9 %prep.1 = (bf16[288,128,256]{2,1,0:T(8,128)(2,1)S(1)}, f32[48,1,128]{2,1,0:T(1,128)S(1)}, s32[578]{0:T(1024)S(1)}) custom-call(s32[2]{0:T(128)S(1)} %pad_add_fusion.ids_ref, s32[1,288]{1,0:T(1,128)} %own_ref.1, s32[1,288]{1,0:T(1,128)} %col_ref.1, f32[288,128,128]{2,1,0:T(8,128)} %blk_ref.1), custom_call_target="tpu_custom_call" | custom-call | flops 1207959552 | bytes 18874368 | tf_op jit(solution)/shard_map/prep/pallas_call | solution.py:115
  20.0 4.2 %apply.4 = (f32[24,16,128]{2,1,0:T(8,128)S(1)}, f32[24,16,128]{2,1,0:T(8,128)S(1)}) custom-call(s32[578]{0:T(1024)S(1)} %get-tuple-element.123.refs_0_, bf16[288,128,256]{2,1,0:T(8,128)(2,1)S(1)} %get-tuple-element.124.refs_1_, f32[48,1,128]{2,1,0:T(1,128)S(1)} %get-tuple-element.125.refs_2_, f32[24,16,128]{2,1,0:T(8,128)S(1)} %get-tuple-element.126.refs_3_.refs_7_, ...), custom_call_target="tpu_custom_call" | custom-call | bytes 4194304 | tf_op jit(solution)/shard_map/apply/pallas_call | solution.py:194
  26.0 3.6 %collective-permute-start.3 = (f32[24,16,128]{2,1,0:T(8,128)S(1)}, f32[24,16,128]{2,1,0:T(8,128)S(1)}, u32[]{:S(2)}, u32[]{:S(2)}) collective-permute-start(f32[24,16,128]{2,1,0:T(8,128)S(1)} %get-tuple-element.129.refs_4_.refs_8_), channel_id=1, source_target_pairs={{0,28},{4,8},{8,4},{12,16},{16,12},{20,24},{24,20},{28,0},{1,29},{... | collective-permute-start | bytes 589832 | tf_op jit(solution)/shard_map/ppermute | solution.py:333
  29.6 4.2 %apply.6 = (f32[24,16,128]{2,1,0:T(8,128)S(1)}, f32[24,16,128]{2,1,0:T(8,128)S(1)}) custom-call(s32[578]{0:T(1024)S(1)} %get-tuple-element.123.refs_0_, bf16[288,128,256]{2,1,0:T(8,128)(2,1)S(1)} %get-tuple-element.124.refs_1_, f32[48,1,128]{2,1,0:T(1,128)S(1)} %get-tuple-element.125.refs_2_, f32[24,16,128]{2,1,0:T(8,128)S(1)} %get-tuple-element.138.refs_3_.refs_7_, ...), custom_call_target="tpu_custom_call" | custom-call | bytes 4194304 | tf_op jit(solution)/shard_map/apply/pallas_call | solution.py:194
  33.9 1.9 collective-permute-start.15
  35.9 4.3 %apply_recur.10 = (f32[24,16,128]{2,1,0:T(8,128)S(1)}, f32[24,16,128]{2,1,0:T(8,128)S(1)}) custom-call(s32[578]{0:T(1024)S(1)} %get-tuple-element.123.refs_0_, bf16[288,128,256]{2,1,0:T(8,128)(2,1)S(1)} %get-tuple-element.124.refs_1_, f32[48,1,128]{2,1,0:T(1,128)S(1)} %get-tuple-element.125.refs_2_, f32[24,16,128]{2,1,0:T(8,128)S(1)} %get-tuple-element.128.refs_3_.refs_7_, ...), custom_call_target="tpu_custom_call" | custom-call | bytes 4194304 | tf_op jit(solution)/shard_map/apply_recur/pallas_call | solution.py:194
  40.8 8.2 %collective-permute-start.5 = (f32[24,16,128]{2,1,0:T(8,128)S(1)}, f32[24,16,128]{2,1,0:T(8,128)S(1)}, u32[]{:S(2)}, u32[]{:S(2)}) collective-permute-start(f32[24,16,128]{2,1,0:T(8,128)S(1)} %get-tuple-element.131.refs_4_.refs_8_), channel_id=1, source_target_pairs={{0,28},{4,8},{8,4},{12,16},{16,12},{20,24},{24,20},{28,0},{1,29},{... | collective-permute-start | bytes 589832 | tf_op jit(solution)/shard_map/ppermute | solution.py:333
  49.0 4.3 %apply_recur.13 = (f32[24,16,128]{2,1,0:T(8,128)S(1)}, f32[24,16,128]{2,1,0:T(8,128)S(1)}) custom-call(s32[578]{0:T(1024)S(1)} %get-tuple-element.123.refs_0_, bf16[288,128,256]{2,1,0:T(8,128)(2,1)S(1)} %get-tuple-element.124.refs_1_, f32[48,1,128]{2,1,0:T(1,128)S(1)} %get-tuple-element.125.refs_2_, f32[24,16,128]{2,1,0:T(8,128)S(1)} %get-tuple-element.140.refs_3_.refs_7_, ...), custom_call_target="tpu_custom_call" | custom-call | bytes 4194304 | tf_op jit(solution)/shard_map/apply_recur/pallas_call | solution.py:194
  53.4 2.0 collective-permute-start.17
  55.3 4.2 %apply_recur.11 = (f32[24,16,128]{2,1,0:T(8,128)S(1)}, f32[24,16,128]{2,1,0:T(8,128)S(1)}) custom-call(s32[578]{0:T(1024)S(1)} %get-tuple-element.123.refs_0_, bf16[288,128,256]{2,1,0:T(8,128)(2,1)S(1)} %get-tuple-element.124.refs_1_, f32[48,1,128]{2,1,0:T(1,128)S(1)} %get-tuple-element.125.refs_2_, f32[24,16,128]{2,1,0:T(8,128)S(1)} %get-tuple-element.130.refs_3_.refs_7_, ...), custom_call_target="tpu_custom_call" | custom-call | bytes 4194304 | tf_op jit(solution)/shard_map/apply_recur/pallas_call | solution.py:194
  59.7 2.9 %collective-permute-start.7 = (f32[24,16,128]{2,1,0:T(8,128)S(1)}, f32[24,16,128]{2,1,0:T(8,128)S(1)}, u32[]{:S(2)}, u32[]{:S(2)}) collective-permute-start(f32[24,16,128]{2,1,0:T(8,128)S(1)} %get-tuple-element.133.refs_4_), channel_id=1, source_target_pairs={{0,28},{4,8},{8,4},{12,16},{16,12},{20,24},{24,20},{28,0},{1,29},{... | collective-permute-start | bytes 589832 | tf_op jit(solution)/shard_map/ppermute | solution.py:333
  62.7 4.3 %apply_recur.14 = (f32[24,16,128]{2,1,0:T(8,128)S(1)}, f32[24,16,128]{2,1,0:T(8,128)S(1)}) custom-call(s32[578]{0:T(1024)S(1)} %get-tuple-element.123.refs_0_, bf16[288,128,256]{2,1,0:T(8,128)(2,1)S(1)} %get-tuple-element.124.refs_1_, f32[48,1,128]{2,1,0:T(1,128)S(1)} %get-tuple-element.125.refs_2_, f32[24,16,128]{2,1,0:T(8,128)S(1)} %get-tuple-element.142.refs_3_.refs_7_, ...), custom_call_target="tpu_custom_call" | custom-call | bytes 4194304 | tf_op jit(solution)/shard_map/apply_recur/pallas_call | solution.py:194
  68.0 4.9 %collective-permute-start.19 = (f32[24,16,128]{2,1,0:T(8,128)S(1)}, f32[24,16,128]{2,1,0:T(8,128)S(1)}, u32[]{:S(2)}, u32[]{:S(2)}) collective-permute-start(f32[24,16,128]{2,1,0:T(8,128)S(1)} %get-tuple-element.145.refs_4_), channel_id=1, source_target_pairs={{0,28},{4,8},{8,4},{12,16},{16,12},{20,24},{24,20},{28,0},{1,29},{... | collective-permute-start | bytes 589832 | tf_op jit(solution)/shard_map/ppermute | solution.py:333
  72.9 4.2 %apply_recur.12 = (f32[24,16,128]{2,1,0:T(8,128)S(1)}, f32[24,16,128]{2,1,0:T(8,128)S(1)}) custom-call(s32[578]{0:T(1024)S(1)} %get-tuple-element.123.refs_0_, bf16[288,128,256]{2,1,0:T(8,128)(2,1)S(1)} %get-tuple-element.124.refs_1_, f32[48,1,128]{2,1,0:T(1,128)S(1)} %get-tuple-element.125.refs_2_, f32[24,16,128]{2,1,0:T(8,128)S(1)} %get-tuple-element.132.refs_3_, ...), custom_call_target="tpu_custom_call" | custom-call | bytes 4194304 | tf_op jit(solution)/shard_map/apply_recur/pallas_call | solution.py:194
  77.2 2.0 collective-permute-start.9
  79.2 4.4 %apply_recur_parts.2 = (f32[24,16,128]{2,1,0:T(8,128)S(1)}, f32[24,16,128]{2,1,0:T(8,128)S(1)}, f32[12,32,128]{2,1,0:T(8,128)S(1)}, f32[12,32,128]{2,1,0:T(8,128...) custom-call(s32[578]{0:T(1024)S(1)} %get-tuple-element.123.refs_0_, ...), custom_call_target="tpu_custom_call" | custom-call | bytes 4194304 | tf_op jit(solution)/shard_map/apply_recur_parts/pallas_call | solution.py:194
  83.7 9.5 %collective-permute-start.28 = (f32[24,16,128]{2,1,0:T(8,128)S(1)}, f32[24,16,128]{2,1,0:T(8,128)S(1)}, u32[]{:S(2)}, u32[]{:S(2)}) collective-permute-start(f32[24,16,128]{2,1,0:T(8,128)S(1)} %get-tuple-element.165.refs_4_.refs_8_), channel_id=1, source_target_pairs={{0,28},{4,8},{8,4},{12,16},{16,12},{20,24},{24,20},{28,0},{1,29},{... | collective-permute-start | bytes 589832 | tf_op jit(solution)/shard_map/ppermute | solution.py:333
  95.1 4.2 %apply.5 = (f32[24,16,128]{2,1,0:T(8,128)S(1)}, f32[24,16,128]{2,1,0:T(8,128)S(1)}) custom-call(s32[578]{0:T(1024)S(1)} %get-tuple-element.123.refs_0_, bf16[288,128,256]{2,1,0:T(8,128)(2,1)S(1)} %get-tuple-element.124.refs_1_, f32[48,1,128]{2,1,0:T(1,128)S(1)} %get-tuple-element.125.refs_2_, f32[24,16,128]{2,1,0:T(8,128)S(1)} %get-tuple-element.151.refs_3_.refs_9_.refs_7_, ...), custom_call_target="tpu_custom_call" | custom-call | bytes 4194304 | tf_op jit(solution)/shard_map/apply/pallas_call | solution.py:194
  99.4 2.1 collective-permute-start.11
  101.6 4.5 %apply_parts.2 = (f32[24,16,128]{2,1,0:T(8,128)S(1)}, f32[24,16,128]{2,1,0:T(8,128)S(1)}, f32[12,32,128]{2,1,0:T(8,128)S(1)}, f32[12,32,128]{2,1,0:T(8,128)S(1)}...) custom-call(s32[578]{0:T(1024)S(1)} %get-tuple-element.123.refs_0_, ...), custom_call_target="tpu_custom_call" | custom-call | bytes 4194304 | tf_op jit(solution)/shard_map/apply_parts/pallas_call | solution.py:194
  106.3 2.7 %collective-permute-start.30 = (f32[24,16,128]{2,1,0:T(8,128)S(1)}, f32[24,16,128]{2,1,0:T(8,128)S(1)}, u32[]{:S(2)}, u32[]{:S(2)}) collective-permute-start(f32[24,16,128]{2,1,0:T(8,128)S(1)} %get-tuple-element.187.refs_4_.refs_8_), channel_id=1, source_target_pairs={{0,28},{4,8},{8,4},{12,16},{16,12},{20,24},{24,20},{28,0},{1,29},{... | collective-permute-start | bytes 589832 | tf_op jit(solution)/shard_map/ppermute | solution.py:333
  109.0 2.0 gram.1
  111.4 4.3 %apply_recur.15 = (f32[24,16,128]{2,1,0:T(8,128)S(1)}, f32[24,16,128]{2,1,0:T(8,128)S(1)}) custom-call(s32[578]{0:T(1024)S(1)} %get-tuple-element.123.refs_0_, bf16[288,128,256]{2,1,0:T(8,128)(2,1)S(1)} %get-tuple-element.124.refs_1_, f32[48,1,128]{2,1,0:T(1,128)S(1)} %get-tuple-element.125.refs_2_, f32[24,16,128]{2,1,0:T(8,128)S(1)} %get-tuple-element.170.refs_3_.refs_7_, ...), custom_call_target="tpu_custom_call" | custom-call | bytes 4194304 | tf_op jit(solution)/shard_map/apply_recur/pallas_call | solution.py:194
  121.3 4.2 %apply_recur.16 = (f32[24,16,128]{2,1,0:T(8,128)S(1)}, f32[24,16,128]{2,1,0:T(8,128)S(1)}) custom-call(s32[578]{0:T(1024)S(1)} %get-tuple-element.123.refs_0_, bf16[288,128,256]{2,1,0:T(8,128)(2,1)S(1)} %get-tuple-element.124.refs_1_, f32[48,1,128]{2,1,0:T(1,128)S(1)} %get-tuple-element.125.refs_2_, f32[24,16,128]{2,1,0:T(8,128)S(1)} %get-tuple-element.186.refs_3_.refs_7_, ...), custom_call_target="tpu_custom_call" | custom-call | bytes 4194304 | tf_op jit(solution)/shard_map/apply_recur/pallas_call | solution.py:194
  129.5 4.3 %apply_recur.17 = (f32[24,16,128]{2,1,0:T(8,128)S(1)}, f32[24,16,128]{2,1,0:T(8,128)S(1)}) custom-call(s32[578]{0:T(1024)S(1)} %get-tuple-element.123.refs_0_, bf16[288,128,256]{2,1,0:T(8,128)(2,1)S(1)} %get-tuple-element.124.refs_1_, f32[48,1,128]{2,1,0:T(1,128)S(1)} %get-tuple-element.125.refs_2_, f32[24,16,128]{2,1,0:T(8,128)S(1)} %get-tuple-element.192.refs_3_.refs_7_, ...), custom_call_target="tpu_custom_call" | custom-call | bytes 4194304 | tf_op jit(solution)/shard_map/apply_recur/pallas_call | solution.py:194
  133.8 2.0 collective-permute-start.31
  135.8 3.0 %collective-permute-done.33 = f32[128,128]{1,0:T(8,128)S(1)} collective-permute-done((f32[128,128]{1,0:T(8,128)S(1)}, f32[128,128]{1,0:T(8,128)S(1)}, u32[]{:S(2)}, u32[]{:S(2)}) %collective-permute-start.33) | collective-permute-done | bytes 65568 | tf_op jit(solution)/shard_map/ppermute | solution.py:337
  138.8 2.9 %collective-permute-start.32 = (f32[24,16,128]{2,1,0:T(8,128)S(1)}, f32[24,16,128]{2,1,0:T(8,128)S(1)}, u32[]{:S(2)}, u32[]{:S(2)}) collective-permute-start(f32[24,16,128]{2,1,0:T(8,128)S(1)} %get-tuple-element.173.refs_4_), channel_id=1, source_target_pairs={{0,28},{4,8},{8,4},{12,16},{16,12},{20,24},{24,20},{28,0},{1,29},{... | collective-permute-start | bytes 589832 | tf_op jit(solution)/shard_map/ppermute | solution.py:333
  141.8 4.3 %apply_recur.18 = (f32[24,16,128]{2,1,0:T(8,128)S(1)}, f32[24,16,128]{2,1,0:T(8,128)S(1)}) custom-call(s32[578]{0:T(1024)S(1)} %get-tuple-element.123.refs_0_, bf16[288,128,256]{2,1,0:T(8,128)(2,1)S(1)} %get-tuple-element.124.refs_1_, f32[48,1,128]{2,1,0:T(1,128)S(1)} %get-tuple-element.125.refs_2_, f32[24,16,128]{2,1,0:T(8,128)S(1)} %get-tuple-element.203.refs_3_.refs_7_, ...), custom_call_target="tpu_custom_call" | custom-call | bytes 4194304 | tf_op jit(solution)/shard_map/apply_recur/pallas_call | solution.py:194
  149.7 6.1 %collective-permute-done.34 = f32[128,128]{1,0:T(8,128)S(1)} collective-permute-done((f32[128,128]{1,0:T(8,128)S(1)}, f32[128,128]{1,0:T(8,128)S(1)}, u32[]{:S(2)}, u32[]{:S(2)}) %collective-permute-start.34) | collective-permute-done | bytes 65568 | tf_op jit(solution)/shard_map/ppermute | solution.py:337
  156.2 4.2 %apply_recur.19 = (f32[24,16,128]{2,1,0:T(8,128)S(1)}, f32[24,16,128]{2,1,0:T(8,128)S(1)}) custom-call(s32[578]{0:T(1024)S(1)} %get-tuple-element.123.refs_0_, bf16[288,128,256]{2,1,0:T(8,128)(2,1)S(1)} %get-tuple-element.124.refs_1_, f32[48,1,128]{2,1,0:T(1,128)S(1)} %get-tuple-element.125.refs_2_, f32[24,16,128]{2,1,0:T(8,128)S(1)} %get-tuple-element.172.refs_3_, ...), custom_call_target="tpu_custom_call" | custom-call | bytes 4194304 | tf_op jit(solution)/shard_map/apply_recur/pallas_call | solution.py:194
  160.5 2.5 %collective-permute-start.40 = (f32[24,16,128]{2,1,0:T(8,128)S(1)}, f32[24,16,128]{2,1,0:T(8,128)S(1)}, u32[]{:S(2)}, u32[]{:S(2)}) collective-permute-start(f32[24,16,128]{2,1,0:T(8,128)S(1)} %get-tuple-element.194.refs_9_.refs_3_), channel_id=1, source_target_pairs={{0,4},{4,0},{8,12},{12,8},{16,20},{20,16},{24,28},{28,24},{1,5},{5... | collective-permute-start | bytes 589832 | tf_op jit(solution)/shard_map/ppermute | solution.py:333
  164.6 4.6 %apply_recur_parts.3 = (f32[24,16,128]{2,1,0:T(8,128)S(1)}, f32[24,16,128]{2,1,0:T(8,128)S(1)}, f32[12,32,128]{2,1,0:T(8,128)S(1)}, f32[12,32,128]{2,1,0:T(8,128...) custom-call(s32[578]{0:T(1024)S(1)} %get-tuple-element.123.refs_0_, ...), custom_call_target="tpu_custom_call" | custom-call | bytes 4194304 | tf_op jit(solution)/shard_map/apply_recur_parts/pallas_call | solution.py:194
  174.7 7.1 %factor.2.inv_ref.refs_0_ = f32[128,128]{1,0:T(8,128)S(1)} custom-call(f32[128,128]{1,0:T(8,128)S(1)} %add.61.g_ref), custom_call_target="tpu_custom_call" | custom-call | tf_op jit(solution)/shard_map/factor/pallas_call | solution.py:41
  181.9 4.0 %turn.1 = (f32[12,128,128]{2,1,0:T(8,128)S(1)}, f32[128,128]{1,0:T(8,128)S(1)}) custom-call(s32[2]{0:T(128)S(1)} %pad_add_fusion.ids_ref, f32[128,128]{1,0:T(8,128)S(1)} %factor.2.inv_ref.refs_0_, f32[12,32,128]{2,1,0:T(8,128)S(1)} %get-tuple-element.205.refs_0_, f32[12,32,128]{2,1,0:T(8,128)S(1)} %collective-permute-done.45.refs_1_, ...), custom_call_target="tpu_custom_call" | custom-call | tf_op jit(solution)/shard_map/turn/pallas_call | solution.py:41
  187.9 4.2 %apply.7 = (f32[24,16,128]{2,1,0:T(8,128)S(1)}, f32[24,16,128]{2,1,0:T(8,128)S(1)}) custom-call(s32[578]{0:T(1024)S(1)} %get-tuple-element.123.refs_0_, bf16[288,128,256]{2,1,0:T(8,128)(2,1)S(1)} %get-tuple-element.124.refs_1_, f32[48,1,128]{2,1,0:T(1,128)S(1)} %get-tuple-element.125.refs_2_, f32[24,16,128]{2,1,0:T(8,128)S(1)} %get-tuple-element.194.refs_9_.refs_3_, ...), custom_call_target="tpu_custom_call" | custom-call | bytes 4194304 | tf_op jit(solution)/shard_map/apply/pallas_call | solution.py:194
  192.2 5.3 %apply_parts.3 = (f32[24,16,128]{2,1,0:T(8,128)}, f32[24,16,128]{2,1,0:T(8,128)}, f32[12,32,128]{2,1,0:T(8,128)S(1)}, f32[12,32,128]{2,1,0:T(8,128)S(1)}, f32[12...) custom-call(s32[578]{0:T(1024)S(1)} %get-tuple-element.123.refs_0_, ...), custom_call_target="tpu_custom_call" | custom-call | bytes 4194304 | tf_op jit(solution)/shard_map/apply_parts/pallas_call | solution.py:194
  199.9 2.2 cross.1
  203.8 2.0 collective-permute-start.54
  205.9 2.7 %collective-permute-done.57.refs_3_ = f32[12,32,128]{2,1,0:T(8,128)S(1)} collective-permute-done((f32[12,32,128]{2,1,0:T(8,128)S(1)}, f32[12,32,128]{2,1,0:T(8,128)S(1)}, u32[]{:S(2)}, u32[]{:S(2)}) %collective-permute-start.57) | collective-permute-done | bytes 196640 | tf_op jit(solution)/shard_map/ppermute | solution.py:337
  208.7 2.7 %turn_cross.1 = f32[128,128]{1,0:T(8,128)S(1)} custom-call(s32[2]{0:T(128)S(1)} %pad_add_fusion.ids_ref, f32[128,128]{1,0:T(8,128)S(1)} %factor.2.inv_ref.refs_0_, f32[12,128,128]{2,1,0:T(8,128)S(1)} %get-tuple-element.219.f_ref, f32[128,128]{1,0:T(8,128)S(1)} %get-tuple-element.209.g_ref, f32[12,32,128]{2,1,0:T(8,128)S(1)} %get-tuple-element.226.refs_0_, ...), custom_call_target="tpu_custom_call" | custom-call | tf_op jit(solution)/shard_map/turn_cross/pallas_call | solution.py:41
  211.4 2.1 collective-permute-start.64
  213.5 7.1 %factor.3.inv_ref.refs_2_ = f32[128,128]{1,0:T(8,128)S(1)} custom-call(f32[128,128]{1,0:T(8,128)S(1)} %add.66.g_ref), custom_call_target="tpu_custom_call" | custom-call | tf_op jit(solution)/shard_map/factor/pallas_call | solution.py:41
  226.1 2.8 %collective-permute-done.62 = f32[128,128]{1,0:T(8,128)S(1)} collective-permute-done((f32[128,128]{1,0:T(8,128)S(1)}, f32[128,128]{1,0:T(8,128)S(1)}, u32[]{:S(2)}, u32[]{:S(2)}) %collective-permute-start.62) | collective-permute-done | bytes 65568 | tf_op jit(solution)/shard_map/ppermute | solution.py:337
  229.9 2.0 collective-permute-start.66
  231.9 4.6 %collective-permute-done.63 = f32[128,128]{1,0:T(8,128)S(1)} collective-permute-done((f32[128,128]{1,0:T(8,128)S(1)}, f32[128,128]{1,0:T(8,128)S(1)}, u32[]{:S(2)}, u32[]{:S(2)}) %collective-permute-start.63) | collective-permute-done | bytes 65568 | tf_op jit(solution)/shard_map/ppermute | solution.py:337
  (142 shorter events, 51.6 us)
Async XLA Ops:
  2.5 17.4 %collective-permute-start = (f32[24,16,128]{2,1,0:T(8,128)S(1)}, f32[24,16,128]{2,1,0:T(8,128)S(1)}, u32[]{:S(2)}, u32[]{:S(2)}) collective-permute-start(f32[24,16,128]{2,1,0:T(8,128)S(1)} %get-tuple-element.126.refs_3_.refs_7_), channel_id=1, source_target_pairs={{0,4},{4,0},{8,12},{12,8},{16,20},{20,16},{24,28},{28,24},{1,5},{5... | collective-permute-start | bytes 589832 | tf_op jit(solution)/shard_map/ppermute | solution.py:333
  5.5 14.4 %collective-permute-start.1 = (f32[24,16,128]{2,1,0:T(8,128)S(1)}, f32[24,16,128]{2,1,0:T(8,128)S(1)}, u32[]{:S(2)}, u32[]{:S(2)}) collective-permute-start(f32[24,16,128]{2,1,0:T(8,128)S(1)} %get-tuple-element.127.refs_4_.refs_8_), channel_id=1, source_target_pairs={{0,28},{4,8},{8,4},{12,16},{16,12},{20,24},{24,20},{28,0},{1,29},{... | collective-permute-start | bytes 589832 | tf_op jit(solution)/shard_map/ppermute | solution.py:333
  9.1 20.5 %collective-permute-start.12 = (f32[24,16,128]{2,1,0:T(8,128)S(1)}, f32[24,16,128]{2,1,0:T(8,128)S(1)}, u32[]{:S(2)}, u32[]{:S(2)}) collective-permute-start(f32[24,16,128]{2,1,0:T(8,128)S(1)} %get-tuple-element.138.refs_3_.refs_7_), channel_id=1, source_target_pairs={{0,4},{4,0},{8,12},{12,8},{16,20},{20,16},{24,28},{28,24},{1,5},{5... | collective-permute-start | bytes 589832 | tf_op jit(solution)/shard_map/ppermute | solution.py:333
  9.1 20.5 %collective-permute-start.13 = (f32[24,16,128]{2,1,0:T(8,128)S(1)}, f32[24,16,128]{2,1,0:T(8,128)S(1)}, u32[]{:S(2)}, u32[]{:S(2)}) collective-permute-start(f32[24,16,128]{2,1,0:T(8,128)S(1)} %get-tuple-element.139.refs_4_.refs_8_), channel_id=1, source_target_pairs={{0,28},{4,8},{8,4},{12,16},{16,12},{20,24},{24,20},{28,0},{1,29},{... | collective-permute-start | bytes 589832 | tf_op jit(solution)/shard_map/ppermute | solution.py:333
  24.2 11.7 %collective-permute-start.2 = (f32[24,16,128]{2,1,0:T(8,128)S(1)}, f32[24,16,128]{2,1,0:T(8,128)S(1)}, u32[]{:S(2)}, u32[]{:S(2)}) collective-permute-start(f32[24,16,128]{2,1,0:T(8,128)S(1)} %get-tuple-element.128.refs_3_.refs_7_), channel_id=1, source_target_pairs={{0,4},{4,0},{8,12},{12,8},{16,20},{20,16},{24,28},{28,24},{1,5},{5... | collective-permute-start | bytes 589832 | tf_op jit(solution)/shard_map/ppermute | solution.py:333
  26.0 9.8 %collective-permute-start.3 = (f32[24,16,128]{2,1,0:T(8,128)S(1)}, f32[24,16,128]{2,1,0:T(8,128)S(1)}, u32[]{:S(2)}, u32[]{:S(2)}) collective-permute-start(f32[24,16,128]{2,1,0:T(8,128)S(1)} %get-tuple-element.129.refs_4_.refs_8_), channel_id=1, source_target_pairs={{0,28},{4,8},{8,4},{12,16},{16,12},{20,24},{24,20},{28,0},{1,29},{... | collective-permute-start | bytes 589832 | tf_op jit(solution)/shard_map/ppermute | solution.py:333
  33.9 15.2 %collective-permute-start.14 = (f32[24,16,128]{2,1,0:T(8,128)S(1)}, f32[24,16,128]{2,1,0:T(8,128)S(1)}, u32[]{:S(2)}, u32[]{:S(2)}) collective-permute-start(f32[24,16,128]{2,1,0:T(8,128)S(1)} %get-tuple-element.140.refs_3_.refs_7_), channel_id=1, source_target_pairs={{0,4},{4,0},{8,12},{12,8},{16,20},{20,16},{24,28},{28,24},{1,5},{5... | collective-permute-start | bytes 589832 | tf_op jit(solution)/shard_map/ppermute | solution.py:333
  33.9 15.1 %collective-permute-start.15 = (f32[24,16,128]{2,1,0:T(8,128)S(1)}, f32[24,16,128]{2,1,0:T(8,128)S(1)}, u32[]{:S(2)}, u32[]{:S(2)}) collective-permute-start(f32[24,16,128]{2,1,0:T(8,128)S(1)} %get-tuple-element.141.refs_4_.refs_8_), channel_id=1, source_target_pairs={{0,28},{4,8},{8,4},{12,16},{16,12},{20,24},{24,20},{28,0},{1,29},{... | collective-permute-start | bytes 589832 | tf_op jit(solution)/shard_map/ppermute | solution.py:333
  40.1 15.2 %collective-permute-start.4 = (f32[24,16,128]{2,1,0:T(8,128)S(1)}, f32[24,16,128]{2,1,0:T(8,128)S(1)}, u32[]{:S(2)}, u32[]{:S(2)}) collective-permute-start(f32[24,16,128]{2,1,0:T(8,128)S(1)} %get-tuple-element.130.refs_3_.refs_7_), channel_id=1, source_target_pairs={{0,4},{4,0},{8,12},{12,8},{16,20},{20,16},{24,28},{28,24},{1,5},{5... | collective-permute-start | bytes 589832 | tf_op jit(solution)/shard_map/ppermute | solution.py:333
  40.8 14.5 %collective-permute-start.5 = (f32[24,16,128]{2,1,0:T(8,128)S(1)}, f32[24,16,128]{2,1,0:T(8,128)S(1)}, u32[]{:S(2)}, u32[]{:S(2)}) collective-permute-start(f32[24,16,128]{2,1,0:T(8,128)S(1)} %get-tuple-element.131.refs_4_.refs_8_), channel_id=1, source_target_pairs={{0,28},{4,8},{8,4},{12,16},{16,12},{20,24},{24,20},{28,0},{1,29},{... | collective-permute-start | bytes 589832 | tf_op jit(solution)/shard_map/ppermute | solution.py:333
  59.6 13.3 %collective-permute-start.6 = (f32[24,16,128]{2,1,0:T(8,128)S(1)}, f32[24,16,128]{2,1,0:T(8,128)S(1)}, u32[]{:S(2)}, u32[]{:S(2)}) collective-permute-start(f32[24,16,128]{2,1,0:T(8,128)S(1)} %get-tuple-element.132.refs_3_), channel_id=1, source_target_pairs={{0,4},{4,0},{8,12},{12,8},{16,20},{20,16},{24,28},{28,24},{1,5},{5... | collective-permute-start | bytes 589832 | tf_op jit(solution)/shard_map/ppermute | solution.py:333
  59.7 13.2 %collective-permute-start.7 = (f32[24,16,128]{2,1,0:T(8,128)S(1)}, f32[24,16,128]{2,1,0:T(8,128)S(1)}, u32[]{:S(2)}, u32[]{:S(2)}) collective-permute-start(f32[24,16,128]{2,1,0:T(8,128)S(1)} %get-tuple-element.133.refs_4_), channel_id=1, source_target_pairs={{0,28},{4,8},{8,4},{12,16},{16,12},{20,24},{24,20},{28,0},{1,29},{... | collective-permute-start | bytes 589832 | tf_op jit(solution)/shard_map/ppermute | solution.py:333
  66.9 12.3 %collective-permute-start.18 = (f32[24,16,128]{2,1,0:T(8,128)S(1)}, f32[24,16,128]{2,1,0:T(8,128)S(1)}, u32[]{:S(2)}, u32[]{:S(2)}) collective-permute-start(f32[24,16,128]{2,1,0:T(8,128)S(1)} %get-tuple-element.144.refs_3_), channel_id=1, source_target_pairs={{0,4},{4,0},{8,12},{12,8},{16,20},{20,16},{24,28},{28,24},{1,5},{5... | collective-permute-start | bytes 589832 | tf_op jit(solution)/shard_map/ppermute | solution.py:333
  68.0 11.2 %collective-permute-start.19 = (f32[24,16,128]{2,1,0:T(8,128)S(1)}, f32[24,16,128]{2,1,0:T(8,128)S(1)}, u32[]{:S(2)}, u32[]{:S(2)}) collective-permute-start(f32[24,16,128]{2,1,0:T(8,128)S(1)} %get-tuple-element.145.refs_4_), channel_id=1, source_target_pairs={{0,28},{4,8},{8,4},{12,16},{16,12},{20,24},{24,20},{28,0},{1,29},{... | collective-permute-start | bytes 589832 | tf_op jit(solution)/shard_map/ppermute | solution.py:333
  77.2 16.1 %collective-permute-start.8 = (f32[24,16,128]{2,1,0:T(8,128)S(1)}, f32[24,16,128]{2,1,0:T(8,128)S(1)}, u32[]{:S(2)}, u32[]{:S(2)}) collective-permute-start(f32[24,16,128]{2,1,0:T(8,128)S(1)} %get-tuple-element.151.refs_3_.refs_9_.refs_7_), channel_id=1, source_target_pairs={{0,4},{4,0},{8,12},{12,8},{16,20},{20,16},{24,28},{28,24},{1,5},{5... | collective-permute-start | bytes 589832 | tf_op jit(solution)/shard_map/ppermute | solution.py:333
  77.2 17.5 %collective-permute-start.9 = (f32[24,16,128]{2,1,0:T(8,128)S(1)}, f32[24,16,128]{2,1,0:T(8,128)S(1)}, u32[]{:S(2)}, u32[]{:S(2)}) collective-permute-start(f32[24,16,128]{2,1,0:T(8,128)S(1)} %get-tuple-element.152.refs_4_.refs_10_.refs_8_), channel_id=1, source_target_pairs={{0,28},{4,8},{8,4},{12,16},{16,12},{20,24},{24,20},{28,0},{1,29},{... | collective-permute-start | bytes 589832 | tf_op jit(solution)/shard_map/ppermute | solution.py:333
  83.6 15.8 %collective-permute-start.27 = (f32[24,16,128]{2,1,0:T(8,128)S(1)}, f32[24,16,128]{2,1,0:T(8,128)S(1)}, u32[]{:S(2)}, u32[]{:S(2)}) collective-permute-start(f32[24,16,128]{2,1,0:T(8,128)S(1)} %get-tuple-element.164.refs_3_.refs_7_), channel_id=1, source_target_pairs={{0,4},{4,0},{8,12},{12,8},{16,20},{20,16},{24,28},{28,24},{1,5},{5... | collective-permute-start | bytes 589832 | tf_op jit(solution)/shard_map/ppermute | solution.py:333
  83.7 15.7 %collective-permute-start.28 = (f32[24,16,128]{2,1,0:T(8,128)S(1)}, f32[24,16,128]{2,1,0:T(8,128)S(1)}, u32[]{:S(2)}, u32[]{:S(2)}) collective-permute-start(f32[24,16,128]{2,1,0:T(8,128)S(1)} %get-tuple-element.165.refs_4_.refs_8_), channel_id=1, source_target_pairs={{0,28},{4,8},{8,4},{12,16},{16,12},{20,24},{24,20},{28,0},{1,29},{... | collective-permute-start | bytes 589832 | tf_op jit(solution)/shard_map/ppermute | solution.py:333
  93.2 12.9 %collective-permute-start.20 = (f32[12,32,128]{2,1,0:T(8,128)S(1)}, f32[12,32,128]{2,1,0:T(8,128)S(1)}, u32[]{:S(2)}, u32[]{:S(2)}) collective-permute-start(f32[12,32,128]{2,1,0:T(8,128)S(1)} %get-tuple-element.147), channel_id=1, source_target_pairs={{0,1},{1,0},{2,3},{3,2},{4,5},{5,4},{6,7},{7,6},{8,9},{9,8},{10,11... | collective-permute-start | bytes 589832 | tf_op jit(solution)/shard_map/ppermute | solution.py:337
  93.2 13.0 %collective-permute-start.21 = (f32[12,32,128]{2,1,0:T(8,128)S(1)}, f32[12,32,128]{2,1,0:T(8,128)S(1)}, u32[]{:S(2)}, u32[]{:S(2)}) collective-permute-start(f32[12,32,128]{2,1,0:T(8,128)S(1)} %get-tuple-element.148), channel_id=1, source_target_pairs={{0,2},{1,3},{2,0},{3,1},{4,6},{5,7},{6,4},{7,5},{8,10},{9,11},{10,... | collective-permute-start | bytes 589832 | tf_op jit(solution)/shard_map/ppermute | solution.py:337
  94.7 11.6 %collective-permute-start.22 = (f32[12,32,128]{2,1,0:T(8,128)S(1)}, f32[12,32,128]{2,1,0:T(8,128)S(1)}, u32[]{:S(2)}, u32[]{:S(2)}) collective-permute-start(f32[12,32,128]{2,1,0:T(8,128)S(1)} %get-tuple-element.149), channel_id=1, source_target_pairs={{0,3},{1,2},{2,1},{3,0},{4,7},{5,6},{6,5},{7,4},{8,11},{9,10},{10,... | collective-permute-start | bytes 589832 | tf_op jit(solution)/shard_map/ppermute | solution.py:337
  99.4 12.0 %collective-permute-start.10 = (f32[24,16,128]{2,1,0:T(8,128)S(1)}, f32[24,16,128]{2,1,0:T(8,128)S(1)}, u32[]{:S(2)}, u32[]{:S(2)}) collective-permute-start(f32[24,16,128]{2,1,0:T(8,128)S(1)} %get-tuple-element.170.refs_3_.refs_7_), channel_id=1, source_target_pairs={{0,4},{4,0},{8,12},{12,8},{16,20},{20,16},{24,28},{28,24},{1,5},{5... | collective-permute-start | bytes 589832 | tf_op jit(solution)/shard_map/ppermute | solution.py:333
  99.4 11.9 %collective-permute-start.11 = (f32[24,16,128]{2,1,0:T(8,128)S(1)}, f32[24,16,128]{2,1,0:T(8,128)S(1)}, u32[]{:S(2)}, u32[]{:S(2)}) collective-permute-start(f32[24,16,128]{2,1,0:T(8,128)S(1)} %get-tuple-element.171.refs_4_.refs_8_), channel_id=1, source_target_pairs={{0,28},{4,8},{8,4},{12,16},{16,12},{20,24},{24,20},{28,0},{1,29},{... | collective-permute-start | bytes 589832 | tf_op jit(solution)/shard_map/ppermute | solution.py:333
  106.1 12.6 %collective-permute-start.37 = (f32[12,32,128]{2,1,0:T(8,128)S(1)}, f32[12,32,128]{2,1,0:T(8,128)S(1)}, u32[]{:S(2)}, u32[]{:S(2)}) collective-permute-start(f32[12,32,128]{2,1,0:T(8,128)S(1)} %get-tuple-element.183), channel_id=1, source_target_pairs={{0,1},{1,0},{2,3},{3,2},{4,5},{5,4},{6,7},{7,6},{8,9},{9,8},{10,11... | collective-permute-start | bytes 589832 | tf_op jit(solution)/shard_map/ppermute | solution.py:337
  106.2 14.1 %collective-permute-start.29 = (f32[24,16,128]{2,1,0:T(8,128)S(1)}, f32[24,16,128]{2,1,0:T(8,128)S(1)}, u32[]{:S(2)}, u32[]{:S(2)}) collective-permute-start(f32[24,16,128]{2,1,0:T(8,128)S(1)} %get-tuple-element.186.refs_3_.refs_7_), channel_id=1, source_target_pairs={{0,4},{4,0},{8,12},{12,8},{16,20},{20,16},{24,28},{28,24},{1,5},{5... | collective-permute-start | bytes 589832 | tf_op jit(solution)/shard_map/ppermute | solution.py:333
  106.3 15.0 %collective-permute-start.30 = (f32[24,16,128]{2,1,0:T(8,128)S(1)}, f32[24,16,128]{2,1,0:T(8,128)S(1)}, u32[]{:S(2)}, u32[]{:S(2)}) collective-permute-start(f32[24,16,128]{2,1,0:T(8,128)S(1)} %get-tuple-element.187.refs_4_.refs_8_), channel_id=1, source_target_pairs={{0,28},{4,8},{8,4},{12,16},{16,12},{20,24},{24,20},{28,0},{1,29},{... | collective-permute-start | bytes 589832 | tf_op jit(solution)/shard_map/ppermute | solution.py:333
  115.6 11.9 %collective-permute-start.23 = (f32[24,16,128]{2,1,0:T(8,128)S(1)}, f32[24,16,128]{2,1,0:T(8,128)S(1)}, u32[]{:S(2)}, u32[]{:S(2)}) collective-permute-start(f32[24,16,128]{2,1,0:T(8,128)S(1)} %get-tuple-element.192.refs_3_.refs_7_), channel_id=1, source_target_pairs={{0,4},{4,0},{8,12},{12,8},{16,20},{20,16},{24,28},{28,24},{1,5},{5... | collective-permute-start | bytes 589832 | tf_op jit(solution)/shard_map/ppermute | solution.py:333
  117.0 12.4 %collective-permute-start.24 = (f32[24,16,128]{2,1,0:T(8,128)S(1)}, f32[24,16,128]{2,1,0:T(8,128)S(1)}, u32[]{:S(2)}, u32[]{:S(2)}) collective-permute-start(f32[24,16,128]{2,1,0:T(8,128)S(1)} %get-tuple-element.193.refs_4_.refs_8_), channel_id=1, source_target_pairs={{0,28},{4,8},{8,4},{12,16},{16,12},{20,24},{24,20},{28,0},{1,29},{... | collective-permute-start | bytes 589832 | tf_op jit(solution)/shard_map/ppermute | solution.py:333
  120.3 13.5 %collective-permute-start.38 = (f32[12,32,128]{2,1,0:T(8,128)S(1)}, f32[12,32,128]{2,1,0:T(8,128)S(1)}, u32[]{:S(2)}, u32[]{:S(2)}) collective-permute-start(f32[12,32,128]{2,1,0:T(8,128)S(1)} %get-tuple-element.184), channel_id=1, source_target_pairs={{0,2},{1,3},{2,0},{3,1},{4,6},{5,7},{6,4},{7,5},{8,10},{9,11},{10,... | collective-permute-start | bytes 589832 | tf_op jit(solution)/shard_map/ppermute | solution.py:337
  121.3 20.5 %collective-permute-start.39 = (f32[12,32,128]{2,1,0:T(8,128)S(1)}, f32[12,32,128]{2,1,0:T(8,128)S(1)}, u32[]{:S(2)}, u32[]{:S(2)}) collective-permute-start(f32[12,32,128]{2,1,0:T(8,128)S(1)} %get-tuple-element.185), channel_id=1, source_target_pairs={{0,3},{1,2},{2,1},{3,0},{4,7},{5,6},{6,5},{7,4},{8,11},{9,10},{10,... | collective-permute-start | bytes 589832 | tf_op jit(solution)/shard_map/ppermute | solution.py:337
  125.6 16.2 %collective-permute-start.35 = (f32[24,16,128]{2,1,0:T(8,128)S(1)}, f32[24,16,128]{2,1,0:T(8,128)S(1)}, u32[]{:S(2)}, u32[]{:S(2)}) collective-permute-start(f32[24,16,128]{2,1,0:T(8,128)S(1)} %get-tuple-element.203.refs_3_.refs_7_), channel_id=1, source_target_pairs={{0,4},{4,0},{8,12},{12,8},{16,20},{20,16},{24,28},{28,24},{1,5},{5... | collective-permute-start | bytes 589832 | tf_op jit(solution)/shard_map/ppermute | solution.py:333
  127.6 14.2 %collective-permute-start.36 = (f32[24,16,128]{2,1,0:T(8,128)S(1)}, f32[24,16,128]{2,1,0:T(8,128)S(1)}, u32[]{:S(2)}, u32[]{:S(2)}) collective-permute-start(f32[24,16,128]{2,1,0:T(8,128)S(1)} %get-tuple-element.204.refs_4_.refs_8_), channel_id=1, source_target_pairs={{0,28},{4,8},{8,4},{12,16},{16,12},{20,24},{24,20},{28,0},{1,29},{... | collective-permute-start | bytes 589832 | tf_op jit(solution)/shard_map/ppermute | solution.py:333
  133.8 22.4 %collective-permute-start.31 = (f32[24,16,128]{2,1,0:T(8,128)S(1)}, f32[24,16,128]{2,1,0:T(8,128)S(1)}, u32[]{:S(2)}, u32[]{:S(2)}) collective-permute-start(f32[24,16,128]{2,1,0:T(8,128)S(1)} %get-tuple-element.172.refs_3_), channel_id=1, source_target_pairs={{0,4},{4,0},{8,12},{12,8},{16,20},{20,16},{24,28},{28,24},{1,5},{5... | collective-permute-start | bytes 589832 | tf_op jit(solution)/shard_map/ppermute | solution.py:333
  138.8 17.4 %collective-permute-start.32 = (f32[24,16,128]{2,1,0:T(8,128)S(1)}, f32[24,16,128]{2,1,0:T(8,128)S(1)}, u32[]{:S(2)}, u32[]{:S(2)}) collective-permute-start(f32[24,16,128]{2,1,0:T(8,128)S(1)} %get-tuple-element.173.refs_4_), channel_id=1, source_target_pairs={{0,28},{4,8},{8,4},{12,16},{16,12},{20,24},{24,20},{28,0},{1,29},{... | collective-permute-start | bytes 589832 | tf_op jit(solution)/shard_map/ppermute | solution.py:333
  146.1 18.6 %collective-permute-start.43 = (f32[24,16,128]{2,1,0:T(8,128)S(1)}, f32[24,16,128]{2,1,0:T(8,128)S(1)}, u32[]{:S(2)}, u32[]{:S(2)}) collective-permute-start(f32[24,16,128]{2,1,0:T(8,128)S(1)} %get-tuple-element.188.refs_3_), channel_id=1, source_target_pairs={{0,4},{4,0},{8,12},{12,8},{16,20},{20,16},{24,28},{28,24},{1,5},{5... | collective-permute-start | bytes 589832 | tf_op jit(solution)/shard_map/ppermute | solution.py:333
  146.3 18.4 %collective-permute-start.44 = (f32[24,16,128]{2,1,0:T(8,128)S(1)}, f32[24,16,128]{2,1,0:T(8,128)S(1)}, u32[]{:S(2)}, u32[]{:S(2)}) collective-permute-start(f32[24,16,128]{2,1,0:T(8,128)S(1)} %get-tuple-element.189.refs_4_), channel_id=1, source_target_pairs={{0,28},{4,8},{8,4},{12,16},{16,12},{20,24},{24,20},{28,0},{1,29},{... | collective-permute-start | bytes 589832 | tf_op jit(solution)/shard_map/ppermute | solution.py:333
  160.5 10.7 %collective-permute-start.40 = (f32[24,16,128]{2,1,0:T(8,128)S(1)}, f32[24,16,128]{2,1,0:T(8,128)S(1)}, u32[]{:S(2)}, u32[]{:S(2)}) collective-permute-start(f32[24,16,128]{2,1,0:T(8,128)S(1)} %get-tuple-element.194.refs_9_.refs_3_), channel_id=1, source_target_pairs={{0,4},{4,0},{8,12},{12,8},{16,20},{20,16},{24,28},{28,24},{1,5},{5... | collective-permute-start | bytes 589832 | tf_op jit(solution)/shard_map/ppermute | solution.py:333
  162.9 10.1 %collective-permute-start.41 = (f32[24,16,128]{2,1,0:T(8,128)S(1)}, f32[24,16,128]{2,1,0:T(8,128)S(1)}, u32[]{:S(2)}, u32[]{:S(2)}) collective-permute-start(f32[24,16,128]{2,1,0:T(8,128)S(1)} %get-tuple-element.195.refs_10_.refs_4_), channel_id=1, source_target_pairs={{0,28},{4,8},{8,4},{12,16},{16,12},{20,24},{24,20},{28,0},{1,29},{... | collective-permute-start | bytes 589832 | tf_op jit(solution)/shard_map/ppermute | solution.py:333
  169.2 12.6 %collective-permute-start.45 = (f32[12,32,128]{2,1,0:T(8,128)S(1)}, f32[12,32,128]{2,1,0:T(8,128)S(1)}, u32[]{:S(2)}, u32[]{:S(2)}) collective-permute-start(f32[12,32,128]{2,1,0:T(8,128)S(1)} %get-tuple-element.206), channel_id=1, source_target_pairs={{0,1},{1,0},{2,3},{3,2},{4,5},{5,4},{6,7},{7,6},{8,9},{9,8},{10,11... | collective-permute-start | bytes 589832 | tf_op jit(solution)/shard_map/ppermute | solution.py:337
  169.3 12.5 %collective-permute-start.46 = (f32[12,32,128]{2,1,0:T(8,128)S(1)}, f32[12,32,128]{2,1,0:T(8,128)S(1)}, u32[]{:S(2)}, u32[]{:S(2)}) collective-permute-start(f32[12,32,128]{2,1,0:T(8,128)S(1)} %get-tuple-element.207), channel_id=1, source_target_pairs={{0,2},{1,3},{2,0},{3,1},{4,6},{5,7},{6,4},{7,5},{8,10},{9,11},{10,... | collective-permute-start | bytes 589832 | tf_op jit(solution)/shard_map/ppermute | solution.py:337
  170.4 11.4 %collective-permute-start.47 = (f32[12,32,128]{2,1,0:T(8,128)S(1)}, f32[12,32,128]{2,1,0:T(8,128)S(1)}, u32[]{:S(2)}, u32[]{:S(2)}) collective-permute-start(f32[12,32,128]{2,1,0:T(8,128)S(1)} %get-tuple-element.208), channel_id=1, source_target_pairs={{0,3},{1,2},{2,1},{3,0},{4,7},{5,6},{6,5},{7,4},{8,11},{9,10},{10,... | collective-permute-start | bytes 589832 | tf_op jit(solution)/shard_map/ppermute | solution.py:337
  171.2 20.9 %collective-permute-start.50 = (f32[24,16,128]{2,1,0:T(8,128)S(1)}, f32[24,16,128]{2,1,0:T(8,128)S(1)}, u32[]{:S(2)}, u32[]{:S(2)}) collective-permute-start(f32[24,16,128]{2,1,0:T(8,128)S(1)} %get-tuple-element.210.refs_3_), channel_id=1, source_target_pairs={{0,4},{4,0},{8,12},{12,8},{16,20},{20,16},{24,28},{28,24},{1,5},{5... | collective-permute-start | bytes 589832 | tf_op jit(solution)/shard_map/ppermute | solution.py:333
  173.0 19.1 %collective-permute-start.51 = (f32[24,16,128]{2,1,0:T(8,128)S(1)}, f32[24,16,128]{2,1,0:T(8,128)S(1)}, u32[]{:S(2)}, u32[]{:S(2)}) collective-permute-start(f32[24,16,128]{2,1,0:T(8,128)S(1)} %get-tuple-element.211.refs_4_), channel_id=1, source_target_pairs={{0,28},{4,8},{8,4},{12,16},{16,12},{20,24},{24,20},{28,0},{1,29},{... | collective-permute-start | bytes 589832 | tf_op jit(solution)/shard_map/ppermute | solution.py:333
  205.7 18.1 %collective-permute-start.61 = (f32[128,128]{1,0:T(8,128)S(1)}, f32[128,128]{1,0:T(8,128)S(1)}, u32[]{:S(2)}, u32[]{:S(2)}) collective-permute-start(f32[128,128]{1,0:T(8,128)S(1)} %cross.1), channel_id=1, source_target_pairs={{0,4},{4,0},{8,12},{12,8},{16,20},{20,16},{24,28},{28,24},{1,5},{5... | collective-permute-start | bytes 196616 | tf_op jit(solution)/shard_map/ppermute | solution.py:337
  211.4 13.0 %collective-permute-start.64 = (f32[128,128]{1,0:T(8,128)S(1)}, f32[128,128]{1,0:T(8,128)S(1)}, u32[]{:S(2)}, u32[]{:S(2)}) collective-permute-start(f32[128,128]{1,0:T(8,128)S(1)} %turn_cross.1), channel_id=1, source_target_pairs={{0,4},{4,0},{8,12},{12,8},{16,20},{20,16},{24,28},{28,24},{1,5},{5... | collective-permute-start | bytes 196616 | tf_op jit(solution)/shard_map/ppermute | solution.py:337
  221.9 18.2 %collective-permute-start.58 = (f32[12,32,128]{2,1,0:T(8,128)S(1)}, f32[12,32,128]{2,1,0:T(8,128)S(1)}, u32[]{:S(2)}, u32[]{:S(2)}) collective-permute-start(f32[12,32,128]{2,1,0:T(8,128)S(1)} %get-tuple-element.232), channel_id=1, source_target_pairs={{0,1},{1,0},{2,3},{3,2},{4,5},{5,4},{6,7},{7,6},{8,9},{9,8},{10,11... | collective-permute-start | bytes 589832 | tf_op jit(solution)/shard_map/ppermute | solution.py:337
  222.2 18.2 %collective-permute-start.59 = (f32[12,32,128]{2,1,0:T(8,128)S(1)}, f32[12,32,128]{2,1,0:T(8,128)S(1)}, u32[]{:S(2)}, u32[]{:S(2)}) collective-permute-start(f32[12,32,128]{2,1,0:T(8,128)S(1)} %get-tuple-element.233), channel_id=1, source_target_pairs={{0,2},{1,3},{2,0},{3,1},{4,6},{5,7},{6,4},{7,5},{8,10},{9,11},{10,... | collective-permute-start | bytes 589832 | tf_op jit(solution)/shard_map/ppermute | solution.py:337
  223.7 16.7 %collective-permute-start.60 = (f32[12,32,128]{2,1,0:T(8,128)S(1)}, f32[12,32,128]{2,1,0:T(8,128)S(1)}, u32[]{:S(2)}, u32[]{:S(2)}) collective-permute-start(f32[12,32,128]{2,1,0:T(8,128)S(1)} %get-tuple-element.234), channel_id=1, source_target_pairs={{0,3},{1,2},{2,1},{3,0},{4,7},{5,6},{6,5},{7,4},{8,11},{9,10},{10,... | collective-permute-start | bytes 589832 | tf_op jit(solution)/shard_map/ppermute | solution.py:337
  (23 other events, 142.2 us)

commit v7 on v6

--- a/solution.py
+++ b/solution.py
@@ -11,6 +11,8 @@
 UNROLL = 72
 CHUNK = 24
 TURNS = 3
+TIE_HALO = 0
+TIE_FIRST = 1
 APPLY_BYTES = 4 << 20
 F32, BF16, I32 = jnp.float32, jnp.bfloat16, jnp.int32
 precise = lax.Precision.HIGHEST
@@ -343,6 +345,27 @@
 
 def hops_of(*axes):
     return [(axis, 1 << i) for axis in axes for i in range((lax.axis_size(axis) - 1).bit_length())]
+
+
+def rounds_of(*axes):
+    rounds = []
+    for axis in axes:
+        bits = (lax.axis_size(axis) - 1).bit_length()
+        while bits > 0:
+            low = max(bits - 2, 0)
+            rounds.append((axis, [1 << bit for bit in range(low, bits)]))
+            bits = low
+    return rounds
+
+
+def round_swaps(value, axis, hops):
+    hops = hops if len(hops) == 1 else [hops[0], hops[1], hops[0] ^ hops[1]]
+    return [swap(value, axis, hop) for hop in hops]
+
+
+def round_sum(value, got):
+    value = value + got[0]
+    return value if len(got) == 1 else value + (got[1] + got[2])
 
 
 def body(blocks, owner_row, block_col, start):
@@ -406,45 +429,51 @@
     (image_first,) = call(
         cross_kernel, "cross", [square], ids, panel, gram_first, *image, scalars=1, scratch=[held]
     )
+    first, _ = apply(meta, now[0], halos[0])
+    arrived, first = lax.optimization_barrier((swapped(parts), first))
     turned, gram_last = call(
-        turn_kernel, "turn", [wide, square], ids, inverse_first, *swapped(parts), scalars=1, scratch=[held]
-    )
-    first, _ = apply(meta, now[0], halos[0])
+        turn_kernel, "turn", [wide, square], ids, inverse_first, *arrived, scalars=1, scratch=[held]
+    )
     gram = gram_last
-    hops = hops_of("col", "node")
-    for i, hop in enumerate(hops):
-        got = swap(gram, *hop)
-        if i == 1:
+    rounds = rounds_of("col", "node")
+    for i, each_round in enumerate(rounds):
+        got = round_swaps(gram, *each_round)
+        if i == TIE_HALO:
             got, halos[1] = lax.optimization_barrier((got, halos[1]))
             _, parts = apply(meta, now[1], halos[1], (), first, count)
             (image_last,) = call(
                 turn_cross_kernel, "turn_cross", [square], ids, inverse_first, turned, gram_last,
                 *swapped(parts), scalars=1, scratch=[held],
             )
-        if i == len(hops) - 2:
+        if i == len(rounds) - TIE_FIRST:
             got, image_first = lax.optimization_barrier((got, image_first))
-        if i == len(hops) - 1:
+        if i == len(rounds) - 1:
             got, image_last = lax.optimization_barrier((got, image_last))
-        gram = gram + got
+        gram = round_sum(gram, got)
     inverse_last = inverse_factor(gram, nodes)
-    for i, hop in enumerate(hops_of("node")):
-        image_first = image_first + swap(image_first, *hop)
-        got = swap(image_last, *hop)
-        if i == 0:
-            got, image_last, _ = lax.optimization_barrier((got, image_last, inverse_last))
-        image_last = image_last + got
     parts = call(
         basis_kernel, "basis", [(quarter, cols_here, block)] * count, ids, inverse_last, turned,
         scalars=1, scratch=[held],
     )
-    (basis,) = call(
-        functools.partial(join_kernel, half), "join", [(cols_here, width)], ids, *swapped(parts), scalars=1
-    )
+    for i, each_round in enumerate(rounds_of("node")):
+        if i == 1:
+            parts, image_last = lax.optimization_barrier((parts, image_last))
+        got_first = round_swaps(image_first, *each_round)
+        got = round_swaps(image_last, *each_round)
+        if i == 0:
+            got, got_first, image_last, _ = lax.optimization_barrier((got, got_first, image_last, inverse_last))
+        image_first = round_sum(image_first, got_first)
+        image_last = round_sum(image_last, got)
+    arrived = swapped(parts)
     parts = call(
         functools.partial(proj_kernel, nodes), "proj", [(2, cols_here, vecs)] * count, ids,
         inverse_first, image_first, inverse_last, image_last, scalars=1, scratch=[pltpu.VMEM(square, F32)],
     )
-    projected = sum(swapped(parts))
+    received, arrived = lax.optimization_barrier((swapped(parts), arrived))
+    projected = sum(received)
+    (basis,) = call(
+        functools.partial(join_kernel, half), "join", [(cols_here, width)], ids, *arrived, scalars=1
+    )
     return basis, projected[0], projected[1]
 
 

time: 244 us -> 253 us (1.037)
  starting transfers between devices: 95.5 us -> 103 us
    ppermute x34 -> x38, starting transfers between devices: 24.1 us -> 31.9 us  [swap(): lax.ppermute(value, axis, [(i, i ^ hop) for i in range(lax.axis_size(axis...]
    ppermute x34 -> x38, waiting for transfers between devices: 26.6 us -> 27.2 us  [swap(): lax.ppermute(value, axis, [(i, i ^ hop) for i in range(lax.axis_size(axis...]
  transfers between devices with their start and end apart: 70 -> 74, of which waited for: 14 -> 13; matrix products, arithmetic and copies ran while one was open for 0% -> 0% of each run, Pallas kernels for 48% -> 45%
where the time goes in v7:
time: 253 us
  Pallas kernels  117 us (46%)
  starting transfers between devices  103 us (41%)
  waiting for transfers between devices  29.9 us (12%)
    pallas_call x18, Pallas kernels, apply(): pl.pallas_call(functools.partial(apply_kernel, bool(old), bool(mate)), in...  78.1 us
    ppermute x18, starting transfers between devices, exchange(): lax.ppermute(pair[1], 'node', odd)  57.8 us
    ppermute x38, starting transfers between devices, swap(): lax.ppermute(value, axis, [(i, i ^ hop) for i in range(lax.axis_size(axis...  31.9 us
    pallas_call x10, Pallas kernels, call(): pl.pallas_call(kernel, in_specs=[IN_SMEM] * scalars + [IN_VMEM] * (len(ar...  29.8 us
    ppermute x38, waiting for transfers between devices, swap(): lax.ppermute(value, axis, [(i, i ^ hop) for i in range(lax.axis_size(axis...  27.2 us
    ppermute x18, starting transfers between devices, exchange(): lax.ppermute(pair[0], 'node', even)  13.1 us
    pallas_call x1, Pallas kernels, prep(): pl.pallas_call(functools.partial(prep_kernel, rows), in_specs=[IN_SMEM] *...  8.93 us
  transfers between devices with their start and end apart: 74, of which 13 were waited for; matrix products, arithmetic and copies ran while one was open for 0% of the time, Pallas kernels for 45%

profile of v7, /device:TPU:0, one launch (start us, length us, event | category | flops | bytes accessed | tf_op | source)
XLA Modules:
  0.0 252.7 jit_solution(17479995122393082426)
XLA Ops:
  2.5 3.0 %collective-permute-start = (f32[24,16,128]{2,1,0:T(8,128)S(1)}, f32[24,16,128]{2,1,0:T(8,128)S(1)}, u32[]{:S(2)}, u32[]{:S(2)}) collective-permute-start(f32[24,16,128]{2,1,0:T(8,128)S(1)} %get-tuple-element.152.refs_3_.refs_7_), channel_id=1, source_target_pairs={{0,4},{4,0},{8,12},{12,8},{16,20},{20,16},{24,28},{28,24},{1,5},{5... | collective-permute-start | bytes 589832 | tf_op jit(solution)/shard_map/ppermute | solution.py:335
  5.5 3.5 %collective-permute-start.1 = (f32[24,16,128]{2,1,0:T(8,128)S(1)}, f32[24,16,128]{2,1,0:T(8,128)S(1)}, u32[]{:S(2)}, u32[]{:S(2)}) collective-permute-start(f32[24,16,128]{2,1,0:T(8,128)S(1)} %get-tuple-element.153.refs_4_.refs_8_), channel_id=1, source_target_pairs={{0,28},{4,8},{8,4},{12,16},{16,12},{20,24},{24,20},{28,0},{1,29},{... | collective-permute-start | bytes 589832 | tf_op jit(solution)/shard_map/ppermute | solution.py:335
  11.0 8.9 %prep.1 = (bf16[288,128,256]{2,1,0:T(8,128)(2,1)S(1)}, f32[48,1,128]{2,1,0:T(1,128)S(1)}, s32[578]{0:T(1024)S(1)}) custom-call(s32[2]{0:T(128)S(1)} %pad_add_fusion.ids_ref, s32[1,288]{1,0:T(1,128)} %own_ref.1, s32[1,288]{1,0:T(1,128)} %col_ref.1, f32[288,128,128]{2,1,0:T(8,128)} %blk_ref.1), custom_call_target="tpu_custom_call" | custom-call | flops 1207959552 | bytes 18874368 | tf_op jit(solution)/shard_map/prep/pallas_call | solution.py:117
  19.9 4.2 %apply.4 = (f32[24,16,128]{2,1,0:T(8,128)S(1)}, f32[24,16,128]{2,1,0:T(8,128)S(1)}) custom-call(s32[578]{0:T(1024)S(1)} %get-tuple-element.149.refs_0_, bf16[288,128,256]{2,1,0:T(8,128)(2,1)S(1)} %get-tuple-element.150.refs_1_, f32[48,1,128]{2,1,0:T(1,128)S(1)} %get-tuple-element.151.refs_2_, f32[24,16,128]{2,1,0:T(8,128)S(1)} %get-tuple-element.152.refs_3_.refs_7_, ...), custom_call_target="tpu_custom_call" | custom-call | bytes 4194304 | tf_op jit(solution)/shard_map/apply/pallas_call | solution.py:196
  26.1 3.6 %collective-permute-start.3 = (f32[24,16,128]{2,1,0:T(8,128)S(1)}, f32[24,16,128]{2,1,0:T(8,128)S(1)}, u32[]{:S(2)}, u32[]{:S(2)}) collective-permute-start(f32[24,16,128]{2,1,0:T(8,128)S(1)} %get-tuple-element.155.refs_4_.refs_8_), channel_id=1, source_target_pairs={{0,28},{4,8},{8,4},{12,16},{16,12},{20,24},{24,20},{28,0},{1,29},{... | collective-permute-start | bytes 589832 | tf_op jit(solution)/shard_map/ppermute | solution.py:335
  29.6 4.2 %apply.6 = (f32[24,16,128]{2,1,0:T(8,128)S(1)}, f32[24,16,128]{2,1,0:T(8,128)S(1)}) custom-call(s32[578]{0:T(1024)S(1)} %get-tuple-element.149.refs_0_, bf16[288,128,256]{2,1,0:T(8,128)(2,1)S(1)} %get-tuple-element.150.refs_1_, f32[48,1,128]{2,1,0:T(1,128)S(1)} %get-tuple-element.151.refs_2_, f32[24,16,128]{2,1,0:T(8,128)S(1)} %get-tuple-element.164.refs_3_.refs_7_, ...), custom_call_target="tpu_custom_call" | custom-call | bytes 4194304 | tf_op jit(solution)/shard_map/apply/pallas_call | solution.py:196
  35.9 4.3 %apply_recur.10 = (f32[24,16,128]{2,1,0:T(8,128)S(1)}, f32[24,16,128]{2,1,0:T(8,128)S(1)}) custom-call(s32[578]{0:T(1024)S(1)} %get-tuple-element.149.refs_0_, bf16[288,128,256]{2,1,0:T(8,128)(2,1)S(1)} %get-tuple-element.150.refs_1_, f32[48,1,128]{2,1,0:T(1,128)S(1)} %get-tuple-element.151.refs_2_, f32[24,16,128]{2,1,0:T(8,128)S(1)} %get-tuple-element.154.refs_3_.refs_7_, ...), custom_call_target="tpu_custom_call" | custom-call | bytes 4194304 | tf_op jit(solution)/shard_map/apply_recur/pallas_call | solution.py:196
  40.8 8.2 %collective-permute-start.5 = (f32[24,16,128]{2,1,0:T(8,128)S(1)}, f32[24,16,128]{2,1,0:T(8,128)S(1)}, u32[]{:S(2)}, u32[]{:S(2)}) collective-permute-start(f32[24,16,128]{2,1,0:T(8,128)S(1)} %get-tuple-element.157.refs_4_.refs_8_), channel_id=1, source_target_pairs={{0,28},{4,8},{8,4},{12,16},{16,12},{20,24},{24,20},{28,0},{1,29},{... | collective-permute-start | bytes 589832 | tf_op jit(solution)/shard_map/ppermute | solution.py:335
  49.0 4.3 %apply_recur.13 = (f32[24,16,128]{2,1,0:T(8,128)S(1)}, f32[24,16,128]{2,1,0:T(8,128)S(1)}) custom-call(s32[578]{0:T(1024)S(1)} %get-tuple-element.149.refs_0_, bf16[288,128,256]{2,1,0:T(8,128)(2,1)S(1)} %get-tuple-element.150.refs_1_, f32[48,1,128]{2,1,0:T(1,128)S(1)} %get-tuple-element.151.refs_2_, f32[24,16,128]{2,1,0:T(8,128)S(1)} %get-tuple-element.166.refs_3_.refs_7_, ...), custom_call_target="tpu_custom_call" | custom-call | bytes 4194304 | tf_op jit(solution)/shard_map/apply_recur/pallas_call | solution.py:196
  55.3 4.2 %apply_recur.11 = (f32[24,16,128]{2,1,0:T(8,128)S(1)}, f32[24,16,128]{2,1,0:T(8,128)S(1)}) custom-call(s32[578]{0:T(1024)S(1)} %get-tuple-element.149.refs_0_, bf16[288,128,256]{2,1,0:T(8,128)(2,1)S(1)} %get-tuple-element.150.refs_1_, f32[48,1,128]{2,1,0:T(1,128)S(1)} %get-tuple-element.151.refs_2_, f32[24,16,128]{2,1,0:T(8,128)S(1)} %get-tuple-element.156.refs_3_.refs_7_, ...), custom_call_target="tpu_custom_call" | custom-call | bytes 4194304 | tf_op jit(solution)/shard_map/apply_recur/pallas_call | solution.py:196
  59.7 2.9 %collective-permute-start.7 = (f32[24,16,128]{2,1,0:T(8,128)S(1)}, f32[24,16,128]{2,1,0:T(8,128)S(1)}, u32[]{:S(2)}, u32[]{:S(2)}) collective-permute-start(f32[24,16,128]{2,1,0:T(8,128)S(1)} %get-tuple-element.159.refs_4_), channel_id=1, source_target_pairs={{0,28},{4,8},{8,4},{12,16},{16,12},{20,24},{24,20},{28,0},{1,29},{... | collective-permute-start | bytes 589832 | tf_op jit(solution)/shard_map/ppermute | solution.py:335
  62.6 4.3 %apply_recur.14 = (f32[24,16,128]{2,1,0:T(8,128)S(1)}, f32[24,16,128]{2,1,0:T(8,128)S(1)}) custom-call(s32[578]{0:T(1024)S(1)} %get-tuple-element.149.refs_0_, bf16[288,128,256]{2,1,0:T(8,128)(2,1)S(1)} %get-tuple-element.150.refs_1_, f32[48,1,128]{2,1,0:T(1,128)S(1)} %get-tuple-element.151.refs_2_, f32[24,16,128]{2,1,0:T(8,128)S(1)} %get-tuple-element.168.refs_3_.refs_7_, ...), custom_call_target="tpu_custom_call" | custom-call | bytes 4194304 | tf_op jit(solution)/shard_map/apply_recur/pallas_call | solution.py:196
  68.0 4.9 %collective-permute-start.19 = (f32[24,16,128]{2,1,0:T(8,128)S(1)}, f32[24,16,128]{2,1,0:T(8,128)S(1)}, u32[]{:S(2)}, u32[]{:S(2)}) collective-permute-start(f32[24,16,128]{2,1,0:T(8,128)S(1)} %get-tuple-element.171.refs_4_), channel_id=1, source_target_pairs={{0,28},{4,8},{8,4},{12,16},{16,12},{20,24},{24,20},{28,0},{1,29},{... | collective-permute-start | bytes 589832 | tf_op jit(solution)/shard_map/ppermute | solution.py:335
  72.9 4.3 %apply_recur.12 = (f32[24,16,128]{2,1,0:T(8,128)S(1)}, f32[24,16,128]{2,1,0:T(8,128)S(1)}) custom-call(s32[578]{0:T(1024)S(1)} %get-tuple-element.149.refs_0_, bf16[288,128,256]{2,1,0:T(8,128)(2,1)S(1)} %get-tuple-element.150.refs_1_, f32[48,1,128]{2,1,0:T(1,128)S(1)} %get-tuple-element.151.refs_2_, f32[24,16,128]{2,1,0:T(8,128)S(1)} %get-tuple-element.158.refs_3_, ...), custom_call_target="tpu_custom_call" | custom-call | bytes 4194304 | tf_op jit(solution)/shard_map/apply_recur/pallas_call | solution.py:196
  79.2 4.4 %apply_recur_parts.2 = (f32[24,16,128]{2,1,0:T(8,128)S(1)}, f32[24,16,128]{2,1,0:T(8,128)S(1)}, f32[12,32,128]{2,1,0:T(8,128)S(1)}, f32[12,32,128]{2,1,0:T(8,128...) custom-call(s32[578]{0:T(1024)S(1)} %get-tuple-element.149.refs_0_, ...), custom_call_target="tpu_custom_call" | custom-call | bytes 4194304 | tf_op jit(solution)/shard_map/apply_recur_parts/pallas_call | solution.py:196
  83.8 9.5 %collective-permute-start.28 = (f32[24,16,128]{2,1,0:T(8,128)S(1)}, f32[24,16,128]{2,1,0:T(8,128)S(1)}, u32[]{:S(2)}, u32[]{:S(2)}) collective-permute-start(f32[24,16,128]{2,1,0:T(8,128)S(1)} %get-tuple-element.191.refs_4_.refs_8_), channel_id=1, source_target_pairs={{0,28},{4,8},{8,4},{12,16},{16,12},{20,24},{24,20},{28,0},{1,29},{... | collective-permute-start | bytes 589832 | tf_op jit(solution)/shard_map/ppermute | solution.py:335
  95.1 4.2 %apply.5 = (f32[24,16,128]{2,1,0:T(8,128)S(1)}, f32[24,16,128]{2,1,0:T(8,128)S(1)}) custom-call(s32[578]{0:T(1024)S(1)} %get-tuple-element.149.refs_0_, bf16[288,128,256]{2,1,0:T(8,128)(2,1)S(1)} %get-tuple-element.150.refs_1_, f32[48,1,128]{2,1,0:T(1,128)S(1)} %get-tuple-element.151.refs_2_, f32[24,16,128]{2,1,0:T(8,128)S(1)} %get-tuple-element.177.refs_3_.refs_9_.refs_7_, ...), custom_call_target="tpu_custom_call" | custom-call | bytes 4194304 | tf_op jit(solution)/shard_map/apply/pallas_call | solution.py:196
  99.4 2.1 collective-permute-start.11
  101.6 4.5 %apply_parts.2 = (f32[24,16,128]{2,1,0:T(8,128)S(1)}, f32[24,16,128]{2,1,0:T(8,128)S(1)}, f32[12,32,128]{2,1,0:T(8,128)S(1)}, f32[12,32,128]{2,1,0:T(8,128)S(1)}...) custom-call(s32[578]{0:T(1024)S(1)} %get-tuple-element.149.refs_0_, ...), custom_call_target="tpu_custom_call" | custom-call | bytes 4194304 | tf_op jit(solution)/shard_map/apply_parts/pallas_call | solution.py:196
  108.8 2.6 %collective-permute-done.10.refs_5_ = f32[24,16,128]{2,1,0:T(8,128)S(1)} collective-permute-done((f32[24,16,128]{2,1,0:T(8,128)S(1)}, f32[24,16,128]{2,1,0:T(8,128)S(1)}, u32[]{:S(2)}, u32[]{:S(2)}) %collective-permute-start.10) | collective-permute-done | bytes 196640 | tf_op jit(solution)/shard_map/ppermute | solution.py:335
  111.7 4.3 %apply_recur.15 = (f32[24,16,128]{2,1,0:T(8,128)S(1)}, f32[24,16,128]{2,1,0:T(8,128)S(1)}) custom-call(s32[578]{0:T(1024)S(1)} %get-tuple-element.149.refs_0_, bf16[288,128,256]{2,1,0:T(8,128)(2,1)S(1)} %get-tuple-element.150.refs_1_, f32[48,1,128]{2,1,0:T(1,128)S(1)} %get-tuple-element.151.refs_2_, f32[24,16,128]{2,1,0:T(8,128)S(1)} %get-tuple-element.196.refs_3_.refs_7_, ...), custom_call_target="tpu_custom_call" | custom-call | bytes 4194304 | tf_op jit(solution)/shard_map/apply_recur/pallas_call | solution.py:196
  116.1 4.4 %collective-permute-start.24 = (f32[24,16,128]{2,1,0:T(8,128)S(1)}, f32[24,16,128]{2,1,0:T(8,128)S(1)}, u32[]{:S(2)}, u32[]{:S(2)}) collective-permute-start(f32[24,16,128]{2,1,0:T(8,128)S(1)} %get-tuple-element.219.refs_4_.refs_8_), channel_id=1, source_target_pairs={{0,28},{4,8},{8,4},{12,16},{16,12},{20,24},{24,20},{28,0},{1,29},{... | collective-permute-start | bytes 589832 | tf_op jit(solution)/shard_map/ppermute | solution.py:335
  122.6 4.2 %apply_recur.16 = (f32[24,16,128]{2,1,0:T(8,128)S(1)}, f32[24,16,128]{2,1,0:T(8,128)S(1)}) custom-call(s32[578]{0:T(1024)S(1)} %get-tuple-element.149.refs_0_, bf16[288,128,256]{2,1,0:T(8,128)(2,1)S(1)} %get-tuple-element.150.refs_1_, f32[48,1,128]{2,1,0:T(1,128)S(1)} %get-tuple-element.151.refs_2_, f32[24,16,128]{2,1,0:T(8,128)S(1)} %get-tuple-element.212.refs_3_.refs_7_, ...), custom_call_target="tpu_custom_call" | custom-call | bytes 4194304 | tf_op jit(solution)/shard_map/apply_recur/pallas_call | solution.py:196
  128.3 2.3 collective-permute-start.36
  130.9 4.3 %apply_recur.17 = (f32[24,16,128]{2,1,0:T(8,128)S(1)}, f32[24,16,128]{2,1,0:T(8,128)S(1)}) custom-call(s32[578]{0:T(1024)S(1)} %get-tuple-element.149.refs_0_, bf16[288,128,256]{2,1,0:T(8,128)(2,1)S(1)} %get-tuple-element.150.refs_1_, f32[48,1,128]{2,1,0:T(1,128)S(1)} %get-tuple-element.151.refs_2_, f32[24,16,128]{2,1,0:T(8,128)S(1)} %get-tuple-element.218.refs_3_.refs_7_, ...), custom_call_target="tpu_custom_call" | custom-call | bytes 4194304 | tf_op jit(solution)/shard_map/apply_recur/pallas_call | solution.py:196
  137.1 4.5 %collective-permute-done.33 = f32[128,128]{1,0:T(8,128)S(1)} collective-permute-done((f32[128,128]{1,0:T(8,128)S(1)}, f32[128,128]{1,0:T(8,128)S(1)}, u32[]{:S(2)}, u32[]{:S(2)}) %collective-permute-start.33) | collective-permute-done | bytes 65568 | tf_op jit(solution)/shard_map/ppermute | solution.py:339
  141.7 4.3 %apply_recur.18 = (f32[24,16,128]{2,1,0:T(8,128)S(1)}, f32[24,16,128]{2,1,0:T(8,128)S(1)}) custom-call(s32[578]{0:T(1024)S(1)} %get-tuple-element.149.refs_0_, bf16[288,128,256]{2,1,0:T(8,128)(2,1)S(1)} %get-tuple-element.150.refs_1_, f32[48,1,128]{2,1,0:T(1,128)S(1)} %get-tuple-element.151.refs_2_, f32[24,16,128]{2,1,0:T(8,128)S(1)} %get-tuple-element.229.refs_3_.refs_7_, ...), custom_call_target="tpu_custom_call" | custom-call | bytes 4194304 | tf_op jit(solution)/shard_map/apply_recur/pallas_call | solution.py:196
  146.4 4.4 %collective-permute-start.44 = (f32[24,16,128]{2,1,0:T(8,128)S(1)}, f32[24,16,128]{2,1,0:T(8,128)S(1)}, u32[]{:S(2)}, u32[]{:S(2)}) collective-permute-start(f32[24,16,128]{2,1,0:T(8,128)S(1)} %get-tuple-element.215.refs_4_), channel_id=1, source_target_pairs={{0,28},{4,8},{8,4},{12,16},{16,12},{20,24},{24,20},{28,0},{1,29},{... | collective-permute-start | bytes 589832 | tf_op jit(solution)/shard_map/ppermute | solution.py:335
  150.9 4.3 %collective-permute-done.34 = f32[128,128]{1,0:T(8,128)S(1)} collective-permute-done((f32[128,128]{1,0:T(8,128)S(1)}, f32[128,128]{1,0:T(8,128)S(1)}, u32[]{:S(2)}, u32[]{:S(2)}) %collective-permute-start.34) | collective-permute-done | bytes 65568 | tf_op jit(solution)/shard_map/ppermute | solution.py:339
  155.2 4.3 %apply_recur.19 = (f32[24,16,128]{2,1,0:T(8,128)S(1)}, f32[24,16,128]{2,1,0:T(8,128)S(1)}) custom-call(s32[578]{0:T(1024)S(1)} %get-tuple-element.149.refs_0_, bf16[288,128,256]{2,1,0:T(8,128)(2,1)S(1)} %get-tuple-element.150.refs_1_, f32[48,1,128]{2,1,0:T(1,128)S(1)} %get-tuple-element.151.refs_2_, f32[24,16,128]{2,1,0:T(8,128)S(1)} %get-tuple-element.198.refs_3_, ...), custom_call_target="tpu_custom_call" | custom-call | bytes 4194304 | tf_op jit(solution)/shard_map/apply_recur/pallas_call | solution.py:196
  161.1 2.0 collective-permute-start.41
  164.9 5.0 %collective-permute-done.42 = f32[128,128]{1,0:T(8,128)S(1)} collective-permute-done((f32[128,128]{1,0:T(8,128)S(1)}, f32[128,128]{1,0:T(8,128)S(1)}, u32[]{:S(2)}, u32[]{:S(2)}) %collective-permute-start.42) | collective-permute-done | bytes 65568 | tf_op jit(solution)/shard_map/ppermute | solution.py:339
  169.9 4.4 %apply_recur_parts.3 = (f32[24,16,128]{2,1,0:T(8,128)S(1)}, f32[24,16,128]{2,1,0:T(8,128)S(1)}, f32[12,32,128]{2,1,0:T(8,128)S(1)}, f32[12,32,128]{2,1,0:T(8,128...) custom-call(s32[578]{0:T(1024)S(1)} %get-tuple-element.149.refs_0_, ...), custom_call_target="tpu_custom_call" | custom-call | bytes 4194304 | tf_op jit(solution)/shard_map/apply_recur_parts/pallas_call | solution.py:196
  179.7 7.1 %factor.2.inv_ref.refs_0_ = f32[128,128]{1,0:T(8,128)S(1)} custom-call(f32[128,128]{1,0:T(8,128)S(1)} %add.73.g_ref), custom_call_target="tpu_custom_call" | custom-call | tf_op jit(solution)/shard_map/factor/pallas_call | solution.py:43
  186.8 4.5 %apply.7 = (f32[24,16,128]{2,1,0:T(8,128)S(1)}, f32[24,16,128]{2,1,0:T(8,128)S(1)}) custom-call(s32[578]{0:T(1024)S(1)} %get-tuple-element.149.refs_0_, bf16[288,128,256]{2,1,0:T(8,128)(2,1)S(1)} %get-tuple-element.150.refs_1_, f32[48,1,128]{2,1,0:T(1,128)S(1)} %get-tuple-element.151.refs_2_, f32[24,16,128]{2,1,0:T(8,128)S(1)} %get-tuple-element.220.refs_9_.refs_3_, ...), custom_call_target="tpu_custom_call" | custom-call | bytes 4194304 | tf_op jit(solution)/shard_map/apply/pallas_call | solution.py:196
  191.3 4.0 %turn.1 = (f32[12,128,128]{2,1,0:T(8,128)S(1)}, f32[128,128]{1,0:T(8,128)S(1)}) custom-call(s32[2]{0:T(128)S(1)} %pad_add_fusion.ids_ref, f32[128,128]{1,0:T(8,128)S(1)} %factor.2.inv_ref.refs_0_, f32[12,32,128]{2,1,0:T(8,128)S(1)} %get-tuple-element.239.refs_0_, f32[12,32,128]{2,1,0:T(8,128)S(1)} %collective-permute-done.45.refs_1_, ...), custom_call_target="tpu_custom_call" | custom-call | tf_op jit(solution)/shard_map/turn/pallas_call | solution.py:43
  197.3 2.5 collective-permute-done.50
  202.7 2.9 %collective-permute-start.53 = (f32[128,128]{1,0:T(8,128)S(1)}, f32[128,128]{1,0:T(8,128)S(1)}, u32[]{:S(2)}, u32[]{:S(2)}) collective-permute-start(f32[128,128]{1,0:T(8,128)S(1)} %add_add_fusion.3), channel_id=1, source_target_pairs={{0,8},{4,12},{8,0},{12,4},{16,24},{20,28},{24,16},{28,20},{1,9},{5... | collective-permute-start | bytes 196616 | tf_op jit(solution)/shard_map/ppermute | solution.py:339
  205.6 5.1 %apply_parts.3 = (f32[24,16,128]{2,1,0:T(8,128)}, f32[24,16,128]{2,1,0:T(8,128)}, f32[12,32,128]{2,1,0:T(8,128)S(1)}, f32[12,32,128]{2,1,0:T(8,128)S(1)}, f32[12...) custom-call(s32[578]{0:T(1024)S(1)} %get-tuple-element.149.refs_0_, ...), custom_call_target="tpu_custom_call" | custom-call | bytes 4194304 | tf_op jit(solution)/shard_map/apply_parts/pallas_call | solution.py:196
  212.6 2.2 cross.1
  214.8 2.1 collective-permute-done.56
  218.6 2.7 %collective-permute-start.63 = (f32[128,128]{1,0:T(8,128)S(1)}, f32[128,128]{1,0:T(8,128)S(1)}, u32[]{:S(2)}, u32[]{:S(2)}) collective-permute-start(f32[128,128]{1,0:T(8,128)S(1)} %cross.1), channel_id=1, source_target_pairs={{0,8},{4,12},{8,0},{12,4},{16,24},{20,28},{24,16},{28,20},{1,9},{5... | collective-permute-start | bytes 196616 | tf_op jit(solution)/shard_map/ppermute | solution.py:339
  221.8 2.7 %turn_cross.1 = f32[128,128]{1,0:T(8,128)S(1)} custom-call(s32[2]{0:T(128)S(1)} %pad_add_fusion.ids_ref, f32[128,128]{1,0:T(8,128)S(1)} %factor.2.inv_ref.refs_0_, f32[12,128,128]{2,1,0:T(8,128)S(1)} %get-tuple-element.256.f_ref, f32[128,128]{1,0:T(8,128)S(1)} %get-tuple-element.243.g_ref, f32[12,32,128]{2,1,0:T(8,128)S(1)} %get-tuple-element.261.refs_0_, ...), custom_call_target="tpu_custom_call" | custom-call | tf_op jit(solution)/shard_map/turn_cross/pallas_call | solution.py:43
  226.1 2.9 %collective-permute-start.60 = (f32[128,128]{1,0:T(8,128)S(1)}, f32[128,128]{1,0:T(8,128)S(1)}, u32[]{:S(2)}, u32[]{:S(2)}) collective-permute-start(f32[128,128]{1,0:T(8,128)S(1)} %turn_cross.1), channel_id=1, source_target_pairs={{0,8},{4,12},{8,0},{12,4},{16,24},{20,28},{24,16},{28,20},{1,9},{5... | collective-permute-start | bytes 196616 | tf_op jit(solution)/shard_map/ppermute | solution.py:339
  229.0 7.1 %factor.3.inv_ref.refs_2_ = f32[128,128]{1,0:T(8,128)S(1)} custom-call(f32[128,128]{1,0:T(8,128)S(1)} %add.80.g_ref), custom_call_target="tpu_custom_call" | custom-call | tf_op jit(solution)/shard_map/factor/pallas_call | solution.py:43
  239.6 2.0 collective-permute-start.66
  241.9 2.2 collective-permute-done.66
  247.6 2.5 collective-permute-done.69
  (146 shorter events, 54.2 us)
Async XLA Ops:
  2.5 17.4 %collective-permute-start = (f32[24,16,128]{2,1,0:T(8,128)S(1)}, f32[24,16,128]{2,1,0:T(8,128)S(1)}, u32[]{:S(2)}, u32[]{:S(2)}) collective-permute-start(f32[24,16,128]{2,1,0:T(8,128)S(1)} %get-tuple-element.152.refs_3_.refs_7_), channel_id=1, source_target_pairs={{0,4},{4,0},{8,12},{12,8},{16,20},{20,16},{24,28},{28,24},{1,5},{5... | collective-permute-start | bytes 589832 | tf_op jit(solution)/shard_map/ppermute | solution.py:335
  5.5 14.4 %collective-permute-start.1 = (f32[24,16,128]{2,1,0:T(8,128)S(1)}, f32[24,16,128]{2,1,0:T(8,128)S(1)}, u32[]{:S(2)}, u32[]{:S(2)}) collective-permute-start(f32[24,16,128]{2,1,0:T(8,128)S(1)} %get-tuple-element.153.refs_4_.refs_8_), channel_id=1, source_target_pairs={{0,28},{4,8},{8,4},{12,16},{16,12},{20,24},{24,20},{28,0},{1,29},{... | collective-permute-start | bytes 589832 | tf_op jit(solution)/shard_map/ppermute | solution.py:335
  9.1 20.5 %collective-permute-start.12 = (f32[24,16,128]{2,1,0:T(8,128)S(1)}, f32[24,16,128]{2,1,0:T(8,128)S(1)}, u32[]{:S(2)}, u32[]{:S(2)}) collective-permute-start(f32[24,16,128]{2,1,0:T(8,128)S(1)} %get-tuple-element.164.refs_3_.refs_7_), channel_id=1, source_target_pairs={{0,4},{4,0},{8,12},{12,8},{16,20},{20,16},{24,28},{28,24},{1,5},{5... | collective-permute-start | bytes 589832 | tf_op jit(solution)/shard_map/ppermute | solution.py:335
  9.1 20.5 %collective-permute-start.13 = (f32[24,16,128]{2,1,0:T(8,128)S(1)}, f32[24,16,128]{2,1,0:T(8,128)S(1)}, u32[]{:S(2)}, u32[]{:S(2)}) collective-permute-start(f32[24,16,128]{2,1,0:T(8,128)S(1)} %get-tuple-element.165.refs_4_.refs_8_), channel_id=1, source_target_pairs={{0,28},{4,8},{8,4},{12,16},{16,12},{20,24},{24,20},{28,0},{1,29},{... | collective-permute-start | bytes 589832 | tf_op jit(solution)/shard_map/ppermute | solution.py:335
  24.2 11.7 %collective-permute-start.2 = (f32[24,16,128]{2,1,0:T(8,128)S(1)}, f32[24,16,128]{2,1,0:T(8,128)S(1)}, u32[]{:S(2)}, u32[]{:S(2)}) collective-permute-start(f32[24,16,128]{2,1,0:T(8,128)S(1)} %get-tuple-element.154.refs_3_.refs_7_), channel_id=1, source_target_pairs={{0,4},{4,0},{8,12},{12,8},{16,20},{20,16},{24,28},{28,24},{1,5},{5... | collective-permute-start | bytes 589832 | tf_op jit(solution)/shard_map/ppermute | solution.py:335
  33.9 15.1 %collective-permute-start.14 = (f32[24,16,128]{2,1,0:T(8,128)S(1)}, f32[24,16,128]{2,1,0:T(8,128)S(1)}, u32[]{:S(2)}, u32[]{:S(2)}) collective-permute-start(f32[24,16,128]{2,1,0:T(8,128)S(1)} %get-tuple-element.166.refs_3_.refs_7_), channel_id=1, source_target_pairs={{0,4},{4,0},{8,12},{12,8},{16,20},{20,16},{24,28},{28,24},{1,5},{5... | collective-permute-start | bytes 589832 | tf_op jit(solution)/shard_map/ppermute | solution.py:335
  34.0 15.1 %collective-permute-start.15 = (f32[24,16,128]{2,1,0:T(8,128)S(1)}, f32[24,16,128]{2,1,0:T(8,128)S(1)}, u32[]{:S(2)}, u32[]{:S(2)}) collective-permute-start(f32[24,16,128]{2,1,0:T(8,128)S(1)} %get-tuple-element.167.refs_4_.refs_8_), channel_id=1, source_target_pairs={{0,28},{4,8},{8,4},{12,16},{16,12},{20,24},{24,20},{28,0},{1,29},{... | collective-permute-start | bytes 589832 | tf_op jit(solution)/shard_map/ppermute | solution.py:335
  40.1 15.2 %collective-permute-start.4 = (f32[24,16,128]{2,1,0:T(8,128)S(1)}, f32[24,16,128]{2,1,0:T(8,128)S(1)}, u32[]{:S(2)}, u32[]{:S(2)}) collective-permute-start(f32[24,16,128]{2,1,0:T(8,128)S(1)} %get-tuple-element.156.refs_3_.refs_7_), channel_id=1, source_target_pairs={{0,4},{4,0},{8,12},{12,8},{16,20},{20,16},{24,28},{28,24},{1,5},{5... | collective-permute-start | bytes 589832 | tf_op jit(solution)/shard_map/ppermute | solution.py:335
  40.8 14.5 %collective-permute-start.5 = (f32[24,16,128]{2,1,0:T(8,128)S(1)}, f32[24,16,128]{2,1,0:T(8,128)S(1)}, u32[]{:S(2)}, u32[]{:S(2)}) collective-permute-start(f32[24,16,128]{2,1,0:T(8,128)S(1)} %get-tuple-element.157.refs_4_.refs_8_), channel_id=1, source_target_pairs={{0,28},{4,8},{8,4},{12,16},{16,12},{20,24},{24,20},{28,0},{1,29},{... | collective-permute-start | bytes 589832 | tf_op jit(solution)/shard_map/ppermute | solution.py:335
  59.6 13.4 %collective-permute-start.6 = (f32[24,16,128]{2,1,0:T(8,128)S(1)}, f32[24,16,128]{2,1,0:T(8,128)S(1)}, u32[]{:S(2)}, u32[]{:S(2)}) collective-permute-start(f32[24,16,128]{2,1,0:T(8,128)S(1)} %get-tuple-element.158.refs_3_), channel_id=1, source_target_pairs={{0,4},{4,0},{8,12},{12,8},{16,20},{20,16},{24,28},{28,24},{1,5},{5... | collective-permute-start | bytes 589832 | tf_op jit(solution)/shard_map/ppermute | solution.py:335
  59.7 13.2 %collective-permute-start.7 = (f32[24,16,128]{2,1,0:T(8,128)S(1)}, f32[24,16,128]{2,1,0:T(8,128)S(1)}, u32[]{:S(2)}, u32[]{:S(2)}) collective-permute-start(f32[24,16,128]{2,1,0:T(8,128)S(1)} %get-tuple-element.159.refs_4_), channel_id=1, source_target_pairs={{0,28},{4,8},{8,4},{12,16},{16,12},{20,24},{24,20},{28,0},{1,29},{... | collective-permute-start | bytes 589832 | tf_op jit(solution)/shard_map/ppermute | solution.py:335
  66.9 12.3 %collective-permute-start.18 = (f32[24,16,128]{2,1,0:T(8,128)S(1)}, f32[24,16,128]{2,1,0:T(8,128)S(1)}, u32[]{:S(2)}, u32[]{:S(2)}) collective-permute-start(f32[24,16,128]{2,1,0:T(8,128)S(1)} %get-tuple-element.170.refs_3_), channel_id=1, source_target_pairs={{0,4},{4,0},{8,12},{12,8},{16,20},{20,16},{24,28},{28,24},{1,5},{5... | collective-permute-start | bytes 589832 | tf_op jit(solution)/shard_map/ppermute | solution.py:335
  77.2 16.0 %collective-permute-start.8 = (f32[24,16,128]{2,1,0:T(8,128)S(1)}, f32[24,16,128]{2,1,0:T(8,128)S(1)}, u32[]{:S(2)}, u32[]{:S(2)}) collective-permute-start(f32[24,16,128]{2,1,0:T(8,128)S(1)} %get-tuple-element.177.refs_3_.refs_9_.refs_7_), channel_id=1, source_target_pairs={{0,4},{4,0},{8,12},{12,8},{16,20},{20,16},{24,28},{28,24},{1,5},{5... | collective-permute-start | bytes 589832 | tf_op jit(solution)/shard_map/ppermute | solution.py:335
  77.3 17.4 %collective-permute-start.9 = (f32[24,16,128]{2,1,0:T(8,128)S(1)}, f32[24,16,128]{2,1,0:T(8,128)S(1)}, u32[]{:S(2)}, u32[]{:S(2)}) collective-permute-start(f32[24,16,128]{2,1,0:T(8,128)S(1)} %get-tuple-element.178.refs_4_.refs_10_.refs_8_), channel_id=1, source_target_pairs={{0,28},{4,8},{8,4},{12,16},{16,12},{20,24},{24,20},{28,0},{1,29},{... | collective-permute-start | bytes 589832 | tf_op jit(solution)/shard_map/ppermute | solution.py:335
  83.6 15.7 %collective-permute-start.27 = (f32[24,16,128]{2,1,0:T(8,128)S(1)}, f32[24,16,128]{2,1,0:T(8,128)S(1)}, u32[]{:S(2)}, u32[]{:S(2)}) collective-permute-start(f32[24,16,128]{2,1,0:T(8,128)S(1)} %get-tuple-element.190.refs_3_.refs_7_), channel_id=1, source_target_pairs={{0,4},{4,0},{8,12},{12,8},{16,20},{20,16},{24,28},{28,24},{1,5},{5... | collective-permute-start | bytes 589832 | tf_op jit(solution)/shard_map/ppermute | solution.py:335
  83.8 15.7 %collective-permute-start.28 = (f32[24,16,128]{2,1,0:T(8,128)S(1)}, f32[24,16,128]{2,1,0:T(8,128)S(1)}, u32[]{:S(2)}, u32[]{:S(2)}) collective-permute-start(f32[24,16,128]{2,1,0:T(8,128)S(1)} %get-tuple-element.191.refs_4_.refs_8_), channel_id=1, source_target_pairs={{0,28},{4,8},{8,4},{12,16},{16,12},{20,24},{24,20},{28,0},{1,29},{... | collective-permute-start | bytes 589832 | tf_op jit(solution)/shard_map/ppermute | solution.py:335
  93.2 12.9 %collective-permute-start.20 = (f32[12,32,128]{2,1,0:T(8,128)S(1)}, f32[12,32,128]{2,1,0:T(8,128)S(1)}, u32[]{:S(2)}, u32[]{:S(2)}) collective-permute-start(f32[12,32,128]{2,1,0:T(8,128)S(1)} %get-tuple-element.173), channel_id=1, source_target_pairs={{0,1},{1,0},{2,3},{3,2},{4,5},{5,4},{6,7},{7,6},{8,9},{9,8},{10,11... | collective-permute-start | bytes 589832 | tf_op jit(solution)/shard_map/ppermute | solution.py:339
  93.2 13.0 %collective-permute-start.21 = (f32[12,32,128]{2,1,0:T(8,128)S(1)}, f32[12,32,128]{2,1,0:T(8,128)S(1)}, u32[]{:S(2)}, u32[]{:S(2)}) collective-permute-start(f32[12,32,128]{2,1,0:T(8,128)S(1)} %get-tuple-element.174), channel_id=1, source_target_pairs={{0,2},{1,3},{2,0},{3,1},{4,6},{5,7},{6,4},{7,5},{8,10},{9,11},{10,... | collective-permute-start | bytes 589832 | tf_op jit(solution)/shard_map/ppermute | solution.py:339
  94.7 11.6 %collective-permute-start.22 = (f32[12,32,128]{2,1,0:T(8,128)S(1)}, f32[12,32,128]{2,1,0:T(8,128)S(1)}, u32[]{:S(2)}, u32[]{:S(2)}) collective-permute-start(f32[12,32,128]{2,1,0:T(8,128)S(1)} %get-tuple-element.175), channel_id=1, source_target_pairs={{0,3},{1,2},{2,1},{3,0},{4,7},{5,6},{6,5},{7,4},{8,11},{9,10},{10,... | collective-permute-start | bytes 589832 | tf_op jit(solution)/shard_map/ppermute | solution.py:339
  99.4 12.0 %collective-permute-start.10 = (f32[24,16,128]{2,1,0:T(8,128)S(1)}, f32[24,16,128]{2,1,0:T(8,128)S(1)}, u32[]{:S(2)}, u32[]{:S(2)}) collective-permute-start(f32[24,16,128]{2,1,0:T(8,128)S(1)} %get-tuple-element.196.refs_3_.refs_7_), channel_id=1, source_target_pairs={{0,4},{4,0},{8,12},{12,8},{16,20},{20,16},{24,28},{28,24},{1,5},{5... | collective-permute-start | bytes 589832 | tf_op jit(solution)/shard_map/ppermute | solution.py:335
  99.4 12.3 %collective-permute-start.11 = (f32[24,16,128]{2,1,0:T(8,128)S(1)}, f32[24,16,128]{2,1,0:T(8,128)S(1)}, u32[]{:S(2)}, u32[]{:S(2)}) collective-permute-start(f32[24,16,128]{2,1,0:T(8,128)S(1)} %get-tuple-element.197.refs_4_.refs_8_), channel_id=1, source_target_pairs={{0,28},{4,8},{8,4},{12,16},{16,12},{20,24},{24,20},{28,0},{1,29},{... | collective-permute-start | bytes 589832 | tf_op jit(solution)/shard_map/ppermute | solution.py:335
  106.1 14.4 %collective-permute-start.37 = (f32[12,32,128]{2,1,0:T(8,128)S(1)}, f32[12,32,128]{2,1,0:T(8,128)S(1)}, u32[]{:S(2)}, u32[]{:S(2)}) collective-permute-start(f32[12,32,128]{2,1,0:T(8,128)S(1)} %get-tuple-element.209), channel_id=1, source_target_pairs={{0,1},{1,0},{2,3},{3,2},{4,5},{5,4},{6,7},{7,6},{8,9},{9,8},{10,11... | collective-permute-start | bytes 589832 | tf_op jit(solution)/shard_map/ppermute | solution.py:339
  106.2 15.8 %collective-permute-start.29 = (f32[24,16,128]{2,1,0:T(8,128)S(1)}, f32[24,16,128]{2,1,0:T(8,128)S(1)}, u32[]{:S(2)}, u32[]{:S(2)}) collective-permute-start(f32[24,16,128]{2,1,0:T(8,128)S(1)} %get-tuple-element.212.refs_3_.refs_7_), channel_id=1, source_target_pairs={{0,4},{4,0},{8,12},{12,8},{16,20},{20,16},{24,28},{28,24},{1,5},{5... | collective-permute-start | bytes 589832 | tf_op jit(solution)/shard_map/ppermute | solution.py:335
  116.0 12.3 %collective-permute-start.23 = (f32[24,16,128]{2,1,0:T(8,128)S(1)}, f32[24,16,128]{2,1,0:T(8,128)S(1)}, u32[]{:S(2)}, u32[]{:S(2)}) collective-permute-start(f32[24,16,128]{2,1,0:T(8,128)S(1)} %get-tuple-element.218.refs_3_.refs_7_), channel_id=1, source_target_pairs={{0,4},{4,0},{8,12},{12,8},{16,20},{20,16},{24,28},{28,24},{1,5},{5... | collective-permute-start | bytes 589832 | tf_op jit(solution)/shard_map/ppermute | solution.py:335
  116.1 14.6 %collective-permute-start.24 = (f32[24,16,128]{2,1,0:T(8,128)S(1)}, f32[24,16,128]{2,1,0:T(8,128)S(1)}, u32[]{:S(2)}, u32[]{:S(2)}) collective-permute-start(f32[24,16,128]{2,1,0:T(8,128)S(1)} %get-tuple-element.219.refs_4_.refs_8_), channel_id=1, source_target_pairs={{0,28},{4,8},{8,4},{12,16},{16,12},{20,24},{24,20},{28,0},{1,29},{... | collective-permute-start | bytes 589832 | tf_op jit(solution)/shard_map/ppermute | solution.py:335
  120.5 14.6 %collective-permute-start.38 = (f32[12,32,128]{2,1,0:T(8,128)S(1)}, f32[12,32,128]{2,1,0:T(8,128)S(1)}, u32[]{:S(2)}, u32[]{:S(2)}) collective-permute-start(f32[12,32,128]{2,1,0:T(8,128)S(1)} %get-tuple-element.210), channel_id=1, source_target_pairs={{0,2},{1,3},{2,0},{3,1},{4,6},{5,7},{6,4},{7,5},{8,10},{9,11},{10,... | collective-permute-start | bytes 589832 | tf_op jit(solution)/shard_map/ppermute | solution.py:339
  122.6 19.0 %collective-permute-start.39 = (f32[12,32,128]{2,1,0:T(8,128)S(1)}, f32[12,32,128]{2,1,0:T(8,128)S(1)}, u32[]{:S(2)}, u32[]{:S(2)}) collective-permute-start(f32[12,32,128]{2,1,0:T(8,128)S(1)} %get-tuple-element.211), channel_id=1, source_target_pairs={{0,3},{1,2},{2,1},{3,0},{4,7},{5,6},{6,5},{7,4},{8,11},{9,10},{10,... | collective-permute-start | bytes 589832 | tf_op jit(solution)/shard_map/ppermute | solution.py:339
  128.3 13.4 %collective-permute-start.35 = (f32[24,16,128]{2,1,0:T(8,128)S(1)}, f32[24,16,128]{2,1,0:T(8,128)S(1)}, u32[]{:S(2)}, u32[]{:S(2)}) collective-permute-start(f32[24,16,128]{2,1,0:T(8,128)S(1)} %get-tuple-element.229.refs_3_.refs_7_), channel_id=1, source_target_pairs={{0,4},{4,0},{8,12},{12,8},{16,20},{20,16},{24,28},{28,24},{1,5},{5... | collective-permute-start | bytes 589832 | tf_op jit(solution)/shard_map/ppermute | solution.py:335
  128.3 13.4 %collective-permute-start.36 = (f32[24,16,128]{2,1,0:T(8,128)S(1)}, f32[24,16,128]{2,1,0:T(8,128)S(1)}, u32[]{:S(2)}, u32[]{:S(2)}) collective-permute-start(f32[24,16,128]{2,1,0:T(8,128)S(1)} %get-tuple-element.230.refs_4_.refs_8_), channel_id=1, source_target_pairs={{0,28},{4,8},{8,4},{12,16},{16,12},{20,24},{24,20},{28,0},{1,29},{... | collective-permute-start | bytes 589832 | tf_op jit(solution)/shard_map/ppermute | solution.py:335
  135.2 20.0 %collective-permute-start.31 = (f32[24,16,128]{2,1,0:T(8,128)S(1)}, f32[24,16,128]{2,1,0:T(8,128)S(1)}, u32[]{:S(2)}, u32[]{:S(2)}) collective-permute-start(f32[24,16,128]{2,1,0:T(8,128)S(1)} %get-tuple-element.198.refs_3_), channel_id=1, source_target_pairs={{0,4},{4,0},{8,12},{12,8},{16,20},{20,16},{24,28},{28,24},{1,5},{5... | collective-permute-start | bytes 589832 | tf_op jit(solution)/shard_map/ppermute | solution.py:335
  141.7 13.5 %collective-permute-start.32 = (f32[24,16,128]{2,1,0:T(8,128)S(1)}, f32[24,16,128]{2,1,0:T(8,128)S(1)}, u32[]{:S(2)}, u32[]{:S(2)}) collective-permute-start(f32[24,16,128]{2,1,0:T(8,128)S(1)} %get-tuple-element.199.refs_4_), channel_id=1, source_target_pairs={{0,28},{4,8},{8,4},{12,16},{16,12},{20,24},{24,20},{28,0},{1,29},{... | collective-permute-start | bytes 589832 | tf_op jit(solution)/shard_map/ppermute | solution.py:335
  146.0 24.0 %collective-permute-start.43 = (f32[24,16,128]{2,1,0:T(8,128)S(1)}, f32[24,16,128]{2,1,0:T(8,128)S(1)}, u32[]{:S(2)}, u32[]{:S(2)}) collective-permute-start(f32[24,16,128]{2,1,0:T(8,128)S(1)} %get-tuple-element.214.refs_3_), channel_id=1, source_target_pairs={{0,4},{4,0},{8,12},{12,8},{16,20},{20,16},{24,28},{28,24},{1,5},{5... | collective-permute-start | bytes 589832 | tf_op jit(solution)/shard_map/ppermute | solution.py:335
  146.4 23.5 %collective-permute-start.44 = (f32[24,16,128]{2,1,0:T(8,128)S(1)}, f32[24,16,128]{2,1,0:T(8,128)S(1)}, u32[]{:S(2)}, u32[]{:S(2)}) collective-permute-start(f32[24,16,128]{2,1,0:T(8,128)S(1)} %get-tuple-element.215.refs_4_), channel_id=1, source_target_pairs={{0,28},{4,8},{8,4},{12,16},{16,12},{20,24},{24,20},{28,0},{1,29},{... | collective-permute-start | bytes 589832 | tf_op jit(solution)/shard_map/ppermute | solution.py:335
  159.4 16.8 %collective-permute-start.40 = (f32[24,16,128]{2,1,0:T(8,128)S(1)}, f32[24,16,128]{2,1,0:T(8,128)S(1)}, u32[]{:S(2)}, u32[]{:S(2)}) collective-permute-start(f32[24,16,128]{2,1,0:T(8,128)S(1)} %get-tuple-element.220.refs_9_.refs_3_), channel_id=1, source_target_pairs={{0,4},{4,0},{8,12},{12,8},{16,20},{20,16},{24,28},{28,24},{1,5},{5... | collective-permute-start | bytes 589832 | tf_op jit(solution)/shard_map/ppermute | solution.py:335
  161.1 16.7 %collective-permute-start.41 = (f32[24,16,128]{2,1,0:T(8,128)S(1)}, f32[24,16,128]{2,1,0:T(8,128)S(1)}, u32[]{:S(2)}, u32[]{:S(2)}) collective-permute-start(f32[24,16,128]{2,1,0:T(8,128)S(1)} %get-tuple-element.221.refs_10_.refs_4_), channel_id=1, source_target_pairs={{0,28},{4,8},{8,4},{12,16},{16,12},{20,24},{24,20},{28,0},{1,29},{... | collective-permute-start | bytes 589832 | tf_op jit(solution)/shard_map/ppermute | solution.py:335
  174.3 17.0 %collective-permute-start.45 = (f32[12,32,128]{2,1,0:T(8,128)S(1)}, f32[12,32,128]{2,1,0:T(8,128)S(1)}, u32[]{:S(2)}, u32[]{:S(2)}) collective-permute-start(f32[12,32,128]{2,1,0:T(8,128)S(1)} %get-tuple-element.232), channel_id=1, source_target_pairs={{0,1},{1,0},{2,3},{3,2},{4,5},{5,4},{6,7},{7,6},{8,9},{9,8},{10,11... | collective-permute-start | bytes 589832 | tf_op jit(solution)/shard_map/ppermute | solution.py:339
  174.4 16.9 %collective-permute-start.46 = (f32[12,32,128]{2,1,0:T(8,128)S(1)}, f32[12,32,128]{2,1,0:T(8,128)S(1)}, u32[]{:S(2)}, u32[]{:S(2)}) collective-permute-start(f32[12,32,128]{2,1,0:T(8,128)S(1)} %get-tuple-element.233), channel_id=1, source_target_pairs={{0,2},{1,3},{2,0},{3,1},{4,6},{5,7},{6,4},{7,5},{8,10},{9,11},{10,... | collective-permute-start | bytes 589832 | tf_op jit(solution)/shard_map/ppermute | solution.py:339
  175.6 15.7 %collective-permute-start.47 = (f32[12,32,128]{2,1,0:T(8,128)S(1)}, f32[12,32,128]{2,1,0:T(8,128)S(1)}, u32[]{:S(2)}, u32[]{:S(2)}) collective-permute-start(f32[12,32,128]{2,1,0:T(8,128)S(1)} %get-tuple-element.234), channel_id=1, source_target_pairs={{0,3},{1,2},{2,1},{3,0},{4,7},{5,6},{6,5},{7,4},{8,11},{9,10},{10,... | collective-permute-start | bytes 589832 | tf_op jit(solution)/shard_map/ppermute | solution.py:339
  176.2 21.0 %collective-permute-start.51 = (f32[24,16,128]{2,1,0:T(8,128)S(1)}, f32[24,16,128]{2,1,0:T(8,128)S(1)}, u32[]{:S(2)}, u32[]{:S(2)}) collective-permute-start(f32[24,16,128]{2,1,0:T(8,128)S(1)} %get-tuple-element.244.refs_3_), channel_id=1, source_target_pairs={{0,4},{4,0},{8,12},{12,8},{16,20},{20,16},{24,28},{28,24},{1,5},{5... | collective-permute-start | bytes 589832 | tf_op jit(solution)/shard_map/ppermute | solution.py:335
  177.8 19.4 %collective-permute-start.52 = (f32[24,16,128]{2,1,0:T(8,128)S(1)}, f32[24,16,128]{2,1,0:T(8,128)S(1)}, u32[]{:S(2)}, u32[]{:S(2)}) collective-permute-start(f32[24,16,128]{2,1,0:T(8,128)S(1)} %get-tuple-element.245.refs_4_), channel_id=1, source_target_pairs={{0,28},{4,8},{8,4},{12,16},{16,12},{20,24},{24,20},{28,0},{1,29},{... | collective-permute-start | bytes 589832 | tf_op jit(solution)/shard_map/ppermute | solution.py:335
  218.6 18.9 %collective-permute-start.64 = (f32[128,128]{1,0:T(8,128)S(1)}, f32[128,128]{1,0:T(8,128)S(1)}, u32[]{:S(2)}, u32[]{:S(2)}) collective-permute-start(f32[128,128]{1,0:T(8,128)S(1)} %cross.1), channel_id=1, source_target_pairs={{0,16},{4,20},{8,24},{12,28},{16,0},{20,4},{24,8},{28,12},{1,17},{... | collective-permute-start | bytes 196616 | tf_op jit(solution)/shard_map/ppermute | solution.py:339
  218.6 18.9 %collective-permute-start.63 = (f32[128,128]{1,0:T(8,128)S(1)}, f32[128,128]{1,0:T(8,128)S(1)}, u32[]{:S(2)}, u32[]{:S(2)}) collective-permute-start(f32[128,128]{1,0:T(8,128)S(1)} %cross.1), channel_id=1, source_target_pairs={{0,8},{4,12},{8,0},{12,4},{16,24},{20,28},{24,16},{28,20},{1,9},{5... | collective-permute-start | bytes 196616 | tf_op jit(solution)/shard_map/ppermute | solution.py:339
  224.5 13.0 %collective-permute-start.62 = (f32[128,128]{1,0:T(8,128)S(1)}, f32[128,128]{1,0:T(8,128)S(1)}, u32[]{:S(2)}, u32[]{:S(2)}) collective-permute-start(f32[128,128]{1,0:T(8,128)S(1)} %turn_cross.1), channel_id=1, source_target_pairs={{0,24},{4,28},{8,16},{12,20},{16,8},{20,12},{24,0},{28,4},{1,25},{... | collective-permute-start | bytes 196616 | tf_op jit(solution)/shard_map/ppermute | solution.py:339
  225.7 11.8 %collective-permute-start.61 = (f32[128,128]{1,0:T(8,128)S(1)}, f32[128,128]{1,0:T(8,128)S(1)}, u32[]{:S(2)}, u32[]{:S(2)}) collective-permute-start(f32[128,128]{1,0:T(8,128)S(1)} %turn_cross.1), channel_id=1, source_target_pairs={{0,16},{4,20},{8,24},{12,28},{16,0},{20,4},{24,8},{28,12},{1,17},{... | collective-permute-start | bytes 196616 | tf_op jit(solution)/shard_map/ppermute | solution.py:339
  226.1 11.5 %collective-permute-start.60 = (f32[128,128]{1,0:T(8,128)S(1)}, f32[128,128]{1,0:T(8,128)S(1)}, u32[]{:S(2)}, u32[]{:S(2)}) collective-permute-start(f32[128,128]{1,0:T(8,128)S(1)} %turn_cross.1), channel_id=1, source_target_pairs={{0,8},{4,12},{8,0},{12,4},{16,24},{20,28},{24,16},{28,20},{1,9},{5... | collective-permute-start | bytes 196616 | tf_op jit(solution)/shard_map/ppermute | solution.py:339
  237.6 12.9 %collective-permute-start.71 = (f32[12,32,128]{2,1,0:T(8,128)S(1)}, f32[12,32,128]{2,1,0:T(8,128)S(1)}, u32[]{:S(2)}, u32[]{:S(2)}) collective-permute-start(f32[12,32,128]{2,1,0:T(8,128)S(1)} %get-tuple-element.284), channel_id=1, source_target_pairs={{0,1},{1,0},{2,3},{3,2},{4,5},{5,4},{6,7},{7,6},{8,9},{9,8},{10,11... | collective-permute-start | bytes 589832 | tf_op jit(solution)/shard_map/ppermute | solution.py:339
  237.7 12.8 %collective-permute-start.72 = (f32[12,32,128]{2,1,0:T(8,128)S(1)}, f32[12,32,128]{2,1,0:T(8,128)S(1)}, u32[]{:S(2)}, u32[]{:S(2)}) collective-permute-start(f32[12,32,128]{2,1,0:T(8,128)S(1)} %get-tuple-element.285), channel_id=1, source_target_pairs={{0,2},{1,3},{2,0},{3,1},{4,6},{5,7},{6,4},{7,5},{8,10},{9,11},{10,... | collective-permute-start | bytes 589832 | tf_op jit(solution)/shard_map/ppermute | solution.py:339
  239.0 11.5 %collective-permute-start.73 = (f32[12,32,128]{2,1,0:T(8,128)S(1)}, f32[12,32,128]{2,1,0:T(8,128)S(1)}, u32[]{:S(2)}, u32[]{:S(2)}) collective-permute-start(f32[12,32,128]{2,1,0:T(8,128)S(1)} %get-tuple-element.286), channel_id=1, source_target_pairs={{0,3},{1,2},{2,1},{3,0},{4,7},{5,6},{6,5},{7,4},{8,11},{9,10},{10,... | collective-permute-start | bytes 589832 | tf_op jit(solution)/shard_map/ppermute | solution.py:339
  (27 other events, 194.4 us)

commit v8 on v7

--- a/solution.py
+++ b/solution.py
@@ -11,8 +11,6 @@
 UNROLL = 72
 CHUNK = 24
 TURNS = 3
-TIE_HALO = 0
-TIE_FIRST = 1
 APPLY_BYTES = 4 << 20
 F32, BF16, I32 = jnp.float32, jnp.bfloat16, jnp.int32
 precise = lax.Precision.HIGHEST
@@ -429,27 +427,26 @@
     (image_first,) = call(
         cross_kernel, "cross", [square], ids, panel, gram_first, *image, scalars=1, scratch=[held]
     )
+    turned, gram_last = call(
+        turn_kernel, "turn", [wide, square], ids, inverse_first, *swapped(parts), scalars=1, scratch=[held]
+    )
     first, _ = apply(meta, now[0], halos[0])
-    arrived, first = lax.optimization_barrier((swapped(parts), first))
-    turned, gram_last = call(
-        turn_kernel, "turn", [wide, square], ids, inverse_first, *arrived, scalars=1, scratch=[held]
-    )
     gram = gram_last
-    rounds = rounds_of("col", "node")
-    for i, each_round in enumerate(rounds):
-        got = round_swaps(gram, *each_round)
-        if i == TIE_HALO:
+    hops = hops_of("col", "node")
+    for i, hop in enumerate(hops):
+        got = swap(gram, *hop)
+        if i == 1:
             got, halos[1] = lax.optimization_barrier((got, halos[1]))
             _, parts = apply(meta, now[1], halos[1], (), first, count)
             (image_last,) = call(
                 turn_cross_kernel, "turn_cross", [square], ids, inverse_first, turned, gram_last,
                 *swapped(parts), scalars=1, scratch=[held],
             )
-        if i == len(rounds) - TIE_FIRST:
+        if i == len(hops) - 2:
             got, image_first = lax.optimization_barrier((got, image_first))
-        if i == len(rounds) - 1:
+        if i == len(hops) - 1:
             got, image_last = lax.optimization_barrier((got, image_last))
-        gram = round_sum(gram, got)
+        gram = gram + got
     inverse_last = inverse_factor(gram, nodes)
     parts = call(
         basis_kernel, "basis", [(quarter, cols_here, block)] * count, ids, inverse_last, turned,

time: 253 us -> 243 us (0.960)
  waiting for transfers between devices: 29.9 us -> 21.6 us
    ppermute x38 -> x36, waiting for transfers between devices: 27.2 us -> 19.6 us  [swap(): lax.ppermute(value, axis, [(i, i ^ hop) for i in range(lax.axis_size(axis...]
    ppermute x38 -> x36, starting transfers between devices: 31.9 us -> 29.6 us  [swap(): lax.ppermute(value, axis, [(i, i ^ hop) for i in range(lax.axis_size(axis...]
  transfers between devices with their start and end apart: 74 -> 72, of which waited for: 13 -> 11; matrix products, arithmetic and copies ran while one was open for 0% -> 0% of each run, Pallas kernels for 45% -> 47%
where the time goes in v8:
time: 243 us
  Pallas kernels  117 us (48%)
  starting transfers between devices  101 us (42%)
  waiting for transfers between devices  21.6 us (9%)
    pallas_call x18, Pallas kernels, apply(): pl.pallas_call(functools.partial(apply_kernel, bool(old), bool(mate)), in...  78.4 us
    ppermute x18, starting transfers between devices, exchange(): lax.ppermute(pair[1], 'node', odd)  56.8 us
    pallas_call x10, Pallas kernels, call(): pl.pallas_call(kernel, in_specs=[IN_SMEM] * scalars + [IN_VMEM] * (len(ar...  29.8 us
    ppermute x36, starting transfers between devices, swap(): lax.ppermute(value, axis, [(i, i ^ hop) for i in range(lax.axis_size(axis...  29.6 us
    ppermute x36, waiting for transfers between devices, swap(): lax.ppermute(value, axis, [(i, i ^ hop) for i in range(lax.axis_size(axis...  19.6 us
    ppermute x18, starting transfers between devices, exchange(): lax.ppermute(pair[0], 'node', even)  14.5 us
    pallas_call x1, Pallas kernels, prep(): pl.pallas_call(functools.partial(prep_kernel, rows), in_specs=[IN_SMEM] *...  8.92 us
  transfers between devices with their start and end apart: 72, of which 11 were waited for; matrix products, arithmetic and copies ran while one was open for 0% of the time, Pallas kernels for 47%

profile of v8, /device:TPU:0, one launch (start us, length us, event | category | flops | bytes accessed | tf_op | source)
XLA Modules:
  0.0 242.7 jit_solution(10180979311910082650)
XLA Ops:
  2.5 3.0 %collective-permute-start = (f32[24,16,128]{2,1,0:T(8,128)S(1)}, f32[24,16,128]{2,1,0:T(8,128)S(1)}, u32[]{:S(2)}, u32[]{:S(2)}) collective-permute-start(f32[24,16,128]{2,1,0:T(8,128)S(1)} %get-tuple-element.144.refs_3_.refs_7_), channel_id=1, source_target_pairs={{0,4},{4,0},{8,12},{12,8},{16,20},{20,16},{24,28},{28,24},{1,5},{5... | collective-permute-start | bytes 589832 | tf_op jit(solution)/shard_map/ppermute | solution.py:333
  5.5 3.5 %collective-permute-start.1 = (f32[24,16,128]{2,1,0:T(8,128)S(1)}, f32[24,16,128]{2,1,0:T(8,128)S(1)}, u32[]{:S(2)}, u32[]{:S(2)}) collective-permute-start(f32[24,16,128]{2,1,0:T(8,128)S(1)} %get-tuple-element.145.refs_4_.refs_8_), channel_id=1, source_target_pairs={{0,28},{4,8},{8,4},{12,16},{16,12},{20,24},{24,20},{28,0},{1,29},{... | collective-permute-start | bytes 589832 | tf_op jit(solution)/shard_map/ppermute | solution.py:333
  9.1 1.9 collective-permute-start.13
  11.0 8.9 %prep.1 = (bf16[288,128,256]{2,1,0:T(8,128)(2,1)S(1)}, f32[48,1,128]{2,1,0:T(1,128)S(1)}, s32[578]{0:T(1024)S(1)}) custom-call(s32[2]{0:T(128)S(1)} %pad_add_fusion.ids_ref, s32[1,288]{1,0:T(1,128)} %own_ref.1, s32[1,288]{1,0:T(1,128)} %col_ref.1, f32[288,128,128]{2,1,0:T(8,128)} %blk_ref.1), custom_call_target="tpu_custom_call" | custom-call | flops 1207959552 | bytes 18874368 | tf_op jit(solution)/shard_map/prep/pallas_call | solution.py:115
  19.9 4.3 %apply.4 = (f32[24,16,128]{2,1,0:T(8,128)S(1)}, f32[24,16,128]{2,1,0:T(8,128)S(1)}) custom-call(s32[578]{0:T(1024)S(1)} %get-tuple-element.141.refs_0_, bf16[288,128,256]{2,1,0:T(8,128)(2,1)S(1)} %get-tuple-element.142.refs_1_, f32[48,1,128]{2,1,0:T(1,128)S(1)} %get-tuple-element.143.refs_2_, f32[24,16,128]{2,1,0:T(8,128)S(1)} %get-tuple-element.144.refs_3_.refs_7_, ...), custom_call_target="tpu_custom_call" | custom-call | bytes 4194304 | tf_op jit(solution)/shard_map/apply/pallas_call | solution.py:194
  26.1 3.6 %collective-permute-start.3 = (f32[24,16,128]{2,1,0:T(8,128)S(1)}, f32[24,16,128]{2,1,0:T(8,128)S(1)}, u32[]{:S(2)}, u32[]{:S(2)}) collective-permute-start(f32[24,16,128]{2,1,0:T(8,128)S(1)} %get-tuple-element.147.refs_4_.refs_8_), channel_id=1, source_target_pairs={{0,28},{4,8},{8,4},{12,16},{16,12},{20,24},{24,20},{28,0},{1,29},{... | collective-permute-start | bytes 589832 | tf_op jit(solution)/shard_map/ppermute | solution.py:333
  29.6 4.3 %apply.6 = (f32[24,16,128]{2,1,0:T(8,128)S(1)}, f32[24,16,128]{2,1,0:T(8,128)S(1)}) custom-call(s32[578]{0:T(1024)S(1)} %get-tuple-element.141.refs_0_, bf16[288,128,256]{2,1,0:T(8,128)(2,1)S(1)} %get-tuple-element.142.refs_1_, f32[48,1,128]{2,1,0:T(1,128)S(1)} %get-tuple-element.143.refs_2_, f32[24,16,128]{2,1,0:T(8,128)S(1)} %get-tuple-element.156.refs_3_.refs_7_, ...), custom_call_target="tpu_custom_call" | custom-call | bytes 4194304 | tf_op jit(solution)/shard_map/apply/pallas_call | solution.py:194
  34.0 1.9 collective-permute-start.15
  35.9 4.3 %apply_recur.10 = (f32[24,16,128]{2,1,0:T(8,128)S(1)}, f32[24,16,128]{2,1,0:T(8,128)S(1)}) custom-call(s32[578]{0:T(1024)S(1)} %get-tuple-element.141.refs_0_, bf16[288,128,256]{2,1,0:T(8,128)(2,1)S(1)} %get-tuple-element.142.refs_1_, f32[48,1,128]{2,1,0:T(1,128)S(1)} %get-tuple-element.143.refs_2_, f32[24,16,128]{2,1,0:T(8,128)S(1)} %get-tuple-element.146.refs_3_.refs_7_, ...), custom_call_target="tpu_custom_call" | custom-call | bytes 4194304 | tf_op jit(solution)/shard_map/apply_recur/pallas_call | solution.py:194
  40.8 8.2 %collective-permute-start.5 = (f32[24,16,128]{2,1,0:T(8,128)S(1)}, f32[24,16,128]{2,1,0:T(8,128)S(1)}, u32[]{:S(2)}, u32[]{:S(2)}) collective-permute-start(f32[24,16,128]{2,1,0:T(8,128)S(1)} %get-tuple-element.149.refs_4_.refs_8_), channel_id=1, source_target_pairs={{0,28},{4,8},{8,4},{12,16},{16,12},{20,24},{24,20},{28,0},{1,29},{... | collective-permute-start | bytes 589832 | tf_op jit(solution)/shard_map/ppermute | solution.py:333
  49.0 4.3 %apply_recur.13 = (f32[24,16,128]{2,1,0:T(8,128)S(1)}, f32[24,16,128]{2,1,0:T(8,128)S(1)}) custom-call(s32[578]{0:T(1024)S(1)} %get-tuple-element.141.refs_0_, bf16[288,128,256]{2,1,0:T(8,128)(2,1)S(1)} %get-tuple-element.142.refs_1_, f32[48,1,128]{2,1,0:T(1,128)S(1)} %get-tuple-element.143.refs_2_, f32[24,16,128]{2,1,0:T(8,128)S(1)} %get-tuple-element.158.refs_3_.refs_7_, ...), custom_call_target="tpu_custom_call" | custom-call | bytes 4194304 | tf_op jit(solution)/shard_map/apply_recur/pallas_call | solution.py:194
  53.4 2.0 collective-permute-start.17
  55.3 4.2 %apply_recur.11 = (f32[24,16,128]{2,1,0:T(8,128)S(1)}, f32[24,16,128]{2,1,0:T(8,128)S(1)}) custom-call(s32[578]{0:T(1024)S(1)} %get-tuple-element.141.refs_0_, bf16[288,128,256]{2,1,0:T(8,128)(2,1)S(1)} %get-tuple-element.142.refs_1_, f32[48,1,128]{2,1,0:T(1,128)S(1)} %get-tuple-element.143.refs_2_, f32[24,16,128]{2,1,0:T(8,128)S(1)} %get-tuple-element.148.refs_3_.refs_7_, ...), custom_call_target="tpu_custom_call" | custom-call | bytes 4194304 | tf_op jit(solution)/shard_map/apply_recur/pallas_call | solution.py:194
  59.7 2.9 %collective-permute-start.7 = (f32[24,16,128]{2,1,0:T(8,128)S(1)}, f32[24,16,128]{2,1,0:T(8,128)S(1)}, u32[]{:S(2)}, u32[]{:S(2)}) collective-permute-start(f32[24,16,128]{2,1,0:T(8,128)S(1)} %get-tuple-element.151.refs_4_), channel_id=1, source_target_pairs={{0,28},{4,8},{8,4},{12,16},{16,12},{20,24},{24,20},{28,0},{1,29},{... | collective-permute-start | bytes 589832 | tf_op jit(solution)/shard_map/ppermute | solution.py:333
  62.6 4.3 %apply_recur.14 = (f32[24,16,128]{2,1,0:T(8,128)S(1)}, f32[24,16,128]{2,1,0:T(8,128)S(1)}) custom-call(s32[578]{0:T(1024)S(1)} %get-tuple-element.141.refs_0_, bf16[288,128,256]{2,1,0:T(8,128)(2,1)S(1)} %get-tuple-element.142.refs_1_, f32[48,1,128]{2,1,0:T(1,128)S(1)} %get-tuple-element.143.refs_2_, f32[24,16,128]{2,1,0:T(8,128)S(1)} %get-tuple-element.160.refs_3_.refs_7_, ...), custom_call_target="tpu_custom_call" | custom-call | bytes 4194304 | tf_op jit(solution)/shard_map/apply_recur/pallas_call | solution.py:194
  68.0 4.9 %collective-permute-start.19 = (f32[24,16,128]{2,1,0:T(8,128)S(1)}, f32[24,16,128]{2,1,0:T(8,128)S(1)}, u32[]{:S(2)}, u32[]{:S(2)}) collective-permute-start(f32[24,16,128]{2,1,0:T(8,128)S(1)} %get-tuple-element.163.refs_4_), channel_id=1, source_target_pairs={{0,28},{4,8},{8,4},{12,16},{16,12},{20,24},{24,20},{28,0},{1,29},{... | collective-permute-start | bytes 589832 | tf_op jit(solution)/shard_map/ppermute | solution.py:333
  72.9 4.3 %apply_recur.12 = (f32[24,16,128]{2,1,0:T(8,128)S(1)}, f32[24,16,128]{2,1,0:T(8,128)S(1)}) custom-call(s32[578]{0:T(1024)S(1)} %get-tuple-element.141.refs_0_, bf16[288,128,256]{2,1,0:T(8,128)(2,1)S(1)} %get-tuple-element.142.refs_1_, f32[48,1,128]{2,1,0:T(1,128)S(1)} %get-tuple-element.143.refs_2_, f32[24,16,128]{2,1,0:T(8,128)S(1)} %get-tuple-element.150.refs_3_, ...), custom_call_target="tpu_custom_call" | custom-call | bytes 4194304 | tf_op jit(solution)/shard_map/apply_recur/pallas_call | solution.py:194
  77.3 1.9 collective-permute-start.9
  79.2 4.4 %apply_recur_parts.2 = (f32[24,16,128]{2,1,0:T(8,128)S(1)}, f32[24,16,128]{2,1,0:T(8,128)S(1)}, f32[12,32,128]{2,1,0:T(8,128)S(1)}, f32[12,32,128]{2,1,0:T(8,128...) custom-call(s32[578]{0:T(1024)S(1)} %get-tuple-element.141.refs_0_, ...), custom_call_target="tpu_custom_call" | custom-call | bytes 4194304 | tf_op jit(solution)/shard_map/apply_recur_parts/pallas_call | solution.py:194
  83.8 9.5 %collective-permute-start.28 = (f32[24,16,128]{2,1,0:T(8,128)S(1)}, f32[24,16,128]{2,1,0:T(8,128)S(1)}, u32[]{:S(2)}, u32[]{:S(2)}) collective-permute-start(f32[24,16,128]{2,1,0:T(8,128)S(1)} %get-tuple-element.183.refs_4_.refs_8_), channel_id=1, source_target_pairs={{0,28},{4,8},{8,4},{12,16},{16,12},{20,24},{24,20},{28,0},{1,29},{... | collective-permute-start | bytes 589832 | tf_op jit(solution)/shard_map/ppermute | solution.py:333
  95.1 4.3 %apply.5 = (f32[24,16,128]{2,1,0:T(8,128)S(1)}, f32[24,16,128]{2,1,0:T(8,128)S(1)}) custom-call(s32[578]{0:T(1024)S(1)} %get-tuple-element.141.refs_0_, bf16[288,128,256]{2,1,0:T(8,128)(2,1)S(1)} %get-tuple-element.142.refs_1_, f32[48,1,128]{2,1,0:T(1,128)S(1)} %get-tuple-element.143.refs_2_, f32[24,16,128]{2,1,0:T(8,128)S(1)} %get-tuple-element.169.refs_3_.refs_9_.refs_7_, ...), custom_call_target="tpu_custom_call" | custom-call | bytes 4194304 | tf_op jit(solution)/shard_map/apply/pallas_call | solution.py:194
  99.5 2.1 collective-permute-start.11
  101.6 4.5 %apply_parts.2 = (f32[24,16,128]{2,1,0:T(8,128)S(1)}, f32[24,16,128]{2,1,0:T(8,128)S(1)}, f32[12,32,128]{2,1,0:T(8,128)S(1)}, f32[12,32,128]{2,1,0:T(8,128)S(1)}...) custom-call(s32[578]{0:T(1024)S(1)} %get-tuple-element.141.refs_0_, ...), custom_call_target="tpu_custom_call" | custom-call | bytes 4194304 | tf_op jit(solution)/shard_map/apply_parts/pallas_call | solution.py:194
  106.3 2.7 %collective-permute-start.30 = (f32[24,16,128]{2,1,0:T(8,128)S(1)}, f32[24,16,128]{2,1,0:T(8,128)S(1)}, u32[]{:S(2)}, u32[]{:S(2)}) collective-permute-start(f32[24,16,128]{2,1,0:T(8,128)S(1)} %get-tuple-element.205.refs_4_.refs_8_), channel_id=1, source_target_pairs={{0,28},{4,8},{8,4},{12,16},{16,12},{20,24},{24,20},{28,0},{1,29},{... | collective-permute-start | bytes 589832 | tf_op jit(solution)/shard_map/ppermute | solution.py:333
  109.0 2.0 gram.1
  111.4 4.3 %apply_recur.15 = (f32[24,16,128]{2,1,0:T(8,128)S(1)}, f32[24,16,128]{2,1,0:T(8,128)S(1)}) custom-call(s32[578]{0:T(1024)S(1)} %get-tuple-element.141.refs_0_, bf16[288,128,256]{2,1,0:T(8,128)(2,1)S(1)} %get-tuple-element.142.refs_1_, f32[48,1,128]{2,1,0:T(1,128)S(1)} %get-tuple-element.143.refs_2_, f32[24,16,128]{2,1,0:T(8,128)S(1)} %get-tuple-element.188.refs_3_.refs_7_, ...), custom_call_target="tpu_custom_call" | custom-call | bytes 4194304 | tf_op jit(solution)/shard_map/apply_recur/pallas_call | solution.py:194
  121.3 4.2 %apply_recur.16 = (f32[24,16,128]{2,1,0:T(8,128)S(1)}, f32[24,16,128]{2,1,0:T(8,128)S(1)}) custom-call(s32[578]{0:T(1024)S(1)} %get-tuple-element.141.refs_0_, bf16[288,128,256]{2,1,0:T(8,128)(2,1)S(1)} %get-tuple-element.142.refs_1_, f32[48,1,128]{2,1,0:T(1,128)S(1)} %get-tuple-element.143.refs_2_, f32[24,16,128]{2,1,0:T(8,128)S(1)} %get-tuple-element.204.refs_3_.refs_7_, ...), custom_call_target="tpu_custom_call" | custom-call | bytes 4194304 | tf_op jit(solution)/shard_map/apply_recur/pallas_call | solution.py:194
  129.6 4.3 %apply_recur.17 = (f32[24,16,128]{2,1,0:T(8,128)S(1)}, f32[24,16,128]{2,1,0:T(8,128)S(1)}) custom-call(s32[578]{0:T(1024)S(1)} %get-tuple-element.141.refs_0_, bf16[288,128,256]{2,1,0:T(8,128)(2,1)S(1)} %get-tuple-element.142.refs_1_, f32[48,1,128]{2,1,0:T(1,128)S(1)} %get-tuple-element.143.refs_2_, f32[24,16,128]{2,1,0:T(8,128)S(1)} %get-tuple-element.210.refs_3_.refs_7_, ...), custom_call_target="tpu_custom_call" | custom-call | bytes 4194304 | tf_op jit(solution)/shard_map/apply_recur/pallas_call | solution.py:194
  133.9 2.0 collective-permute-start.31
  135.9 3.0 %collective-permute-done.33 = f32[128,128]{1,0:T(8,128)S(1)} collective-permute-done((f32[128,128]{1,0:T(8,128)S(1)}, f32[128,128]{1,0:T(8,128)S(1)}, u32[]{:S(2)}, u32[]{:S(2)}) %collective-permute-start.33) | collective-permute-done | bytes 65568 | tf_op jit(solution)/shard_map/ppermute | solution.py:337
  138.8 3.0 %collective-permute-start.32 = (f32[24,16,128]{2,1,0:T(8,128)S(1)}, f32[24,16,128]{2,1,0:T(8,128)S(1)}, u32[]{:S(2)}, u32[]{:S(2)}) collective-permute-start(f32[24,16,128]{2,1,0:T(8,128)S(1)} %get-tuple-element.191.refs_4_), channel_id=1, source_target_pairs={{0,28},{4,8},{8,4},{12,16},{16,12},{20,24},{24,20},{28,0},{1,29},{... | collective-permute-start | bytes 589832 | tf_op jit(solution)/shard_map/ppermute | solution.py:333
  141.8 4.3 %apply_recur.18 = (f32[24,16,128]{2,1,0:T(8,128)S(1)}, f32[24,16,128]{2,1,0:T(8,128)S(1)}) custom-call(s32[578]{0:T(1024)S(1)} %get-tuple-element.141.refs_0_, bf16[288,128,256]{2,1,0:T(8,128)(2,1)S(1)} %get-tuple-element.142.refs_1_, f32[48,1,128]{2,1,0:T(1,128)S(1)} %get-tuple-element.143.refs_2_, f32[24,16,128]{2,1,0:T(8,128)S(1)} %get-tuple-element.221.refs_3_.refs_7_, ...), custom_call_target="tpu_custom_call" | custom-call | bytes 4194304 | tf_op jit(solution)/shard_map/apply_recur/pallas_call | solution.py:194
  149.7 6.2 %collective-permute-done.34 = f32[128,128]{1,0:T(8,128)S(1)} collective-permute-done((f32[128,128]{1,0:T(8,128)S(1)}, f32[128,128]{1,0:T(8,128)S(1)}, u32[]{:S(2)}, u32[]{:S(2)}) %collective-permute-start.34) | collective-permute-done | bytes 65568 | tf_op jit(solution)/shard_map/ppermute | solution.py:337
  156.2 4.3 %apply_recur.19 = (f32[24,16,128]{2,1,0:T(8,128)S(1)}, f32[24,16,128]{2,1,0:T(8,128)S(1)}) custom-call(s32[578]{0:T(1024)S(1)} %get-tuple-element.141.refs_0_, bf16[288,128,256]{2,1,0:T(8,128)(2,1)S(1)} %get-tuple-element.142.refs_1_, f32[48,1,128]{2,1,0:T(1,128)S(1)} %get-tuple-element.143.refs_2_, f32[24,16,128]{2,1,0:T(8,128)S(1)} %get-tuple-element.190.refs_3_, ...), custom_call_target="tpu_custom_call" | custom-call | bytes 4194304 | tf_op jit(solution)/shard_map/apply_recur/pallas_call | solution.py:194
  160.5 2.4 %collective-permute-start.40 = (f32[24,16,128]{2,1,0:T(8,128)S(1)}, f32[24,16,128]{2,1,0:T(8,128)S(1)}, u32[]{:S(2)}, u32[]{:S(2)}) collective-permute-start(f32[24,16,128]{2,1,0:T(8,128)S(1)} %get-tuple-element.212.refs_9_.refs_3_), channel_id=1, source_target_pairs={{0,4},{4,0},{8,12},{12,8},{16,20},{20,16},{24,28},{28,24},{1,5},{5... | collective-permute-start | bytes 589832 | tf_op jit(solution)/shard_map/ppermute | solution.py:333
  164.7 4.6 %apply_recur_parts.3 = (f32[24,16,128]{2,1,0:T(8,128)S(1)}, f32[24,16,128]{2,1,0:T(8,128)S(1)}, f32[12,32,128]{2,1,0:T(8,128)S(1)}, f32[12,32,128]{2,1,0:T(8,128...) custom-call(s32[578]{0:T(1024)S(1)} %get-tuple-element.141.refs_0_, ...), custom_call_target="tpu_custom_call" | custom-call | bytes 4194304 | tf_op jit(solution)/shard_map/apply_recur_parts/pallas_call | solution.py:194
  174.8 7.1 %factor.2.inv_ref.refs_0_ = f32[128,128]{1,0:T(8,128)S(1)} custom-call(f32[128,128]{1,0:T(8,128)S(1)} %add.67.g_ref), custom_call_target="tpu_custom_call" | custom-call | tf_op jit(solution)/shard_map/factor/pallas_call | solution.py:41
  181.9 4.0 %turn.1 = (f32[12,128,128]{2,1,0:T(8,128)S(1)}, f32[128,128]{1,0:T(8,128)S(1)}) custom-call(s32[2]{0:T(128)S(1)} %pad_add_fusion.ids_ref, f32[128,128]{1,0:T(8,128)S(1)} %factor.2.inv_ref.refs_0_, f32[12,32,128]{2,1,0:T(8,128)S(1)} %get-tuple-element.223.refs_0_, f32[12,32,128]{2,1,0:T(8,128)S(1)} %collective-permute-done.45.refs_1_, ...), custom_call_target="tpu_custom_call" | custom-call | tf_op jit(solution)/shard_map/turn/pallas_call | solution.py:41
  187.9 4.2 %apply.7 = (f32[24,16,128]{2,1,0:T(8,128)S(1)}, f32[24,16,128]{2,1,0:T(8,128)S(1)}) custom-call(s32[578]{0:T(1024)S(1)} %get-tuple-element.141.refs_0_, bf16[288,128,256]{2,1,0:T(8,128)(2,1)S(1)} %get-tuple-element.142.refs_1_, f32[48,1,128]{2,1,0:T(1,128)S(1)} %get-tuple-element.143.refs_2_, f32[24,16,128]{2,1,0:T(8,128)S(1)} %get-tuple-element.212.refs_9_.refs_3_, ...), custom_call_target="tpu_custom_call" | custom-call | bytes 4194304 | tf_op jit(solution)/shard_map/apply/pallas_call | solution.py:194
  192.2 5.3 %apply_parts.3 = (f32[24,16,128]{2,1,0:T(8,128)}, f32[24,16,128]{2,1,0:T(8,128)}, f32[12,32,128]{2,1,0:T(8,128)S(1)}, f32[12,32,128]{2,1,0:T(8,128)S(1)}, f32[12...) custom-call(s32[578]{0:T(1024)S(1)} %get-tuple-element.141.refs_0_, ...), custom_call_target="tpu_custom_call" | custom-call | bytes 4194304 | tf_op jit(solution)/shard_map/apply_parts/pallas_call | solution.py:194
  199.9 2.2 cross.1
  203.8 2.0 collective-permute-start.54
  207.2 1.9 collective-permute-start.62
  210.2 2.7 %turn_cross.1 = f32[128,128]{1,0:T(8,128)S(1)} custom-call(s32[2]{0:T(128)S(1)} %pad_add_fusion.ids_ref, f32[128,128]{1,0:T(8,128)S(1)} %factor.2.inv_ref.refs_0_, f32[12,128,128]{2,1,0:T(8,128)S(1)} %get-tuple-element.238.f_ref, f32[128,128]{1,0:T(8,128)S(1)} %get-tuple-element.227.g_ref, f32[12,32,128]{2,1,0:T(8,128)S(1)} %get-tuple-element.245.refs_0_, ...), custom_call_target="tpu_custom_call" | custom-call | tf_op jit(solution)/shard_map/turn_cross/pallas_call | solution.py:41
  212.9 2.8 %collective-permute-start.60 = (f32[128,128]{1,0:T(8,128)S(1)}, f32[128,128]{1,0:T(8,128)S(1)}, u32[]{:S(2)}, u32[]{:S(2)}) collective-permute-start(f32[128,128]{1,0:T(8,128)S(1)} %turn_cross.1), channel_id=1, source_target_pairs={{0,24},{4,28},{8,16},{12,20},{16,8},{20,12},{24,0},{28,4},{1,25},{... | collective-permute-start | bytes 196616 | tf_op jit(solution)/shard_map/ppermute | solution.py:337
  217.4 7.1 %factor.3.inv_ref.refs_2_ = f32[128,128]{1,0:T(8,128)S(1)} custom-call(f32[128,128]{1,0:T(8,128)S(1)} %add.72.g_ref), custom_call_target="tpu_custom_call" | custom-call | tf_op jit(solution)/shard_map/factor/pallas_call | solution.py:41
  230.3 3.8 %collective-permute-done.64 = f32[128,128]{1,0:T(8,128)S(1)} collective-permute-done((f32[128,128]{1,0:T(8,128)S(1)}, f32[128,128]{1,0:T(8,128)S(1)}, u32[]{:S(2)}, u32[]{:S(2)}) %collective-permute-start.64) | collective-permute-done | bytes 65568 | tf_op jit(solution)/shard_map/ppermute | solution.py:337
  238.1 2.0 collective-permute-done.67
  (144 shorter events, 51.9 us)
Async XLA Ops:
  2.5 17.4 %collective-permute-start = (f32[24,16,128]{2,1,0:T(8,128)S(1)}, f32[24,16,128]{2,1,0:T(8,128)S(1)}, u32[]{:S(2)}, u32[]{:S(2)}) collective-permute-start(f32[24,16,128]{2,1,0:T(8,128)S(1)} %get-tuple-element.144.refs_3_.refs_7_), channel_id=1, source_target_pairs={{0,4},{4,0},{8,12},{12,8},{16,20},{20,16},{24,28},{28,24},{1,5},{5... | collective-permute-start | bytes 589832 | tf_op jit(solution)/shard_map/ppermute | solution.py:333
  5.5 14.4 %collective-permute-start.1 = (f32[24,16,128]{2,1,0:T(8,128)S(1)}, f32[24,16,128]{2,1,0:T(8,128)S(1)}, u32[]{:S(2)}, u32[]{:S(2)}) collective-permute-start(f32[24,16,128]{2,1,0:T(8,128)S(1)} %get-tuple-element.145.refs_4_.refs_8_), channel_id=1, source_target_pairs={{0,28},{4,8},{8,4},{12,16},{16,12},{20,24},{24,20},{28,0},{1,29},{... | collective-permute-start | bytes 589832 | tf_op jit(solution)/shard_map/ppermute | solution.py:333
  9.1 20.5 %collective-permute-start.12 = (f32[24,16,128]{2,1,0:T(8,128)S(1)}, f32[24,16,128]{2,1,0:T(8,128)S(1)}, u32[]{:S(2)}, u32[]{:S(2)}) collective-permute-start(f32[24,16,128]{2,1,0:T(8,128)S(1)} %get-tuple-element.156.refs_3_.refs_7_), channel_id=1, source_target_pairs={{0,4},{4,0},{8,12},{12,8},{16,20},{20,16},{24,28},{28,24},{1,5},{5... | collective-permute-start | bytes 589832 | tf_op jit(solution)/shard_map/ppermute | solution.py:333
  9.1 20.5 %collective-permute-start.13 = (f32[24,16,128]{2,1,0:T(8,128)S(1)}, f32[24,16,128]{2,1,0:T(8,128)S(1)}, u32[]{:S(2)}, u32[]{:S(2)}) collective-permute-start(f32[24,16,128]{2,1,0:T(8,128)S(1)} %get-tuple-element.157.refs_4_.refs_8_), channel_id=1, source_target_pairs={{0,28},{4,8},{8,4},{12,16},{16,12},{20,24},{24,20},{28,0},{1,29},{... | collective-permute-start | bytes 589832 | tf_op jit(solution)/shard_map/ppermute | solution.py:333
  24.2 11.7 %collective-permute-start.2 = (f32[24,16,128]{2,1,0:T(8,128)S(1)}, f32[24,16,128]{2,1,0:T(8,128)S(1)}, u32[]{:S(2)}, u32[]{:S(2)}) collective-permute-start(f32[24,16,128]{2,1,0:T(8,128)S(1)} %get-tuple-element.146.refs_3_.refs_7_), channel_id=1, source_target_pairs={{0,4},{4,0},{8,12},{12,8},{16,20},{20,16},{24,28},{28,24},{1,5},{5... | collective-permute-start | bytes 589832 | tf_op jit(solution)/shard_map/ppermute | solution.py:333
  33.9 15.1 %collective-permute-start.14 = (f32[24,16,128]{2,1,0:T(8,128)S(1)}, f32[24,16,128]{2,1,0:T(8,128)S(1)}, u32[]{:S(2)}, u32[]{:S(2)}) collective-permute-start(f32[24,16,128]{2,1,0:T(8,128)S(1)} %get-tuple-element.158.refs_3_.refs_7_), channel_id=1, source_target_pairs={{0,4},{4,0},{8,12},{12,8},{16,20},{20,16},{24,28},{28,24},{1,5},{5... | collective-permute-start | bytes 589832 | tf_op jit(solution)/shard_map/ppermute | solution.py:333
  34.0 15.0 %collective-permute-start.15 = (f32[24,16,128]{2,1,0:T(8,128)S(1)}, f32[24,16,128]{2,1,0:T(8,128)S(1)}, u32[]{:S(2)}, u32[]{:S(2)}) collective-permute-start(f32[24,16,128]{2,1,0:T(8,128)S(1)} %get-tuple-element.159.refs_4_.refs_8_), channel_id=1, source_target_pairs={{0,28},{4,8},{8,4},{12,16},{16,12},{20,24},{24,20},{28,0},{1,29},{... | collective-permute-start | bytes 589832 | tf_op jit(solution)/shard_map/ppermute | solution.py:333
  40.1 15.2 %collective-permute-start.4 = (f32[24,16,128]{2,1,0:T(8,128)S(1)}, f32[24,16,128]{2,1,0:T(8,128)S(1)}, u32[]{:S(2)}, u32[]{:S(2)}) collective-permute-start(f32[24,16,128]{2,1,0:T(8,128)S(1)} %get-tuple-element.148.refs_3_.refs_7_), channel_id=1, source_target_pairs={{0,4},{4,0},{8,12},{12,8},{16,20},{20,16},{24,28},{28,24},{1,5},{5... | collective-permute-start | bytes 589832 | tf_op jit(solution)/shard_map/ppermute | solution.py:333
  40.8 14.5 %collective-permute-start.5 = (f32[24,16,128]{2,1,0:T(8,128)S(1)}, f32[24,16,128]{2,1,0:T(8,128)S(1)}, u32[]{:S(2)}, u32[]{:S(2)}) collective-permute-start(f32[24,16,128]{2,1,0:T(8,128)S(1)} %get-tuple-element.149.refs_4_.refs_8_), channel_id=1, source_target_pairs={{0,28},{4,8},{8,4},{12,16},{16,12},{20,24},{24,20},{28,0},{1,29},{... | collective-permute-start | bytes 589832 | tf_op jit(solution)/shard_map/ppermute | solution.py:333
  59.6 13.4 %collective-permute-start.6 = (f32[24,16,128]{2,1,0:T(8,128)S(1)}, f32[24,16,128]{2,1,0:T(8,128)S(1)}, u32[]{:S(2)}, u32[]{:S(2)}) collective-permute-start(f32[24,16,128]{2,1,0:T(8,128)S(1)} %get-tuple-element.150.refs_3_), channel_id=1, source_target_pairs={{0,4},{4,0},{8,12},{12,8},{16,20},{20,16},{24,28},{28,24},{1,5},{5... | collective-permute-start | bytes 589832 | tf_op jit(solution)/shard_map/ppermute | solution.py:333
  59.7 13.2 %collective-permute-start.7 = (f32[24,16,128]{2,1,0:T(8,128)S(1)}, f32[24,16,128]{2,1,0:T(8,128)S(1)}, u32[]{:S(2)}, u32[]{:S(2)}) collective-permute-start(f32[24,16,128]{2,1,0:T(8,128)S(1)} %get-tuple-element.151.refs_4_), channel_id=1, source_target_pairs={{0,28},{4,8},{8,4},{12,16},{16,12},{20,24},{24,20},{28,0},{1,29},{... | collective-permute-start | bytes 589832 | tf_op jit(solution)/shard_map/ppermute | solution.py:333
  66.9 12.3 %collective-permute-start.18 = (f32[24,16,128]{2,1,0:T(8,128)S(1)}, f32[24,16,128]{2,1,0:T(8,128)S(1)}, u32[]{:S(2)}, u32[]{:S(2)}) collective-permute-start(f32[24,16,128]{2,1,0:T(8,128)S(1)} %get-tuple-element.162.refs_3_), channel_id=1, source_target_pairs={{0,4},{4,0},{8,12},{12,8},{16,20},{20,16},{24,28},{28,24},{1,5},{5... | collective-permute-start | bytes 589832 | tf_op jit(solution)/shard_map/ppermute | solution.py:333
  68.0 11.2 %collective-permute-start.19 = (f32[24,16,128]{2,1,0:T(8,128)S(1)}, f32[24,16,128]{2,1,0:T(8,128)S(1)}, u32[]{:S(2)}, u32[]{:S(2)}) collective-permute-start(f32[24,16,128]{2,1,0:T(8,128)S(1)} %get-tuple-element.163.refs_4_), channel_id=1, source_target_pairs={{0,28},{4,8},{8,4},{12,16},{16,12},{20,24},{24,20},{28,0},{1,29},{... | collective-permute-start | bytes 589832 | tf_op jit(solution)/shard_map/ppermute | solution.py:333
  77.2 16.0 %collective-permute-start.8 = (f32[24,16,128]{2,1,0:T(8,128)S(1)}, f32[24,16,128]{2,1,0:T(8,128)S(1)}, u32[]{:S(2)}, u32[]{:S(2)}) collective-permute-start(f32[24,16,128]{2,1,0:T(8,128)S(1)} %get-tuple-element.169.refs_3_.refs_9_.refs_7_), channel_id=1, source_target_pairs={{0,4},{4,0},{8,12},{12,8},{16,20},{20,16},{24,28},{28,24},{1,5},{5... | collective-permute-start | bytes 589832 | tf_op jit(solution)/shard_map/ppermute | solution.py:333
  77.3 17.4 %collective-permute-start.9 = (f32[24,16,128]{2,1,0:T(8,128)S(1)}, f32[24,16,128]{2,1,0:T(8,128)S(1)}, u32[]{:S(2)}, u32[]{:S(2)}) collective-permute-start(f32[24,16,128]{2,1,0:T(8,128)S(1)} %get-tuple-element.170.refs_4_.refs_10_.refs_8_), channel_id=1, source_target_pairs={{0,28},{4,8},{8,4},{12,16},{16,12},{20,24},{24,20},{28,0},{1,29},{... | collective-permute-start | bytes 589832 | tf_op jit(solution)/shard_map/ppermute | solution.py:333
  83.6 15.7 %collective-permute-start.27 = (f32[24,16,128]{2,1,0:T(8,128)S(1)}, f32[24,16,128]{2,1,0:T(8,128)S(1)}, u32[]{:S(2)}, u32[]{:S(2)}) collective-permute-start(f32[24,16,128]{2,1,0:T(8,128)S(1)} %get-tuple-element.182.refs_3_.refs_7_), channel_id=1, source_target_pairs={{0,4},{4,0},{8,12},{12,8},{16,20},{20,16},{24,28},{28,24},{1,5},{5... | collective-permute-start | bytes 589832 | tf_op jit(solution)/shard_map/ppermute | solution.py:333
  83.8 15.7 %collective-permute-start.28 = (f32[24,16,128]{2,1,0:T(8,128)S(1)}, f32[24,16,128]{2,1,0:T(8,128)S(1)}, u32[]{:S(2)}, u32[]{:S(2)}) collective-permute-start(f32[24,16,128]{2,1,0:T(8,128)S(1)} %get-tuple-element.183.refs_4_.refs_8_), channel_id=1, source_target_pairs={{0,28},{4,8},{8,4},{12,16},{16,12},{20,24},{24,20},{28,0},{1,29},{... | collective-permute-start | bytes 589832 | tf_op jit(solution)/shard_map/ppermute | solution.py:333
  93.2 12.9 %collective-permute-start.20 = (f32[12,32,128]{2,1,0:T(8,128)S(1)}, f32[12,32,128]{2,1,0:T(8,128)S(1)}, u32[]{:S(2)}, u32[]{:S(2)}) collective-permute-start(f32[12,32,128]{2,1,0:T(8,128)S(1)} %get-tuple-element.165), channel_id=1, source_target_pairs={{0,1},{1,0},{2,3},{3,2},{4,5},{5,4},{6,7},{7,6},{8,9},{9,8},{10,11... | collective-permute-start | bytes 589832 | tf_op jit(solution)/shard_map/ppermute | solution.py:337
  93.2 13.0 %collective-permute-start.21 = (f32[12,32,128]{2,1,0:T(8,128)S(1)}, f32[12,32,128]{2,1,0:T(8,128)S(1)}, u32[]{:S(2)}, u32[]{:S(2)}) collective-permute-start(f32[12,32,128]{2,1,0:T(8,128)S(1)} %get-tuple-element.166), channel_id=1, source_target_pairs={{0,2},{1,3},{2,0},{3,1},{4,6},{5,7},{6,4},{7,5},{8,10},{9,11},{10,... | collective-permute-start | bytes 589832 | tf_op jit(solution)/shard_map/ppermute | solution.py:337
  94.7 11.6 %collective-permute-start.22 = (f32[12,32,128]{2,1,0:T(8,128)S(1)}, f32[12,32,128]{2,1,0:T(8,128)S(1)}, u32[]{:S(2)}, u32[]{:S(2)}) collective-permute-start(f32[12,32,128]{2,1,0:T(8,128)S(1)} %get-tuple-element.167), channel_id=1, source_target_pairs={{0,3},{1,2},{2,1},{3,0},{4,7},{5,6},{6,5},{7,4},{8,11},{9,10},{10,... | collective-permute-start | bytes 589832 | tf_op jit(solution)/shard_map/ppermute | solution.py:337
  99.4 12.0 %collective-permute-start.10 = (f32[24,16,128]{2,1,0:T(8,128)S(1)}, f32[24,16,128]{2,1,0:T(8,128)S(1)}, u32[]{:S(2)}, u32[]{:S(2)}) collective-permute-start(f32[24,16,128]{2,1,0:T(8,128)S(1)} %get-tuple-element.188.refs_3_.refs_7_), channel_id=1, source_target_pairs={{0,4},{4,0},{8,12},{12,8},{16,20},{20,16},{24,28},{28,24},{1,5},{5... | collective-permute-start | bytes 589832 | tf_op jit(solution)/shard_map/ppermute | solution.py:333
  99.5 11.9 %collective-permute-start.11 = (f32[24,16,128]{2,1,0:T(8,128)S(1)}, f32[24,16,128]{2,1,0:T(8,128)S(1)}, u32[]{:S(2)}, u32[]{:S(2)}) collective-permute-start(f32[24,16,128]{2,1,0:T(8,128)S(1)} %get-tuple-element.189.refs_4_.refs_8_), channel_id=1, source_target_pairs={{0,28},{4,8},{8,4},{12,16},{16,12},{20,24},{24,20},{28,0},{1,29},{... | collective-permute-start | bytes 589832 | tf_op jit(solution)/shard_map/ppermute | solution.py:333
  106.1 12.7 %collective-permute-start.37 = (f32[12,32,128]{2,1,0:T(8,128)S(1)}, f32[12,32,128]{2,1,0:T(8,128)S(1)}, u32[]{:S(2)}, u32[]{:S(2)}) collective-permute-start(f32[12,32,128]{2,1,0:T(8,128)S(1)} %get-tuple-element.201), channel_id=1, source_target_pairs={{0,1},{1,0},{2,3},{3,2},{4,5},{5,4},{6,7},{7,6},{8,9},{9,8},{10,11... | collective-permute-start | bytes 589832 | tf_op jit(solution)/shard_map/ppermute | solution.py:337
  106.2 14.1 %collective-permute-start.29 = (f32[24,16,128]{2,1,0:T(8,128)S(1)}, f32[24,16,128]{2,1,0:T(8,128)S(1)}, u32[]{:S(2)}, u32[]{:S(2)}) collective-permute-start(f32[24,16,128]{2,1,0:T(8,128)S(1)} %get-tuple-element.204.refs_3_.refs_7_), channel_id=1, source_target_pairs={{0,4},{4,0},{8,12},{12,8},{16,20},{20,16},{24,28},{28,24},{1,5},{5... | collective-permute-start | bytes 589832 | tf_op jit(solution)/shard_map/ppermute | solution.py:333
  106.3 15.0 %collective-permute-start.30 = (f32[24,16,128]{2,1,0:T(8,128)S(1)}, f32[24,16,128]{2,1,0:T(8,128)S(1)}, u32[]{:S(2)}, u32[]{:S(2)}) collective-permute-start(f32[24,16,128]{2,1,0:T(8,128)S(1)} %get-tuple-element.205.refs_4_.refs_8_), channel_id=1, source_target_pairs={{0,28},{4,8},{8,4},{12,16},{16,12},{20,24},{24,20},{28,0},{1,29},{... | collective-permute-start | bytes 589832 | tf_op jit(solution)/shard_map/ppermute | solution.py:333
  115.7 11.9 %collective-permute-start.23 = (f32[24,16,128]{2,1,0:T(8,128)S(1)}, f32[24,16,128]{2,1,0:T(8,128)S(1)}, u32[]{:S(2)}, u32[]{:S(2)}) collective-permute-start(f32[24,16,128]{2,1,0:T(8,128)S(1)} %get-tuple-element.210.refs_3_.refs_7_), channel_id=1, source_target_pairs={{0,4},{4,0},{8,12},{12,8},{16,20},{20,16},{24,28},{28,24},{1,5},{5... | collective-permute-start | bytes 589832 | tf_op jit(solution)/shard_map/ppermute | solution.py:333
  117.0 12.3 %collective-permute-start.24 = (f32[24,16,128]{2,1,0:T(8,128)S(1)}, f32[24,16,128]{2,1,0:T(8,128)S(1)}, u32[]{:S(2)}, u32[]{:S(2)}) collective-permute-start(f32[24,16,128]{2,1,0:T(8,128)S(1)} %get-tuple-element.211.refs_4_.refs_8_), channel_id=1, source_target_pairs={{0,28},{4,8},{8,4},{12,16},{16,12},{20,24},{24,20},{28,0},{1,29},{... | collective-permute-start | bytes 589832 | tf_op jit(solution)/shard_map/ppermute | solution.py:333
  120.3 13.5 %collective-permute-start.38 = (f32[12,32,128]{2,1,0:T(8,128)S(1)}, f32[12,32,128]{2,1,0:T(8,128)S(1)}, u32[]{:S(2)}, u32[]{:S(2)}) collective-permute-start(f32[12,32,128]{2,1,0:T(8,128)S(1)} %get-tuple-element.202), channel_id=1, source_target_pairs={{0,2},{1,3},{2,0},{3,1},{4,6},{5,7},{6,4},{7,5},{8,10},{9,11},{10,... | collective-permute-start | bytes 589832 | tf_op jit(solution)/shard_map/ppermute | solution.py:337
  121.3 20.5 %collective-permute-start.39 = (f32[12,32,128]{2,1,0:T(8,128)S(1)}, f32[12,32,128]{2,1,0:T(8,128)S(1)}, u32[]{:S(2)}, u32[]{:S(2)}) collective-permute-start(f32[12,32,128]{2,1,0:T(8,128)S(1)} %get-tuple-element.203), channel_id=1, source_target_pairs={{0,3},{1,2},{2,1},{3,0},{4,7},{5,6},{6,5},{7,4},{8,11},{9,10},{10,... | collective-permute-start | bytes 589832 | tf_op jit(solution)/shard_map/ppermute | solution.py:337
  125.6 16.2 %collective-permute-start.35 = (f32[24,16,128]{2,1,0:T(8,128)S(1)}, f32[24,16,128]{2,1,0:T(8,128)S(1)}, u32[]{:S(2)}, u32[]{:S(2)}) collective-permute-start(f32[24,16,128]{2,1,0:T(8,128)S(1)} %get-tuple-element.221.refs_3_.refs_7_), channel_id=1, source_target_pairs={{0,4},{4,0},{8,12},{12,8},{16,20},{20,16},{24,28},{28,24},{1,5},{5... | collective-permute-start | bytes 589832 | tf_op jit(solution)/shard_map/ppermute | solution.py:333
  127.6 14.2 %collective-permute-start.36 = (f32[24,16,128]{2,1,0:T(8,128)S(1)}, f32[24,16,128]{2,1,0:T(8,128)S(1)}, u32[]{:S(2)}, u32[]{:S(2)}) collective-permute-start(f32[24,16,128]{2,1,0:T(8,128)S(1)} %get-tuple-element.222.refs_4_.refs_8_), channel_id=1, source_target_pairs={{0,28},{4,8},{8,4},{12,16},{16,12},{20,24},{24,20},{28,0},{1,29},{... | collective-permute-start | bytes 589832 | tf_op jit(solution)/shard_map/ppermute | solution.py:333
  133.9 22.4 %collective-permute-start.31 = (f32[24,16,128]{2,1,0:T(8,128)S(1)}, f32[24,16,128]{2,1,0:T(8,128)S(1)}, u32[]{:S(2)}, u32[]{:S(2)}) collective-permute-start(f32[24,16,128]{2,1,0:T(8,128)S(1)} %get-tuple-element.190.refs_3_), channel_id=1, source_target_pairs={{0,4},{4,0},{8,12},{12,8},{16,20},{20,16},{24,28},{28,24},{1,5},{5... | collective-permute-start | bytes 589832 | tf_op jit(solution)/shard_map/ppermute | solution.py:333
  138.8 17.4 %collective-permute-start.32 = (f32[24,16,128]{2,1,0:T(8,128)S(1)}, f32[24,16,128]{2,1,0:T(8,128)S(1)}, u32[]{:S(2)}, u32[]{:S(2)}) collective-permute-start(f32[24,16,128]{2,1,0:T(8,128)S(1)} %get-tuple-element.191.refs_4_), channel_id=1, source_target_pairs={{0,28},{4,8},{8,4},{12,16},{16,12},{20,24},{24,20},{28,0},{1,29},{... | collective-permute-start | bytes 589832 | tf_op jit(solution)/shard_map/ppermute | solution.py:333
  146.1 18.6 %collective-permute-start.43 = (f32[24,16,128]{2,1,0:T(8,128)S(1)}, f32[24,16,128]{2,1,0:T(8,128)S(1)}, u32[]{:S(2)}, u32[]{:S(2)}) collective-permute-start(f32[24,16,128]{2,1,0:T(8,128)S(1)} %get-tuple-element.206.refs_3_), channel_id=1, source_target_pairs={{0,4},{4,0},{8,12},{12,8},{16,20},{20,16},{24,28},{28,24},{1,5},{5... | collective-permute-start | bytes 589832 | tf_op jit(solution)/shard_map/ppermute | solution.py:333
  146.3 18.4 %collective-permute-start.44 = (f32[24,16,128]{2,1,0:T(8,128)S(1)}, f32[24,16,128]{2,1,0:T(8,128)S(1)}, u32[]{:S(2)}, u32[]{:S(2)}) collective-permute-start(f32[24,16,128]{2,1,0:T(8,128)S(1)} %get-tuple-element.207.refs_4_), channel_id=1, source_target_pairs={{0,28},{4,8},{8,4},{12,16},{16,12},{20,24},{24,20},{28,0},{1,29},{... | collective-permute-start | bytes 589832 | tf_op jit(solution)/shard_map/ppermute | solution.py:333
  169.3 12.6 %collective-permute-start.45 = (f32[12,32,128]{2,1,0:T(8,128)S(1)}, f32[12,32,128]{2,1,0:T(8,128)S(1)}, u32[]{:S(2)}, u32[]{:S(2)}) collective-permute-start(f32[12,32,128]{2,1,0:T(8,128)S(1)} %get-tuple-element.224), channel_id=1, source_target_pairs={{0,1},{1,0},{2,3},{3,2},{4,5},{5,4},{6,7},{7,6},{8,9},{9,8},{10,11... | collective-permute-start | bytes 589832 | tf_op jit(solution)/shard_map/ppermute | solution.py:337
  169.4 12.6 %collective-permute-start.46 = (f32[12,32,128]{2,1,0:T(8,128)S(1)}, f32[12,32,128]{2,1,0:T(8,128)S(1)}, u32[]{:S(2)}, u32[]{:S(2)}) collective-permute-start(f32[12,32,128]{2,1,0:T(8,128)S(1)} %get-tuple-element.225), channel_id=1, source_target_pairs={{0,2},{1,3},{2,0},{3,1},{4,6},{5,7},{6,4},{7,5},{8,10},{9,11},{10,... | collective-permute-start | bytes 589832 | tf_op jit(solution)/shard_map/ppermute | solution.py:337
  170.4 11.5 %collective-permute-start.47 = (f32[12,32,128]{2,1,0:T(8,128)S(1)}, f32[12,32,128]{2,1,0:T(8,128)S(1)}, u32[]{:S(2)}, u32[]{:S(2)}) collective-permute-start(f32[12,32,128]{2,1,0:T(8,128)S(1)} %get-tuple-element.226), channel_id=1, source_target_pairs={{0,3},{1,2},{2,1},{3,0},{4,7},{5,6},{6,5},{7,4},{8,11},{9,10},{10,... | collective-permute-start | bytes 589832 | tf_op jit(solution)/shard_map/ppermute | solution.py:337
  171.2 20.9 %collective-permute-start.50 = (f32[24,16,128]{2,1,0:T(8,128)S(1)}, f32[24,16,128]{2,1,0:T(8,128)S(1)}, u32[]{:S(2)}, u32[]{:S(2)}) collective-permute-start(f32[24,16,128]{2,1,0:T(8,128)S(1)} %get-tuple-element.228.refs_3_), channel_id=1, source_target_pairs={{0,4},{4,0},{8,12},{12,8},{16,20},{20,16},{24,28},{28,24},{1,5},{5... | collective-permute-start | bytes 589832 | tf_op jit(solution)/shard_map/ppermute | solution.py:333
  173.1 19.1 %collective-permute-start.51 = (f32[24,16,128]{2,1,0:T(8,128)S(1)}, f32[24,16,128]{2,1,0:T(8,128)S(1)}, u32[]{:S(2)}, u32[]{:S(2)}) collective-permute-start(f32[24,16,128]{2,1,0:T(8,128)S(1)} %get-tuple-element.229.refs_4_), channel_id=1, source_target_pairs={{0,28},{4,8},{8,4},{12,16},{16,12},{20,24},{24,20},{28,0},{1,29},{... | collective-permute-start | bytes 589832 | tf_op jit(solution)/shard_map/ppermute | solution.py:333
  197.5 11.6 %collective-permute-start.56 = (f32[12,32,128]{2,1,0:T(8,128)S(1)}, f32[12,32,128]{2,1,0:T(8,128)S(1)}, u32[]{:S(2)}, u32[]{:S(2)}) collective-permute-start(f32[12,32,128]{2,1,0:T(8,128)S(1)} %get-tuple-element.247), channel_id=1, source_target_pairs={{0,2},{1,3},{2,0},{3,1},{4,6},{5,7},{6,4},{7,5},{8,10},{9,11},{10,... | collective-permute-start | bytes 589832 | tf_op jit(solution)/shard_map/ppermute | solution.py:337
  199.1 11.1 %collective-permute-start.57 = (f32[12,32,128]{2,1,0:T(8,128)S(1)}, f32[12,32,128]{2,1,0:T(8,128)S(1)}, u32[]{:S(2)}, u32[]{:S(2)}) collective-permute-start(f32[12,32,128]{2,1,0:T(8,128)S(1)} %get-tuple-element.248), channel_id=1, source_target_pairs={{0,3},{1,2},{2,1},{3,0},{4,7},{5,6},{6,5},{7,4},{8,11},{9,10},{10,... | collective-permute-start | bytes 589832 | tf_op jit(solution)/shard_map/ppermute | solution.py:337
  207.2 18.6 %collective-permute-start.62 = (f32[128,128]{1,0:T(8,128)S(1)}, f32[128,128]{1,0:T(8,128)S(1)}, u32[]{:S(2)}, u32[]{:S(2)}) collective-permute-start(f32[128,128]{1,0:T(8,128)S(1)} %cross.1), channel_id=1, source_target_pairs={{0,16},{4,20},{8,24},{12,28},{16,0},{20,4},{24,8},{28,12},{1,17},{... | collective-permute-start | bytes 196616 | tf_op jit(solution)/shard_map/ppermute | solution.py:337
  209.2 16.7 %collective-permute-start.61 = (f32[128,128]{1,0:T(8,128)S(1)}, f32[128,128]{1,0:T(8,128)S(1)}, u32[]{:S(2)}, u32[]{:S(2)}) collective-permute-start(f32[128,128]{1,0:T(8,128)S(1)} %cross.1), channel_id=1, source_target_pairs={{0,8},{4,12},{8,0},{12,4},{16,24},{20,28},{24,16},{28,20},{1,9},{5... | collective-permute-start | bytes 196616 | tf_op jit(solution)/shard_map/ppermute | solution.py:337
  212.9 13.0 %collective-permute-start.60 = (f32[128,128]{1,0:T(8,128)S(1)}, f32[128,128]{1,0:T(8,128)S(1)}, u32[]{:S(2)}, u32[]{:S(2)}) collective-permute-start(f32[128,128]{1,0:T(8,128)S(1)} %turn_cross.1), channel_id=1, source_target_pairs={{0,24},{4,28},{8,16},{12,20},{16,8},{20,12},{24,0},{28,4},{1,25},{... | collective-permute-start | bytes 196616 | tf_op jit(solution)/shard_map/ppermute | solution.py:337
  227.8 12.7 %collective-permute-start.69 = (f32[12,32,128]{2,1,0:T(8,128)S(1)}, f32[12,32,128]{2,1,0:T(8,128)S(1)}, u32[]{:S(2)}, u32[]{:S(2)}) collective-permute-start(f32[12,32,128]{2,1,0:T(8,128)S(1)} %get-tuple-element.268), channel_id=1, source_target_pairs={{0,1},{1,0},{2,3},{3,2},{4,5},{5,4},{6,7},{7,6},{8,9},{9,8},{10,11... | collective-permute-start | bytes 589832 | tf_op jit(solution)/shard_map/ppermute | solution.py:337
  227.8 12.7 %collective-permute-start.70 = (f32[12,32,128]{2,1,0:T(8,128)S(1)}, f32[12,32,128]{2,1,0:T(8,128)S(1)}, u32[]{:S(2)}, u32[]{:S(2)}) collective-permute-start(f32[12,32,128]{2,1,0:T(8,128)S(1)} %get-tuple-element.269), channel_id=1, source_target_pairs={{0,2},{1,3},{2,0},{3,1},{4,6},{5,7},{6,4},{7,5},{8,10},{9,11},{10,... | collective-permute-start | bytes 589832 | tf_op jit(solution)/shard_map/ppermute | solution.py:337
  229.6 11.0 %collective-permute-start.71 = (f32[12,32,128]{2,1,0:T(8,128)S(1)}, f32[12,32,128]{2,1,0:T(8,128)S(1)}, u32[]{:S(2)}, u32[]{:S(2)}) collective-permute-start(f32[12,32,128]{2,1,0:T(8,128)S(1)} %get-tuple-element.270), channel_id=1, source_target_pairs={{0,3},{1,2},{2,1},{3,0},{4,7},{5,6},{6,5},{7,4},{8,11},{9,10},{10,... | collective-permute-start | bytes 589832 | tf_op jit(solution)/shard_map/ppermute | solution.py:337
  (25 other events, 170.0 us)

commit v9 on v8

--- a/solution.py
+++ b/solution.py
@@ -11,6 +11,7 @@
 UNROLL = 72
 CHUNK = 24
 TURNS = 3
+PANEL = 16
 APPLY_BYTES = 4 << 20
 F32, BF16, I32 = jnp.float32, jnp.bfloat16, jnp.int32
 precise = lax.Precision.HIGHEST
@@ -208,7 +209,7 @@
 
 def factor_kernel(nodes, g_ref, out_ref):
     n = g_ref.shape[0]
-    p = 8
+    p = PANEL
     out_ref[...] = g_ref[...] * (1.0 / nodes)
     sub = lax.broadcasted_iota(I32, (p, n), 0)
     lane = lax.broadcasted_iota(I32, (p, n), 1)
@@ -246,11 +247,19 @@
     return x_ref[b]
 
 
+def couples(count):
+    return [range(b, min(b + 2, count)) for b in range(0, count, 2)]
+
+
+def wide(pieces):
+    return jnp.concatenate(list(pieces), axis=1)
+
+
 def gram_kernel(ids_ref, *refs):
     parts, (f_ref, g_ref) = refs[:-2], refs[-2:]
     total = jnp.zeros(g_ref.shape, F32)
-    for b in range(f_ref.shape[0]):
-        f = gathered(ids_ref, parts, b, f_ref)
+    for pair in couples(f_ref.shape[0]):
+        f = wide(gathered(ids_ref, parts, b, f_ref) for b in pair)
         total = total + nt(f, f)
     g_ref[...] = total
 
@@ -258,17 +267,20 @@
 def cross_kernel(ids_ref, f_ref, g_ref, *refs):
     parts, (k_ref, x_ref) = refs[:-2], refs[-2:]
     total = jnp.zeros(k_ref.shape, F32)
-    for b in range(f_ref.shape[0]):
-        total = total + nt(f_ref[b], gathered(ids_ref, parts, b, x_ref))
+    for pair in couples(f_ref.shape[0]):
+        z = wide(gathered(ids_ref, parts, b, x_ref) for b in pair)
+        total = total + nt(wide(f_ref[b] for b in pair), z)
     k_ref[...] = half_width * total + center * g_ref[...]
 
 
 def turn_kernel(ids_ref, inv_ref, *refs):
     parts, (f_ref, g_ref, x_ref) = refs[:-3], refs[-3:]
+    n = x_ref.shape[-1]
     total = jnp.zeros(g_ref.shape, F32)
-    for b in range(f_ref.shape[0]):
-        f = nn(inv_ref[...], gathered(ids_ref, parts, b, x_ref))
-        f_ref[b] = f
+    for pair in couples(f_ref.shape[0]):
+        f = nn(inv_ref[...], wide(gathered(ids_ref, parts, b, x_ref) for b in pair))
+        for i, b in enumerate(pair):
+            f_ref[b] = f[:, i * n:(i + 1) * n]
         total = total + nt(f, f)
     g_ref[...] = total
 
@@ -276,8 +288,9 @@
 def turn_cross_kernel(ids_ref, inv_ref, f_ref, g_ref, *refs):
     parts, (k_ref, x_ref) = refs[:-2], refs[-2:]
     total = jnp.zeros(g_ref.shape, F32)
-    for b in range(f_ref.shape[0]):
-        total = total + nt(f_ref[b], gathered(ids_ref, parts, b, x_ref))
+    for pair in couples(f_ref.shape[0]):
+        z = wide(gathered(ids_ref, parts, b, x_ref) for b in pair)
+        total = total + nt(wide(f_ref[b] for b in pair), z)
     k_ref[...] = half_width * nt(total, inv_ref[...]) + center * g_ref[...]
 
 
@@ -285,10 +298,13 @@
     parts, x_ref = refs[:-1], refs[-1]
     each = parts[0].shape[1]
     me = ids_ref[1]
-    for b in range(f_ref.shape[0]):
-        x_ref[b] = nn(inv_ref[...], f_ref[b])
-        for s, part in enumerate(parts):
-            part[b] = x_ref[b, pl.ds(pl.multiple_of((me ^ s) * each, each), each)]
+    n = x_ref.shape[-1]
+    for pair in couples(f_ref.shape[0]):
+        q = nn(inv_ref[...], wide(f_ref[b] for b in pair))
+        for i, b in enumerate(pair):
+            x_ref[b] = q[:, i * n:(i + 1) * n]
+            for s, part in enumerate(parts):
+                part[b] = x_ref[b, pl.ds(pl.multiple_of((me ^ s) * each, each), each)]
 
 
 def proj_kernel(nodes, ids_ref, *refs):
@@ -377,8 +393,8 @@
     each = cols_here // 2
     quarter = slots // count
     square = (vecs, vecs)
-    wide = (quarter, vecs, block)
-    held = pltpu.VMEM(wide, F32)
+    held_shape = (quarter, vecs, block)
+    held = pltpu.VMEM(held_shape, F32)
     ids = jnp.stack([lax.axis_index("node"), lax.axis_index("col")]).astype(I32)
 
     halves = call(split_kernel, "split", [(half, each, block)] * 4, ids, start, scalars=1)
@@ -396,7 +412,7 @@
     for step in range(DEGREE - 1):
         after, parts = advance(now, before, step == DEGREE - 2)
         before, now = now, after
-    panel, gram_first = call(gram_kernel, "gram", [wide, square], ids, *swapped(parts), scalars=1)
+    panel, gram_first = call(gram_kernel, "gram", [held_shape, square], ids, *swapped(parts), scalars=1)
     after, parts = advance(now, parts=True)
     before, now = now, after
     image = swapped(parts)
@@ -428,7 +444,7 @@
         cross_kernel, "cross", [square], ids, panel, gram_first, *image, scalars=1, scratch=[held]
     )
     turned, gram_last = call(
-        turn_kernel, "turn", [wide, square], ids, inverse_first, *swapped(parts), scalars=1, scratch=[held]
+        turn_kernel, "turn", [held_shape, square], ids, inverse_first, *swapped(parts), scalars=1, scratch=[held]
     )
     first, _ = apply(meta, now[0], halos[0])
     gram = gram_last

time: 243 us -> 238 us (0.979)
  Pallas kernels: 117 us -> 107 us
  waiting for transfers between devices: 21.6 us -> 27.6 us
    pallas_call x10, Pallas kernels: 29.8 us -> 20.1 us  [call(): pl.pallas_call(kernel, in_specs=[IN_SMEM] * scalars + [IN_VMEM] * (len(ar...]
    ppermute x36, waiting for transfers between devices: 19.6 us -> 25.1 us  [swap(): lax.ppermute(value, axis, [(i, i ^ hop) for i in range(lax.axis_size(axis...]
  transfers between devices with their start and end apart: 72 -> 72, of which waited for: 11 -> 13; matrix products, arithmetic and copies ran while one was open for 0% -> 0% of each run, Pallas kernels for 47% -> 44%
where the time goes in v9:
time: 238 us; the launch traced here: 237 us
  Pallas kernels  107 us (45%)
  starting transfers between devices  99.1 us (42%)
  waiting for transfers between devices  27.6 us (12%)
    pallas_call x18, Pallas kernels, apply(): pl.pallas_call(functools.partial(apply_kernel, bool(old), bool(mate)), in...  78.5 us
    ppermute x18, starting transfers between devices, exchange(): lax.ppermute(pair[1], 'node', odd)  55.1 us
    ppermute x36, starting transfers between devices, swap(): lax.ppermute(value, axis, [(i, i ^ hop) for i in range(lax.axis_size(axis...  29 us
    ppermute x36, waiting for transfers between devices, swap(): lax.ppermute(value, axis, [(i, i ^ hop) for i in range(lax.axis_size(axis...  25.1 us
    pallas_call x10, Pallas kernels, call(): pl.pallas_call(kernel, in_specs=[IN_SMEM] * scalars + [IN_VMEM] * (len(ar...  20.1 us
    ppermute x18, starting transfers between devices, exchange(): lax.ppermute(pair[0], 'node', even)  15 us
    pallas_call x1, Pallas kernels, prep(): pl.pallas_call(functools.partial(prep_kernel, rows), in_specs=[IN_SMEM] *...  8.91 us
  transfers between devices with their start and end apart: 72, of which 13 were waited for; matrix products, arithmetic and copies ran while one was open for 0% of the time, Pallas kernels for 44%

profile of v9, /device:TPU:0, one launch (start us, length us, event | category | flops | bytes accessed | tf_op | source)
XLA Modules:
  0.0 237.4 jit_solution(1273001486148556642)
XLA Ops:
  2.5 3.0 %collective-permute-start = (f32[24,16,128]{2,1,0:T(8,128)S(1)}, f32[24,16,128]{2,1,0:T(8,128)S(1)}, u32[]{:S(2)}, u32[]{:S(2)}) collective-permute-start(f32[24,16,128]{2,1,0:T(8,128)S(1)} %get-tuple-element.144.refs_3_.refs_7_), channel_id=1, source_target_pairs={{0,4},{4,0},{8,12},{12,8},{16,20},{20,16},{24,28},{28,24},{1,5},{5... | collective-permute-start | bytes 589832 | tf_op jit(solution)/shard_map/ppermute | solution.py:349
  5.5 3.5 %collective-permute-start.1 = (f32[24,16,128]{2,1,0:T(8,128)S(1)}, f32[24,16,128]{2,1,0:T(8,128)S(1)}, u32[]{:S(2)}, u32[]{:S(2)}) collective-permute-start(f32[24,16,128]{2,1,0:T(8,128)S(1)} %get-tuple-element.145.refs_4_.refs_8_), channel_id=1, source_target_pairs={{0,28},{4,8},{8,4},{12,16},{16,12},{20,24},{24,20},{28,0},{1,29},{... | collective-permute-start | bytes 589832 | tf_op jit(solution)/shard_map/ppermute | solution.py:349
  9.1 1.9 collective-permute-start.13
  11.0 8.9 %prep.1 = (bf16[288,128,256]{2,1,0:T(8,128)(2,1)S(1)}, f32[48,1,128]{2,1,0:T(1,128)S(1)}, s32[578]{0:T(1024)S(1)}) custom-call(s32[2]{0:T(128)S(1)} %pad_add_fusion.ids_ref, s32[1,288]{1,0:T(1,128)} %own_ref.1, s32[1,288]{1,0:T(1,128)} %col_ref.1, f32[288,128,128]{2,1,0:T(8,128)} %blk_ref.1), custom_call_target="tpu_custom_call" | custom-call | flops 1207959552 | bytes 18874368 | tf_op jit(solution)/shard_map/prep/pallas_call | solution.py:116
  19.9 4.3 %apply.4 = (f32[24,16,128]{2,1,0:T(8,128)S(1)}, f32[24,16,128]{2,1,0:T(8,128)S(1)}) custom-call(s32[578]{0:T(1024)S(1)} %get-tuple-element.141.refs_0_, bf16[288,128,256]{2,1,0:T(8,128)(2,1)S(1)} %get-tuple-element.142.refs_1_, f32[48,1,128]{2,1,0:T(1,128)S(1)} %get-tuple-element.143.refs_2_, f32[24,16,128]{2,1,0:T(8,128)S(1)} %get-tuple-element.144.refs_3_.refs_7_, ...), custom_call_target="tpu_custom_call" | custom-call | bytes 4194304 | tf_op jit(solution)/shard_map/apply/pallas_call | solution.py:195
  26.1 3.6 %collective-permute-start.3 = (f32[24,16,128]{2,1,0:T(8,128)S(1)}, f32[24,16,128]{2,1,0:T(8,128)S(1)}, u32[]{:S(2)}, u32[]{:S(2)}) collective-permute-start(f32[24,16,128]{2,1,0:T(8,128)S(1)} %get-tuple-element.147.refs_4_.refs_8_), channel_id=1, source_target_pairs={{0,28},{4,8},{8,4},{12,16},{16,12},{20,24},{24,20},{28,0},{1,29},{... | collective-permute-start | bytes 589832 | tf_op jit(solution)/shard_map/ppermute | solution.py:349
  29.6 4.3 %apply.6 = (f32[24,16,128]{2,1,0:T(8,128)S(1)}, f32[24,16,128]{2,1,0:T(8,128)S(1)}) custom-call(s32[578]{0:T(1024)S(1)} %get-tuple-element.141.refs_0_, bf16[288,128,256]{2,1,0:T(8,128)(2,1)S(1)} %get-tuple-element.142.refs_1_, f32[48,1,128]{2,1,0:T(1,128)S(1)} %get-tuple-element.143.refs_2_, f32[24,16,128]{2,1,0:T(8,128)S(1)} %get-tuple-element.156.refs_3_.refs_7_, ...), custom_call_target="tpu_custom_call" | custom-call | bytes 4194304 | tf_op jit(solution)/shard_map/apply/pallas_call | solution.py:195
  34.0 1.9 collective-permute-start.15
  35.9 4.3 %apply_recur.10 = (f32[24,16,128]{2,1,0:T(8,128)S(1)}, f32[24,16,128]{2,1,0:T(8,128)S(1)}) custom-call(s32[578]{0:T(1024)S(1)} %get-tuple-element.141.refs_0_, bf16[288,128,256]{2,1,0:T(8,128)(2,1)S(1)} %get-tuple-element.142.refs_1_, f32[48,1,128]{2,1,0:T(1,128)S(1)} %get-tuple-element.143.refs_2_, f32[24,16,128]{2,1,0:T(8,128)S(1)} %get-tuple-element.146.refs_3_.refs_7_, ...), custom_call_target="tpu_custom_call" | custom-call | bytes 4194304 | tf_op jit(solution)/shard_map/apply_recur/pallas_call | solution.py:195
  40.8 8.2 %collective-permute-start.5 = (f32[24,16,128]{2,1,0:T(8,128)S(1)}, f32[24,16,128]{2,1,0:T(8,128)S(1)}, u32[]{:S(2)}, u32[]{:S(2)}) collective-permute-start(f32[24,16,128]{2,1,0:T(8,128)S(1)} %get-tuple-element.149.refs_4_.refs_8_), channel_id=1, source_target_pairs={{0,28},{4,8},{8,4},{12,16},{16,12},{20,24},{24,20},{28,0},{1,29},{... | collective-permute-start | bytes 589832 | tf_op jit(solution)/shard_map/ppermute | solution.py:349
  49.0 4.3 %apply_recur.13 = (f32[24,16,128]{2,1,0:T(8,128)S(1)}, f32[24,16,128]{2,1,0:T(8,128)S(1)}) custom-call(s32[578]{0:T(1024)S(1)} %get-tuple-element.141.refs_0_, bf16[288,128,256]{2,1,0:T(8,128)(2,1)S(1)} %get-tuple-element.142.refs_1_, f32[48,1,128]{2,1,0:T(1,128)S(1)} %get-tuple-element.143.refs_2_, f32[24,16,128]{2,1,0:T(8,128)S(1)} %get-tuple-element.158.refs_3_.refs_7_, ...), custom_call_target="tpu_custom_call" | custom-call | bytes 4194304 | tf_op jit(solution)/shard_map/apply_recur/pallas_call | solution.py:195
  53.4 2.0 collective-permute-start.17
  55.3 4.3 %apply_recur.11 = (f32[24,16,128]{2,1,0:T(8,128)S(1)}, f32[24,16,128]{2,1,0:T(8,128)S(1)}) custom-call(s32[578]{0:T(1024)S(1)} %get-tuple-element.141.refs_0_, bf16[288,128,256]{2,1,0:T(8,128)(2,1)S(1)} %get-tuple-element.142.refs_1_, f32[48,1,128]{2,1,0:T(1,128)S(1)} %get-tuple-element.143.refs_2_, f32[24,16,128]{2,1,0:T(8,128)S(1)} %get-tuple-element.148.refs_3_.refs_7_, ...), custom_call_target="tpu_custom_call" | custom-call | bytes 4194304 | tf_op jit(solution)/shard_map/apply_recur/pallas_call | solution.py:195
  59.7 2.9 %collective-permute-start.7 = (f32[24,16,128]{2,1,0:T(8,128)S(1)}, f32[24,16,128]{2,1,0:T(8,128)S(1)}, u32[]{:S(2)}, u32[]{:S(2)}) collective-permute-start(f32[24,16,128]{2,1,0:T(8,128)S(1)} %get-tuple-element.151.refs_4_), channel_id=1, source_target_pairs={{0,28},{4,8},{8,4},{12,16},{16,12},{20,24},{24,20},{28,0},{1,29},{... | collective-permute-start | bytes 589832 | tf_op jit(solution)/shard_map/ppermute | solution.py:349
  62.6 4.3 %apply_recur.14 = (f32[24,16,128]{2,1,0:T(8,128)S(1)}, f32[24,16,128]{2,1,0:T(8,128)S(1)}) custom-call(s32[578]{0:T(1024)S(1)} %get-tuple-element.141.refs_0_, bf16[288,128,256]{2,1,0:T(8,128)(2,1)S(1)} %get-tuple-element.142.refs_1_, f32[48,1,128]{2,1,0:T(1,128)S(1)} %get-tuple-element.143.refs_2_, f32[24,16,128]{2,1,0:T(8,128)S(1)} %get-tuple-element.160.refs_3_.refs_7_, ...), custom_call_target="tpu_custom_call" | custom-call | bytes 4194304 | tf_op jit(solution)/shard_map/apply_recur/pallas_call | solution.py:195
  68.0 4.9 %collective-permute-start.19 = (f32[24,16,128]{2,1,0:T(8,128)S(1)}, f32[24,16,128]{2,1,0:T(8,128)S(1)}, u32[]{:S(2)}, u32[]{:S(2)}) collective-permute-start(f32[24,16,128]{2,1,0:T(8,128)S(1)} %get-tuple-element.163.refs_4_), channel_id=1, source_target_pairs={{0,28},{4,8},{8,4},{12,16},{16,12},{20,24},{24,20},{28,0},{1,29},{... | collective-permute-start | bytes 589832 | tf_op jit(solution)/shard_map/ppermute | solution.py:349
  72.9 4.3 %apply_recur.12 = (f32[24,16,128]{2,1,0:T(8,128)S(1)}, f32[24,16,128]{2,1,0:T(8,128)S(1)}) custom-call(s32[578]{0:T(1024)S(1)} %get-tuple-element.141.refs_0_, bf16[288,128,256]{2,1,0:T(8,128)(2,1)S(1)} %get-tuple-element.142.refs_1_, f32[48,1,128]{2,1,0:T(1,128)S(1)} %get-tuple-element.143.refs_2_, f32[24,16,128]{2,1,0:T(8,128)S(1)} %get-tuple-element.150.refs_3_, ...), custom_call_target="tpu_custom_call" | custom-call | bytes 4194304 | tf_op jit(solution)/shard_map/apply_recur/pallas_call | solution.py:195
  77.3 1.9 collective-permute-start.9
  79.2 4.4 %apply_recur_parts.2 = (f32[24,16,128]{2,1,0:T(8,128)S(1)}, f32[24,16,128]{2,1,0:T(8,128)S(1)}, f32[12,32,128]{2,1,0:T(8,128)S(1)}, f32[12,32,128]{2,1,0:T(8,128...) custom-call(s32[578]{0:T(1024)S(1)} %get-tuple-element.141.refs_0_, ...), custom_call_target="tpu_custom_call" | custom-call | bytes 4194304 | tf_op jit(solution)/shard_map/apply_recur_parts/pallas_call | solution.py:195
  83.8 9.5 %collective-permute-start.28 = (f32[24,16,128]{2,1,0:T(8,128)S(1)}, f32[24,16,128]{2,1,0:T(8,128)S(1)}, u32[]{:S(2)}, u32[]{:S(2)}) collective-permute-start(f32[24,16,128]{2,1,0:T(8,128)S(1)} %get-tuple-element.183.refs_4_.refs_8_), channel_id=1, source_target_pairs={{0,28},{4,8},{8,4},{12,16},{16,12},{20,24},{24,20},{28,0},{1,29},{... | collective-permute-start | bytes 589832 | tf_op jit(solution)/shard_map/ppermute | solution.py:349
  95.1 4.3 %apply.5 = (f32[24,16,128]{2,1,0:T(8,128)S(1)}, f32[24,16,128]{2,1,0:T(8,128)S(1)}) custom-call(s32[578]{0:T(1024)S(1)} %get-tuple-element.141.refs_0_, bf16[288,128,256]{2,1,0:T(8,128)(2,1)S(1)} %get-tuple-element.142.refs_1_, f32[48,1,128]{2,1,0:T(1,128)S(1)} %get-tuple-element.143.refs_2_, f32[24,16,128]{2,1,0:T(8,128)S(1)} %get-tuple-element.169.refs_3_.refs_9_.refs_7_, ...), custom_call_target="tpu_custom_call" | custom-call | bytes 4194304 | tf_op jit(solution)/shard_map/apply/pallas_call | solution.py:195
  99.5 2.1 collective-permute-start.11
  101.6 4.5 %apply_parts.2 = (f32[24,16,128]{2,1,0:T(8,128)S(1)}, f32[24,16,128]{2,1,0:T(8,128)S(1)}, f32[12,32,128]{2,1,0:T(8,128)S(1)}, f32[12,32,128]{2,1,0:T(8,128)S(1)}...) custom-call(s32[578]{0:T(1024)S(1)} %get-tuple-element.141.refs_0_, ...), custom_call_target="tpu_custom_call" | custom-call | bytes 4194304 | tf_op jit(solution)/shard_map/apply_parts/pallas_call | solution.py:195
  106.3 2.7 %collective-permute-start.30 = (f32[24,16,128]{2,1,0:T(8,128)S(1)}, f32[24,16,128]{2,1,0:T(8,128)S(1)}, u32[]{:S(2)}, u32[]{:S(2)}) collective-permute-start(f32[24,16,128]{2,1,0:T(8,128)S(1)} %get-tuple-element.205.refs_4_.refs_8_), channel_id=1, source_target_pairs={{0,28},{4,8},{8,4},{12,16},{16,12},{20,24},{24,20},{28,0},{1,29},{... | collective-permute-start | bytes 589832 | tf_op jit(solution)/shard_map/ppermute | solution.py:349
  111.4 4.3 %apply_recur.15 = (f32[24,16,128]{2,1,0:T(8,128)S(1)}, f32[24,16,128]{2,1,0:T(8,128)S(1)}) custom-call(s32[578]{0:T(1024)S(1)} %get-tuple-element.141.refs_0_, bf16[288,128,256]{2,1,0:T(8,128)(2,1)S(1)} %get-tuple-element.142.refs_1_, f32[48,1,128]{2,1,0:T(1,128)S(1)} %get-tuple-element.143.refs_2_, f32[24,16,128]{2,1,0:T(8,128)S(1)} %get-tuple-element.188.refs_3_.refs_7_, ...), custom_call_target="tpu_custom_call" | custom-call | bytes 4194304 | tf_op jit(solution)/shard_map/apply_recur/pallas_call | solution.py:195
  121.3 4.3 %apply_recur.16 = (f32[24,16,128]{2,1,0:T(8,128)S(1)}, f32[24,16,128]{2,1,0:T(8,128)S(1)}) custom-call(s32[578]{0:T(1024)S(1)} %get-tuple-element.141.refs_0_, bf16[288,128,256]{2,1,0:T(8,128)(2,1)S(1)} %get-tuple-element.142.refs_1_, f32[48,1,128]{2,1,0:T(1,128)S(1)} %get-tuple-element.143.refs_2_, f32[24,16,128]{2,1,0:T(8,128)S(1)} %get-tuple-element.204.refs_3_.refs_7_, ...), custom_call_target="tpu_custom_call" | custom-call | bytes 4194304 | tf_op jit(solution)/shard_map/apply_recur/pallas_call | solution.py:195
  129.1 4.3 %apply_recur.17 = (f32[24,16,128]{2,1,0:T(8,128)S(1)}, f32[24,16,128]{2,1,0:T(8,128)S(1)}) custom-call(s32[578]{0:T(1024)S(1)} %get-tuple-element.141.refs_0_, bf16[288,128,256]{2,1,0:T(8,128)(2,1)S(1)} %get-tuple-element.142.refs_1_, f32[48,1,128]{2,1,0:T(1,128)S(1)} %get-tuple-element.143.refs_2_, f32[24,16,128]{2,1,0:T(8,128)S(1)} %get-tuple-element.210.refs_3_.refs_7_, ...), custom_call_target="tpu_custom_call" | custom-call | bytes 4194304 | tf_op jit(solution)/shard_map/apply_recur/pallas_call | solution.py:195
  133.4 2.0 collective-permute-start.31
  135.3 3.7 %collective-permute-done.33 = f32[128,128]{1,0:T(8,128)S(1)} collective-permute-done((f32[128,128]{1,0:T(8,128)S(1)}, f32[128,128]{1,0:T(8,128)S(1)}, u32[]{:S(2)}, u32[]{:S(2)}) %collective-permute-start.33) | collective-permute-done | bytes 65568 | tf_op jit(solution)/shard_map/ppermute | solution.py:353
  139.1 2.8 %collective-permute-start.32 = (f32[24,16,128]{2,1,0:T(8,128)S(1)}, f32[24,16,128]{2,1,0:T(8,128)S(1)}, u32[]{:S(2)}, u32[]{:S(2)}) collective-permute-start(f32[24,16,128]{2,1,0:T(8,128)S(1)} %get-tuple-element.191.refs_4_), channel_id=1, source_target_pairs={{0,28},{4,8},{8,4},{12,16},{16,12},{20,24},{24,20},{28,0},{1,29},{... | collective-permute-start | bytes 589832 | tf_op jit(solution)/shard_map/ppermute | solution.py:349
  141.9 4.3 %apply_recur.18 = (f32[24,16,128]{2,1,0:T(8,128)S(1)}, f32[24,16,128]{2,1,0:T(8,128)S(1)}) custom-call(s32[578]{0:T(1024)S(1)} %get-tuple-element.141.refs_0_, bf16[288,128,256]{2,1,0:T(8,128)(2,1)S(1)} %get-tuple-element.142.refs_1_, f32[48,1,128]{2,1,0:T(1,128)S(1)} %get-tuple-element.143.refs_2_, f32[24,16,128]{2,1,0:T(8,128)S(1)} %get-tuple-element.221.refs_3_.refs_7_, ...), custom_call_target="tpu_custom_call" | custom-call | bytes 4194304 | tf_op jit(solution)/shard_map/apply_recur/pallas_call | solution.py:195
  146.4 1.9 collective-permute-start.44
  149.8 6.2 %collective-permute-done.34 = f32[128,128]{1,0:T(8,128)S(1)} collective-permute-done((f32[128,128]{1,0:T(8,128)S(1)}, f32[128,128]{1,0:T(8,128)S(1)}, u32[]{:S(2)}, u32[]{:S(2)}) %collective-permute-start.34) | collective-permute-done | bytes 65568 | tf_op jit(solution)/shard_map/ppermute | solution.py:353
  156.0 4.3 %apply_recur.19 = (f32[24,16,128]{2,1,0:T(8,128)S(1)}, f32[24,16,128]{2,1,0:T(8,128)S(1)}) custom-call(s32[578]{0:T(1024)S(1)} %get-tuple-element.141.refs_0_, bf16[288,128,256]{2,1,0:T(8,128)(2,1)S(1)} %get-tuple-element.142.refs_1_, f32[48,1,128]{2,1,0:T(1,128)S(1)} %get-tuple-element.143.refs_2_, f32[24,16,128]{2,1,0:T(8,128)S(1)} %get-tuple-element.190.refs_3_, ...), custom_call_target="tpu_custom_call" | custom-call | bytes 4194304 | tf_op jit(solution)/shard_map/apply_recur/pallas_call | solution.py:195
  160.3 2.7 %collective-permute-start.40 = (f32[24,16,128]{2,1,0:T(8,128)S(1)}, f32[24,16,128]{2,1,0:T(8,128)S(1)}, u32[]{:S(2)}, u32[]{:S(2)}) collective-permute-start(f32[24,16,128]{2,1,0:T(8,128)S(1)} %get-tuple-element.212.refs_9_.refs_3_), channel_id=1, source_target_pairs={{0,4},{4,0},{8,12},{12,8},{16,20},{20,16},{24,28},{28,24},{1,5},{5... | collective-permute-start | bytes 589832 | tf_op jit(solution)/shard_map/ppermute | solution.py:349
  164.4 4.6 %apply_recur_parts.3 = (f32[24,16,128]{2,1,0:T(8,128)S(1)}, f32[24,16,128]{2,1,0:T(8,128)S(1)}, f32[12,32,128]{2,1,0:T(8,128)S(1)}, f32[12,32,128]{2,1,0:T(8,128...) custom-call(s32[578]{0:T(1024)S(1)} %get-tuple-element.141.refs_0_, ...), custom_call_target="tpu_custom_call" | custom-call | bytes 4194304 | tf_op jit(solution)/shard_map/apply_recur_parts/pallas_call | solution.py:195
  171.0 2.2 collective-permute-start.50
  174.4 4.1 %factor.2.inv_ref.refs_0_ = f32[128,128]{1,0:T(8,128)S(1)} custom-call(f32[128,128]{1,0:T(8,128)S(1)} %add.67.g_ref), custom_call_target="tpu_custom_call" | custom-call | tf_op jit(solution)/shard_map/factor/pallas_call | solution.py:42
  180.2 2.4 %turn.1 = (f32[12,128,128]{2,1,0:T(8,128)S(1)}, f32[128,128]{1,0:T(8,128)S(1)}) custom-call(s32[2]{0:T(128)S(1)} %pad_add_fusion.ids_ref, f32[128,128]{1,0:T(8,128)S(1)} %factor.2.inv_ref.refs_0_, f32[12,32,128]{2,1,0:T(8,128)S(1)} %get-tuple-element.223.refs_0_, f32[12,32,128]{2,1,0:T(8,128)S(1)} %collective-permute-done.45.refs_1_, ...), custom_call_target="tpu_custom_call" | custom-call | tf_op jit(solution)/shard_map/turn/pallas_call | solution.py:42
  185.4 4.2 %apply.7 = (f32[24,16,128]{2,1,0:T(8,128)S(1)}, f32[24,16,128]{2,1,0:T(8,128)S(1)}) custom-call(s32[578]{0:T(1024)S(1)} %get-tuple-element.141.refs_0_, bf16[288,128,256]{2,1,0:T(8,128)(2,1)S(1)} %get-tuple-element.142.refs_1_, f32[48,1,128]{2,1,0:T(1,128)S(1)} %get-tuple-element.143.refs_2_, f32[24,16,128]{2,1,0:T(8,128)S(1)} %get-tuple-element.212.refs_9_.refs_3_, ...), custom_call_target="tpu_custom_call" | custom-call | bytes 4194304 | tf_op jit(solution)/shard_map/apply/pallas_call | solution.py:195
  189.8 5.3 %apply_parts.3 = (f32[24,16,128]{2,1,0:T(8,128)}, f32[24,16,128]{2,1,0:T(8,128)}, f32[12,32,128]{2,1,0:T(8,128)S(1)}, f32[12,32,128]{2,1,0:T(8,128)S(1)}, f32[12...) custom-call(s32[578]{0:T(1024)S(1)} %get-tuple-element.141.refs_0_, ...), custom_call_target="tpu_custom_call" | custom-call | bytes 4194304 | tf_op jit(solution)/shard_map/apply_parts/pallas_call | solution.py:195
  198.8 2.6 %collective-permute-done.53 = f32[128,128]{1,0:T(8,128)S(1)} collective-permute-done((f32[128,128]{1,0:T(8,128)S(1)}, f32[128,128]{1,0:T(8,128)S(1)}, u32[]{:S(2)}, u32[]{:S(2)}) %collective-permute-start.53) | collective-permute-done | bytes 65568 | tf_op jit(solution)/shard_map/ppermute | solution.py:353
  204.5 1.9 collective-permute-start.62
  210.8 2.3 collective-permute-start.60
  213.2 2.1 collective-permute-start.58
  215.3 4.1 %factor.3.inv_ref.refs_2_ = f32[128,128]{1,0:T(8,128)S(1)} custom-call(f32[128,128]{1,0:T(8,128)S(1)} %add.72.g_ref), custom_call_target="tpu_custom_call" | custom-call | tf_op jit(solution)/shard_map/factor/pallas_call | solution.py:42
  225.2 3.7 %collective-permute-done.64 = f32[128,128]{1,0:T(8,128)S(1)} collective-permute-done((f32[128,128]{1,0:T(8,128)S(1)}, f32[128,128]{1,0:T(8,128)S(1)}, u32[]{:S(2)}, u32[]{:S(2)}) %collective-permute-start.64) | collective-permute-done | bytes 65568 | tf_op jit(solution)/shard_map/ppermute | solution.py:353
  232.1 3.1 %collective-permute-done.67 = f32[2,32,128]{2,1,0:T(8,128)S(1)} collective-permute-done((f32[2,32,128]{2,1,0:T(8,128)S(1)}, f32[2,32,128]{2,1,0:T(8,128)S(1)}, u32[]{:S(2)}, u32[]{:S(2)}) %collective-permute-start.67) | collective-permute-done | bytes 32800 | tf_op jit(solution)/shard_map/ppermute | solution.py:353
  (144 shorter events, 52.9 us)
Async XLA Ops:
  2.5 17.4 %collective-permute-start = (f32[24,16,128]{2,1,0:T(8,128)S(1)}, f32[24,16,128]{2,1,0:T(8,128)S(1)}, u32[]{:S(2)}, u32[]{:S(2)}) collective-permute-start(f32[24,16,128]{2,1,0:T(8,128)S(1)} %get-tuple-element.144.refs_3_.refs_7_), channel_id=1, source_target_pairs={{0,4},{4,0},{8,12},{12,8},{16,20},{20,16},{24,28},{28,24},{1,5},{5... | collective-permute-start | bytes 589832 | tf_op jit(solution)/shard_map/ppermute | solution.py:349
  5.5 14.4 %collective-permute-start.1 = (f32[24,16,128]{2,1,0:T(8,128)S(1)}, f32[24,16,128]{2,1,0:T(8,128)S(1)}, u32[]{:S(2)}, u32[]{:S(2)}) collective-permute-start(f32[24,16,128]{2,1,0:T(8,128)S(1)} %get-tuple-element.145.refs_4_.refs_8_), channel_id=1, source_target_pairs={{0,28},{4,8},{8,4},{12,16},{16,12},{20,24},{24,20},{28,0},{1,29},{... | collective-permute-start | bytes 589832 | tf_op jit(solution)/shard_map/ppermute | solution.py:349
  9.1 20.5 %collective-permute-start.12 = (f32[24,16,128]{2,1,0:T(8,128)S(1)}, f32[24,16,128]{2,1,0:T(8,128)S(1)}, u32[]{:S(2)}, u32[]{:S(2)}) collective-permute-start(f32[24,16,128]{2,1,0:T(8,128)S(1)} %get-tuple-element.156.refs_3_.refs_7_), channel_id=1, source_target_pairs={{0,4},{4,0},{8,12},{12,8},{16,20},{20,16},{24,28},{28,24},{1,5},{5... | collective-permute-start | bytes 589832 | tf_op jit(solution)/shard_map/ppermute | solution.py:349
  9.1 20.5 %collective-permute-start.13 = (f32[24,16,128]{2,1,0:T(8,128)S(1)}, f32[24,16,128]{2,1,0:T(8,128)S(1)}, u32[]{:S(2)}, u32[]{:S(2)}) collective-permute-start(f32[24,16,128]{2,1,0:T(8,128)S(1)} %get-tuple-element.157.refs_4_.refs_8_), channel_id=1, source_target_pairs={{0,28},{4,8},{8,4},{12,16},{16,12},{20,24},{24,20},{28,0},{1,29},{... | collective-permute-start | bytes 589832 | tf_op jit(solution)/shard_map/ppermute | solution.py:349
  24.2 11.7 %collective-permute-start.2 = (f32[24,16,128]{2,1,0:T(8,128)S(1)}, f32[24,16,128]{2,1,0:T(8,128)S(1)}, u32[]{:S(2)}, u32[]{:S(2)}) collective-permute-start(f32[24,16,128]{2,1,0:T(8,128)S(1)} %get-tuple-element.146.refs_3_.refs_7_), channel_id=1, source_target_pairs={{0,4},{4,0},{8,12},{12,8},{16,20},{20,16},{24,28},{28,24},{1,5},{5... | collective-permute-start | bytes 589832 | tf_op jit(solution)/shard_map/ppermute | solution.py:349
  33.9 15.1 %collective-permute-start.14 = (f32[24,16,128]{2,1,0:T(8,128)S(1)}, f32[24,16,128]{2,1,0:T(8,128)S(1)}, u32[]{:S(2)}, u32[]{:S(2)}) collective-permute-start(f32[24,16,128]{2,1,0:T(8,128)S(1)} %get-tuple-element.158.refs_3_.refs_7_), channel_id=1, source_target_pairs={{0,4},{4,0},{8,12},{12,8},{16,20},{20,16},{24,28},{28,24},{1,5},{5... | collective-permute-start | bytes 589832 | tf_op jit(solution)/shard_map/ppermute | solution.py:349
  34.0 15.0 %collective-permute-start.15 = (f32[24,16,128]{2,1,0:T(8,128)S(1)}, f32[24,16,128]{2,1,0:T(8,128)S(1)}, u32[]{:S(2)}, u32[]{:S(2)}) collective-permute-start(f32[24,16,128]{2,1,0:T(8,128)S(1)} %get-tuple-element.159.refs_4_.refs_8_), channel_id=1, source_target_pairs={{0,28},{4,8},{8,4},{12,16},{16,12},{20,24},{24,20},{28,0},{1,29},{... | collective-permute-start | bytes 589832 | tf_op jit(solution)/shard_map/ppermute | solution.py:349
  40.1 15.2 %collective-permute-start.4 = (f32[24,16,128]{2,1,0:T(8,128)S(1)}, f32[24,16,128]{2,1,0:T(8,128)S(1)}, u32[]{:S(2)}, u32[]{:S(2)}) collective-permute-start(f32[24,16,128]{2,1,0:T(8,128)S(1)} %get-tuple-element.148.refs_3_.refs_7_), channel_id=1, source_target_pairs={{0,4},{4,0},{8,12},{12,8},{16,20},{20,16},{24,28},{28,24},{1,5},{5... | collective-permute-start | bytes 589832 | tf_op jit(solution)/shard_map/ppermute | solution.py:349
  40.8 14.5 %collective-permute-start.5 = (f32[24,16,128]{2,1,0:T(8,128)S(1)}, f32[24,16,128]{2,1,0:T(8,128)S(1)}, u32[]{:S(2)}, u32[]{:S(2)}) collective-permute-start(f32[24,16,128]{2,1,0:T(8,128)S(1)} %get-tuple-element.149.refs_4_.refs_8_), channel_id=1, source_target_pairs={{0,28},{4,8},{8,4},{12,16},{16,12},{20,24},{24,20},{28,0},{1,29},{... | collective-permute-start | bytes 589832 | tf_op jit(solution)/shard_map/ppermute | solution.py:349
  59.6 13.3 %collective-permute-start.6 = (f32[24,16,128]{2,1,0:T(8,128)S(1)}, f32[24,16,128]{2,1,0:T(8,128)S(1)}, u32[]{:S(2)}, u32[]{:S(2)}) collective-permute-start(f32[24,16,128]{2,1,0:T(8,128)S(1)} %get-tuple-element.150.refs_3_), channel_id=1, source_target_pairs={{0,4},{4,0},{8,12},{12,8},{16,20},{20,16},{24,28},{28,24},{1,5},{5... | collective-permute-start | bytes 589832 | tf_op jit(solution)/shard_map/ppermute | solution.py:349
  59.7 13.2 %collective-permute-start.7 = (f32[24,16,128]{2,1,0:T(8,128)S(1)}, f32[24,16,128]{2,1,0:T(8,128)S(1)}, u32[]{:S(2)}, u32[]{:S(2)}) collective-permute-start(f32[24,16,128]{2,1,0:T(8,128)S(1)} %get-tuple-element.151.refs_4_), channel_id=1, source_target_pairs={{0,28},{4,8},{8,4},{12,16},{16,12},{20,24},{24,20},{28,0},{1,29},{... | collective-permute-start | bytes 589832 | tf_op jit(solution)/shard_map/ppermute | solution.py:349
  66.9 12.3 %collective-permute-start.18 = (f32[24,16,128]{2,1,0:T(8,128)S(1)}, f32[24,16,128]{2,1,0:T(8,128)S(1)}, u32[]{:S(2)}, u32[]{:S(2)}) collective-permute-start(f32[24,16,128]{2,1,0:T(8,128)S(1)} %get-tuple-element.162.refs_3_), channel_id=1, source_target_pairs={{0,4},{4,0},{8,12},{12,8},{16,20},{20,16},{24,28},{28,24},{1,5},{5... | collective-permute-start | bytes 589832 | tf_op jit(solution)/shard_map/ppermute | solution.py:349
  68.0 11.2 %collective-permute-start.19 = (f32[24,16,128]{2,1,0:T(8,128)S(1)}, f32[24,16,128]{2,1,0:T(8,128)S(1)}, u32[]{:S(2)}, u32[]{:S(2)}) collective-permute-start(f32[24,16,128]{2,1,0:T(8,128)S(1)} %get-tuple-element.163.refs_4_), channel_id=1, source_target_pairs={{0,28},{4,8},{8,4},{12,16},{16,12},{20,24},{24,20},{28,0},{1,29},{... | collective-permute-start | bytes 589832 | tf_op jit(solution)/shard_map/ppermute | solution.py:349
  77.2 16.0 %collective-permute-start.8 = (f32[24,16,128]{2,1,0:T(8,128)S(1)}, f32[24,16,128]{2,1,0:T(8,128)S(1)}, u32[]{:S(2)}, u32[]{:S(2)}) collective-permute-start(f32[24,16,128]{2,1,0:T(8,128)S(1)} %get-tuple-element.169.refs_3_.refs_9_.refs_7_), channel_id=1, source_target_pairs={{0,4},{4,0},{8,12},{12,8},{16,20},{20,16},{24,28},{28,24},{1,5},{5... | collective-permute-start | bytes 589832 | tf_op jit(solution)/shard_map/ppermute | solution.py:349
  77.3 17.5 %collective-permute-start.9 = (f32[24,16,128]{2,1,0:T(8,128)S(1)}, f32[24,16,128]{2,1,0:T(8,128)S(1)}, u32[]{:S(2)}, u32[]{:S(2)}) collective-permute-start(f32[24,16,128]{2,1,0:T(8,128)S(1)} %get-tuple-element.170.refs_4_.refs_10_.refs_8_), channel_id=1, source_target_pairs={{0,28},{4,8},{8,4},{12,16},{16,12},{20,24},{24,20},{28,0},{1,29},{... | collective-permute-start | bytes 589832 | tf_op jit(solution)/shard_map/ppermute | solution.py:349
  83.6 15.7 %collective-permute-start.27 = (f32[24,16,128]{2,1,0:T(8,128)S(1)}, f32[24,16,128]{2,1,0:T(8,128)S(1)}, u32[]{:S(2)}, u32[]{:S(2)}) collective-permute-start(f32[24,16,128]{2,1,0:T(8,128)S(1)} %get-tuple-element.182.refs_3_.refs_7_), channel_id=1, source_target_pairs={{0,4},{4,0},{8,12},{12,8},{16,20},{20,16},{24,28},{28,24},{1,5},{5... | collective-permute-start | bytes 589832 | tf_op jit(solution)/shard_map/ppermute | solution.py:349
  83.8 15.7 %collective-permute-start.28 = (f32[24,16,128]{2,1,0:T(8,128)S(1)}, f32[24,16,128]{2,1,0:T(8,128)S(1)}, u32[]{:S(2)}, u32[]{:S(2)}) collective-permute-start(f32[24,16,128]{2,1,0:T(8,128)S(1)} %get-tuple-element.183.refs_4_.refs_8_), channel_id=1, source_target_pairs={{0,28},{4,8},{8,4},{12,16},{16,12},{20,24},{24,20},{28,0},{1,29},{... | collective-permute-start | bytes 589832 | tf_op jit(solution)/shard_map/ppermute | solution.py:349
  93.2 12.9 %collective-permute-start.20 = (f32[12,32,128]{2,1,0:T(8,128)S(1)}, f32[12,32,128]{2,1,0:T(8,128)S(1)}, u32[]{:S(2)}, u32[]{:S(2)}) collective-permute-start(f32[12,32,128]{2,1,0:T(8,128)S(1)} %get-tuple-element.165), channel_id=1, source_target_pairs={{0,1},{1,0},{2,3},{3,2},{4,5},{5,4},{6,7},{7,6},{8,9},{9,8},{10,11... | collective-permute-start | bytes 589832 | tf_op jit(solution)/shard_map/ppermute | solution.py:353
  93.2 13.0 %collective-permute-start.21 = (f32[12,32,128]{2,1,0:T(8,128)S(1)}, f32[12,32,128]{2,1,0:T(8,128)S(1)}, u32[]{:S(2)}, u32[]{:S(2)}) collective-permute-start(f32[12,32,128]{2,1,0:T(8,128)S(1)} %get-tuple-element.166), channel_id=1, source_target_pairs={{0,2},{1,3},{2,0},{3,1},{4,6},{5,7},{6,4},{7,5},{8,10},{9,11},{10,... | collective-permute-start | bytes 589832 | tf_op jit(solution)/shard_map/ppermute | solution.py:353
  94.8 11.5 %collective-permute-start.22 = (f32[12,32,128]{2,1,0:T(8,128)S(1)}, f32[12,32,128]{2,1,0:T(8,128)S(1)}, u32[]{:S(2)}, u32[]{:S(2)}) collective-permute-start(f32[12,32,128]{2,1,0:T(8,128)S(1)} %get-tuple-element.167), channel_id=1, source_target_pairs={{0,3},{1,2},{2,1},{3,0},{4,7},{5,6},{6,5},{7,4},{8,11},{9,10},{10,... | collective-permute-start | bytes 589832 | tf_op jit(solution)/shard_map/ppermute | solution.py:353
  99.4 12.0 %collective-permute-start.10 = (f32[24,16,128]{2,1,0:T(8,128)S(1)}, f32[24,16,128]{2,1,0:T(8,128)S(1)}, u32[]{:S(2)}, u32[]{:S(2)}) collective-permute-start(f32[24,16,128]{2,1,0:T(8,128)S(1)} %get-tuple-element.188.refs_3_.refs_7_), channel_id=1, source_target_pairs={{0,4},{4,0},{8,12},{12,8},{16,20},{20,16},{24,28},{28,24},{1,5},{5... | collective-permute-start | bytes 589832 | tf_op jit(solution)/shard_map/ppermute | solution.py:349
  99.5 11.9 %collective-permute-start.11 = (f32[24,16,128]{2,1,0:T(8,128)S(1)}, f32[24,16,128]{2,1,0:T(8,128)S(1)}, u32[]{:S(2)}, u32[]{:S(2)}) collective-permute-start(f32[24,16,128]{2,1,0:T(8,128)S(1)} %get-tuple-element.189.refs_4_.refs_8_), channel_id=1, source_target_pairs={{0,28},{4,8},{8,4},{12,16},{16,12},{20,24},{24,20},{28,0},{1,29},{... | collective-permute-start | bytes 589832 | tf_op jit(solution)/shard_map/ppermute | solution.py:349
  106.1 12.4 %collective-permute-start.37 = (f32[12,32,128]{2,1,0:T(8,128)S(1)}, f32[12,32,128]{2,1,0:T(8,128)S(1)}, u32[]{:S(2)}, u32[]{:S(2)}) collective-permute-start(f32[12,32,128]{2,1,0:T(8,128)S(1)} %get-tuple-element.201), channel_id=1, source_target_pairs={{0,1},{1,0},{2,3},{3,2},{4,5},{5,4},{6,7},{7,6},{8,9},{9,8},{10,11... | collective-permute-start | bytes 589832 | tf_op jit(solution)/shard_map/ppermute | solution.py:353
  106.2 13.9 %collective-permute-start.29 = (f32[24,16,128]{2,1,0:T(8,128)S(1)}, f32[24,16,128]{2,1,0:T(8,128)S(1)}, u32[]{:S(2)}, u32[]{:S(2)}) collective-permute-start(f32[24,16,128]{2,1,0:T(8,128)S(1)} %get-tuple-element.204.refs_3_.refs_7_), channel_id=1, source_target_pairs={{0,4},{4,0},{8,12},{12,8},{16,20},{20,16},{24,28},{28,24},{1,5},{5... | collective-permute-start | bytes 589832 | tf_op jit(solution)/shard_map/ppermute | solution.py:349
  106.3 15.0 %collective-permute-start.30 = (f32[24,16,128]{2,1,0:T(8,128)S(1)}, f32[24,16,128]{2,1,0:T(8,128)S(1)}, u32[]{:S(2)}, u32[]{:S(2)}) collective-permute-start(f32[24,16,128]{2,1,0:T(8,128)S(1)} %get-tuple-element.205.refs_4_.refs_8_), channel_id=1, source_target_pairs={{0,28},{4,8},{8,4},{12,16},{16,12},{20,24},{24,20},{28,0},{1,29},{... | collective-permute-start | bytes 589832 | tf_op jit(solution)/shard_map/ppermute | solution.py:349
  115.7 11.9 %collective-permute-start.23 = (f32[24,16,128]{2,1,0:T(8,128)S(1)}, f32[24,16,128]{2,1,0:T(8,128)S(1)}, u32[]{:S(2)}, u32[]{:S(2)}) collective-permute-start(f32[24,16,128]{2,1,0:T(8,128)S(1)} %get-tuple-element.210.refs_3_.refs_7_), channel_id=1, source_target_pairs={{0,4},{4,0},{8,12},{12,8},{16,20},{20,16},{24,28},{28,24},{1,5},{5... | collective-permute-start | bytes 589832 | tf_op jit(solution)/shard_map/ppermute | solution.py:349
  117.1 11.8 %collective-permute-start.24 = (f32[24,16,128]{2,1,0:T(8,128)S(1)}, f32[24,16,128]{2,1,0:T(8,128)S(1)}, u32[]{:S(2)}, u32[]{:S(2)}) collective-permute-start(f32[24,16,128]{2,1,0:T(8,128)S(1)} %get-tuple-element.211.refs_4_.refs_8_), channel_id=1, source_target_pairs={{0,28},{4,8},{8,4},{12,16},{16,12},{20,24},{24,20},{28,0},{1,29},{... | collective-permute-start | bytes 589832 | tf_op jit(solution)/shard_map/ppermute | solution.py:349
  120.1 13.2 %collective-permute-start.38 = (f32[12,32,128]{2,1,0:T(8,128)S(1)}, f32[12,32,128]{2,1,0:T(8,128)S(1)}, u32[]{:S(2)}, u32[]{:S(2)}) collective-permute-start(f32[12,32,128]{2,1,0:T(8,128)S(1)} %get-tuple-element.202), channel_id=1, source_target_pairs={{0,2},{1,3},{2,0},{3,1},{4,6},{5,7},{6,4},{7,5},{8,10},{9,11},{10,... | collective-permute-start | bytes 589832 | tf_op jit(solution)/shard_map/ppermute | solution.py:353
  121.3 20.5 %collective-permute-start.39 = (f32[12,32,128]{2,1,0:T(8,128)S(1)}, f32[12,32,128]{2,1,0:T(8,128)S(1)}, u32[]{:S(2)}, u32[]{:S(2)}) collective-permute-start(f32[12,32,128]{2,1,0:T(8,128)S(1)} %get-tuple-element.203), channel_id=1, source_target_pairs={{0,3},{1,2},{2,1},{3,0},{4,7},{5,6},{6,5},{7,4},{8,11},{9,10},{10,... | collective-permute-start | bytes 589832 | tf_op jit(solution)/shard_map/ppermute | solution.py:353
  125.6 16.2 %collective-permute-start.35 = (f32[24,16,128]{2,1,0:T(8,128)S(1)}, f32[24,16,128]{2,1,0:T(8,128)S(1)}, u32[]{:S(2)}, u32[]{:S(2)}) collective-permute-start(f32[24,16,128]{2,1,0:T(8,128)S(1)} %get-tuple-element.221.refs_3_.refs_7_), channel_id=1, source_target_pairs={{0,4},{4,0},{8,12},{12,8},{16,20},{20,16},{24,28},{28,24},{1,5},{5... | collective-permute-start | bytes 589832 | tf_op jit(solution)/shard_map/ppermute | solution.py:349
  127.6 14.3 %collective-permute-start.36 = (f32[24,16,128]{2,1,0:T(8,128)S(1)}, f32[24,16,128]{2,1,0:T(8,128)S(1)}, u32[]{:S(2)}, u32[]{:S(2)}) collective-permute-start(f32[24,16,128]{2,1,0:T(8,128)S(1)} %get-tuple-element.222.refs_4_.refs_8_), channel_id=1, source_target_pairs={{0,28},{4,8},{8,4},{12,16},{16,12},{20,24},{24,20},{28,0},{1,29},{... | collective-permute-start | bytes 589832 | tf_op jit(solution)/shard_map/ppermute | solution.py:349
  128.9 10.2 %collective-permute-start.33 = (f32[128,128]{1,0:T(8,128)S(1)}, f32[128,128]{1,0:T(8,128)S(1)}, u32[]{:S(2)}, u32[]{:S(2)}) collective-permute-start(f32[128,128]{1,0:T(8,128)S(1)} %add.64), channel_id=1, source_target_pairs={{0,4},{4,0},{8,12},{12,8},{16,20},{20,16},{24,28},{28,24},{1,5},{5... | collective-permute-start | bytes 196616 | tf_op jit(solution)/shard_map/ppermute | solution.py:353
  133.4 22.7 %collective-permute-start.31 = (f32[24,16,128]{2,1,0:T(8,128)S(1)}, f32[24,16,128]{2,1,0:T(8,128)S(1)}, u32[]{:S(2)}, u32[]{:S(2)}) collective-permute-start(f32[24,16,128]{2,1,0:T(8,128)S(1)} %get-tuple-element.190.refs_3_), channel_id=1, source_target_pairs={{0,4},{4,0},{8,12},{12,8},{16,20},{20,16},{24,28},{28,24},{1,5},{5... | collective-permute-start | bytes 589832 | tf_op jit(solution)/shard_map/ppermute | solution.py:349
  139.1 17.0 %collective-permute-start.32 = (f32[24,16,128]{2,1,0:T(8,128)S(1)}, f32[24,16,128]{2,1,0:T(8,128)S(1)}, u32[]{:S(2)}, u32[]{:S(2)}) collective-permute-start(f32[24,16,128]{2,1,0:T(8,128)S(1)} %get-tuple-element.191.refs_4_), channel_id=1, source_target_pairs={{0,28},{4,8},{8,4},{12,16},{16,12},{20,24},{24,20},{28,0},{1,29},{... | collective-permute-start | bytes 589832 | tf_op jit(solution)/shard_map/ppermute | solution.py:349
  146.1 18.3 %collective-permute-start.43 = (f32[24,16,128]{2,1,0:T(8,128)S(1)}, f32[24,16,128]{2,1,0:T(8,128)S(1)}, u32[]{:S(2)}, u32[]{:S(2)}) collective-permute-start(f32[24,16,128]{2,1,0:T(8,128)S(1)} %get-tuple-element.206.refs_3_), channel_id=1, source_target_pairs={{0,4},{4,0},{8,12},{12,8},{16,20},{20,16},{24,28},{28,24},{1,5},{5... | collective-permute-start | bytes 589832 | tf_op jit(solution)/shard_map/ppermute | solution.py:349
  146.4 18.1 %collective-permute-start.44 = (f32[24,16,128]{2,1,0:T(8,128)S(1)}, f32[24,16,128]{2,1,0:T(8,128)S(1)}, u32[]{:S(2)}, u32[]{:S(2)}) collective-permute-start(f32[24,16,128]{2,1,0:T(8,128)S(1)} %get-tuple-element.207.refs_4_), channel_id=1, source_target_pairs={{0,28},{4,8},{8,4},{12,16},{16,12},{20,24},{24,20},{28,0},{1,29},{... | collective-permute-start | bytes 589832 | tf_op jit(solution)/shard_map/ppermute | solution.py:349
  160.3 10.7 %collective-permute-start.40 = (f32[24,16,128]{2,1,0:T(8,128)S(1)}, f32[24,16,128]{2,1,0:T(8,128)S(1)}, u32[]{:S(2)}, u32[]{:S(2)}) collective-permute-start(f32[24,16,128]{2,1,0:T(8,128)S(1)} %get-tuple-element.212.refs_9_.refs_3_), channel_id=1, source_target_pairs={{0,4},{4,0},{8,12},{12,8},{16,20},{20,16},{24,28},{28,24},{1,5},{5... | collective-permute-start | bytes 589832 | tf_op jit(solution)/shard_map/ppermute | solution.py:349
  163.0 10.1 %collective-permute-start.41 = (f32[24,16,128]{2,1,0:T(8,128)S(1)}, f32[24,16,128]{2,1,0:T(8,128)S(1)}, u32[]{:S(2)}, u32[]{:S(2)}) collective-permute-start(f32[24,16,128]{2,1,0:T(8,128)S(1)} %get-tuple-element.213.refs_10_.refs_4_), channel_id=1, source_target_pairs={{0,28},{4,8},{8,4},{12,16},{16,12},{20,24},{24,20},{28,0},{1,29},{... | collective-permute-start | bytes 589832 | tf_op jit(solution)/shard_map/ppermute | solution.py:349
  171.0 18.7 %collective-permute-start.50 = (f32[24,16,128]{2,1,0:T(8,128)S(1)}, f32[24,16,128]{2,1,0:T(8,128)S(1)}, u32[]{:S(2)}, u32[]{:S(2)}) collective-permute-start(f32[24,16,128]{2,1,0:T(8,128)S(1)} %get-tuple-element.228.refs_3_), channel_id=1, source_target_pairs={{0,4},{4,0},{8,12},{12,8},{16,20},{20,16},{24,28},{28,24},{1,5},{5... | collective-permute-start | bytes 589832 | tf_op jit(solution)/shard_map/ppermute | solution.py:349
  173.1 16.6 %collective-permute-start.51 = (f32[24,16,128]{2,1,0:T(8,128)S(1)}, f32[24,16,128]{2,1,0:T(8,128)S(1)}, u32[]{:S(2)}, u32[]{:S(2)}) collective-permute-start(f32[24,16,128]{2,1,0:T(8,128)S(1)} %get-tuple-element.229.refs_4_), channel_id=1, source_target_pairs={{0,28},{4,8},{8,4},{12,16},{16,12},{20,24},{24,20},{28,0},{1,29},{... | collective-permute-start | bytes 589832 | tf_op jit(solution)/shard_map/ppermute | solution.py:349
  195.2 11.2 %collective-permute-start.56 = (f32[12,32,128]{2,1,0:T(8,128)S(1)}, f32[12,32,128]{2,1,0:T(8,128)S(1)}, u32[]{:S(2)}, u32[]{:S(2)}) collective-permute-start(f32[12,32,128]{2,1,0:T(8,128)S(1)} %get-tuple-element.247), channel_id=1, source_target_pairs={{0,2},{1,3},{2,0},{3,1},{4,6},{5,7},{6,4},{7,5},{8,10},{9,11},{10,... | collective-permute-start | bytes 589832 | tf_op jit(solution)/shard_map/ppermute | solution.py:353
  196.0 11.6 %collective-permute-start.57 = (f32[12,32,128]{2,1,0:T(8,128)S(1)}, f32[12,32,128]{2,1,0:T(8,128)S(1)}, u32[]{:S(2)}, u32[]{:S(2)}) collective-permute-start(f32[12,32,128]{2,1,0:T(8,128)S(1)} %get-tuple-element.248), channel_id=1, source_target_pairs={{0,3},{1,2},{2,1},{3,0},{4,7},{5,6},{6,5},{7,4},{8,11},{9,10},{10,... | collective-permute-start | bytes 589832 | tf_op jit(solution)/shard_map/ppermute | solution.py:353
  203.2 10.0 %collective-permute-start.63 = (f32[128,128]{1,0:T(8,128)S(1)}, f32[128,128]{1,0:T(8,128)S(1)}, u32[]{:S(2)}, u32[]{:S(2)}) collective-permute-start(f32[128,128]{1,0:T(8,128)S(1)} %cross.1), channel_id=1, source_target_pairs={{0,24},{4,28},{8,16},{12,20},{16,8},{20,12},{24,0},{28,4},{1,25},{... | collective-permute-start | bytes 196616 | tf_op jit(solution)/shard_map/ppermute | solution.py:353
  204.5 16.3 %collective-permute-start.62 = (f32[128,128]{1,0:T(8,128)S(1)}, f32[128,128]{1,0:T(8,128)S(1)}, u32[]{:S(2)}, u32[]{:S(2)}) collective-permute-start(f32[128,128]{1,0:T(8,128)S(1)} %cross.1), channel_id=1, source_target_pairs={{0,16},{4,20},{8,24},{12,28},{16,0},{20,4},{24,8},{28,12},{1,17},{... | collective-permute-start | bytes 196616 | tf_op jit(solution)/shard_map/ppermute | solution.py:353
  206.4 14.3 %collective-permute-start.61 = (f32[128,128]{1,0:T(8,128)S(1)}, f32[128,128]{1,0:T(8,128)S(1)}, u32[]{:S(2)}, u32[]{:S(2)}) collective-permute-start(f32[128,128]{1,0:T(8,128)S(1)} %cross.1), channel_id=1, source_target_pairs={{0,8},{4,12},{8,0},{12,4},{16,24},{20,28},{24,16},{28,20},{1,9},{5... | collective-permute-start | bytes 196616 | tf_op jit(solution)/shard_map/ppermute | solution.py:353
  222.6 12.6 %collective-permute-start.69 = (f32[12,32,128]{2,1,0:T(8,128)S(1)}, f32[12,32,128]{2,1,0:T(8,128)S(1)}, u32[]{:S(2)}, u32[]{:S(2)}) collective-permute-start(f32[12,32,128]{2,1,0:T(8,128)S(1)} %get-tuple-element.268), channel_id=1, source_target_pairs={{0,1},{1,0},{2,3},{3,2},{4,5},{5,4},{6,7},{7,6},{8,9},{9,8},{10,11... | collective-permute-start | bytes 589832 | tf_op jit(solution)/shard_map/ppermute | solution.py:353
  222.6 12.6 %collective-permute-start.70 = (f32[12,32,128]{2,1,0:T(8,128)S(1)}, f32[12,32,128]{2,1,0:T(8,128)S(1)}, u32[]{:S(2)}, u32[]{:S(2)}) collective-permute-start(f32[12,32,128]{2,1,0:T(8,128)S(1)} %get-tuple-element.269), channel_id=1, source_target_pairs={{0,2},{1,3},{2,0},{3,1},{4,6},{5,7},{6,4},{7,5},{8,10},{9,11},{10,... | collective-permute-start | bytes 589832 | tf_op jit(solution)/shard_map/ppermute | solution.py:353
  223.6 11.6 %collective-permute-start.71 = (f32[12,32,128]{2,1,0:T(8,128)S(1)}, f32[12,32,128]{2,1,0:T(8,128)S(1)}, u32[]{:S(2)}, u32[]{:S(2)}) collective-permute-start(f32[12,32,128]{2,1,0:T(8,128)S(1)} %get-tuple-element.270), channel_id=1, source_target_pairs={{0,3},{1,2},{2,1},{3,0},{4,7},{5,6},{6,5},{7,4},{8,11},{9,10},{10,... | collective-permute-start | bytes 589832 | tf_op jit(solution)/shard_map/ppermute | solution.py:353
  (25 other events, 164.2 us)

commit v10 on v9

--- a/solution.py
+++ b/solution.py
@@ -51,13 +51,16 @@
     )(*args)
 
 
-def prep_kernel(rows, ids_ref, own_ref, col_ref, blk_ref, w_ref, inv_ref, table_ref, held_ref, eye_ref, sem_ref):
+def prep_kernel(rows, groups, ids_ref, own_ref, col_ref, blk_ref, w_ref, inv_ref, table_ref, held_ref, eye_ref, sem_ref):
     count, n, _ = held_ref.shape
     steps = sem_ref.shape[0]
     chunk = count // steps
     half = rows // 2
     me = ids_ref[0]
     odd = me % 2
+    base = me * rows
+    base_next = jnp.where(me == groups - 1, 0, me + 1) * rows
+    base_last = jnp.where(me == 0, groups - 1, me - 1) * rows
 
     def fetch(step):
         span = pl.ds(step * chunk, chunk)
@@ -78,12 +81,13 @@
             b = step * chunk + c
             r = own_ref[0, b]
             k = col_ref[0, b]
-            owner = k // rows
-            local = k - owner * rows
+            mine = (k >= base) & (k < base + rows)
+            ahead = (k >= base_next) & (k < base_next + half)
+            local = k - jnp.where(mine, base, jnp.where(ahead, base_next, base_last))
             upper = (local >= half).astype(I32)
             near = local - half * upper
             swap = odd * upper + (1 - odd) * (1 - upper)
-            slot = jnp.where(owner == me, near + half * swap, 2 * half + near + half * (1 - swap))
+            slot = jnp.where(mine, near + half * swap, 2 * half + near + half * (1 - swap))
             top = (r >= half).astype(I32)
             r_at = r + half * (1 - odd) * (1 - 2 * top)
             table_ref[2 + b] = slot
@@ -110,11 +114,11 @@
     inv_ref[...] = 1.0 / inv_ref[...]
 
 
-def prep(ids, own, col, blocks, rows):
+def prep(ids, own, col, blocks, rows, groups):
     count, n, _ = blocks.shape
     own, col, blocks = (pltpu.with_memory_space_constraint(x, pltpu.HBM) for x in (own, col, blocks))
     return pl.pallas_call(
-        functools.partial(prep_kernel, rows),
+        functools.partial(prep_kernel, rows, groups),
         in_specs=[IN_SMEM] * 3 + [pl.BlockSpec(memory_space=pl.ANY)],
         out_specs=[IN_VMEM, IN_VMEM, IN_SMEM],
         out_shape=[pltpu.VMEM((count, n, 2 * n), BF16),
@@ -399,7 +403,7 @@
 
     halves = call(split_kernel, "split", [(half, each, block)] * 4, ids, start, scalars=1)
     before = [tuple(halves[:2]), tuple(halves[2:])]
-    w, inv, table = prep(ids, owner_row, block_col, blocks, slots)
+    w, inv, table = prep(ids, owner_row, block_col, blocks, slots, lax.axis_size("node"))
     meta = (table, w, inv)
 
     def advance(now, before=((), ()), parts=False):
@@ -417,6 +421,7 @@
     before, now = now, after
     image = swapped(parts)
     got, hops = None, hops_of("col", "node")
+    hops = hops[:1] + hops[2:4] + hops[1:2] + hops[4:]
     gram = gram_first
     for step in range(DEGREE - 1):
         after = []
@@ -424,6 +429,11 @@
             old, gram, got = lax.optimization_barrier((before[i], gram, got))
             if (step, i) == (1, 1):
                 old, image = lax.optimization_barrier((old, image))
+                (image_first,) = call(
+                    cross_kernel, "cross", [square], ids, panel, gram_first, *image, scalars=1, scratch=[held]
+                )
+            if (step, i) == (2, 1):
+                old, image_first = lax.optimization_barrier((old, image_first))
             if got is not None:
                 gram = gram + got
             got = swap(gram, *hops.pop(0)) if hops else None
@@ -440,26 +450,26 @@
     halos = [exchange(panels) for panels in now]
     halos[0], gram = lax.optimization_barrier((halos[0], gram))
     inverse_first = inverse_factor(gram, nodes)
-    (image_first,) = call(
-        cross_kernel, "cross", [square], ids, panel, gram_first, *image, scalars=1, scratch=[held]
-    )
     turned, gram_last = call(
         turn_kernel, "turn", [held_shape, square], ids, inverse_first, *swapped(parts), scalars=1, scratch=[held]
     )
     first, _ = apply(meta, now[0], halos[0])
     gram = gram_last
     hops = hops_of("col", "node")
+    first_hops = hops_of("node")
     for i, hop in enumerate(hops):
         got = swap(gram, *hop)
         if i == 1:
-            got, halos[1] = lax.optimization_barrier((got, halos[1]))
+            got, halos[1], first = lax.optimization_barrier((got, halos[1], first))
             _, parts = apply(meta, now[1], halos[1], (), first, count)
             (image_last,) = call(
                 turn_cross_kernel, "turn_cross", [square], ids, inverse_first, turned, gram_last,
                 *swapped(parts), scalars=1, scratch=[held],
             )
-        if i == len(hops) - 2:
-            got, image_first = lax.optimization_barrier((got, image_first))
+        if i >= len(hops) - 2:
+            got_first = swap(image_first, *first_hops.pop(0))
+            got, got_first = lax.optimization_barrier((got, got_first))
+            image_first = image_first + got_first
         if i == len(hops) - 1:
             got, image_last = lax.optimization_barrier((got, image_last))
         gram = gram + got
@@ -471,22 +481,24 @@
     for i, each_round in enumerate(rounds_of("node")):
         if i == 1:
             parts, image_last = lax.optimization_barrier((parts, image_last))
-        got_first = round_swaps(image_first, *each_round)
         got = round_swaps(image_last, *each_round)
         if i == 0:
+            got_first = swap(image_first, *first_hops.pop(0))
             got, got_first, image_last, _ = lax.optimization_barrier((got, got_first, image_last, inverse_last))
-        image_first = round_sum(image_first, got_first)
+            image_first = image_first + got_first
         image_last = round_sum(image_last, got)
+    for hop in first_hops:
+        image_first = image_first + swap(image_first, *hop)
     arrived = swapped(parts)
     parts = call(
         functools.partial(proj_kernel, nodes), "proj", [(2, cols_here, vecs)] * count, ids,
         inverse_first, image_first, inverse_last, image_last, scalars=1, scratch=[pltpu.VMEM(square, F32)],
     )
-    received, arrived = lax.optimization_barrier((swapped(parts), arrived))
-    projected = sum(received)
     (basis,) = call(
         functools.partial(join_kernel, half), "join", [(cols_here, width)], ids, *arrived, scalars=1
     )
+    received, basis = lax.optimization_barrier((swapped(parts), basis))
+    projected = sum(received)
     return basis, projected[0], projected[1]
 
 

time: 238 us -> 239 us (level)
    ppermute x18, starting transfers between devices: 55.1 us -> 59.9 us  [exchange(): lax.ppermute(pair[1], 'node', odd)]
    ppermute x18, waiting for transfers between devices: 2.41 us -> 6.56 us  [exchange(): lax.ppermute(pair[0], 'node', even)]
    ppermute x36 -> x35, waiting for transfers between devices: 25.1 us -> 21.3 us  [swap(): lax.ppermute(value, axis, [(i, i ^ hop) for i in range(lax.axis_size(axis...]
    ppermute x18, starting transfers between devices: 15 us -> 12.4 us  [exchange(): lax.ppermute(pair[0], 'node', even)]
    ppermute x36 -> x35, starting transfers between devices: 29 us -> 28.8 us  [swap(): lax.ppermute(value, axis, [(i, i ^ hop) for i in range(lax.axis_size(axis...]
  transfers between devices with their start and end apart: 72 -> 71, of which waited for: 13 -> 14; matrix products, arithmetic and copies ran while one was open for 0% -> 0% of each run, Pallas kernels for 44% -> 44%
where the time goes in v10:
time: 239 us
  Pallas kernels  107 us (45%)
  starting transfers between devices  101 us (42%)
  waiting for transfers between devices  28 us (12%)
    pallas_call x18, Pallas kernels, apply(): pl.pallas_call(functools.partial(apply_kernel, bool(old), bool(mate)), in...  78.3 us
    ppermute x18, starting transfers between devices, exchange(): lax.ppermute(pair[1], 'node', odd)  59.9 us
    ppermute x35, starting transfers between devices, swap(): lax.ppermute(value, axis, [(i, i ^ hop) for i in range(lax.axis_size(axis...  28.8 us
    ppermute x35, waiting for transfers between devices, swap(): lax.ppermute(value, axis, [(i, i ^ hop) for i in range(lax.axis_size(axis...  21.3 us
    pallas_call x10, Pallas kernels, call(): pl.pallas_call(kernel, in_specs=[IN_SMEM] * scalars + [IN_VMEM] * (len(ar...  20.1 us
    ppermute x18, starting transfers between devices, exchange(): lax.ppermute(pair[0], 'node', even)  12.4 us
    pallas_call x1, Pallas kernels, prep(): pl.pallas_call(functools.partial(prep_kernel, rows, groups), in_specs=[IN...  8.32 us
    ppermute x18, waiting for transfers between devices, exchange(): lax.ppermute(pair[0], 'node', even)  6.56 us
  transfers between devices with their start and end apart: 71, of which 14 were waited for; matrix products, arithmetic and copies ran while one was open for 0% of the time, Pallas kernels for 44%

profile of v10, /device:TPU:0, one launch (start us, length us, event | category | flops | bytes accessed | tf_op | source)
XLA Modules:
  0.0 238.9 jit_solution(12465884594218273519)
XLA Ops:
  2.5 3.0 %collective-permute-start = (f32[24,16,128]{2,1,0:T(8,128)S(1)}, f32[24,16,128]{2,1,0:T(8,128)S(1)}, u32[]{:S(2)}, u32[]{:S(2)}) collective-permute-start(f32[24,16,128]{2,1,0:T(8,128)S(1)} %get-tuple-element.146.refs_3_.refs_7_), channel_id=1, source_target_pairs={{0,4},{4,0},{8,12},{12,8},{16,20},{20,16},{24,28},{28,24},{1,5},{5... | collective-permute-start | bytes 589832 | tf_op jit(solution)/shard_map/ppermute | solution.py:353
  5.5 3.5 %collective-permute-start.1 = (f32[24,16,128]{2,1,0:T(8,128)S(1)}, f32[24,16,128]{2,1,0:T(8,128)S(1)}, u32[]{:S(2)}, u32[]{:S(2)}) collective-permute-start(f32[24,16,128]{2,1,0:T(8,128)S(1)} %get-tuple-element.147.refs_4_.refs_8_), channel_id=1, source_target_pairs={{0,28},{4,8},{8,4},{12,16},{16,12},{20,24},{24,20},{28,0},{1,29},{... | collective-permute-start | bytes 589832 | tf_op jit(solution)/shard_map/ppermute | solution.py:353
  9.1 1.9 collective-permute-start.13
  11.0 8.3 %prep.1 = (bf16[288,128,256]{2,1,0:T(8,128)(2,1)S(1)}, f32[48,1,128]{2,1,0:T(1,128)S(1)}, s32[578]{0:T(1024)S(1)}) custom-call(s32[2]{0:T(128)S(1)} %pad_add_fusion.ids_ref, s32[1,288]{1,0:T(1,128)} %own_ref.1, s32[1,288]{1,0:T(1,128)} %col_ref.1, f32[288,128,128]{2,1,0:T(8,128)} %blk_ref.1), custom_call_target="tpu_custom_call" | custom-call | flops 1207959552 | bytes 18874368 | tf_op jit(solution)/shard_map/prep/pallas_call | solution.py:120
  19.3 4.2 %apply.4 = (f32[24,16,128]{2,1,0:T(8,128)S(1)}, f32[24,16,128]{2,1,0:T(8,128)S(1)}) custom-call(s32[578]{0:T(1024)S(1)} %get-tuple-element.143.refs_0_, bf16[288,128,256]{2,1,0:T(8,128)(2,1)S(1)} %get-tuple-element.144.refs_1_, f32[48,1,128]{2,1,0:T(1,128)S(1)} %get-tuple-element.145.refs_2_, f32[24,16,128]{2,1,0:T(8,128)S(1)} %get-tuple-element.146.refs_3_.refs_7_, ...), custom_call_target="tpu_custom_call" | custom-call | bytes 4194304 | tf_op jit(solution)/shard_map/apply/pallas_call | solution.py:199
  23.6 2.5 %collective-permute-start.2 = (f32[24,16,128]{2,1,0:T(8,128)S(1)}, f32[24,16,128]{2,1,0:T(8,128)S(1)}, u32[]{:S(2)}, u32[]{:S(2)}) collective-permute-start(f32[24,16,128]{2,1,0:T(8,128)S(1)} %get-tuple-element.148.refs_3_.refs_7_), channel_id=1, source_target_pairs={{0,4},{4,0},{8,12},{12,8},{16,20},{20,16},{24,28},{28,24},{1,5},{5... | collective-permute-start | bytes 589832 | tf_op jit(solution)/shard_map/ppermute | solution.py:353
  26.0 3.6 %collective-permute-start.3 = (f32[24,16,128]{2,1,0:T(8,128)S(1)}, f32[24,16,128]{2,1,0:T(8,128)S(1)}, u32[]{:S(2)}, u32[]{:S(2)}) collective-permute-start(f32[24,16,128]{2,1,0:T(8,128)S(1)} %get-tuple-element.149.refs_4_.refs_8_), channel_id=1, source_target_pairs={{0,28},{4,8},{8,4},{12,16},{16,12},{20,24},{24,20},{28,0},{1,29},{... | collective-permute-start | bytes 589832 | tf_op jit(solution)/shard_map/ppermute | solution.py:353
  29.6 4.2 %apply.6 = (f32[24,16,128]{2,1,0:T(8,128)S(1)}, f32[24,16,128]{2,1,0:T(8,128)S(1)}) custom-call(s32[578]{0:T(1024)S(1)} %get-tuple-element.143.refs_0_, bf16[288,128,256]{2,1,0:T(8,128)(2,1)S(1)} %get-tuple-element.144.refs_1_, f32[48,1,128]{2,1,0:T(1,128)S(1)} %get-tuple-element.145.refs_2_, f32[24,16,128]{2,1,0:T(8,128)S(1)} %get-tuple-element.158.refs_3_.refs_7_, ...), custom_call_target="tpu_custom_call" | custom-call | bytes 4194304 | tf_op jit(solution)/shard_map/apply/pallas_call | solution.py:199
  33.9 1.9 collective-permute-start.15
  35.9 4.3 %apply_recur.10 = (f32[24,16,128]{2,1,0:T(8,128)S(1)}, f32[24,16,128]{2,1,0:T(8,128)S(1)}) custom-call(s32[578]{0:T(1024)S(1)} %get-tuple-element.143.refs_0_, bf16[288,128,256]{2,1,0:T(8,128)(2,1)S(1)} %get-tuple-element.144.refs_1_, f32[48,1,128]{2,1,0:T(1,128)S(1)} %get-tuple-element.145.refs_2_, f32[24,16,128]{2,1,0:T(8,128)S(1)} %get-tuple-element.148.refs_3_.refs_7_, ...), custom_call_target="tpu_custom_call" | custom-call | bytes 4194304 | tf_op jit(solution)/shard_map/apply_recur/pallas_call | solution.py:199
  40.8 8.2 %collective-permute-start.5 = (f32[24,16,128]{2,1,0:T(8,128)S(1)}, f32[24,16,128]{2,1,0:T(8,128)S(1)}, u32[]{:S(2)}, u32[]{:S(2)}) collective-permute-start(f32[24,16,128]{2,1,0:T(8,128)S(1)} %get-tuple-element.151.refs_4_.refs_8_), channel_id=1, source_target_pairs={{0,28},{4,8},{8,4},{12,16},{16,12},{20,24},{24,20},{28,0},{1,29},{... | collective-permute-start | bytes 589832 | tf_op jit(solution)/shard_map/ppermute | solution.py:353
  49.0 4.3 %apply_recur.13 = (f32[24,16,128]{2,1,0:T(8,128)S(1)}, f32[24,16,128]{2,1,0:T(8,128)S(1)}) custom-call(s32[578]{0:T(1024)S(1)} %get-tuple-element.143.refs_0_, bf16[288,128,256]{2,1,0:T(8,128)(2,1)S(1)} %get-tuple-element.144.refs_1_, f32[48,1,128]{2,1,0:T(1,128)S(1)} %get-tuple-element.145.refs_2_, f32[24,16,128]{2,1,0:T(8,128)S(1)} %get-tuple-element.160.refs_3_.refs_7_, ...), custom_call_target="tpu_custom_call" | custom-call | bytes 4194304 | tf_op jit(solution)/shard_map/apply_recur/pallas_call | solution.py:199
  53.4 2.0 collective-permute-start.17
  55.3 4.2 %apply_recur.11 = (f32[24,16,128]{2,1,0:T(8,128)S(1)}, f32[24,16,128]{2,1,0:T(8,128)S(1)}) custom-call(s32[578]{0:T(1024)S(1)} %get-tuple-element.143.refs_0_, bf16[288,128,256]{2,1,0:T(8,128)(2,1)S(1)} %get-tuple-element.144.refs_1_, f32[48,1,128]{2,1,0:T(1,128)S(1)} %get-tuple-element.145.refs_2_, f32[24,16,128]{2,1,0:T(8,128)S(1)} %get-tuple-element.150.refs_3_.refs_7_, ...), custom_call_target="tpu_custom_call" | custom-call | bytes 4194304 | tf_op jit(solution)/shard_map/apply_recur/pallas_call | solution.py:199
  59.7 2.9 %collective-permute-start.7 = (f32[24,16,128]{2,1,0:T(8,128)S(1)}, f32[24,16,128]{2,1,0:T(8,128)S(1)}, u32[]{:S(2)}, u32[]{:S(2)}) collective-permute-start(f32[24,16,128]{2,1,0:T(8,128)S(1)} %get-tuple-element.153.refs_4_), channel_id=1, source_target_pairs={{0,28},{4,8},{8,4},{12,16},{16,12},{20,24},{24,20},{28,0},{1,29},{... | collective-permute-start | bytes 589832 | tf_op jit(solution)/shard_map/ppermute | solution.py:353
  62.6 4.3 %apply_recur.14 = (f32[24,16,128]{2,1,0:T(8,128)S(1)}, f32[24,16,128]{2,1,0:T(8,128)S(1)}) custom-call(s32[578]{0:T(1024)S(1)} %get-tuple-element.143.refs_0_, bf16[288,128,256]{2,1,0:T(8,128)(2,1)S(1)} %get-tuple-element.144.refs_1_, f32[48,1,128]{2,1,0:T(1,128)S(1)} %get-tuple-element.145.refs_2_, f32[24,16,128]{2,1,0:T(8,128)S(1)} %get-tuple-element.162.refs_3_.refs_7_, ...), custom_call_target="tpu_custom_call" | custom-call | bytes 4194304 | tf_op jit(solution)/shard_map/apply_recur/pallas_call | solution.py:199
  68.0 4.9 %collective-permute-start.19 = (f32[24,16,128]{2,1,0:T(8,128)S(1)}, f32[24,16,128]{2,1,0:T(8,128)S(1)}, u32[]{:S(2)}, u32[]{:S(2)}) collective-permute-start(f32[24,16,128]{2,1,0:T(8,128)S(1)} %get-tuple-element.165.refs_4_), channel_id=1, source_target_pairs={{0,28},{4,8},{8,4},{12,16},{16,12},{20,24},{24,20},{28,0},{1,29},{... | collective-permute-start | bytes 589832 | tf_op jit(solution)/shard_map/ppermute | solution.py:353
  72.9 4.3 %apply_recur.12 = (f32[24,16,128]{2,1,0:T(8,128)S(1)}, f32[24,16,128]{2,1,0:T(8,128)S(1)}) custom-call(s32[578]{0:T(1024)S(1)} %get-tuple-element.143.refs_0_, bf16[288,128,256]{2,1,0:T(8,128)(2,1)S(1)} %get-tuple-element.144.refs_1_, f32[48,1,128]{2,1,0:T(1,128)S(1)} %get-tuple-element.145.refs_2_, f32[24,16,128]{2,1,0:T(8,128)S(1)} %get-tuple-element.152.refs_3_, ...), custom_call_target="tpu_custom_call" | custom-call | bytes 4194304 | tf_op jit(solution)/shard_map/apply_recur/pallas_call | solution.py:199
  77.3 1.9 collective-permute-start.9
  79.2 4.4 %apply_recur_parts.2 = (f32[24,16,128]{2,1,0:T(8,128)S(1)}, f32[24,16,128]{2,1,0:T(8,128)S(1)}, f32[12,32,128]{2,1,0:T(8,128)S(1)}, f32[12,32,128]{2,1,0:T(8,128...) custom-call(s32[578]{0:T(1024)S(1)} %get-tuple-element.143.refs_0_, ...), custom_call_target="tpu_custom_call" | custom-call | bytes 4194304 | tf_op jit(solution)/shard_map/apply_recur_parts/pallas_call | solution.py:199
  84.5 8.7 %collective-permute-start.28 = (f32[24,16,128]{2,1,0:T(8,128)S(1)}, f32[24,16,128]{2,1,0:T(8,128)S(1)}, u32[]{:S(2)}, u32[]{:S(2)}) collective-permute-start(f32[24,16,128]{2,1,0:T(8,128)S(1)} %get-tuple-element.185.refs_4_.refs_8_), channel_id=1, source_target_pairs={{0,28},{4,8},{8,4},{12,16},{16,12},{20,24},{24,20},{28,0},{1,29},{... | collective-permute-start | bytes 589832 | tf_op jit(solution)/shard_map/ppermute | solution.py:353
  95.1 4.2 %apply.5 = (f32[24,16,128]{2,1,0:T(8,128)S(1)}, f32[24,16,128]{2,1,0:T(8,128)S(1)}) custom-call(s32[578]{0:T(1024)S(1)} %get-tuple-element.143.refs_0_, bf16[288,128,256]{2,1,0:T(8,128)(2,1)S(1)} %get-tuple-element.144.refs_1_, f32[48,1,128]{2,1,0:T(1,128)S(1)} %get-tuple-element.145.refs_2_, f32[24,16,128]{2,1,0:T(8,128)S(1)} %get-tuple-element.171.refs_3_.refs_9_.refs_7_, ...), custom_call_target="tpu_custom_call" | custom-call | bytes 4194304 | tf_op jit(solution)/shard_map/apply/pallas_call | solution.py:199
  99.5 2.1 collective-permute-start.11
  101.6 4.5 %apply_parts.2 = (f32[24,16,128]{2,1,0:T(8,128)S(1)}, f32[24,16,128]{2,1,0:T(8,128)S(1)}, f32[12,32,128]{2,1,0:T(8,128)S(1)}, f32[12,32,128]{2,1,0:T(8,128)S(1)}...) custom-call(s32[578]{0:T(1024)S(1)} %get-tuple-element.143.refs_0_, ...), custom_call_target="tpu_custom_call" | custom-call | bytes 4194304 | tf_op jit(solution)/shard_map/apply_parts/pallas_call | solution.py:199
  106.2 2.7 %collective-permute-start.30 = (f32[24,16,128]{2,1,0:T(8,128)S(1)}, f32[24,16,128]{2,1,0:T(8,128)S(1)}, u32[]{:S(2)}, u32[]{:S(2)}) collective-permute-start(f32[24,16,128]{2,1,0:T(8,128)S(1)} %get-tuple-element.207.refs_4_.refs_8_), channel_id=1, source_target_pairs={{0,28},{4,8},{8,4},{12,16},{16,12},{20,24},{24,20},{28,0},{1,29},{... | collective-permute-start | bytes 589832 | tf_op jit(solution)/shard_map/ppermute | solution.py:353
  110.3 5.2 %collective-permute-done.10.refs_5_ = f32[24,16,128]{2,1,0:T(8,128)S(1)} collective-permute-done((f32[24,16,128]{2,1,0:T(8,128)S(1)}, f32[24,16,128]{2,1,0:T(8,128)S(1)}, u32[]{:S(2)}, u32[]{:S(2)}) %collective-permute-start.10) | collective-permute-done | bytes 196640 | tf_op jit(solution)/shard_map/ppermute | solution.py:353
  115.6 4.3 %apply_recur.15 = (f32[24,16,128]{2,1,0:T(8,128)S(1)}, f32[24,16,128]{2,1,0:T(8,128)S(1)}) custom-call(s32[578]{0:T(1024)S(1)} %get-tuple-element.143.refs_0_, bf16[288,128,256]{2,1,0:T(8,128)(2,1)S(1)} %get-tuple-element.144.refs_1_, f32[48,1,128]{2,1,0:T(1,128)S(1)} %get-tuple-element.145.refs_2_, f32[24,16,128]{2,1,0:T(8,128)S(1)} %get-tuple-element.190.refs_3_.refs_7_, ...), custom_call_target="tpu_custom_call" | custom-call | bytes 4194304 | tf_op jit(solution)/shard_map/apply_recur/pallas_call | solution.py:199
  121.3 2.0 collective-permute-start.26
  124.8 4.2 %apply_recur.16 = (f32[24,16,128]{2,1,0:T(8,128)S(1)}, f32[24,16,128]{2,1,0:T(8,128)S(1)}) custom-call(s32[578]{0:T(1024)S(1)} %get-tuple-element.143.refs_0_, bf16[288,128,256]{2,1,0:T(8,128)(2,1)S(1)} %get-tuple-element.144.refs_1_, f32[48,1,128]{2,1,0:T(1,128)S(1)} %get-tuple-element.145.refs_2_, f32[24,16,128]{2,1,0:T(8,128)S(1)} %get-tuple-element.206.refs_3_.refs_7_, ...), custom_call_target="tpu_custom_call" | custom-call | bytes 4194304 | tf_op jit(solution)/shard_map/apply_recur/pallas_call | solution.py:199
  129.0 2.2 collective-permute-done.26
  131.8 2.2 collective-permute-start.36
  134.8 4.3 %apply_recur.17 = (f32[24,16,128]{2,1,0:T(8,128)S(1)}, f32[24,16,128]{2,1,0:T(8,128)S(1)}) custom-call(s32[578]{0:T(1024)S(1)} %get-tuple-element.143.refs_0_, bf16[288,128,256]{2,1,0:T(8,128)(2,1)S(1)} %get-tuple-element.144.refs_1_, f32[48,1,128]{2,1,0:T(1,128)S(1)} %get-tuple-element.145.refs_2_, f32[24,16,128]{2,1,0:T(8,128)S(1)} %get-tuple-element.212.refs_3_.refs_7_, ...), custom_call_target="tpu_custom_call" | custom-call | bytes 4194304 | tf_op jit(solution)/shard_map/apply_recur/pallas_call | solution.py:199
  140.0 2.3 collective-permute-start.32
  142.4 4.3 %apply_recur.18 = (f32[24,16,128]{2,1,0:T(8,128)S(1)}, f32[24,16,128]{2,1,0:T(8,128)S(1)}) custom-call(s32[578]{0:T(1024)S(1)} %get-tuple-element.143.refs_0_, bf16[288,128,256]{2,1,0:T(8,128)(2,1)S(1)} %get-tuple-element.144.refs_1_, f32[48,1,128]{2,1,0:T(1,128)S(1)} %get-tuple-element.145.refs_2_, f32[24,16,128]{2,1,0:T(8,128)S(1)} %get-tuple-element.231.refs_3_.refs_7_, ...), custom_call_target="tpu_custom_call" | custom-call | bytes 4194304 | tf_op jit(solution)/shard_map/apply_recur/pallas_call | solution.py:199
  148.3 6.1 %collective-permute-start.44 = (f32[24,16,128]{2,1,0:T(8,128)S(1)}, f32[24,16,128]{2,1,0:T(8,128)S(1)}, u32[]{:S(2)}, u32[]{:S(2)}) collective-permute-start(f32[24,16,128]{2,1,0:T(8,128)S(1)} %get-tuple-element.209.refs_4_), channel_id=1, source_target_pairs={{0,28},{4,8},{8,4},{12,16},{16,12},{20,24},{24,20},{28,0},{1,29},{... | collective-permute-start | bytes 589832 | tf_op jit(solution)/shard_map/ppermute | solution.py:353
  154.6 4.3 %collective-permute-done.34 = f32[128,128]{1,0:T(8,128)S(1)} collective-permute-done((f32[128,128]{1,0:T(8,128)S(1)}, f32[128,128]{1,0:T(8,128)S(1)}, u32[]{:S(2)}, u32[]{:S(2)}) %collective-permute-start.34) | collective-permute-done | bytes 65568 | tf_op jit(solution)/shard_map/ppermute | solution.py:357
  158.9 4.2 %apply_recur.19 = (f32[24,16,128]{2,1,0:T(8,128)S(1)}, f32[24,16,128]{2,1,0:T(8,128)S(1)}) custom-call(s32[578]{0:T(1024)S(1)} %get-tuple-element.143.refs_0_, bf16[288,128,256]{2,1,0:T(8,128)(2,1)S(1)} %get-tuple-element.144.refs_1_, f32[48,1,128]{2,1,0:T(1,128)S(1)} %get-tuple-element.145.refs_2_, f32[24,16,128]{2,1,0:T(8,128)S(1)} %get-tuple-element.192.refs_3_, ...), custom_call_target="tpu_custom_call" | custom-call | bytes 4194304 | tf_op jit(solution)/shard_map/apply_recur/pallas_call | solution.py:199
  165.3 4.6 %apply_recur_parts.3 = (f32[24,16,128]{2,1,0:T(8,128)S(1)}, f32[24,16,128]{2,1,0:T(8,128)S(1)}, f32[12,32,128]{2,1,0:T(8,128)S(1)}, f32[12,32,128]{2,1,0:T(8,128...) custom-call(s32[578]{0:T(1024)S(1)} %get-tuple-element.143.refs_0_, ...), custom_call_target="tpu_custom_call" | custom-call | bytes 4194304 | tf_op jit(solution)/shard_map/apply_recur_parts/pallas_call | solution.py:199
  173.8 4.7 %collective-permute-start.51 = (f32[24,16,128]{2,1,0:T(8,128)S(1)}, f32[24,16,128]{2,1,0:T(8,128)S(1)}, u32[]{:S(2)}, u32[]{:S(2)}) collective-permute-start(f32[24,16,128]{2,1,0:T(8,128)S(1)} %get-tuple-element.239.refs_4_), channel_id=1, source_target_pairs={{0,28},{4,8},{8,4},{12,16},{16,12},{20,24},{24,20},{28,0},{1,29},{... | collective-permute-start | bytes 589832 | tf_op jit(solution)/shard_map/ppermute | solution.py:353
  178.5 4.1 %factor.2.inv_ref.refs_0_ = f32[128,128]{1,0:T(8,128)S(1)} custom-call(f32[128,128]{1,0:T(8,128)S(1)} %add.64.g_ref), custom_call_target="tpu_custom_call" | custom-call | tf_op jit(solution)/shard_map/factor/pallas_call | solution.py:42
  182.7 2.5 %turn.1 = (f32[12,128,128]{2,1,0:T(8,128)S(1)}, f32[128,128]{1,0:T(8,128)S(1)}) custom-call(s32[2]{0:T(128)S(1)} %pad_add_fusion.ids_ref, f32[128,128]{1,0:T(8,128)S(1)} %factor.2.inv_ref.refs_0_, f32[12,32,128]{2,1,0:T(8,128)S(1)} %get-tuple-element.233.refs_0_, f32[12,32,128]{2,1,0:T(8,128)S(1)} %collective-permute-done.45.refs_1_, ...), custom_call_target="tpu_custom_call" | custom-call | tf_op jit(solution)/shard_map/turn/pallas_call | solution.py:42
  186.9 4.2 %apply.7 = (f32[24,16,128]{2,1,0:T(8,128)S(1)}, f32[24,16,128]{2,1,0:T(8,128)S(1)}) custom-call(s32[578]{0:T(1024)S(1)} %get-tuple-element.143.refs_0_, bf16[288,128,256]{2,1,0:T(8,128)(2,1)S(1)} %get-tuple-element.144.refs_1_, f32[48,1,128]{2,1,0:T(1,128)S(1)} %get-tuple-element.145.refs_2_, f32[24,16,128]{2,1,0:T(8,128)S(1)} %get-tuple-element.214.refs_9_.refs_3_, ...), custom_call_target="tpu_custom_call" | custom-call | bytes 4194304 | tf_op jit(solution)/shard_map/apply/pallas_call | solution.py:199
  192.1 5.3 %apply_parts.3 = (f32[24,16,128]{2,1,0:T(8,128)}, f32[24,16,128]{2,1,0:T(8,128)}, f32[12,32,128]{2,1,0:T(8,128)S(1)}, f32[12,32,128]{2,1,0:T(8,128)S(1)}, f32[12...) custom-call(s32[578]{0:T(1024)S(1)} %get-tuple-element.143.refs_0_, ...), custom_call_target="tpu_custom_call" | custom-call | bytes 4194304 | tf_op jit(solution)/shard_map/apply_parts/pallas_call | solution.py:199
  204.8 2.5 %collective-permute-start.55 = (f32[128,128]{1,0:T(8,128)S(1)}, f32[128,128]{1,0:T(8,128)S(1)}, u32[]{:S(2)}, u32[]{:S(2)}) collective-permute-start(f32[128,128]{1,0:T(8,128)S(1)} %add.69), channel_id=1, source_target_pairs={{0,16},{4,20},{8,24},{12,28},{16,0},{20,4},{24,8},{28,12},{1,17},{... | collective-permute-start | bytes 196616 | tf_op jit(solution)/shard_map/ppermute | solution.py:357
  207.3 2.1 collective-permute-start.56
  213.5 2.1 collective-permute-start.60
  218.7 4.1 %factor.3.inv_ref.refs_2_ = f32[128,128]{1,0:T(8,128)S(1)} custom-call(f32[128,128]{1,0:T(8,128)S(1)} %add.71.g_ref), custom_call_target="tpu_custom_call" | custom-call | tf_op jit(solution)/shard_map/factor/pallas_call | solution.py:42
  228.1 3.6 %collective-permute-done.64 = f32[128,128]{1,0:T(8,128)S(1)} collective-permute-done((f32[128,128]{1,0:T(8,128)S(1)}, f32[128,128]{1,0:T(8,128)S(1)}, u32[]{:S(2)}, u32[]{:S(2)}) %collective-permute-start.64) | collective-permute-done | bytes 65568 | tf_op jit(solution)/shard_map/ppermute | solution.py:357
  (143 shorter events, 51.2 us)
Async XLA Ops:
  2.5 16.8 %collective-permute-start = (f32[24,16,128]{2,1,0:T(8,128)S(1)}, f32[24,16,128]{2,1,0:T(8,128)S(1)}, u32[]{:S(2)}, u32[]{:S(2)}) collective-permute-start(f32[24,16,128]{2,1,0:T(8,128)S(1)} %get-tuple-element.146.refs_3_.refs_7_), channel_id=1, source_target_pairs={{0,4},{4,0},{8,12},{12,8},{16,20},{20,16},{24,28},{28,24},{1,5},{5... | collective-permute-start | bytes 589832 | tf_op jit(solution)/shard_map/ppermute | solution.py:353
  5.5 13.8 %collective-permute-start.1 = (f32[24,16,128]{2,1,0:T(8,128)S(1)}, f32[24,16,128]{2,1,0:T(8,128)S(1)}, u32[]{:S(2)}, u32[]{:S(2)}) collective-permute-start(f32[24,16,128]{2,1,0:T(8,128)S(1)} %get-tuple-element.147.refs_4_.refs_8_), channel_id=1, source_target_pairs={{0,28},{4,8},{8,4},{12,16},{16,12},{20,24},{24,20},{28,0},{1,29},{... | collective-permute-start | bytes 589832 | tf_op jit(solution)/shard_map/ppermute | solution.py:353
  9.1 20.5 %collective-permute-start.12 = (f32[24,16,128]{2,1,0:T(8,128)S(1)}, f32[24,16,128]{2,1,0:T(8,128)S(1)}, u32[]{:S(2)}, u32[]{:S(2)}) collective-permute-start(f32[24,16,128]{2,1,0:T(8,128)S(1)} %get-tuple-element.158.refs_3_.refs_7_), channel_id=1, source_target_pairs={{0,4},{4,0},{8,12},{12,8},{16,20},{20,16},{24,28},{28,24},{1,5},{5... | collective-permute-start | bytes 589832 | tf_op jit(solution)/shard_map/ppermute | solution.py:353
  9.1 20.5 %collective-permute-start.13 = (f32[24,16,128]{2,1,0:T(8,128)S(1)}, f32[24,16,128]{2,1,0:T(8,128)S(1)}, u32[]{:S(2)}, u32[]{:S(2)}) collective-permute-start(f32[24,16,128]{2,1,0:T(8,128)S(1)} %get-tuple-element.159.refs_4_.refs_8_), channel_id=1, source_target_pairs={{0,28},{4,8},{8,4},{12,16},{16,12},{20,24},{24,20},{28,0},{1,29},{... | collective-permute-start | bytes 589832 | tf_op jit(solution)/shard_map/ppermute | solution.py:353
  23.6 12.3 %collective-permute-start.2 = (f32[24,16,128]{2,1,0:T(8,128)S(1)}, f32[24,16,128]{2,1,0:T(8,128)S(1)}, u32[]{:S(2)}, u32[]{:S(2)}) collective-permute-start(f32[24,16,128]{2,1,0:T(8,128)S(1)} %get-tuple-element.148.refs_3_.refs_7_), channel_id=1, source_target_pairs={{0,4},{4,0},{8,12},{12,8},{16,20},{20,16},{24,28},{28,24},{1,5},{5... | collective-permute-start | bytes 589832 | tf_op jit(solution)/shard_map/ppermute | solution.py:353
  26.0 9.8 %collective-permute-start.3 = (f32[24,16,128]{2,1,0:T(8,128)S(1)}, f32[24,16,128]{2,1,0:T(8,128)S(1)}, u32[]{:S(2)}, u32[]{:S(2)}) collective-permute-start(f32[24,16,128]{2,1,0:T(8,128)S(1)} %get-tuple-element.149.refs_4_.refs_8_), channel_id=1, source_target_pairs={{0,28},{4,8},{8,4},{12,16},{16,12},{20,24},{24,20},{28,0},{1,29},{... | collective-permute-start | bytes 589832 | tf_op jit(solution)/shard_map/ppermute | solution.py:353
  33.9 15.2 %collective-permute-start.14 = (f32[24,16,128]{2,1,0:T(8,128)S(1)}, f32[24,16,128]{2,1,0:T(8,128)S(1)}, u32[]{:S(2)}, u32[]{:S(2)}) collective-permute-start(f32[24,16,128]{2,1,0:T(8,128)S(1)} %get-tuple-element.160.refs_3_.refs_7_), channel_id=1, source_target_pairs={{0,4},{4,0},{8,12},{12,8},{16,20},{20,16},{24,28},{28,24},{1,5},{5... | collective-permute-start | bytes 589832 | tf_op jit(solution)/shard_map/ppermute | solution.py:353
  33.9 15.1 %collective-permute-start.15 = (f32[24,16,128]{2,1,0:T(8,128)S(1)}, f32[24,16,128]{2,1,0:T(8,128)S(1)}, u32[]{:S(2)}, u32[]{:S(2)}) collective-permute-start(f32[24,16,128]{2,1,0:T(8,128)S(1)} %get-tuple-element.161.refs_4_.refs_8_), channel_id=1, source_target_pairs={{0,28},{4,8},{8,4},{12,16},{16,12},{20,24},{24,20},{28,0},{1,29},{... | collective-permute-start | bytes 589832 | tf_op jit(solution)/shard_map/ppermute | solution.py:353
  40.1 15.2 %collective-permute-start.4 = (f32[24,16,128]{2,1,0:T(8,128)S(1)}, f32[24,16,128]{2,1,0:T(8,128)S(1)}, u32[]{:S(2)}, u32[]{:S(2)}) collective-permute-start(f32[24,16,128]{2,1,0:T(8,128)S(1)} %get-tuple-element.150.refs_3_.refs_7_), channel_id=1, source_target_pairs={{0,4},{4,0},{8,12},{12,8},{16,20},{20,16},{24,28},{28,24},{1,5},{5... | collective-permute-start | bytes 589832 | tf_op jit(solution)/shard_map/ppermute | solution.py:353
  40.8 14.5 %collective-permute-start.5 = (f32[24,16,128]{2,1,0:T(8,128)S(1)}, f32[24,16,128]{2,1,0:T(8,128)S(1)}, u32[]{:S(2)}, u32[]{:S(2)}) collective-permute-start(f32[24,16,128]{2,1,0:T(8,128)S(1)} %get-tuple-element.151.refs_4_.refs_8_), channel_id=1, source_target_pairs={{0,28},{4,8},{8,4},{12,16},{16,12},{20,24},{24,20},{28,0},{1,29},{... | collective-permute-start | bytes 589832 | tf_op jit(solution)/shard_map/ppermute | solution.py:353
  59.6 13.3 %collective-permute-start.6 = (f32[24,16,128]{2,1,0:T(8,128)S(1)}, f32[24,16,128]{2,1,0:T(8,128)S(1)}, u32[]{:S(2)}, u32[]{:S(2)}) collective-permute-start(f32[24,16,128]{2,1,0:T(8,128)S(1)} %get-tuple-element.152.refs_3_), channel_id=1, source_target_pairs={{0,4},{4,0},{8,12},{12,8},{16,20},{20,16},{24,28},{28,24},{1,5},{5... | collective-permute-start | bytes 589832 | tf_op jit(solution)/shard_map/ppermute | solution.py:353
  59.7 13.2 %collective-permute-start.7 = (f32[24,16,128]{2,1,0:T(8,128)S(1)}, f32[24,16,128]{2,1,0:T(8,128)S(1)}, u32[]{:S(2)}, u32[]{:S(2)}) collective-permute-start(f32[24,16,128]{2,1,0:T(8,128)S(1)} %get-tuple-element.153.refs_4_), channel_id=1, source_target_pairs={{0,28},{4,8},{8,4},{12,16},{16,12},{20,24},{24,20},{28,0},{1,29},{... | collective-permute-start | bytes 589832 | tf_op jit(solution)/shard_map/ppermute | solution.py:353
  66.9 12.3 %collective-permute-start.18 = (f32[24,16,128]{2,1,0:T(8,128)S(1)}, f32[24,16,128]{2,1,0:T(8,128)S(1)}, u32[]{:S(2)}, u32[]{:S(2)}) collective-permute-start(f32[24,16,128]{2,1,0:T(8,128)S(1)} %get-tuple-element.164.refs_3_), channel_id=1, source_target_pairs={{0,4},{4,0},{8,12},{12,8},{16,20},{20,16},{24,28},{28,24},{1,5},{5... | collective-permute-start | bytes 589832 | tf_op jit(solution)/shard_map/ppermute | solution.py:353
  68.0 11.2 %collective-permute-start.19 = (f32[24,16,128]{2,1,0:T(8,128)S(1)}, f32[24,16,128]{2,1,0:T(8,128)S(1)}, u32[]{:S(2)}, u32[]{:S(2)}) collective-permute-start(f32[24,16,128]{2,1,0:T(8,128)S(1)} %get-tuple-element.165.refs_4_), channel_id=1, source_target_pairs={{0,28},{4,8},{8,4},{12,16},{16,12},{20,24},{24,20},{28,0},{1,29},{... | collective-permute-start | bytes 589832 | tf_op jit(solution)/shard_map/ppermute | solution.py:353
  77.2 16.0 %collective-permute-start.8 = (f32[24,16,128]{2,1,0:T(8,128)S(1)}, f32[24,16,128]{2,1,0:T(8,128)S(1)}, u32[]{:S(2)}, u32[]{:S(2)}) collective-permute-start(f32[24,16,128]{2,1,0:T(8,128)S(1)} %get-tuple-element.171.refs_3_.refs_9_.refs_7_), channel_id=1, source_target_pairs={{0,4},{4,0},{8,12},{12,8},{16,20},{20,16},{24,28},{28,24},{1,5},{5... | collective-permute-start | bytes 589832 | tf_op jit(solution)/shard_map/ppermute | solution.py:353
  77.3 17.5 %collective-permute-start.9 = (f32[24,16,128]{2,1,0:T(8,128)S(1)}, f32[24,16,128]{2,1,0:T(8,128)S(1)}, u32[]{:S(2)}, u32[]{:S(2)}) collective-permute-start(f32[24,16,128]{2,1,0:T(8,128)S(1)} %get-tuple-element.172.refs_4_.refs_10_.refs_8_), channel_id=1, source_target_pairs={{0,28},{4,8},{8,4},{12,16},{16,12},{20,24},{24,20},{28,0},{1,29},{... | collective-permute-start | bytes 589832 | tf_op jit(solution)/shard_map/ppermute | solution.py:353
  83.6 15.8 %collective-permute-start.27 = (f32[24,16,128]{2,1,0:T(8,128)S(1)}, f32[24,16,128]{2,1,0:T(8,128)S(1)}, u32[]{:S(2)}, u32[]{:S(2)}) collective-permute-start(f32[24,16,128]{2,1,0:T(8,128)S(1)} %get-tuple-element.184.refs_3_.refs_7_), channel_id=1, source_target_pairs={{0,4},{4,0},{8,12},{12,8},{16,20},{20,16},{24,28},{28,24},{1,5},{5... | collective-permute-start | bytes 589832 | tf_op jit(solution)/shard_map/ppermute | solution.py:353
  84.5 14.9 %collective-permute-start.28 = (f32[24,16,128]{2,1,0:T(8,128)S(1)}, f32[24,16,128]{2,1,0:T(8,128)S(1)}, u32[]{:S(2)}, u32[]{:S(2)}) collective-permute-start(f32[24,16,128]{2,1,0:T(8,128)S(1)} %get-tuple-element.185.refs_4_.refs_8_), channel_id=1, source_target_pairs={{0,28},{4,8},{8,4},{12,16},{16,12},{20,24},{24,20},{28,0},{1,29},{... | collective-permute-start | bytes 589832 | tf_op jit(solution)/shard_map/ppermute | solution.py:353
  93.2 12.9 %collective-permute-start.20 = (f32[12,32,128]{2,1,0:T(8,128)S(1)}, f32[12,32,128]{2,1,0:T(8,128)S(1)}, u32[]{:S(2)}, u32[]{:S(2)}) collective-permute-start(f32[12,32,128]{2,1,0:T(8,128)S(1)} %get-tuple-element.167), channel_id=1, source_target_pairs={{0,1},{1,0},{2,3},{3,2},{4,5},{5,4},{6,7},{7,6},{8,9},{9,8},{10,11... | collective-permute-start | bytes 589832 | tf_op jit(solution)/shard_map/ppermute | solution.py:357
  93.2 13.0 %collective-permute-start.21 = (f32[12,32,128]{2,1,0:T(8,128)S(1)}, f32[12,32,128]{2,1,0:T(8,128)S(1)}, u32[]{:S(2)}, u32[]{:S(2)}) collective-permute-start(f32[12,32,128]{2,1,0:T(8,128)S(1)} %get-tuple-element.168), channel_id=1, source_target_pairs={{0,2},{1,3},{2,0},{3,1},{4,6},{5,7},{6,4},{7,5},{8,10},{9,11},{10,... | collective-permute-start | bytes 589832 | tf_op jit(solution)/shard_map/ppermute | solution.py:357
  94.7 14.2 %collective-permute-start.22 = (f32[12,32,128]{2,1,0:T(8,128)S(1)}, f32[12,32,128]{2,1,0:T(8,128)S(1)}, u32[]{:S(2)}, u32[]{:S(2)}) collective-permute-start(f32[12,32,128]{2,1,0:T(8,128)S(1)} %get-tuple-element.169), channel_id=1, source_target_pairs={{0,3},{1,2},{2,1},{3,0},{4,7},{5,6},{6,5},{7,4},{8,11},{9,10},{10,... | collective-permute-start | bytes 589832 | tf_op jit(solution)/shard_map/ppermute | solution.py:357
  99.4 16.2 %collective-permute-start.10 = (f32[24,16,128]{2,1,0:T(8,128)S(1)}, f32[24,16,128]{2,1,0:T(8,128)S(1)}, u32[]{:S(2)}, u32[]{:S(2)}) collective-permute-start(f32[24,16,128]{2,1,0:T(8,128)S(1)} %get-tuple-element.190.refs_3_.refs_7_), channel_id=1, source_target_pairs={{0,4},{4,0},{8,12},{12,8},{16,20},{20,16},{24,28},{28,24},{1,5},{5... | collective-permute-start | bytes 589832 | tf_op jit(solution)/shard_map/ppermute | solution.py:353
  99.5 16.1 %collective-permute-start.11 = (f32[24,16,128]{2,1,0:T(8,128)S(1)}, f32[24,16,128]{2,1,0:T(8,128)S(1)}, u32[]{:S(2)}, u32[]{:S(2)}) collective-permute-start(f32[24,16,128]{2,1,0:T(8,128)S(1)} %get-tuple-element.191.refs_4_.refs_8_), channel_id=1, source_target_pairs={{0,28},{4,8},{8,4},{12,16},{16,12},{20,24},{24,20},{28,0},{1,29},{... | collective-permute-start | bytes 589832 | tf_op jit(solution)/shard_map/ppermute | solution.py:353
  106.1 15.2 %collective-permute-start.29 = (f32[24,16,128]{2,1,0:T(8,128)S(1)}, f32[24,16,128]{2,1,0:T(8,128)S(1)}, u32[]{:S(2)}, u32[]{:S(2)}) collective-permute-start(f32[24,16,128]{2,1,0:T(8,128)S(1)} %get-tuple-element.206.refs_3_.refs_7_), channel_id=1, source_target_pairs={{0,4},{4,0},{8,12},{12,8},{16,20},{20,16},{24,28},{28,24},{1,5},{5... | collective-permute-start | bytes 589832 | tf_op jit(solution)/shard_map/ppermute | solution.py:353
  106.2 17.1 %collective-permute-start.30 = (f32[24,16,128]{2,1,0:T(8,128)S(1)}, f32[24,16,128]{2,1,0:T(8,128)S(1)}, u32[]{:S(2)}, u32[]{:S(2)}) collective-permute-start(f32[24,16,128]{2,1,0:T(8,128)S(1)} %get-tuple-element.207.refs_4_.refs_8_), channel_id=1, source_target_pairs={{0,28},{4,8},{8,4},{12,16},{16,12},{20,24},{24,20},{28,0},{1,29},{... | collective-permute-start | bytes 589832 | tf_op jit(solution)/shard_map/ppermute | solution.py:353
  108.9 15.9 %collective-permute-start.37 = (f32[12,32,128]{2,1,0:T(8,128)S(1)}, f32[12,32,128]{2,1,0:T(8,128)S(1)}, u32[]{:S(2)}, u32[]{:S(2)}) collective-permute-start(f32[12,32,128]{2,1,0:T(8,128)S(1)} %get-tuple-element.203), channel_id=1, source_target_pairs={{0,1},{1,0},{2,3},{3,2},{4,5},{5,4},{6,7},{7,6},{8,9},{9,8},{10,11... | collective-permute-start | bytes 589832 | tf_op jit(solution)/shard_map/ppermute | solution.py:357
  119.9 11.9 %collective-permute-start.23 = (f32[24,16,128]{2,1,0:T(8,128)S(1)}, f32[24,16,128]{2,1,0:T(8,128)S(1)}, u32[]{:S(2)}, u32[]{:S(2)}) collective-permute-start(f32[24,16,128]{2,1,0:T(8,128)S(1)} %get-tuple-element.212.refs_3_.refs_7_), channel_id=1, source_target_pairs={{0,4},{4,0},{8,12},{12,8},{16,20},{20,16},{24,28},{28,24},{1,5},{5... | collective-permute-start | bytes 589832 | tf_op jit(solution)/shard_map/ppermute | solution.py:353
  121.3 12.7 %collective-permute-start.24 = (f32[24,16,128]{2,1,0:T(8,128)S(1)}, f32[24,16,128]{2,1,0:T(8,128)S(1)}, u32[]{:S(2)}, u32[]{:S(2)}) collective-permute-start(f32[24,16,128]{2,1,0:T(8,128)S(1)} %get-tuple-element.213.refs_4_.refs_8_), channel_id=1, source_target_pairs={{0,28},{4,8},{8,4},{12,16},{16,12},{20,24},{24,20},{28,0},{1,29},{... | collective-permute-start | bytes 589832 | tf_op jit(solution)/shard_map/ppermute | solution.py:353
  121.3 9.9 %collective-permute-start.26 = (f32[128,128]{1,0:T(8,128)S(1)}, f32[128,128]{1,0:T(8,128)S(1)}, u32[]{:S(2)}, u32[]{:S(2)}) collective-permute-start(f32[128,128]{1,0:T(8,128)S(1)} %add.60), channel_id=1, source_target_pairs={{0,4},{4,0},{8,12},{12,8},{16,20},{20,16},{24,28},{28,24},{1,5},{5... | collective-permute-start | bytes 196616 | tf_op jit(solution)/shard_map/ppermute | solution.py:357
  123.3 15.8 %collective-permute-start.38 = (f32[12,32,128]{2,1,0:T(8,128)S(1)}, f32[12,32,128]{2,1,0:T(8,128)S(1)}, u32[]{:S(2)}, u32[]{:S(2)}) collective-permute-start(f32[12,32,128]{2,1,0:T(8,128)S(1)} %get-tuple-element.204), channel_id=1, source_target_pairs={{0,2},{1,3},{2,0},{3,1},{4,6},{5,7},{6,4},{7,5},{8,10},{9,11},{10,... | collective-permute-start | bytes 589832 | tf_op jit(solution)/shard_map/ppermute | solution.py:357
  124.8 17.6 %collective-permute-start.39 = (f32[12,32,128]{2,1,0:T(8,128)S(1)}, f32[12,32,128]{2,1,0:T(8,128)S(1)}, u32[]{:S(2)}, u32[]{:S(2)}) collective-permute-start(f32[12,32,128]{2,1,0:T(8,128)S(1)} %get-tuple-element.205), channel_id=1, source_target_pairs={{0,3},{1,2},{2,1},{3,0},{4,7},{5,6},{6,5},{7,4},{8,11},{9,10},{10,... | collective-permute-start | bytes 589832 | tf_op jit(solution)/shard_map/ppermute | solution.py:357
  131.2 11.1 %collective-permute-start.35 = (f32[24,16,128]{2,1,0:T(8,128)S(1)}, f32[24,16,128]{2,1,0:T(8,128)S(1)}, u32[]{:S(2)}, u32[]{:S(2)}) collective-permute-start(f32[24,16,128]{2,1,0:T(8,128)S(1)} %get-tuple-element.231.refs_3_.refs_7_), channel_id=1, source_target_pairs={{0,4},{4,0},{8,12},{12,8},{16,20},{20,16},{24,28},{28,24},{1,5},{5... | collective-permute-start | bytes 589832 | tf_op jit(solution)/shard_map/ppermute | solution.py:353
  131.8 10.6 %collective-permute-start.36 = (f32[24,16,128]{2,1,0:T(8,128)S(1)}, f32[24,16,128]{2,1,0:T(8,128)S(1)}, u32[]{:S(2)}, u32[]{:S(2)}) collective-permute-start(f32[24,16,128]{2,1,0:T(8,128)S(1)} %get-tuple-element.232.refs_4_.refs_8_), channel_id=1, source_target_pairs={{0,28},{4,8},{8,4},{12,16},{16,12},{20,24},{24,20},{28,0},{1,29},{... | collective-permute-start | bytes 589832 | tf_op jit(solution)/shard_map/ppermute | solution.py:353
  139.1 19.8 %collective-permute-start.31 = (f32[24,16,128]{2,1,0:T(8,128)S(1)}, f32[24,16,128]{2,1,0:T(8,128)S(1)}, u32[]{:S(2)}, u32[]{:S(2)}) collective-permute-start(f32[24,16,128]{2,1,0:T(8,128)S(1)} %get-tuple-element.192.refs_3_), channel_id=1, source_target_pairs={{0,4},{4,0},{8,12},{12,8},{16,20},{20,16},{24,28},{28,24},{1,5},{5... | collective-permute-start | bytes 589832 | tf_op jit(solution)/shard_map/ppermute | solution.py:353
  140.0 18.9 %collective-permute-start.32 = (f32[24,16,128]{2,1,0:T(8,128)S(1)}, f32[24,16,128]{2,1,0:T(8,128)S(1)}, u32[]{:S(2)}, u32[]{:S(2)}) collective-permute-start(f32[24,16,128]{2,1,0:T(8,128)S(1)} %get-tuple-element.193.refs_4_), channel_id=1, source_target_pairs={{0,28},{4,8},{8,4},{12,16},{16,12},{20,24},{24,20},{28,0},{1,29},{... | collective-permute-start | bytes 589832 | tf_op jit(solution)/shard_map/ppermute | solution.py:353
  146.6 18.6 %collective-permute-start.43 = (f32[24,16,128]{2,1,0:T(8,128)S(1)}, f32[24,16,128]{2,1,0:T(8,128)S(1)}, u32[]{:S(2)}, u32[]{:S(2)}) collective-permute-start(f32[24,16,128]{2,1,0:T(8,128)S(1)} %get-tuple-element.208.refs_3_), channel_id=1, source_target_pairs={{0,4},{4,0},{8,12},{12,8},{16,20},{20,16},{24,28},{28,24},{1,5},{5... | collective-permute-start | bytes 589832 | tf_op jit(solution)/shard_map/ppermute | solution.py:353
  148.3 17.0 %collective-permute-start.44 = (f32[24,16,128]{2,1,0:T(8,128)S(1)}, f32[24,16,128]{2,1,0:T(8,128)S(1)}, u32[]{:S(2)}, u32[]{:S(2)}) collective-permute-start(f32[24,16,128]{2,1,0:T(8,128)S(1)} %get-tuple-element.209.refs_4_), channel_id=1, source_target_pairs={{0,28},{4,8},{8,4},{12,16},{16,12},{20,24},{24,20},{28,0},{1,29},{... | collective-permute-start | bytes 589832 | tf_op jit(solution)/shard_map/ppermute | solution.py:353
  163.2 9.9 %collective-permute-start.40 = (f32[24,16,128]{2,1,0:T(8,128)S(1)}, f32[24,16,128]{2,1,0:T(8,128)S(1)}, u32[]{:S(2)}, u32[]{:S(2)}) collective-permute-start(f32[24,16,128]{2,1,0:T(8,128)S(1)} %get-tuple-element.214.refs_9_.refs_3_), channel_id=1, source_target_pairs={{0,4},{4,0},{8,12},{12,8},{16,20},{20,16},{24,28},{28,24},{1,5},{5... | collective-permute-start | bytes 589832 | tf_op jit(solution)/shard_map/ppermute | solution.py:353
  163.8 9.9 %collective-permute-start.41 = (f32[24,16,128]{2,1,0:T(8,128)S(1)}, f32[24,16,128]{2,1,0:T(8,128)S(1)}, u32[]{:S(2)}, u32[]{:S(2)}) collective-permute-start(f32[24,16,128]{2,1,0:T(8,128)S(1)} %get-tuple-element.215.refs_10_.refs_4_), channel_id=1, source_target_pairs={{0,28},{4,8},{8,4},{12,16},{16,12},{20,24},{24,20},{28,0},{1,29},{... | collective-permute-start | bytes 589832 | tf_op jit(solution)/shard_map/ppermute | solution.py:353
  169.9 12.7 %collective-permute-start.45 = (f32[12,32,128]{2,1,0:T(8,128)S(1)}, f32[12,32,128]{2,1,0:T(8,128)S(1)}, u32[]{:S(2)}, u32[]{:S(2)}) collective-permute-start(f32[12,32,128]{2,1,0:T(8,128)S(1)} %get-tuple-element.234), channel_id=1, source_target_pairs={{0,1},{1,0},{2,3},{3,2},{4,5},{5,4},{6,7},{7,6},{8,9},{9,8},{10,11... | collective-permute-start | bytes 589832 | tf_op jit(solution)/shard_map/ppermute | solution.py:357
  170.0 12.7 %collective-permute-start.46 = (f32[12,32,128]{2,1,0:T(8,128)S(1)}, f32[12,32,128]{2,1,0:T(8,128)S(1)}, u32[]{:S(2)}, u32[]{:S(2)}) collective-permute-start(f32[12,32,128]{2,1,0:T(8,128)S(1)} %get-tuple-element.235), channel_id=1, source_target_pairs={{0,2},{1,3},{2,0},{3,1},{4,6},{5,7},{6,4},{7,5},{8,10},{9,11},{10,... | collective-permute-start | bytes 589832 | tf_op jit(solution)/shard_map/ppermute | solution.py:357
  170.7 12.0 %collective-permute-start.47 = (f32[12,32,128]{2,1,0:T(8,128)S(1)}, f32[12,32,128]{2,1,0:T(8,128)S(1)}, u32[]{:S(2)}, u32[]{:S(2)}) collective-permute-start(f32[12,32,128]{2,1,0:T(8,128)S(1)} %get-tuple-element.236), channel_id=1, source_target_pairs={{0,3},{1,2},{2,1},{3,0},{4,7},{5,6},{6,5},{7,4},{8,11},{9,10},{10,... | collective-permute-start | bytes 589832 | tf_op jit(solution)/shard_map/ppermute | solution.py:357
  173.1 18.0 %collective-permute-start.50 = (f32[24,16,128]{2,1,0:T(8,128)S(1)}, f32[24,16,128]{2,1,0:T(8,128)S(1)}, u32[]{:S(2)}, u32[]{:S(2)}) collective-permute-start(f32[24,16,128]{2,1,0:T(8,128)S(1)} %get-tuple-element.238.refs_3_), channel_id=1, source_target_pairs={{0,4},{4,0},{8,12},{12,8},{16,20},{20,16},{24,28},{28,24},{1,5},{5... | collective-permute-start | bytes 589832 | tf_op jit(solution)/shard_map/ppermute | solution.py:353
  173.8 17.4 %collective-permute-start.51 = (f32[24,16,128]{2,1,0:T(8,128)S(1)}, f32[24,16,128]{2,1,0:T(8,128)S(1)}, u32[]{:S(2)}, u32[]{:S(2)}) collective-permute-start(f32[24,16,128]{2,1,0:T(8,128)S(1)} %get-tuple-element.239.refs_4_), channel_id=1, source_target_pairs={{0,28},{4,8},{8,4},{12,16},{16,12},{20,24},{24,20},{28,0},{1,29},{... | collective-permute-start | bytes 589832 | tf_op jit(solution)/shard_map/ppermute | solution.py:353
  197.4 14.2 %collective-permute-start.57 = (f32[12,32,128]{2,1,0:T(8,128)S(1)}, f32[12,32,128]{2,1,0:T(8,128)S(1)}, u32[]{:S(2)}, u32[]{:S(2)}) collective-permute-start(f32[12,32,128]{2,1,0:T(8,128)S(1)} %get-tuple-element.255), channel_id=1, source_target_pairs={{0,1},{1,0},{2,3},{3,2},{4,5},{5,4},{6,7},{7,6},{8,9},{9,8},{10,11... | collective-permute-start | bytes 589832 | tf_op jit(solution)/shard_map/ppermute | solution.py:357
  197.4 14.2 %collective-permute-start.58 = (f32[12,32,128]{2,1,0:T(8,128)S(1)}, f32[12,32,128]{2,1,0:T(8,128)S(1)}, u32[]{:S(2)}, u32[]{:S(2)}) collective-permute-start(f32[12,32,128]{2,1,0:T(8,128)S(1)} %get-tuple-element.256), channel_id=1, source_target_pairs={{0,2},{1,3},{2,0},{3,1},{4,6},{5,7},{6,4},{7,5},{8,10},{9,11},{10,... | collective-permute-start | bytes 589832 | tf_op jit(solution)/shard_map/ppermute | solution.py:357
  198.7 12.9 %collective-permute-start.59 = (f32[12,32,128]{2,1,0:T(8,128)S(1)}, f32[12,32,128]{2,1,0:T(8,128)S(1)}, u32[]{:S(2)}, u32[]{:S(2)}) collective-permute-start(f32[12,32,128]{2,1,0:T(8,128)S(1)} %get-tuple-element.257), channel_id=1, source_target_pairs={{0,3},{1,2},{2,1},{3,0},{4,7},{5,6},{6,5},{7,4},{8,11},{9,10},{10,... | collective-permute-start | bytes 589832 | tf_op jit(solution)/shard_map/ppermute | solution.py:357
  213.5 10.8 %collective-permute-start.60 = (f32[128,128]{1,0:T(8,128)S(1)}, f32[128,128]{1,0:T(8,128)S(1)}, u32[]{:S(2)}, u32[]{:S(2)}) collective-permute-start(f32[128,128]{1,0:T(8,128)S(1)} %turn_cross.1), channel_id=1, source_target_pairs={{0,8},{4,12},{8,0},{12,4},{16,24},{20,28},{24,16},{28,20},{1,9},{5... | collective-permute-start | bytes 196616 | tf_op jit(solution)/shard_map/ppermute | solution.py:357
  (24 other events, 141.6 us)

commit v11 on v9

--- a/solution.py
+++ b/solution.py
@@ -51,13 +51,16 @@
     )(*args)
 
 
-def prep_kernel(rows, ids_ref, own_ref, col_ref, blk_ref, w_ref, inv_ref, table_ref, held_ref, eye_ref, sem_ref):
+def prep_kernel(rows, groups, ids_ref, own_ref, col_ref, blk_ref, w_ref, inv_ref, table_ref, held_ref, eye_ref, sem_ref):
     count, n, _ = held_ref.shape
     steps = sem_ref.shape[0]
     chunk = count // steps
     half = rows // 2
     me = ids_ref[0]
     odd = me % 2
+    base = me * rows
+    base_next = jnp.where(me == groups - 1, 0, me + 1) * rows
+    base_last = jnp.where(me == 0, groups - 1, me - 1) * rows
 
     def fetch(step):
         span = pl.ds(step * chunk, chunk)
@@ -78,12 +81,13 @@
             b = step * chunk + c
             r = own_ref[0, b]
             k = col_ref[0, b]
-            owner = k // rows
-            local = k - owner * rows
+            mine = (k >= base) & (k < base + rows)
+            ahead = (k >= base_next) & (k < base_next + half)
+            local = k - jnp.where(mine, base, jnp.where(ahead, base_next, base_last))
             upper = (local >= half).astype(I32)
             near = local - half * upper
             swap = odd * upper + (1 - odd) * (1 - upper)
-            slot = jnp.where(owner == me, near + half * swap, 2 * half + near + half * (1 - swap))
+            slot = jnp.where(mine, near + half * swap, 2 * half + near + half * (1 - swap))
             top = (r >= half).astype(I32)
             r_at = r + half * (1 - odd) * (1 - 2 * top)
             table_ref[2 + b] = slot
@@ -110,11 +114,11 @@
     inv_ref[...] = 1.0 / inv_ref[...]
 
 
-def prep(ids, own, col, blocks, rows):
+def prep(ids, own, col, blocks, rows, groups):
     count, n, _ = blocks.shape
     own, col, blocks = (pltpu.with_memory_space_constraint(x, pltpu.HBM) for x in (own, col, blocks))
     return pl.pallas_call(
-        functools.partial(prep_kernel, rows),
+        functools.partial(prep_kernel, rows, groups),
         in_specs=[IN_SMEM] * 3 + [pl.BlockSpec(memory_space=pl.ANY)],
         out_specs=[IN_VMEM, IN_VMEM, IN_SMEM],
         out_shape=[pltpu.VMEM((count, n, 2 * n), BF16),
@@ -399,7 +403,7 @@
 
     halves = call(split_kernel, "split", [(half, each, block)] * 4, ids, start, scalars=1)
     before = [tuple(halves[:2]), tuple(halves[2:])]
-    w, inv, table = prep(ids, owner_row, block_col, blocks, slots)
+    w, inv, table = prep(ids, owner_row, block_col, blocks, slots, lax.axis_size("node"))
     meta = (table, w, inv)
 
     def advance(now, before=((), ()), parts=False):
@@ -482,11 +486,11 @@
         functools.partial(proj_kernel, nodes), "proj", [(2, cols_here, vecs)] * count, ids,
         inverse_first, image_first, inverse_last, image_last, scalars=1, scratch=[pltpu.VMEM(square, F32)],
     )
-    received, arrived = lax.optimization_barrier((swapped(parts), arrived))
-    projected = sum(received)
     (basis,) = call(
         functools.partial(join_kernel, half), "join", [(cols_here, width)], ids, *arrived, scalars=1
     )
+    received, basis = lax.optimization_barrier((swapped(parts), basis))
+    projected = sum(received)
     return basis, projected[0], projected[1]
 
 

time: 238 us -> 236 us (level)
  transfers between devices with their start and end apart: 72 -> 72, of which waited for: 13 -> 12; matrix products, arithmetic and copies ran while one was open for 0% -> 0% of each run, Pallas kernels for 44% -> 45%
where the time goes in v11:
time: 236 us
  Pallas kernels  107 us (45%)
  starting transfers between devices  99.9 us (42%)
  waiting for transfers between devices  25.9 us (11%)
    pallas_call x18, Pallas kernels, apply(): pl.pallas_call(functools.partial(apply_kernel, bool(old), bool(mate)), in...  78.4 us
    ppermute x18, starting transfers between devices, exchange(): lax.ppermute(pair[1], 'node', odd)  54.2 us
    ppermute x36, starting transfers between devices, swap(): lax.ppermute(value, axis, [(i, i ^ hop) for i in range(lax.axis_size(axis...  29.3 us
    ppermute x36, waiting for transfers between devices, swap(): lax.ppermute(value, axis, [(i, i ^ hop) for i in range(lax.axis_size(axis...  23.4 us
    pallas_call x10, Pallas kernels, call(): pl.pallas_call(kernel, in_specs=[IN_SMEM] * scalars + [IN_VMEM] * (len(ar...  20.1 us
    ppermute x18, starting transfers between devices, exchange(): lax.ppermute(pair[0], 'node', even)  16.4 us
    pallas_call x1, Pallas kernels, prep(): pl.pallas_call(functools.partial(prep_kernel, rows, groups), in_specs=[IN...  8.32 us
  transfers between devices with their start and end apart: 72, of which 12 were waited for; matrix products, arithmetic and copies ran while one was open for 0% of the time, Pallas kernels for 45%

profile of v11, /device:TPU:0, one launch (start us, length us, event | category | flops | bytes accessed | tf_op | source)
XLA Modules:
  0.0 235.8 jit_solution(11388575212343628435)
XLA Ops:
  2.5 3.0 %collective-permute-start = (f32[24,16,128]{2,1,0:T(8,128)S(1)}, f32[24,16,128]{2,1,0:T(8,128)S(1)}, u32[]{:S(2)}, u32[]{:S(2)}) collective-permute-start(f32[24,16,128]{2,1,0:T(8,128)S(1)} %get-tuple-element.141.refs_3_.refs_7_), channel_id=1, source_target_pairs={{0,4},{4,0},{8,12},{12,8},{16,20},{20,16},{24,28},{28,24},{1,5},{5... | collective-permute-start | bytes 589832 | tf_op jit(solution)/shard_map/ppermute | solution.py:353
  5.5 3.5 %collective-permute-start.1 = (f32[24,16,128]{2,1,0:T(8,128)S(1)}, f32[24,16,128]{2,1,0:T(8,128)S(1)}, u32[]{:S(2)}, u32[]{:S(2)}) collective-permute-start(f32[24,16,128]{2,1,0:T(8,128)S(1)} %get-tuple-element.142.refs_4_.refs_8_), channel_id=1, source_target_pairs={{0,28},{4,8},{8,4},{12,16},{16,12},{20,24},{24,20},{28,0},{1,29},{... | collective-permute-start | bytes 589832 | tf_op jit(solution)/shard_map/ppermute | solution.py:353
  9.1 1.9 collective-permute-start.13
  11.0 8.3 %prep.1 = (bf16[288,128,256]{2,1,0:T(8,128)(2,1)S(1)}, f32[48,1,128]{2,1,0:T(1,128)S(1)}, s32[578]{0:T(1024)S(1)}) custom-call(s32[2]{0:T(128)S(1)} %pad_add_fusion.ids_ref, s32[1,288]{1,0:T(1,128)} %own_ref.1, s32[1,288]{1,0:T(1,128)} %col_ref.1, f32[288,128,128]{2,1,0:T(8,128)} %blk_ref.1), custom_call_target="tpu_custom_call" | custom-call | flops 1207959552 | bytes 18874368 | tf_op jit(solution)/shard_map/prep/pallas_call | solution.py:120
  19.3 4.3 %apply.4 = (f32[24,16,128]{2,1,0:T(8,128)S(1)}, f32[24,16,128]{2,1,0:T(8,128)S(1)}) custom-call(s32[578]{0:T(1024)S(1)} %get-tuple-element.138.refs_0_, bf16[288,128,256]{2,1,0:T(8,128)(2,1)S(1)} %get-tuple-element.139.refs_1_, f32[48,1,128]{2,1,0:T(1,128)S(1)} %get-tuple-element.140.refs_2_, f32[24,16,128]{2,1,0:T(8,128)S(1)} %get-tuple-element.141.refs_3_.refs_7_, ...), custom_call_target="tpu_custom_call" | custom-call | bytes 4194304 | tf_op jit(solution)/shard_map/apply/pallas_call | solution.py:199
  23.6 2.5 %collective-permute-start.2 = (f32[24,16,128]{2,1,0:T(8,128)S(1)}, f32[24,16,128]{2,1,0:T(8,128)S(1)}, u32[]{:S(2)}, u32[]{:S(2)}) collective-permute-start(f32[24,16,128]{2,1,0:T(8,128)S(1)} %get-tuple-element.143.refs_3_.refs_7_), channel_id=1, source_target_pairs={{0,4},{4,0},{8,12},{12,8},{16,20},{20,16},{24,28},{28,24},{1,5},{5... | collective-permute-start | bytes 589832 | tf_op jit(solution)/shard_map/ppermute | solution.py:353
  26.1 3.5 %collective-permute-start.3 = (f32[24,16,128]{2,1,0:T(8,128)S(1)}, f32[24,16,128]{2,1,0:T(8,128)S(1)}, u32[]{:S(2)}, u32[]{:S(2)}) collective-permute-start(f32[24,16,128]{2,1,0:T(8,128)S(1)} %get-tuple-element.144.refs_4_.refs_8_), channel_id=1, source_target_pairs={{0,28},{4,8},{8,4},{12,16},{16,12},{20,24},{24,20},{28,0},{1,29},{... | collective-permute-start | bytes 589832 | tf_op jit(solution)/shard_map/ppermute | solution.py:353
  29.6 4.3 %apply.6 = (f32[24,16,128]{2,1,0:T(8,128)S(1)}, f32[24,16,128]{2,1,0:T(8,128)S(1)}) custom-call(s32[578]{0:T(1024)S(1)} %get-tuple-element.138.refs_0_, bf16[288,128,256]{2,1,0:T(8,128)(2,1)S(1)} %get-tuple-element.139.refs_1_, f32[48,1,128]{2,1,0:T(1,128)S(1)} %get-tuple-element.140.refs_2_, f32[24,16,128]{2,1,0:T(8,128)S(1)} %get-tuple-element.153.refs_3_.refs_7_, ...), custom_call_target="tpu_custom_call" | custom-call | bytes 4194304 | tf_op jit(solution)/shard_map/apply/pallas_call | solution.py:199
  34.0 1.9 collective-permute-start.15
  35.9 4.3 %apply_recur.10 = (f32[24,16,128]{2,1,0:T(8,128)S(1)}, f32[24,16,128]{2,1,0:T(8,128)S(1)}) custom-call(s32[578]{0:T(1024)S(1)} %get-tuple-element.138.refs_0_, bf16[288,128,256]{2,1,0:T(8,128)(2,1)S(1)} %get-tuple-element.139.refs_1_, f32[48,1,128]{2,1,0:T(1,128)S(1)} %get-tuple-element.140.refs_2_, f32[24,16,128]{2,1,0:T(8,128)S(1)} %get-tuple-element.143.refs_3_.refs_7_, ...), custom_call_target="tpu_custom_call" | custom-call | bytes 4194304 | tf_op jit(solution)/shard_map/apply_recur/pallas_call | solution.py:199
  40.8 8.2 %collective-permute-start.5 = (f32[24,16,128]{2,1,0:T(8,128)S(1)}, f32[24,16,128]{2,1,0:T(8,128)S(1)}, u32[]{:S(2)}, u32[]{:S(2)}) collective-permute-start(f32[24,16,128]{2,1,0:T(8,128)S(1)} %get-tuple-element.146.refs_4_.refs_8_), channel_id=1, source_target_pairs={{0,28},{4,8},{8,4},{12,16},{16,12},{20,24},{24,20},{28,0},{1,29},{... | collective-permute-start | bytes 589832 | tf_op jit(solution)/shard_map/ppermute | solution.py:353
  49.0 4.3 %apply_recur.13 = (f32[24,16,128]{2,1,0:T(8,128)S(1)}, f32[24,16,128]{2,1,0:T(8,128)S(1)}) custom-call(s32[578]{0:T(1024)S(1)} %get-tuple-element.138.refs_0_, bf16[288,128,256]{2,1,0:T(8,128)(2,1)S(1)} %get-tuple-element.139.refs_1_, f32[48,1,128]{2,1,0:T(1,128)S(1)} %get-tuple-element.140.refs_2_, f32[24,16,128]{2,1,0:T(8,128)S(1)} %get-tuple-element.155.refs_3_.refs_7_, ...), custom_call_target="tpu_custom_call" | custom-call | bytes 4194304 | tf_op jit(solution)/shard_map/apply_recur/pallas_call | solution.py:199
  53.3 2.0 collective-permute-start.17
  55.3 4.3 %apply_recur.11 = (f32[24,16,128]{2,1,0:T(8,128)S(1)}, f32[24,16,128]{2,1,0:T(8,128)S(1)}) custom-call(s32[578]{0:T(1024)S(1)} %get-tuple-element.138.refs_0_, bf16[288,128,256]{2,1,0:T(8,128)(2,1)S(1)} %get-tuple-element.139.refs_1_, f32[48,1,128]{2,1,0:T(1,128)S(1)} %get-tuple-element.140.refs_2_, f32[24,16,128]{2,1,0:T(8,128)S(1)} %get-tuple-element.145.refs_3_.refs_7_, ...), custom_call_target="tpu_custom_call" | custom-call | bytes 4194304 | tf_op jit(solution)/shard_map/apply_recur/pallas_call | solution.py:199
  59.7 2.9 %collective-permute-start.7 = (f32[24,16,128]{2,1,0:T(8,128)S(1)}, f32[24,16,128]{2,1,0:T(8,128)S(1)}, u32[]{:S(2)}, u32[]{:S(2)}) collective-permute-start(f32[24,16,128]{2,1,0:T(8,128)S(1)} %get-tuple-element.148.refs_4_), channel_id=1, source_target_pairs={{0,28},{4,8},{8,4},{12,16},{16,12},{20,24},{24,20},{28,0},{1,29},{... | collective-permute-start | bytes 589832 | tf_op jit(solution)/shard_map/ppermute | solution.py:353
  62.6 4.3 %apply_recur.14 = (f32[24,16,128]{2,1,0:T(8,128)S(1)}, f32[24,16,128]{2,1,0:T(8,128)S(1)}) custom-call(s32[578]{0:T(1024)S(1)} %get-tuple-element.138.refs_0_, bf16[288,128,256]{2,1,0:T(8,128)(2,1)S(1)} %get-tuple-element.139.refs_1_, f32[48,1,128]{2,1,0:T(1,128)S(1)} %get-tuple-element.140.refs_2_, f32[24,16,128]{2,1,0:T(8,128)S(1)} %get-tuple-element.157.refs_3_.refs_7_, ...), custom_call_target="tpu_custom_call" | custom-call | bytes 4194304 | tf_op jit(solution)/shard_map/apply_recur/pallas_call | solution.py:199
  68.0 4.9 %collective-permute-start.19 = (f32[24,16,128]{2,1,0:T(8,128)S(1)}, f32[24,16,128]{2,1,0:T(8,128)S(1)}, u32[]{:S(2)}, u32[]{:S(2)}) collective-permute-start(f32[24,16,128]{2,1,0:T(8,128)S(1)} %get-tuple-element.160.refs_4_), channel_id=1, source_target_pairs={{0,28},{4,8},{8,4},{12,16},{16,12},{20,24},{24,20},{28,0},{1,29},{... | collective-permute-start | bytes 589832 | tf_op jit(solution)/shard_map/ppermute | solution.py:353
  72.9 4.3 %apply_recur.12 = (f32[24,16,128]{2,1,0:T(8,128)S(1)}, f32[24,16,128]{2,1,0:T(8,128)S(1)}) custom-call(s32[578]{0:T(1024)S(1)} %get-tuple-element.138.refs_0_, bf16[288,128,256]{2,1,0:T(8,128)(2,1)S(1)} %get-tuple-element.139.refs_1_, f32[48,1,128]{2,1,0:T(1,128)S(1)} %get-tuple-element.140.refs_2_, f32[24,16,128]{2,1,0:T(8,128)S(1)} %get-tuple-element.147.refs_3_, ...), custom_call_target="tpu_custom_call" | custom-call | bytes 4194304 | tf_op jit(solution)/shard_map/apply_recur/pallas_call | solution.py:199
  77.3 1.9 collective-permute-start.9
  79.2 4.4 %apply_recur_parts.2 = (f32[24,16,128]{2,1,0:T(8,128)S(1)}, f32[24,16,128]{2,1,0:T(8,128)S(1)}, f32[12,32,128]{2,1,0:T(8,128)S(1)}, f32[12,32,128]{2,1,0:T(8,128...) custom-call(s32[578]{0:T(1024)S(1)} %get-tuple-element.138.refs_0_, ...), custom_call_target="tpu_custom_call" | custom-call | bytes 4194304 | tf_op jit(solution)/shard_map/apply_recur_parts/pallas_call | solution.py:199
  84.5 8.7 %collective-permute-start.28 = (f32[24,16,128]{2,1,0:T(8,128)S(1)}, f32[24,16,128]{2,1,0:T(8,128)S(1)}, u32[]{:S(2)}, u32[]{:S(2)}) collective-permute-start(f32[24,16,128]{2,1,0:T(8,128)S(1)} %get-tuple-element.180.refs_4_.refs_8_), channel_id=1, source_target_pairs={{0,28},{4,8},{8,4},{12,16},{16,12},{20,24},{24,20},{28,0},{1,29},{... | collective-permute-start | bytes 589832 | tf_op jit(solution)/shard_map/ppermute | solution.py:353
  95.1 4.3 %apply.5 = (f32[24,16,128]{2,1,0:T(8,128)S(1)}, f32[24,16,128]{2,1,0:T(8,128)S(1)}) custom-call(s32[578]{0:T(1024)S(1)} %get-tuple-element.138.refs_0_, bf16[288,128,256]{2,1,0:T(8,128)(2,1)S(1)} %get-tuple-element.139.refs_1_, f32[48,1,128]{2,1,0:T(1,128)S(1)} %get-tuple-element.140.refs_2_, f32[24,16,128]{2,1,0:T(8,128)S(1)} %get-tuple-element.166.refs_3_.refs_9_.refs_7_, ...), custom_call_target="tpu_custom_call" | custom-call | bytes 4194304 | tf_op jit(solution)/shard_map/apply/pallas_call | solution.py:199
  99.4 2.1 collective-permute-start.11
  101.6 4.5 %apply_parts.2 = (f32[24,16,128]{2,1,0:T(8,128)S(1)}, f32[24,16,128]{2,1,0:T(8,128)S(1)}, f32[12,32,128]{2,1,0:T(8,128)S(1)}, f32[12,32,128]{2,1,0:T(8,128)S(1)}...) custom-call(s32[578]{0:T(1024)S(1)} %get-tuple-element.138.refs_0_, ...), custom_call_target="tpu_custom_call" | custom-call | bytes 4194304 | tf_op jit(solution)/shard_map/apply_parts/pallas_call | solution.py:199
  106.3 2.7 %collective-permute-start.30 = (f32[24,16,128]{2,1,0:T(8,128)S(1)}, f32[24,16,128]{2,1,0:T(8,128)S(1)}, u32[]{:S(2)}, u32[]{:S(2)}) collective-permute-start(f32[24,16,128]{2,1,0:T(8,128)S(1)} %get-tuple-element.202.refs_4_.refs_8_), channel_id=1, source_target_pairs={{0,28},{4,8},{8,4},{12,16},{16,12},{20,24},{24,20},{28,0},{1,29},{... | collective-permute-start | bytes 589832 | tf_op jit(solution)/shard_map/ppermute | solution.py:353
  111.3 4.3 %apply_recur.15 = (f32[24,16,128]{2,1,0:T(8,128)S(1)}, f32[24,16,128]{2,1,0:T(8,128)S(1)}) custom-call(s32[578]{0:T(1024)S(1)} %get-tuple-element.138.refs_0_, bf16[288,128,256]{2,1,0:T(8,128)(2,1)S(1)} %get-tuple-element.139.refs_1_, f32[48,1,128]{2,1,0:T(1,128)S(1)} %get-tuple-element.140.refs_2_, f32[24,16,128]{2,1,0:T(8,128)S(1)} %get-tuple-element.185.refs_3_.refs_7_, ...), custom_call_target="tpu_custom_call" | custom-call | bytes 4194304 | tf_op jit(solution)/shard_map/apply_recur/pallas_call | solution.py:199
  121.3 4.2 %apply_recur.16 = (f32[24,16,128]{2,1,0:T(8,128)S(1)}, f32[24,16,128]{2,1,0:T(8,128)S(1)}) custom-call(s32[578]{0:T(1024)S(1)} %get-tuple-element.138.refs_0_, bf16[288,128,256]{2,1,0:T(8,128)(2,1)S(1)} %get-tuple-element.139.refs_1_, f32[48,1,128]{2,1,0:T(1,128)S(1)} %get-tuple-element.140.refs_2_, f32[24,16,128]{2,1,0:T(8,128)S(1)} %get-tuple-element.201.refs_3_.refs_7_, ...), custom_call_target="tpu_custom_call" | custom-call | bytes 4194304 | tf_op jit(solution)/shard_map/apply_recur/pallas_call | solution.py:199
  129.0 4.3 %apply_recur.17 = (f32[24,16,128]{2,1,0:T(8,128)S(1)}, f32[24,16,128]{2,1,0:T(8,128)S(1)}) custom-call(s32[578]{0:T(1024)S(1)} %get-tuple-element.138.refs_0_, bf16[288,128,256]{2,1,0:T(8,128)(2,1)S(1)} %get-tuple-element.139.refs_1_, f32[48,1,128]{2,1,0:T(1,128)S(1)} %get-tuple-element.140.refs_2_, f32[24,16,128]{2,1,0:T(8,128)S(1)} %get-tuple-element.207.refs_3_.refs_7_, ...), custom_call_target="tpu_custom_call" | custom-call | bytes 4194304 | tf_op jit(solution)/shard_map/apply_recur/pallas_call | solution.py:199
  133.3 1.9 collective-permute-start.31
  135.2 3.7 %collective-permute-done.33 = f32[128,128]{1,0:T(8,128)S(1)} collective-permute-done((f32[128,128]{1,0:T(8,128)S(1)}, f32[128,128]{1,0:T(8,128)S(1)}, u32[]{:S(2)}, u32[]{:S(2)}) %collective-permute-start.33) | collective-permute-done | bytes 65568 | tf_op jit(solution)/shard_map/ppermute | solution.py:357
  139.0 2.8 %collective-permute-start.32 = (f32[24,16,128]{2,1,0:T(8,128)S(1)}, f32[24,16,128]{2,1,0:T(8,128)S(1)}, u32[]{:S(2)}, u32[]{:S(2)}) collective-permute-start(f32[24,16,128]{2,1,0:T(8,128)S(1)} %get-tuple-element.188.refs_4_), channel_id=1, source_target_pairs={{0,28},{4,8},{8,4},{12,16},{16,12},{20,24},{24,20},{28,0},{1,29},{... | collective-permute-start | bytes 589832 | tf_op jit(solution)/shard_map/ppermute | solution.py:353
  141.8 4.3 %apply_recur.18 = (f32[24,16,128]{2,1,0:T(8,128)S(1)}, f32[24,16,128]{2,1,0:T(8,128)S(1)}) custom-call(s32[578]{0:T(1024)S(1)} %get-tuple-element.138.refs_0_, bf16[288,128,256]{2,1,0:T(8,128)(2,1)S(1)} %get-tuple-element.139.refs_1_, f32[48,1,128]{2,1,0:T(1,128)S(1)} %get-tuple-element.140.refs_2_, f32[24,16,128]{2,1,0:T(8,128)S(1)} %get-tuple-element.218.refs_3_.refs_7_, ...), custom_call_target="tpu_custom_call" | custom-call | bytes 4194304 | tf_op jit(solution)/shard_map/apply_recur/pallas_call | solution.py:199
  146.3 1.9 collective-permute-start.44
  149.7 6.1 %collective-permute-done.34 = f32[128,128]{1,0:T(8,128)S(1)} collective-permute-done((f32[128,128]{1,0:T(8,128)S(1)}, f32[128,128]{1,0:T(8,128)S(1)}, u32[]{:S(2)}, u32[]{:S(2)}) %collective-permute-start.34) | collective-permute-done | bytes 65568 | tf_op jit(solution)/shard_map/ppermute | solution.py:357
  155.9 4.2 %apply_recur.19 = (f32[24,16,128]{2,1,0:T(8,128)S(1)}, f32[24,16,128]{2,1,0:T(8,128)S(1)}) custom-call(s32[578]{0:T(1024)S(1)} %get-tuple-element.138.refs_0_, bf16[288,128,256]{2,1,0:T(8,128)(2,1)S(1)} %get-tuple-element.139.refs_1_, f32[48,1,128]{2,1,0:T(1,128)S(1)} %get-tuple-element.140.refs_2_, f32[24,16,128]{2,1,0:T(8,128)S(1)} %get-tuple-element.187.refs_3_, ...), custom_call_target="tpu_custom_call" | custom-call | bytes 4194304 | tf_op jit(solution)/shard_map/apply_recur/pallas_call | solution.py:199
  160.2 2.7 %collective-permute-start.40 = (f32[24,16,128]{2,1,0:T(8,128)S(1)}, f32[24,16,128]{2,1,0:T(8,128)S(1)}, u32[]{:S(2)}, u32[]{:S(2)}) collective-permute-start(f32[24,16,128]{2,1,0:T(8,128)S(1)} %get-tuple-element.209.refs_9_.refs_3_), channel_id=1, source_target_pairs={{0,4},{4,0},{8,12},{12,8},{16,20},{20,16},{24,28},{28,24},{1,5},{5... | collective-permute-start | bytes 589832 | tf_op jit(solution)/shard_map/ppermute | solution.py:353
  164.3 4.6 %apply_recur_parts.3 = (f32[24,16,128]{2,1,0:T(8,128)S(1)}, f32[24,16,128]{2,1,0:T(8,128)S(1)}, f32[12,32,128]{2,1,0:T(8,128)S(1)}, f32[12,32,128]{2,1,0:T(8,128...) custom-call(s32[578]{0:T(1024)S(1)} %get-tuple-element.138.refs_0_, ...), custom_call_target="tpu_custom_call" | custom-call | bytes 4194304 | tf_op jit(solution)/shard_map/apply_recur_parts/pallas_call | solution.py:199
  170.8 2.2 collective-permute-start.50
  174.3 4.1 %factor.2.inv_ref.refs_0_ = f32[128,128]{1,0:T(8,128)S(1)} custom-call(f32[128,128]{1,0:T(8,128)S(1)} %add.67.g_ref), custom_call_target="tpu_custom_call" | custom-call | tf_op jit(solution)/shard_map/factor/pallas_call | solution.py:42
  180.1 2.5 %turn.1 = (f32[12,128,128]{2,1,0:T(8,128)S(1)}, f32[128,128]{1,0:T(8,128)S(1)}) custom-call(s32[2]{0:T(128)S(1)} %pad_add_fusion.ids_ref, f32[128,128]{1,0:T(8,128)S(1)} %factor.2.inv_ref.refs_0_, f32[12,32,128]{2,1,0:T(8,128)S(1)} %get-tuple-element.220.refs_0_, f32[12,32,128]{2,1,0:T(8,128)S(1)} %collective-permute-done.45.refs_1_, ...), custom_call_target="tpu_custom_call" | custom-call | tf_op jit(solution)/shard_map/turn/pallas_call | solution.py:42
  185.3 4.2 %apply.7 = (f32[24,16,128]{2,1,0:T(8,128)S(1)}, f32[24,16,128]{2,1,0:T(8,128)S(1)}) custom-call(s32[578]{0:T(1024)S(1)} %get-tuple-element.138.refs_0_, bf16[288,128,256]{2,1,0:T(8,128)(2,1)S(1)} %get-tuple-element.139.refs_1_, f32[48,1,128]{2,1,0:T(1,128)S(1)} %get-tuple-element.140.refs_2_, f32[24,16,128]{2,1,0:T(8,128)S(1)} %get-tuple-element.209.refs_9_.refs_3_, ...), custom_call_target="tpu_custom_call" | custom-call | bytes 4194304 | tf_op jit(solution)/shard_map/apply/pallas_call | solution.py:199
  189.6 5.3 %apply_parts.3 = (f32[24,16,128]{2,1,0:T(8,128)}, f32[24,16,128]{2,1,0:T(8,128)}, f32[12,32,128]{2,1,0:T(8,128)S(1)}, f32[12,32,128]{2,1,0:T(8,128)S(1)}, f32[12...) custom-call(s32[578]{0:T(1024)S(1)} %get-tuple-element.138.refs_0_, ...), custom_call_target="tpu_custom_call" | custom-call | bytes 4194304 | tf_op jit(solution)/shard_map/apply_parts/pallas_call | solution.py:199
  198.7 2.6 %collective-permute-done.53 = f32[128,128]{1,0:T(8,128)S(1)} collective-permute-done((f32[128,128]{1,0:T(8,128)S(1)}, f32[128,128]{1,0:T(8,128)S(1)}, u32[]{:S(2)}, u32[]{:S(2)}) %collective-permute-start.53) | collective-permute-done | bytes 65568 | tf_op jit(solution)/shard_map/ppermute | solution.py:357
  204.4 1.9 collective-permute-start.62
  210.5 2.5 %collective-permute-start.60 = (f32[128,128]{1,0:T(8,128)S(1)}, f32[128,128]{1,0:T(8,128)S(1)}, u32[]{:S(2)}, u32[]{:S(2)}) collective-permute-start(f32[128,128]{1,0:T(8,128)S(1)} %turn_cross.1), channel_id=1, source_target_pairs={{0,24},{4,28},{8,16},{12,20},{16,8},{20,12},{24,0},{28,4},{1,25},{... | collective-permute-start | bytes 196616 | tf_op jit(solution)/shard_map/ppermute | solution.py:357
  214.9 4.1 %factor.3.inv_ref.refs_2_ = f32[128,128]{1,0:T(8,128)S(1)} custom-call(f32[128,128]{1,0:T(8,128)S(1)} %add.72.g_ref), custom_call_target="tpu_custom_call" | custom-call | tf_op jit(solution)/shard_map/factor/pallas_call | solution.py:42
  220.5 1.9 collective-permute-start.65
  224.8 3.8 %collective-permute-done.64 = f32[128,128]{1,0:T(8,128)S(1)} collective-permute-done((f32[128,128]{1,0:T(8,128)S(1)}, f32[128,128]{1,0:T(8,128)S(1)}, u32[]{:S(2)}, u32[]{:S(2)}) %collective-permute-start.64) | collective-permute-done | bytes 65568 | tf_op jit(solution)/shard_map/ppermute | solution.py:357
  (144 shorter events, 53.2 us)
Async XLA Ops:
  2.5 16.8 %collective-permute-start = (f32[24,16,128]{2,1,0:T(8,128)S(1)}, f32[24,16,128]{2,1,0:T(8,128)S(1)}, u32[]{:S(2)}, u32[]{:S(2)}) collective-permute-start(f32[24,16,128]{2,1,0:T(8,128)S(1)} %get-tuple-element.141.refs_3_.refs_7_), channel_id=1, source_target_pairs={{0,4},{4,0},{8,12},{12,8},{16,20},{20,16},{24,28},{28,24},{1,5},{5... | collective-permute-start | bytes 589832 | tf_op jit(solution)/shard_map/ppermute | solution.py:353
  5.5 13.8 %collective-permute-start.1 = (f32[24,16,128]{2,1,0:T(8,128)S(1)}, f32[24,16,128]{2,1,0:T(8,128)S(1)}, u32[]{:S(2)}, u32[]{:S(2)}) collective-permute-start(f32[24,16,128]{2,1,0:T(8,128)S(1)} %get-tuple-element.142.refs_4_.refs_8_), channel_id=1, source_target_pairs={{0,28},{4,8},{8,4},{12,16},{16,12},{20,24},{24,20},{28,0},{1,29},{... | collective-permute-start | bytes 589832 | tf_op jit(solution)/shard_map/ppermute | solution.py:353
  9.1 20.5 %collective-permute-start.12 = (f32[24,16,128]{2,1,0:T(8,128)S(1)}, f32[24,16,128]{2,1,0:T(8,128)S(1)}, u32[]{:S(2)}, u32[]{:S(2)}) collective-permute-start(f32[24,16,128]{2,1,0:T(8,128)S(1)} %get-tuple-element.153.refs_3_.refs_7_), channel_id=1, source_target_pairs={{0,4},{4,0},{8,12},{12,8},{16,20},{20,16},{24,28},{28,24},{1,5},{5... | collective-permute-start | bytes 589832 | tf_op jit(solution)/shard_map/ppermute | solution.py:353
  9.1 20.5 %collective-permute-start.13 = (f32[24,16,128]{2,1,0:T(8,128)S(1)}, f32[24,16,128]{2,1,0:T(8,128)S(1)}, u32[]{:S(2)}, u32[]{:S(2)}) collective-permute-start(f32[24,16,128]{2,1,0:T(8,128)S(1)} %get-tuple-element.154.refs_4_.refs_8_), channel_id=1, source_target_pairs={{0,28},{4,8},{8,4},{12,16},{16,12},{20,24},{24,20},{28,0},{1,29},{... | collective-permute-start | bytes 589832 | tf_op jit(solution)/shard_map/ppermute | solution.py:353
  23.6 12.2 %collective-permute-start.2 = (f32[24,16,128]{2,1,0:T(8,128)S(1)}, f32[24,16,128]{2,1,0:T(8,128)S(1)}, u32[]{:S(2)}, u32[]{:S(2)}) collective-permute-start(f32[24,16,128]{2,1,0:T(8,128)S(1)} %get-tuple-element.143.refs_3_.refs_7_), channel_id=1, source_target_pairs={{0,4},{4,0},{8,12},{12,8},{16,20},{20,16},{24,28},{28,24},{1,5},{5... | collective-permute-start | bytes 589832 | tf_op jit(solution)/shard_map/ppermute | solution.py:353
  33.9 15.1 %collective-permute-start.14 = (f32[24,16,128]{2,1,0:T(8,128)S(1)}, f32[24,16,128]{2,1,0:T(8,128)S(1)}, u32[]{:S(2)}, u32[]{:S(2)}) collective-permute-start(f32[24,16,128]{2,1,0:T(8,128)S(1)} %get-tuple-element.155.refs_3_.refs_7_), channel_id=1, source_target_pairs={{0,4},{4,0},{8,12},{12,8},{16,20},{20,16},{24,28},{28,24},{1,5},{5... | collective-permute-start | bytes 589832 | tf_op jit(solution)/shard_map/ppermute | solution.py:353
  34.0 15.0 %collective-permute-start.15 = (f32[24,16,128]{2,1,0:T(8,128)S(1)}, f32[24,16,128]{2,1,0:T(8,128)S(1)}, u32[]{:S(2)}, u32[]{:S(2)}) collective-permute-start(f32[24,16,128]{2,1,0:T(8,128)S(1)} %get-tuple-element.156.refs_4_.refs_8_), channel_id=1, source_target_pairs={{0,28},{4,8},{8,4},{12,16},{16,12},{20,24},{24,20},{28,0},{1,29},{... | collective-permute-start | bytes 589832 | tf_op jit(solution)/shard_map/ppermute | solution.py:353
  40.1 15.2 %collective-permute-start.4 = (f32[24,16,128]{2,1,0:T(8,128)S(1)}, f32[24,16,128]{2,1,0:T(8,128)S(1)}, u32[]{:S(2)}, u32[]{:S(2)}) collective-permute-start(f32[24,16,128]{2,1,0:T(8,128)S(1)} %get-tuple-element.145.refs_3_.refs_7_), channel_id=1, source_target_pairs={{0,4},{4,0},{8,12},{12,8},{16,20},{20,16},{24,28},{28,24},{1,5},{5... | collective-permute-start | bytes 589832 | tf_op jit(solution)/shard_map/ppermute | solution.py:353
  40.8 14.5 %collective-permute-start.5 = (f32[24,16,128]{2,1,0:T(8,128)S(1)}, f32[24,16,128]{2,1,0:T(8,128)S(1)}, u32[]{:S(2)}, u32[]{:S(2)}) collective-permute-start(f32[24,16,128]{2,1,0:T(8,128)S(1)} %get-tuple-element.146.refs_4_.refs_8_), channel_id=1, source_target_pairs={{0,28},{4,8},{8,4},{12,16},{16,12},{20,24},{24,20},{28,0},{1,29},{... | collective-permute-start | bytes 589832 | tf_op jit(solution)/shard_map/ppermute | solution.py:353
  59.6 13.3 %collective-permute-start.6 = (f32[24,16,128]{2,1,0:T(8,128)S(1)}, f32[24,16,128]{2,1,0:T(8,128)S(1)}, u32[]{:S(2)}, u32[]{:S(2)}) collective-permute-start(f32[24,16,128]{2,1,0:T(8,128)S(1)} %get-tuple-element.147.refs_3_), channel_id=1, source_target_pairs={{0,4},{4,0},{8,12},{12,8},{16,20},{20,16},{24,28},{28,24},{1,5},{5... | collective-permute-start | bytes 589832 | tf_op jit(solution)/shard_map/ppermute | solution.py:353
  59.7 13.2 %collective-permute-start.7 = (f32[24,16,128]{2,1,0:T(8,128)S(1)}, f32[24,16,128]{2,1,0:T(8,128)S(1)}, u32[]{:S(2)}, u32[]{:S(2)}) collective-permute-start(f32[24,16,128]{2,1,0:T(8,128)S(1)} %get-tuple-element.148.refs_4_), channel_id=1, source_target_pairs={{0,28},{4,8},{8,4},{12,16},{16,12},{20,24},{24,20},{28,0},{1,29},{... | collective-permute-start | bytes 589832 | tf_op jit(solution)/shard_map/ppermute | solution.py:353
  66.9 12.3 %collective-permute-start.18 = (f32[24,16,128]{2,1,0:T(8,128)S(1)}, f32[24,16,128]{2,1,0:T(8,128)S(1)}, u32[]{:S(2)}, u32[]{:S(2)}) collective-permute-start(f32[24,16,128]{2,1,0:T(8,128)S(1)} %get-tuple-element.159.refs_3_), channel_id=1, source_target_pairs={{0,4},{4,0},{8,12},{12,8},{16,20},{20,16},{24,28},{28,24},{1,5},{5... | collective-permute-start | bytes 589832 | tf_op jit(solution)/shard_map/ppermute | solution.py:353
  68.0 11.2 %collective-permute-start.19 = (f32[24,16,128]{2,1,0:T(8,128)S(1)}, f32[24,16,128]{2,1,0:T(8,128)S(1)}, u32[]{:S(2)}, u32[]{:S(2)}) collective-permute-start(f32[24,16,128]{2,1,0:T(8,128)S(1)} %get-tuple-element.160.refs_4_), channel_id=1, source_target_pairs={{0,28},{4,8},{8,4},{12,16},{16,12},{20,24},{24,20},{28,0},{1,29},{... | collective-permute-start | bytes 589832 | tf_op jit(solution)/shard_map/ppermute | solution.py:353
  77.2 16.0 %collective-permute-start.8 = (f32[24,16,128]{2,1,0:T(8,128)S(1)}, f32[24,16,128]{2,1,0:T(8,128)S(1)}, u32[]{:S(2)}, u32[]{:S(2)}) collective-permute-start(f32[24,16,128]{2,1,0:T(8,128)S(1)} %get-tuple-element.166.refs_3_.refs_9_.refs_7_), channel_id=1, source_target_pairs={{0,4},{4,0},{8,12},{12,8},{16,20},{20,16},{24,28},{28,24},{1,5},{5... | collective-permute-start | bytes 589832 | tf_op jit(solution)/shard_map/ppermute | solution.py:353
  77.3 17.4 %collective-permute-start.9 = (f32[24,16,128]{2,1,0:T(8,128)S(1)}, f32[24,16,128]{2,1,0:T(8,128)S(1)}, u32[]{:S(2)}, u32[]{:S(2)}) collective-permute-start(f32[24,16,128]{2,1,0:T(8,128)S(1)} %get-tuple-element.167.refs_4_.refs_10_.refs_8_), channel_id=1, source_target_pairs={{0,28},{4,8},{8,4},{12,16},{16,12},{20,24},{24,20},{28,0},{1,29},{... | collective-permute-start | bytes 589832 | tf_op jit(solution)/shard_map/ppermute | solution.py:353
  83.6 15.7 %collective-permute-start.27 = (f32[24,16,128]{2,1,0:T(8,128)S(1)}, f32[24,16,128]{2,1,0:T(8,128)S(1)}, u32[]{:S(2)}, u32[]{:S(2)}) collective-permute-start(f32[24,16,128]{2,1,0:T(8,128)S(1)} %get-tuple-element.179.refs_3_.refs_7_), channel_id=1, source_target_pairs={{0,4},{4,0},{8,12},{12,8},{16,20},{20,16},{24,28},{28,24},{1,5},{5... | collective-permute-start | bytes 589832 | tf_op jit(solution)/shard_map/ppermute | solution.py:353
  84.5 14.9 %collective-permute-start.28 = (f32[24,16,128]{2,1,0:T(8,128)S(1)}, f32[24,16,128]{2,1,0:T(8,128)S(1)}, u32[]{:S(2)}, u32[]{:S(2)}) collective-permute-start(f32[24,16,128]{2,1,0:T(8,128)S(1)} %get-tuple-element.180.refs_4_.refs_8_), channel_id=1, source_target_pairs={{0,28},{4,8},{8,4},{12,16},{16,12},{20,24},{24,20},{28,0},{1,29},{... | collective-permute-start | bytes 589832 | tf_op jit(solution)/shard_map/ppermute | solution.py:353
  93.2 12.9 %collective-permute-start.20 = (f32[12,32,128]{2,1,0:T(8,128)S(1)}, f32[12,32,128]{2,1,0:T(8,128)S(1)}, u32[]{:S(2)}, u32[]{:S(2)}) collective-permute-start(f32[12,32,128]{2,1,0:T(8,128)S(1)} %get-tuple-element.162), channel_id=1, source_target_pairs={{0,1},{1,0},{2,3},{3,2},{4,5},{5,4},{6,7},{7,6},{8,9},{9,8},{10,11... | collective-permute-start | bytes 589832 | tf_op jit(solution)/shard_map/ppermute | solution.py:357
  93.2 13.0 %collective-permute-start.21 = (f32[12,32,128]{2,1,0:T(8,128)S(1)}, f32[12,32,128]{2,1,0:T(8,128)S(1)}, u32[]{:S(2)}, u32[]{:S(2)}) collective-permute-start(f32[12,32,128]{2,1,0:T(8,128)S(1)} %get-tuple-element.163), channel_id=1, source_target_pairs={{0,2},{1,3},{2,0},{3,1},{4,6},{5,7},{6,4},{7,5},{8,10},{9,11},{10,... | collective-permute-start | bytes 589832 | tf_op jit(solution)/shard_map/ppermute | solution.py:357
  94.7 11.6 %collective-permute-start.22 = (f32[12,32,128]{2,1,0:T(8,128)S(1)}, f32[12,32,128]{2,1,0:T(8,128)S(1)}, u32[]{:S(2)}, u32[]{:S(2)}) collective-permute-start(f32[12,32,128]{2,1,0:T(8,128)S(1)} %get-tuple-element.164), channel_id=1, source_target_pairs={{0,3},{1,2},{2,1},{3,0},{4,7},{5,6},{6,5},{7,4},{8,11},{9,10},{10,... | collective-permute-start | bytes 589832 | tf_op jit(solution)/shard_map/ppermute | solution.py:357
  99.3 12.0 %collective-permute-start.10 = (f32[24,16,128]{2,1,0:T(8,128)S(1)}, f32[24,16,128]{2,1,0:T(8,128)S(1)}, u32[]{:S(2)}, u32[]{:S(2)}) collective-permute-start(f32[24,16,128]{2,1,0:T(8,128)S(1)} %get-tuple-element.185.refs_3_.refs_7_), channel_id=1, source_target_pairs={{0,4},{4,0},{8,12},{12,8},{16,20},{20,16},{24,28},{28,24},{1,5},{5... | collective-permute-start | bytes 589832 | tf_op jit(solution)/shard_map/ppermute | solution.py:353
  99.4 11.9 %collective-permute-start.11 = (f32[24,16,128]{2,1,0:T(8,128)S(1)}, f32[24,16,128]{2,1,0:T(8,128)S(1)}, u32[]{:S(2)}, u32[]{:S(2)}) collective-permute-start(f32[24,16,128]{2,1,0:T(8,128)S(1)} %get-tuple-element.186.refs_4_.refs_8_), channel_id=1, source_target_pairs={{0,28},{4,8},{8,4},{12,16},{16,12},{20,24},{24,20},{28,0},{1,29},{... | collective-permute-start | bytes 589832 | tf_op jit(solution)/shard_map/ppermute | solution.py:353
  106.1 12.4 %collective-permute-start.37 = (f32[12,32,128]{2,1,0:T(8,128)S(1)}, f32[12,32,128]{2,1,0:T(8,128)S(1)}, u32[]{:S(2)}, u32[]{:S(2)}) collective-permute-start(f32[12,32,128]{2,1,0:T(8,128)S(1)} %get-tuple-element.198), channel_id=1, source_target_pairs={{0,1},{1,0},{2,3},{3,2},{4,5},{5,4},{6,7},{7,6},{8,9},{9,8},{10,11... | collective-permute-start | bytes 589832 | tf_op jit(solution)/shard_map/ppermute | solution.py:357
  106.2 13.8 %collective-permute-start.29 = (f32[24,16,128]{2,1,0:T(8,128)S(1)}, f32[24,16,128]{2,1,0:T(8,128)S(1)}, u32[]{:S(2)}, u32[]{:S(2)}) collective-permute-start(f32[24,16,128]{2,1,0:T(8,128)S(1)} %get-tuple-element.201.refs_3_.refs_7_), channel_id=1, source_target_pairs={{0,4},{4,0},{8,12},{12,8},{16,20},{20,16},{24,28},{28,24},{1,5},{5... | collective-permute-start | bytes 589832 | tf_op jit(solution)/shard_map/ppermute | solution.py:353
  106.3 15.0 %collective-permute-start.30 = (f32[24,16,128]{2,1,0:T(8,128)S(1)}, f32[24,16,128]{2,1,0:T(8,128)S(1)}, u32[]{:S(2)}, u32[]{:S(2)}) collective-permute-start(f32[24,16,128]{2,1,0:T(8,128)S(1)} %get-tuple-element.202.refs_4_.refs_8_), channel_id=1, source_target_pairs={{0,28},{4,8},{8,4},{12,16},{16,12},{20,24},{24,20},{28,0},{1,29},{... | collective-permute-start | bytes 589832 | tf_op jit(solution)/shard_map/ppermute | solution.py:353
  115.6 11.9 %collective-permute-start.23 = (f32[24,16,128]{2,1,0:T(8,128)S(1)}, f32[24,16,128]{2,1,0:T(8,128)S(1)}, u32[]{:S(2)}, u32[]{:S(2)}) collective-permute-start(f32[24,16,128]{2,1,0:T(8,128)S(1)} %get-tuple-element.207.refs_3_.refs_7_), channel_id=1, source_target_pairs={{0,4},{4,0},{8,12},{12,8},{16,20},{20,16},{24,28},{28,24},{1,5},{5... | collective-permute-start | bytes 589832 | tf_op jit(solution)/shard_map/ppermute | solution.py:353
  117.0 11.8 %collective-permute-start.24 = (f32[24,16,128]{2,1,0:T(8,128)S(1)}, f32[24,16,128]{2,1,0:T(8,128)S(1)}, u32[]{:S(2)}, u32[]{:S(2)}) collective-permute-start(f32[24,16,128]{2,1,0:T(8,128)S(1)} %get-tuple-element.208.refs_4_.refs_8_), channel_id=1, source_target_pairs={{0,28},{4,8},{8,4},{12,16},{16,12},{20,24},{24,20},{28,0},{1,29},{... | collective-permute-start | bytes 589832 | tf_op jit(solution)/shard_map/ppermute | solution.py:353
  120.0 13.3 %collective-permute-start.38 = (f32[12,32,128]{2,1,0:T(8,128)S(1)}, f32[12,32,128]{2,1,0:T(8,128)S(1)}, u32[]{:S(2)}, u32[]{:S(2)}) collective-permute-start(f32[12,32,128]{2,1,0:T(8,128)S(1)} %get-tuple-element.199), channel_id=1, source_target_pairs={{0,2},{1,3},{2,0},{3,1},{4,6},{5,7},{6,4},{7,5},{8,10},{9,11},{10,... | collective-permute-start | bytes 589832 | tf_op jit(solution)/shard_map/ppermute | solution.py:357
  121.3 20.5 %collective-permute-start.39 = (f32[12,32,128]{2,1,0:T(8,128)S(1)}, f32[12,32,128]{2,1,0:T(8,128)S(1)}, u32[]{:S(2)}, u32[]{:S(2)}) collective-permute-start(f32[12,32,128]{2,1,0:T(8,128)S(1)} %get-tuple-element.200), channel_id=1, source_target_pairs={{0,3},{1,2},{2,1},{3,0},{4,7},{5,6},{6,5},{7,4},{8,11},{9,10},{10,... | collective-permute-start | bytes 589832 | tf_op jit(solution)/shard_map/ppermute | solution.py:357
  125.5 16.3 %collective-permute-start.35 = (f32[24,16,128]{2,1,0:T(8,128)S(1)}, f32[24,16,128]{2,1,0:T(8,128)S(1)}, u32[]{:S(2)}, u32[]{:S(2)}) collective-permute-start(f32[24,16,128]{2,1,0:T(8,128)S(1)} %get-tuple-element.218.refs_3_.refs_7_), channel_id=1, source_target_pairs={{0,4},{4,0},{8,12},{12,8},{16,20},{20,16},{24,28},{28,24},{1,5},{5... | collective-permute-start | bytes 589832 | tf_op jit(solution)/shard_map/ppermute | solution.py:353
  127.5 14.2 %collective-permute-start.36 = (f32[24,16,128]{2,1,0:T(8,128)S(1)}, f32[24,16,128]{2,1,0:T(8,128)S(1)}, u32[]{:S(2)}, u32[]{:S(2)}) collective-permute-start(f32[24,16,128]{2,1,0:T(8,128)S(1)} %get-tuple-element.219.refs_4_.refs_8_), channel_id=1, source_target_pairs={{0,28},{4,8},{8,4},{12,16},{16,12},{20,24},{24,20},{28,0},{1,29},{... | collective-permute-start | bytes 589832 | tf_op jit(solution)/shard_map/ppermute | solution.py:353
  128.8 10.2 %collective-permute-start.33 = (f32[128,128]{1,0:T(8,128)S(1)}, f32[128,128]{1,0:T(8,128)S(1)}, u32[]{:S(2)}, u32[]{:S(2)}) collective-permute-start(f32[128,128]{1,0:T(8,128)S(1)} %add.64), channel_id=1, source_target_pairs={{0,4},{4,0},{8,12},{12,8},{16,20},{20,16},{24,28},{28,24},{1,5},{5... | collective-permute-start | bytes 196616 | tf_op jit(solution)/shard_map/ppermute | solution.py:357
  133.3 22.6 %collective-permute-start.31 = (f32[24,16,128]{2,1,0:T(8,128)S(1)}, f32[24,16,128]{2,1,0:T(8,128)S(1)}, u32[]{:S(2)}, u32[]{:S(2)}) collective-permute-start(f32[24,16,128]{2,1,0:T(8,128)S(1)} %get-tuple-element.187.refs_3_), channel_id=1, source_target_pairs={{0,4},{4,0},{8,12},{12,8},{16,20},{20,16},{24,28},{28,24},{1,5},{5... | collective-permute-start | bytes 589832 | tf_op jit(solution)/shard_map/ppermute | solution.py:353
  139.0 17.0 %collective-permute-start.32 = (f32[24,16,128]{2,1,0:T(8,128)S(1)}, f32[24,16,128]{2,1,0:T(8,128)S(1)}, u32[]{:S(2)}, u32[]{:S(2)}) collective-permute-start(f32[24,16,128]{2,1,0:T(8,128)S(1)} %get-tuple-element.188.refs_4_), channel_id=1, source_target_pairs={{0,28},{4,8},{8,4},{12,16},{16,12},{20,24},{24,20},{28,0},{1,29},{... | collective-permute-start | bytes 589832 | tf_op jit(solution)/shard_map/ppermute | solution.py:353
  146.1 18.2 %collective-permute-start.43 = (f32[24,16,128]{2,1,0:T(8,128)S(1)}, f32[24,16,128]{2,1,0:T(8,128)S(1)}, u32[]{:S(2)}, u32[]{:S(2)}) collective-permute-start(f32[24,16,128]{2,1,0:T(8,128)S(1)} %get-tuple-element.203.refs_3_), channel_id=1, source_target_pairs={{0,4},{4,0},{8,12},{12,8},{16,20},{20,16},{24,28},{28,24},{1,5},{5... | collective-permute-start | bytes 589832 | tf_op jit(solution)/shard_map/ppermute | solution.py:353
  146.3 18.0 %collective-permute-start.44 = (f32[24,16,128]{2,1,0:T(8,128)S(1)}, f32[24,16,128]{2,1,0:T(8,128)S(1)}, u32[]{:S(2)}, u32[]{:S(2)}) collective-permute-start(f32[24,16,128]{2,1,0:T(8,128)S(1)} %get-tuple-element.204.refs_4_), channel_id=1, source_target_pairs={{0,28},{4,8},{8,4},{12,16},{16,12},{20,24},{24,20},{28,0},{1,29},{... | collective-permute-start | bytes 589832 | tf_op jit(solution)/shard_map/ppermute | solution.py:353
  160.2 10.6 %collective-permute-start.40 = (f32[24,16,128]{2,1,0:T(8,128)S(1)}, f32[24,16,128]{2,1,0:T(8,128)S(1)}, u32[]{:S(2)}, u32[]{:S(2)}) collective-permute-start(f32[24,16,128]{2,1,0:T(8,128)S(1)} %get-tuple-element.209.refs_9_.refs_3_), channel_id=1, source_target_pairs={{0,4},{4,0},{8,12},{12,8},{16,20},{20,16},{24,28},{28,24},{1,5},{5... | collective-permute-start | bytes 589832 | tf_op jit(solution)/shard_map/ppermute | solution.py:353
  162.9 10.1 %collective-permute-start.41 = (f32[24,16,128]{2,1,0:T(8,128)S(1)}, f32[24,16,128]{2,1,0:T(8,128)S(1)}, u32[]{:S(2)}, u32[]{:S(2)}) collective-permute-start(f32[24,16,128]{2,1,0:T(8,128)S(1)} %get-tuple-element.210.refs_10_.refs_4_), channel_id=1, source_target_pairs={{0,28},{4,8},{8,4},{12,16},{16,12},{20,24},{24,20},{28,0},{1,29},{... | collective-permute-start | bytes 589832 | tf_op jit(solution)/shard_map/ppermute | solution.py:353
  170.2 9.9 %collective-permute-start.47 = (f32[12,32,128]{2,1,0:T(8,128)S(1)}, f32[12,32,128]{2,1,0:T(8,128)S(1)}, u32[]{:S(2)}, u32[]{:S(2)}) collective-permute-start(f32[12,32,128]{2,1,0:T(8,128)S(1)} %get-tuple-element.223), channel_id=1, source_target_pairs={{0,3},{1,2},{2,1},{3,0},{4,7},{5,6},{6,5},{7,4},{8,11},{9,10},{10,... | collective-permute-start | bytes 589832 | tf_op jit(solution)/shard_map/ppermute | solution.py:357
  170.8 18.7 %collective-permute-start.50 = (f32[24,16,128]{2,1,0:T(8,128)S(1)}, f32[24,16,128]{2,1,0:T(8,128)S(1)}, u32[]{:S(2)}, u32[]{:S(2)}) collective-permute-start(f32[24,16,128]{2,1,0:T(8,128)S(1)} %get-tuple-element.225.refs_3_), channel_id=1, source_target_pairs={{0,4},{4,0},{8,12},{12,8},{16,20},{20,16},{24,28},{28,24},{1,5},{5... | collective-permute-start | bytes 589832 | tf_op jit(solution)/shard_map/ppermute | solution.py:353
  173.1 16.5 %collective-permute-start.51 = (f32[24,16,128]{2,1,0:T(8,128)S(1)}, f32[24,16,128]{2,1,0:T(8,128)S(1)}, u32[]{:S(2)}, u32[]{:S(2)}) collective-permute-start(f32[24,16,128]{2,1,0:T(8,128)S(1)} %get-tuple-element.226.refs_4_), channel_id=1, source_target_pairs={{0,28},{4,8},{8,4},{12,16},{16,12},{20,24},{24,20},{28,0},{1,29},{... | collective-permute-start | bytes 589832 | tf_op jit(solution)/shard_map/ppermute | solution.py:353
  195.0 11.3 %collective-permute-start.56 = (f32[12,32,128]{2,1,0:T(8,128)S(1)}, f32[12,32,128]{2,1,0:T(8,128)S(1)}, u32[]{:S(2)}, u32[]{:S(2)}) collective-permute-start(f32[12,32,128]{2,1,0:T(8,128)S(1)} %get-tuple-element.244), channel_id=1, source_target_pairs={{0,2},{1,3},{2,0},{3,1},{4,6},{5,7},{6,4},{7,5},{8,10},{9,11},{10,... | collective-permute-start | bytes 589832 | tf_op jit(solution)/shard_map/ppermute | solution.py:357
  195.9 11.6 %collective-permute-start.57 = (f32[12,32,128]{2,1,0:T(8,128)S(1)}, f32[12,32,128]{2,1,0:T(8,128)S(1)}, u32[]{:S(2)}, u32[]{:S(2)}) collective-permute-start(f32[12,32,128]{2,1,0:T(8,128)S(1)} %get-tuple-element.245), channel_id=1, source_target_pairs={{0,3},{1,2},{2,1},{3,0},{4,7},{5,6},{6,5},{7,4},{8,11},{9,10},{10,... | collective-permute-start | bytes 589832 | tf_op jit(solution)/shard_map/ppermute | solution.py:357
  203.1 10.0 %collective-permute-start.63 = (f32[128,128]{1,0:T(8,128)S(1)}, f32[128,128]{1,0:T(8,128)S(1)}, u32[]{:S(2)}, u32[]{:S(2)}) collective-permute-start(f32[128,128]{1,0:T(8,128)S(1)} %cross.1), channel_id=1, source_target_pairs={{0,24},{4,28},{8,16},{12,20},{16,8},{20,12},{24,0},{28,4},{1,25},{... | collective-permute-start | bytes 196616 | tf_op jit(solution)/shard_map/ppermute | solution.py:357
  204.4 16.1 %collective-permute-start.62 = (f32[128,128]{1,0:T(8,128)S(1)}, f32[128,128]{1,0:T(8,128)S(1)}, u32[]{:S(2)}, u32[]{:S(2)}) collective-permute-start(f32[128,128]{1,0:T(8,128)S(1)} %cross.1), channel_id=1, source_target_pairs={{0,16},{4,20},{8,24},{12,28},{16,0},{20,4},{24,8},{28,12},{1,17},{... | collective-permute-start | bytes 196616 | tf_op jit(solution)/shard_map/ppermute | solution.py:357
  206.3 14.1 %collective-permute-start.61 = (f32[128,128]{1,0:T(8,128)S(1)}, f32[128,128]{1,0:T(8,128)S(1)}, u32[]{:S(2)}, u32[]{:S(2)}) collective-permute-start(f32[128,128]{1,0:T(8,128)S(1)} %cross.1), channel_id=1, source_target_pairs={{0,8},{4,12},{8,0},{12,4},{16,24},{20,28},{24,16},{28,20},{1,9},{5... | collective-permute-start | bytes 196616 | tf_op jit(solution)/shard_map/ppermute | solution.py:357
  210.5 9.9 %collective-permute-start.60 = (f32[128,128]{1,0:T(8,128)S(1)}, f32[128,128]{1,0:T(8,128)S(1)}, u32[]{:S(2)}, u32[]{:S(2)}) collective-permute-start(f32[128,128]{1,0:T(8,128)S(1)} %turn_cross.1), channel_id=1, source_target_pairs={{0,24},{4,28},{8,16},{12,20},{16,8},{20,12},{24,0},{28,4},{1,25},{... | collective-permute-start | bytes 196616 | tf_op jit(solution)/shard_map/ppermute | solution.py:357
  223.5 10.1 %collective-permute-start.71 = (f32[12,32,128]{2,1,0:T(8,128)S(1)}, f32[12,32,128]{2,1,0:T(8,128)S(1)}, u32[]{:S(2)}, u32[]{:S(2)}) collective-permute-start(f32[12,32,128]{2,1,0:T(8,128)S(1)} %get-tuple-element.267), channel_id=1, source_target_pairs={{0,3},{1,2},{2,1},{3,0},{4,7},{5,6},{6,5},{7,4},{8,11},{9,10},{10,... | collective-permute-start | bytes 589832 | tf_op jit(solution)/shard_map/ppermute | solution.py:357
  (25 other events, 166.3 us)

commit v12 on v11

--- a/solution.py
+++ b/solution.py
@@ -430,7 +430,7 @@
                 old, image = lax.optimization_barrier((old, image))
             if got is not None:
                 gram = gram + got
-            got = swap(gram, *hops.pop(0)) if hops else None
+            got = swap(gram, *hops.pop(0)) if hops and (step, i) != (1, 1) else None
             mate = after[0] if i == 1 and step == DEGREE - 2 else ()
             done, parts = apply(meta, now[i], exchange(now[i]), old, mate, count)
             after.append(done)

time: 236 us -> 234 us (level)
  waiting for transfers between devices: 25.9 us -> 21.8 us
    ppermute x18, starting transfers between devices: 16.4 us -> 11.3 us  [exchange(): lax.ppermute(pair[0], 'node', even)]
    ppermute x36, starting transfers between devices: 29.3 us -> 33.8 us  [swap(): lax.ppermute(value, axis, [(i, i ^ hop) for i in range(lax.axis_size(axis...]
    ppermute x36, waiting for transfers between devices: 23.4 us -> 19.6 us  [swap(): lax.ppermute(value, axis, [(i, i ^ hop) for i in range(lax.axis_size(axis...]
  transfers between devices with their start and end apart: 72 -> 72, of which waited for: 12 -> 13; matrix products, arithmetic and copies ran while one was open for 0% -> 0% of each run, Pallas kernels for 45% -> 45%
where the time goes in v12:
time: 234 us; the launch traced here: 233 us
  Pallas kernels  107 us (46%)
  starting transfers between devices  101 us (43%)
  waiting for transfers between devices  21.8 us (9%)
    pallas_call x18, Pallas kernels, apply(): pl.pallas_call(functools.partial(apply_kernel, bool(old), bool(mate)), in...  78.2 us
    ppermute x18, starting transfers between devices, exchange(): lax.ppermute(pair[1], 'node', odd)  56.4 us
    ppermute x36, starting transfers between devices, swap(): lax.ppermute(value, axis, [(i, i ^ hop) for i in range(lax.axis_size(axis...  33.8 us
    pallas_call x10, Pallas kernels, call(): pl.pallas_call(kernel, in_specs=[IN_SMEM] * scalars + [IN_VMEM] * (len(ar...  20.1 us
    ppermute x36, waiting for transfers between devices, swap(): lax.ppermute(value, axis, [(i, i ^ hop) for i in range(lax.axis_size(axis...  19.6 us
    ppermute x18, starting transfers between devices, exchange(): lax.ppermute(pair[0], 'node', even)  11.3 us
    pallas_call x1, Pallas kernels, prep(): pl.pallas_call(functools.partial(prep_kernel, rows, groups), in_specs=[IN...  8.32 us
  transfers between devices with their start and end apart: 72, of which 13 were waited for; matrix products, arithmetic and copies ran while one was open for 0% of the time, Pallas kernels for 45%

profile of v12, /device:TPU:0, one launch (start us, length us, event | category | flops | bytes accessed | tf_op | source)
XLA Modules:
  0.0 233.1 jit_solution(11816035574407260366)
XLA Ops:
  2.5 3.0 %collective-permute-start = (f32[24,16,128]{2,1,0:T(8,128)S(1)}, f32[24,16,128]{2,1,0:T(8,128)S(1)}, u32[]{:S(2)}, u32[]{:S(2)}) collective-permute-start(f32[24,16,128]{2,1,0:T(8,128)S(1)} %get-tuple-element.140.refs_3_.refs_7_), channel_id=1, source_target_pairs={{0,4},{4,0},{8,12},{12,8},{16,20},{20,16},{24,28},{28,24},{1,5},{5... | collective-permute-start | bytes 589832 | tf_op jit(solution)/shard_map/ppermute | solution.py:353
  5.5 3.5 %collective-permute-start.1 = (f32[24,16,128]{2,1,0:T(8,128)S(1)}, f32[24,16,128]{2,1,0:T(8,128)S(1)}, u32[]{:S(2)}, u32[]{:S(2)}) collective-permute-start(f32[24,16,128]{2,1,0:T(8,128)S(1)} %get-tuple-element.141.refs_4_.refs_8_), channel_id=1, source_target_pairs={{0,28},{4,8},{8,4},{12,16},{16,12},{20,24},{24,20},{28,0},{1,29},{... | collective-permute-start | bytes 589832 | tf_op jit(solution)/shard_map/ppermute | solution.py:353
  11.0 8.3 %prep.1 = (bf16[288,128,256]{2,1,0:T(8,128)(2,1)S(1)}, f32[48,1,128]{2,1,0:T(1,128)S(1)}, s32[578]{0:T(1024)S(1)}) custom-call(s32[2]{0:T(128)S(1)} %pad_add_fusion.ids_ref, s32[1,288]{1,0:T(1,128)} %own_ref.1, s32[1,288]{1,0:T(1,128)} %col_ref.1, f32[288,128,128]{2,1,0:T(8,128)} %blk_ref.1), custom_call_target="tpu_custom_call" | custom-call | flops 1207959552 | bytes 18874368 | tf_op jit(solution)/shard_map/prep/pallas_call | solution.py:120
  19.3 4.2 %apply.4 = (f32[24,16,128]{2,1,0:T(8,128)S(1)}, f32[24,16,128]{2,1,0:T(8,128)S(1)}) custom-call(s32[578]{0:T(1024)S(1)} %get-tuple-element.137.refs_0_, bf16[288,128,256]{2,1,0:T(8,128)(2,1)S(1)} %get-tuple-element.138.refs_1_, f32[48,1,128]{2,1,0:T(1,128)S(1)} %get-tuple-element.139.refs_2_, f32[24,16,128]{2,1,0:T(8,128)S(1)} %get-tuple-element.140.refs_3_.refs_7_, ...), custom_call_target="tpu_custom_call" | custom-call | bytes 4194304 | tf_op jit(solution)/shard_map/apply/pallas_call | solution.py:199
  23.6 2.5 %collective-permute-start.2 = (f32[24,16,128]{2,1,0:T(8,128)S(1)}, f32[24,16,128]{2,1,0:T(8,128)S(1)}, u32[]{:S(2)}, u32[]{:S(2)}) collective-permute-start(f32[24,16,128]{2,1,0:T(8,128)S(1)} %get-tuple-element.142.refs_3_.refs_7_), channel_id=1, source_target_pairs={{0,4},{4,0},{8,12},{12,8},{16,20},{20,16},{24,28},{28,24},{1,5},{5... | collective-permute-start | bytes 589832 | tf_op jit(solution)/shard_map/ppermute | solution.py:353
  26.1 3.6 %collective-permute-start.3 = (f32[24,16,128]{2,1,0:T(8,128)S(1)}, f32[24,16,128]{2,1,0:T(8,128)S(1)}, u32[]{:S(2)}, u32[]{:S(2)}) collective-permute-start(f32[24,16,128]{2,1,0:T(8,128)S(1)} %get-tuple-element.143.refs_4_.refs_8_), channel_id=1, source_target_pairs={{0,28},{4,8},{8,4},{12,16},{16,12},{20,24},{24,20},{28,0},{1,29},{... | collective-permute-start | bytes 589832 | tf_op jit(solution)/shard_map/ppermute | solution.py:353
  29.6 4.2 %apply.6 = (f32[24,16,128]{2,1,0:T(8,128)S(1)}, f32[24,16,128]{2,1,0:T(8,128)S(1)}) custom-call(s32[578]{0:T(1024)S(1)} %get-tuple-element.137.refs_0_, bf16[288,128,256]{2,1,0:T(8,128)(2,1)S(1)} %get-tuple-element.138.refs_1_, f32[48,1,128]{2,1,0:T(1,128)S(1)} %get-tuple-element.139.refs_2_, f32[24,16,128]{2,1,0:T(8,128)S(1)} %get-tuple-element.152.refs_3_.refs_7_, ...), custom_call_target="tpu_custom_call" | custom-call | bytes 4194304 | tf_op jit(solution)/shard_map/apply/pallas_call | solution.py:199
  35.9 4.3 %apply_recur.10 = (f32[24,16,128]{2,1,0:T(8,128)S(1)}, f32[24,16,128]{2,1,0:T(8,128)S(1)}) custom-call(s32[578]{0:T(1024)S(1)} %get-tuple-element.137.refs_0_, bf16[288,128,256]{2,1,0:T(8,128)(2,1)S(1)} %get-tuple-element.138.refs_1_, f32[48,1,128]{2,1,0:T(1,128)S(1)} %get-tuple-element.139.refs_2_, f32[24,16,128]{2,1,0:T(8,128)S(1)} %get-tuple-element.142.refs_3_.refs_7_, ...), custom_call_target="tpu_custom_call" | custom-call | bytes 4194304 | tf_op jit(solution)/shard_map/apply_recur/pallas_call | solution.py:199
  40.8 8.2 %collective-permute-start.5 = (f32[24,16,128]{2,1,0:T(8,128)S(1)}, f32[24,16,128]{2,1,0:T(8,128)S(1)}, u32[]{:S(2)}, u32[]{:S(2)}) collective-permute-start(f32[24,16,128]{2,1,0:T(8,128)S(1)} %get-tuple-element.145.refs_4_.refs_8_), channel_id=1, source_target_pairs={{0,28},{4,8},{8,4},{12,16},{16,12},{20,24},{24,20},{28,0},{1,29},{... | collective-permute-start | bytes 589832 | tf_op jit(solution)/shard_map/ppermute | solution.py:353
  49.0 4.3 %apply_recur.13 = (f32[24,16,128]{2,1,0:T(8,128)S(1)}, f32[24,16,128]{2,1,0:T(8,128)S(1)}) custom-call(s32[578]{0:T(1024)S(1)} %get-tuple-element.137.refs_0_, bf16[288,128,256]{2,1,0:T(8,128)(2,1)S(1)} %get-tuple-element.138.refs_1_, f32[48,1,128]{2,1,0:T(1,128)S(1)} %get-tuple-element.139.refs_2_, f32[24,16,128]{2,1,0:T(8,128)S(1)} %get-tuple-element.154.refs_3_.refs_7_, ...), custom_call_target="tpu_custom_call" | custom-call | bytes 4194304 | tf_op jit(solution)/shard_map/apply_recur/pallas_call | solution.py:199
  53.4 2.0 collective-permute-start.17
  55.3 4.2 %apply_recur.11 = (f32[24,16,128]{2,1,0:T(8,128)S(1)}, f32[24,16,128]{2,1,0:T(8,128)S(1)}) custom-call(s32[578]{0:T(1024)S(1)} %get-tuple-element.137.refs_0_, bf16[288,128,256]{2,1,0:T(8,128)(2,1)S(1)} %get-tuple-element.138.refs_1_, f32[48,1,128]{2,1,0:T(1,128)S(1)} %get-tuple-element.139.refs_2_, f32[24,16,128]{2,1,0:T(8,128)S(1)} %get-tuple-element.144.refs_3_.refs_7_, ...), custom_call_target="tpu_custom_call" | custom-call | bytes 4194304 | tf_op jit(solution)/shard_map/apply_recur/pallas_call | solution.py:199
  59.7 2.9 %collective-permute-start.7 = (f32[24,16,128]{2,1,0:T(8,128)S(1)}, f32[24,16,128]{2,1,0:T(8,128)S(1)}, u32[]{:S(2)}, u32[]{:S(2)}) collective-permute-start(f32[24,16,128]{2,1,0:T(8,128)S(1)} %get-tuple-element.147.refs_4_), channel_id=1, source_target_pairs={{0,28},{4,8},{8,4},{12,16},{16,12},{20,24},{24,20},{28,0},{1,29},{... | collective-permute-start | bytes 589832 | tf_op jit(solution)/shard_map/ppermute | solution.py:353
  62.6 4.3 %apply_recur.14 = (f32[24,16,128]{2,1,0:T(8,128)S(1)}, f32[24,16,128]{2,1,0:T(8,128)S(1)}) custom-call(s32[578]{0:T(1024)S(1)} %get-tuple-element.137.refs_0_, bf16[288,128,256]{2,1,0:T(8,128)(2,1)S(1)} %get-tuple-element.138.refs_1_, f32[48,1,128]{2,1,0:T(1,128)S(1)} %get-tuple-element.139.refs_2_, f32[24,16,128]{2,1,0:T(8,128)S(1)} %get-tuple-element.156.refs_3_.refs_7_, ...), custom_call_target="tpu_custom_call" | custom-call | bytes 4194304 | tf_op jit(solution)/shard_map/apply_recur/pallas_call | solution.py:199
  68.0 4.9 %collective-permute-start.19 = (f32[24,16,128]{2,1,0:T(8,128)S(1)}, f32[24,16,128]{2,1,0:T(8,128)S(1)}, u32[]{:S(2)}, u32[]{:S(2)}) collective-permute-start(f32[24,16,128]{2,1,0:T(8,128)S(1)} %get-tuple-element.159.refs_4_), channel_id=1, source_target_pairs={{0,28},{4,8},{8,4},{12,16},{16,12},{20,24},{24,20},{28,0},{1,29},{... | collective-permute-start | bytes 589832 | tf_op jit(solution)/shard_map/ppermute | solution.py:353
  72.9 4.2 %apply_recur.12 = (f32[24,16,128]{2,1,0:T(8,128)S(1)}, f32[24,16,128]{2,1,0:T(8,128)S(1)}) custom-call(s32[578]{0:T(1024)S(1)} %get-tuple-element.137.refs_0_, bf16[288,128,256]{2,1,0:T(8,128)(2,1)S(1)} %get-tuple-element.138.refs_1_, f32[48,1,128]{2,1,0:T(1,128)S(1)} %get-tuple-element.139.refs_2_, f32[24,16,128]{2,1,0:T(8,128)S(1)} %get-tuple-element.146.refs_3_, ...), custom_call_target="tpu_custom_call" | custom-call | bytes 4194304 | tf_op jit(solution)/shard_map/apply_recur/pallas_call | solution.py:199
  77.3 2.0 collective-permute-start.9
  79.2 4.4 %apply_recur_parts.2 = (f32[24,16,128]{2,1,0:T(8,128)S(1)}, f32[24,16,128]{2,1,0:T(8,128)S(1)}, f32[12,32,128]{2,1,0:T(8,128)S(1)}, f32[12,32,128]{2,1,0:T(8,128...) custom-call(s32[578]{0:T(1024)S(1)} %get-tuple-element.137.refs_0_, ...), custom_call_target="tpu_custom_call" | custom-call | bytes 4194304 | tf_op jit(solution)/shard_map/apply_recur_parts/pallas_call | solution.py:199
  84.5 8.7 %collective-permute-start.28 = (f32[24,16,128]{2,1,0:T(8,128)S(1)}, f32[24,16,128]{2,1,0:T(8,128)S(1)}, u32[]{:S(2)}, u32[]{:S(2)}) collective-permute-start(f32[24,16,128]{2,1,0:T(8,128)S(1)} %get-tuple-element.179.refs_4_.refs_8_), channel_id=1, source_target_pairs={{0,28},{4,8},{8,4},{12,16},{16,12},{20,24},{24,20},{28,0},{1,29},{... | collective-permute-start | bytes 589832 | tf_op jit(solution)/shard_map/ppermute | solution.py:353
  95.1 4.2 %apply.5 = (f32[24,16,128]{2,1,0:T(8,128)S(1)}, f32[24,16,128]{2,1,0:T(8,128)S(1)}) custom-call(s32[578]{0:T(1024)S(1)} %get-tuple-element.137.refs_0_, bf16[288,128,256]{2,1,0:T(8,128)(2,1)S(1)} %get-tuple-element.138.refs_1_, f32[48,1,128]{2,1,0:T(1,128)S(1)} %get-tuple-element.139.refs_2_, f32[24,16,128]{2,1,0:T(8,128)S(1)} %get-tuple-element.165.refs_3_.refs_9_.refs_7_, ...), custom_call_target="tpu_custom_call" | custom-call | bytes 4194304 | tf_op jit(solution)/shard_map/apply/pallas_call | solution.py:199
  99.5 2.2 collective-permute-start.11
  101.6 4.5 %apply_parts.2 = (f32[24,16,128]{2,1,0:T(8,128)S(1)}, f32[24,16,128]{2,1,0:T(8,128)S(1)}, f32[12,32,128]{2,1,0:T(8,128)S(1)}, f32[12,32,128]{2,1,0:T(8,128)S(1)}...) custom-call(s32[578]{0:T(1024)S(1)} %get-tuple-element.137.refs_0_, ...), custom_call_target="tpu_custom_call" | custom-call | bytes 4194304 | tf_op jit(solution)/shard_map/apply_parts/pallas_call | solution.py:199
  107.7 2.7 %collective-permute-start.30 = (f32[24,16,128]{2,1,0:T(8,128)S(1)}, f32[24,16,128]{2,1,0:T(8,128)S(1)}, u32[]{:S(2)}, u32[]{:S(2)}) collective-permute-start(f32[24,16,128]{2,1,0:T(8,128)S(1)} %get-tuple-element.210.refs_4_.refs_8_), channel_id=1, source_target_pairs={{0,28},{4,8},{8,4},{12,16},{16,12},{20,24},{24,20},{28,0},{1,29},{... | collective-permute-start | bytes 589832 | tf_op jit(solution)/shard_map/ppermute | solution.py:353
  111.4 4.3 %apply_recur.15 = (f32[24,16,128]{2,1,0:T(8,128)S(1)}, f32[24,16,128]{2,1,0:T(8,128)S(1)}) custom-call(s32[578]{0:T(1024)S(1)} %get-tuple-element.137.refs_0_, bf16[288,128,256]{2,1,0:T(8,128)(2,1)S(1)} %get-tuple-element.138.refs_1_, f32[48,1,128]{2,1,0:T(1,128)S(1)} %get-tuple-element.139.refs_2_, f32[24,16,128]{2,1,0:T(8,128)S(1)} %get-tuple-element.184.refs_3_.refs_7_, ...), custom_call_target="tpu_custom_call" | custom-call | bytes 4194304 | tf_op jit(solution)/shard_map/apply_recur/pallas_call | solution.py:199
  120.9 4.2 %apply_recur.16 = (f32[24,16,128]{2,1,0:T(8,128)S(1)}, f32[24,16,128]{2,1,0:T(8,128)S(1)}) custom-call(s32[578]{0:T(1024)S(1)} %get-tuple-element.137.refs_0_, bf16[288,128,256]{2,1,0:T(8,128)(2,1)S(1)} %get-tuple-element.138.refs_1_, f32[48,1,128]{2,1,0:T(1,128)S(1)} %get-tuple-element.139.refs_2_, f32[24,16,128]{2,1,0:T(8,128)S(1)} %get-tuple-element.209.refs_3_.refs_7_, ...), custom_call_target="tpu_custom_call" | custom-call | bytes 4194304 | tf_op jit(solution)/shard_map/apply_recur/pallas_call | solution.py:199
  127.6 2.4 %collective-permute-start.39 = (f32[24,16,128]{2,1,0:T(8,128)S(1)}, f32[24,16,128]{2,1,0:T(8,128)S(1)}, u32[]{:S(2)}, u32[]{:S(2)}) collective-permute-start(f32[24,16,128]{2,1,0:T(8,128)S(1)} %get-tuple-element.214.refs_4_.refs_8_), channel_id=1, source_target_pairs={{0,28},{4,8},{8,4},{12,16},{16,12},{20,24},{24,20},{28,0},{1,29},{... | collective-permute-start | bytes 589832 | tf_op jit(solution)/shard_map/ppermute | solution.py:353
  130.2 4.3 %apply_recur.17 = (f32[24,16,128]{2,1,0:T(8,128)S(1)}, f32[24,16,128]{2,1,0:T(8,128)S(1)}) custom-call(s32[578]{0:T(1024)S(1)} %get-tuple-element.137.refs_0_, bf16[288,128,256]{2,1,0:T(8,128)(2,1)S(1)} %get-tuple-element.138.refs_1_, f32[48,1,128]{2,1,0:T(1,128)S(1)} %get-tuple-element.139.refs_2_, f32[24,16,128]{2,1,0:T(8,128)S(1)} %get-tuple-element.194.refs_3_.refs_7_, ...), custom_call_target="tpu_custom_call" | custom-call | bytes 4194304 | tf_op jit(solution)/shard_map/apply_recur/pallas_call | solution.py:199
  134.5 2.0 collective-permute-start.31
  136.5 3.1 %collective-permute-done.33 = f32[128,128]{1,0:T(8,128)S(1)} collective-permute-done((f32[128,128]{1,0:T(8,128)S(1)}, f32[128,128]{1,0:T(8,128)S(1)}, u32[]{:S(2)}, u32[]{:S(2)}) %collective-permute-start.33) | collective-permute-done | bytes 65568 | tf_op jit(solution)/shard_map/ppermute | solution.py:357
  139.6 2.8 %collective-permute-start.32 = (f32[24,16,128]{2,1,0:T(8,128)S(1)}, f32[24,16,128]{2,1,0:T(8,128)S(1)}, u32[]{:S(2)}, u32[]{:S(2)}) collective-permute-start(f32[24,16,128]{2,1,0:T(8,128)S(1)} %get-tuple-element.187.refs_4_), channel_id=1, source_target_pairs={{0,28},{4,8},{8,4},{12,16},{16,12},{20,24},{24,20},{28,0},{1,29},{... | collective-permute-start | bytes 589832 | tf_op jit(solution)/shard_map/ppermute | solution.py:353
  142.3 4.3 %apply_recur.19 = (f32[24,16,128]{2,1,0:T(8,128)S(1)}, f32[24,16,128]{2,1,0:T(8,128)S(1)}) custom-call(s32[578]{0:T(1024)S(1)} %get-tuple-element.137.refs_0_, bf16[288,128,256]{2,1,0:T(8,128)(2,1)S(1)} %get-tuple-element.138.refs_1_, f32[48,1,128]{2,1,0:T(1,128)S(1)} %get-tuple-element.139.refs_2_, f32[24,16,128]{2,1,0:T(8,128)S(1)} %get-tuple-element.213.refs_3_.refs_7_, ...), custom_call_target="tpu_custom_call" | custom-call | bytes 4194304 | tf_op jit(solution)/shard_map/apply_recur/pallas_call | solution.py:199
  146.7 2.0 collective-permute-start.44
  150.2 4.2 %apply_recur.18 = (f32[24,16,128]{2,1,0:T(8,128)S(1)}, f32[24,16,128]{2,1,0:T(8,128)S(1)}) custom-call(s32[578]{0:T(1024)S(1)} %get-tuple-element.137.refs_0_, bf16[288,128,256]{2,1,0:T(8,128)(2,1)S(1)} %get-tuple-element.138.refs_1_, f32[48,1,128]{2,1,0:T(1,128)S(1)} %get-tuple-element.139.refs_2_, f32[24,16,128]{2,1,0:T(8,128)S(1)} %get-tuple-element.186.refs_3_, ...), custom_call_target="tpu_custom_call" | custom-call | bytes 4194304 | tf_op jit(solution)/shard_map/apply_recur/pallas_call | solution.py:199
  154.6 4.0 %collective-permute-start.37 = (f32[128,128]{1,0:T(8,128)S(1)}, f32[128,128]{1,0:T(8,128)S(1)}, u32[]{:S(2)}, u32[]{:S(2)}) collective-permute-start(f32[128,128]{1,0:T(8,128)S(1)} %add.66), channel_id=1, source_target_pairs={{0,16},{4,20},{8,24},{12,28},{16,0},{20,4},{24,8},{28,12},{1,17},{... | collective-permute-start | bytes 196616 | tf_op jit(solution)/shard_map/ppermute | solution.py:357
  159.7 4.6 %apply_recur_parts.3 = (f32[24,16,128]{2,1,0:T(8,128)S(1)}, f32[24,16,128]{2,1,0:T(8,128)S(1)}, f32[12,32,128]{2,1,0:T(8,128)S(1)}, f32[12,32,128]{2,1,0:T(8,128...) custom-call(s32[578]{0:T(1024)S(1)} %get-tuple-element.137.refs_0_, ...), custom_call_target="tpu_custom_call" | custom-call | bytes 4194304 | tf_op jit(solution)/shard_map/apply_recur_parts/pallas_call | solution.py:199
  164.3 3.4 %collective-permute-start.46 = (f32[12,32,128]{2,1,0:T(8,128)S(1)}, f32[12,32,128]{2,1,0:T(8,128)S(1)}, u32[]{:S(2)}, u32[]{:S(2)}) collective-permute-start(f32[12,32,128]{2,1,0:T(8,128)S(1)} %get-tuple-element.222), channel_id=1, source_target_pairs={{0,2},{1,3},{2,0},{3,1},{4,6},{5,7},{6,4},{7,5},{8,10},{9,11},{10,... | collective-permute-start | bytes 589832 | tf_op jit(solution)/shard_map/ppermute | solution.py:357
  167.8 2.1 collective-permute-start.51
  169.9 4.1 %factor.2.inv_ref.refs_0_ = f32[128,128]{1,0:T(8,128)S(1)} custom-call(f32[128,128]{1,0:T(8,128)S(1)} %add.67.g_ref), custom_call_target="tpu_custom_call" | custom-call | tf_op jit(solution)/shard_map/factor/pallas_call | solution.py:42
  174.0 3.1 %collective-permute-done.47.refs_3_ = f32[12,32,128]{2,1,0:T(8,128)S(1)} collective-permute-done((f32[12,32,128]{2,1,0:T(8,128)S(1)}, f32[12,32,128]{2,1,0:T(8,128)S(1)}, u32[]{:S(2)}, u32[]{:S(2)}) %collective-permute-start.47) | collective-permute-done | bytes 196640 | tf_op jit(solution)/shard_map/ppermute | solution.py:357
  177.2 2.5 %turn.1 = (f32[12,128,128]{2,1,0:T(8,128)S(1)}, f32[128,128]{1,0:T(8,128)S(1)}) custom-call(s32[2]{0:T(128)S(1)} %pad_add_fusion.ids_ref, f32[128,128]{1,0:T(8,128)S(1)} %factor.2.inv_ref.refs_0_, f32[12,32,128]{2,1,0:T(8,128)S(1)} %get-tuple-element.220.refs_0_, f32[12,32,128]{2,1,0:T(8,128)S(1)} %collective-permute-done.45.refs_1_, ...), custom_call_target="tpu_custom_call" | custom-call | tf_op jit(solution)/shard_map/turn/pallas_call | solution.py:42
  182.8 4.2 %apply.7 = (f32[24,16,128]{2,1,0:T(8,128)S(1)}, f32[24,16,128]{2,1,0:T(8,128)S(1)}) custom-call(s32[578]{0:T(1024)S(1)} %get-tuple-element.137.refs_0_, bf16[288,128,256]{2,1,0:T(8,128)(2,1)S(1)} %get-tuple-element.138.refs_1_, f32[48,1,128]{2,1,0:T(1,128)S(1)} %get-tuple-element.139.refs_2_, f32[24,16,128]{2,1,0:T(8,128)S(1)} %get-tuple-element.196.refs_9_.refs_3_, ...), custom_call_target="tpu_custom_call" | custom-call | bytes 4194304 | tf_op jit(solution)/shard_map/apply/pallas_call | solution.py:199
  187.2 5.3 %apply_parts.3 = (f32[24,16,128]{2,1,0:T(8,128)}, f32[24,16,128]{2,1,0:T(8,128)}, f32[12,32,128]{2,1,0:T(8,128)S(1)}, f32[12,32,128]{2,1,0:T(8,128)S(1)}, f32[12...) custom-call(s32[578]{0:T(1024)S(1)} %get-tuple-element.137.refs_0_, ...), custom_call_target="tpu_custom_call" | custom-call | bytes 4194304 | tf_op jit(solution)/shard_map/apply_parts/pallas_call | solution.py:199
  195.9 2.9 %collective-permute-done.53 = f32[128,128]{1,0:T(8,128)S(1)} collective-permute-done((f32[128,128]{1,0:T(8,128)S(1)}, f32[128,128]{1,0:T(8,128)S(1)}, u32[]{:S(2)}, u32[]{:S(2)}) %collective-permute-start.53) | collective-permute-done | bytes 65568 | tf_op jit(solution)/shard_map/ppermute | solution.py:357
  199.4 2.1 collective-permute-start.63
  205.6 2.3 collective-permute-done.54
  209.8 2.6 %collective-permute-start.58 = (f32[128,128]{1,0:T(8,128)S(1)}, f32[128,128]{1,0:T(8,128)S(1)}, u32[]{:S(2)}, u32[]{:S(2)}) collective-permute-start(f32[128,128]{1,0:T(8,128)S(1)} %turn_cross.1), channel_id=1, source_target_pairs={{0,8},{4,12},{8,0},{12,4},{16,24},{20,28},{24,16},{28,20},{1,9},{5... | collective-permute-start | bytes 196616 | tf_op jit(solution)/shard_map/ppermute | solution.py:357
  212.3 4.1 %factor.3.inv_ref.refs_2_ = f32[128,128]{1,0:T(8,128)S(1)} custom-call(f32[128,128]{1,0:T(8,128)S(1)} %add.72.g_ref), custom_call_target="tpu_custom_call" | custom-call | tf_op jit(solution)/shard_map/factor/pallas_call | solution.py:42
  222.2 3.7 %collective-permute-done.64 = f32[128,128]{1,0:T(8,128)S(1)} collective-permute-done((f32[128,128]{1,0:T(8,128)S(1)}, f32[128,128]{1,0:T(8,128)S(1)}, u32[]{:S(2)}, u32[]{:S(2)}) %collective-permute-start.64) | collective-permute-done | bytes 65568 | tf_op jit(solution)/shard_map/ppermute | solution.py:357
  (144 shorter events, 50.1 us)
Async XLA Ops:
  2.5 16.8 %collective-permute-start = (f32[24,16,128]{2,1,0:T(8,128)S(1)}, f32[24,16,128]{2,1,0:T(8,128)S(1)}, u32[]{:S(2)}, u32[]{:S(2)}) collective-permute-start(f32[24,16,128]{2,1,0:T(8,128)S(1)} %get-tuple-element.140.refs_3_.refs_7_), channel_id=1, source_target_pairs={{0,4},{4,0},{8,12},{12,8},{16,20},{20,16},{24,28},{28,24},{1,5},{5... | collective-permute-start | bytes 589832 | tf_op jit(solution)/shard_map/ppermute | solution.py:353
  5.5 13.8 %collective-permute-start.1 = (f32[24,16,128]{2,1,0:T(8,128)S(1)}, f32[24,16,128]{2,1,0:T(8,128)S(1)}, u32[]{:S(2)}, u32[]{:S(2)}) collective-permute-start(f32[24,16,128]{2,1,0:T(8,128)S(1)} %get-tuple-element.141.refs_4_.refs_8_), channel_id=1, source_target_pairs={{0,28},{4,8},{8,4},{12,16},{16,12},{20,24},{24,20},{28,0},{1,29},{... | collective-permute-start | bytes 589832 | tf_op jit(solution)/shard_map/ppermute | solution.py:353
  9.1 20.5 %collective-permute-start.12 = (f32[24,16,128]{2,1,0:T(8,128)S(1)}, f32[24,16,128]{2,1,0:T(8,128)S(1)}, u32[]{:S(2)}, u32[]{:S(2)}) collective-permute-start(f32[24,16,128]{2,1,0:T(8,128)S(1)} %get-tuple-element.152.refs_3_.refs_7_), channel_id=1, source_target_pairs={{0,4},{4,0},{8,12},{12,8},{16,20},{20,16},{24,28},{28,24},{1,5},{5... | collective-permute-start | bytes 589832 | tf_op jit(solution)/shard_map/ppermute | solution.py:353
  9.1 20.5 %collective-permute-start.13 = (f32[24,16,128]{2,1,0:T(8,128)S(1)}, f32[24,16,128]{2,1,0:T(8,128)S(1)}, u32[]{:S(2)}, u32[]{:S(2)}) collective-permute-start(f32[24,16,128]{2,1,0:T(8,128)S(1)} %get-tuple-element.153.refs_4_.refs_8_), channel_id=1, source_target_pairs={{0,28},{4,8},{8,4},{12,16},{16,12},{20,24},{24,20},{28,0},{1,29},{... | collective-permute-start | bytes 589832 | tf_op jit(solution)/shard_map/ppermute | solution.py:353
  23.6 12.3 %collective-permute-start.2 = (f32[24,16,128]{2,1,0:T(8,128)S(1)}, f32[24,16,128]{2,1,0:T(8,128)S(1)}, u32[]{:S(2)}, u32[]{:S(2)}) collective-permute-start(f32[24,16,128]{2,1,0:T(8,128)S(1)} %get-tuple-element.142.refs_3_.refs_7_), channel_id=1, source_target_pairs={{0,4},{4,0},{8,12},{12,8},{16,20},{20,16},{24,28},{28,24},{1,5},{5... | collective-permute-start | bytes 589832 | tf_op jit(solution)/shard_map/ppermute | solution.py:353
  26.1 9.8 %collective-permute-start.3 = (f32[24,16,128]{2,1,0:T(8,128)S(1)}, f32[24,16,128]{2,1,0:T(8,128)S(1)}, u32[]{:S(2)}, u32[]{:S(2)}) collective-permute-start(f32[24,16,128]{2,1,0:T(8,128)S(1)} %get-tuple-element.143.refs_4_.refs_8_), channel_id=1, source_target_pairs={{0,28},{4,8},{8,4},{12,16},{16,12},{20,24},{24,20},{28,0},{1,29},{... | collective-permute-start | bytes 589832 | tf_op jit(solution)/shard_map/ppermute | solution.py:353
  33.9 15.1 %collective-permute-start.14 = (f32[24,16,128]{2,1,0:T(8,128)S(1)}, f32[24,16,128]{2,1,0:T(8,128)S(1)}, u32[]{:S(2)}, u32[]{:S(2)}) collective-permute-start(f32[24,16,128]{2,1,0:T(8,128)S(1)} %get-tuple-element.154.refs_3_.refs_7_), channel_id=1, source_target_pairs={{0,4},{4,0},{8,12},{12,8},{16,20},{20,16},{24,28},{28,24},{1,5},{5... | collective-permute-start | bytes 589832 | tf_op jit(solution)/shard_map/ppermute | solution.py:353
  33.9 15.1 %collective-permute-start.15 = (f32[24,16,128]{2,1,0:T(8,128)S(1)}, f32[24,16,128]{2,1,0:T(8,128)S(1)}, u32[]{:S(2)}, u32[]{:S(2)}) collective-permute-start(f32[24,16,128]{2,1,0:T(8,128)S(1)} %get-tuple-element.155.refs_4_.refs_8_), channel_id=1, source_target_pairs={{0,28},{4,8},{8,4},{12,16},{16,12},{20,24},{24,20},{28,0},{1,29},{... | collective-permute-start | bytes 589832 | tf_op jit(solution)/shard_map/ppermute | solution.py:353
  40.1 15.2 %collective-permute-start.4 = (f32[24,16,128]{2,1,0:T(8,128)S(1)}, f32[24,16,128]{2,1,0:T(8,128)S(1)}, u32[]{:S(2)}, u32[]{:S(2)}) collective-permute-start(f32[24,16,128]{2,1,0:T(8,128)S(1)} %get-tuple-element.144.refs_3_.refs_7_), channel_id=1, source_target_pairs={{0,4},{4,0},{8,12},{12,8},{16,20},{20,16},{24,28},{28,24},{1,5},{5... | collective-permute-start | bytes 589832 | tf_op jit(solution)/shard_map/ppermute | solution.py:353
  40.8 14.5 %collective-permute-start.5 = (f32[24,16,128]{2,1,0:T(8,128)S(1)}, f32[24,16,128]{2,1,0:T(8,128)S(1)}, u32[]{:S(2)}, u32[]{:S(2)}) collective-permute-start(f32[24,16,128]{2,1,0:T(8,128)S(1)} %get-tuple-element.145.refs_4_.refs_8_), channel_id=1, source_target_pairs={{0,28},{4,8},{8,4},{12,16},{16,12},{20,24},{24,20},{28,0},{1,29},{... | collective-permute-start | bytes 589832 | tf_op jit(solution)/shard_map/ppermute | solution.py:353
  59.6 13.3 %collective-permute-start.6 = (f32[24,16,128]{2,1,0:T(8,128)S(1)}, f32[24,16,128]{2,1,0:T(8,128)S(1)}, u32[]{:S(2)}, u32[]{:S(2)}) collective-permute-start(f32[24,16,128]{2,1,0:T(8,128)S(1)} %get-tuple-element.146.refs_3_), channel_id=1, source_target_pairs={{0,4},{4,0},{8,12},{12,8},{16,20},{20,16},{24,28},{28,24},{1,5},{5... | collective-permute-start | bytes 589832 | tf_op jit(solution)/shard_map/ppermute | solution.py:353
  59.7 13.2 %collective-permute-start.7 = (f32[24,16,128]{2,1,0:T(8,128)S(1)}, f32[24,16,128]{2,1,0:T(8,128)S(1)}, u32[]{:S(2)}, u32[]{:S(2)}) collective-permute-start(f32[24,16,128]{2,1,0:T(8,128)S(1)} %get-tuple-element.147.refs_4_), channel_id=1, source_target_pairs={{0,28},{4,8},{8,4},{12,16},{16,12},{20,24},{24,20},{28,0},{1,29},{... | collective-permute-start | bytes 589832 | tf_op jit(solution)/shard_map/ppermute | solution.py:353
  66.9 12.3 %collective-permute-start.18 = (f32[24,16,128]{2,1,0:T(8,128)S(1)}, f32[24,16,128]{2,1,0:T(8,128)S(1)}, u32[]{:S(2)}, u32[]{:S(2)}) collective-permute-start(f32[24,16,128]{2,1,0:T(8,128)S(1)} %get-tuple-element.158.refs_3_), channel_id=1, source_target_pairs={{0,4},{4,0},{8,12},{12,8},{16,20},{20,16},{24,28},{28,24},{1,5},{5... | collective-permute-start | bytes 589832 | tf_op jit(solution)/shard_map/ppermute | solution.py:353
  68.0 11.2 %collective-permute-start.19 = (f32[24,16,128]{2,1,0:T(8,128)S(1)}, f32[24,16,128]{2,1,0:T(8,128)S(1)}, u32[]{:S(2)}, u32[]{:S(2)}) collective-permute-start(f32[24,16,128]{2,1,0:T(8,128)S(1)} %get-tuple-element.159.refs_4_), channel_id=1, source_target_pairs={{0,28},{4,8},{8,4},{12,16},{16,12},{20,24},{24,20},{28,0},{1,29},{... | collective-permute-start | bytes 589832 | tf_op jit(solution)/shard_map/ppermute | solution.py:353
  77.2 16.1 %collective-permute-start.8 = (f32[24,16,128]{2,1,0:T(8,128)S(1)}, f32[24,16,128]{2,1,0:T(8,128)S(1)}, u32[]{:S(2)}, u32[]{:S(2)}) collective-permute-start(f32[24,16,128]{2,1,0:T(8,128)S(1)} %get-tuple-element.165.refs_3_.refs_9_.refs_7_), channel_id=1, source_target_pairs={{0,4},{4,0},{8,12},{12,8},{16,20},{20,16},{24,28},{28,24},{1,5},{5... | collective-permute-start | bytes 589832 | tf_op jit(solution)/shard_map/ppermute | solution.py:353
  77.3 17.5 %collective-permute-start.9 = (f32[24,16,128]{2,1,0:T(8,128)S(1)}, f32[24,16,128]{2,1,0:T(8,128)S(1)}, u32[]{:S(2)}, u32[]{:S(2)}) collective-permute-start(f32[24,16,128]{2,1,0:T(8,128)S(1)} %get-tuple-element.166.refs_4_.refs_10_.refs_8_), channel_id=1, source_target_pairs={{0,28},{4,8},{8,4},{12,16},{16,12},{20,24},{24,20},{28,0},{1,29},{... | collective-permute-start | bytes 589832 | tf_op jit(solution)/shard_map/ppermute | solution.py:353
  83.6 15.8 %collective-permute-start.27 = (f32[24,16,128]{2,1,0:T(8,128)S(1)}, f32[24,16,128]{2,1,0:T(8,128)S(1)}, u32[]{:S(2)}, u32[]{:S(2)}) collective-permute-start(f32[24,16,128]{2,1,0:T(8,128)S(1)} %get-tuple-element.178.refs_3_.refs_7_), channel_id=1, source_target_pairs={{0,4},{4,0},{8,12},{12,8},{16,20},{20,16},{24,28},{28,24},{1,5},{5... | collective-permute-start | bytes 589832 | tf_op jit(solution)/shard_map/ppermute | solution.py:353
  84.5 14.9 %collective-permute-start.28 = (f32[24,16,128]{2,1,0:T(8,128)S(1)}, f32[24,16,128]{2,1,0:T(8,128)S(1)}, u32[]{:S(2)}, u32[]{:S(2)}) collective-permute-start(f32[24,16,128]{2,1,0:T(8,128)S(1)} %get-tuple-element.179.refs_4_.refs_8_), channel_id=1, source_target_pairs={{0,28},{4,8},{8,4},{12,16},{16,12},{20,24},{24,20},{28,0},{1,29},{... | collective-permute-start | bytes 589832 | tf_op jit(solution)/shard_map/ppermute | solution.py:353
  93.2 12.9 %collective-permute-start.20 = (f32[12,32,128]{2,1,0:T(8,128)S(1)}, f32[12,32,128]{2,1,0:T(8,128)S(1)}, u32[]{:S(2)}, u32[]{:S(2)}) collective-permute-start(f32[12,32,128]{2,1,0:T(8,128)S(1)} %get-tuple-element.161), channel_id=1, source_target_pairs={{0,1},{1,0},{2,3},{3,2},{4,5},{5,4},{6,7},{7,6},{8,9},{9,8},{10,11... | collective-permute-start | bytes 589832 | tf_op jit(solution)/shard_map/ppermute | solution.py:357
  93.2 13.0 %collective-permute-start.21 = (f32[12,32,128]{2,1,0:T(8,128)S(1)}, f32[12,32,128]{2,1,0:T(8,128)S(1)}, u32[]{:S(2)}, u32[]{:S(2)}) collective-permute-start(f32[12,32,128]{2,1,0:T(8,128)S(1)} %get-tuple-element.162), channel_id=1, source_target_pairs={{0,2},{1,3},{2,0},{3,1},{4,6},{5,7},{6,4},{7,5},{8,10},{9,11},{10,... | collective-permute-start | bytes 589832 | tf_op jit(solution)/shard_map/ppermute | solution.py:357
  94.7 11.6 %collective-permute-start.22 = (f32[12,32,128]{2,1,0:T(8,128)S(1)}, f32[12,32,128]{2,1,0:T(8,128)S(1)}, u32[]{:S(2)}, u32[]{:S(2)}) collective-permute-start(f32[12,32,128]{2,1,0:T(8,128)S(1)} %get-tuple-element.163), channel_id=1, source_target_pairs={{0,3},{1,2},{2,1},{3,0},{4,7},{5,6},{6,5},{7,4},{8,11},{9,10},{10,... | collective-permute-start | bytes 589832 | tf_op jit(solution)/shard_map/ppermute | solution.py:357
  99.4 12.0 %collective-permute-start.10 = (f32[24,16,128]{2,1,0:T(8,128)S(1)}, f32[24,16,128]{2,1,0:T(8,128)S(1)}, u32[]{:S(2)}, u32[]{:S(2)}) collective-permute-start(f32[24,16,128]{2,1,0:T(8,128)S(1)} %get-tuple-element.184.refs_3_.refs_7_), channel_id=1, source_target_pairs={{0,4},{4,0},{8,12},{12,8},{16,20},{20,16},{24,28},{28,24},{1,5},{5... | collective-permute-start | bytes 589832 | tf_op jit(solution)/shard_map/ppermute | solution.py:353
  99.5 11.9 %collective-permute-start.11 = (f32[24,16,128]{2,1,0:T(8,128)S(1)}, f32[24,16,128]{2,1,0:T(8,128)S(1)}, u32[]{:S(2)}, u32[]{:S(2)}) collective-permute-start(f32[24,16,128]{2,1,0:T(8,128)S(1)} %get-tuple-element.185.refs_4_.refs_8_), channel_id=1, source_target_pairs={{0,28},{4,8},{8,4},{12,16},{16,12},{20,24},{24,20},{28,0},{1,29},{... | collective-permute-start | bytes 589832 | tf_op jit(solution)/shard_map/ppermute | solution.py:353
  106.1 11.2 %collective-permute-start.40 = (f32[12,32,128]{2,1,0:T(8,128)S(1)}, f32[12,32,128]{2,1,0:T(8,128)S(1)}, u32[]{:S(2)}, u32[]{:S(2)}) collective-permute-start(f32[12,32,128]{2,1,0:T(8,128)S(1)} %get-tuple-element.206), channel_id=1, source_target_pairs={{0,1},{1,0},{2,3},{3,2},{4,5},{5,4},{6,7},{7,6},{8,9},{9,8},{10,11... | collective-permute-start | bytes 589832 | tf_op jit(solution)/shard_map/ppermute | solution.py:357
  106.2 13.2 %collective-permute-start.29 = (f32[24,16,128]{2,1,0:T(8,128)S(1)}, f32[24,16,128]{2,1,0:T(8,128)S(1)}, u32[]{:S(2)}, u32[]{:S(2)}) collective-permute-start(f32[24,16,128]{2,1,0:T(8,128)S(1)} %get-tuple-element.209.refs_3_.refs_7_), channel_id=1, source_target_pairs={{0,4},{4,0},{8,12},{12,8},{16,20},{20,16},{24,28},{28,24},{1,5},{5... | collective-permute-start | bytes 589832 | tf_op jit(solution)/shard_map/ppermute | solution.py:353
  107.7 13.2 %collective-permute-start.30 = (f32[24,16,128]{2,1,0:T(8,128)S(1)}, f32[24,16,128]{2,1,0:T(8,128)S(1)}, u32[]{:S(2)}, u32[]{:S(2)}) collective-permute-start(f32[24,16,128]{2,1,0:T(8,128)S(1)} %get-tuple-element.210.refs_4_.refs_8_), channel_id=1, source_target_pairs={{0,28},{4,8},{8,4},{12,16},{16,12},{20,24},{24,20},{28,0},{1,29},{... | collective-permute-start | bytes 589832 | tf_op jit(solution)/shard_map/ppermute | solution.py:353
  115.7 11.9 %collective-permute-start.23 = (f32[24,16,128]{2,1,0:T(8,128)S(1)}, f32[24,16,128]{2,1,0:T(8,128)S(1)}, u32[]{:S(2)}, u32[]{:S(2)}) collective-permute-start(f32[24,16,128]{2,1,0:T(8,128)S(1)} %get-tuple-element.194.refs_3_.refs_7_), channel_id=1, source_target_pairs={{0,4},{4,0},{8,12},{12,8},{16,20},{20,16},{24,28},{28,24},{1,5},{5... | collective-permute-start | bytes 589832 | tf_op jit(solution)/shard_map/ppermute | solution.py:353
  115.7 14.3 %collective-permute-start.24 = (f32[24,16,128]{2,1,0:T(8,128)S(1)}, f32[24,16,128]{2,1,0:T(8,128)S(1)}, u32[]{:S(2)}, u32[]{:S(2)}) collective-permute-start(f32[24,16,128]{2,1,0:T(8,128)S(1)} %get-tuple-element.195.refs_4_.refs_8_), channel_id=1, source_target_pairs={{0,28},{4,8},{8,4},{12,16},{16,12},{20,24},{24,20},{28,0},{1,29},{... | collective-permute-start | bytes 589832 | tf_op jit(solution)/shard_map/ppermute | solution.py:353
  117.3 17.2 %collective-permute-start.41 = (f32[12,32,128]{2,1,0:T(8,128)S(1)}, f32[12,32,128]{2,1,0:T(8,128)S(1)}, u32[]{:S(2)}, u32[]{:S(2)}) collective-permute-start(f32[12,32,128]{2,1,0:T(8,128)S(1)} %get-tuple-element.207), channel_id=1, source_target_pairs={{0,2},{1,3},{2,0},{3,1},{4,6},{5,7},{6,4},{7,5},{8,10},{9,11},{10,... | collective-permute-start | bytes 589832 | tf_op jit(solution)/shard_map/ppermute | solution.py:357
  120.9 21.4 %collective-permute-start.42 = (f32[12,32,128]{2,1,0:T(8,128)S(1)}, f32[12,32,128]{2,1,0:T(8,128)S(1)}, u32[]{:S(2)}, u32[]{:S(2)}) collective-permute-start(f32[12,32,128]{2,1,0:T(8,128)S(1)} %get-tuple-element.208), channel_id=1, source_target_pairs={{0,3},{1,2},{2,1},{3,0},{4,7},{5,6},{6,5},{7,4},{8,11},{9,10},{10,... | collective-permute-start | bytes 589832 | tf_op jit(solution)/shard_map/ppermute | solution.py:357
  126.5 15.8 %collective-permute-start.38 = (f32[24,16,128]{2,1,0:T(8,128)S(1)}, f32[24,16,128]{2,1,0:T(8,128)S(1)}, u32[]{:S(2)}, u32[]{:S(2)}) collective-permute-start(f32[24,16,128]{2,1,0:T(8,128)S(1)} %get-tuple-element.213.refs_3_.refs_7_), channel_id=1, source_target_pairs={{0,4},{4,0},{8,12},{12,8},{16,20},{20,16},{24,28},{28,24},{1,5},{5... | collective-permute-start | bytes 589832 | tf_op jit(solution)/shard_map/ppermute | solution.py:353
  127.6 14.7 %collective-permute-start.39 = (f32[24,16,128]{2,1,0:T(8,128)S(1)}, f32[24,16,128]{2,1,0:T(8,128)S(1)}, u32[]{:S(2)}, u32[]{:S(2)}) collective-permute-start(f32[24,16,128]{2,1,0:T(8,128)S(1)} %get-tuple-element.214.refs_4_.refs_8_), channel_id=1, source_target_pairs={{0,28},{4,8},{8,4},{12,16},{16,12},{20,24},{24,20},{28,0},{1,29},{... | collective-permute-start | bytes 589832 | tf_op jit(solution)/shard_map/ppermute | solution.py:353
  134.5 15.7 %collective-permute-start.31 = (f32[24,16,128]{2,1,0:T(8,128)S(1)}, f32[24,16,128]{2,1,0:T(8,128)S(1)}, u32[]{:S(2)}, u32[]{:S(2)}) collective-permute-start(f32[24,16,128]{2,1,0:T(8,128)S(1)} %get-tuple-element.186.refs_3_), channel_id=1, source_target_pairs={{0,4},{4,0},{8,12},{12,8},{16,20},{20,16},{24,28},{28,24},{1,5},{5... | collective-permute-start | bytes 589832 | tf_op jit(solution)/shard_map/ppermute | solution.py:353
  139.6 10.7 %collective-permute-start.32 = (f32[24,16,128]{2,1,0:T(8,128)S(1)}, f32[24,16,128]{2,1,0:T(8,128)S(1)}, u32[]{:S(2)}, u32[]{:S(2)}) collective-permute-start(f32[24,16,128]{2,1,0:T(8,128)S(1)} %get-tuple-element.187.refs_4_), channel_id=1, source_target_pairs={{0,28},{4,8},{8,4},{12,16},{16,12},{20,24},{24,20},{28,0},{1,29},{... | collective-permute-start | bytes 589832 | tf_op jit(solution)/shard_map/ppermute | solution.py:353
  146.6 13.1 %collective-permute-start.43 = (f32[24,16,128]{2,1,0:T(8,128)S(1)}, f32[24,16,128]{2,1,0:T(8,128)S(1)}, u32[]{:S(2)}, u32[]{:S(2)}) collective-permute-start(f32[24,16,128]{2,1,0:T(8,128)S(1)} %get-tuple-element.211.refs_3_), channel_id=1, source_target_pairs={{0,4},{4,0},{8,12},{12,8},{16,20},{20,16},{24,28},{28,24},{1,5},{5... | collective-permute-start | bytes 589832 | tf_op jit(solution)/shard_map/ppermute | solution.py:353
  146.7 13.0 %collective-permute-start.44 = (f32[24,16,128]{2,1,0:T(8,128)S(1)}, f32[24,16,128]{2,1,0:T(8,128)S(1)}, u32[]{:S(2)}, u32[]{:S(2)}) collective-permute-start(f32[24,16,128]{2,1,0:T(8,128)S(1)} %get-tuple-element.212.refs_4_), channel_id=1, source_target_pairs={{0,28},{4,8},{8,4},{12,16},{16,12},{20,24},{24,20},{28,0},{1,29},{... | collective-permute-start | bytes 589832 | tf_op jit(solution)/shard_map/ppermute | solution.py:353
  154.6 13.2 %collective-permute-start.37 = (f32[128,128]{1,0:T(8,128)S(1)}, f32[128,128]{1,0:T(8,128)S(1)}, u32[]{:S(2)}, u32[]{:S(2)}) collective-permute-start(f32[128,128]{1,0:T(8,128)S(1)} %add.66), channel_id=1, source_target_pairs={{0,16},{4,20},{8,24},{12,28},{16,0},{20,4},{24,8},{28,12},{1,17},{... | collective-permute-start | bytes 196616 | tf_op jit(solution)/shard_map/ppermute | solution.py:357
  164.3 9.8 %collective-permute-start.45 = (f32[12,32,128]{2,1,0:T(8,128)S(1)}, f32[12,32,128]{2,1,0:T(8,128)S(1)}, u32[]{:S(2)}, u32[]{:S(2)}) collective-permute-start(f32[12,32,128]{2,1,0:T(8,128)S(1)} %get-tuple-element.221), channel_id=1, source_target_pairs={{0,1},{1,0},{2,3},{3,2},{4,5},{5,4},{6,7},{7,6},{8,9},{9,8},{10,11... | collective-permute-start | bytes 589832 | tf_op jit(solution)/shard_map/ppermute | solution.py:357
  164.3 9.7 %collective-permute-start.46 = (f32[12,32,128]{2,1,0:T(8,128)S(1)}, f32[12,32,128]{2,1,0:T(8,128)S(1)}, u32[]{:S(2)}, u32[]{:S(2)}) collective-permute-start(f32[12,32,128]{2,1,0:T(8,128)S(1)} %get-tuple-element.222), channel_id=1, source_target_pairs={{0,2},{1,3},{2,0},{3,1},{4,6},{5,7},{6,4},{7,5},{8,10},{9,11},{10,... | collective-permute-start | bytes 589832 | tf_op jit(solution)/shard_map/ppermute | solution.py:357
  167.8 19.3 %collective-permute-start.50 = (f32[24,16,128]{2,1,0:T(8,128)S(1)}, f32[24,16,128]{2,1,0:T(8,128)S(1)}, u32[]{:S(2)}, u32[]{:S(2)}) collective-permute-start(f32[24,16,128]{2,1,0:T(8,128)S(1)} %get-tuple-element.215.refs_3_), channel_id=1, source_target_pairs={{0,4},{4,0},{8,12},{12,8},{16,20},{20,16},{24,28},{28,24},{1,5},{5... | collective-permute-start | bytes 589832 | tf_op jit(solution)/shard_map/ppermute | solution.py:353
  167.8 19.2 %collective-permute-start.51 = (f32[24,16,128]{2,1,0:T(8,128)S(1)}, f32[24,16,128]{2,1,0:T(8,128)S(1)}, u32[]{:S(2)}, u32[]{:S(2)}) collective-permute-start(f32[24,16,128]{2,1,0:T(8,128)S(1)} %get-tuple-element.216.refs_4_), channel_id=1, source_target_pairs={{0,28},{4,8},{8,4},{12,16},{16,12},{20,24},{24,20},{28,0},{1,29},{... | collective-permute-start | bytes 589832 | tf_op jit(solution)/shard_map/ppermute | solution.py:353
  192.6 9.8 %collective-permute-start.56 = (f32[12,32,128]{2,1,0:T(8,128)S(1)}, f32[12,32,128]{2,1,0:T(8,128)S(1)}, u32[]{:S(2)}, u32[]{:S(2)}) collective-permute-start(f32[12,32,128]{2,1,0:T(8,128)S(1)} %get-tuple-element.242), channel_id=1, source_target_pairs={{0,2},{1,3},{2,0},{3,1},{4,6},{5,7},{6,4},{7,5},{8,10},{9,11},{10,... | collective-permute-start | bytes 589832 | tf_op jit(solution)/shard_map/ppermute | solution.py:357
  192.9 10.9 %collective-permute-start.57 = (f32[12,32,128]{2,1,0:T(8,128)S(1)}, f32[12,32,128]{2,1,0:T(8,128)S(1)}, u32[]{:S(2)}, u32[]{:S(2)}) collective-permute-start(f32[12,32,128]{2,1,0:T(8,128)S(1)} %get-tuple-element.243), channel_id=1, source_target_pairs={{0,3},{1,2},{2,1},{3,0},{4,7},{5,6},{6,5},{7,4},{8,11},{9,10},{10,... | collective-permute-start | bytes 589832 | tf_op jit(solution)/shard_map/ppermute | solution.py:357
  199.4 10.4 %collective-permute-start.63 = (f32[128,128]{1,0:T(8,128)S(1)}, f32[128,128]{1,0:T(8,128)S(1)}, u32[]{:S(2)}, u32[]{:S(2)}) collective-permute-start(f32[128,128]{1,0:T(8,128)S(1)} %cross.1), channel_id=1, source_target_pairs={{0,24},{4,28},{8,16},{12,20},{16,8},{20,12},{24,0},{28,4},{1,25},{... | collective-permute-start | bytes 196616 | tf_op jit(solution)/shard_map/ppermute | solution.py:357
  201.5 16.3 %collective-permute-start.62 = (f32[128,128]{1,0:T(8,128)S(1)}, f32[128,128]{1,0:T(8,128)S(1)}, u32[]{:S(2)}, u32[]{:S(2)}) collective-permute-start(f32[128,128]{1,0:T(8,128)S(1)} %cross.1), channel_id=1, source_target_pairs={{0,16},{4,20},{8,24},{12,28},{16,0},{20,4},{24,8},{28,12},{1,17},{... | collective-permute-start | bytes 196616 | tf_op jit(solution)/shard_map/ppermute | solution.py:357
  202.4 15.5 %collective-permute-start.61 = (f32[128,128]{1,0:T(8,128)S(1)}, f32[128,128]{1,0:T(8,128)S(1)}, u32[]{:S(2)}, u32[]{:S(2)}) collective-permute-start(f32[128,128]{1,0:T(8,128)S(1)} %cross.1), channel_id=1, source_target_pairs={{0,8},{4,12},{8,0},{12,4},{16,24},{20,28},{24,16},{28,20},{1,9},{5... | collective-permute-start | bytes 196616 | tf_op jit(solution)/shard_map/ppermute | solution.py:357
  207.9 9.9 %collective-permute-start.60 = (f32[128,128]{1,0:T(8,128)S(1)}, f32[128,128]{1,0:T(8,128)S(1)}, u32[]{:S(2)}, u32[]{:S(2)}) collective-permute-start(f32[128,128]{1,0:T(8,128)S(1)} %turn_cross.1), channel_id=1, source_target_pairs={{0,24},{4,28},{8,16},{12,20},{16,8},{20,12},{24,0},{28,4},{1,25},{... | collective-permute-start | bytes 196616 | tf_op jit(solution)/shard_map/ppermute | solution.py:357
  220.1 10.7 %collective-permute-start.71 = (f32[12,32,128]{2,1,0:T(8,128)S(1)}, f32[12,32,128]{2,1,0:T(8,128)S(1)}, u32[]{:S(2)}, u32[]{:S(2)}) collective-permute-start(f32[12,32,128]{2,1,0:T(8,128)S(1)} %get-tuple-element.265), channel_id=1, source_target_pairs={{0,3},{1,2},{2,1},{3,0},{4,7},{5,6},{6,5},{7,4},{8,11},{9,10},{10,... | collective-permute-start | bytes 589832 | tf_op jit(solution)/shard_map/ppermute | solution.py:357
  (25 other events, 169.2 us)

commit v13 on v12

--- a/solution.py
+++ b/solution.py
@@ -462,7 +462,7 @@
                 turn_cross_kernel, "turn_cross", [square], ids, inverse_first, turned, gram_last,
                 *swapped(parts), scalars=1, scratch=[held],
             )
-        if i == len(hops) - 2:
+        if i == len(hops) - 3:
             got, image_first = lax.optimization_barrier((got, image_first))
         if i == len(hops) - 1:
             got, image_last = lax.optimization_barrier((got, image_last))

time: 234 us -> 235 us (level)
  starting transfers between devices: 101 us -> 105 us
    ppermute x36, starting transfers between devices: 33.8 us -> 36.4 us  [swap(): lax.ppermute(value, axis, [(i, i ^ hop) for i in range(lax.axis_size(axis...]
  transfers between devices with their start and end apart: 72 -> 72, of which waited for: 13 -> 12; matrix products, arithmetic and copies ran while one was open for 0% -> 0% of each run, Pallas kernels for 45% -> 45%
where the time goes in v13:
time: 235 us
  Pallas kernels  107 us (46%)
  starting transfers between devices  105 us (45%)
  waiting for transfers between devices  20 us (9%)
    pallas_call x18, Pallas kernels, apply(): pl.pallas_call(functools.partial(apply_kernel, bool(old), bool(mate)), in...  78.1 us
    ppermute x18, starting transfers between devices, exchange(): lax.ppermute(pair[1], 'node', odd)  57.4 us
    ppermute x36, starting transfers between devices, swap(): lax.ppermute(value, axis, [(i, i ^ hop) for i in range(lax.axis_size(axis...  36.4 us
    pallas_call x10, Pallas kernels, call(): pl.pallas_call(kernel, in_specs=[IN_SMEM] * scalars + [IN_VMEM] * (len(ar...  20.1 us
    ppermute x36, waiting for transfers between devices, swap(): lax.ppermute(value, axis, [(i, i ^ hop) for i in range(lax.axis_size(axis...  17.7 us
    ppermute x18, starting transfers between devices, exchange(): lax.ppermute(pair[0], 'node', even)  11.4 us
    pallas_call x1, Pallas kernels, prep(): pl.pallas_call(functools.partial(prep_kernel, rows, groups), in_specs=[IN...  8.31 us
  transfers between devices with their start and end apart: 72, of which 12 were waited for; matrix products, arithmetic and copies ran while one was open for 0% of the time, Pallas kernels for 45%

profile of v13, /device:TPU:0, one launch (start us, length us, event | category | flops | bytes accessed | tf_op | source)
XLA Modules:
  0.0 234.8 jit_solution(1514618830000766639)
XLA Ops:
  2.5 3.0 %collective-permute-start = (f32[24,16,128]{2,1,0:T(8,128)S(1)}, f32[24,16,128]{2,1,0:T(8,128)S(1)}, u32[]{:S(2)}, u32[]{:S(2)}) collective-permute-start(f32[24,16,128]{2,1,0:T(8,128)S(1)} %get-tuple-element.140.refs_3_.refs_7_), channel_id=1, source_target_pairs={{0,4},{4,0},{8,12},{12,8},{16,20},{20,16},{24,28},{28,24},{1,5},{5... | collective-permute-start | bytes 589832 | tf_op jit(solution)/shard_map/ppermute | solution.py:353
  5.5 3.5 %collective-permute-start.1 = (f32[24,16,128]{2,1,0:T(8,128)S(1)}, f32[24,16,128]{2,1,0:T(8,128)S(1)}, u32[]{:S(2)}, u32[]{:S(2)}) collective-permute-start(f32[24,16,128]{2,1,0:T(8,128)S(1)} %get-tuple-element.141.refs_4_.refs_8_), channel_id=1, source_target_pairs={{0,28},{4,8},{8,4},{12,16},{16,12},{20,24},{24,20},{28,0},{1,29},{... | collective-permute-start | bytes 589832 | tf_op jit(solution)/shard_map/ppermute | solution.py:353
  11.0 8.3 %prep.1 = (bf16[288,128,256]{2,1,0:T(8,128)(2,1)S(1)}, f32[48,1,128]{2,1,0:T(1,128)S(1)}, s32[578]{0:T(1024)S(1)}) custom-call(s32[2]{0:T(128)S(1)} %pad_add_fusion.ids_ref, s32[1,288]{1,0:T(1,128)} %own_ref.1, s32[1,288]{1,0:T(1,128)} %col_ref.1, f32[288,128,128]{2,1,0:T(8,128)} %blk_ref.1), custom_call_target="tpu_custom_call" | custom-call | flops 1207959552 | bytes 18874368 | tf_op jit(solution)/shard_map/prep/pallas_call | solution.py:120
  19.3 4.2 %apply.4 = (f32[24,16,128]{2,1,0:T(8,128)S(1)}, f32[24,16,128]{2,1,0:T(8,128)S(1)}) custom-call(s32[578]{0:T(1024)S(1)} %get-tuple-element.137.refs_0_, bf16[288,128,256]{2,1,0:T(8,128)(2,1)S(1)} %get-tuple-element.138.refs_1_, f32[48,1,128]{2,1,0:T(1,128)S(1)} %get-tuple-element.139.refs_2_, f32[24,16,128]{2,1,0:T(8,128)S(1)} %get-tuple-element.140.refs_3_.refs_7_, ...), custom_call_target="tpu_custom_call" | custom-call | bytes 4194304 | tf_op jit(solution)/shard_map/apply/pallas_call | solution.py:199
  23.6 2.5 %collective-permute-start.2 = (f32[24,16,128]{2,1,0:T(8,128)S(1)}, f32[24,16,128]{2,1,0:T(8,128)S(1)}, u32[]{:S(2)}, u32[]{:S(2)}) collective-permute-start(f32[24,16,128]{2,1,0:T(8,128)S(1)} %get-tuple-element.142.refs_3_.refs_7_), channel_id=1, source_target_pairs={{0,4},{4,0},{8,12},{12,8},{16,20},{20,16},{24,28},{28,24},{1,5},{5... | collective-permute-start | bytes 589832 | tf_op jit(solution)/shard_map/ppermute | solution.py:353
  26.1 3.6 %collective-permute-start.3 = (f32[24,16,128]{2,1,0:T(8,128)S(1)}, f32[24,16,128]{2,1,0:T(8,128)S(1)}, u32[]{:S(2)}, u32[]{:S(2)}) collective-permute-start(f32[24,16,128]{2,1,0:T(8,128)S(1)} %get-tuple-element.143.refs_4_.refs_8_), channel_id=1, source_target_pairs={{0,28},{4,8},{8,4},{12,16},{16,12},{20,24},{24,20},{28,0},{1,29},{... | collective-permute-start | bytes 589832 | tf_op jit(solution)/shard_map/ppermute | solution.py:353
  29.6 4.2 %apply.6 = (f32[24,16,128]{2,1,0:T(8,128)S(1)}, f32[24,16,128]{2,1,0:T(8,128)S(1)}) custom-call(s32[578]{0:T(1024)S(1)} %get-tuple-element.137.refs_0_, bf16[288,128,256]{2,1,0:T(8,128)(2,1)S(1)} %get-tuple-element.138.refs_1_, f32[48,1,128]{2,1,0:T(1,128)S(1)} %get-tuple-element.139.refs_2_, f32[24,16,128]{2,1,0:T(8,128)S(1)} %get-tuple-element.152.refs_3_.refs_7_, ...), custom_call_target="tpu_custom_call" | custom-call | bytes 4194304 | tf_op jit(solution)/shard_map/apply/pallas_call | solution.py:199
  35.9 4.3 %apply_recur.10 = (f32[24,16,128]{2,1,0:T(8,128)S(1)}, f32[24,16,128]{2,1,0:T(8,128)S(1)}) custom-call(s32[578]{0:T(1024)S(1)} %get-tuple-element.137.refs_0_, bf16[288,128,256]{2,1,0:T(8,128)(2,1)S(1)} %get-tuple-element.138.refs_1_, f32[48,1,128]{2,1,0:T(1,128)S(1)} %get-tuple-element.139.refs_2_, f32[24,16,128]{2,1,0:T(8,128)S(1)} %get-tuple-element.142.refs_3_.refs_7_, ...), custom_call_target="tpu_custom_call" | custom-call | bytes 4194304 | tf_op jit(solution)/shard_map/apply_recur/pallas_call | solution.py:199
  40.8 8.2 %collective-permute-start.5 = (f32[24,16,128]{2,1,0:T(8,128)S(1)}, f32[24,16,128]{2,1,0:T(8,128)S(1)}, u32[]{:S(2)}, u32[]{:S(2)}) collective-permute-start(f32[24,16,128]{2,1,0:T(8,128)S(1)} %get-tuple-element.145.refs_4_.refs_8_), channel_id=1, source_target_pairs={{0,28},{4,8},{8,4},{12,16},{16,12},{20,24},{24,20},{28,0},{1,29},{... | collective-permute-start | bytes 589832 | tf_op jit(solution)/shard_map/ppermute | solution.py:353
  49.0 4.3 %apply_recur.13 = (f32[24,16,128]{2,1,0:T(8,128)S(1)}, f32[24,16,128]{2,1,0:T(8,128)S(1)}) custom-call(s32[578]{0:T(1024)S(1)} %get-tuple-element.137.refs_0_, bf16[288,128,256]{2,1,0:T(8,128)(2,1)S(1)} %get-tuple-element.138.refs_1_, f32[48,1,128]{2,1,0:T(1,128)S(1)} %get-tuple-element.139.refs_2_, f32[24,16,128]{2,1,0:T(8,128)S(1)} %get-tuple-element.154.refs_3_.refs_7_, ...), custom_call_target="tpu_custom_call" | custom-call | bytes 4194304 | tf_op jit(solution)/shard_map/apply_recur/pallas_call | solution.py:199
  53.4 2.0 collective-permute-start.17
  55.3 4.2 %apply_recur.11 = (f32[24,16,128]{2,1,0:T(8,128)S(1)}, f32[24,16,128]{2,1,0:T(8,128)S(1)}) custom-call(s32[578]{0:T(1024)S(1)} %get-tuple-element.137.refs_0_, bf16[288,128,256]{2,1,0:T(8,128)(2,1)S(1)} %get-tuple-element.138.refs_1_, f32[48,1,128]{2,1,0:T(1,128)S(1)} %get-tuple-element.139.refs_2_, f32[24,16,128]{2,1,0:T(8,128)S(1)} %get-tuple-element.144.refs_3_.refs_7_, ...), custom_call_target="tpu_custom_call" | custom-call | bytes 4194304 | tf_op jit(solution)/shard_map/apply_recur/pallas_call | solution.py:199
  59.7 2.9 %collective-permute-start.7 = (f32[24,16,128]{2,1,0:T(8,128)S(1)}, f32[24,16,128]{2,1,0:T(8,128)S(1)}, u32[]{:S(2)}, u32[]{:S(2)}) collective-permute-start(f32[24,16,128]{2,1,0:T(8,128)S(1)} %get-tuple-element.147.refs_4_), channel_id=1, source_target_pairs={{0,28},{4,8},{8,4},{12,16},{16,12},{20,24},{24,20},{28,0},{1,29},{... | collective-permute-start | bytes 589832 | tf_op jit(solution)/shard_map/ppermute | solution.py:353
  62.7 4.3 %apply_recur.14 = (f32[24,16,128]{2,1,0:T(8,128)S(1)}, f32[24,16,128]{2,1,0:T(8,128)S(1)}) custom-call(s32[578]{0:T(1024)S(1)} %get-tuple-element.137.refs_0_, bf16[288,128,256]{2,1,0:T(8,128)(2,1)S(1)} %get-tuple-element.138.refs_1_, f32[48,1,128]{2,1,0:T(1,128)S(1)} %get-tuple-element.139.refs_2_, f32[24,16,128]{2,1,0:T(8,128)S(1)} %get-tuple-element.156.refs_3_.refs_7_, ...), custom_call_target="tpu_custom_call" | custom-call | bytes 4194304 | tf_op jit(solution)/shard_map/apply_recur/pallas_call | solution.py:199
  68.0 4.9 %collective-permute-start.19 = (f32[24,16,128]{2,1,0:T(8,128)S(1)}, f32[24,16,128]{2,1,0:T(8,128)S(1)}, u32[]{:S(2)}, u32[]{:S(2)}) collective-permute-start(f32[24,16,128]{2,1,0:T(8,128)S(1)} %get-tuple-element.159.refs_4_), channel_id=1, source_target_pairs={{0,28},{4,8},{8,4},{12,16},{16,12},{20,24},{24,20},{28,0},{1,29},{... | collective-permute-start | bytes 589832 | tf_op jit(solution)/shard_map/ppermute | solution.py:353
  72.9 4.2 %apply_recur.12 = (f32[24,16,128]{2,1,0:T(8,128)S(1)}, f32[24,16,128]{2,1,0:T(8,128)S(1)}) custom-call(s32[578]{0:T(1024)S(1)} %get-tuple-element.137.refs_0_, bf16[288,128,256]{2,1,0:T(8,128)(2,1)S(1)} %get-tuple-element.138.refs_1_, f32[48,1,128]{2,1,0:T(1,128)S(1)} %get-tuple-element.139.refs_2_, f32[24,16,128]{2,1,0:T(8,128)S(1)} %get-tuple-element.146.refs_3_, ...), custom_call_target="tpu_custom_call" | custom-call | bytes 4194304 | tf_op jit(solution)/shard_map/apply_recur/pallas_call | solution.py:199
  77.3 2.0 collective-permute-start.9
  79.2 4.4 %apply_recur_parts.2 = (f32[24,16,128]{2,1,0:T(8,128)S(1)}, f32[24,16,128]{2,1,0:T(8,128)S(1)}, f32[12,32,128]{2,1,0:T(8,128)S(1)}, f32[12,32,128]{2,1,0:T(8,128...) custom-call(s32[578]{0:T(1024)S(1)} %get-tuple-element.137.refs_0_, ...), custom_call_target="tpu_custom_call" | custom-call | bytes 4194304 | tf_op jit(solution)/shard_map/apply_recur_parts/pallas_call | solution.py:199
  84.5 8.7 %collective-permute-start.28 = (f32[24,16,128]{2,1,0:T(8,128)S(1)}, f32[24,16,128]{2,1,0:T(8,128)S(1)}, u32[]{:S(2)}, u32[]{:S(2)}) collective-permute-start(f32[24,16,128]{2,1,0:T(8,128)S(1)} %get-tuple-element.179.refs_4_.refs_8_), channel_id=1, source_target_pairs={{0,28},{4,8},{8,4},{12,16},{16,12},{20,24},{24,20},{28,0},{1,29},{... | collective-permute-start | bytes 589832 | tf_op jit(solution)/shard_map/ppermute | solution.py:353
  95.1 4.2 %apply.5 = (f32[24,16,128]{2,1,0:T(8,128)S(1)}, f32[24,16,128]{2,1,0:T(8,128)S(1)}) custom-call(s32[578]{0:T(1024)S(1)} %get-tuple-element.137.refs_0_, bf16[288,128,256]{2,1,0:T(8,128)(2,1)S(1)} %get-tuple-element.138.refs_1_, f32[48,1,128]{2,1,0:T(1,128)S(1)} %get-tuple-element.139.refs_2_, f32[24,16,128]{2,1,0:T(8,128)S(1)} %get-tuple-element.165.refs_3_.refs_9_.refs_7_, ...), custom_call_target="tpu_custom_call" | custom-call | bytes 4194304 | tf_op jit(solution)/shard_map/apply/pallas_call | solution.py:199
  99.4 2.2 collective-permute-start.11
  101.6 4.5 %apply_parts.2 = (f32[24,16,128]{2,1,0:T(8,128)S(1)}, f32[24,16,128]{2,1,0:T(8,128)S(1)}, f32[12,32,128]{2,1,0:T(8,128)S(1)}, f32[12,32,128]{2,1,0:T(8,128)S(1)}...) custom-call(s32[578]{0:T(1024)S(1)} %get-tuple-element.137.refs_0_, ...), custom_call_target="tpu_custom_call" | custom-call | bytes 4194304 | tf_op jit(solution)/shard_map/apply_parts/pallas_call | solution.py:199
  107.7 2.7 %collective-permute-start.30 = (f32[24,16,128]{2,1,0:T(8,128)S(1)}, f32[24,16,128]{2,1,0:T(8,128)S(1)}, u32[]{:S(2)}, u32[]{:S(2)}) collective-permute-start(f32[24,16,128]{2,1,0:T(8,128)S(1)} %get-tuple-element.210.refs_4_.refs_8_), channel_id=1, source_target_pairs={{0,28},{4,8},{8,4},{12,16},{16,12},{20,24},{24,20},{28,0},{1,29},{... | collective-permute-start | bytes 589832 | tf_op jit(solution)/shard_map/ppermute | solution.py:353
  111.3 4.3 %apply_recur.15 = (f32[24,16,128]{2,1,0:T(8,128)S(1)}, f32[24,16,128]{2,1,0:T(8,128)S(1)}) custom-call(s32[578]{0:T(1024)S(1)} %get-tuple-element.137.refs_0_, bf16[288,128,256]{2,1,0:T(8,128)(2,1)S(1)} %get-tuple-element.138.refs_1_, f32[48,1,128]{2,1,0:T(1,128)S(1)} %get-tuple-element.139.refs_2_, f32[24,16,128]{2,1,0:T(8,128)S(1)} %get-tuple-element.184.refs_3_.refs_7_, ...), custom_call_target="tpu_custom_call" | custom-call | bytes 4194304 | tf_op jit(solution)/shard_map/apply_recur/pallas_call | solution.py:199
  120.9 4.2 %apply_recur.16 = (f32[24,16,128]{2,1,0:T(8,128)S(1)}, f32[24,16,128]{2,1,0:T(8,128)S(1)}) custom-call(s32[578]{0:T(1024)S(1)} %get-tuple-element.137.refs_0_, bf16[288,128,256]{2,1,0:T(8,128)(2,1)S(1)} %get-tuple-element.138.refs_1_, f32[48,1,128]{2,1,0:T(1,128)S(1)} %get-tuple-element.139.refs_2_, f32[24,16,128]{2,1,0:T(8,128)S(1)} %get-tuple-element.209.refs_3_.refs_7_, ...), custom_call_target="tpu_custom_call" | custom-call | bytes 4194304 | tf_op jit(solution)/shard_map/apply_recur/pallas_call | solution.py:199
  127.6 2.4 %collective-permute-start.39 = (f32[24,16,128]{2,1,0:T(8,128)S(1)}, f32[24,16,128]{2,1,0:T(8,128)S(1)}, u32[]{:S(2)}, u32[]{:S(2)}) collective-permute-start(f32[24,16,128]{2,1,0:T(8,128)S(1)} %get-tuple-element.214.refs_4_.refs_8_), channel_id=1, source_target_pairs={{0,28},{4,8},{8,4},{12,16},{16,12},{20,24},{24,20},{28,0},{1,29},{... | collective-permute-start | bytes 589832 | tf_op jit(solution)/shard_map/ppermute | solution.py:353
  130.2 4.2 %apply_recur.17 = (f32[24,16,128]{2,1,0:T(8,128)S(1)}, f32[24,16,128]{2,1,0:T(8,128)S(1)}) custom-call(s32[578]{0:T(1024)S(1)} %get-tuple-element.137.refs_0_, bf16[288,128,256]{2,1,0:T(8,128)(2,1)S(1)} %get-tuple-element.138.refs_1_, f32[48,1,128]{2,1,0:T(1,128)S(1)} %get-tuple-element.139.refs_2_, f32[24,16,128]{2,1,0:T(8,128)S(1)} %get-tuple-element.194.refs_3_.refs_7_, ...), custom_call_target="tpu_custom_call" | custom-call | bytes 4194304 | tf_op jit(solution)/shard_map/apply_recur/pallas_call | solution.py:199
  134.5 2.0 collective-permute-start.31
  136.5 3.1 %collective-permute-done.33 = f32[128,128]{1,0:T(8,128)S(1)} collective-permute-done((f32[128,128]{1,0:T(8,128)S(1)}, f32[128,128]{1,0:T(8,128)S(1)}, u32[]{:S(2)}, u32[]{:S(2)}) %collective-permute-start.33) | collective-permute-done | bytes 65568 | tf_op jit(solution)/shard_map/ppermute | solution.py:357
  139.6 2.7 %collective-permute-start.32 = (f32[24,16,128]{2,1,0:T(8,128)S(1)}, f32[24,16,128]{2,1,0:T(8,128)S(1)}, u32[]{:S(2)}, u32[]{:S(2)}) collective-permute-start(f32[24,16,128]{2,1,0:T(8,128)S(1)} %get-tuple-element.187.refs_4_), channel_id=1, source_target_pairs={{0,28},{4,8},{8,4},{12,16},{16,12},{20,24},{24,20},{28,0},{1,29},{... | collective-permute-start | bytes 589832 | tf_op jit(solution)/shard_map/ppermute | solution.py:353
  142.3 4.3 %apply_recur.19 = (f32[24,16,128]{2,1,0:T(8,128)S(1)}, f32[24,16,128]{2,1,0:T(8,128)S(1)}) custom-call(s32[578]{0:T(1024)S(1)} %get-tuple-element.137.refs_0_, bf16[288,128,256]{2,1,0:T(8,128)(2,1)S(1)} %get-tuple-element.138.refs_1_, f32[48,1,128]{2,1,0:T(1,128)S(1)} %get-tuple-element.139.refs_2_, f32[24,16,128]{2,1,0:T(8,128)S(1)} %get-tuple-element.213.refs_3_.refs_7_, ...), custom_call_target="tpu_custom_call" | custom-call | bytes 4194304 | tf_op jit(solution)/shard_map/apply_recur/pallas_call | solution.py:199
  146.6 2.1 collective-permute-start.44
  150.2 4.2 %apply_recur.18 = (f32[24,16,128]{2,1,0:T(8,128)S(1)}, f32[24,16,128]{2,1,0:T(8,128)S(1)}) custom-call(s32[578]{0:T(1024)S(1)} %get-tuple-element.137.refs_0_, bf16[288,128,256]{2,1,0:T(8,128)(2,1)S(1)} %get-tuple-element.138.refs_1_, f32[48,1,128]{2,1,0:T(1,128)S(1)} %get-tuple-element.139.refs_2_, f32[24,16,128]{2,1,0:T(8,128)S(1)} %get-tuple-element.186.refs_3_, ...), custom_call_target="tpu_custom_call" | custom-call | bytes 4194304 | tf_op jit(solution)/shard_map/apply_recur/pallas_call | solution.py:199
  154.6 4.0 %collective-permute-start.37 = (f32[128,128]{1,0:T(8,128)S(1)}, f32[128,128]{1,0:T(8,128)S(1)}, u32[]{:S(2)}, u32[]{:S(2)}) collective-permute-start(f32[128,128]{1,0:T(8,128)S(1)} %add.66), channel_id=1, source_target_pairs={{0,16},{4,20},{8,24},{12,28},{16,0},{20,4},{24,8},{28,12},{1,17},{... | collective-permute-start | bytes 196616 | tf_op jit(solution)/shard_map/ppermute | solution.py:357
  159.7 4.6 %apply_recur_parts.3 = (f32[24,16,128]{2,1,0:T(8,128)S(1)}, f32[24,16,128]{2,1,0:T(8,128)S(1)}, f32[12,32,128]{2,1,0:T(8,128)S(1)}, f32[12,32,128]{2,1,0:T(8,128...) custom-call(s32[578]{0:T(1024)S(1)} %get-tuple-element.137.refs_0_, ...), custom_call_target="tpu_custom_call" | custom-call | bytes 4194304 | tf_op jit(solution)/shard_map/apply_recur_parts/pallas_call | solution.py:199
  164.4 3.3 %collective-permute-start.46 = (f32[12,32,128]{2,1,0:T(8,128)S(1)}, f32[12,32,128]{2,1,0:T(8,128)S(1)}, u32[]{:S(2)}, u32[]{:S(2)}) collective-permute-start(f32[12,32,128]{2,1,0:T(8,128)S(1)} %get-tuple-element.222), channel_id=1, source_target_pairs={{0,2},{1,3},{2,0},{3,1},{4,6},{5,7},{6,4},{7,5},{8,10},{9,11},{10,... | collective-permute-start | bytes 589832 | tf_op jit(solution)/shard_map/ppermute | solution.py:357
  167.8 3.0 %collective-permute-start.51 = (f32[24,16,128]{2,1,0:T(8,128)S(1)}, f32[24,16,128]{2,1,0:T(8,128)S(1)}, u32[]{:S(2)}, u32[]{:S(2)}) collective-permute-start(f32[24,16,128]{2,1,0:T(8,128)S(1)} %get-tuple-element.216.refs_4_), channel_id=1, source_target_pairs={{0,28},{4,8},{8,4},{12,16},{16,12},{20,24},{24,20},{28,0},{1,29},{... | collective-permute-start | bytes 589832 | tf_op jit(solution)/shard_map/ppermute | solution.py:353
  170.8 4.1 %factor.2.inv_ref.refs_0_ = f32[128,128]{1,0:T(8,128)S(1)} custom-call(f32[128,128]{1,0:T(8,128)S(1)} %add.67.g_ref), custom_call_target="tpu_custom_call" | custom-call | tf_op jit(solution)/shard_map/factor/pallas_call | solution.py:42
  174.9 2.2 collective-permute-done.47.refs_3_
  177.1 2.4 %turn.1 = (f32[12,128,128]{2,1,0:T(8,128)S(1)}, f32[128,128]{1,0:T(8,128)S(1)}) custom-call(s32[2]{0:T(128)S(1)} %pad_add_fusion.ids_ref, f32[128,128]{1,0:T(8,128)S(1)} %factor.2.inv_ref.refs_0_, f32[12,32,128]{2,1,0:T(8,128)S(1)} %get-tuple-element.220.refs_0_, f32[12,32,128]{2,1,0:T(8,128)S(1)} %collective-permute-done.45.refs_1_, ...), custom_call_target="tpu_custom_call" | custom-call | tf_op jit(solution)/shard_map/turn/pallas_call | solution.py:42
  182.8 4.2 %apply.7 = (f32[24,16,128]{2,1,0:T(8,128)S(1)}, f32[24,16,128]{2,1,0:T(8,128)S(1)}) custom-call(s32[578]{0:T(1024)S(1)} %get-tuple-element.137.refs_0_, bf16[288,128,256]{2,1,0:T(8,128)(2,1)S(1)} %get-tuple-element.138.refs_1_, f32[48,1,128]{2,1,0:T(1,128)S(1)} %get-tuple-element.139.refs_2_, f32[24,16,128]{2,1,0:T(8,128)S(1)} %get-tuple-element.196.refs_9_.refs_3_, ...), custom_call_target="tpu_custom_call" | custom-call | bytes 4194304 | tf_op jit(solution)/shard_map/apply/pallas_call | solution.py:199
  187.1 5.3 %apply_parts.3 = (f32[24,16,128]{2,1,0:T(8,128)}, f32[24,16,128]{2,1,0:T(8,128)}, f32[12,32,128]{2,1,0:T(8,128)S(1)}, f32[12,32,128]{2,1,0:T(8,128)S(1)}, f32[12...) custom-call(s32[578]{0:T(1024)S(1)} %get-tuple-element.137.refs_0_, ...), custom_call_target="tpu_custom_call" | custom-call | bytes 4194304 | tf_op jit(solution)/shard_map/apply_parts/pallas_call | solution.py:199
  196.1 4.0 %collective-permute-done.53 = f32[128,128]{1,0:T(8,128)S(1)} collective-permute-done((f32[128,128]{1,0:T(8,128)S(1)}, f32[128,128]{1,0:T(8,128)S(1)}, u32[]{:S(2)}, u32[]{:S(2)}) %collective-permute-start.53) | collective-permute-done | bytes 65568 | tf_op jit(solution)/shard_map/ppermute | solution.py:357
  200.2 2.3 collective-permute-start.54
  208.8 3.8 %collective-permute-start.60 = (f32[128,128]{1,0:T(8,128)S(1)}, f32[128,128]{1,0:T(8,128)S(1)}, u32[]{:S(2)}, u32[]{:S(2)}) collective-permute-start(f32[128,128]{1,0:T(8,128)S(1)} %turn_cross.1), channel_id=1, source_target_pairs={{0,24},{4,28},{8,16},{12,20},{16,8},{20,12},{24,0},{28,4},{1,25},{... | collective-permute-start | bytes 196616 | tf_op jit(solution)/shard_map/ppermute | solution.py:357
  213.2 4.1 %factor.3.inv_ref.refs_2_ = f32[128,128]{1,0:T(8,128)S(1)} custom-call(f32[128,128]{1,0:T(8,128)S(1)} %add.72.g_ref), custom_call_target="tpu_custom_call" | custom-call | tf_op jit(solution)/shard_map/factor/pallas_call | solution.py:42
  218.8 2.6 %collective-permute-start.65 = (f32[128,128]{1,0:T(8,128)S(1)}, f32[128,128]{1,0:T(8,128)S(1)}, u32[]{:S(2)}, u32[]{:S(2)}) collective-permute-start(f32[128,128]{1,0:T(8,128)S(1)} %add_add_fusion), channel_id=1, source_target_pairs={{0,4},{4,0},{8,12},{12,8},{16,20},{20,16},{24,28},{28,24},{1,5},{5... | collective-permute-start | bytes 196616 | tf_op jit(solution)/shard_map/ppermute | solution.py:357
  223.7 4.0 %collective-permute-done.64 = f32[128,128]{1,0:T(8,128)S(1)} collective-permute-done((f32[128,128]{1,0:T(8,128)S(1)}, f32[128,128]{1,0:T(8,128)S(1)}, u32[]{:S(2)}, u32[]{:S(2)}) %collective-permute-start.64) | collective-permute-done | bytes 65568 | tf_op jit(solution)/shard_map/ppermute | solution.py:357
  (144 shorter events, 48.8 us)
Async XLA Ops:
  2.5 16.8 %collective-permute-start = (f32[24,16,128]{2,1,0:T(8,128)S(1)}, f32[24,16,128]{2,1,0:T(8,128)S(1)}, u32[]{:S(2)}, u32[]{:S(2)}) collective-permute-start(f32[24,16,128]{2,1,0:T(8,128)S(1)} %get-tuple-element.140.refs_3_.refs_7_), channel_id=1, source_target_pairs={{0,4},{4,0},{8,12},{12,8},{16,20},{20,16},{24,28},{28,24},{1,5},{5... | collective-permute-start | bytes 589832 | tf_op jit(solution)/shard_map/ppermute | solution.py:353
  5.5 13.8 %collective-permute-start.1 = (f32[24,16,128]{2,1,0:T(8,128)S(1)}, f32[24,16,128]{2,1,0:T(8,128)S(1)}, u32[]{:S(2)}, u32[]{:S(2)}) collective-permute-start(f32[24,16,128]{2,1,0:T(8,128)S(1)} %get-tuple-element.141.refs_4_.refs_8_), channel_id=1, source_target_pairs={{0,28},{4,8},{8,4},{12,16},{16,12},{20,24},{24,20},{28,0},{1,29},{... | collective-permute-start | bytes 589832 | tf_op jit(solution)/shard_map/ppermute | solution.py:353
  9.1 20.5 %collective-permute-start.12 = (f32[24,16,128]{2,1,0:T(8,128)S(1)}, f32[24,16,128]{2,1,0:T(8,128)S(1)}, u32[]{:S(2)}, u32[]{:S(2)}) collective-permute-start(f32[24,16,128]{2,1,0:T(8,128)S(1)} %get-tuple-element.152.refs_3_.refs_7_), channel_id=1, source_target_pairs={{0,4},{4,0},{8,12},{12,8},{16,20},{20,16},{24,28},{28,24},{1,5},{5... | collective-permute-start | bytes 589832 | tf_op jit(solution)/shard_map/ppermute | solution.py:353
  9.1 20.5 %collective-permute-start.13 = (f32[24,16,128]{2,1,0:T(8,128)S(1)}, f32[24,16,128]{2,1,0:T(8,128)S(1)}, u32[]{:S(2)}, u32[]{:S(2)}) collective-permute-start(f32[24,16,128]{2,1,0:T(8,128)S(1)} %get-tuple-element.153.refs_4_.refs_8_), channel_id=1, source_target_pairs={{0,28},{4,8},{8,4},{12,16},{16,12},{20,24},{24,20},{28,0},{1,29},{... | collective-permute-start | bytes 589832 | tf_op jit(solution)/shard_map/ppermute | solution.py:353
  23.6 12.3 %collective-permute-start.2 = (f32[24,16,128]{2,1,0:T(8,128)S(1)}, f32[24,16,128]{2,1,0:T(8,128)S(1)}, u32[]{:S(2)}, u32[]{:S(2)}) collective-permute-start(f32[24,16,128]{2,1,0:T(8,128)S(1)} %get-tuple-element.142.refs_3_.refs_7_), channel_id=1, source_target_pairs={{0,4},{4,0},{8,12},{12,8},{16,20},{20,16},{24,28},{28,24},{1,5},{5... | collective-permute-start | bytes 589832 | tf_op jit(solution)/shard_map/ppermute | solution.py:353
  33.9 15.2 %collective-permute-start.14 = (f32[24,16,128]{2,1,0:T(8,128)S(1)}, f32[24,16,128]{2,1,0:T(8,128)S(1)}, u32[]{:S(2)}, u32[]{:S(2)}) collective-permute-start(f32[24,16,128]{2,1,0:T(8,128)S(1)} %get-tuple-element.154.refs_3_.refs_7_), channel_id=1, source_target_pairs={{0,4},{4,0},{8,12},{12,8},{16,20},{20,16},{24,28},{28,24},{1,5},{5... | collective-permute-start | bytes 589832 | tf_op jit(solution)/shard_map/ppermute | solution.py:353
  33.9 15.1 %collective-permute-start.15 = (f32[24,16,128]{2,1,0:T(8,128)S(1)}, f32[24,16,128]{2,1,0:T(8,128)S(1)}, u32[]{:S(2)}, u32[]{:S(2)}) collective-permute-start(f32[24,16,128]{2,1,0:T(8,128)S(1)} %get-tuple-element.155.refs_4_.refs_8_), channel_id=1, source_target_pairs={{0,28},{4,8},{8,4},{12,16},{16,12},{20,24},{24,20},{28,0},{1,29},{... | collective-permute-start | bytes 589832 | tf_op jit(solution)/shard_map/ppermute | solution.py:353
  40.1 15.2 %collective-permute-start.4 = (f32[24,16,128]{2,1,0:T(8,128)S(1)}, f32[24,16,128]{2,1,0:T(8,128)S(1)}, u32[]{:S(2)}, u32[]{:S(2)}) collective-permute-start(f32[24,16,128]{2,1,0:T(8,128)S(1)} %get-tuple-element.144.refs_3_.refs_7_), channel_id=1, source_target_pairs={{0,4},{4,0},{8,12},{12,8},{16,20},{20,16},{24,28},{28,24},{1,5},{5... | collective-permute-start | bytes 589832 | tf_op jit(solution)/shard_map/ppermute | solution.py:353
  40.8 14.5 %collective-permute-start.5 = (f32[24,16,128]{2,1,0:T(8,128)S(1)}, f32[24,16,128]{2,1,0:T(8,128)S(1)}, u32[]{:S(2)}, u32[]{:S(2)}) collective-permute-start(f32[24,16,128]{2,1,0:T(8,128)S(1)} %get-tuple-element.145.refs_4_.refs_8_), channel_id=1, source_target_pairs={{0,28},{4,8},{8,4},{12,16},{16,12},{20,24},{24,20},{28,0},{1,29},{... | collective-permute-start | bytes 589832 | tf_op jit(solution)/shard_map/ppermute | solution.py:353
  59.6 13.4 %collective-permute-start.6 = (f32[24,16,128]{2,1,0:T(8,128)S(1)}, f32[24,16,128]{2,1,0:T(8,128)S(1)}, u32[]{:S(2)}, u32[]{:S(2)}) collective-permute-start(f32[24,16,128]{2,1,0:T(8,128)S(1)} %get-tuple-element.146.refs_3_), channel_id=1, source_target_pairs={{0,4},{4,0},{8,12},{12,8},{16,20},{20,16},{24,28},{28,24},{1,5},{5... | collective-permute-start | bytes 589832 | tf_op jit(solution)/shard_map/ppermute | solution.py:353
  59.7 13.2 %collective-permute-start.7 = (f32[24,16,128]{2,1,0:T(8,128)S(1)}, f32[24,16,128]{2,1,0:T(8,128)S(1)}, u32[]{:S(2)}, u32[]{:S(2)}) collective-permute-start(f32[24,16,128]{2,1,0:T(8,128)S(1)} %get-tuple-element.147.refs_4_), channel_id=1, source_target_pairs={{0,28},{4,8},{8,4},{12,16},{16,12},{20,24},{24,20},{28,0},{1,29},{... | collective-permute-start | bytes 589832 | tf_op jit(solution)/shard_map/ppermute | solution.py:353
  66.9 12.3 %collective-permute-start.18 = (f32[24,16,128]{2,1,0:T(8,128)S(1)}, f32[24,16,128]{2,1,0:T(8,128)S(1)}, u32[]{:S(2)}, u32[]{:S(2)}) collective-permute-start(f32[24,16,128]{2,1,0:T(8,128)S(1)} %get-tuple-element.158.refs_3_), channel_id=1, source_target_pairs={{0,4},{4,0},{8,12},{12,8},{16,20},{20,16},{24,28},{28,24},{1,5},{5... | collective-permute-start | bytes 589832 | tf_op jit(solution)/shard_map/ppermute | solution.py:353
  68.0 11.2 %collective-permute-start.19 = (f32[24,16,128]{2,1,0:T(8,128)S(1)}, f32[24,16,128]{2,1,0:T(8,128)S(1)}, u32[]{:S(2)}, u32[]{:S(2)}) collective-permute-start(f32[24,16,128]{2,1,0:T(8,128)S(1)} %get-tuple-element.159.refs_4_), channel_id=1, source_target_pairs={{0,28},{4,8},{8,4},{12,16},{16,12},{20,24},{24,20},{28,0},{1,29},{... | collective-permute-start | bytes 589832 | tf_op jit(solution)/shard_map/ppermute | solution.py:353
  77.2 16.0 %collective-permute-start.8 = (f32[24,16,128]{2,1,0:T(8,128)S(1)}, f32[24,16,128]{2,1,0:T(8,128)S(1)}, u32[]{:S(2)}, u32[]{:S(2)}) collective-permute-start(f32[24,16,128]{2,1,0:T(8,128)S(1)} %get-tuple-element.165.refs_3_.refs_9_.refs_7_), channel_id=1, source_target_pairs={{0,4},{4,0},{8,12},{12,8},{16,20},{20,16},{24,28},{28,24},{1,5},{5... | collective-permute-start | bytes 589832 | tf_op jit(solution)/shard_map/ppermute | solution.py:353
  77.3 17.5 %collective-permute-start.9 = (f32[24,16,128]{2,1,0:T(8,128)S(1)}, f32[24,16,128]{2,1,0:T(8,128)S(1)}, u32[]{:S(2)}, u32[]{:S(2)}) collective-permute-start(f32[24,16,128]{2,1,0:T(8,128)S(1)} %get-tuple-element.166.refs_4_.refs_10_.refs_8_), channel_id=1, source_target_pairs={{0,28},{4,8},{8,4},{12,16},{16,12},{20,24},{24,20},{28,0},{1,29},{... | collective-permute-start | bytes 589832 | tf_op jit(solution)/shard_map/ppermute | solution.py:353
  83.6 15.7 %collective-permute-start.27 = (f32[24,16,128]{2,1,0:T(8,128)S(1)}, f32[24,16,128]{2,1,0:T(8,128)S(1)}, u32[]{:S(2)}, u32[]{:S(2)}) collective-permute-start(f32[24,16,128]{2,1,0:T(8,128)S(1)} %get-tuple-element.178.refs_3_.refs_7_), channel_id=1, source_target_pairs={{0,4},{4,0},{8,12},{12,8},{16,20},{20,16},{24,28},{28,24},{1,5},{5... | collective-permute-start | bytes 589832 | tf_op jit(solution)/shard_map/ppermute | solution.py:353
  84.5 14.9 %collective-permute-start.28 = (f32[24,16,128]{2,1,0:T(8,128)S(1)}, f32[24,16,128]{2,1,0:T(8,128)S(1)}, u32[]{:S(2)}, u32[]{:S(2)}) collective-permute-start(f32[24,16,128]{2,1,0:T(8,128)S(1)} %get-tuple-element.179.refs_4_.refs_8_), channel_id=1, source_target_pairs={{0,28},{4,8},{8,4},{12,16},{16,12},{20,24},{24,20},{28,0},{1,29},{... | collective-permute-start | bytes 589832 | tf_op jit(solution)/shard_map/ppermute | solution.py:353
  93.2 12.9 %collective-permute-start.20 = (f32[12,32,128]{2,1,0:T(8,128)S(1)}, f32[12,32,128]{2,1,0:T(8,128)S(1)}, u32[]{:S(2)}, u32[]{:S(2)}) collective-permute-start(f32[12,32,128]{2,1,0:T(8,128)S(1)} %get-tuple-element.161), channel_id=1, source_target_pairs={{0,1},{1,0},{2,3},{3,2},{4,5},{5,4},{6,7},{7,6},{8,9},{9,8},{10,11... | collective-permute-start | bytes 589832 | tf_op jit(solution)/shard_map/ppermute | solution.py:357
  93.2 13.0 %collective-permute-start.21 = (f32[12,32,128]{2,1,0:T(8,128)S(1)}, f32[12,32,128]{2,1,0:T(8,128)S(1)}, u32[]{:S(2)}, u32[]{:S(2)}) collective-permute-start(f32[12,32,128]{2,1,0:T(8,128)S(1)} %get-tuple-element.162), channel_id=1, source_target_pairs={{0,2},{1,3},{2,0},{3,1},{4,6},{5,7},{6,4},{7,5},{8,10},{9,11},{10,... | collective-permute-start | bytes 589832 | tf_op jit(solution)/shard_map/ppermute | solution.py:357
  94.7 11.6 %collective-permute-start.22 = (f32[12,32,128]{2,1,0:T(8,128)S(1)}, f32[12,32,128]{2,1,0:T(8,128)S(1)}, u32[]{:S(2)}, u32[]{:S(2)}) collective-permute-start(f32[12,32,128]{2,1,0:T(8,128)S(1)} %get-tuple-element.163), channel_id=1, source_target_pairs={{0,3},{1,2},{2,1},{3,0},{4,7},{5,6},{6,5},{7,4},{8,11},{9,10},{10,... | collective-permute-start | bytes 589832 | tf_op jit(solution)/shard_map/ppermute | solution.py:357
  99.3 12.0 %collective-permute-start.10 = (f32[24,16,128]{2,1,0:T(8,128)S(1)}, f32[24,16,128]{2,1,0:T(8,128)S(1)}, u32[]{:S(2)}, u32[]{:S(2)}) collective-permute-start(f32[24,16,128]{2,1,0:T(8,128)S(1)} %get-tuple-element.184.refs_3_.refs_7_), channel_id=1, source_target_pairs={{0,4},{4,0},{8,12},{12,8},{16,20},{20,16},{24,28},{28,24},{1,5},{5... | collective-permute-start | bytes 589832 | tf_op jit(solution)/shard_map/ppermute | solution.py:353
  99.4 11.9 %collective-permute-start.11 = (f32[24,16,128]{2,1,0:T(8,128)S(1)}, f32[24,16,128]{2,1,0:T(8,128)S(1)}, u32[]{:S(2)}, u32[]{:S(2)}) collective-permute-start(f32[24,16,128]{2,1,0:T(8,128)S(1)} %get-tuple-element.185.refs_4_.refs_8_), channel_id=1, source_target_pairs={{0,28},{4,8},{8,4},{12,16},{16,12},{20,24},{24,20},{28,0},{1,29},{... | collective-permute-start | bytes 589832 | tf_op jit(solution)/shard_map/ppermute | solution.py:353
  106.1 11.2 %collective-permute-start.40 = (f32[12,32,128]{2,1,0:T(8,128)S(1)}, f32[12,32,128]{2,1,0:T(8,128)S(1)}, u32[]{:S(2)}, u32[]{:S(2)}) collective-permute-start(f32[12,32,128]{2,1,0:T(8,128)S(1)} %get-tuple-element.206), channel_id=1, source_target_pairs={{0,1},{1,0},{2,3},{3,2},{4,5},{5,4},{6,7},{7,6},{8,9},{9,8},{10,11... | collective-permute-start | bytes 589832 | tf_op jit(solution)/shard_map/ppermute | solution.py:357
  106.2 13.2 %collective-permute-start.29 = (f32[24,16,128]{2,1,0:T(8,128)S(1)}, f32[24,16,128]{2,1,0:T(8,128)S(1)}, u32[]{:S(2)}, u32[]{:S(2)}) collective-permute-start(f32[24,16,128]{2,1,0:T(8,128)S(1)} %get-tuple-element.209.refs_3_.refs_7_), channel_id=1, source_target_pairs={{0,4},{4,0},{8,12},{12,8},{16,20},{20,16},{24,28},{28,24},{1,5},{5... | collective-permute-start | bytes 589832 | tf_op jit(solution)/shard_map/ppermute | solution.py:353
  107.7 13.2 %collective-permute-start.30 = (f32[24,16,128]{2,1,0:T(8,128)S(1)}, f32[24,16,128]{2,1,0:T(8,128)S(1)}, u32[]{:S(2)}, u32[]{:S(2)}) collective-permute-start(f32[24,16,128]{2,1,0:T(8,128)S(1)} %get-tuple-element.210.refs_4_.refs_8_), channel_id=1, source_target_pairs={{0,28},{4,8},{8,4},{12,16},{16,12},{20,24},{24,20},{28,0},{1,29},{... | collective-permute-start | bytes 589832 | tf_op jit(solution)/shard_map/ppermute | solution.py:353
  115.6 12.0 %collective-permute-start.23 = (f32[24,16,128]{2,1,0:T(8,128)S(1)}, f32[24,16,128]{2,1,0:T(8,128)S(1)}, u32[]{:S(2)}, u32[]{:S(2)}) collective-permute-start(f32[24,16,128]{2,1,0:T(8,128)S(1)} %get-tuple-element.194.refs_3_.refs_7_), channel_id=1, source_target_pairs={{0,4},{4,0},{8,12},{12,8},{16,20},{20,16},{24,28},{28,24},{1,5},{5... | collective-permute-start | bytes 589832 | tf_op jit(solution)/shard_map/ppermute | solution.py:353
  115.7 14.3 %collective-permute-start.24 = (f32[24,16,128]{2,1,0:T(8,128)S(1)}, f32[24,16,128]{2,1,0:T(8,128)S(1)}, u32[]{:S(2)}, u32[]{:S(2)}) collective-permute-start(f32[24,16,128]{2,1,0:T(8,128)S(1)} %get-tuple-element.195.refs_4_.refs_8_), channel_id=1, source_target_pairs={{0,28},{4,8},{8,4},{12,16},{16,12},{20,24},{24,20},{28,0},{1,29},{... | collective-permute-start | bytes 589832 | tf_op jit(solution)/shard_map/ppermute | solution.py:353
  117.3 17.2 %collective-permute-start.41 = (f32[12,32,128]{2,1,0:T(8,128)S(1)}, f32[12,32,128]{2,1,0:T(8,128)S(1)}, u32[]{:S(2)}, u32[]{:S(2)}) collective-permute-start(f32[12,32,128]{2,1,0:T(8,128)S(1)} %get-tuple-element.207), channel_id=1, source_target_pairs={{0,2},{1,3},{2,0},{3,1},{4,6},{5,7},{6,4},{7,5},{8,10},{9,11},{10,... | collective-permute-start | bytes 589832 | tf_op jit(solution)/shard_map/ppermute | solution.py:357
  120.9 21.4 %collective-permute-start.42 = (f32[12,32,128]{2,1,0:T(8,128)S(1)}, f32[12,32,128]{2,1,0:T(8,128)S(1)}, u32[]{:S(2)}, u32[]{:S(2)}) collective-permute-start(f32[12,32,128]{2,1,0:T(8,128)S(1)} %get-tuple-element.208), channel_id=1, source_target_pairs={{0,3},{1,2},{2,1},{3,0},{4,7},{5,6},{6,5},{7,4},{8,11},{9,10},{10,... | collective-permute-start | bytes 589832 | tf_op jit(solution)/shard_map/ppermute | solution.py:357
  126.5 15.8 %collective-permute-start.38 = (f32[24,16,128]{2,1,0:T(8,128)S(1)}, f32[24,16,128]{2,1,0:T(8,128)S(1)}, u32[]{:S(2)}, u32[]{:S(2)}) collective-permute-start(f32[24,16,128]{2,1,0:T(8,128)S(1)} %get-tuple-element.213.refs_3_.refs_7_), channel_id=1, source_target_pairs={{0,4},{4,0},{8,12},{12,8},{16,20},{20,16},{24,28},{28,24},{1,5},{5... | collective-permute-start | bytes 589832 | tf_op jit(solution)/shard_map/ppermute | solution.py:353
  127.6 14.7 %collective-permute-start.39 = (f32[24,16,128]{2,1,0:T(8,128)S(1)}, f32[24,16,128]{2,1,0:T(8,128)S(1)}, u32[]{:S(2)}, u32[]{:S(2)}) collective-permute-start(f32[24,16,128]{2,1,0:T(8,128)S(1)} %get-tuple-element.214.refs_4_.refs_8_), channel_id=1, source_target_pairs={{0,28},{4,8},{8,4},{12,16},{16,12},{20,24},{24,20},{28,0},{1,29},{... | collective-permute-start | bytes 589832 | tf_op jit(solution)/shard_map/ppermute | solution.py:353
  134.5 15.7 %collective-permute-start.31 = (f32[24,16,128]{2,1,0:T(8,128)S(1)}, f32[24,16,128]{2,1,0:T(8,128)S(1)}, u32[]{:S(2)}, u32[]{:S(2)}) collective-permute-start(f32[24,16,128]{2,1,0:T(8,128)S(1)} %get-tuple-element.186.refs_3_), channel_id=1, source_target_pairs={{0,4},{4,0},{8,12},{12,8},{16,20},{20,16},{24,28},{28,24},{1,5},{5... | collective-permute-start | bytes 589832 | tf_op jit(solution)/shard_map/ppermute | solution.py:353
  139.6 10.6 %collective-permute-start.32 = (f32[24,16,128]{2,1,0:T(8,128)S(1)}, f32[24,16,128]{2,1,0:T(8,128)S(1)}, u32[]{:S(2)}, u32[]{:S(2)}) collective-permute-start(f32[24,16,128]{2,1,0:T(8,128)S(1)} %get-tuple-element.187.refs_4_), channel_id=1, source_target_pairs={{0,28},{4,8},{8,4},{12,16},{16,12},{20,24},{24,20},{28,0},{1,29},{... | collective-permute-start | bytes 589832 | tf_op jit(solution)/shard_map/ppermute | solution.py:353
  146.6 13.2 %collective-permute-start.43 = (f32[24,16,128]{2,1,0:T(8,128)S(1)}, f32[24,16,128]{2,1,0:T(8,128)S(1)}, u32[]{:S(2)}, u32[]{:S(2)}) collective-permute-start(f32[24,16,128]{2,1,0:T(8,128)S(1)} %get-tuple-element.211.refs_3_), channel_id=1, source_target_pairs={{0,4},{4,0},{8,12},{12,8},{16,20},{20,16},{24,28},{28,24},{1,5},{5... | collective-permute-start | bytes 589832 | tf_op jit(solution)/shard_map/ppermute | solution.py:353
  146.6 13.1 %collective-permute-start.44 = (f32[24,16,128]{2,1,0:T(8,128)S(1)}, f32[24,16,128]{2,1,0:T(8,128)S(1)}, u32[]{:S(2)}, u32[]{:S(2)}) collective-permute-start(f32[24,16,128]{2,1,0:T(8,128)S(1)} %get-tuple-element.212.refs_4_), channel_id=1, source_target_pairs={{0,28},{4,8},{8,4},{12,16},{16,12},{20,24},{24,20},{28,0},{1,29},{... | collective-permute-start | bytes 589832 | tf_op jit(solution)/shard_map/ppermute | solution.py:353
  154.6 13.1 %collective-permute-start.37 = (f32[128,128]{1,0:T(8,128)S(1)}, f32[128,128]{1,0:T(8,128)S(1)}, u32[]{:S(2)}, u32[]{:S(2)}) collective-permute-start(f32[128,128]{1,0:T(8,128)S(1)} %add.66), channel_id=1, source_target_pairs={{0,16},{4,20},{8,24},{12,28},{16,0},{20,4},{24,8},{28,12},{1,17},{... | collective-permute-start | bytes 196616 | tf_op jit(solution)/shard_map/ppermute | solution.py:357
  164.3 10.6 %collective-permute-start.45 = (f32[12,32,128]{2,1,0:T(8,128)S(1)}, f32[12,32,128]{2,1,0:T(8,128)S(1)}, u32[]{:S(2)}, u32[]{:S(2)}) collective-permute-start(f32[12,32,128]{2,1,0:T(8,128)S(1)} %get-tuple-element.221), channel_id=1, source_target_pairs={{0,1},{1,0},{2,3},{3,2},{4,5},{5,4},{6,7},{7,6},{8,9},{9,8},{10,11... | collective-permute-start | bytes 589832 | tf_op jit(solution)/shard_map/ppermute | solution.py:357
  164.4 10.5 %collective-permute-start.46 = (f32[12,32,128]{2,1,0:T(8,128)S(1)}, f32[12,32,128]{2,1,0:T(8,128)S(1)}, u32[]{:S(2)}, u32[]{:S(2)}) collective-permute-start(f32[12,32,128]{2,1,0:T(8,128)S(1)} %get-tuple-element.222), channel_id=1, source_target_pairs={{0,2},{1,3},{2,0},{3,1},{4,6},{5,7},{6,4},{7,5},{8,10},{9,11},{10,... | collective-permute-start | bytes 589832 | tf_op jit(solution)/shard_map/ppermute | solution.py:357
  167.8 19.3 %collective-permute-start.50 = (f32[24,16,128]{2,1,0:T(8,128)S(1)}, f32[24,16,128]{2,1,0:T(8,128)S(1)}, u32[]{:S(2)}, u32[]{:S(2)}) collective-permute-start(f32[24,16,128]{2,1,0:T(8,128)S(1)} %get-tuple-element.215.refs_3_), channel_id=1, source_target_pairs={{0,4},{4,0},{8,12},{12,8},{16,20},{20,16},{24,28},{28,24},{1,5},{5... | collective-permute-start | bytes 589832 | tf_op jit(solution)/shard_map/ppermute | solution.py:353
  167.8 19.2 %collective-permute-start.51 = (f32[24,16,128]{2,1,0:T(8,128)S(1)}, f32[24,16,128]{2,1,0:T(8,128)S(1)}, u32[]{:S(2)}, u32[]{:S(2)}) collective-permute-start(f32[24,16,128]{2,1,0:T(8,128)S(1)} %get-tuple-element.216.refs_4_), channel_id=1, source_target_pairs={{0,28},{4,8},{8,4},{12,16},{16,12},{20,24},{24,20},{28,0},{1,29},{... | collective-permute-start | bytes 589832 | tf_op jit(solution)/shard_map/ppermute | solution.py:353
  192.4 11.3 %collective-permute-start.55 = (f32[12,32,128]{2,1,0:T(8,128)S(1)}, f32[12,32,128]{2,1,0:T(8,128)S(1)}, u32[]{:S(2)}, u32[]{:S(2)}) collective-permute-start(f32[12,32,128]{2,1,0:T(8,128)S(1)} %get-tuple-element.241), channel_id=1, source_target_pairs={{0,1},{1,0},{2,3},{3,2},{4,5},{5,4},{6,7},{7,6},{8,9},{9,8},{10,11... | collective-permute-start | bytes 589832 | tf_op jit(solution)/shard_map/ppermute | solution.py:357
  192.5 13.2 %collective-permute-start.56 = (f32[12,32,128]{2,1,0:T(8,128)S(1)}, f32[12,32,128]{2,1,0:T(8,128)S(1)}, u32[]{:S(2)}, u32[]{:S(2)}) collective-permute-start(f32[12,32,128]{2,1,0:T(8,128)S(1)} %get-tuple-element.242), channel_id=1, source_target_pairs={{0,2},{1,3},{2,0},{3,1},{4,6},{5,7},{6,4},{7,5},{8,10},{9,11},{10,... | collective-permute-start | bytes 589832 | tf_op jit(solution)/shard_map/ppermute | solution.py:357
  192.8 14.1 %collective-permute-start.57 = (f32[12,32,128]{2,1,0:T(8,128)S(1)}, f32[12,32,128]{2,1,0:T(8,128)S(1)}, u32[]{:S(2)}, u32[]{:S(2)}) collective-permute-start(f32[12,32,128]{2,1,0:T(8,128)S(1)} %get-tuple-element.243), channel_id=1, source_target_pairs={{0,3},{1,2},{2,1},{3,0},{4,7},{5,6},{6,5},{7,4},{8,11},{9,10},{10,... | collective-permute-start | bytes 589832 | tf_op jit(solution)/shard_map/ppermute | solution.py:357
  202.5 10.0 %collective-permute-start.63 = (f32[128,128]{1,0:T(8,128)S(1)}, f32[128,128]{1,0:T(8,128)S(1)}, u32[]{:S(2)}, u32[]{:S(2)}) collective-permute-start(f32[128,128]{1,0:T(8,128)S(1)} %cross.1), channel_id=1, source_target_pairs={{0,24},{4,28},{8,16},{12,20},{16,8},{20,12},{24,0},{28,4},{1,25},{... | collective-permute-start | bytes 196616 | tf_op jit(solution)/shard_map/ppermute | solution.py:357
  203.8 14.9 %collective-permute-start.62 = (f32[128,128]{1,0:T(8,128)S(1)}, f32[128,128]{1,0:T(8,128)S(1)}, u32[]{:S(2)}, u32[]{:S(2)}) collective-permute-start(f32[128,128]{1,0:T(8,128)S(1)} %cross.1), channel_id=1, source_target_pairs={{0,16},{4,20},{8,24},{12,28},{16,0},{20,4},{24,8},{28,12},{1,17},{... | collective-permute-start | bytes 196616 | tf_op jit(solution)/shard_map/ppermute | solution.py:357
  205.7 13.0 %collective-permute-start.61 = (f32[128,128]{1,0:T(8,128)S(1)}, f32[128,128]{1,0:T(8,128)S(1)}, u32[]{:S(2)}, u32[]{:S(2)}) collective-permute-start(f32[128,128]{1,0:T(8,128)S(1)} %cross.1), channel_id=1, source_target_pairs={{0,8},{4,12},{8,0},{12,4},{16,24},{20,28},{24,16},{28,20},{1,9},{5... | collective-permute-start | bytes 196616 | tf_op jit(solution)/shard_map/ppermute | solution.py:357
  208.8 10.0 %collective-permute-start.60 = (f32[128,128]{1,0:T(8,128)S(1)}, f32[128,128]{1,0:T(8,128)S(1)}, u32[]{:S(2)}, u32[]{:S(2)}) collective-permute-start(f32[128,128]{1,0:T(8,128)S(1)} %turn_cross.1), channel_id=1, source_target_pairs={{0,24},{4,28},{8,16},{12,20},{16,8},{20,12},{24,0},{28,4},{1,25},{... | collective-permute-start | bytes 196616 | tf_op jit(solution)/shard_map/ppermute | solution.py:357
  221.9 10.7 %collective-permute-start.71 = (f32[12,32,128]{2,1,0:T(8,128)S(1)}, f32[12,32,128]{2,1,0:T(8,128)S(1)}, u32[]{:S(2)}, u32[]{:S(2)}) collective-permute-start(f32[12,32,128]{2,1,0:T(8,128)S(1)} %get-tuple-element.265), channel_id=1, source_target_pairs={{0,3},{1,2},{2,1},{3,0},{4,7},{5,6},{6,5},{7,4},{8,11},{9,10},{10,... | collective-permute-start | bytes 589832 | tf_op jit(solution)/shard_map/ppermute | solution.py:357
  (25 other events, 167.5 us)
